TPU v7x, 32 devices: a whole 2x2x4 slice. The times are simulated.
32 devices in a mesh: rep: 8 (over y, x, core), shard: 4 (over z).
Axes of the slice: x: 2, y: 2, z: 4, core: 2. Of those that a mesh axis runs over, the one named last changes fastest.
Arguments:
- layer_input: bfloat16 [16384, 2048], P(('rep', 'shard')), may hold values from -6 to 6
- gain_attn: bfloat16 [2048], P('shard'), may hold values from 0.5 to 1.5
- w_query: bfloat16 [2048, 2048], P('shard'), may hold values from -0.125 to 0.125
- w_key: bfloat16 [2048, 2048], P('shard'), may hold values from -0.125 to 0.125
- w_value: bfloat16 [2048, 2048], P('shard'), may hold values from -0.125 to 0.125
- w_out: bfloat16 [2048, 2048], P(None, 'shard'), may hold values from -0.5 to 0.5
- gain_mlp: bfloat16 [2048], P('shard'), may hold values from 0.5 to 1.5
- w_gate: bfloat16 [2048, 5632], P('shard'), may hold values from -0.125 to 0.125
- w_up: bfloat16 [2048, 5632], P('shard'), may hold values from -0.125 to 0.125
- w_down: bfloat16 [5632, 2048], P(None, 'shard'), may hold values from -0.078125 to 0.078125
- segments: int32 [32, 512], P(('rep', 'shard')), may hold values from 0 to 3, never falling along the last dimension, each value on 1 to 256 neighbouring positions
- attn_route: int32 [16384, 2], P(('rep', 'shard')), may hold values from 0 to 7, all different within a row
- attn_gate: float32 [16384, 2], P(('rep', 'shard')), may hold values from 0.2 to 1
- mlp_route: int32 [16384, 2], P(('rep', 'shard')), may hold values from 0 to 7, all different within a row
- mlp_gate: float32 [16384, 2], P(('rep', 'shard')), may hold values from 0.2 to 1
- cotangent: bfloat16 [16384, 2048], P(('rep', 'shard')), may hold values from -6 to 6
Outputs:
- output: bfloat16 [16384, 2048], P(('rep', 'shard'))
- grad_input: bfloat16 [16384, 2048], P(('rep', 'shard'))
- grad_gain_attn: float32 [2048], P('shard')
- grad_query: float32 [2048, 2048], P('shard')
- grad_key: float32 [2048, 2048], P('shard')
- grad_value: float32 [2048, 2048], P('shard')
- grad_out: float32 [2048, 2048], P(None, 'shard')
- grad_gain_mlp: float32 [2048], P('shard')
- grad_gate: float32 [2048, 5632], P('shard')
- grad_up: float32 [2048, 5632], P('shard')
- grad_down: float32 [5632, 2048], P(None, 'shard')
All inputs are finite; a program needn't handle non-finite values.
Results may differ from a plain program's by a relative error of at most 0.017.
Values may be sent and summed in bfloat16 or wider, within the bound.
A program may use at most 384 MiB of HBM per device.

v0:
```python
import jax
import jax.numpy as jnp
from jax import lax
from jax.sharding import PartitionSpec as P

HEADS = 16
HD = 128
WIN = 256
CAP = 128


EPSILON = 1e-05


def product(left, right):
    return jnp.dot(left, right, preferred_element_type=jnp.float32)


def product_nt(left, right):
    return lax.dot_general(
        left, right, (((1,), (1,)), ((), ())), preferred_element_type=jnp.float32
    )


def product_tn(left, right):
    return lax.dot_general(
        left, right, (((0,), (0,)), ((), ())), preferred_element_type=jnp.float32
    )


def rotary_tables(length, head_width):
    half_width = head_width // 2
    positions = jnp.arange(length, dtype=jnp.float32)
    inverse = 10000.0 ** (-2.0 * jnp.arange(half_width, dtype=jnp.float32) / head_width)
    angles = positions[:, None] * inverse[None, :]
    return (jnp.cos(angles)[:, None, :], jnp.sin(angles)[:, None, :])


def rotate(values, cos_table, sin_table):
    half_width = values.shape[-1] // 2
    first_half = values[..., :half_width]
    second_half = values[..., half_width:]
    return jnp.concatenate(
        [
            first_half * cos_table - second_half * sin_table,
            second_half * cos_table + first_half * sin_table,
        ],
        axis=-1,
    )


def rotate_back(gradient, cos_table, sin_table):
    half_width = gradient.shape[-1] // 2
    first_half = gradient[..., :half_width]
    second_half = gradient[..., half_width:]
    return jnp.concatenate(
        [
            first_half * cos_table + second_half * sin_table,
            second_half * cos_table - first_half * sin_table,
        ],
        axis=-1,
    )


def window_mask(segment_row):
    row_ids = jnp.arange(segment_row.shape[0], dtype=jnp.int32)
    distance = row_ids[:, None] - row_ids[None, :]
    return (segment_row[:, None] == segment_row[None, :]) & (distance >= 0) & (distance < WIN)


def plan_slots(route_ids, gate_values):
    hit_mask = route_ids == 0
    hit_count = jnp.sum(hit_mask.astype(jnp.int32), axis=-1)
    weight = jnp.sum(jnp.where(hit_mask, gate_values, 0.0), axis=-1)
    slot_order = jnp.cumsum(hit_count) - hit_count
    kept_rows = (hit_count > 0) & (slot_order < CAP)
    slot_ids = jnp.arange(CAP, dtype=jnp.int32)
    slot_table = (slot_order[None, :] == slot_ids[:, None]) & kept_rows[None, :]
    token_ids = jnp.arange(route_ids.shape[0], dtype=jnp.int32)
    token_of = jnp.sum(jnp.where(slot_table, token_ids[None, :], 0), axis=1)
    filled = jnp.any(slot_table, axis=1)
    slot_of = jnp.minimum(slot_order, CAP - 1)
    return (token_of, filled, slot_of, jnp.where(kept_rows, weight, 0.0), kept_rows)


def score_rows(queries, key_rows, allowed, score_scale):
    scores = (
        jnp.einsum("qhd,khd->hqk", queries, key_rows, preferred_element_type=jnp.float32)
        * score_scale
    )
    return jnp.where(allowed, scores, -1e30)


def norm_back(grad_normed, source, root_inv, gain_row):
    scaled = grad_normed * gain_row
    grad_gain = jnp.sum(grad_normed * source * root_inv, axis=0)
    cubed = root_inv * root_inv * root_inv
    grad_source = root_inv * scaled - source * cubed * jnp.mean(
        scaled * source, axis=-1, keepdims=True
    )
    return (grad_gain, grad_source)


def per_device(
    layer_input,
    gain_attn,
    w_query,
    w_key,
    w_value,
    w_out,
    gain_mlp,
    w_gate,
    w_up,
    w_down,
    segments,
    attn_route,
    attn_gate,
    mlp_route,
    mlp_gate,
    cotangent,
):
    length = layer_input.shape[0]
    score_scale = HD ** (-0.5)
    shape_heads = (length, HEADS, HD)
    query_full, key_full, value_full, out_full, gain_one = (
        lax.all_gather(w_query, "shard", axis=0, tiled=True),
        lax.all_gather(w_key, "shard", axis=0, tiled=True),
        lax.all_gather(w_value, "shard", axis=0, tiled=True),
        lax.all_gather(w_out, "shard", axis=1, tiled=True),
        lax.all_gather(gain_attn, "shard", axis=0, tiled=True),
    )
    gate_full, up_full, down_full, gain_two = (
        lax.all_gather(w_gate, "shard", axis=0, tiled=True),
        lax.all_gather(w_up, "shard", axis=0, tiled=True),
        lax.all_gather(w_down, "shard", axis=1, tiled=True),
        lax.all_gather(gain_mlp, "shard", axis=0, tiled=True),
    )
    inputs = layer_input.astype(jnp.float32)
    root_one = lax.rsqrt(jnp.mean(inputs * inputs, axis=-1, keepdims=True) + EPSILON)
    gain_first = gain_one.astype(jnp.float32)
    normed = (inputs * root_one * gain_first).astype(jnp.bfloat16)
    cos_table, sin_table = rotary_tables(length, HD)
    queries = rotate(product(normed, query_full).reshape(shape_heads), cos_table, sin_table).astype(
        jnp.bfloat16
    )
    key_rows = rotate(product(normed, key_full).reshape(shape_heads), cos_table, sin_table).astype(
        jnp.bfloat16
    )
    values = product(normed, value_full).astype(jnp.bfloat16).reshape(shape_heads)
    allowed = window_mask(segments[0])[None]
    scores = score_rows(queries, key_rows, allowed, score_scale)
    row_peak = jnp.max(scores, axis=-1, keepdims=True)
    unscaled = jnp.exp(scores - row_peak)
    denominator = jnp.sum(unscaled, axis=-1, keepdims=True)
    probs_low = (unscaled / denominator).astype(jnp.bfloat16)
    log_norm = row_peak + jnp.log(denominator)
    context = (
        jnp.einsum("hqk,khd->qhd", probs_low, values, preferred_element_type=jnp.float32)
        .astype(jnp.bfloat16)
        .reshape(length, HEADS * HD)
    )
    attn_weight = jnp.sum(jnp.where(attn_route == 0, attn_gate, 0.0), axis=-1)[:, None]
    hidden = inputs + product(context, out_full) * attn_weight
    root_two = lax.rsqrt(jnp.mean(hidden * hidden, axis=-1, keepdims=True) + EPSILON)
    gain_second = gain_two.astype(jnp.float32)
    normed_two = (hidden * root_two * gain_second).astype(jnp.bfloat16)
    token_of, filled, slot_of, mix_weight, kept_rows = plan_slots(mlp_route, mlp_gate)
    dispatched = jnp.where(
        filled[:, None], jnp.take(normed_two, token_of, axis=0), jnp.zeros((), jnp.bfloat16)
    )
    gate_act = product(dispatched, gate_full)
    up_act = product(dispatched, up_full)
    sigmoid_gate = jax.nn.sigmoid(gate_act)
    silu_gate = gate_act * sigmoid_gate
    inner_act = (silu_gate * up_act).astype(jnp.bfloat16)
    expert_out = product(inner_act, down_full)
    output = (hidden + jnp.take(expert_out, slot_of, axis=0) * mix_weight[:, None]).astype(
        jnp.bfloat16
    )
    gate_back, up_back, down_back = (gate_full, up_full, down_full)
    upstream = cotangent.astype(jnp.float32)
    slot_weight = jnp.take(mix_weight, token_of, axis=0)[:, None]
    slot_grad = jnp.where(
        filled[:, None], jnp.take(upstream, token_of, axis=0) * slot_weight, 0.0
    ).astype(jnp.bfloat16)
    grad_inner = product_nt(slot_grad, down_back)
    grad_gate_act = (
        grad_inner * up_act * sigmoid_gate * (1.0 + gate_act * (1.0 - sigmoid_gate))
    ).astype(jnp.bfloat16)
    grad_up_act = (grad_inner * silu_gate).astype(jnp.bfloat16)
    grad_dispatched = product_nt(grad_gate_act, gate_back) + product_nt(grad_up_act, up_back)
    grad_normed_two = jnp.where(kept_rows[:, None], jnp.take(grad_dispatched, slot_of, axis=0), 0.0)
    grad_gain_second, grad_through = norm_back(grad_normed_two, hidden, root_two, gain_second)
    grad_hidden = upstream + grad_through
    all_disp, all_inner, all_gate_grad, all_up_grad, all_slot_grad = (
        lax.all_gather(dispatched, "shard", axis=0, tiled=True),
        lax.all_gather(inner_act, "shard", axis=0, tiled=True),
        lax.all_gather(grad_gate_act, "shard", axis=0, tiled=True),
        lax.all_gather(grad_up_act, "shard", axis=0, tiled=True),
        lax.all_gather(slot_grad, "shard", axis=0, tiled=True),
    )
    owned = dispatched.shape[1] // lax.axis_size("shard")
    start = lax.axis_index("shard") * owned
    own_disp = lax.dynamic_slice_in_dim(all_disp, start, owned, 1)
    own_slot_grad = lax.dynamic_slice_in_dim(all_slot_grad, start, owned, 1)
    owned_gate = product_tn(own_disp, all_gate_grad)
    owned_up = product_tn(own_disp, all_up_grad)
    owned_down = product_tn(all_inner, own_slot_grad)
    owned_gain = lax.psum_scatter(grad_gain_second, "shard", scatter_dimension=0, tiled=True)
    mlp_parts = (owned_gate, owned_up, owned_down, owned_gain)
    query_back, key_back, value_back, out_back = (query_full, key_full, value_full, out_full)
    grad_projected = (grad_hidden * attn_weight).astype(jnp.bfloat16)
    grad_out_w = product_tn(context, grad_projected)
    grad_context = product_nt(grad_projected, out_back).astype(jnp.bfloat16).reshape(shape_heads)
    scores = score_rows(queries, key_rows, allowed, score_scale)
    probs = jnp.exp(scores - log_norm)
    probs_back = probs.astype(jnp.bfloat16)
    grad_values = jnp.einsum(
        "hqk,qhd->khd", probs_back, grad_context, preferred_element_type=jnp.float32
    ).astype(jnp.bfloat16)
    grad_probs = jnp.einsum(
        "qhd,khd->hqk", grad_context, values, preferred_element_type=jnp.float32
    )
    row_inner = jnp.sum(probs * grad_probs, axis=-1, keepdims=True)
    grad_scores = (probs * (grad_probs - row_inner)).astype(jnp.bfloat16)
    grad_queries = (
        jnp.einsum("hqk,khd->qhd", grad_scores, key_rows, preferred_element_type=jnp.float32)
        * score_scale
    )
    grad_keys = (
        jnp.einsum("hqk,qhd->khd", grad_scores, queries, preferred_element_type=jnp.float32)
        * score_scale
    )
    grad_qlin = (
        rotate_back(grad_queries, cos_table, sin_table)
        .astype(jnp.bfloat16)
        .reshape(length, HEADS * HD)
    )
    grad_klin = (
        rotate_back(grad_keys, cos_table, sin_table)
        .astype(jnp.bfloat16)
        .reshape(length, HEADS * HD)
    )
    grad_vlin = grad_values.reshape(length, HEADS * HD)
    grad_query_w = product_tn(normed, grad_qlin)
    grad_key_w = product_tn(normed, grad_klin)
    grad_value_w = product_tn(normed, grad_vlin)
    grad_normed = (
        product_nt(grad_qlin, query_back)
        + product_nt(grad_klin, key_back)
        + product_nt(grad_vlin, value_back)
    )
    grad_gain_first, grad_first = norm_back(grad_normed, inputs, root_one, gain_first)
    grad_input = (grad_hidden + grad_first).astype(jnp.bfloat16)
    attn_parts = (
        lax.psum_scatter(
            grad_query_w.astype(jnp.bfloat16), "shard", scatter_dimension=0, tiled=True
        ).astype(jnp.float32),
        lax.psum_scatter(
            grad_key_w.astype(jnp.bfloat16), "shard", scatter_dimension=0, tiled=True
        ).astype(jnp.float32),
        lax.psum_scatter(
            grad_value_w.astype(jnp.bfloat16), "shard", scatter_dimension=0, tiled=True
        ).astype(jnp.float32),
        lax.psum_scatter(
            grad_out_w.astype(jnp.bfloat16), "shard", scatter_dimension=1, tiled=True
        ).astype(jnp.float32),
        lax.psum_scatter(
            grad_gain_first.astype(jnp.bfloat16), "shard", scatter_dimension=0, tiled=True
        ).astype(jnp.float32),
    )
    summed = (
        lax.psum(attn_parts[0].astype(jnp.bfloat16), "rep").astype(jnp.float32),
        lax.psum(attn_parts[1].astype(jnp.bfloat16), "rep").astype(jnp.float32),
        lax.psum(attn_parts[2].astype(jnp.bfloat16), "rep").astype(jnp.float32),
        lax.psum(attn_parts[3].astype(jnp.bfloat16), "rep").astype(jnp.float32),
        lax.psum(attn_parts[4].astype(jnp.bfloat16), "rep").astype(jnp.float32),
        lax.psum(mlp_parts[0].astype(jnp.bfloat16), "rep").astype(jnp.float32),
        lax.psum(mlp_parts[1].astype(jnp.bfloat16), "rep").astype(jnp.float32),
        lax.psum(mlp_parts[2].astype(jnp.bfloat16), "rep").astype(jnp.float32),
        lax.psum(mlp_parts[3].astype(jnp.bfloat16), "rep").astype(jnp.float32),
    )
    return (
        output,
        grad_input,
        summed[4],
        summed[0],
        summed[1],
        summed[2],
        summed[3],
        summed[8],
        summed[5],
        summed[6],
        summed[7],
    )


def solution(mesh):
    placed = (
        P(("rep", "shard"), None),
        P("shard"),
        P("shard", None),
        P("shard", None),
        P("shard", None),
        P(None, "shard"),
        P("shard"),
        P("shard", None),
        P("shard", None),
        P(None, "shard"),
        P(("rep", "shard"), None),
        P(("rep", "shard"), None),
        P(("rep", "shard"), None),
        P(("rep", "shard"), None),
        P(("rep", "shard"), None),
        P(("rep", "shard"), None),
    )
    return jax.shard_map(
        per_device,
        mesh=mesh,
        in_specs=placed,
        out_specs=(
            P(("rep", "shard"), None),
            P(("rep", "shard"), None),
            P("shard"),
            P("shard", None),
            P("shard", None),
            P("shard", None),
            P(None, "shard"),
            P("shard"),
            P("shard", None),
            P("shard", None),
            P(None, "shard"),
        ),
        check_vma=False,
    )
```

profile of v0, /device:TPU:0, one launch (start us, length us, event | category | flops | bytes accessed | tf_op | source)
XLA Modules:
  0.0 3145.0 jit_solution(14300096432098832938)
XLA Ops:
  12.0 13.6 all-gather
  25.6 12.3 all-gather.1
  43.1 3.8 gather_fusion.1
  51.9 110.1 %all-gather.17.cloned.1.call-done = bf16[2048,2048]{1,0:T(8,128)(2,1)} async-done(((bf16[512,2048]{1,0:T(8,128)(2,1)}), bf16[2048,2048]{1,0:T(8,128)(2,1)}) %all-gather.17.cloned.1.call-update) | async-done | bytes 8388624 | tf_op jit(solution)/shard_map/all_gather | solution.py:126
  162.1 7.0 convolution_bitcast_fusion.1
  172.0 139.5 %all-gather.19.cloned.1.call-done = bf16[2048,2048]{1,0:T(8,128)(2,1)} async-done(((bf16[512,2048]{1,0:T(8,128)(2,1)}), bf16[2048,2048]{1,0:T(8,128)(2,1)}) %all-gather.19.cloned.1.call-update) | async-done | bytes 8388624 | tf_op jit(solution)/shard_map/all_gather | solution.py:127
  311.5 7.0 convolution_bitcast_fusion
  321.4 4.7 fusion.56
  326.0 7.8 subtract_convert_fusion.3
  333.9 8.8 fusion.58
  342.7 8.4 fusion
  351.2 109.8 %all-gather.15.cloned.1.call-done = bf16[2048,2048]{1,0:T(8,128)(2,1)} async-done(((bf16[512,2048]{1,0:T(8,128)(2,1)}), bf16[2048,2048]{1,0:T(8,128)(2,1)}) %all-gather.15.cloned.1.call-update) | async-done | bytes 8388624 | tf_op jit(solution)/shard_map/all_gather | solution.py:128
  461.0 8.3 fusion.30
  470.6 9.8 fusion.25
  480.4 129.9 %all-gather.21.cloned.1.call-done = bf16[2048,2048]{1,0:T(8,128)(2,1)} async-done(((bf16[2048,512]{1,0:T(8,128)(2,1)}), bf16[2048,2048]{1,0:T(8,128)(2,1)}) %all-gather.21.cloned.1.call-update) | async-done | bytes 8388624 | tf_op jit(solution)/shard_map/all_gather | solution.py:129
  610.3 8.3 multiply_reduce_fusion.3
  623.8 377.3 %all-gather.23.cloned.1.call-done = bf16[2048,5632]{1,0:T(8,128)(2,1)} async-done(((bf16[512,5632]{1,0:T(8,128)(2,1)}), bf16[2048,5632]{1,0:T(8,128)(2,1)}) %all-gather.23.cloned.1.call-update) | async-done | bytes 23068688 | tf_op jit(solution)/shard_map/all_gather | solution.py:133
  1001.0 10.4 fusion.59
  1011.4 380.5 %all-gather.25.cloned.1.call-done = bf16[2048,5632]{1,0:T(8,128)(2,1)} async-done(((bf16[512,5632]{1,0:T(8,128)(2,1)}), bf16[2048,5632]{1,0:T(8,128)(2,1)}) %all-gather.25.cloned.1.call-update) | async-done | bytes 23068688 | tf_op jit(solution)/shard_map/all_gather | solution.py:134
  1391.9 13.2 fusion.60
  1405.1 377.8 %all-gather.27.cloned.1.call-done = bf16[5632,2048]{1,0:T(8,128)(2,1)} async-done(((bf16[5632,512]{1,0:T(8,128)(2,1)}), bf16[5632,2048]{1,0:T(8,128)(2,1)}) %all-gather.27.cloned.1.call-update) | async-done | bytes 23068688 | tf_op jit(solution)/shard_map/all_gather | solution.py:135
  1782.9 14.5 multiply_convert_fusion.3
  1799.4 12.1 fusion.62
  1811.5 11.9 convolution_add_fusion
  1823.4 3.6 gather_fusion.4
  1827.0 9.2 fusion.61
  1836.3 3.6 gather_fusion.3
  1839.9 5.4 multiply_reduce_fusion.1
  1846.0 4.9 subtract_add_fusion
  1852.8 7.0 convolution_convert_fusion.3
  1860.7 10.6 convolution_convert_fusion.7
  1871.2 3.2 copy.109
  1874.5 12.4 multiply_reduce_fusion
  1886.9 11.8 multiply_convert_fusion
  1898.7 5.6 multiply_bitcast_fusion.1
  1904.3 4.7 multiply_bitcast_fusion
  1909.1 4.3 add_convert_fusion
  1917.3 10.4 convolution_convert_fusion.5
  1929.3 4.1 pad_maximum_fusion.2
  1933.3 4.1 copy.90
  1937.4 8.9 convolution_convert_fusion.6
  1948.0 8.9 fusion.22
  1958.2 7.5 convolution_convert_fusion.4
  1965.9 8.5 convolution_convert_fusion.1
  1974.4 67.9 %all-gather.31.cloned.1.call-done = bf16[512,5632]{1,0:T(8,128)(2,1)} async-done(((bf16[128,5632]{1,0:T(8,128)(2,1)}), bf16[512,5632]{1,0:T(8,128)(2,1)}) %all-gather.31.cloned.1.call-update) | async-done | bytes 5767184 | tf_op jit(solution)/shard_map/all_gather | solution.py:198
  2042.3 8.5 convolution_convert_fusion.2
  2050.7 37.4 %all-gather.37.cloned.1.call-done = bf16[512,2048]{1,0:T(8,128)(2,1)} async-done(((bf16[128,2048]{1,0:T(8,128)(2,1)}), bf16[512,2048]{1,0:T(8,128)(2,1)}) %all-gather.37.cloned.1.call-update) | async-done | bytes 2097168 | tf_op jit(solution)/shard_map/all_gather | solution.py:200
  2088.1 106.9 %all-gather.35.cloned.1.call-done = bf16[512,5632]{1,0:T(8,128)(2,1)} async-done(((bf16[128,5632]{1,0:T(8,128)(2,1)}), bf16[512,5632]{1,0:T(8,128)(2,1)}) %all-gather.35.cloned.1.call-update) | async-done | bytes 5767184 | tf_op jit(solution)/shard_map/all_gather | solution.py:197
  2195.0 8.5 convolution_convert_fusion
  2203.5 136.7 %reduce-scatter.11.cloned.1.call-done = bf16[2048,512]{1,0:T(8,128)(2,1)} async-done(((bf16[2048,2048]{1,0:T(8,128)(2,1)}), bf16[2048,512]{1,0:T(8,128)(2,1)}) %reduce-scatter.11.cloned.1.call-update) | async-done | bytes 2097168 | tf_op jit(solution)/shard_map/reduce_scatter | solution.py:265
  2340.1 148.0 %reduce-scatter.7.cloned.1.call-done = bf16[512,2048]{1,0:T(8,128)(2,1)} async-done(((bf16[2048,2048]{1,0:T(8,128)(2,1)}), bf16[512,2048]{1,0:T(8,128)(2,1)}) %reduce-scatter.7.cloned.1.call-update) | async-done | bytes 2097168 | tf_op jit(solution)/shard_map/reduce_scatter | solution.py:259
  2488.2 148.0 %reduce-scatter.5.cloned.1.call-done = bf16[512,2048]{1,0:T(8,128)(2,1)} async-done(((bf16[2048,2048]{1,0:T(8,128)(2,1)}), bf16[512,2048]{1,0:T(8,128)(2,1)}) %reduce-scatter.5.cloned.1.call-update) | async-done | bytes 2097168 | tf_op jit(solution)/shard_map/reduce_scatter | solution.py:256
  2636.2 148.0 %reduce-scatter.9.cloned.1.call-done = bf16[512,2048]{1,0:T(8,128)(2,1)} async-done(((bf16[2048,2048]{1,0:T(8,128)(2,1)}), bf16[512,2048]{1,0:T(8,128)(2,1)}) %reduce-scatter.9.cloned.1.call-update) | async-done | bytes 2097168 | tf_op jit(solution)/shard_map/reduce_scatter | solution.py:262
  2786.1 7.6 fusion.64
  2793.7 11.0 fusion.63
  2804.7 11.9 fusion.15
  2816.6 10.8 all-reduce
  2827.5 8.9 all-reduce.1
  2836.4 13.0 all-reduce.2
  2850.6 6.5 fusion.12
  2857.1 250.2 %all-reduce.6.cloned.1.call-done = (bf16[512,2048]{1,0:T(8,128)(2,1)}, bf16[512,2048]{1,0:T(8,128)(2,1)}, bf16[512,2048]{1,0:T(8,128)(2,1)}, bf16[2048,512]{1,0:...) async-done(((bf16[512,2048]{1,0:T(8,128)(2,1)}, bf16[512,2048]{1,0:T(8,128)(2,1)}, bf16[512,2048]{1,0:T(8,128)(2,1)}, ...) | async-done | bytes 25690128 | tf_op jit(solution)/shard_map/psum | solution.py:273
  3107.3 8.7 convert_element_type.183
  3116.0 5.9 convert_element_type.185
  3122.0 6.1 convert_element_type.187
  (219 shorter events, 53.9 us)
Async XLA Ops:
  7.2 154.9 %all-gather.17.cloned.1.call-start = ((), (), s32[]{:S(2)}) async-start(), calls=%async_computation.5 | async-start | bytes 10485760 | tf_op jit(solution)/shard_map/all_gather | solution.py:126
  7.9 303.6 %all-gather.19.cloned.1.call-start = ((), (), s32[]{:S(2)}) async-start(), calls=%async_computation.6 | async-start | bytes 10485760 | tf_op jit(solution)/shard_map/all_gather | solution.py:127
  8.7 452.3 %all-gather.15.cloned.1.call-start = ((), (), s32[]{:S(2)}) async-start(), calls=%async_computation.4 | async-start | bytes 10485760 | tf_op jit(solution)/shard_map/all_gather | solution.py:128
  9.4 600.9 %all-gather.21.cloned.1.call-start = ((), (), s32[]{:S(2)}) async-start(), calls=%async_computation.7 | async-start | bytes 10485760 | tf_op jit(solution)/shard_map/all_gather | solution.py:129
  10.0 991.1 %all-gather.23.cloned.1.call-start = ((), (), s32[]{:S(2)}) async-start(), calls=%async_computation.8 | async-start | bytes 28835840 | tf_op jit(solution)/shard_map/all_gather | solution.py:133
  10.6 1381.3 %all-gather.25.cloned.1.call-start = ((), (), s32[]{:S(2)}) async-start(), calls=%async_computation.9 | async-start | bytes 28835840 | tf_op jit(solution)/shard_map/all_gather | solution.py:134
  11.1 14.4 copy-start.62
  11.2 26.7 copy-start.47
  11.2 27.2 copy-start.16
  11.2 1771.7 %all-gather.27.cloned.1.call-start = ((), (), s32[]{:S(2)}) async-start(), calls=%async_computation.10 | async-start | bytes 28835840 | tf_op jit(solution)/shard_map/all_gather | solution.py:135
  11.9 29.1 copy-start.56
  11.9 1953.9 %all-gather.29.cloned.1.call-start = ((), (), s32[]{:S(2)}) async-start(), calls=%async_computation.15 | async-start | bytes 2621440 | tf_op jit(solution)/shard_map/all_gather | solution.py:196
  25.6 435.4 %copy-start.44 = (f32[4,1,512]{2,1,0:T(1,128)}, f32[4,1,512]{2,1,0:T(1,128)S(1)}, u32[]{:S(2)}) copy-start(f32[4,1,512]{2,1,0:T(1,128)S(1)} %convert_element_type.188) | copy-start | bytes 24580
  41.6 5.3 copy-start
  41.6 5.4 copy-start.48
  43.0 3.9 copy-start.57
  43.1 4.1 copy-start.19
  43.1 5.1 copy-start.50
  47.0 563.3 %copy-start.59 = (f32[512]{0:T(512)}, f32[512]{0:T(512)S(1)}, u32[]{:S(2)}) copy-start(f32[512]{0:T(512)S(1)} %fusion.42) | copy-start | bytes 6148
  48.2 412.8 %copy-start.53 = (f32[512]{0:T(512)}, f32[512]{0:T(512)S(1)}, u32[]{:S(2)}) copy-start(f32[512]{0:T(512)S(1)} %get-tuple-element.53) | copy-start | bytes 6148
  50.8 275.2 %copy-start.26 = (f32[512,64]{1,0:T(8,128)}, f32[512,64]{1,0:T(8,128)S(1)}, u32[]{:S(2)}) copy-start(f32[512,64]{1,0:T(8,128)S(1)} %get-tuple-element.56) | copy-start | bytes 393220
  321.4 4.7 copy-start.28
  326.0 7.9 copy-start.39
  333.9 8.8 copy-start.8
  333.9 8.8 copy-start.9
  333.9 8.8 copy-start.10
  333.9 8.8 copy-start.11
  342.7 126.6 %copy-start.40 = (f32[16,512]{1,0:T(8,128)}, f32[16,512]{1,0:T(8,128)S(1)}, u32[]{:S(2)}) copy-start(f32[16,512]{1,0:T(8,128)S(1)} %get-tuple-element.58) | copy-start | bytes 98308
  342.7 118.3 %copy-start.20 = (bf16[512,2048]{1,0:T(8,128)(2,1)S(1)}, bf16[512,2048]{1,0:T(8,128)(2,1)}, u32[]{:S(2)}) copy-start(bf16[512,2048]{1,0:T(8,128)(2,1)} %param.18) | copy-start | bytes 6291460
  351.2 118.1 %copy-start.42 = (f32[16,512]{1,0:T(8,128)}, f32[16,512]{1,0:T(8,128)S(1)}, u32[]{:S(2)}) copy-start(f32[16,512]{1,0:T(8,128)S(1)} %fusion) | copy-start | bytes 98308
  623.7 768.2 %copy-start.15 = (bf16[128,2048]{1,0:T(8,128)(2,1)S(1)}, bf16[128,2048]{1,0:T(8,128)(2,1)}, u32[]{:S(2)}) copy-start(bf16[128,2048]{1,0:T(8,128)(2,1)} %select_select_fusion.1) | copy-start | bytes 1572868
  623.7 1342.1 %all-gather.33.cloned.1.call-start = ((), (), s32[]{:S(2)}) async-start(), calls=%async_computation.17 | async-start | bytes 7208960 | tf_op jit(solution)/shard_map/all_gather | solution.py:199
  1797.4 244.8 %all-gather.31.cloned.1.call-start = ((), (), s32[]{:S(2)}) async-start(), calls=%async_computation.16 | async-start | bytes 7208960 | tf_op jit(solution)/shard_map/all_gather | solution.py:198
  1798.0 290.1 %all-gather.37.cloned.1.call-start = ((), (), s32[]{:S(2)}) async-start(), calls=%async_computation.19 | async-start | bytes 2621440 | tf_op jit(solution)/shard_map/all_gather | solution.py:200
  1798.7 396.2 %all-gather.35.cloned.1.call-start = ((), (), s32[]{:S(2)}) async-start(), calls=%async_computation.18 | async-start | bytes 7208960 | tf_op jit(solution)/shard_map/all_gather | solution.py:197
  1799.3 12.2 copy-start.14
  1799.3 540.8 %reduce-scatter.11.cloned.1.call-start = ((), (), s32[]{:S(2)}) async-start(), calls=%async_computation.14 | async-start | bytes 10485760 | tf_op jit(solution)/shard_map/reduce_scatter | solution.py:265
  1836.3 9.0 copy-start.17
  1839.9 5.4 copy-start.1
  1839.9 5.4 copy-start.2
  1839.9 6.0 copy-start.4
  1839.9 6.0 copy-start.51
  1845.9 6.9 copy-start.60
  1846.0 6.9 copy-start.63
  1859.9 628.3 %reduce-scatter.7.cloned.1.call-start = ((), (), s32[]{:S(2)}) async-start(), calls=%async_computation.12 | async-start | bytes 10485760 | tf_op jit(solution)/shard_map/reduce_scatter | solution.py:259
  1874.5 12.4 copy-start.6
  1904.3 4.8 copy-start.27
  1904.3 4.8 copy-start.29
  1913.3 3.9 copy-start.45
  1913.3 3.9 copy-start.54
  1927.7 708.5 %reduce-scatter.5.cloned.1.call-start = ((), (), s32[]{:S(2)}) async-start(), calls=%async_computation.11 | async-start | bytes 10485760 | tf_op jit(solution)/shard_map/reduce_scatter | solution.py:256
  1933.3 4.1 copy-start.21
  1946.3 837.9 %reduce-scatter.9.cloned.1.call-start = ((), (), s32[]{:S(2)}) async-start(), calls=%async_computation.13 | async-start | bytes 10485760 | tf_op jit(solution)/shard_map/reduce_scatter | solution.py:262
  1948.0 10.2 copy-start.22
  1965.7 1141.5 %all-reduce.6.cloned.1.call-start = ((), (), s32[]{:S(2)}) async-start(), calls=%async_computation.20 | async-start | bytes 51380224 | tf_op jit(solution)/shard_map/psum | solution.py:273
  2786.1 7.6 copy-start.38
  2793.7 11.0 copy-start.23
  2793.7 11.0 copy-start.32
  2804.7 22.7 copy-start.46
  2804.7 45.8 %copy-start.52 = (f32[512]{0:T(512)S(1)}, f32[512]{0:T(512)}, u32[]{:S(2)}) copy-start(f32[512]{0:T(512)} %get-tuple-element.52) | copy-start | bytes 6148
  3107.3 8.7 copy-start.25
  3107.3 14.7 slice-start
  3116.0 5.9 slice-start.1
  3122.0 6.1 copy-start.36
  (20 other events, 42.9 us)
Sparse Core Ops, SparseCore 0:
  9.6 152.4 all-gather.16
  163.6 147.8 all-gather.18
  313.1 147.8 all-gather.14
  462.4 147.8 all-gather.20
  611.7 389.2 all-gather.22
  1002.5 389.3 all-gather.24
  1393.5 389.3 all-gather.26
  1784.5 44.2 all-gather.28
  1830.3 105.4 all-gather.32
  1937.2 104.9 all-gather.30
  2043.8 44.2 all-gather.36
  2089.5 105.4 all-gather.34
  2197.3 142.7 reduce-scatter.10
  2342.9 145.1 reduce-scatter.6
  2490.9 145.1 reduce-scatter.4
  2638.9 145.1 reduce-scatter.8
  2789.2 318.0 all-reduce.5
where the time goes:
time: 3150 us
  waiting for transfers between devices  2670 us (85%)
  matrix products  252 us (8%)
  other arithmetic  97.1 us (3%)
  blocking collectives  58.4 us (2%)
  local copies, waits for them, and re-layouts  46.8 us (1%)
    all_gather x1, waiting for transfers between devices, per_device(): lax.all_gather(w_up, 'shard', axis=0, tiled=True)  380 us
    all_gather x1, waiting for transfers between devices, per_device(): lax.all_gather(w_down, 'shard', axis=1, tiled=True)  378 us
    all_gather x1, waiting for transfers between devices, per_device(): lax.all_gather(w_gate, 'shard', axis=0, tiled=True)  377 us
    psum x1, waiting for transfers between devices, per_device(): lax.psum(attn_parts[0].astype(jnp.bfloat16), 'rep').astype(jnp.float32)  250 us
    reduce_scatter x1, waiting for transfers between devices, per_device(): lax.psum_scatter(grad_key_w.astype(jnp.bfloat16), 'shard', scatter_dimens...  148 us
    reduce_scatter x1, waiting for transfers between devices, per_device(): lax.psum_scatter(grad_value_w.astype(jnp.bfloat16), 'shard', scatter_dime...  148 us
    reduce_scatter x1, waiting for transfers between devices, per_device(): lax.psum_scatter(grad_query_w.astype(jnp.bfloat16), 'shard', scatter_dime...  148 us
    all_gather x1, waiting for transfers between devices, per_device(): lax.all_gather(w_key, 'shard', axis=0, tiled=True)  139 us
  transfers between devices with their start and end apart: 17, of which 15 were waited for; matrix products, arithmetic and copies ran while one was open for 11% of the time, Pallas kernels for 0%

commit v1 on v0

v1 whole, which is shorter than its diff:
```python
import jax
import jax.numpy as jnp
from jax import lax
from jax.sharding import PartitionSpec as P

HEADS = 16
HD = 128
WIN = 256
CAP = 128
EPSILON = 1e-05
BF = jnp.bfloat16
F32 = jnp.float32


def mm(left, right):
    return jnp.dot(left, right, preferred_element_type=F32)


def mm_nt(left, right):
    return lax.dot_general(left, right, (((1,), (1,)), ((), ())), preferred_element_type=F32)


def mm_tn(left, right):
    return lax.dot_general(left, right, (((0,), (0,)), ((), ())), preferred_element_type=F32)


def swap(value, bit):
    size = lax.axis_size("rep")
    return lax.ppermute(value, "rep", [(i, i ^ bit) for i in range(size)])


def chip_bits():
    size, bits, bit = lax.axis_size("rep"), [], 2
    while bit < size:
        bits.append(bit)
        bit *= 2
    return bits


def chip_offsets():
    return list(range(0, lax.axis_size("rep"), 2))


def gather_chips(value):
    bits = chip_bits()
    if len(bits) == 2:
        one, two = bits
        half = value.shape[0] // 2
        by_one, by_two = swap(value, one), swap(value, two)
        far = jnp.concatenate([swap(by_one[:half], two), swap(by_two[half:], one)], axis=0)
        return {0: value, one: by_one, two: by_two, one ^ two: far}
    blocks = {0: value}
    for bit in bits:
        blocks.update({d ^ bit: swap(b, bit) for d, b in list(blocks.items())})
    return blocks


def add(left, right):
    return left.astype(F32) + right.astype(F32)


def scatter_chips(blocks):
    bits = chip_bits()
    if len(bits) == 2:
        one, two = bits
        half = blocks[0].shape[0] // 2
        far = blocks[one ^ two]
        near_one, near_two = blocks[one], blocks[two]
        top, bottom = swap(far[:half], one), swap(far[half:], two)
        two_bottom, one_top = swap(near_two[half:], two), swap(near_one[:half], one)
        two_top = swap(add(near_two[:half], top).astype(BF), two)
        one_bottom = swap(add(near_one[half:], bottom).astype(BF), one)
        by_one = jnp.concatenate([one_top, one_bottom], axis=0)
        by_two = jnp.concatenate([two_top, two_bottom], axis=0)
        return blocks[0].astype(F32) + by_one.astype(F32) + by_two.astype(F32)
    blocks = dict(blocks)
    for bit in reversed(bits):
        kept = {d: b for d, b in blocks.items() if not d & bit}
        blocks = {d: add(b, swap(blocks[d | bit], bit)).astype(BF) for d, b in kept.items()}
    return blocks[0].astype(F32)


def gather_plane(value):
    blocks = gather_chips(value)
    same = jnp.concatenate([blocks[d] for d in chip_offsets()], axis=0)
    return jnp.concatenate([same, swap(same, 1)], axis=0)


def scatter_plane(partial):
    half = partial.shape[0] // 2
    same = add(partial[:half], swap(partial[half:], 1)).astype(BF)
    offsets = chip_offsets()
    rows = half // len(offsets)
    return scatter_chips({d: same[i * rows : (i + 1) * rows] for i, d in enumerate(offsets)})


def rotary_tables(length):
    half = HD // 2
    positions = jnp.arange(length, dtype=F32)
    inverse = 10000.0 ** (-2.0 * jnp.arange(half, dtype=F32) / HD)
    angles = positions[:, None] * inverse[None, :]
    return jnp.cos(angles)[:, None, :], jnp.sin(angles)[:, None, :]


def rotate(values, cos_table, sin_table):
    half = values.shape[-1] // 2
    first, second = values[..., :half], values[..., half:]
    return jnp.concatenate(
        [first * cos_table - second * sin_table, second * cos_table + first * sin_table], axis=-1
    )


def plan_slots(route_ids, gate_values):
    hit_mask = route_ids == 0
    hit = jnp.any(hit_mask, axis=-1)
    weight = jnp.sum(jnp.where(hit_mask, gate_values, 0.0), axis=-1)
    ids = jnp.arange(route_ids.shape[0], dtype=jnp.int32)
    earlier = (ids[None, :] < ids[:, None]) & hit[None, :]
    order = jnp.sum(earlier.astype(jnp.int32), axis=1)
    kept = hit & (order < CAP)
    slots = jnp.arange(CAP, dtype=jnp.int32)
    table = (order[None, :] == slots[:, None]) & kept[None, :]
    return table, jnp.where(kept, weight, 0.0)


def norm_back(grad_normed, source, root, gain):
    scaled = grad_normed * gain
    grad_gain = jnp.sum(grad_normed * source * root, axis=0)
    mean = jnp.mean(scaled * source, axis=-1, keepdims=True)
    return grad_gain, root * scaled - source * (root * root * root) * mean


def gather_vector(rows):
    size, me = lax.axis_size("shard"), lax.axis_index("shard")
    parts = [rows] + [
        lax.ppermute(rows, "shard", [(i, (i - k) % size) for i in range(size)])
        for k in range(1, size)
    ]
    twice = jnp.concatenate(parts + parts, axis=1)
    own = rows.shape[1]
    return lax.dynamic_slice_in_dim(twice, ((size - me) % size) * own, size * own, 1)


def attend(qkv, tables, allowed):
    rows = qkv.shape[0]
    length = allowed.shape[-1]
    seqs = rows // length
    width = qkv.shape[1] // 3
    heads = width // HD
    shape = (seqs, length, heads, HD)
    queries = rotate(qkv[:, :width].reshape(shape), *tables).astype(BF)
    keys = rotate(qkv[:, width : 2 * width].reshape(shape), *tables).astype(BF)
    values = qkv[:, 2 * width :].astype(BF).reshape(shape)
    scores = jnp.einsum("bqhd,bkhd->bhqk", queries, keys, preferred_element_type=F32) * HD**-0.5
    scores = jnp.where(allowed[:, None], scores, -1e30)
    peak = jnp.max(scores, axis=-1, keepdims=True)
    raw = jnp.exp(scores - peak)
    total = jnp.sum(raw, axis=-1, keepdims=True)
    probs = (raw / total).astype(BF)
    context = jnp.einsum("bhqk,bkhd->bqhd", probs, values, preferred_element_type=F32).astype(BF)
    return context.reshape(rows, width), (queries, keys, values, peak + jnp.log(total))


def attend_back(saved, grad_context, tables, allowed):
    queries, keys, values, lse = saved
    shape = queries.shape
    grad_context = grad_context.reshape(shape)
    scale = HD**-0.5
    scores = jnp.einsum("bqhd,bkhd->bhqk", queries, keys, preferred_element_type=F32) * scale
    scores = jnp.where(allowed[:, None], scores, -1e30)
    probs = jnp.exp(scores - lse)
    grad_values = jnp.einsum(
        "bhqk,bqhd->bkhd", probs.astype(BF), grad_context, preferred_element_type=F32
    ).astype(BF)
    grad_probs = jnp.einsum("bqhd,bkhd->bhqk", grad_context, values, preferred_element_type=F32)
    inner = jnp.sum(probs * grad_probs, axis=-1, keepdims=True)
    grad_scores = (probs * (grad_probs - inner)).astype(BF)
    grad_queries = (
        jnp.einsum("bhqk,bkhd->bqhd", grad_scores, keys, preferred_element_type=F32) * scale
    )
    grad_keys = (
        jnp.einsum("bhqk,bqhd->bkhd", grad_scores, queries, preferred_element_type=F32) * scale
    )
    cos_table, sin_table = tables
    rows = shape[0] * shape[1]
    return jnp.concatenate(
        [
            rotate(grad_queries, cos_table, -sin_table).astype(BF).reshape(rows, -1),
            rotate(grad_keys, cos_table, -sin_table).astype(BF).reshape(rows, -1),
            grad_values.reshape(rows, -1),
        ],
        axis=1,
    )


def per_device(
    layer_input,
    gain_attn,
    w_query,
    w_key,
    w_value,
    w_out,
    gain_mlp,
    w_gate,
    w_up,
    w_down,
    segments,
    attn_route,
    attn_gate,
    mlp_route,
    mlp_gate,
    cotangent,
):
    length = layer_input.shape[0]
    size = lax.axis_size("rep")
    me = lax.axis_index("rep")
    block = w_query.shape[1] // size
    hidden_block = w_gate.shape[1] // size
    offsets = chip_offsets()

    def columns(weight, width):
        return lax.dynamic_slice_in_dim(weight, me * width, width, 1)

    def rows_of(weight, height):
        return lax.dynamic_slice_in_dim(weight, me * height, height, 0)

    own_qkv = jnp.concatenate([columns(w, block) for w in (w_query, w_key, w_value)], axis=1)
    own_qkv = lax.all_gather(own_qkv, "shard", axis=0, tiled=True)
    own_out = lax.all_gather(rows_of(w_out, block), "shard", axis=1, tiled=True)
    qkv_w = gather_chips(own_qkv)
    out_w = gather_chips(own_out)
    gate_up = jnp.concatenate([columns(w_gate, hidden_block), columns(w_up, hidden_block)], axis=1)
    gate_up = lax.all_gather(gate_up, "shard", axis=0, tiled=True)
    down = lax.all_gather(rows_of(w_down, hidden_block), "shard", axis=1, tiled=True)

    gains = gather_vector(jnp.stack([gain_attn, gain_mlp])).astype(F32)
    gain_one, gain_two = gains[0], gains[1]

    table, mix = plan_slots(mlp_route, mlp_gate)
    pick = table.astype(BF)
    upstream = cotangent.astype(F32)
    slot_weight = jnp.sum(jnp.where(table, mix[None, :], 0.0), axis=1)[:, None]
    slot_grad = (mm(pick, cotangent) * slot_weight).astype(BF)
    all_slot_grad = gather_plane(slot_grad)

    inputs = layer_input.astype(F32)
    root_one = lax.rsqrt(jnp.mean(inputs * inputs, axis=-1, keepdims=True) + EPSILON)
    normed = (inputs * root_one * gain_one).astype(BF)
    both = jnp.concatenate([normed, swap(normed, 1)], axis=0)
    seg = jnp.concatenate([segments, swap(segments, 1)], axis=0)
    ids = jnp.arange(length, dtype=jnp.int32)
    distance = ids[:, None] - ids[None, :]
    near = (distance >= 0) & (distance < WIN)
    allowed = (seg[:, :, None] == seg[:, None, :]) & near[None]
    tables = rotary_tables(length)
    context, saved = {}, {}
    for d in offsets:
        context[d], saved[d] = attend(mm(both, qkv_w[d]), tables, allowed)
    all_context = jnp.concatenate([context[d] for d in offsets], axis=1)
    all_out = jnp.concatenate([out_w[d] for d in offsets], axis=0)
    projected = mm(all_context, all_out)
    projected = projected[:length] + swap(projected[length:].astype(BF), 1).astype(F32)
    attn_weight = jnp.sum(jnp.where(attn_route == 0, attn_gate, 0.0), axis=-1)[:, None]
    hidden = inputs + projected * attn_weight
    root_two = lax.rsqrt(jnp.mean(hidden * hidden, axis=-1, keepdims=True) + EPSILON)
    normed_two = (hidden * root_two * gain_two).astype(BF)

    dispatched = gather_plane(mm(pick, normed_two).astype(BF))
    act = mm(dispatched, gate_up)
    gate_act, up_act = act[:, :hidden_block], act[:, hidden_block:]
    sigmoid = jax.nn.sigmoid(gate_act)
    silu = gate_act * sigmoid
    inner = (silu * up_act).astype(BF)
    grad_inner = mm_nt(all_slot_grad, down)
    grad_gate_act = (grad_inner * up_act * sigmoid * (1.0 + gate_act * (1.0 - sigmoid))).astype(BF)
    grad_up_act = (grad_inner * silu).astype(BF)
    grad_act = jnp.concatenate([grad_gate_act, grad_up_act], axis=1)
    grad_disp = scatter_plane(mm_nt(grad_act, gate_up).astype(BF)).astype(BF)
    expert_out = scatter_plane(mm(inner, down).astype(BF)).astype(BF)
    output = (hidden + mm_tn(pick, expert_out) * mix[:, None]).astype(BF)
    grad_gate_up = mm_tn(dispatched, grad_act).astype(BF)
    grad_down = mm_tn(inner, all_slot_grad).astype(BF)

    grad_normed_two = mm_tn(pick, grad_disp)
    grad_gain_two, through = norm_back(grad_normed_two, hidden, root_two, gain_two)
    grad_hidden = upstream + through

    grad_projected = (grad_hidden * attn_weight).astype(BF)
    both_grad = jnp.concatenate([grad_projected, swap(grad_projected, 1)], axis=0)
    grad_out_w = mm_tn(all_context, both_grad).astype(BF)
    grad_context = mm_nt(both_grad, all_out).astype(BF)
    grad_lin = {
        d: attend_back(saved[d], grad_context[:, i * block : (i + 1) * block], tables, allowed)
        for i, d in enumerate(offsets)
    }
    grad_qkv_w = {d: mm_tn(both, grad_lin[d]).astype(BF) for d in offsets}
    grad_normed = sum(mm_nt(grad_lin[d], qkv_w[d]) for d in offsets)
    grad_normed = grad_normed[:length] + swap(grad_normed[length:].astype(BF), 1).astype(F32)
    grad_gain_one, first = norm_back(grad_normed, inputs, root_one, gain_one)
    grad_input = (grad_hidden + first).astype(BF)

    def spread(value, axis):
        return lax.all_gather(value, "rep", axis=axis, tiled=True).astype(F32)

    sum_gu = lax.psum_scatter(grad_gate_up, "shard", scatter_dimension=0, tiled=True)
    sum_down = lax.psum_scatter(grad_down, "shard", scatter_dimension=1, tiled=True)
    own_grad_out = scatter_chips(
        {d: grad_out_w[i * block : (i + 1) * block] for i, d in enumerate(offsets)}
    ).astype(BF)
    sum_out = lax.psum_scatter(own_grad_out, "shard", scatter_dimension=1, tiled=True)
    own_grad_qkv = scatter_chips(grad_qkv_w).astype(BF)
    sum_qkv = lax.psum_scatter(own_grad_qkv, "shard", scatter_dimension=0, tiled=True)
    grad_gate = spread(sum_gu[:, :hidden_block], 1)
    grad_up = spread(sum_gu[:, hidden_block:], 1)
    grad_down = spread(sum_down, 0)
    grad_out = spread(sum_out, 0)
    grad_query, grad_key, grad_value = (
        spread(sum_qkv[:, i * block : (i + 1) * block], 1) for i in range(3)
    )
    gain_grads = lax.psum(jnp.stack([grad_gain_one, grad_gain_two]), ("rep", "shard"))
    own = gain_attn.shape[0]
    gain_grads = lax.dynamic_slice_in_dim(gain_grads, lax.axis_index("shard") * own, own, 1)
    return (
        output,
        grad_input,
        gain_grads[0],
        grad_query,
        grad_key,
        grad_value,
        grad_out,
        gain_grads[1],
        grad_gate,
        grad_up,
        grad_down,
    )


def solution(mesh):
    tokens = P(("rep", "shard"), None)
    tall, wide, vector = P("shard", None), P(None, "shard"), P("shard")
    weights = (vector, tall, tall, tall, wide, vector, tall, tall, wide)
    return jax.shard_map(
        per_device,
        mesh=mesh,
        in_specs=(tokens, *weights) + (tokens,) * 6,
        out_specs=(tokens, tokens, *weights),
        check_vma=False,
    )
```

time: 3150 us -> 1190 us (0.38)
  waiting for transfers between devices: 2670 us -> 592 us
  local copies, waits for them, and re-layouts: 46.8 us -> 180 us
  starting transfers between devices: 0.67 us -> 52.3 us
    all_gather x12 -> x11, waiting for transfers between devices: 1840 us -> 203 us  [the longest x7 90.6 us: spread(): return lax.all_gather(value, 'rep', axis=axis, tiled=True).astype(F32)]
    reduce_scatter x4, waiting for transfers between devices: 581 us -> 148 us  [the longest x1 102 us: per_device(): lax.psum_scatter(grad_gate_up, 'shard', scatter_dimension=0, tiled=True)]
    psum x1 -> x0, waiting for transfers between devices: 250 us -> none  [per_device(): lax.psum(attn_parts[0].astype(jnp.bfloat16), 'rep').astype(jnp.float32)]
    ppermute x0 -> x52, waiting for transfers between devices: none -> 238 us  [the longest x49 238 us: swap(): return lax.ppermute(value, 'rep', [(i, i ^ bit) for i in range(size)])]
    slice x2 -> x41, local copies, waits for them, and re-layouts: 4.75 us -> 62.8 us  [the longest x8 24.9 us: rotate(): first, second = (values[..., :half], values[..., half:])]
    ppermute x0 -> x52, starting transfers between devices: none -> 51.7 us  [the longest x49 45.6 us: swap(): return lax.ppermute(value, 'rep', [(i, i ^ bit) for i in range(size)])]
    dot_general x27 -> x49, matrix products: 252 us -> 222 us  [the longest x9 59.7 us: mm_tn(): lax.dot_general(left, right, (((0,), (0,)), ((), ())), preferred_element_...]
  transfers between devices with their start and end apart: 17 -> 67, of which waited for: 15 -> 40; matrix products, arithmetic and copies ran while one was open for 11% -> 36% of each run, Pallas kernels for 0% -> 0%
where the time goes in v1:
time: 1190 us
  waiting for transfers between devices  592 us (50%)
  matrix products  222 us (19%)
  local copies, waits for them, and re-layouts  180 us (15%)
  other arithmetic  85.9 us (7%)
  starting transfers between devices  52.3 us (4%)
  blocking collectives  39.9 us (3%)
  between operations  16.3 us (1%)
    ppermute x49, waiting for transfers between devices, swap(): return lax.ppermute(value, 'rep', [(i, i ^ bit) for i in range(size)])  238 us
    reduce_scatter x1, waiting for transfers between devices, per_device(): lax.psum_scatter(grad_gate_up, 'shard', scatter_dimension=0, tiled=True)  102 us
    all_gather x7, waiting for transfers between devices, spread(): return lax.all_gather(value, 'rep', axis=axis, tiled=True).astype(F32)  90.6 us
    dot_general x9, matrix products, mm_tn(): lax.dot_general(left, right, (((0,), (0,)), ((), ())), preferred_element_...  59.7 us
    dot_general x7, matrix products, mm_nt(): lax.dot_general(left, right, (((1,), (1,)), ((), ())), preferred_element_...  59.5 us
    all_gather x1, waiting for transfers between devices, per_device(): own_qkv = lax.all_gather(own_qkv, 'shard', axis=0, tiled=True)  57.4 us
    dot_general x9, matrix products, mm(): return jnp.dot(left, right, preferred_element_type=F32)  54.5 us
    unnamed x308, local copies, waits for them, and re-layouts  49.1 us
  transfers between devices with their start and end apart: 67, of which 40 were waited for; matrix products, arithmetic and copies ran while one was open for 36% of the time, Pallas kernels for 0%

profile of v1, /device:TPU:0, one launch (start us, length us, event | category | flops | bytes accessed | tf_op | source)
XLA Modules:
  0.0 1188.0 jit_solution(6927684167405556137)
XLA Ops:
  12.8 5.1 collective-permute-start
  25.8 15.1 %all-gather.14.cloned.1.call-done = bf16[256,2048]{1,0:T(8,128)(2,1)} async-done(((bf16[256,512]{1,0:T(8,128)(2,1)}), bf16[256,2048]{1,0:T(8,128)(2,1)}) %all-gather.14.cloned.1.call-update) | async-done | bytes 1048592 | tf_op jit(solution)/shard_map/all_gather | solution.py:229
  48.7 57.4 %all-gather.12.cloned.1.call-done = bf16[2048,768]{1,0:T(8,128)(2,1)} async-done(((bf16[512,768]{1,0:T(8,128)(2,1)}), bf16[2048,768]{1,0:T(8,128)(2,1)}) %all-gather.12.cloned.1.call-update) | async-done | bytes 3145744 | tf_op jit(solution)/shard_map/all_gather | solution.py:228
  117.0 7.0 collective-permute-done.11
  124.0 63.3 %collective-permute-done.12 = bf16[128,2048]{1,0:T(8,128)(2,1)S(1)} collective-permute-done((bf16[128,2048]{1,0:T(8,128)(2,1)S(1)}, bf16[128,2048]{1,0:T(8,128)(2,1)S(1)}, u32[]{:S(2)}, u32[]{:S(2)}) %collective-permute-start.12) | collective-permute-done | bytes 524320 | tf_op jit(solution)/shard_map/ppermute | solution.py:29
  189.4 6.6 fusion.151
  203.8 4.1 fusion.169
  214.4 6.6 fusion.150
  221.0 8.6 fusion.149
  254.1 4.1 fusion.166
  270.7 6.8 fusion.148
  282.7 4.0 fusion.162
  292.3 7.5 subtract_convert_fusion.9
  333.1 4.5 fusion.177
  342.6 11.5 collective-permute-done.26
  364.9 8.4 collective-permute-done.14
  389.3 12.3 %fusion.178 = f32[1024,1408]{1,0:T(8,128)} fusion(bf16[1024,2048]{1,0:T(8,128)(2,1)} %constant_dynamic-update-slice_fusion.20, bf16[2048,1408]{1,0:T(8,128)(2,1)} %all-gather.16.cloned.1.call-done), kind=kOutput, calls=%fused_computation.378 | convolution fusion | flops 5905580032 | bytes 15728640 | tf_op jit(solution)/shard_map/dot_general | solution.py:16
  401.6 40.2 %all-gather.18.cloned.1.call-done = bf16[704,2048]{1,0:T(8,128)(2,1)} async-done(((bf16[704,512]{1,0:T(8,128)(2,1)}), bf16[704,2048]{1,0:T(8,128)(2,1)}) %all-gather.18.cloned.1.call-update) | async-done | bytes 2883600 | tf_op jit(solution)/shard_map/all_gather | solution.py:234
  441.8 10.3 multiply_convert_fusion.7
  452.1 7.0 convolution_convert_fusion.1
  459.3 4.1 collective-permute-done.31
  468.5 5.1 collective-permute-done.35
  490.3 4.2 collective-permute-done.38
  495.7 5.1 convolution_convert_fusion.3
  505.1 10.7 collective-permute-done.49
  519.9 7.2 collective-permute-done.46
  527.7 9.9 collective-permute-done.48
  539.5 7.6 convolution_convert_fusion.8
  547.1 7.3 fusion.40
  575.2 3.5 multiply_reduce_fusion.2
  585.8 3.6 multiply_reduce_fusion.1
  608.0 4.3 subtract_convert_fusion.7
  614.8 6.3 convolution_convert_fusion.5
  626.2 8.0 convolution_convert_fusion.6
  642.6 6.2 convolution_convert_fusion.4
  650.6 10.1 collective-permute-done.41
  673.1 22.7 %collective-permute-done.40 = bf16[1024,768]{1,0:T(8,128)(2,1)} collective-permute-done((bf16[1024,768]{1,0:T(8,128)(2,1)}, bf16[1024,768]{1,0:T(8,128)(2,1)}, u32[]{:S(2)}, u32[]{:S(2)}) %collective-permute-start.40) | collective-permute-done | bytes 1572896 | tf_op jit(solution)/shard_map/ppermute | solution.py:29
  695.8 31.6 %collective-permute-done.42 = bf16[1024,768]{1,0:T(8,128)(2,1)} collective-permute-done((bf16[1024,768]{1,0:T(8,128)(2,1)}, bf16[1024,768]{1,0:T(8,128)(2,1)}, u32[]{:S(2)}, u32[]{:S(2)}) %collective-permute-start.42) | collective-permute-done | bytes 1572896 | tf_op jit(solution)/shard_map/ppermute | solution.py:29
  727.4 9.3 add_convert_fusion
  736.9 10.9 convolution_convert_fusion
  749.2 46.1 %reduce-scatter.5.cloned.1.call-done = bf16[512,768]{1,0:T(8,128)(2,1)} async-done(((bf16[2048,768]{1,0:T(8,128)(2,1)}), bf16[512,768]{1,0:T(8,128)(2,1)}) %reduce-scatter.5.cloned.1.call-update) | async-done | bytes 786448 | tf_op jit(solution)/shard_map/reduce_scatter | solution.py:312
  798.7 101.9 %reduce-scatter.9.cloned.1.call-done = bf16[512,1408]{1,0:T(8,128)(2,1)} async-done(((bf16[2048,1408]{1,0:T(8,128)(2,1)}), bf16[512,1408]{1,0:T(8,128)(2,1)}) %reduce-scatter.9.cloned.1.call-update) | async-done | bytes 1441808 | tf_op jit(solution)/shard_map/reduce_scatter | solution.py:305
  904.8 5.7 convolution_convert_fusion.2
  914.4 7.8 fusion.181
  922.2 7.7 fusion.179
  929.9 7.7 fusion.180
  937.6 11.8 add_add_fusion
  962.2 10.7 collective-permute-done.23
  977.2 6.9 collective-permute-done.20
  985.6 5.8 collective-permute-done.22
  991.4 4.5 add_convert_fusion.2
  995.9 4.3 fusion.9
  1000.2 39.9 %psum.7 = f32[2,2048]{1,0:T(2,128)S(1)} all-reduce(f32[2,2048]{1,0:T(2,128)S(1)} %pad_maximum_fusion.43), channel_id=1, replica_groups=mesh['rep'=8,'shard'=4] {'rep','shard'}, use_global_device_ids=true, to_apply=%region_23.24 | all-reduce | flops 4096 | bytes 32768 | tf_op jit(solution)/shard_map/psum | solution.py:320
  1040.8 6.1 fusion.6
  1046.9 4.2 convert_element_type.485
  1051.2 8.7 convert_element_type.490
  1059.9 4.2 convert_element_type.471
  1064.1 4.1 convert_element_type.472
  1068.2 13.3 %all-gather.24.cloned.1.call-done = bf16[512,2048]{1,0:T(8,128)(2,1)} async-done(((bf16[512,256]{1,0:T(8,128)(2,1)}), bf16[512,2048]{1,0:T(8,128)(2,1)}) %all-gather.24.cloned.1.call-update) | async-done | bytes 2097168 | tf_op jit(solution)/shard_map/all_gather | solution.py:303
  1081.5 4.1 convert_element_type.473
  1085.6 41.1 %all-gather.28.cloned.1.call-done = bf16[512,5632]{0,1:T(8,128)(2,1)} async-done(((bf16[512,704]{0,1:T(8,128)(2,1)}), bf16[512,5632]{0,1:T(8,128)(2,1)}) %all-gather.28.cloned.1.call-update) | async-done | bytes 5767184 | tf_op jit(solution)/shard_map/all_gather | solution.py:303
  1126.8 9.1 copy.333
  1135.8 36.2 %all-gather.30.cloned.1.call-done = bf16[512,5632]{0,1:T(8,128)(2,1)} async-done(((bf16[512,704]{0,1:T(8,128)(2,1)}), bf16[512,5632]{0,1:T(8,128)(2,1)}) %all-gather.30.cloned.1.call-update) | async-done | bytes 5767184 | tf_op jit(solution)/shard_map/all_gather | solution.py:303
  1172.0 9.2 copy.334
  (601 shorter events, 302.7 us)
Async XLA Ops:
  7.2 33.6 %all-gather.14.cloned.1.call-start = ((), (), s32[]{:S(2)}) async-start(), calls=%async_computation.5 | async-start | bytes 1310720 | tf_op jit(solution)/shard_map/all_gather | solution.py:229
  9.5 96.5 %all-gather.12.cloned.1.call-start = ((), (), s32[]{:S(2)}) async-start(), calls=%async_computation.4 | async-start | bytes 3932160 | tf_op jit(solution)/shard_map/all_gather | solution.py:228
  12.7 376.6 %all-gather.16.cloned.1.call-start = ((), (), s32[]{:S(2)}) async-start(), calls=%async_computation.6 | async-start | bytes 7208960 | tf_op jit(solution)/shard_map/all_gather | solution.py:233
  12.8 10.4 collective-permute-start
  17.9 5.3 collective-permute-start.1
  17.9 5.5 collective-permute-start.2
  18.9 88.6 %collective-permute-start.4 = (s32[1,512]{1,0:T(1,128)S(1)}, s32[1,512]{1,0:T(1,128)S(1)}, u32[]{:S(2)}, u32[]{:S(2)}) collective-permute-start(s32[1,512]{1,0:T(1,128)S(1)} %copy-done.131), channel_id=1, source_target_pairs={{0,4},{4,0},{8,12},{12,8},{16,20},{20,16},{24,28},{28,24},{1,5},{5... | collective-permute-start | bytes 6152 | tf_op jit(solution)/shard_map/ppermute | solution.py:29
  25.4 164.0 %collective-permute-start.3 = (bf16[512,2048]{1,0:T(8,128)(2,1)}, bf16[512,2048]{1,0:T(8,128)(2,1)}, u32[]{:S(2)}, u32[]{:S(2)}) collective-permute-start(bf16[512,2048]{1,0:T(8,128)(2,1)} %fusion.2), channel_id=1, source_target_pairs={{0,4},{4,0},{8,12},{12,8},{16,20},{20,16},{24,28},{28,24},{1,5},{5... | collective-permute-start | bytes 6291464 | tf_op jit(solution)/shard_map/ppermute | solution.py:29
  40.9 67.1 %collective-permute-start.9 = (bf16[256,2048]{1,0:T(8,128)(2,1)}, bf16[256,2048]{1,0:T(8,128)(2,1)}, u32[]{:S(2)}, u32[]{:S(2)}) collective-permute-start(bf16[256,2048]{1,0:T(8,128)(2,1)} %all-gather.14.cloned.1.call-done), channel_id=1, source_target_pairs={{0,8},{4,12},{8,0},{12,4},{16,24},{20,28},{24,16},{28,20},{1,9},{5... | collective-permute-start | bytes 3145736 | tf_op jit(solution)/shard_map/ppermute | solution.py:29
  45.0 396.7 %all-gather.18.cloned.1.call-start = ((), (), s32[]{:S(2)}) async-start(), calls=%async_computation.7 | async-start | bytes 3604480 | tf_op jit(solution)/shard_map/all_gather | solution.py:234
  45.1 66.8 %collective-permute-start.10 = (bf16[256,2048]{1,0:T(8,128)(2,1)}, bf16[256,2048]{1,0:T(8,128)(2,1)}, u32[]{:S(2)}, u32[]{:S(2)}) collective-permute-start(bf16[256,2048]{1,0:T(8,128)(2,1)} %all-gather.14.cloned.1.call-done), channel_id=1, source_target_pairs={{0,16},{4,20},{8,24},{12,28},{16,0},{20,4},{24,8},{28,12},{1,17},{... | collective-permute-start | bytes 3145736 | tf_op jit(solution)/shard_map/ppermute | solution.py:29
  106.0 104.2 %collective-permute-start.5 = (bf16[2048,768]{1,0:T(8,128)(2,1)}, bf16[2048,768]{1,0:T(8,128)(2,1)}, u32[]{:S(2)}, u32[]{:S(2)}) collective-permute-start(bf16[2048,768]{1,0:T(8,128)(2,1)} %all-gather.12.cloned.1.call-done), channel_id=1, source_target_pairs={{0,8},{4,12},{8,0},{12,4},{16,24},{20,28},{24,16},{28,20},{1,9},{5... | collective-permute-start | bytes 9437192 | tf_op jit(solution)/shard_map/ppermute | solution.py:29
  109.1 14.9 %collective-permute-start.11 = (bf16[128,2048]{1,0:T(8,128)(2,1)S(1)}, bf16[128,2048]{1,0:T(8,128)(2,1)S(1)}, u32[]{:S(2)}, u32[]{:S(2)}) collective-permute-start(bf16[128,2048]{1,0:T(8,128)(2,1)S(1)} %slice.472), channel_id=1, source_target_pairs={{0,16},{4,20},{8,24},{12,28},{16,0},{20,4},{24,8},{28,12},{1,17},{... | collective-permute-start | bytes 1572872 | tf_op jit(solution)/shard_map/ppermute | solution.py:29
  113.0 74.2 %collective-permute-start.12 = (bf16[128,2048]{1,0:T(8,128)(2,1)S(1)}, bf16[128,2048]{1,0:T(8,128)(2,1)S(1)}, u32[]{:S(2)}, u32[]{:S(2)}) collective-permute-start(bf16[128,2048]{1,0:T(8,128)(2,1)S(1)} %slice.473), channel_id=1, source_target_pairs={{0,8},{4,12},{8,0},{12,4},{16,24},{20,28},{24,16},{28,20},{1,9},{5... | collective-permute-start | bytes 1572872 | tf_op jit(solution)/shard_map/ppermute | solution.py:29
  115.0 106.0 %collective-permute-start.6 = (bf16[2048,768]{1,0:T(8,128)(2,1)}, bf16[2048,768]{1,0:T(8,128)(2,1)}, u32[]{:S(2)}, u32[]{:S(2)}) collective-permute-start(bf16[2048,768]{1,0:T(8,128)(2,1)} %all-gather.12.cloned.1.call-done), channel_id=1, source_target_pairs={{0,16},{4,20},{8,24},{12,28},{16,0},{20,4},{24,8},{28,12},{1,17},{... | collective-permute-start | bytes 9437192 | tf_op jit(solution)/shard_map/ppermute | solution.py:29
  212.9 52.7 %collective-permute-start.7 = (bf16[1024,768]{1,0:T(8,128)(2,1)}, bf16[1024,768]{1,0:T(8,128)(2,1)}, u32[]{:S(2)}, u32[]{:S(2)}) collective-permute-start(bf16[1024,768]{1,0:T(8,128)(2,1)} %slice.463), channel_id=1, source_target_pairs={{0,16},{4,20},{8,24},{12,28},{16,0},{20,4},{24,8},{28,12},{1,17},{... | collective-permute-start | bytes 4718600 | tf_op jit(solution)/shard_map/ppermute | solution.py:29
  233.8 35.3 %collective-permute-start.8 = (bf16[1024,768]{1,0:T(8,128)(2,1)}, bf16[1024,768]{1,0:T(8,128)(2,1)}, u32[]{:S(2)}, u32[]{:S(2)}) collective-permute-start(bf16[1024,768]{1,0:T(8,128)(2,1)} %slice.464), channel_id=1, source_target_pairs={{0,8},{4,12},{8,0},{12,4},{16,24},{20,28},{24,16},{28,20},{1,9},{5... | collective-permute-start | bytes 4718600 | tf_op jit(solution)/shard_map/ppermute | solution.py:29
  338.0 19.1 %collective-permute-start.13 = (bf16[512,2048]{1,0:T(8,128)(2,1)S(1)}, bf16[512,2048]{1,0:T(8,128)(2,1)S(1)}, u32[]{:S(2)}, u32[]{:S(2)}) collective-permute-start(bf16[512,2048]{1,0:T(8,128)(2,1)S(1)} %slice.619), channel_id=1, source_target_pairs={{0,4},{4,0},{8,12},{12,8},{16,20},{20,16},{24,28},{28,24},{1,5},{5... | collective-permute-start | bytes 6291464 | tf_op jit(solution)/shard_map/ppermute | solution.py:29
  340.5 13.6 %collective-permute-start.26 = (bf16[128,2048]{1,0:T(8,128)(2,1)S(1)}, bf16[128,2048]{1,0:T(8,128)(2,1)S(1)}, u32[]{:S(2)}, u32[]{:S(2)}) collective-permute-start(bf16[128,2048]{1,0:T(8,128)(2,1)S(1)} %get-tuple-element.198), channel_id=1, source_target_pairs={{0,8},{4,12},{8,0},{12,4},{16,24},{20,28},{24,16},{28,20},{1,9},{5... | collective-permute-start | bytes 1572872 | tf_op jit(solution)/shard_map/ppermute | solution.py:29
  342.0 13.3 %collective-permute-start.27 = (bf16[128,2048]{1,0:T(8,128)(2,1)S(1)}, bf16[128,2048]{1,0:T(8,128)(2,1)S(1)}, u32[]{:S(2)}, u32[]{:S(2)}) collective-permute-start(bf16[128,2048]{1,0:T(8,128)(2,1)S(1)} %get-tuple-element.198), channel_id=1, source_target_pairs={{0,16},{4,20},{8,24},{12,28},{16,0},{20,4},{24,8},{28,12},{1,17},{... | collective-permute-start | bytes 1572872 | tf_op jit(solution)/shard_map/ppermute | solution.py:29
  354.1 9.3 collective-permute-start.28
  355.3 8.9 collective-permute-start.29
  360.5 12.8 %collective-permute-start.14 = (bf16[128,2048]{1,0:T(8,128)(2,1)S(1)}, bf16[128,2048]{1,0:T(8,128)(2,1)S(1)}, u32[]{:S(2)}, u32[]{:S(2)}) collective-permute-start(bf16[128,2048]{1,0:T(8,128)(2,1)S(1)} %get-tuple-element.199), channel_id=1, source_target_pairs={{0,8},{4,12},{8,0},{12,4},{16,24},{20,28},{24,16},{28,20},{1,9},{5... | collective-permute-start | bytes 1572872 | tf_op jit(solution)/shard_map/ppermute | solution.py:29
  361.6 12.8 %collective-permute-start.15 = (bf16[128,2048]{1,0:T(8,128)(2,1)S(1)}, bf16[128,2048]{1,0:T(8,128)(2,1)S(1)}, u32[]{:S(2)}, u32[]{:S(2)}) collective-permute-start(bf16[128,2048]{1,0:T(8,128)(2,1)S(1)} %get-tuple-element.199), channel_id=1, source_target_pairs={{0,16},{4,20},{8,24},{12,28},{16,0},{20,4},{24,8},{28,12},{1,17},{... | collective-permute-start | bytes 1572872 | tf_op jit(solution)/shard_map/ppermute | solution.py:29
  364.9 18.8 %collective-permute-start.30 = (bf16[512,2048]{1,0:T(8,128)(2,1)}, bf16[512,2048]{1,0:T(8,128)(2,1)S(1)}, u32[]{:S(2)}, u32[]{:S(2)}) collective-permute-start(bf16[512,2048]{1,0:T(8,128)(2,1)} %get-tuple-element.171), channel_id=1, source_target_pairs={{0,4},{4,0},{8,12},{12,8},{16,20},{20,16},{24,28},{28,24},{1,5},{5... | collective-permute-start | bytes 6291464 | tf_op jit(solution)/shard_map/ppermute | solution.py:29
  373.3 6.4 collective-permute-start.16
  374.4 6.4 collective-permute-start.17
  383.7 364.2 %reduce-scatter.7.cloned.1.call-start = ((), (), s32[]{:S(2)}) async-start(), calls=%async_computation.12 | async-start | bytes 1310720 | tf_op jit(solution)/shard_map/reduce_scatter | solution.py:310
  464.4 9.2 collective-permute-start.35
  465.9 9.2 collective-permute-start.33
  467.4 11.8 collective-permute-start.32
  467.9 12.8 %collective-permute-start.37 = (bf16[64,2048]{1,0:T(8,128)(2,1)S(1)}, bf16[64,2048]{1,0:T(8,128)(2,1)S(1)}, u32[]{:S(2)}, u32[]{:S(2)}) collective-permute-start(bf16[64,2048]{1,0:T(8,128)(2,1)S(1)} %get-tuple-element.87), channel_id=1, source_target_pairs={{0,16},{4,20},{8,24},{12,28},{16,0},{20,4},{24,8},{28,12},{1,17},{... | collective-permute-start | bytes 786440 | tf_op jit(solution)/shard_map/ppermute | solution.py:29
  475.2 8.8 collective-permute-start.34
  475.8 9.4 collective-permute-start.36
  501.0 14.8 %collective-permute-start.49 = (bf16[128,2048]{1,0:T(8,128)(2,1)S(1)}, bf16[128,2048]{1,0:T(8,128)(2,1)S(1)}, u32[]{:S(2)}, u32[]{:S(2)}) collective-permute-start(bf16[128,2048]{1,0:T(8,128)(2,1)S(1)} %get-tuple-element.50), channel_id=1, source_target_pairs={{0,8},{4,12},{8,0},{12,4},{16,24},{20,28},{24,16},{28,20},{1,9},{5... | collective-permute-start | bytes 1572872 | tf_op jit(solution)/shard_map/ppermute | solution.py:29
  501.6 14.8 %collective-permute-start.47 = (bf16[128,2048]{1,0:T(8,128)(2,1)S(1)}, bf16[128,2048]{1,0:T(8,128)(2,1)S(1)}, u32[]{:S(2)}, u32[]{:S(2)}) collective-permute-start(bf16[128,2048]{1,0:T(8,128)(2,1)S(1)} %get-tuple-element.52), channel_id=1, source_target_pairs={{0,16},{4,20},{8,24},{12,28},{16,0},{20,4},{24,8},{28,12},{1,17},{... | collective-permute-start | bytes 1572872 | tf_op jit(solution)/shard_map/ppermute | solution.py:29
  503.1 24.0 %collective-permute-start.46 = (bf16[128,2048]{1,0:T(8,128)(2,1)S(1)}, bf16[128,2048]{1,0:T(8,128)(2,1)S(1)}, u32[]{:S(2)}, u32[]{:S(2)}) collective-permute-start(bf16[128,2048]{1,0:T(8,128)(2,1)S(1)} %get-tuple-element.53), channel_id=1, source_target_pairs={{0,8},{4,12},{8,0},{12,4},{16,24},{20,28},{24,16},{28,20},{1,9},{5... | collective-permute-start | bytes 1572872 | tf_op jit(solution)/shard_map/ppermute | solution.py:29
  504.6 23.1 %collective-permute-start.51 = (bf16[128,2048]{1,0:T(8,128)(2,1)S(1)}, bf16[128,2048]{1,0:T(8,128)(2,1)S(1)}, u32[]{:S(2)}, u32[]{:S(2)}) collective-permute-start(bf16[128,2048]{1,0:T(8,128)(2,1)S(1)} %get-tuple-element.51), channel_id=1, source_target_pairs={{0,16},{4,20},{8,24},{12,28},{16,0},{20,4},{24,8},{28,12},{1,17},{... | collective-permute-start | bytes 1572872 | tf_op jit(solution)/shard_map/ppermute | solution.py:29
  516.8 20.7 %collective-permute-start.48 = (bf16[128,2048]{1,0:T(8,128)(2,1)S(1)}, bf16[128,2048]{1,0:T(8,128)(2,1)S(1)}, u32[]{:S(2)}, u32[]{:S(2)}) collective-permute-start(bf16[128,2048]{1,0:T(8,128)(2,1)S(1)} %get-tuple-element.49), channel_id=1, source_target_pairs={{0,8},{4,12},{8,0},{12,4},{16,24},{20,28},{24,16},{28,20},{1,9},{5... | collective-permute-start | bytes 1572872 | tf_op jit(solution)/shard_map/ppermute | solution.py:29
  518.4 19.4 %collective-permute-start.50 = (bf16[128,2048]{1,0:T(8,128)(2,1)S(1)}, bf16[128,2048]{1,0:T(8,128)(2,1)S(1)}, u32[]{:S(2)}, u32[]{:S(2)}) collective-permute-start(bf16[128,2048]{1,0:T(8,128)(2,1)S(1)} %get-tuple-element.48), channel_id=1, source_target_pairs={{0,16},{4,20},{8,24},{12,28},{16,0},{20,4},{24,8},{28,12},{1,17},{... | collective-permute-start | bytes 1572872 | tf_op jit(solution)/shard_map/ppermute | solution.py:29
  539.3 209.3 %reduce-scatter.11.cloned.1.call-start = ((), (), s32[]{:S(2)}) async-start(), calls=%async_computation.17 | async-start | bytes 3604480 | tf_op jit(solution)/shard_map/reduce_scatter | solution.py:306
  547.1 248.2 %reduce-scatter.5.cloned.1.call-start = ((), (), s32[]{:S(2)}) async-start(), calls=%async_computation.8 | async-start | bytes 3932160 | tf_op jit(solution)/shard_map/reduce_scatter | solution.py:312
  623.0 37.6 %collective-permute-start.41 = (bf16[1024,768]{1,0:T(8,128)(2,1)}, bf16[1024,768]{1,0:T(8,128)(2,1)}, u32[]{:S(2)}, u32[]{:S(2)}) collective-permute-start(bf16[1024,768]{1,0:T(8,128)(2,1)} %get-tuple-element.55), channel_id=1, source_target_pairs={{0,16},{4,20},{8,24},{12,28},{16,0},{20,4},{24,8},{28,12},{1,17},{... | collective-permute-start | bytes 4718600 | tf_op jit(solution)/shard_map/ppermute | solution.py:29
  624.5 40.8 %collective-permute-start.43 = (bf16[1024,768]{1,0:T(8,128)(2,1)}, bf16[1024,768]{1,0:T(8,128)(2,1)}, u32[]{:S(2)}, u32[]{:S(2)}) collective-permute-start(bf16[1024,768]{1,0:T(8,128)(2,1)} %get-tuple-element.54), channel_id=1, source_target_pairs={{0,8},{4,12},{8,0},{12,4},{16,24},{20,28},{24,16},{28,20},{1,9},{5... | collective-permute-start | bytes 4718600 | tf_op jit(solution)/shard_map/ppermute | solution.py:29
  640.3 55.5 %collective-permute-start.40 = (bf16[1024,768]{1,0:T(8,128)(2,1)}, bf16[1024,768]{1,0:T(8,128)(2,1)}, u32[]{:S(2)}, u32[]{:S(2)}) collective-permute-start(bf16[1024,768]{1,0:T(8,128)(2,1)} %slice.523), channel_id=1, source_target_pairs={{0,8},{4,12},{8,0},{12,4},{16,24},{20,28},{24,16},{28,20},{1,9},{5... | collective-permute-start | bytes 4718600 | tf_op jit(solution)/shard_map/ppermute | solution.py:29
  650.0 45.8 %collective-permute-start.45 = (bf16[1024,768]{1,0:T(8,128)(2,1)}, bf16[1024,768]{1,0:T(8,128)(2,1)}, u32[]{:S(2)}, u32[]{:S(2)}) collective-permute-start(bf16[1024,768]{1,0:T(8,128)(2,1)} %slice.528), channel_id=1, source_target_pairs={{0,16},{4,20},{8,24},{12,28},{16,0},{20,4},{24,8},{28,12},{1,17},{... | collective-permute-start | bytes 4718600 | tf_op jit(solution)/shard_map/ppermute | solution.py:29
  663.7 63.7 %collective-permute-start.42 = (bf16[1024,768]{1,0:T(8,128)(2,1)}, bf16[1024,768]{1,0:T(8,128)(2,1)}, u32[]{:S(2)}, u32[]{:S(2)}) collective-permute-start(bf16[1024,768]{1,0:T(8,128)(2,1)} %add_convert_fusion.5), channel_id=1, source_target_pairs={{0,8},{4,12},{8,0},{12,4},{16,24},{20,28},{24,16},{28,20},{1,9},{5... | collective-permute-start | bytes 4718600 | tf_op jit(solution)/shard_map/ppermute | solution.py:29
  668.4 59.1 %collective-permute-start.44 = (bf16[1024,768]{1,0:T(8,128)(2,1)}, bf16[1024,768]{1,0:T(8,128)(2,1)}, u32[]{:S(2)}, u32[]{:S(2)}) collective-permute-start(bf16[1024,768]{1,0:T(8,128)(2,1)} %add_convert_fusion.4), channel_id=1, source_target_pairs={{0,16},{4,20},{8,24},{12,28},{16,0},{20,4},{24,8},{28,12},{1,17},{... | collective-permute-start | bytes 4718600 | tf_op jit(solution)/shard_map/ppermute | solution.py:29
  736.8 163.8 %reduce-scatter.9.cloned.1.call-start = ((), (), s32[]{:S(2)}) async-start(), calls=%async_computation.14 | async-start | bytes 7208960 | tf_op jit(solution)/shard_map/reduce_scatter | solution.py:305
  747.8 299.1 %all-gather.26.cloned.1.call-start = ((), (), s32[]{:S(2)}) async-start(), calls=%async_computation.13 | async-start | bytes 2359296 | tf_op jit(solution)/shard_map/all_gather | solution.py:303
  748.6 302.6 %all-gather.32.cloned.1.call-start = ((), (), s32[]{:S(2)}) async-start(), calls=%async_computation.18 | async-start | bytes 6488064 | tf_op jit(solution)/shard_map/all_gather | solution.py:303
  749.1 310.7 %all-gather.20.cloned.1.call-start = ((), (), s32[]{:S(2)}) async-start(), calls=%async_computation.9 | async-start | bytes 2359296 | tf_op jit(solution)/shard_map/all_gather | solution.py:303
  797.3 266.8 %all-gather.22.cloned.1.call-start = ((), (), s32[]{:S(2)}) async-start(), calls=%async_computation.10 | async-start | bytes 2359296 | tf_op jit(solution)/shard_map/all_gather | solution.py:303
  797.9 283.6 %all-gather.24.cloned.1.call-start = ((), (), s32[]{:S(2)}) async-start(), calls=%async_computation.11 | async-start | bytes 2359296 | tf_op jit(solution)/shard_map/all_gather | solution.py:303
  798.7 328.1 %all-gather.28.cloned.1.call-start = ((), (), s32[]{:S(2)}) async-start(), calls=%async_computation.15 | async-start | bytes 6488064 | tf_op jit(solution)/shard_map/all_gather | solution.py:303
  903.6 268.4 %all-gather.30.cloned.1.call-start = ((), (), s32[]{:S(2)}) async-start(), calls=%async_computation.16 | async-start | bytes 6488064 | tf_op jit(solution)/shard_map/all_gather | solution.py:303
  914.1 37.1 %collective-permute-start.19 = (bf16[512,2048]{1,0:T(8,128)(2,1)}, bf16[512,2048]{1,0:T(8,128)(2,1)}, u32[]{:S(2)}, u32[]{:S(2)}) collective-permute-start(bf16[512,2048]{1,0:T(8,128)(2,1)} %slice.482), channel_id=1, source_target_pairs={{0,4},{4,0},{8,12},{12,8},{16,20},{20,16},{24,28},{28,24},{1,5},{5... | collective-permute-start | bytes 6291464 | tf_op jit(solution)/shard_map/ppermute | solution.py:29
  951.0 44.8 %collective-permute-start.39 = (bf16[512,2048]{1,0:T(8,128)(2,1)}, bf16[512,2048]{1,0:T(8,128)(2,1)}, u32[]{:S(2)}, u32[]{:S(2)}) collective-permute-start(bf16[512,2048]{1,0:T(8,128)(2,1)} %slice.618), channel_id=1, source_target_pairs={{0,4},{4,0},{8,12},{12,8},{16,20},{20,16},{24,28},{28,24},{1,5},{5... | collective-permute-start | bytes 6291464 | tf_op jit(solution)/shard_map/ppermute | solution.py:29
  958.1 14.8 %collective-permute-start.23 = (bf16[64,2048]{1,0:T(8,128)(2,1)S(1)}, bf16[64,2048]{1,0:T(8,128)(2,1)S(1)}, u32[]{:S(2)}, u32[]{:S(2)}) collective-permute-start(bf16[64,2048]{1,0:T(8,128)(2,1)S(1)} %get-tuple-element.92), channel_id=1, source_target_pairs={{0,8},{4,12},{8,0},{12,4},{16,24},{20,28},{24,16},{28,20},{1,9},{5... | collective-permute-start | bytes 786440 | tf_op jit(solution)/shard_map/ppermute | solution.py:29
  959.6 14.8 %collective-permute-start.21 = (bf16[64,2048]{1,0:T(8,128)(2,1)S(1)}, bf16[64,2048]{1,0:T(8,128)(2,1)S(1)}, u32[]{:S(2)}, u32[]{:S(2)}) collective-permute-start(bf16[64,2048]{1,0:T(8,128)(2,1)S(1)} %get-tuple-element.94), channel_id=1, source_target_pairs={{0,16},{4,20},{8,24},{12,28},{16,0},{20,4},{24,8},{28,12},{1,17},{... | collective-permute-start | bytes 786440 | tf_op jit(solution)/shard_map/ppermute | solution.py:29
  961.0 23.1 %collective-permute-start.20 = (bf16[64,2048]{1,0:T(8,128)(2,1)}, bf16[64,2048]{1,0:T(8,128)(2,1)S(1)}, u32[]{:S(2)}, u32[]{:S(2)}) collective-permute-start(bf16[64,2048]{1,0:T(8,128)(2,1)} %get-tuple-element.95), channel_id=1, source_target_pairs={{0,8},{4,12},{8,0},{12,4},{16,24},{20,28},{24,16},{28,20},{1,9},{5... | collective-permute-start | bytes 786440 | tf_op jit(solution)/shard_map/ppermute | solution.py:29
  961.6 23.9 %collective-permute-start.25 = (bf16[64,2048]{1,0:T(8,128)(2,1)}, bf16[64,2048]{1,0:T(8,128)(2,1)S(1)}, u32[]{:S(2)}, u32[]{:S(2)}) collective-permute-start(bf16[64,2048]{1,0:T(8,128)(2,1)} %get-tuple-element.93), channel_id=1, source_target_pairs={{0,16},{4,20},{8,24},{12,28},{16,0},{20,4},{24,8},{28,12},{1,17},{... | collective-permute-start | bytes 786440 | tf_op jit(solution)/shard_map/ppermute | solution.py:29
  975.2 16.2 %collective-permute-start.22 = (bf16[64,2048]{1,0:T(8,128)(2,1)}, bf16[64,2048]{1,0:T(8,128)(2,1)S(1)}, u32[]{:S(2)}, u32[]{:S(2)}) collective-permute-start(bf16[64,2048]{1,0:T(8,128)(2,1)} %get-tuple-element.91), channel_id=1, source_target_pairs={{0,8},{4,12},{8,0},{12,4},{16,24},{20,28},{24,16},{28,20},{1,9},{5... | collective-permute-start | bytes 786440 | tf_op jit(solution)/shard_map/ppermute | solution.py:29
  975.7 15.6 %collective-permute-start.24 = (bf16[64,2048]{1,0:T(8,128)(2,1)S(1)}, bf16[64,2048]{1,0:T(8,128)(2,1)S(1)}, u32[]{:S(2)}, u32[]{:S(2)}) collective-permute-start(bf16[64,2048]{1,0:T(8,128)(2,1)S(1)} %get-tuple-element.90), channel_id=1, source_target_pairs={{0,16},{4,20},{8,24},{12,28},{16,0},{20,4},{24,8},{28,12},{1,17},{... | collective-permute-start | bytes 786440 | tf_op jit(solution)/shard_map/ppermute | solution.py:29
  (142 other events, 1611.7 us)
Sparse Core Ops, SparseCore 0:
  10.2 30.6 all-gather.13
  43.0 62.9 all-gather.11
  107.6 105.3 all-gather.15
  383.8 57.9 all-gather.17
  539.5 25.8 reduce-scatter.6
  567.6 54.8 reduce-scatter.10
  736.9 58.3 reduce-scatter.4
  798.3 102.2 reduce-scatter.8
  902.6 28.3 all-gather.25
  933.0 56.7 all-gather.31
  991.8 29.1 all-gather.19
  1022.8 28.3 all-gather.21
  1053.3 28.1 all-gather.23
  1083.4 43.3 all-gather.27
  1128.6 43.3 all-gather.29

commit v2 on v1

v2 whole, which is shorter than its diff:
```python
import functools

import jax
import jax.numpy as jnp
from jax import lax
from jax.experimental import pallas as pl
from jax.experimental.pallas import tpu as pltpu
from jax.sharding import PartitionSpec as P

HEADS = 16
HD = 128
WIN = 256
CAP = 128
EPSILON = 1e-05
BF = jnp.bfloat16
F32 = jnp.float32


def mm(left, right):
    return jnp.dot(left, right, preferred_element_type=F32)


def mm_nt(left, right):
    return lax.dot_general(left, right, (((1,), (1,)), ((), ())), preferred_element_type=F32)


def mm_tn(left, right):
    return lax.dot_general(left, right, (((0,), (0,)), ((), ())), preferred_element_type=F32)


def swap(value, bit):
    size = lax.axis_size("rep")
    return lax.ppermute(value, "rep", [(i, i ^ bit) for i in range(size)])


def chip_bits():
    size, bits, bit = lax.axis_size("rep"), [], 2
    while bit < size:
        bits.append(bit)
        bit *= 2
    return bits


def chip_offsets():
    return list(range(0, lax.axis_size("rep"), 2))


def gather_chips(value):
    bits = chip_bits()
    if len(bits) == 2:
        one, two = bits
        half = value.shape[0] // 2
        by_one, by_two = swap(value, one), swap(value, two)
        far = jnp.concatenate([swap(by_one[:half], two), swap(by_two[half:], one)], axis=0)
        return {0: value, one: by_one, two: by_two, one ^ two: far}
    blocks = {0: value}
    for bit in bits:
        blocks.update({d ^ bit: swap(b, bit) for d, b in list(blocks.items())})
    return blocks


def add(left, right):
    return left.astype(F32) + right.astype(F32)


def scatter_chips(blocks):
    bits = chip_bits()
    if len(bits) == 2:
        one, two = bits
        far = blocks[one ^ two]
        near_one, near_two = blocks[one], blocks[two]
        top, bottom = swap(far[0], one), swap(far[1], two)
        one_top, two_bottom = swap(near_one[0], one), swap(near_two[1], two)
        two_top = swap(add(near_two[0], top).astype(BF), two)
        one_bottom = swap(add(near_one[1], bottom).astype(BF), one)
        return jnp.concatenate(
            [
                blocks[0][0].astype(F32) + one_top.astype(F32) + two_top.astype(F32),
                blocks[0][1].astype(F32) + one_bottom.astype(F32) + two_bottom.astype(F32),
            ],
            axis=0,
        )
    blocks = {d: jnp.concatenate(b, axis=0) for d, b in blocks.items()}
    for bit in reversed(bits):
        kept = {d: b for d, b in blocks.items() if not d & bit}
        blocks = {d: add(b, swap(blocks[d | bit], bit)).astype(BF) for d, b in kept.items()}
    return blocks[0].astype(F32)


def halves(value):
    half = value.shape[0] // 2
    return value[:half], value[half:]


def gather_plane(value):
    blocks = gather_chips(value)
    same = jnp.concatenate([blocks[d] for d in chip_offsets()], axis=0)
    return jnp.concatenate([same, swap(same, 1)], axis=0)


def scatter_plane(partial):
    half = partial.shape[0] // 2
    same = add(partial[:half], swap(partial[half:], 1)).astype(BF)
    offsets = chip_offsets()
    rows = half // len(offsets)
    return scatter_chips({d: halves(same[i * rows : (i + 1) * rows]) for i, d in enumerate(offsets)})


def rotary_tables(length):
    half = HD // 2
    positions = jnp.arange(length, dtype=F32)
    inverse = 10000.0 ** (-2.0 * jnp.arange(half, dtype=F32) / HD)
    angles = positions[:, None] * inverse[None, :]
    cos, sin = jnp.cos(angles), jnp.sin(angles)
    return jnp.concatenate([cos, cos], axis=1), jnp.concatenate([-sin, sin], axis=1)


def rotate(values, cos, sin):
    return values * cos + pltpu.roll(values, HD // 2, 1) * sin


def window(step, seg_col, seg_row):
    low, high = max(0, step - 1) * WIN, (step + 1) * WIN
    shape = (WIN, high - low)
    row = lax.broadcasted_iota(jnp.int32, shape, 0) + step * WIN
    col = lax.broadcasted_iota(jnp.int32, shape, 1) + low
    near = (row >= col) & (row - col < WIN)
    same = seg_col[0, step * WIN : (step + 1) * WIN, :] == seg_row[0, :, low:high]
    return low, high, near & same


def attend_kernel(parts, z_ref, *refs):
    x_refs, w_refs = refs[:parts], refs[parts : 2 * parts]
    cos_ref, sin_ref, col_ref, row_ref, context_ref, qkv_ref, lse_ref, lin_ref = refs[2 * parts :]
    length, width = context_ref.shape
    tile = min(length, 256)

    @pl.loop(0, length // tile)
    def _(t):
        rows = pl.ds(pl.multiple_of(t * tile, tile), tile)
        total = mm(x_refs[0][rows, :], w_refs[0][...])
        for x, w in zip(x_refs[1:], w_refs[1:]):
            total += mm(x[rows, :], w[...])
        lin_ref[rows, :] = total

    cos, sin = cos_ref[...], sin_ref[...]
    for h in range(width // HD):
        q_at, k_at, v_at = (slice(i * width + h * HD, i * width + (h + 1) * HD) for i in range(3))
        qkv_ref[:, q_at] = rotate(lin_ref[:, q_at], cos, sin).astype(BF)
        qkv_ref[:, k_at] = rotate(lin_ref[:, k_at], cos, sin).astype(BF)
        qkv_ref[:, v_at] = lin_ref[:, v_at].astype(BF)
    for step in range(length // WIN):
        low, high, allowed = window(step, col_ref, row_ref)
        rows = slice(step * WIN, (step + 1) * WIN)
        for h in range(width // HD):
            q_at, k_at, v_at = (
                slice(i * width + h * HD, i * width + (h + 1) * HD) for i in range(3)
            )
            scores = mm_nt(qkv_ref[rows, q_at], qkv_ref[low:high, k_at]) * HD**-0.5
            scores = jnp.where(allowed, scores, -1e30)
            peak = jnp.max(scores, axis=1, keepdims=True)
            raw = jnp.exp(scores - peak)
            total = jnp.sum(raw, axis=1, keepdims=True)
            probs = (raw * (1.0 / total)).astype(BF)
            context_ref[rows, h * HD : (h + 1) * HD] = mm(probs, qkv_ref[low:high, v_at]).astype(BF)
            lse_ref[rows, h : h + 1] = peak + jnp.log(total)


def attend(shard, both, weights, tables, seg):
    parts = len(weights)
    rows, depth = both.shape
    length = tables[0].shape[0]
    wide = weights[0].shape[1]
    width = wide // 3
    piece = depth // parts
    whole = lambda *shape: pl.BlockSpec(shape, lambda s, z: (0,) * len(shape))
    take = lambda k: pl.BlockSpec((length, piece), lambda s, z: (s, (z[0] + parts - k) % parts))
    by_seq = lambda cols: pl.BlockSpec((length, cols), lambda s, z: (s, 0))
    return pl.pallas_call(
        functools.partial(attend_kernel, parts),
        grid_spec=pltpu.PrefetchScalarGridSpec(
            num_scalar_prefetch=1,
            grid=(rows // length,),
            in_specs=[take(k) for k in range(parts)]
            + [whole(piece, wide)] * parts
            + [whole(length, HD)] * 2
            + [
                pl.BlockSpec((1, length, 1), lambda s, z: (s, 0, 0)),
                pl.BlockSpec((1, 1, length), lambda s, z: (s, 0, 0)),
            ],
            out_specs=[by_seq(width), by_seq(wide), by_seq(width // HD)],
            scratch_shapes=[pltpu.VMEM((length, wide), F32)],
        ),
        out_shape=[
            jax.ShapeDtypeStruct((rows, width), BF),
            jax.ShapeDtypeStruct((rows, wide), BF),
            jax.ShapeDtypeStruct((rows, width // HD), F32),
        ],
        compiler_params=pltpu.CompilerParams(vmem_limit_bytes=40 << 20),
        cost_estimate=pl.CostEstimate(
            flops=2 * rows * depth * wide + 4 * rows * 2 * WIN * width,
            bytes_accessed=2 * (rows * depth + depth * wide + 2 * rows * wide),
            transcendentals=rows * 2 * WIN * width // HD,
        ),
        name="attend",
    )(shard, *[both] * parts, *weights, *tables, *seg)


def attend_back_kernel(
    grad_ref, out_ref, qkv_ref, lse_ref, x_ref, cos_ref, sin_ref, col_ref, row_ref,
    lin_ref, top_ref, bottom_ref, kept_ref, context_ref, keys_ref, values_ref,
):
    length, wide = qkv_ref.shape
    width = wide // 3
    seq = pl.program_id(0)
    tile = min(length, 256)

    @pl.loop(0, length // tile)
    def _(t):
        rows = pl.ds(pl.multiple_of(t * tile, tile), tile)
        context_ref[rows, :] = mm_nt(grad_ref[rows, :], out_ref[...]).astype(BF)

    cos, sin = cos_ref[...], sin_ref[...]
    scale = HD**-0.5
    for h in range(width // HD):
        q_at, k_at, v_at = (slice(i * width + h * HD, i * width + (h + 1) * HD) for i in range(3))
        head = slice(h * HD, (h + 1) * HD)
        keys_ref[...] = jnp.zeros_like(keys_ref)
        values_ref[...] = jnp.zeros_like(values_ref)
        for step in range(length // WIN):
            low, high, allowed = window(step, col_ref, row_ref)
            rows = slice(step * WIN, (step + 1) * WIN)
            queries, keys = qkv_ref[rows, q_at], qkv_ref[low:high, k_at]
            grad = context_ref[rows, head]
            scores = jnp.where(allowed, mm_nt(queries, keys) * scale, -1e30)
            probs = jnp.exp(scores - lse_ref[rows, h : h + 1])
            values_ref[low:high, :] += mm_tn(probs.astype(BF), grad)
            grad_probs = mm_nt(grad, qkv_ref[low:high, v_at])
            inner = jnp.sum(probs * grad_probs, axis=1, keepdims=True)
            grad_scores = (probs * (grad_probs - inner)).astype(BF)
            grad_queries = mm(grad_scores, keys) * scale
            keys_ref[low:high, :] += mm_tn(grad_scores, queries)
            lin_ref[rows, q_at] = rotate(grad_queries, cos[rows], -sin[rows]).astype(BF)
        lin_ref[:, k_at] = rotate(keys_ref[...] * scale, cos, -sin).astype(BF)
        lin_ref[:, v_at] = values_ref[...].astype(BF)
    kept_ref[pl.ds(pl.multiple_of(seq * length, length), length), :] = lin_ref[...]

    @pl.when(seq == pl.num_programs(0) - 1)
    def _():
        half = top_ref.shape[0]
        step = 256
        for n, ref in enumerate((top_ref, bottom_ref)):

            @pl.loop(0, half // step)
            def _(t):
                cols = pl.ds(pl.multiple_of(n * half + t * step, step), step)
                rows = pl.ds(pl.multiple_of(t * step, step), step)
                ref[rows, :] = mm_tn(x_ref[:, cols], kept_ref[...]).astype(BF)


def attend_back(grad, out_w, qkv, lse, both, tables, seg):
    rows, depth = both.shape
    length = tables[0].shape[0]
    wide = qkv.shape[1]
    width = wide // 3
    whole = lambda *shape: pl.BlockSpec(shape, lambda s: (0,) * len(shape))
    by_seq = lambda cols: pl.BlockSpec((length, cols), lambda s: (s, 0))
    return pl.pallas_call(
        attend_back_kernel,
        grid=(rows // length,),
        in_specs=[by_seq(depth), whole(width, depth), by_seq(wide), by_seq(width // HD)]
        + [whole(rows, depth), whole(length, HD), whole(length, HD)]
        + [
            pl.BlockSpec((1, length, 1), lambda s: (s, 0, 0)),
            pl.BlockSpec((1, 1, length), lambda s: (s, 0, 0)),
        ],
        out_specs=[by_seq(wide), whole(depth // 2, wide), whole(depth // 2, wide)],
        scratch_shapes=[
            pltpu.VMEM((rows, wide), BF),
            pltpu.VMEM((length, width), BF),
            pltpu.VMEM((length, HD), F32),
            pltpu.VMEM((length, HD), F32),
        ],
        out_shape=[
            jax.ShapeDtypeStruct((rows, wide), BF),
            jax.ShapeDtypeStruct((depth // 2, wide), BF),
            jax.ShapeDtypeStruct((depth // 2, wide), BF),
        ],
        compiler_params=pltpu.CompilerParams(vmem_limit_bytes=48 << 20),
        cost_estimate=pl.CostEstimate(
            flops=2 * rows * depth * (wide + width) + 10 * rows * 2 * WIN * width,
            bytes_accessed=2 * (2 * rows * depth + depth * (wide + width) + 2 * rows * wide),
            transcendentals=rows * 2 * WIN * width // HD,
        ),
        name="attend_back",
    )(grad, out_w, qkv, lse, both, *tables, *seg)


def normed_back_kernel(blocks, parts, z_ref, *refs):
    lins, weights, total_ref = refs[:blocks], refs[blocks:-1], refs[-1]
    piece = total_ref.shape[1] // parts
    for k in range(parts):
        total = mm_nt(lins[0][...], weights[k][...])
        for n in range(1, blocks):
            total += mm_nt(lins[n][...], weights[n * parts + k][...])
        at = pl.multiple_of(((z_ref[0] + parts - k) % parts) * piece, piece)
        total_ref[:, pl.ds(at, piece)] = total


def normed_back(shard, lins, weights, depth):
    parts = len(weights[0])
    rows, wide = lins[0].shape
    tile = min(rows, 256)
    flat = [w for block in weights for w in block]
    return pl.pallas_call(
        functools.partial(normed_back_kernel, len(lins), parts),
        grid_spec=pltpu.PrefetchScalarGridSpec(
            num_scalar_prefetch=1,
            grid=(rows // tile,),
            in_specs=[pl.BlockSpec((tile, wide), lambda s, z: (s, 0))] * len(lins)
            + [
                pl.BlockSpec(flat[0].shape, lambda s, z: (0, 0), pipeline_mode=pl.Buffered(1))
            ] * len(flat),
            out_specs=pl.BlockSpec((tile, depth), lambda s, z: (s, 0)),
        ),
        out_shape=jax.ShapeDtypeStruct((rows, depth), F32),
        compiler_params=pltpu.CompilerParams(vmem_limit_bytes=48 << 20),
        cost_estimate=pl.CostEstimate(
            flops=2 * rows * depth * wide * len(lins),
            bytes_accessed=2 * len(lins) * wide * (rows + depth) + 4 * rows * depth,
            transcendentals=0,
        ),
        name="normed_back",
    )(shard, *lins, *flat)


def plan_slots(route_ids, gate_values):
    hit_mask = route_ids == 0
    hit = jnp.any(hit_mask, axis=-1)
    weight = jnp.sum(jnp.where(hit_mask, gate_values, 0.0), axis=-1)
    ids = jnp.arange(route_ids.shape[0], dtype=jnp.int32)
    earlier = (ids[None, :] < ids[:, None]) & hit[None, :]
    order = jnp.sum(earlier.astype(jnp.int32), axis=1)
    kept = hit & (order < CAP)
    slots = jnp.arange(CAP, dtype=jnp.int32)
    table = (order[None, :] == slots[:, None]) & kept[None, :]
    return table, jnp.where(kept, weight, 0.0)


def norm_back(grad_normed, source, root, gain):
    scaled = grad_normed * gain
    grad_gain = jnp.sum(grad_normed * source * root, axis=0)
    mean = jnp.mean(scaled * source, axis=-1, keepdims=True)
    return grad_gain, root * scaled - source * (root * root * root) * mean


def gather_vector(rows):
    size, me = lax.axis_size("shard"), lax.axis_index("shard")
    parts = [rows] + [
        lax.ppermute(rows, "shard", [(i, (i - k) % size) for i in range(size)])
        for k in range(1, size)
    ]
    twice = jnp.concatenate(parts + parts, axis=1)
    own = rows.shape[1]
    return lax.dynamic_slice_in_dim(twice, ((size - me) % size) * own, size * own, 1)


def place_kernel(me_ref, same_ref, other_ref, out_ref):
    odd = jnp.bitwise_xor(pl.program_id(0), me_ref[0]) % 2
    out_ref[...] = jnp.where(odd == 0, same_ref[...], other_ref[...]).astype(F32)


def place(me, same, other, height, width, group, columns):
    size = lax.axis_size("rep")
    spec = pl.BlockSpec(
        (height, width), lambda j, me: (jnp.bitwise_xor(j, me[0]) // 2, group)
    )
    shape = (height, size * width) if columns else (size * height, width)
    return pl.pallas_call(
        place_kernel,
        grid_spec=pltpu.PrefetchScalarGridSpec(
            num_scalar_prefetch=1,
            grid=(size,),
            in_specs=[spec, spec],
            out_specs=pl.BlockSpec(
                (height, width), (lambda j, me: (0, j)) if columns else (lambda j, me: (j, 0))
            ),
        ),
        out_shape=jax.ShapeDtypeStruct(shape, F32),
        cost_estimate=pl.CostEstimate(
            flops=0, bytes_accessed=8 * size * height * width, transcendentals=0
        ),
        name="place",
    )(me, same, other)


def place_turned_kernel(me_ref, same_ref, other_ref, out_ref):
    odd = me_ref[0] % 2
    first = jnp.where(odd == 0, same_ref[...], other_ref[...])
    second = jnp.where(odd == 0, other_ref[...], same_ref[...])
    out_ref[...] = jnp.concatenate([first, second], axis=0).T.astype(F32)


def place_turned(me, same, other, height):
    size, width = lax.axis_size("rep"), same.shape[1]
    if 2 * height % 128:
        return place(me, same, other, height, width, 0, False).T
    spec = pl.BlockSpec((height, width), lambda j, me: (jnp.bitwise_xor(j, me[0] // 2), 0))
    return pl.pallas_call(
        place_turned_kernel,
        grid_spec=pltpu.PrefetchScalarGridSpec(
            num_scalar_prefetch=1,
            grid=(size // 2,),
            in_specs=[spec, spec],
            out_specs=pl.BlockSpec((width, 2 * height), lambda j, me: (0, j)),
        ),
        out_shape=jax.ShapeDtypeStruct((width, size * height), F32),
        compiler_params=pltpu.CompilerParams(vmem_limit_bytes=32 << 20),
        cost_estimate=pl.CostEstimate(
            flops=0, bytes_accessed=12 * same.size, transcendentals=0
        ),
        name="place_turned",
    )(me, same, other)


def gather_copies(value):
    blocks = gather_chips(value)
    same = jnp.concatenate([blocks[d] for d in chip_offsets()], axis=0)
    return same, swap(same, 1)


def sum_vectors(rows):
    size, bit = lax.axis_size("rep"), 1
    while bit < size:
        rows, bit = rows + swap(rows, bit), 2 * bit
    shards, at = lax.axis_size("shard"), lax.axis_index("shard")
    own = rows.shape[1] // shards
    total = lax.dynamic_slice_in_dim(rows, at * own, own, 1)
    for k in range(1, shards):
        part = lax.dynamic_slice_in_dim(rows, ((at + k) % shards) * own, own, 1)
        total += lax.ppermute(part, "shard", [(i, (i + k) % shards) for i in range(shards)])
    return total


def per_device(
    layer_input,
    gain_attn,
    w_query,
    w_key,
    w_value,
    w_out,
    gain_mlp,
    w_gate,
    w_up,
    w_down,
    segments,
    attn_route,
    attn_gate,
    mlp_route,
    mlp_gate,
    cotangent,
):
    length = layer_input.shape[0]
    size = lax.axis_size("rep")
    me = lax.axis_index("rep")
    block = w_query.shape[1] // size
    hidden_block = w_gate.shape[1] // size
    offsets = chip_offsets()

    def columns(weight, width):
        return lax.dynamic_slice_in_dim(weight, me * width, width, 1)

    def rows_of(weight, height):
        return lax.dynamic_slice_in_dim(weight, me * height, height, 0)

    shards = lax.axis_size("shard")
    shard = lax.axis_index("shard").astype(jnp.int32).reshape(1)
    three = (w_query, w_key, w_value)

    def local(d):
        at = jnp.bitwise_xor(me, d) * block
        return jnp.concatenate(
            [lax.dynamic_slice_in_dim(w, at, block, 1) for w in three], axis=1
        )

    piece = local(0)
    qkv_w = {d: [piece if d == 0 else local(d)] for d in offsets}
    ring = [(i, (i + 1) % shards) for i in range(shards)]
    for _ in range(1, shards):
        piece = lax.ppermute(piece, "shard", ring)
        for d, w in gather_chips(piece).items():
            qkv_w[d].append(w)
    own_out, piece = lax.optimization_barrier((rows_of(w_out, block), piece))
    qkv_w[0][-1] = piece
    own_out = lax.all_gather(own_out, "shard", axis=1, tiled=True)
    gate_up = jnp.concatenate([columns(w_gate, hidden_block), columns(w_up, hidden_block)], axis=1)
    out_w = gather_chips(own_out)
    gate_up, _ = lax.optimization_barrier((gate_up, own_out))
    gate_up = lax.all_gather(gate_up, "shard", axis=0, tiled=True)
    own_down, _ = lax.optimization_barrier((rows_of(w_down, hidden_block), gate_up))
    down = lax.all_gather(own_down, "shard", axis=1, tiled=True)

    gains = gather_vector(jnp.stack([gain_attn, gain_mlp])).astype(F32)
    gain_one, gain_two = gains[0], gains[1]

    table, mix = plan_slots(mlp_route, mlp_gate)
    pick = table.astype(BF)
    upstream = cotangent.astype(F32)
    slot_weight = jnp.sum(jnp.where(table, mix[None, :], 0.0), axis=1)[:, None]
    slot_grad = (mm(pick, cotangent) * slot_weight).astype(BF)
    all_slot_grad = gather_plane(slot_grad)

    inputs = layer_input.astype(F32)
    root_one = lax.rsqrt(jnp.mean(inputs * inputs, axis=-1, keepdims=True) + EPSILON)
    normed = (inputs * root_one * gain_one).astype(BF)
    both = jnp.concatenate([normed, swap(normed, 1)], axis=0)
    seg = jnp.concatenate([segments, swap(segments, 1)], axis=0)
    seg = (seg[:, :, None], seg[:, None, :])
    tables = rotary_tables(length)
    context, saved = {}, {}
    for d in offsets:
        context[d], *saved[d] = attend(shard, both, qkv_w[d], tables, seg)
    all_context = jnp.concatenate([context[d] for d in offsets], axis=1)
    all_out = jnp.concatenate([out_w[d] for d in offsets], axis=0)
    projected = mm(all_context, all_out)
    projected = projected[:length] + swap(projected[length:].astype(BF), 1).astype(F32)
    attn_weight = jnp.sum(jnp.where(attn_route == 0, attn_gate, 0.0), axis=-1)[:, None]
    hidden = inputs + projected * attn_weight
    root_two = lax.rsqrt(jnp.mean(hidden * hidden, axis=-1, keepdims=True) + EPSILON)
    normed_two = (hidden * root_two * gain_two).astype(BF)
    normed_two, gate_up = lax.optimization_barrier((normed_two, gate_up))

    dispatched = gather_plane(mm(pick, normed_two).astype(BF))
    act = mm(dispatched, gate_up)
    gate_act, up_act = act[:, :hidden_block], act[:, hidden_block:]
    sigmoid = jax.nn.sigmoid(gate_act)
    silu = gate_act * sigmoid
    inner = (silu * up_act).astype(BF)
    grad_inner = mm_nt(all_slot_grad, down)
    grad_gate_act = (grad_inner * up_act * sigmoid * (1.0 + gate_act * (1.0 - sigmoid))).astype(BF)
    grad_up_act = (grad_inner * silu).astype(BF)
    grad_act = jnp.concatenate([grad_gate_act, grad_up_act], axis=1)
    grad_disp = scatter_plane(mm_nt(grad_act, gate_up).astype(BF)).astype(BF)
    expert_out = scatter_plane(mm(inner, down).astype(BF)).astype(BF)
    output = (hidden + mm_tn(pick, expert_out) * mix[:, None]).astype(BF)
    grad_mlp = [
        mm_tn(grad_gate_act, dispatched).astype(BF),
        mm_tn(grad_up_act, dispatched).astype(BF),
        mm_tn(inner, all_slot_grad).astype(BF),
    ]

    grad_normed_two = mm_tn(pick, grad_disp)
    grad_gain_two, through = norm_back(grad_normed_two, hidden, root_two, gain_two)
    grad_hidden = upstream + through
    grad_hidden, grad_mlp = lax.optimization_barrier((grad_hidden, grad_mlp))

    grad_projected = (grad_hidden * attn_weight).astype(BF)
    both_grad = jnp.concatenate([grad_projected, swap(grad_projected, 1)], axis=0)
    grad_out_w = mm_tn(all_context, both_grad).astype(BF)
    lins, grad_qkv_w = {}, {}
    for d in reversed(offsets):
        lins[d], *grad_qkv_w[d] = attend_back(both_grad, out_w[d], *saved[d], both, tables, seg)
        both_grad, lins[d] = lax.optimization_barrier((both_grad, lins[d]))
    grad_normed = normed_back(
        shard, [lins[d] for d in offsets], [qkv_w[d] for d in offsets], both.shape[1]
    )
    grad_normed = grad_normed[:length] + swap(grad_normed[length:].astype(BF), 1).astype(F32)
    grad_gain_one, first = norm_back(grad_normed, inputs, root_one, gain_one)
    grad_input = (grad_hidden + first).astype(BF)

    whoami = me.astype(jnp.int32).reshape(1)
    sums = [lax.psum_scatter(g, "shard", scatter_dimension=1, tiled=True) for g in grad_mlp]
    own_grad_out = scatter_chips(
        {d: halves(grad_out_w[i * block : (i + 1) * block]) for i, d in enumerate(offsets)}
    ).astype(BF)
    own_grad_out, _ = lax.optimization_barrier((own_grad_out, sums))
    sum_out = lax.psum_scatter(own_grad_out, "shard", scatter_dimension=1, tiled=True)
    own_grad_qkv = scatter_chips(grad_qkv_w).astype(BF)
    own_grad_qkv, _ = lax.optimization_barrier((own_grad_qkv, sum_out))
    sum_qkv = lax.psum_scatter(own_grad_qkv, "shard", scatter_dimension=0, tiled=True)
    own = gain_attn.shape[0]
    grad_gate, grad_up = (
        place_turned(whoami, *gather_copies(g), hidden_block) for g in sums[:2]
    )
    grad_down = place(whoami, *gather_copies(sums[2]), hidden_block, own, 0, False)
    grad_out = place(whoami, *gather_copies(sum_out), block, own, 0, False)
    copies = gather_copies(sum_qkv)
    grad_query, grad_key, grad_value = (
        place(whoami, *copies, own, block, group, True) for group in range(3)
    )
    gain_grads = sum_vectors(jnp.stack([grad_gain_one, grad_gain_two]))
    return (
        output,
        grad_input,
        gain_grads[0],
        grad_query,
        grad_key,
        grad_value,
        grad_out,
        gain_grads[1],
        grad_gate,
        grad_up,
        grad_down,
    )


def solution(mesh):
    tokens = P(("rep", "shard"), None)
    tall, wide, vector = P("shard", None), P(None, "shard"), P("shard")
    weights = (vector, tall, tall, tall, wide, vector, tall, tall, wide)
    return jax.shard_map(
        per_device,
        mesh=mesh,
        in_specs=(tokens, *weights) + (tokens,) * 6,
        out_specs=(tokens, tokens, *weights),
        check_vma=False,
    )
```

time: 1190 us -> 873 us (0.73)
  waiting for transfers between devices: 592 us -> 348 us
  Pallas kernels: 0 us -> 182 us
  matrix products: 222 us -> 76.9 us
  local copies, waits for them, and re-layouts: 180 us -> 83.6 us
  blocking collectives: 39.9 us -> 0 us
  starting transfers between devices: 52.3 us -> 88.8 us
  other arithmetic: 85.9 us -> 70.1 us
    pallas_call x0 -> x16, Pallas kernels: none -> 182 us  [the longest x4 69.8 us: attend_back(): pl.pallas_call(attend_back_kernel, grid=(rows // length,), in_specs=[by_s...]
    all_gather x10 -> x2, waiting for transfers between devices: 203 us -> 39.3 us  [the longest x1 39.3 us: per_device(): down = lax.all_gather(own_down, 'shard', axis=1, tiled=True)]
    reduce_scatter x2 -> x3, waiting for transfers between devices: 102 us -> 13.3 us  [per_device(): lax.psum_scatter(g, 'shard', scatter_dimension=1, tiled=True)]
    dot_general x24 -> x0, matrix products: 47.9 us -> none  [the longest x4 13.7 us: attend_back(): jnp.einsum('bqhd,bkhd->bhqk', grad_context, values, preferred_element_typ...]
    slice x27 -> x3, local copies, waits for them, and re-layouts: 50.9 us -> 3.16 us  [halves(): return (value[:half], value[half:])]
    reduce_scatter x1, waiting for transfers between devices: 46.1 us -> 0.02 us  [per_device(): lax.psum_scatter(own_grad_qkv, 'shard', scatter_dimension=0, tiled=True)]
    ppermute x0 -> x6, waiting for transfers between devices: none -> 45.2 us  [the longest x3 39.1 us: per_device(): piece = lax.ppermute(piece, 'shard', ring)]
    dot_general x7 -> x2, matrix products: 59.5 us -> 19.5 us  [mm_nt(): lax.dot_general(left, right, (((1,), (1,)), ((), ())), preferred_element_...]
  transfers between devices with their start and end apart: 67 -> 102, of which waited for: 40 -> 43; matrix products, arithmetic and copies ran while one was open for 36% -> 21% of each run, Pallas kernels for 0% -> 19%
where the time goes in v2:
time: 873 us; the launch traced here: 865 us
  waiting for transfers between devices  348 us (40%)
  Pallas kernels  182 us (21%)
  starting transfers between devices  88.8 us (10%)
  local copies, waits for them, and re-layouts  83.6 us (10%)
  matrix products  76.9 us (9%)
  other arithmetic  70.1 us (8%)
  between operations  15.8 us (2%)
    ppermute x85, waiting for transfers between devices, swap(): return lax.ppermute(value, 'rep', [(i, i ^ bit) for i in range(size)])  238 us
    ppermute x85, starting transfers between devices, swap(): return lax.ppermute(value, 'rep', [(i, i ^ bit) for i in range(size)])  76.1 us
    pallas_call x4, Pallas kernels, attend_back(): pl.pallas_call(attend_back_kernel, grid=(rows // length,), in_specs=[by_s...  69.8 us
    pallas_call x4, Pallas kernels, attend(): pl.pallas_call(functools.partial(attend_kernel, parts), grid_spec=pltpu.P...  41.5 us
    unnamed x220, local copies, waits for them, and re-layouts  41.4 us
    all_gather x1, waiting for transfers between devices, per_device(): down = lax.all_gather(own_down, 'shard', axis=1, tiled=True)  39.3 us
    ppermute x3, waiting for transfers between devices, per_device(): piece = lax.ppermute(piece, 'shard', ring)  39.1 us
    pallas_call x5, Pallas kernels, place(): pl.pallas_call(place_kernel, grid_spec=pltpu.PrefetchScalarGridSpec(num_s...  36.5 us
  transfers between devices with their start and end apart: 102, of which 43 were waited for; matrix products, arithmetic and copies ran while one was open for 21% of the time, Pallas kernels for 19%

profile of v2, /device:TPU:0, one launch (start us, length us, event | category | flops | bytes accessed | tf_op | source)
XLA Modules:
  0.0 865.4 jit_solution(17050979223043460922)
XLA Ops:
  21.2 11.1 %collective-permute-done = bf16[2,512]{1,0:T(2,128)(2,1)S(1)} collective-permute-done((bf16[2,512]{1,0:T(2,128)(2,1)S(1)}, bf16[2,512]{1,0:T(2,128)(2,1)S(1)}, u32[]{:S(2)}, u32[]{:S(2)}) %collective-permute-start) | collective-permute-done | bytes 2080 | tf_op jit(solution)/shard_map/ppermute | solution.py:360
  35.3 20.6 %collective-permute-done.5.refs_6_ = bf16[512,768]{1,0:T(8,128)(2,1)} collective-permute-done((bf16[512,768]{1,0:T(8,128)(2,1)}, bf16[512,768]{1,0:T(8,128)(2,1)}, u32[]{:S(2)}, u32[]{:S(2)}) %collective-permute-start.5) | collective-permute-done | bytes 786464 | tf_op jit(solution)/shard_map/ppermute | solution.py:490
  55.9 3.5 fusion.2
  60.1 15.6 %collective-permute-done.6.refs_7_ = bf16[512,768]{1,0:T(8,128)(2,1)} collective-permute-done((bf16[512,768]{1,0:T(8,128)(2,1)}, bf16[512,768]{1,0:T(8,128)(2,1)}, u32[]{:S(2)}, u32[]{:S(2)}) %collective-permute-start.6) | collective-permute-done | bytes 786464 | tf_op jit(solution)/shard_map/ppermute | solution.py:490
  85.2 10.9 %collective-permute-done.8.refs_5_.refs_9_ = bf16[512,768]{1,0:T(8,128)(2,1)S(1)} collective-permute-done((bf16[512,768]{1,0:T(8,128)(2,1)}, bf16[512,768]{1,0:T(8,128)(2,1)S(1)}, u32[]{:S(2)}, u32[]{:S(2)}) %collective-permute-start.8) | collective-permute-done | bytes 786464 | tf_op jit(solution)/shard_map/ppermute | solution.py:33
  110.3 3.6 collective-permute-done.15
  118.8 12.0 %collective-permute-done.9.refs_6_.refs_10_ = bf16[512,768]{1,0:T(8,128)(2,1)} collective-permute-done((bf16[512,768]{1,0:T(8,128)(2,1)}, bf16[512,768]{1,0:T(8,128)(2,1)}, u32[]{:S(2)}, u32[]{:S(2)}) %collective-permute-start.9) | collective-permute-done | bytes 786464 | tf_op jit(solution)/shard_map/ppermute | solution.py:33
  135.1 11.0 %attend.4 = (bf16[1024,256]{1,0:T(8,128)(2,1)S(1)}, bf16[1024,768]{1,0:T(8,128)(2,1)S(1)}, f32[1024,2]{1,0:T(8,128)S(1)}) custom-call(s32[1]{0:T(128)} %bitcast.z_ref, bf16[1024,2048]{1,0:T(8,128)(2,1)S(1)} %pad_maximum_fusion.refs_0_.refs_1_.refs_2_.refs_3_.x_ref, bf16[1024,2048]{1,0:T(8,128)(2,1)S(1)} %pad_maximum_fusion.refs_0_.refs_1_.refs_2_.refs_3_.x_ref, ...), custom_call_target="tpu_custom_call" | custom-call | flops 3758096384 | bytes 10485760 | tf_op jit(solution)/shard_map/attend/pallas_call | solution.py:179
  146.2 3.8 collective-permute-done.16
  150.0 4.5 collective-permute-done.17
  156.8 10.3 %attend.5 = (bf16[1024,256]{1,0:T(8,128)(2,1)S(1)}, bf16[1024,768]{1,0:T(8,128)(2,1)S(1)}, f32[1024,2]{1,0:T(8,128)S(1)}) custom-call(s32[1]{0:T(128)} %bitcast.z_ref, bf16[1024,2048]{1,0:T(8,128)(2,1)S(1)} %pad_maximum_fusion.refs_0_.refs_1_.refs_2_.refs_3_.x_ref, bf16[1024,2048]{1,0:T(8,128)(2,1)S(1)} %pad_maximum_fusion.refs_0_.refs_1_.refs_2_.refs_3_.x_ref, ...), custom_call_target="tpu_custom_call" | custom-call | flops 3758096384 | bytes 10485760 | tf_op jit(solution)/shard_map/attend/pallas_call | solution.py:179
  169.0 10.6 %attend.6 = (bf16[1024,256]{1,0:T(8,128)(2,1)S(1)}, bf16[1024,768]{1,0:T(8,128)(2,1)S(1)}, f32[1024,2]{1,0:T(8,128)S(1)}) custom-call(s32[1]{0:T(128)} %bitcast.z_ref, bf16[1024,2048]{1,0:T(8,128)(2,1)S(1)} %pad_maximum_fusion.refs_0_.refs_1_.refs_2_.refs_3_.x_ref, bf16[1024,2048]{1,0:T(8,128)(2,1)S(1)} %pad_maximum_fusion.refs_0_.refs_1_.refs_2_.refs_3_.x_ref, ...), custom_call_target="tpu_custom_call" | custom-call | flops 3758096384 | bytes 10485760 | tf_op jit(solution)/shard_map/attend/pallas_call | solution.py:179
  181.4 9.6 %attend.7 = (bf16[1024,256]{1,0:T(8,128)(2,1)S(1)}, bf16[1024,768]{1,0:T(8,128)(2,1)S(1)}, f32[1024,2]{1,0:T(8,128)S(1)}) custom-call(s32[1]{0:T(128)} %bitcast.z_ref, bf16[1024,2048]{1,0:T(8,128)(2,1)S(1)} %pad_maximum_fusion.refs_0_.refs_1_.refs_2_.refs_3_.x_ref, bf16[1024,2048]{1,0:T(8,128)(2,1)S(1)} %pad_maximum_fusion.refs_0_.refs_1_.refs_2_.refs_3_.x_ref, ...), custom_call_target="tpu_custom_call" | custom-call | flops 3758096384 | bytes 10485760 | tf_op jit(solution)/shard_map/attend/pallas_call | solution.py:179
  192.9 13.0 %collective-permute-done.21.out_ref = bf16[256,2048]{1,0:T(8,128)(2,1)S(1)} collective-permute-done((bf16[256,2048]{1,0:T(8,128)(2,1)S(1)}, bf16[256,2048]{1,0:T(8,128)(2,1)S(1)}, u32[]{:S(2)}, u32[]{:S(2)}) %collective-permute-start.21) | collective-permute-done | bytes 1048608 | tf_op jit(solution)/shard_map/ppermute | solution.py:33
  207.2 6.7 collective-permute-done.22
  216.0 4.5 fusion.55
  226.1 11.0 %collective-permute-done.37 = bf16[128,2048]{1,0:T(8,128)(2,1)S(1)} collective-permute-done((bf16[128,2048]{1,0:T(8,128)(2,1)S(1)}, bf16[128,2048]{1,0:T(8,128)(2,1)S(1)}, u32[]{:S(2)}, u32[]{:S(2)}) %collective-permute-start.37) | collective-permute-done | bytes 524320 | tf_op jit(solution)/shard_map/ppermute | solution.py:33
  256.2 5.9 collective-permute-done.25
  281.5 10.6 %fusion.56 = f32[1024,1408]{1,0:T(8,128)} fusion(bf16[1024,2048]{1,0:T(8,128)(2,1)S(1)} %constant_dynamic-update-slice_fusion.28, bf16[2048,1408]{1,0:T(8,128)(2,1)} %all-gather.6.cloned.1.call-done), kind=kOutput, calls=%fused_computation.222 | convolution fusion | flops 5905580032 | bytes 15728640 | tf_op jit(solution)/shard_map/dot_general | solution.py:20
  292.1 39.3 %all-gather.8.cloned.1.call-done = bf16[704,2048]{1,0:T(8,128)(2,1)} async-done(((bf16[704,512]{1,0:T(8,128)(2,1)}), bf16[704,2048]{1,0:T(8,128)(2,1)}) %all-gather.8.cloned.1.call-update) | async-done | bytes 2883600 | tf_op jit(solution)/shard_map/all_gather | solution.py:501
  331.4 10.1 %multiply_convert_fusion.3 = (bf16[1024,704]{1,0:T(8,128)(2,1)S(1)}, bf16[1024,704]{1,0:T(8,128)(2,1)S(1)}, bf16[1024,704]{1,0:T(8,128)(2,1)}) fusion(f32[1024,1408]{1,0:T(8,128)} %fusion.56, bf16[1024,2048]{1,0:T(8,128)(2,1)} %constant_dynamic-update-slice_fusion.39, bf16[704,2048]{1,0:T(8,128)(2,1)} %all-gather.8.cloned.1.call-done), kind=kOutput, calls=%fused_computation.44 | convolution fusion | flops 2963603456 | bytes 17170432 | tf_op jit(solution)/shard_map/dot_general | solution.py:24
  341.5 9.3 %convolution_convert_fusion = bf16[1024,2048]{1,0:T(8,128)(2,1)S(1)} fusion(bf16[2048,1408]{1,0:T(8,128)(2,1)} %all-gather.6.cloned.1.call-done, bf16[1024,704]{1,0:T(8,128)(2,1)S(1)} %get-tuple-element.108, bf16[1024,704]{1,0:T(8,128)(2,1)S(1)} %get-tuple-element.107), kind=kOutput, calls=%fused_computation.32 | convolution fusion | flops 5913444352 | bytes 12845056 | tf_op jit(solution)/shard_map/dot_general | solution.py:24
  351.1 4.1 collective-permute-done.42
  359.8 4.7 convolution_convert_fusion.5
  370.3 7.4 convolution_convert_fusion.4
  382.5 7.4 convolution_convert_fusion.3
  391.2 3.6 multiply_reduce_fusion
  399.2 3.9 multiply_convert_fusion
  407.6 4.8 pad_maximum_fusion.1.grad_ref
  412.4 17.3 %attend_back.4 = (bf16[1024,768]{1,0:T(8,128)(2,1)S(1)}, bf16[1024,768]{1,0:T(8,128)(2,1)S(1)}, bf16[1024,768]{1,0:T(8,128)(2,1)}) custom-call(bf16[1024,2048]{1,0:T(8,128)(2,1)} %pad_maximum_fusion.1.grad_ref, bf16[256,2048]{1,0:T(8,128)(2,1)S(1)} %copy-done.19, bf16[1024,768]{1,0:T(8,128)(2,1)} %copy-done.23, f32[1024,2]{1,0:T(8,128)S(1)} %copy-done.29, ...), custom_call_target="tpu_custom_call" | custom-call | flops 5637144576 | bytes 15728640 | tf_op jit(solution)/shard_map/attend_back/pallas_call | solution.py:268
  431.3 7.0 convolution_convert_fusion.2
  440.5 17.1 %attend_back.5 = (bf16[1024,768]{1,0:T(8,128)(2,1)S(1)}, bf16[1024,768]{1,0:T(8,128)(2,1)S(1)}, bf16[1024,768]{1,0:T(8,128)(2,1)}) custom-call(bf16[1024,2048]{1,0:T(8,128)(2,1)} %pad_maximum_fusion.1.grad_ref, bf16[256,2048]{1,0:T(8,128)(2,1)S(1)} %copy-done.8, bf16[1024,768]{1,0:T(8,128)(2,1)} %copy-done.22, f32[1024,2]{1,0:T(8,128)S(1)} %copy-done.27, ...), custom_call_target="tpu_custom_call" | custom-call | flops 5637144576 | bytes 15728640 | tf_op jit(solution)/shard_map/attend_back/pallas_call | solution.py:268
  464.9 17.8 %attend_back.6 = (bf16[1024,768]{1,0:T(8,128)(2,1)S(1)}, bf16[1024,768]{1,0:T(8,128)(2,1)}, bf16[1024,768]{1,0:T(8,128)(2,1)}) custom-call(bf16[1024,2048]{1,0:T(8,128)(2,1)} %pad_maximum_fusion.1.grad_ref, bf16[256,2048]{1,0:T(8,128)(2,1)S(1)} %copy-done.6, bf16[1024,768]{1,0:T(8,128)(2,1)} %copy-done.21, f32[1024,2]{1,0:T(8,128)S(1)} %copy-done.25, ...), custom_call_target="tpu_custom_call" | custom-call | flops 5637144576 | bytes 15728640 | tf_op jit(solution)/shard_map/attend_back/pallas_call | solution.py:268
  482.8 23.4 %collective-permute-done.63 = bf16[128,2048]{1,0:T(8,128)(2,1)S(1)} collective-permute-done((bf16[128,2048]{1,0:T(8,128)(2,1)}, bf16[128,2048]{1,0:T(8,128)(2,1)S(1)}, u32[]{:S(2)}, u32[]{:S(2)}) %collective-permute-start.63) | collective-permute-done | bytes 524320 | tf_op jit(solution)/shard_map/ppermute | solution.py:33
  518.9 34.0 %collective-permute-done.68 = bf16[128,2048]{1,0:T(8,128)(2,1)S(1)} collective-permute-done((bf16[128,2048]{1,0:T(8,128)(2,1)}, bf16[128,2048]{1,0:T(8,128)(2,1)S(1)}, u32[]{:S(2)}, u32[]{:S(2)}) %collective-permute-start.68) | collective-permute-done | bytes 524320 | tf_op jit(solution)/shard_map/ppermute | solution.py:33
  557.2 13.3 %reduce-scatter.10.cloned.1.call-done = bf16[704,512]{1,0:T(8,128)(2,1)} async-done(((bf16[704,2048]{1,0:T(8,128)(2,1)}), bf16[704,512]{1,0:T(8,128)(2,1)}) %reduce-scatter.10.cloned.1.call-update) | async-done | bytes 720912 | tf_op jit(solution)/shard_map/reduce_scatter | solution.py:572
  570.5 5.7 convolution_convert_fusion.1
  578.2 17.5 %attend_back.7 = (bf16[1024,768]{1,0:T(8,128)(2,1)S(1)}, bf16[1024,768]{1,0:T(8,128)(2,1)S(1)}, bf16[1024,768]{1,0:T(8,128)(2,1)}) custom-call(bf16[1024,2048]{1,0:T(8,128)(2,1)} %pad_maximum_fusion.1.grad_ref, bf16[256,2048]{1,0:T(8,128)(2,1)S(1)} %copy-done.18, bf16[1024,768]{1,0:T(8,128)(2,1)} %copy-done.20, f32[1024,2]{1,0:T(8,128)S(1)} %get-tuple-element.78.lse_ref, ...), custom_call_target="tpu_custom_call" | custom-call | flops 5637144576 | bytes 15728640 | tf_op jit(solution)/shard_map/attend_back/pallas_call | solution.py:268
  595.8 3.5 add_convert_fusion.3
  604.8 19.9 %normed_back.1 = f32[1024,2048]{1,0:T(8,128)} custom-call(s32[1]{0:T(128)} %bitcast.z_ref, bf16[1024,768]{1,0:T(8,128)(2,1)} %copy-done.33, bf16[1024,768]{1,0:T(8,128)(2,1)} %copy-done.32, bf16[1024,768]{1,0:T(8,128)(2,1)} %copy-done.31, bf16[1024,768]{1,0:T(8,128)(2,1)} %copy-done.30, bf16[512,768]{1,0:T(8,128)(2,1)S(1)} %pad_maximum_fusion.6.refs_4_, ...), custom_call_target="tpu_custom_call" | custom-call | flops 12884901888 | bytes 27262976 | tf_op jit(solution)/shard_map/normed_back/pallas_call | solution.py:315
  624.8 3.9 slice.374
  633.2 4.3 fusion.9
  643.6 4.1 collective-permute-done.32
  649.2 3.9 collective-permute-done.52
  662.6 11.1 %collective-permute-done.79 = bf16[704,512]{1,0:T(8,128)(2,1)S(1)} collective-permute-done((bf16[704,512]{1,0:T(8,128)(2,1)S(1)}, bf16[704,512]{1,0:T(8,128)(2,1)S(1)}, u32[]{:S(2)}, u32[]{:S(2)}) %collective-permute-start.79) | collective-permute-done | bytes 720928 | tf_op jit(solution)/shard_map/ppermute | solution.py:33
  680.7 8.4 collective-permute-done.84
  696.4 8.3 collective-permute-done.89
  716.2 13.0 %collective-permute-done.82 = bf16[352,512]{1,0:T(8,128)(2,1)S(1)} collective-permute-done((bf16[352,512]{1,0:T(8,128)(2,1)S(1)}, bf16[352,512]{1,0:T(8,128)(2,1)S(1)}, u32[]{:S(2)}, u32[]{:S(2)}) %collective-permute-start.82) | collective-permute-done | bytes 360480 | tf_op jit(solution)/shard_map/ppermute | solution.py:33
  730.5 7.8 collective-permute-done.86
  745.7 12.6 %collective-permute-done.71 = bf16[256,768]{1,0:T(8,128)(2,1)S(1)} collective-permute-done((bf16[256,768]{1,0:T(8,128)(2,1)S(1)}, bf16[256,768]{1,0:T(8,128)(2,1)S(1)}, u32[]{:S(2)}, u32[]{:S(2)}) %collective-permute-start.71) | collective-permute-done | bytes 393248 | tf_op jit(solution)/shard_map/ppermute | solution.py:33
  763.4 3.3 collective-permute-done.92
  772.8 6.1 collective-permute-done.74
  781.7 4.0 collective-permute-done.75
  786.4 4.2 collective-permute-done.76
  791.3 4.3 collective-permute-done.77
  795.9 5.1 collective-permute-done.54
  801.0 4.6 fusion.6
  807.2 6.4 place.8
  813.6 7.8 place_turned.2
  821.5 6.8 place_turned.3
  828.3 10.5 %place.9 = f32[5632,512]{1,0:T(8,128)} custom-call(s32[1]{0:T(128)} %bitcast.7.me_ref, bf16[2816,512]{1,0:T(8,128)(2,1)} %constant_dynamic-update-slice_fusion.65.same_ref, bf16[2816,512]{1,0:T(8,128)(2,1)} %collective-permute-done.93.other_ref), custom_call_target="tpu_custom_call" | custom-call | bytes 23068672 | tf_op jit(solution)/shard_map/place/pallas_call | solution.py:379
  838.8 6.5 place.5
  845.2 6.6 place.6
  851.9 6.5 place.7
  (507 shorter events, 239.4 us)
Async XLA Ops:
  7.2 98.7 %all-gather.4.cloned.1.call-start = ((), (), s32[]{:S(2)}) async-start(), calls=%async_computation.5 | async-start | bytes 1310720 | tf_op jit(solution)/shard_map/all_gather | solution.py:495
  12.3 22.9 %collective-permute-start.4 = (bf16[512,768]{1,0:T(8,128)(2,1)S(1)}, bf16[512,768]{1,0:T(8,128)(2,1)}, u32[]{:S(2)}, u32[]{:S(2)}) collective-permute-start(bf16[512,768]{1,0:T(8,128)(2,1)S(1)} %pad_maximum_fusion.6.refs_4_), channel_id=1, source_target_pairs={{0,1},{1,2},{2,3},{3,0},{4,5},{5,6},{6,7},{7,4},{8,9},{9,10},{10,1... | collective-permute-start | bytes 2359304 | tf_op jit(solution)/shard_map/ppermute | solution.py:490
  15.4 16.8 %collective-permute-start = (bf16[2,512]{1,0:T(2,128)(2,1)S(1)}, bf16[2,512]{1,0:T(2,128)(2,1)S(1)}, u32[]{:S(2)}, u32[]{:S(2)}) collective-permute-start(bf16[2,512]{1,0:T(2,128)(2,1)S(1)} %get-tuple-element.106), channel_id=1, source_target_pairs={{0,3},{1,0},{2,1},{3,2},{4,7},{5,4},{6,5},{7,6},{8,11},{9,8},{10,9... | collective-permute-start | bytes 6152 | tf_op jit(solution)/shard_map/ppermute | solution.py:360
  17.5 17.7 %collective-permute-start.1 = (bf16[2,512]{1,0:T(2,128)(2,1)S(1)}, bf16[2,512]{1,0:T(2,128)(2,1)S(1)}, u32[]{:S(2)}, u32[]{:S(2)}) collective-permute-start(bf16[2,512]{1,0:T(2,128)(2,1)S(1)} %get-tuple-element.106), channel_id=1, source_target_pairs={{0,2},{1,3},{2,0},{3,1},{4,6},{5,7},{6,4},{7,5},{8,10},{9,11},{10,... | collective-permute-start | bytes 6152 | tf_op jit(solution)/shard_map/ppermute | solution.py:360
  35.2 20.7 %collective-permute-start.5 = (bf16[512,768]{1,0:T(8,128)(2,1)}, bf16[512,768]{1,0:T(8,128)(2,1)}, u32[]{:S(2)}, u32[]{:S(2)}) collective-permute-start(bf16[512,768]{1,0:T(8,128)(2,1)} %collective-permute-done.4.refs_5_), channel_id=1, source_target_pairs={{0,1},{1,2},{2,3},{3,0},{4,5},{5,6},{6,7},{7,4},{8,9},{9,10},{10,1... | collective-permute-start | bytes 2359304 | tf_op jit(solution)/shard_map/ppermute | solution.py:490
  55.9 19.8 %collective-permute-start.6 = (bf16[512,768]{1,0:T(8,128)(2,1)}, bf16[512,768]{1,0:T(8,128)(2,1)}, u32[]{:S(2)}, u32[]{:S(2)}) collective-permute-start(bf16[512,768]{1,0:T(8,128)(2,1)} %collective-permute-done.5.refs_6_), channel_id=1, source_target_pairs={{0,1},{1,2},{2,3},{3,0},{4,5},{5,6},{6,7},{7,4},{8,9},{9,10},{10,1... | collective-permute-start | bytes 2359304 | tf_op jit(solution)/shard_map/ppermute | solution.py:490
  59.4 56.6 %collective-permute-start.3 = (bf16[512,2048]{1,0:T(8,128)(2,1)}, bf16[512,2048]{1,0:T(8,128)(2,1)}, u32[]{:S(2)}, u32[]{:S(2)}) collective-permute-start(bf16[512,2048]{1,0:T(8,128)(2,1)} %fusion.2), channel_id=1, source_target_pairs={{0,4},{4,0},{8,12},{12,8},{16,20},{20,16},{24,28},{28,24},{1,5},{5... | collective-permute-start | bytes 6291464 | tf_op jit(solution)/shard_map/ppermute | solution.py:33
  75.8 171.3 %all-gather.6.cloned.1.call-start = ((), (), s32[]{:S(2)}) async-start(), calls=%async_computation.6 | async-start | bytes 7208960 | tf_op jit(solution)/shard_map/all_gather | solution.py:499
  75.8 28.9 %collective-permute-start.7 = (s32[1,512]{1,0:T(1,128)S(1)}, s32[1,512]{1,0:T(1,128)S(1)}, u32[]{:S(2)}, u32[]{:S(2)}) collective-permute-start(s32[1,512]{1,0:T(1,128)S(1)} %copy-done.85), channel_id=1, source_target_pairs={{0,4},{4,0},{8,12},{12,8},{16,20},{20,16},{24,28},{28,24},{1,5},{5... | collective-permute-start | bytes 6152 | tf_op jit(solution)/shard_map/ppermute | solution.py:33
  75.9 20.2 %collective-permute-start.8 = (bf16[512,768]{1,0:T(8,128)(2,1)}, bf16[512,768]{1,0:T(8,128)(2,1)S(1)}, u32[]{:S(2)}, u32[]{:S(2)}) collective-permute-start(bf16[512,768]{1,0:T(8,128)(2,1)} %collective-permute-done.4.refs_5_), channel_id=1, source_target_pairs={{0,8},{4,12},{8,0},{12,4},{16,24},{20,28},{24,16},{28,20},{1,9},{5... | collective-permute-start | bytes 2359304 | tf_op jit(solution)/shard_map/ppermute | solution.py:33
  79.2 20.7 %collective-permute-start.11 = (bf16[512,768]{1,0:T(8,128)(2,1)}, bf16[512,768]{1,0:T(8,128)(2,1)}, u32[]{:S(2)}, u32[]{:S(2)}) collective-permute-start(bf16[512,768]{1,0:T(8,128)(2,1)} %collective-permute-done.4.refs_5_), channel_id=1, source_target_pairs={{0,16},{4,20},{8,24},{12,28},{16,0},{20,4},{24,8},{28,12},{1,17},{... | collective-permute-start | bytes 2359304 | tf_op jit(solution)/shard_map/ppermute | solution.py:33
  104.2 26.7 %collective-permute-start.9 = (bf16[512,768]{1,0:T(8,128)(2,1)}, bf16[512,768]{1,0:T(8,128)(2,1)}, u32[]{:S(2)}, u32[]{:S(2)}) collective-permute-start(bf16[512,768]{1,0:T(8,128)(2,1)} %collective-permute-done.5.refs_6_), channel_id=1, source_target_pairs={{0,8},{4,12},{8,0},{12,4},{16,24},{20,28},{24,16},{28,20},{1,9},{5... | collective-permute-start | bytes 2359304 | tf_op jit(solution)/shard_map/ppermute | solution.py:33
  104.7 28.3 %collective-permute-start.12 = (bf16[512,768]{1,0:T(8,128)(2,1)}, bf16[512,768]{1,0:T(8,128)(2,1)}, u32[]{:S(2)}, u32[]{:S(2)}) collective-permute-start(bf16[512,768]{1,0:T(8,128)(2,1)} %collective-permute-done.5.refs_6_), channel_id=1, source_target_pairs={{0,16},{4,20},{8,24},{12,28},{16,0},{20,4},{24,8},{28,12},{1,17},{... | collective-permute-start | bytes 2359304 | tf_op jit(solution)/shard_map/ppermute | solution.py:33
  106.0 225.4 %all-gather.8.cloned.1.call-start = ((), (), s32[]{:S(2)}) async-start(), calls=%async_computation.7 | async-start | bytes 3604480 | tf_op jit(solution)/shard_map/all_gather | solution.py:501
  113.9 40.6 %collective-permute-start.10 = (bf16[512,768]{1,0:T(8,128)(2,1)}, bf16[512,768]{1,0:T(8,128)(2,1)S(1)}, u32[]{:S(2)}, u32[]{:S(2)}) collective-permute-start(bf16[512,768]{1,0:T(8,128)(2,1)} %collective-permute-done.6.refs_7_), channel_id=1, source_target_pairs={{0,8},{4,12},{8,0},{12,4},{16,24},{20,28},{24,16},{28,20},{1,9},{5... | collective-permute-start | bytes 2359304 | tf_op jit(solution)/shard_map/ppermute | solution.py:33
  115.5 40.2 %collective-permute-start.13 = (bf16[512,768]{1,0:T(8,128)(2,1)}, bf16[512,768]{1,0:T(8,128)(2,1)S(1)}, u32[]{:S(2)}, u32[]{:S(2)}) collective-permute-start(bf16[512,768]{1,0:T(8,128)(2,1)} %collective-permute-done.6.refs_7_), channel_id=1, source_target_pairs={{0,16},{4,20},{8,24},{12,28},{16,0},{20,4},{24,8},{28,12},{1,17},{... | collective-permute-start | bytes 2359304 | tf_op jit(solution)/shard_map/ppermute | solution.py:33
  131.9 18.1 %collective-permute-start.16 = (bf16[256,768]{1,0:T(8,128)(2,1)S(1)}, bf16[256,768]{1,0:T(8,128)(2,1)S(1)}, u32[]{:S(2)}, u32[]{:S(2)}) collective-permute-start(bf16[256,768]{1,0:T(8,128)(2,1)S(1)} %slice.281), channel_id=1, source_target_pairs={{0,16},{4,20},{8,24},{12,28},{16,0},{20,4},{24,8},{28,12},{1,17},{... | collective-permute-start | bytes 1179656 | tf_op jit(solution)/shard_map/ppermute | solution.py:33
  134.0 20.5 %collective-permute-start.17 = (bf16[256,768]{1,0:T(8,128)(2,1)S(1)}, bf16[256,768]{1,0:T(8,128)(2,1)S(1)}, u32[]{:S(2)}, u32[]{:S(2)}) collective-permute-start(bf16[256,768]{1,0:T(8,128)(2,1)S(1)} %slice.282), channel_id=1, source_target_pairs={{0,8},{4,12},{8,0},{12,4},{16,24},{20,28},{24,16},{28,20},{1,9},{5... | collective-permute-start | bytes 1179656 | tf_op jit(solution)/shard_map/ppermute | solution.py:33
  154.6 26.3 %collective-permute-start.18 = (bf16[256,768]{1,0:T(8,128)(2,1)S(1)}, bf16[256,768]{1,0:T(8,128)(2,1)S(1)}, u32[]{:S(2)}, u32[]{:S(2)}) collective-permute-start(bf16[256,768]{1,0:T(8,128)(2,1)S(1)} %slice.283), channel_id=1, source_target_pairs={{0,16},{4,20},{8,24},{12,28},{16,0},{20,4},{24,8},{28,12},{1,17},{... | collective-permute-start | bytes 1179656 | tf_op jit(solution)/shard_map/ppermute | solution.py:33
  155.7 25.2 %collective-permute-start.19 = (bf16[256,768]{1,0:T(8,128)(2,1)S(1)}, bf16[256,768]{1,0:T(8,128)(2,1)S(1)}, u32[]{:S(2)}, u32[]{:S(2)}) collective-permute-start(bf16[256,768]{1,0:T(8,128)(2,1)S(1)} %slice.284), channel_id=1, source_target_pairs={{0,8},{4,12},{8,0},{12,4},{16,24},{20,28},{24,16},{28,20},{1,9},{5... | collective-permute-start | bytes 1179656 | tf_op jit(solution)/shard_map/ppermute | solution.py:33
  168.0 23.2 %collective-permute-start.20 = (bf16[256,2048]{1,0:T(8,128)(2,1)S(1)}, bf16[256,2048]{1,0:T(8,128)(2,1)S(1)}, u32[]{:S(2)}, u32[]{:S(2)}) collective-permute-start(bf16[256,2048]{1,0:T(8,128)(2,1)S(1)} %copy-done.17), channel_id=1, source_target_pairs={{0,8},{4,12},{8,0},{12,4},{16,24},{20,28},{24,16},{28,20},{1,9},{5... | collective-permute-start | bytes 3145736 | tf_op jit(solution)/shard_map/ppermute | solution.py:33
  179.7 26.2 %collective-permute-start.21 = (bf16[256,2048]{1,0:T(8,128)(2,1)S(1)}, bf16[256,2048]{1,0:T(8,128)(2,1)S(1)}, u32[]{:S(2)}, u32[]{:S(2)}) collective-permute-start(bf16[256,2048]{1,0:T(8,128)(2,1)S(1)} %copy-done.17), channel_id=1, source_target_pairs={{0,16},{4,20},{8,24},{12,28},{16,0},{20,4},{24,8},{28,12},{1,17},{... | collective-permute-start | bytes 3145736 | tf_op jit(solution)/shard_map/ppermute | solution.py:33
  191.2 22.7 %collective-permute-start.22 = (bf16[128,2048]{1,0:T(8,128)(2,1)S(1)}, bf16[128,2048]{1,0:T(8,128)(2,1)S(1)}, u32[]{:S(2)}, u32[]{:S(2)}) collective-permute-start(bf16[128,2048]{1,0:T(8,128)(2,1)S(1)} %slice.285), channel_id=1, source_target_pairs={{0,16},{4,20},{8,24},{12,28},{16,0},{20,4},{24,8},{28,12},{1,17},{... | collective-permute-start | bytes 1572872 | tf_op jit(solution)/shard_map/ppermute | solution.py:33
  220.9 21.3 %collective-permute-start.24 = (bf16[512,2048]{1,0:T(8,128)(2,1)S(1)}, bf16[512,2048]{1,0:T(8,128)(2,1)S(1)}, u32[]{:S(2)}, u32[]{:S(2)}) collective-permute-start(bf16[512,2048]{1,0:T(8,128)(2,1)S(1)} %slice.375), channel_id=1, source_target_pairs={{0,4},{4,0},{8,12},{12,8},{16,20},{20,16},{24,28},{28,24},{1,5},{5... | collective-permute-start | bytes 6291464 | tf_op jit(solution)/shard_map/ppermute | solution.py:33
  256.2 18.0 %collective-permute-start.41 = (bf16[512,2048]{1,0:T(8,128)(2,1)}, bf16[512,2048]{1,0:T(8,128)(2,1)}, u32[]{:S(2)}, u32[]{:S(2)}) collective-permute-start(bf16[512,2048]{1,0:T(8,128)(2,1)} %get-tuple-element.152), channel_id=1, source_target_pairs={{0,4},{4,0},{8,12},{12,8},{16,20},{20,16},{24,28},{28,24},{1,5},{5... | collective-permute-start | bytes 6291464 | tf_op jit(solution)/shard_map/ppermute | solution.py:33
  274.1 283.0 %reduce-scatter.6.cloned.1.call-start = ((), (), s32[]{:S(2)}) async-start(), calls=%async_computation.8 | async-start | bytes 3604480 | tf_op jit(solution)/shard_map/reduce_scatter | solution.py:572
  398.6 158.6 %reduce-scatter.8.cloned.1.call-start = ((), (), s32[]{:S(2)}) async-start(), calls=%async_computation.9 | async-start | bytes 3604480 | tf_op jit(solution)/shard_map/reduce_scatter | solution.py:572
  399.2 171.3 %reduce-scatter.10.cloned.1.call-start = ((), (), s32[]{:S(2)}) async-start(), calls=%async_computation.10 | async-start | bytes 3604480 | tf_op jit(solution)/shard_map/reduce_scatter | solution.py:572
  404.2 199.5 %reduce-scatter.12.cloned.1.call-start = ((), (), s32[]{:S(2)}) async-start(), calls=%async_computation.11 | async-start | bytes 1310720 | tf_op jit(solution)/shard_map/reduce_scatter | solution.py:577
  429.8 81.2 %collective-permute-start.60 = (bf16[1024,768]{1,0:T(8,128)(2,1)}, bf16[1024,768]{1,0:T(8,128)(2,1)}, u32[]{:S(2)}, u32[]{:S(2)}) collective-permute-start(bf16[1024,768]{1,0:T(8,128)(2,1)} %get-tuple-element.90), channel_id=1, source_target_pairs={{0,16},{4,20},{8,24},{12,28},{16,0},{20,4},{24,8},{28,12},{1,17},{... | collective-permute-start | bytes 4718600 | tf_op jit(solution)/shard_map/ppermute | solution.py:33
  439.7 21.7 %collective-permute-start.64 = (bf16[128,2048]{1,0:T(8,128)(2,1)}, bf16[128,2048]{1,0:T(8,128)(2,1)}, u32[]{:S(2)}, u32[]{:S(2)}) collective-permute-start(bf16[128,2048]{1,0:T(8,128)(2,1)} %get-tuple-element.115), channel_id=1, source_target_pairs={{0,8},{4,12},{8,0},{12,4},{16,24},{20,28},{24,16},{28,20},{1,9},{5... | collective-permute-start | bytes 1572872 | tf_op jit(solution)/shard_map/ppermute | solution.py:33
  458.8 56.2 %collective-permute-start.58 = (bf16[1024,768]{1,0:T(8,128)(2,1)S(1)}, bf16[1024,768]{1,0:T(8,128)(2,1)}, u32[]{:S(2)}, u32[]{:S(2)}) collective-permute-start(bf16[1024,768]{1,0:T(8,128)(2,1)S(1)} %get-tuple-element.87), channel_id=1, source_target_pairs={{0,8},{4,12},{8,0},{12,4},{16,24},{20,28},{24,16},{28,20},{1,9},{5... | collective-permute-start | bytes 4718600 | tf_op jit(solution)/shard_map/ppermute | solution.py:33
  460.1 46.1 %collective-permute-start.63 = (bf16[128,2048]{1,0:T(8,128)(2,1)}, bf16[128,2048]{1,0:T(8,128)(2,1)S(1)}, u32[]{:S(2)}, u32[]{:S(2)}) collective-permute-start(bf16[128,2048]{1,0:T(8,128)(2,1)} %get-tuple-element.112), channel_id=1, source_target_pairs={{0,8},{4,12},{8,0},{12,4},{16,24},{20,28},{24,16},{28,20},{1,9},{5... | collective-permute-start | bytes 1572872 | tf_op jit(solution)/shard_map/ppermute | solution.py:33
  460.8 46.3 %collective-permute-start.66 = (bf16[128,2048]{1,0:T(8,128)(2,1)}, bf16[128,2048]{1,0:T(8,128)(2,1)S(1)}, u32[]{:S(2)}, u32[]{:S(2)}) collective-permute-start(bf16[128,2048]{1,0:T(8,128)(2,1)} %get-tuple-element.114), channel_id=1, source_target_pairs={{0,16},{4,20},{8,24},{12,28},{16,0},{20,4},{24,8},{28,12},{1,17},{... | collective-permute-start | bytes 1572872 | tf_op jit(solution)/shard_map/ppermute | solution.py:33
  463.5 44.6 %collective-permute-start.65 = (bf16[128,2048]{1,0:T(8,128)(2,1)}, bf16[128,2048]{1,0:T(8,128)(2,1)}, u32[]{:S(2)}, u32[]{:S(2)}) collective-permute-start(bf16[128,2048]{1,0:T(8,128)(2,1)} %add_convert_fusion.10), channel_id=1, source_target_pairs={{0,16},{4,20},{8,24},{12,28},{16,0},{20,4},{24,8},{28,12},{1,17},{... | collective-permute-start | bytes 1572872 | tf_op jit(solution)/shard_map/ppermute | solution.py:33
  506.1 89.6 %collective-permute-start.62 = (bf16[1024,768]{1,0:T(8,128)(2,1)}, bf16[1024,768]{1,0:T(8,128)(2,1)}, u32[]{:S(2)}, u32[]{:S(2)}) collective-permute-start(bf16[1024,768]{1,0:T(8,128)(2,1)} %get-tuple-element.91), channel_id=1, source_target_pairs={{0,16},{4,20},{8,24},{12,28},{16,0},{20,4},{24,8},{28,12},{1,17},{... | collective-permute-start | bytes 4718600 | tf_op jit(solution)/shard_map/ppermute | solution.py:33
  507.1 92.2 %collective-permute-start.57 = (bf16[1024,768]{1,0:T(8,128)(2,1)}, bf16[1024,768]{1,0:T(8,128)(2,1)}, u32[]{:S(2)}, u32[]{:S(2)}) collective-permute-start(bf16[1024,768]{1,0:T(8,128)(2,1)} %get-tuple-element.85), channel_id=1, source_target_pairs={{0,8},{4,12},{8,0},{12,4},{16,24},{20,28},{24,16},{28,20},{1,9},{5... | collective-permute-start | bytes 4718600 | tf_op jit(solution)/shard_map/ppermute | solution.py:33
  508.1 44.9 %collective-permute-start.68 = (bf16[128,2048]{1,0:T(8,128)(2,1)}, bf16[128,2048]{1,0:T(8,128)(2,1)S(1)}, u32[]{:S(2)}, u32[]{:S(2)}) collective-permute-start(bf16[128,2048]{1,0:T(8,128)(2,1)} %get-tuple-element.113), channel_id=1, source_target_pairs={{0,16},{4,20},{8,24},{12,28},{16,0},{20,4},{24,8},{28,12},{1,17},{... | collective-permute-start | bytes 1572872 | tf_op jit(solution)/shard_map/ppermute | solution.py:33
  511.0 44.9 %collective-permute-start.67 = (bf16[128,2048]{1,0:T(8,128)(2,1)S(1)}, bf16[128,2048]{1,0:T(8,128)(2,1)S(1)}, u32[]{:S(2)}, u32[]{:S(2)}) collective-permute-start(bf16[128,2048]{1,0:T(8,128)(2,1)S(1)} %get-tuple-element.111), channel_id=1, source_target_pairs={{0,8},{4,12},{8,0},{12,4},{16,24},{20,28},{24,16},{28,20},{1,9},{5... | collective-permute-start | bytes 1572872 | tf_op jit(solution)/shard_map/ppermute | solution.py:33
  514.9 80.9 %collective-permute-start.61 = (bf16[1024,768]{1,0:T(8,128)(2,1)}, bf16[1024,768]{1,0:T(8,128)(2,1)}, u32[]{:S(2)}, u32[]{:S(2)}) collective-permute-start(bf16[1024,768]{1,0:T(8,128)(2,1)} %add_convert_fusion.4), channel_id=1, source_target_pairs={{0,8},{4,12},{8,0},{12,4},{16,24},{20,28},{24,16},{28,20},{1,9},{5... | collective-permute-start | bytes 4718600 | tf_op jit(solution)/shard_map/ppermute | solution.py:33
  553.0 46.4 %collective-permute-start.59 = (bf16[1024,768]{1,0:T(8,128)(2,1)}, bf16[1024,768]{1,0:T(8,128)(2,1)}, u32[]{:S(2)}, u32[]{:S(2)}) collective-permute-start(bf16[1024,768]{1,0:T(8,128)(2,1)} %add_convert_fusion.6), channel_id=1, source_target_pairs={{0,16},{4,20},{8,24},{12,28},{16,0},{20,4},{24,8},{28,12},{1,17},{... | collective-permute-start | bytes 4718600 | tf_op jit(solution)/shard_map/ppermute | solution.py:33
  570.5 119.6 %reduce-scatter.14.cloned.1.call-start = ((), (), s32[]{:S(2)}) async-start(), calls=%async_computation.12 | async-start | bytes 3932160 | tf_op jit(solution)/shard_map/reduce_scatter | solution.py:580
  577.9 50.8 %collective-permute-start.30 = (bf16[512,2048]{1,0:T(8,128)(2,1)}, bf16[512,2048]{1,0:T(8,128)(2,1)}, u32[]{:S(2)}, u32[]{:S(2)}) collective-permute-start(bf16[512,2048]{1,0:T(8,128)(2,1)} %slice.295), channel_id=1, source_target_pairs={{0,4},{4,0},{8,12},{12,8},{16,20},{20,16},{24,28},{28,24},{1,5},{5... | collective-permute-start | bytes 6291464 | tf_op jit(solution)/shard_map/ppermute | solution.py:33
  654.6 19.1 %collective-permute-start.79 = (bf16[704,512]{1,0:T(8,128)(2,1)S(1)}, bf16[704,512]{1,0:T(8,128)(2,1)S(1)}, u32[]{:S(2)}, u32[]{:S(2)}) collective-permute-start(bf16[704,512]{1,0:T(8,128)(2,1)S(1)} %copy-done.62), channel_id=1, source_target_pairs={{0,8},{4,12},{8,0},{12,4},{16,24},{20,28},{24,16},{28,20},{1,9},{5... | collective-permute-start | bytes 2162696 | tf_op jit(solution)/shard_map/ppermute | solution.py:33
  656.1 22.3 %collective-permute-start.80 = (bf16[704,512]{1,0:T(8,128)(2,1)S(1)}, bf16[704,512]{1,0:T(8,128)(2,1)S(1)}, u32[]{:S(2)}, u32[]{:S(2)}) collective-permute-start(bf16[704,512]{1,0:T(8,128)(2,1)S(1)} %copy-done.62), channel_id=1, source_target_pairs={{0,16},{4,20},{8,24},{12,28},{16,0},{20,4},{24,8},{28,12},{1,17},{... | collective-permute-start | bytes 2162696 | tf_op jit(solution)/shard_map/ppermute | solution.py:33
  657.5 31.6 %collective-permute-start.84 = (bf16[704,512]{1,0:T(8,128)(2,1)}, bf16[704,512]{1,0:T(8,128)(2,1)S(1)}, u32[]{:S(2)}, u32[]{:S(2)}) collective-permute-start(bf16[704,512]{1,0:T(8,128)(2,1)} %reduce-scatter.8.cloned.1.call-done), channel_id=1, source_target_pairs={{0,8},{4,12},{8,0},{12,4},{16,24},{20,28},{24,16},{28,20},{1,9},{5... | collective-permute-start | bytes 2162696 | tf_op jit(solution)/shard_map/ppermute | solution.py:33
  659.0 32.6 %collective-permute-start.85 = (bf16[704,512]{1,0:T(8,128)(2,1)}, bf16[704,512]{1,0:T(8,128)(2,1)}, u32[]{:S(2)}, u32[]{:S(2)}) collective-permute-start(bf16[704,512]{1,0:T(8,128)(2,1)} %reduce-scatter.8.cloned.1.call-done), channel_id=1, source_target_pairs={{0,16},{4,20},{8,24},{12,28},{16,0},{20,4},{24,8},{28,12},{1,17},{... | collective-permute-start | bytes 2162696 | tf_op jit(solution)/shard_map/ppermute | solution.py:33
  660.6 44.0 %collective-permute-start.89 = (bf16[704,512]{1,0:T(8,128)(2,1)}, bf16[704,512]{1,0:T(8,128)(2,1)}, u32[]{:S(2)}, u32[]{:S(2)}) collective-permute-start(bf16[704,512]{1,0:T(8,128)(2,1)} %reduce-scatter.10.cloned.1.call-done), channel_id=1, source_target_pairs={{0,8},{4,12},{8,0},{12,4},{16,24},{20,28},{24,16},{28,20},{1,9},{5... | collective-permute-start | bytes 2162696 | tf_op jit(solution)/shard_map/ppermute | solution.py:33
  673.7 33.5 %collective-permute-start.90 = (bf16[704,512]{1,0:T(8,128)(2,1)}, bf16[704,512]{1,0:T(8,128)(2,1)}, u32[]{:S(2)}, u32[]{:S(2)}) collective-permute-start(bf16[704,512]{1,0:T(8,128)(2,1)} %reduce-scatter.10.cloned.1.call-done), channel_id=1, source_target_pairs={{0,16},{4,20},{8,24},{12,28},{16,0},{20,4},{24,8},{28,12},{1,17},{... | collective-permute-start | bytes 2162696 | tf_op jit(solution)/shard_map/ppermute | solution.py:33
  678.4 35.5 %collective-permute-start.81 = (bf16[352,512]{1,0:T(8,128)(2,1)S(1)}, bf16[352,512]{1,0:T(8,128)(2,1)}, u32[]{:S(2)}, u32[]{:S(2)}) collective-permute-start(bf16[352,512]{1,0:T(8,128)(2,1)S(1)} %slice.332), channel_id=1, source_target_pairs={{0,16},{4,20},{8,24},{12,28},{16,0},{20,4},{24,8},{28,12},{1,17},{... | collective-permute-start | bytes 1081352 | tf_op jit(solution)/shard_map/ppermute | solution.py:33
  690.1 49.6 %collective-permute-start.69 = (bf16[512,768]{1,0:T(8,128)(2,1)}, bf16[512,768]{1,0:T(8,128)(2,1)S(1)}, u32[]{:S(2)}, u32[]{:S(2)}) collective-permute-start(bf16[512,768]{1,0:T(8,128)(2,1)} %reduce-scatter.14.cloned.1.call-done), channel_id=1, source_target_pairs={{0,8},{4,12},{8,0},{12,4},{16,24},{20,28},{24,16},{28,20},{1,9},{5... | collective-permute-start | bytes 2359304 | tf_op jit(solution)/shard_map/ppermute | solution.py:33
  691.6 49.6 %collective-permute-start.70 = (bf16[512,768]{1,0:T(8,128)(2,1)}, bf16[512,768]{1,0:T(8,128)(2,1)S(1)}, u32[]{:S(2)}, u32[]{:S(2)}) collective-permute-start(bf16[512,768]{1,0:T(8,128)(2,1)} %reduce-scatter.14.cloned.1.call-done), channel_id=1, source_target_pairs={{0,16},{4,20},{8,24},{12,28},{16,0},{20,4},{24,8},{28,12},{1,17},{... | collective-permute-start | bytes 2359304 | tf_op jit(solution)/shard_map/ppermute | solution.py:33
  704.7 24.5 %collective-permute-start.82 = (bf16[352,512]{1,0:T(8,128)(2,1)S(1)}, bf16[352,512]{1,0:T(8,128)(2,1)S(1)}, u32[]{:S(2)}, u32[]{:S(2)}) collective-permute-start(bf16[352,512]{1,0:T(8,128)(2,1)S(1)} %slice.333), channel_id=1, source_target_pairs={{0,8},{4,12},{8,0},{12,4},{16,24},{20,28},{24,16},{28,20},{1,9},{5... | collective-permute-start | bytes 1081352 | tf_op jit(solution)/shard_map/ppermute | solution.py:33
  707.2 31.2 %collective-permute-start.86 = (bf16[352,512]{1,0:T(8,128)(2,1)S(1)}, bf16[352,512]{1,0:T(8,128)(2,1)S(1)}, u32[]{:S(2)}, u32[]{:S(2)}) collective-permute-start(bf16[352,512]{1,0:T(8,128)(2,1)S(1)} %slice.334), channel_id=1, source_target_pairs={{0,16},{4,20},{8,24},{12,28},{16,0},{20,4},{24,8},{28,12},{1,17},{... | collective-permute-start | bytes 1081352 | tf_op jit(solution)/shard_map/ppermute | solution.py:33
  713.9 25.0 %collective-permute-start.87 = (bf16[352,512]{1,0:T(8,128)(2,1)S(1)}, bf16[352,512]{1,0:T(8,128)(2,1)S(1)}, u32[]{:S(2)}, u32[]{:S(2)}) collective-permute-start(bf16[352,512]{1,0:T(8,128)(2,1)S(1)} %slice.335), channel_id=1, source_target_pairs={{0,8},{4,12},{8,0},{12,4},{16,24},{20,28},{24,16},{28,20},{1,9},{5... | collective-permute-start | bytes 1081352 | tf_op jit(solution)/shard_map/ppermute | solution.py:33
  729.2 40.5 %collective-permute-start.36 = (bf16[64,2048]{1,0:T(8,128)(2,1)S(1)}, bf16[64,2048]{1,0:T(8,128)(2,1)S(1)}, u32[]{:S(2)}, u32[]{:S(2)}) collective-permute-start(bf16[64,2048]{1,0:T(8,128)(2,1)S(1)} %copy-done.66), channel_id=1, source_target_pairs={{0,16},{4,20},{8,24},{12,28},{16,0},{20,4},{24,8},{28,12},{1,17},{... | collective-permute-start | bytes 786440 | tf_op jit(solution)/shard_map/ppermute | solution.py:33
  738.4 31.3 %collective-permute-start.35 = (bf16[64,2048]{1,0:T(8,128)(2,1)S(1)}, bf16[64,2048]{1,0:T(8,128)(2,1)S(1)}, u32[]{:S(2)}, u32[]{:S(2)}) collective-permute-start(bf16[64,2048]{1,0:T(8,128)(2,1)S(1)} %copy-done.64), channel_id=1, source_target_pairs={{0,8},{4,12},{8,0},{12,4},{16,24},{20,28},{24,16},{28,20},{1,9},{5... | collective-permute-start | bytes 786440 | tf_op jit(solution)/shard_map/ppermute | solution.py:33
  739.0 23.6 %collective-permute-start.91 = (bf16[352,512]{1,0:T(8,128)(2,1)S(1)}, bf16[352,512]{1,0:T(8,128)(2,1)S(1)}, u32[]{:S(2)}, u32[]{:S(2)}) collective-permute-start(bf16[352,512]{1,0:T(8,128)(2,1)S(1)} %slice.336), channel_id=1, source_target_pairs={{0,16},{4,20},{8,24},{12,28},{16,0},{20,4},{24,8},{28,12},{1,17},{... | collective-permute-start | bytes 1081352 | tf_op jit(solution)/shard_map/ppermute | solution.py:33
  739.7 18.5 %collective-permute-start.71 = (bf16[256,768]{1,0:T(8,128)(2,1)S(1)}, bf16[256,768]{1,0:T(8,128)(2,1)S(1)}, u32[]{:S(2)}, u32[]{:S(2)}) collective-permute-start(bf16[256,768]{1,0:T(8,128)(2,1)S(1)} %slice.327), channel_id=1, source_target_pairs={{0,16},{4,20},{8,24},{12,28},{16,0},{20,4},{24,8},{28,12},{1,17},{... | collective-permute-start | bytes 1179656 | tf_op jit(solution)/shard_map/ppermute | solution.py:33
  741.2 18.3 %collective-permute-start.72 = (bf16[256,768]{1,0:T(8,128)(2,1)S(1)}, bf16[256,768]{1,0:T(8,128)(2,1)S(1)}, u32[]{:S(2)}, u32[]{:S(2)}) collective-permute-start(bf16[256,768]{1,0:T(8,128)(2,1)S(1)} %slice.328), channel_id=1, source_target_pairs={{0,8},{4,12},{8,0},{12,4},{16,24},{20,28},{24,16},{28,20},{1,9},{5... | collective-permute-start | bytes 1179656 | tf_op jit(solution)/shard_map/ppermute | solution.py:33
  762.6 76.2 %collective-permute-start.73 = (bf16[2048,768]{1,0:T(8,128)(2,1)}, bf16[2048,768]{1,0:T(8,128)(2,1)}, u32[]{:S(2)}, u32[]{:S(2)}) collective-permute-start(bf16[2048,768]{1,0:T(8,128)(2,1)} %constant_dynamic-update-slice_fusion.45.same_ref), channel_id=1, source_target_pairs={{0,4},{4,0},{8,12},{12,8},{16,20},{20,16},{24,28},{28,24},{1,5},{5... | collective-permute-start | bytes 9437192 | tf_op jit(solution)/shard_map/ppermute | solution.py:33
  769.6 44.0 %collective-permute-start.83 = (bf16[2816,512]{1,0:T(8,128)(2,1)}, bf16[2816,512]{1,0:T(8,128)(2,1)}, u32[]{:S(2)}, u32[]{:S(2)}) collective-permute-start(bf16[2816,512]{1,0:T(8,128)(2,1)} %constant_dynamic-update-slice_fusion.55.same_ref), channel_id=1, source_target_pairs={{0,4},{4,0},{8,12},{12,8},{16,20},{20,16},{24,28},{28,24},{1,5},{5... | collective-permute-start | bytes 8650760 | tf_op jit(solution)/shard_map/ppermute | solution.py:33
  769.7 51.8 %collective-permute-start.88 = (bf16[2816,512]{1,0:T(8,128)(2,1)S(1)}, bf16[2816,512]{1,0:T(8,128)(2,1)}, u32[]{:S(2)}, u32[]{:S(2)}) collective-permute-start(bf16[2816,512]{1,0:T(8,128)(2,1)S(1)} %constant_dynamic-update-slice_fusion.60.same_ref), channel_id=1, source_target_pairs={{0,4},{4,0},{8,12},{12,8},{16,20},{20,16},{24,28},{28,24},{1,5},{5... | collective-permute-start | bytes 8650760 | tf_op jit(solution)/shard_map/ppermute | solution.py:33
  770.2 58.1 %collective-permute-start.93 = (bf16[2816,512]{1,0:T(8,128)(2,1)}, bf16[2816,512]{1,0:T(8,128)(2,1)}, u32[]{:S(2)}, u32[]{:S(2)}) collective-permute-start(bf16[2816,512]{1,0:T(8,128)(2,1)} %constant_dynamic-update-slice_fusion.65.same_ref), channel_id=1, source_target_pairs={{0,4},{4,0},{8,12},{12,8},{16,20},{20,16},{24,28},{28,24},{1,5},{5... | collective-permute-start | bytes 8650760 | tf_op jit(solution)/shard_map/ppermute | solution.py:33
  (127 other events, 1624.6 us)
Sparse Core Ops, SparseCore 0:
  75.9 25.6 all-gather.3
  106.1 104.4 all-gather.5
  274.3 57.0 all-gather.7
  398.7 54.1 reduce-scatter.5
  455.6 56.0 reduce-scatter.7
  514.4 56.0 reduce-scatter.9
  572.8 26.9 reduce-scatter.11
  603.8 60.0 reduce-scatter.13

commit v3 on v2

--- a/solution.py
+++ b/solution.py
@@ -45,65 +45,137 @@
     return list(range(0, lax.axis_size("rep"), 2))
 
 
-def gather_chips(value):
+def add(left, right):
+    return left.astype(F32) + right.astype(F32)
+
+
+def halves(value):
+    half = value.shape[0] // 2
+    return value[:half], value[half:]
+
+
+class Flow:
+    def __init__(self, steps):
+        self.steps, self.result, self.done = steps, None, False
+        self.pending = next(steps)
+
+    def advance(self, arrived):
+        try:
+            self.pending = self.steps.send(arrived)
+        except StopIteration as end:
+            self.pending, self.result, self.done = [], end.value, True
+
+
+def stage(flows, extra=()):
+    flows = [f for f in flows if not f.done]
+    arrived, extra = lax.optimization_barrier(([f.pending for f in flows], extra))
+    for flow, values in zip(flows, arrived):
+        flow.advance(values)
+    return extra
+
+
+def finish(flow):
+    while not flow.done:
+        flow.advance(flow.pending)
+    return flow.result
+
+
+def gather_steps(value, sink=lambda offset, block: None):
     bits = chip_bits()
     if len(bits) == 2:
         one, two = bits
         half = value.shape[0] // 2
-        by_one, by_two = swap(value, one), swap(value, two)
-        far = jnp.concatenate([swap(by_one[:half], two), swap(by_two[half:], one)], axis=0)
+        by_one, by_two = yield [swap(value, one), swap(value, two)]
+        sink(one, by_one)
+        sink(two, by_two)
+        top, bottom = yield [swap(by_one[:half], two), swap(by_two[half:], one)]
+        far = jnp.concatenate([top, bottom], axis=0)
+        sink(one ^ two, far)
         return {0: value, one: by_one, two: by_two, one ^ two: far}
     blocks = {0: value}
     for bit in bits:
-        blocks.update({d ^ bit: swap(b, bit) for d, b in list(blocks.items())})
+        old = list(blocks.items())
+        new = yield [swap(b, bit) for _, b in old]
+        for (d, _), b in zip(old, new):
+            blocks[d ^ bit] = b
+            sink(d ^ bit, b)
     return blocks
 
 
-def add(left, right):
-    return left.astype(F32) + right.astype(F32)
-
-
-def scatter_chips(blocks):
+def copies_steps(value):
+    blocks = yield from gather_steps(value)
+    same = jnp.concatenate([blocks[d] for d in chip_offsets()], axis=0)
+    (other,) = yield [swap(same, 1)]
+    return same, other
+
+
+def scatter_steps(blocks):
     bits = chip_bits()
     if len(bits) == 2:
         one, two = bits
         far = blocks[one ^ two]
+        top, bottom = yield [swap(far[0], one), swap(far[1], two)]
         near_one, near_two = blocks[one], blocks[two]
-        top, bottom = swap(far[0], one), swap(far[1], two)
-        one_top, two_bottom = swap(near_one[0], one), swap(near_two[1], two)
-        two_top = swap(add(near_two[0], top).astype(BF), two)
-        one_bottom = swap(add(near_one[1], bottom).astype(BF), one)
+        one_top, two_bottom = yield [swap(near_one[0], one), swap(near_two[1], two)]
+        two_top, one_bottom = yield [
+            swap(add(near_two[0], top).astype(BF), two),
+            swap(add(near_one[1], bottom).astype(BF), one),
+        ]
         return jnp.concatenate(
             [
-                blocks[0][0].astype(F32) + one_top.astype(F32) + two_top.astype(F32),
-                blocks[0][1].astype(F32) + one_bottom.astype(F32) + two_bottom.astype(F32),
+                (add(blocks[0][0], one_top) + two_top.astype(F32)).astype(BF),
+                (add(blocks[0][1], one_bottom) + two_bottom.astype(F32)).astype(BF),
             ],
             axis=0,
         )
-    blocks = {d: jnp.concatenate(b, axis=0) for d, b in blocks.items()}
+    while len(blocks) < len(chip_offsets()):
+        yield []
+    sums = {d: jnp.concatenate(b, axis=0) for d, b in blocks.items()}
     for bit in reversed(bits):
-        kept = {d: b for d, b in blocks.items() if not d & bit}
-        blocks = {d: add(b, swap(blocks[d | bit], bit)).astype(BF) for d, b in kept.items()}
-    return blocks[0].astype(F32)
-
-
-def halves(value):
-    half = value.shape[0] // 2
-    return value[:half], value[half:]
-
-
-def gather_plane(value):
-    blocks = gather_chips(value)
-    same = jnp.concatenate([blocks[d] for d in chip_offsets()], axis=0)
-    return jnp.concatenate([same, swap(same, 1)], axis=0)
-
-
-def scatter_plane(partial):
+        kept = [d for d in sorted(sums) if not d & bit]
+        new = yield [swap(sums[d | bit], bit) for d in kept]
+        sums = {d: add(sums[d], n).astype(BF) for d, n in zip(kept, new)}
+    return sums[0]
+
+
+def plane_sum_steps(partial):
     half = partial.shape[0] // 2
-    same = add(partial[:half], swap(partial[half:], 1)).astype(BF)
+    (other,) = yield [swap(partial[half:], 1)]
+    same = add(partial[:half], other).astype(BF)
     offsets = chip_offsets()
     rows = half // len(offsets)
-    return scatter_chips({d: halves(same[i * rows : (i + 1) * rows]) for i, d in enumerate(offsets)})
+    blocks = {d: halves(same[i * rows : (i + 1) * rows]) for i, d in enumerate(offsets)}
+    return (yield from scatter_steps(blocks))
+
+
+def vector_sum_steps(rows):
+    size, bit = lax.axis_size("rep"), 1
+    while bit < size:
+        (other,) = yield [swap(rows, bit)]
+        rows, bit = rows + other, 2 * bit
+    shards, at = lax.axis_size("shard"), lax.axis_index("shard")
+    own = rows.shape[1] // shards
+    parts = yield [
+        lax.ppermute(
+            lax.dynamic_slice_in_dim(rows, ((at + k) % shards) * own, own, 1),
+            "shard",
+            [(i, (i + k) % shards) for i in range(shards)],
+        )
+        for k in range(1, shards)
+    ]
+    return lax.dynamic_slice_in_dim(rows, at * own, own, 1) + sum(parts)
+
+
+def vector_gather_steps(rows):
+    size, me = lax.axis_size("shard"), lax.axis_index("shard")
+    others = yield [
+        lax.ppermute(rows, "shard", [(i, (i - k) % size) for i in range(size)])
+        for k in range(1, size)
+    ]
+    parts = [rows, *others]
+    twice = jnp.concatenate(parts + parts, axis=1)
+    own = rows.shape[1]
+    return lax.dynamic_slice_in_dim(twice, ((size - me) % size) * own, size * own, 1)
 
 
 def rotary_tables(length):
@@ -354,41 +426,34 @@
     return grad_gain, root * scaled - source * (root * root * root) * mean
 
 
-def gather_vector(rows):
-    size, me = lax.axis_size("shard"), lax.axis_index("shard")
-    parts = [rows] + [
-        lax.ppermute(rows, "shard", [(i, (i - k) % size) for i in range(size)])
-        for k in range(1, size)
-    ]
-    twice = jnp.concatenate(parts + parts, axis=1)
-    own = rows.shape[1]
-    return lax.dynamic_slice_in_dim(twice, ((size - me) % size) * own, size * own, 1)
-
-
-def place_kernel(me_ref, same_ref, other_ref, out_ref):
+def place_kernel(me_ref, same_ref, other_ref, *out_refs):
     odd = jnp.bitwise_xor(pl.program_id(0), me_ref[0]) % 2
-    out_ref[...] = jnp.where(odd == 0, same_ref[...], other_ref[...]).astype(F32)
-
-
-def place(me, same, other, height, width, group, columns):
-    size = lax.axis_size("rep")
-    spec = pl.BlockSpec(
-        (height, width), lambda j, me: (jnp.bitwise_xor(j, me[0]) // 2, group)
-    )
+    block = jnp.where(odd == 0, same_ref[...], other_ref[...]).astype(F32)
+    width = out_refs[0].shape[1]
+    for i, ref in enumerate(out_refs):
+        ref[...] = block[:, i * width : (i + 1) * width]
+
+
+def place(me, same, other, height, width, columns):
+    size, total = lax.axis_size("rep"), same.shape[1]
+    spec = pl.BlockSpec((height, total), lambda j, me: (jnp.bitwise_xor(j, me[0]) // 2, 0))
     shape = (height, size * width) if columns else (size * height, width)
+    count = total // width
     return pl.pallas_call(
         place_kernel,
         grid_spec=pltpu.PrefetchScalarGridSpec(
             num_scalar_prefetch=1,
             grid=(size,),
             in_specs=[spec, spec],
-            out_specs=pl.BlockSpec(
-                (height, width), (lambda j, me: (0, j)) if columns else (lambda j, me: (j, 0))
-            ),
-        ),
-        out_shape=jax.ShapeDtypeStruct(shape, F32),
+            out_specs=[
+                pl.BlockSpec(
+                    (height, width), (lambda j, me: (0, j)) if columns else (lambda j, me: (j, 0))
+                )
+            ] * count,
+        ),
+        out_shape=[jax.ShapeDtypeStruct(shape, F32)] * count,
         cost_estimate=pl.CostEstimate(
-            flops=0, bytes_accessed=8 * size * height * width, transcendentals=0
+            flops=0, bytes_accessed=8 * size * height * total, transcendentals=0
         ),
         name="place",
     )(me, same, other)
@@ -404,7 +469,7 @@
 def place_turned(me, same, other, height):
     size, width = lax.axis_size("rep"), same.shape[1]
     if 2 * height % 128:
-        return place(me, same, other, height, width, 0, False).T
+        return place(me, same, other, height, width, False)[0].T
     spec = pl.BlockSpec((height, width), lambda j, me: (jnp.bitwise_xor(j, me[0] // 2), 0))
     return pl.pallas_call(
         place_turned_kernel,
@@ -421,25 +486,6 @@
         ),
         name="place_turned",
     )(me, same, other)
-
-
-def gather_copies(value):
-    blocks = gather_chips(value)
-    same = jnp.concatenate([blocks[d] for d in chip_offsets()], axis=0)
-    return same, swap(same, 1)
-
-
-def sum_vectors(rows):
-    size, bit = lax.axis_size("rep"), 1
-    while bit < size:
-        rows, bit = rows + swap(rows, bit), 2 * bit
-    shards, at = lax.axis_size("shard"), lax.axis_index("shard")
-    own = rows.shape[1] // shards
-    total = lax.dynamic_slice_in_dim(rows, at * own, own, 1)
-    for k in range(1, shards):
-        part = lax.dynamic_slice_in_dim(rows, ((at + k) % shards) * own, own, 1)
-        total += lax.ppermute(part, "shard", [(i, (i + k) % shards) for i in range(shards)])
-    return total
 
 
 def per_device(
@@ -461,65 +507,81 @@
     cotangent,
 ):
     length = layer_input.shape[0]
-    size = lax.axis_size("rep")
+    size, shards = lax.axis_size("rep"), lax.axis_size("shard")
     me = lax.axis_index("rep")
+    whoami = me.astype(jnp.int32).reshape(1)
+    shard = lax.axis_index("shard").astype(jnp.int32).reshape(1)
     block = w_query.shape[1] // size
-    hidden_block = w_gate.shape[1] // size
+    units = w_gate.shape[1] // size
+    own = gain_attn.shape[0]
     offsets = chip_offsets()
-
-    def columns(weight, width):
-        return lax.dynamic_slice_in_dim(weight, me * width, width, 1)
+    staged = len(chip_bits()) == 2
+
+    def columns(weight, d, width):
+        return lax.dynamic_slice_in_dim(weight, jnp.bitwise_xor(me, d) * width, width, 1)
 
     def rows_of(weight, height):
         return lax.dynamic_slice_in_dim(weight, me * height, height, 0)
 
-    shards = lax.axis_size("shard")
-    shard = lax.axis_index("shard").astype(jnp.int32).reshape(1)
-    three = (w_query, w_key, w_value)
-
     def local(d):
-        at = jnp.bitwise_xor(me, d) * block
-        return jnp.concatenate(
-            [lax.dynamic_slice_in_dim(w, at, block, 1) for w in three], axis=1
-        )
-
+        return jnp.concatenate([columns(w, d, block) for w in (w_query, w_key, w_value)], axis=1)
+
+    inputs = layer_input.astype(F32)
+    root_one = lax.rsqrt(jnp.mean(inputs * inputs, axis=-1, keepdims=True) + EPSILON)
+    tables = rotary_tables(length)
+    ring = [(i, (i + 1) % shards) for i in range(shards)]
     piece = local(0)
-    qkv_w = {d: [piece if d == 0 else local(d)] for d in offsets}
-    ring = [(i, (i + 1) % shards) for i in range(shards)]
-    for _ in range(1, shards):
-        piece = lax.ppermute(piece, "shard", ring)
-        for d, w in gather_chips(piece).items():
-            qkv_w[d].append(w)
-    own_out, piece = lax.optimization_barrier((rows_of(w_out, block), piece))
-    qkv_w[0][-1] = piece
+    qkv_w = {d: [local(d)] for d in offsets}
+    flows, context, saved = [], {}, {}
+    gain_flow = Flow(vector_gather_steps(jnp.stack([gain_attn, gain_mlp])))
+    piece, seg_other, own_gate_up = stage(
+        [gain_flow],
+        (
+            lax.ppermute(piece, "shard", ring),
+            swap(segments, 1),
+            jnp.concatenate([columns(w_gate, 0, units), columns(w_up, 0, units)], axis=1),
+        ),
+    )
+    gain_one, gain_two = gain_flow.result.astype(F32)
+    normed = (inputs * root_one * gain_one).astype(BF)
+    seg = jnp.concatenate([segments, seg_other], axis=0)
+    seg = (seg[:, :, None], seg[:, None, :])
+    other = swap(normed, 1)
+    for step in range(1, shards):
+        qkv_w[0].append(piece)
+        flows.append(Flow(gather_steps(piece, lambda d, b: qkv_w[d].append(b))))
+        if step < shards - 1:
+            piece, other = stage(flows, (lax.ppermute(piece, "shard", ring), other))
+    own_out, own_gate_up, qkv_w[0][-1] = lax.optimization_barrier(
+        (rows_of(w_out, block), own_gate_up, qkv_w[0][-1])
+    )
     own_out = lax.all_gather(own_out, "shard", axis=1, tiled=True)
-    gate_up = jnp.concatenate([columns(w_gate, hidden_block), columns(w_up, hidden_block)], axis=1)
-    out_w = gather_chips(own_out)
-    gate_up, _ = lax.optimization_barrier((gate_up, own_out))
-    gate_up = lax.all_gather(gate_up, "shard", axis=0, tiled=True)
-    own_down, _ = lax.optimization_barrier((rows_of(w_down, hidden_block), gate_up))
+    both = jnp.concatenate([normed, other], axis=0)
+
+    def run(d):
+        context[d], *saved[d] = attend(shard, both, qkv_w[d], tables, seg)
+        return context[d]
+
+    context[0], own_out = stage(flows, (run(0), own_out))
+    own_gate_up, own_out = lax.optimization_barrier((own_gate_up, own_out))
+    gate_up = lax.all_gather(own_gate_up, "shard", axis=0, tiled=True)
+    own_down, _ = lax.optimization_barrier((rows_of(w_down, units), gate_up))
     down = lax.all_gather(own_down, "shard", axis=1, tiled=True)
-
-    gains = gather_vector(jnp.stack([gain_attn, gain_mlp])).astype(F32)
-    gain_one, gain_two = gains[0], gains[1]
+    early = offsets[1:2] if staged else []
+    early = stage(flows, [run(d) for d in early])
+    for flow in flows:
+        finish(flow)
+    out_flow = Flow(gather_steps(own_out))
+    rest = [d for d in offsets if d not in context]
+    stage([out_flow], [run(d) for d in rest])
+    out_w = finish(out_flow)
 
     table, mix = plan_slots(mlp_route, mlp_gate)
     pick = table.astype(BF)
     upstream = cotangent.astype(F32)
     slot_weight = jnp.sum(jnp.where(table, mix[None, :], 0.0), axis=1)[:, None]
     slot_grad = (mm(pick, cotangent) * slot_weight).astype(BF)
-    all_slot_grad = gather_plane(slot_grad)
-
-    inputs = layer_input.astype(F32)
-    root_one = lax.rsqrt(jnp.mean(inputs * inputs, axis=-1, keepdims=True) + EPSILON)
-    normed = (inputs * root_one * gain_one).astype(BF)
-    both = jnp.concatenate([normed, swap(normed, 1)], axis=0)
-    seg = jnp.concatenate([segments, swap(segments, 1)], axis=0)
-    seg = (seg[:, :, None], seg[:, None, :])
-    tables = rotary_tables(length)
-    context, saved = {}, {}
-    for d in offsets:
-        context[d], *saved[d] = attend(shard, both, qkv_w[d], tables, seg)
+
     all_context = jnp.concatenate([context[d] for d in offsets], axis=1)
     all_out = jnp.concatenate([out_w[d] for d in offsets], axis=0)
     projected = mm(all_context, all_out)
@@ -528,11 +590,16 @@
     hidden = inputs + projected * attn_weight
     root_two = lax.rsqrt(jnp.mean(hidden * hidden, axis=-1, keepdims=True) + EPSILON)
     normed_two = (hidden * root_two * gain_two).astype(BF)
-    normed_two, gate_up = lax.optimization_barrier((normed_two, gate_up))
-
-    dispatched = gather_plane(mm(pick, normed_two).astype(BF))
+
+    disp_flow = Flow(copies_steps(mm(pick, normed_two).astype(BF)))
+    stage([disp_flow])
+    slot_grad, gate_up = stage([disp_flow], (slot_grad, gate_up))
+    slot_flow = Flow(copies_steps(slot_grad))
+    stage([disp_flow, slot_flow])
+    dispatched = jnp.concatenate(finish(disp_flow), axis=0)
     act = mm(dispatched, gate_up)
-    gate_act, up_act = act[:, :hidden_block], act[:, hidden_block:]
+    all_slot_grad = jnp.concatenate(finish(slot_flow), axis=0)
+    gate_act, up_act = act[:, :units], act[:, units:]
     sigmoid = jax.nn.sigmoid(gate_act)
     silu = gate_act * sigmoid
     inner = (silu * up_act).astype(BF)
@@ -540,55 +607,82 @@
     grad_gate_act = (grad_inner * up_act * sigmoid * (1.0 + gate_act * (1.0 - sigmoid))).astype(BF)
     grad_up_act = (grad_inner * silu).astype(BF)
     grad_act = jnp.concatenate([grad_gate_act, grad_up_act], axis=1)
-    grad_disp = scatter_plane(mm_nt(grad_act, gate_up).astype(BF)).astype(BF)
-    expert_out = scatter_plane(mm(inner, down).astype(BF)).astype(BF)
-    output = (hidden + mm_tn(pick, expert_out) * mix[:, None]).astype(BF)
-    grad_mlp = [
-        mm_tn(grad_gate_act, dispatched).astype(BF),
-        mm_tn(grad_up_act, dispatched).astype(BF),
-        mm_tn(inner, all_slot_grad).astype(BF),
-    ]
-
-    grad_normed_two = mm_tn(pick, grad_disp)
+    back_flow = Flow(plane_sum_steps(mm_nt(grad_act, gate_up).astype(BF)))
+    grad_mlp, sums = [], []
+    for left, right in (
+        (grad_gate_act, dispatched),
+        (grad_up_act, dispatched),
+        (inner, all_slot_grad),
+    ):
+        grad = stage([back_flow], mm_tn(left, right).astype(BF))
+        sums.append(lax.psum_scatter(grad, "shard", scatter_dimension=1, tiled=True))
+    grad_normed_two = mm_tn(pick, finish(back_flow))
     grad_gain_two, through = norm_back(grad_normed_two, hidden, root_two, gain_two)
     grad_hidden = upstream + through
-    grad_hidden, grad_mlp = lax.optimization_barrier((grad_hidden, grad_mlp))
 
     grad_projected = (grad_hidden * attn_weight).astype(BF)
     both_grad = jnp.concatenate([grad_projected, swap(grad_projected, 1)], axis=0)
-    grad_out_w = mm_tn(all_context, both_grad).astype(BF)
     lins, grad_qkv_w = {}, {}
-    for d in reversed(offsets):
-        lins[d], *grad_qkv_w[d] = attend_back(both_grad, out_w[d], *saved[d], both, tables, seg)
-        both_grad, lins[d] = lax.optimization_barrier((both_grad, lins[d]))
+
+    def run_back(*ds):
+        for d in ds:
+            lins[d], *grad_qkv_w[d] = attend_back(
+                both_grad, out_w[d], *saved[d], both, tables, seg
+            )
+        return [(lins[d], grad_qkv_w[d]) for d in ds]
+
+    def keep(ds, values):
+        for d, (lin, grad) in zip(ds, values):
+            lins[d], grad_qkv_w[d] = lin, grad
+
+    far, near = offsets[-1:], offsets[1:-1]
+    values, both_grad = lax.optimization_barrier((run_back(*far), both_grad))
+    keep(far, values)
+    qkv_flow = Flow(scatter_steps(grad_qkv_w))
+    values, both_grad = stage([qkv_flow], (run_back(*near), both_grad))
+    keep(near, values)
+    values, grad_out_w = stage([qkv_flow], (run_back(0), mm_tn(all_context, both_grad).astype(BF)))
+    keep([0], values)
     grad_normed = normed_back(
         shard, [lins[d] for d in offsets], [qkv_w[d] for d in offsets], both.shape[1]
     )
+    sums[0], sums[1], grad_normed, grad_out_w = stage(
+        [qkv_flow], (sums[0], sums[1], grad_normed, grad_out_w)
+    )
+    own_grad_qkv, sums[2] = lax.optimization_barrier((finish(qkv_flow), sums[2]))
+    sum_qkv = lax.psum_scatter(own_grad_qkv, "shard", scatter_dimension=0, tiled=True)
     grad_normed = grad_normed[:length] + swap(grad_normed[length:].astype(BF), 1).astype(F32)
     grad_gain_one, first = norm_back(grad_normed, inputs, root_one, gain_one)
     grad_input = (grad_hidden + first).astype(BF)
 
-    whoami = me.astype(jnp.int32).reshape(1)
-    sums = [lax.psum_scatter(g, "shard", scatter_dimension=1, tiled=True) for g in grad_mlp]
-    own_grad_out = scatter_chips(
-        {d: halves(grad_out_w[i * block : (i + 1) * block]) for i, d in enumerate(offsets)}
-    ).astype(BF)
-    own_grad_out, _ = lax.optimization_barrier((own_grad_out, sums))
+    out_blocks = {d: halves(grad_out_w[i * block : (i + 1) * block]) for i, d in enumerate(offsets)}
+    expert_out = mm(inner, down).astype(BF)
+    gate_flow, expert_flow = Flow(copies_steps(sums[0])), Flow(plane_sum_steps(expert_out))
+    up_flow = Flow(copies_steps(sums[1]))
+    grad_input, gains, out_blocks = stage(
+        [gate_flow, up_flow, expert_flow],
+        (grad_input, jnp.stack([grad_gain_one, grad_gain_two]), out_blocks),
+    )
+    gain_flow, out_flow = Flow(vector_sum_steps(gains)), Flow(scatter_steps(out_blocks))
+    stage([gate_flow, up_flow, gain_flow])
+    stage([gate_flow, up_flow, out_flow, gain_flow])
+    stage([out_flow, expert_flow, gain_flow])
+    sums[2] = stage([out_flow, expert_flow], sums[2])
+    grad_gate = place_turned(whoami, *finish(gate_flow), units)
+    grad_up = place_turned(whoami, *finish(up_flow), units)
+    own_grad_out, sum_qkv = lax.optimization_barrier((finish(out_flow), sum_qkv))
     sum_out = lax.psum_scatter(own_grad_out, "shard", scatter_dimension=1, tiled=True)
-    own_grad_qkv = scatter_chips(grad_qkv_w).astype(BF)
-    own_grad_qkv, _ = lax.optimization_barrier((own_grad_qkv, sum_out))
-    sum_qkv = lax.psum_scatter(own_grad_qkv, "shard", scatter_dimension=0, tiled=True)
-    own = gain_attn.shape[0]
-    grad_gate, grad_up = (
-        place_turned(whoami, *gather_copies(g), hidden_block) for g in sums[:2]
-    )
-    grad_down = place(whoami, *gather_copies(sums[2]), hidden_block, own, 0, False)
-    grad_out = place(whoami, *gather_copies(sum_out), block, own, 0, False)
-    copies = gather_copies(sum_qkv)
-    grad_query, grad_key, grad_value = (
-        place(whoami, *copies, own, block, group, True) for group in range(3)
-    )
-    gain_grads = sum_vectors(jnp.stack([grad_gain_one, grad_gain_two]))
+    down_flow, qkv_flow = Flow(copies_steps(sums[2])), Flow(copies_steps(sum_qkv))
+    grad_gate, grad_up = stage([down_flow, qkv_flow], (grad_gate, grad_up))
+    stage([qkv_flow, down_flow])
+    stage([qkv_flow, down_flow, expert_flow])
+    (grad_down,) = place(whoami, *finish(down_flow), units, own, False)
+    out_flow = Flow(copies_steps(sum_out))
+    grad_down = stage([out_flow, gain_flow], grad_down)
+    grad_query, grad_key, grad_value = place(whoami, *finish(qkv_flow), own, block, True)
+    output = (hidden + mm_tn(pick, finish(expert_flow)) * mix[:, None]).astype(BF)
+    (grad_out,) = place(whoami, *finish(out_flow), block, own, False)
+    gain_grads = finish(gain_flow)
     return (
         output,
         grad_input,

time: 873 us -> 768 us (0.88)
  waiting for transfers between devices: 348 us -> 249 us
  local copies, waits for them, and re-layouts: 83.6 us -> 104 us
  other arithmetic: 70.1 us -> 56.2 us
  Pallas kernels: 182 us -> 170 us
    ppermute x85, waiting for transfers between devices: 238 us -> 182 us  [swap(): return lax.ppermute(value, 'rep', [(i, i ^ bit) for i in range(size)])]
    ppermute x9, waiting for transfers between devices: 56.3 us -> 16 us  [the longest x1 12.9 us: per_device(): lax.ppermute(piece, 'shard', ring)]
    reduce_scatter x1, waiting for transfers between devices: 0.01 us -> 23.1 us  [per_device(): lax.psum_scatter(own_grad_out, 'shard', scatter_dimension=1, tiled=True)]
    all_gather x1, waiting for transfers between devices: 39.3 us -> 21.9 us  [per_device(): down = lax.all_gather(own_down, 'shard', axis=1, tiled=True)]
    unnamed x220 -> x242, local copies, waits for them, and re-layouts: 41.4 us -> 58.8 us
    reduce_scatter x3, waiting for transfers between devices: 13.3 us -> 0.02 us  [per_device(): lax.psum_scatter(grad, 'shard', scatter_dimension=1, tiled=True)]
    another operation x9 -> x1, other arithmetic: 13.3 us -> 0.02 us  [per_device(): jnp.stack([grad_gain_one, grad_gain_two])]
    pallas_call x5 -> x3, Pallas kernels: 36.5 us -> 27.9 us  [place(): pl.pallas_call(place_kernel, grid_spec=pltpu.PrefetchScalarGridSpec(num_s...]
  transfers between devices with their start and end apart: 102 -> 102, of which waited for: 43 -> 39; matrix products, arithmetic and copies ran while one was open for 21% -> 23% of each run, Pallas kernels for 19% -> 21%
where the time goes in v3:
time: 768 us; the launch traced here: 759 us
  waiting for transfers between devices  249 us (32%)
  Pallas kernels  170 us (22%)
  local copies, waits for them, and re-layouts  104 us (14%)
  starting transfers between devices  90.3 us (12%)
  matrix products  73.9 us (10%)
  other arithmetic  56.2 us (7%)
  between operations  16.1 us (2%)
    ppermute x85, waiting for transfers between devices, swap(): return lax.ppermute(value, 'rep', [(i, i ^ bit) for i in range(size)])  182 us
    ppermute x85, starting transfers between devices, swap(): return lax.ppermute(value, 'rep', [(i, i ^ bit) for i in range(size)])  76.2 us
    pallas_call x4, Pallas kernels, attend_back(): pl.pallas_call(attend_back_kernel, grid=(rows // length,), in_specs=[by_s...  68.7 us
    unnamed x242, local copies, waits for them, and re-layouts  58.8 us
    pallas_call x4, Pallas kernels, attend(): pl.pallas_call(functools.partial(attend_kernel, parts), grid_spec=pltpu.P...  43.1 us
    dot_general x6, matrix products, mm_tn(): lax.dot_general(left, right, (((0,), (0,)), ((), ())), preferred_element_...  32.7 us
    pallas_call x3, Pallas kernels, place(): pl.pallas_call(place_kernel, grid_spec=pltpu.PrefetchScalarGridSpec(num_s...  27.9 us
    reduce_scatter x1, waiting for transfers between devices, per_device(): lax.psum_scatter(own_grad_out, 'shard', scatter_dimension=1, tiled=True)  23.1 us
  transfers between devices with their start and end apart: 102, of which 39 were waited for; matrix products, arithmetic and copies ran while one was open for 23% of the time, Pallas kernels for 21%

profile of v3, /device:TPU:0, one launch (start us, length us, event | category | flops | bytes accessed | tf_op | source)
XLA Modules:
  0.0 759.0 jit_solution(17472880826273508554)
XLA Ops:
  8.8 5.1 collective-permute-start
  16.8 2.7 constant_dynamic-slice_fusion.5
  19.6 2.5 collective-permute-start.3
  27.1 12.9 %collective-permute-done.3.refs_5_ = bf16[512,768]{1,0:T(8,128)(2,1)} collective-permute-done((bf16[512,768]{1,0:T(8,128)(2,1)S(1)}, bf16[512,768]{1,0:T(8,128)(2,1)}, u32[]{:S(2)}, u32[]{:S(2)}) %collective-permute-start.3) | collective-permute-done | bytes 786464 | tf_op jit(solution)/shard_map/ppermute | solution.py:540
  46.1 16.4 %collective-permute-done.5.refs_5_.refs_9_ = bf16[512,768]{1,0:T(8,128)(2,1)S(1)} collective-permute-done((bf16[512,768]{1,0:T(8,128)(2,1)}, bf16[512,768]{1,0:T(8,128)(2,1)S(1)}, u32[]{:S(2)}, u32[]{:S(2)}) %collective-permute-start.5) | collective-permute-done | bytes 786464 | tf_op jit(solution)/shard_map/ppermute | solution.py:33
  63.8 3.1 collective-permute-done.7.refs_6_
  74.2 20.2 %collective-permute-done.9 = bf16[256,768]{1,0:T(8,128)(2,1)} collective-permute-done((bf16[256,768]{1,0:T(8,128)(2,1)}, bf16[256,768]{1,0:T(8,128)(2,1)}, u32[]{:S(2)}, u32[]{:S(2)}) %collective-permute-start.9) | collective-permute-done | bytes 393248 | tf_op jit(solution)/shard_map/ppermute | solution.py:33
  106.3 2.8 pad_maximum_fusion.refs_0_.refs_1_.refs_2_.refs_3_.x_ref
  109.1 12.2 %attend.4 = (bf16[1024,256]{1,0:T(8,128)(2,1)S(1)}, bf16[1024,768]{1,0:T(8,128)(2,1)S(1)}, f32[1024,2]{1,0:T(8,128)S(1)}) custom-call(s32[1]{0:T(128)} %bitcast.1.z_ref, bf16[1024,2048]{1,0:T(8,128)(2,1)S(1)} %pad_maximum_fusion.refs_0_.refs_1_.refs_2_.refs_3_.x_ref, bf16[1024,2048]{1,0:T(8,128)(2,1)S(1)} %pad_maximum_fusion.refs_0_.refs_1_.refs_2_.refs_3_.x_ref, ...), custom_call_target="tpu_custom_call" | custom-call | flops 3758096384 | bytes 10485760 | tf_op jit(solution)/shard_map/attend/pallas_call | solution.py:251
  123.2 3.7 collective-permute-done.14
  140.1 10.7 %attend.5 = (bf16[1024,256]{1,0:T(8,128)(2,1)S(1)}, bf16[1024,768]{1,0:T(8,128)(2,1)S(1)}, f32[1024,2]{1,0:T(8,128)S(1)}) custom-call(s32[1]{0:T(128)} %bitcast.1.z_ref, bf16[1024,2048]{1,0:T(8,128)(2,1)S(1)} %copy-done.3, bf16[1024,2048]{1,0:T(8,128)(2,1)S(1)} %copy-done.3, bf16[1024,2048]{1,0:T(8,128)(2,1)S(1)} %copy-done.3, ...), custom_call_target="tpu_custom_call" | custom-call | flops 3758096384 | bytes 10485760 | tf_op jit(solution)/shard_map/attend/pallas_call | solution.py:251
  153.6 10.7 %attend.6 = (bf16[1024,256]{1,0:T(8,128)(2,1)S(1)}, bf16[1024,768]{1,0:T(8,128)(2,1)S(1)}, f32[1024,2]{1,0:T(8,128)S(1)}) custom-call(s32[1]{0:T(128)} %bitcast.1.z_ref, bf16[1024,2048]{1,0:T(8,128)(2,1)S(1)} %copy-done.3, bf16[1024,2048]{1,0:T(8,128)(2,1)S(1)} %copy-done.3, bf16[1024,2048]{1,0:T(8,128)(2,1)S(1)} %copy-done.3, ...), custom_call_target="tpu_custom_call" | custom-call | flops 3758096384 | bytes 10485760 | tf_op jit(solution)/shard_map/attend/pallas_call | solution.py:251
  166.8 9.6 %attend.7 = (bf16[1024,256]{1,0:T(8,128)(2,1)S(1)}, bf16[1024,768]{1,0:T(8,128)(2,1)S(1)}, f32[1024,2]{1,0:T(8,128)S(1)}) custom-call(s32[1]{0:T(128)} %bitcast.1.z_ref, bf16[1024,2048]{1,0:T(8,128)(2,1)S(1)} %copy-done.3, bf16[1024,2048]{1,0:T(8,128)(2,1)S(1)} %copy-done.3, bf16[1024,2048]{1,0:T(8,128)(2,1)S(1)} %copy-done.3, ...), custom_call_target="tpu_custom_call" | custom-call | flops 3758096384 | bytes 10485760 | tf_op jit(solution)/shard_map/attend/pallas_call | solution.py:251
  179.3 6.8 collective-permute-done.22
  188.7 6.1 fusion.54
  195.7 3.6 collective-permute-done.24
  205.7 10.8 %collective-permute-done.25 = bf16[128,2048]{1,0:T(8,128)(2,1)S(1)} collective-permute-done((bf16[128,2048]{1,0:T(8,128)(2,1)S(1)}, bf16[128,2048]{1,0:T(8,128)(2,1)S(1)}, u32[]{:S(2)}, u32[]{:S(2)}) %collective-permute-start.25) | collective-permute-done | bytes 524320 | tf_op jit(solution)/shard_map/ppermute | solution.py:33
  219.8 4.6 collective-permute-done.27
  225.3 5.6 all-gather.6.cloned.1.call-done
  241.6 9.6 %collective-permute-done.30 = bf16[128,2048]{1,0:T(8,128)(2,1)S(1)} collective-permute-done((bf16[128,2048]{1,0:T(8,128)(2,1)}, bf16[128,2048]{1,0:T(8,128)(2,1)S(1)}, u32[]{:S(2)}, u32[]{:S(2)}) %collective-permute-start.30) | collective-permute-done | bytes 524320 | tf_op jit(solution)/shard_map/ppermute | solution.py:33
  254.6 3.2 constant_dynamic-update-slice_fusion.28
  262.2 8.6 %fusion.55 = f32[1024,1408]{1,0:T(8,128)} fusion(bf16[1024,2048]{1,0:T(8,128)(2,1)S(1)} %copy-done.82, bf16[2048,1408]{1,0:T(8,128)(2,1)S(1)} %copy-done.95), kind=kOutput, calls=%fused_computation.221 | convolution fusion | flops 5905580032 | bytes 15728640 | tf_op jit(solution)/shard_map/dot_general | solution.py:20
  272.4 21.9 %all-gather.8.cloned.1.call-done = bf16[704,2048]{1,0:T(8,128)(2,1)} async-done(((bf16[704,512]{1,0:T(8,128)(2,1)}), bf16[704,2048]{1,0:T(8,128)(2,1)}) %all-gather.8.cloned.1.call-update) | async-done | bytes 2883600 | tf_op jit(solution)/shard_map/all_gather | solution.py:569
  294.3 10.1 %multiply_convert_fusion.3 = (bf16[1024,704]{1,0:T(8,128)(2,1)S(1)}, bf16[1024,704]{1,0:T(8,128)(2,1)S(1)}, bf16[1024,704]{1,0:T(8,128)(2,1)}) fusion(f32[1024,1408]{1,0:T(8,128)} %fusion.55, bf16[1024,2048]{1,0:T(8,128)(2,1)} %constant_dynamic-update-slice_fusion.39, bf16[704,2048]{1,0:T(8,128)(2,1)} %all-gather.8.cloned.1.call-done), kind=kOutput, calls=%fused_computation.44 | convolution fusion | flops 2963603456 | bytes 17170432 | tf_op jit(solution)/shard_map/dot_general | solution.py:24
  304.4 9.3 %convolution_convert_fusion = bf16[1024,2048]{1,0:T(8,128)(2,1)S(1)} fusion(bf16[2048,1408]{1,0:T(8,128)(2,1)} %all-gather.6.cloned.1.call-done, bf16[1024,704]{1,0:T(8,128)(2,1)S(1)} %get-tuple-element.336, bf16[1024,704]{1,0:T(8,128)(2,1)S(1)} %get-tuple-element.335), kind=kOutput, calls=%fused_computation.32 | convolution fusion | flops 5913444352 | bytes 12845056 | tf_op jit(solution)/shard_map/dot_general | solution.py:24
  318.7 4.5 convolution_convert_fusion.5
  323.3 3.2 add_convert_fusion.2
  331.8 4.9 convolution_convert_fusion.3
  341.8 7.5 convolution_convert_fusion.4
  353.3 4.9 collective-permute-done.41
  359.4 3.6 multiply_reduce_fusion
  363.6 3.2 multiply_convert_fusion
  366.9 4.1 collective-permute-done.42
  370.9 2.6 pad_maximum_fusion.1.grad_ref
  373.5 17.5 %attend_back.4 = (bf16[1024,768]{1,0:T(8,128)(2,1)S(1)}, bf16[1024,768]{1,0:T(8,128)(2,1)}, bf16[1024,768]{1,0:T(8,128)(2,1)}) custom-call(bf16[1024,2048]{1,0:T(8,128)(2,1)} %pad_maximum_fusion.1.grad_ref, bf16[256,2048]{1,0:T(8,128)(2,1)S(1)} %pad_maximum_fusion.4.out_ref, bf16[1024,768]{1,0:T(8,128)(2,1)} %copy-done.31, f32[1024,2]{1,0:T(8,128)S(1)} %copy-done.37, ...), custom_call_target="tpu_custom_call" | custom-call | flops 5637144576 | bytes 15728640 | tf_op jit(solution)/shard_map/attend_back/pallas_call | solution.py:340
  396.5 17.2 %attend_back.6 = (bf16[1024,768]{1,0:T(8,128)(2,1)S(1)}, bf16[1024,768]{1,0:T(8,128)(2,1)S(1)}, bf16[1024,768]{1,0:T(8,128)(2,1)}) custom-call(bf16[1024,2048]{1,0:T(8,128)(2,1)} %pad_maximum_fusion.1.grad_ref, bf16[256,2048]{1,0:T(8,128)(2,1)S(1)} %copy-done.15, bf16[1024,768]{1,0:T(8,128)(2,1)} %copy-done.30, f32[1024,2]{1,0:T(8,128)S(1)} %copy-done.35, ...), custom_call_target="tpu_custom_call" | custom-call | flops 5637144576 | bytes 15728640 | tf_op jit(solution)/shard_map/attend_back/pallas_call | solution.py:340
  415.7 16.9 %attend_back.5 = (bf16[1024,768]{1,0:T(8,128)(2,1)S(1)}, bf16[1024,768]{1,0:T(8,128)(2,1)S(1)}, bf16[1024,768]{1,0:T(8,128)(2,1)}) custom-call(bf16[1024,2048]{1,0:T(8,128)(2,1)} %pad_maximum_fusion.1.grad_ref, bf16[256,2048]{1,0:T(8,128)(2,1)S(1)} %copy-done.13, bf16[1024,768]{1,0:T(8,128)(2,1)} %copy-done.29, f32[1024,2]{1,0:T(8,128)S(1)} %get-tuple-element.224.lse_ref, ...), custom_call_target="tpu_custom_call" | custom-call | flops 5637144576 | bytes 15728640 | tf_op jit(solution)/shard_map/attend_back/pallas_call | solution.py:340
  433.7 3.0 add_convert_fusion.6
  437.8 3.2 add_convert_fusion.5
  442.5 7.7 %convolution_convert_fusion.2 = bf16[1024,2048]{1,0:T(8,128)(2,1)} fusion(bf16[1024,1024]{1,0:T(8,128)(2,1)} %constant_dynamic-update-slice_fusion.14, bf16[1024,2048]{1,0:T(8,128)(2,1)S(1)} %copy-done.57), kind=kOutput, calls=%fused_computation.34 | convolution fusion | flops 4297064448 | bytes 10485760 | tf_op jit(solution)/shard_map/dot_general | solution.py:28
  450.2 17.2 %attend_back.7 = (bf16[1024,768]{1,0:T(8,128)(2,1)S(1)}, bf16[1024,768]{1,0:T(8,128)(2,1)S(1)}, bf16[1024,768]{1,0:T(8,128)(2,1)}) custom-call(bf16[1024,2048]{1,0:T(8,128)(2,1)} %pad_maximum_fusion.1.grad_ref, bf16[256,2048]{1,0:T(8,128)(2,1)S(1)} %copy-done.27, bf16[1024,768]{1,0:T(8,128)(2,1)} %copy-done.28, f32[1024,2]{1,0:T(8,128)S(1)} %copy-done.33, ...), custom_call_target="tpu_custom_call" | custom-call | flops 5637144576 | bytes 15728640 | tf_op jit(solution)/shard_map/attend_back/pallas_call | solution.py:340
  470.8 19.8 %normed_back.1 = f32[1024,2048]{1,0:T(8,128)} custom-call(s32[1]{0:T(128)} %bitcast.1.z_ref, bf16[1024,768]{1,0:T(8,128)(2,1)} %copy-done.41, bf16[1024,768]{1,0:T(8,128)(2,1)} %copy-done.39, bf16[1024,768]{1,0:T(8,128)(2,1)} %copy-done.40, bf16[1024,768]{1,0:T(8,128)(2,1)} %copy-done.38, bf16[512,768]{1,0:T(8,128)(2,1)S(1)} %pad_maximum_fusion.6.refs_4_, ...), custom_call_target="tpu_custom_call" | custom-call | flops 12884901888 | bytes 27262976 | tf_op jit(solution)/shard_map/normed_back/pallas_call | solution.py:387
  490.7 11.6 %collective-permute-done.45 = bf16[1024,768]{1,0:T(8,128)(2,1)} collective-permute-done((bf16[1024,768]{1,0:T(8,128)(2,1)}, bf16[1024,768]{1,0:T(8,128)(2,1)}, u32[]{:S(2)}, u32[]{:S(2)}) %collective-permute-start.45) | collective-permute-done | bytes 1572896 | tf_op jit(solution)/shard_map/ppermute | solution.py:33
  502.3 3.8 slice.329
  506.1 5.0 convolution_convert_fusion.1
  516.3 2.5 add_convert_fusion.3
  522.8 2.7 fusion.49
  529.1 4.7 fusion.9
  533.9 4.9 fusion.6
  538.8 8.2 %collective-permute-done.51 = bf16[704,512]{1,0:T(8,128)(2,1)} collective-permute-done((bf16[704,512]{1,0:T(8,128)(2,1)}, bf16[704,512]{1,0:T(8,128)(2,1)}, u32[]{:S(2)}, u32[]{:S(2)}) %collective-permute-start.51) | collective-permute-done | bytes 720928 | tf_op jit(solution)/shard_map/ppermute | solution.py:33
  560.2 2.5 collective-permute-done.56
  562.8 3.1 collective-permute-done.57
  574.1 9.0 %collective-permute-done.64 = f32[2,2048]{1,0:T(2,128)S(1)} collective-permute-done((f32[2,2048]{1,0:T(2,128)S(1)}, f32[2,2048]{1,0:T(2,128)S(1)}, u32[]{:S(2)}, u32[]{:S(2)}) %collective-permute-start.64) | collective-permute-done | bytes 16416 | tf_op jit(solution)/shard_map/ppermute | solution.py:33
  588.1 13.7 %collective-permute-done.71 = bf16[64,2048]{1,0:T(8,128)(2,1)S(1)} collective-permute-done((bf16[64,2048]{1,0:T(8,128)(2,1)S(1)}, bf16[64,2048]{1,0:T(8,128)(2,1)S(1)}, u32[]{:S(2)}, u32[]{:S(2)}) %collective-permute-start.71) | collective-permute-done | bytes 262176 | tf_op jit(solution)/shard_map/ppermute | solution.py:33
  607.8 11.6 %collective-permute-done.73 = f32[2,2048]{1,0:T(2,128)S(1)} collective-permute-done((f32[2,2048]{1,0:T(2,128)S(1)}, f32[2,2048]{1,0:T(2,128)S(1)}, u32[]{:S(2)}, u32[]{:S(2)}) %collective-permute-start.73) | collective-permute-done | bytes 16416 | tf_op jit(solution)/shard_map/ppermute | solution.py:33
  629.7 5.0 place_turned.2
  634.6 5.0 place_turned.3
  641.5 13.4 %collective-permute-done.74 = bf16[704,512]{1,0:T(8,128)(2,1)S(1)} collective-permute-done((bf16[704,512]{1,0:T(8,128)(2,1)}, bf16[704,512]{1,0:T(8,128)(2,1)S(1)}, u32[]{:S(2)}, u32[]{:S(2)}) %collective-permute-start.74) | collective-permute-done | bytes 720928 | tf_op jit(solution)/shard_map/ppermute | solution.py:33
  663.6 8.5 %collective-permute-done.80 = bf16[352,512]{1,0:T(8,128)(2,1)S(1)} collective-permute-done((bf16[352,512]{1,0:T(8,128)(2,1)S(1)}, bf16[352,512]{1,0:T(8,128)(2,1)S(1)}, u32[]{:S(2)}, u32[]{:S(2)}) %collective-permute-start.80) | collective-permute-done | bytes 360480 | tf_op jit(solution)/shard_map/ppermute | solution.py:33
  678.8 23.1 %reduce-scatter.14.cloned.1.call-done = bf16[256,512]{1,0:T(8,128)(2,1)} async-done(((bf16[256,2048]{1,0:T(8,128)(2,1)}), bf16[256,512]{1,0:T(8,128)(2,1)}) %reduce-scatter.14.cloned.1.call-update) | async-done | bytes 262160 | tf_op jit(solution)/shard_map/reduce_scatter | solution.py:674
  710.7 10.5 %place.3 = f32[5632,512]{1,0:T(8,128)} custom-call(s32[1]{0:T(128)} %bitcast.6.me_ref, bf16[2816,512]{1,0:T(8,128)(2,1)} %constant_dynamic-update-slice_fusion.60.same_ref, bf16[2816,512]{1,0:T(8,128)(2,1)} %collective-permute-done.83.other_ref), custom_call_target="tpu_custom_call" | custom-call | bytes 23068672 | tf_op jit(solution)/shard_map/place/pallas_call | solution.py:442
  725.8 11.0 %place.4 = (f32[512,2048]{1,0:T(8,128)}, f32[512,2048]{1,0:T(8,128)}, f32[512,2048]{1,0:T(8,128)}) custom-call(s32[1]{0:T(128)} %bitcast.6.me_ref, bf16[2048,768]{1,0:T(8,128)(2,1)} %constant_dynamic-update-slice_fusion.55.same_ref, bf16[2048,768]{1,0:T(8,128)(2,1)} %collective-permute-done.82.other_ref), custom_call_target="tpu_custom_call" | custom-call | bytes 25165824 | tf_op jit(solution)/shard_map/place/pallas_call | solution.py:442
  740.8 4.4 add_convert_fusion
  745.2 6.4 place.5
  (524 shorter events, 218.4 us)
Async XLA Ops:
  7.2 120.5 %all-gather.4.cloned.1.call-start = ((), (), s32[]{:S(2)}) async-start(), calls=%async_computation.5 | async-start | bytes 1310720 | tf_op jit(solution)/shard_map/all_gather | solution.py:558
  8.8 18.3 %collective-permute-start = (bf16[2,512]{1,0:T(2,128)(2,1)S(1)}, bf16[2,512]{1,0:T(2,128)(2,1)S(1)}, u32[]{:S(2)}, u32[]{:S(2)}) collective-permute-start(bf16[2,512]{1,0:T(2,128)(2,1)S(1)} %get-tuple-element.334), channel_id=1, source_target_pairs={{0,3},{1,0},{2,1},{3,2},{4,7},{5,4},{6,5},{7,6},{8,11},{9,8},{10,9... | collective-permute-start | bytes 6152 | tf_op jit(solution)/shard_map/ppermute | solution.py:172
  19.6 20.4 %collective-permute-start.3 = (bf16[512,768]{1,0:T(8,128)(2,1)S(1)}, bf16[512,768]{1,0:T(8,128)(2,1)}, u32[]{:S(2)}, u32[]{:S(2)}) collective-permute-start(bf16[512,768]{1,0:T(8,128)(2,1)S(1)} %pad_maximum_fusion.6.refs_4_), channel_id=1, source_target_pairs={{0,1},{1,2},{2,3},{3,0},{4,5},{5,6},{6,7},{7,4},{8,9},{9,10},{10,1... | collective-permute-start | bytes 2359304 | tf_op jit(solution)/shard_map/ppermute | solution.py:540
  42.3 24.6 %collective-permute-start.8 = (bf16[512,2048]{1,0:T(8,128)(2,1)S(1)}, bf16[512,2048]{1,0:T(8,128)(2,1)S(1)}, u32[]{:S(2)}, u32[]{:S(2)}) collective-permute-start(bf16[512,2048]{1,0:T(8,128)(2,1)S(1)} %fusion.2), channel_id=1, source_target_pairs={{0,4},{4,0},{8,12},{12,8},{16,20},{20,16},{24,28},{28,24},{1,5},{5... | collective-permute-start | bytes 6291464 | tf_op jit(solution)/shard_map/ppermute | solution.py:33
  42.4 20.2 %collective-permute-start.5 = (bf16[512,768]{1,0:T(8,128)(2,1)}, bf16[512,768]{1,0:T(8,128)(2,1)S(1)}, u32[]{:S(2)}, u32[]{:S(2)}) collective-permute-start(bf16[512,768]{1,0:T(8,128)(2,1)} %collective-permute-done.3.refs_5_), channel_id=1, source_target_pairs={{0,8},{4,12},{8,0},{12,4},{16,24},{20,28},{24,16},{28,20},{1,9},{5... | collective-permute-start | bytes 2359304 | tf_op jit(solution)/shard_map/ppermute | solution.py:33
  43.9 19.8 %collective-permute-start.6 = (bf16[512,768]{1,0:T(8,128)(2,1)}, bf16[512,768]{1,0:T(8,128)(2,1)S(1)}, u32[]{:S(2)}, u32[]{:S(2)}) collective-permute-start(bf16[512,768]{1,0:T(8,128)(2,1)} %collective-permute-done.3.refs_5_), channel_id=1, source_target_pairs={{0,16},{4,20},{8,24},{12,28},{16,0},{20,4},{24,8},{28,12},{1,17},{... | collective-permute-start | bytes 2359304 | tf_op jit(solution)/shard_map/ppermute | solution.py:33
  45.5 21.4 %collective-permute-start.7 = (bf16[512,768]{1,0:T(8,128)(2,1)}, bf16[512,768]{1,0:T(8,128)(2,1)}, u32[]{:S(2)}, u32[]{:S(2)}) collective-permute-start(bf16[512,768]{1,0:T(8,128)(2,1)} %collective-permute-done.3.refs_5_), channel_id=1, source_target_pairs={{0,1},{1,2},{2,3},{3,0},{4,5},{5,6},{6,7},{7,4},{8,9},{9,10},{10,1... | collective-permute-start | bytes 2359304 | tf_op jit(solution)/shard_map/ppermute | solution.py:554
  66.9 27.5 %collective-permute-start.11 = (bf16[512,768]{1,0:T(8,128)(2,1)}, bf16[512,768]{1,0:T(8,128)(2,1)}, u32[]{:S(2)}, u32[]{:S(2)}) collective-permute-start(bf16[512,768]{1,0:T(8,128)(2,1)} %collective-permute-done.7.refs_6_), channel_id=1, source_target_pairs={{0,8},{4,12},{8,0},{12,4},{16,24},{20,28},{24,16},{28,20},{1,9},{5... | collective-permute-start | bytes 2359304 | tf_op jit(solution)/shard_map/ppermute | solution.py:33
  67.4 26.9 %collective-permute-start.12 = (bf16[512,768]{1,0:T(8,128)(2,1)}, bf16[512,768]{1,0:T(8,128)(2,1)}, u32[]{:S(2)}, u32[]{:S(2)}) collective-permute-start(bf16[512,768]{1,0:T(8,128)(2,1)} %collective-permute-done.7.refs_6_), channel_id=1, source_target_pairs={{0,16},{4,20},{8,24},{12,28},{16,0},{20,4},{24,8},{28,12},{1,17},{... | collective-permute-start | bytes 2359304 | tf_op jit(solution)/shard_map/ppermute | solution.py:33
  67.9 26.4 %collective-permute-start.13 = (bf16[512,768]{1,0:T(8,128)(2,1)}, bf16[512,768]{1,0:T(8,128)(2,1)}, u32[]{:S(2)}, u32[]{:S(2)}) collective-permute-start(bf16[512,768]{1,0:T(8,128)(2,1)} %collective-permute-done.7.refs_6_), channel_id=1, source_target_pairs={{0,1},{1,2},{2,3},{3,0},{4,5},{5,6},{6,7},{7,4},{8,9},{9,10},{10,1... | collective-permute-start | bytes 2359304 | tf_op jit(solution)/shard_map/ppermute | solution.py:554
  69.6 24.7 %collective-permute-start.9 = (bf16[256,768]{1,0:T(8,128)(2,1)}, bf16[256,768]{1,0:T(8,128)(2,1)}, u32[]{:S(2)}, u32[]{:S(2)}) collective-permute-start(bf16[256,768]{1,0:T(8,128)(2,1)} %slice.212), channel_id=1, source_target_pairs={{0,16},{4,20},{8,24},{12,28},{16,0},{20,4},{24,8},{28,12},{1,17},{... | collective-permute-start | bytes 1179656 | tf_op jit(solution)/shard_map/ppermute | solution.py:33
  71.9 22.4 %collective-permute-start.10 = (bf16[256,768]{1,0:T(8,128)(2,1)}, bf16[256,768]{1,0:T(8,128)(2,1)}, u32[]{:S(2)}, u32[]{:S(2)}) collective-permute-start(bf16[256,768]{1,0:T(8,128)(2,1)} %slice.213), channel_id=1, source_target_pairs={{0,8},{4,12},{8,0},{12,4},{16,24},{20,28},{24,16},{28,20},{1,9},{5... | collective-permute-start | bytes 1179656 | tf_op jit(solution)/shard_map/ppermute | solution.py:33
  94.4 136.5 %all-gather.6.cloned.1.call-start = ((), (), s32[]{:S(2)}) async-start(), calls=%async_computation.6 | async-start | bytes 7208960 | tf_op jit(solution)/shard_map/all_gather | solution.py:567
  99.8 27.9 %collective-permute-start.16 = (bf16[512,768]{1,0:T(8,128)(2,1)}, bf16[512,768]{1,0:T(8,128)(2,1)}, u32[]{:S(2)}, u32[]{:S(2)}) collective-permute-start(bf16[512,768]{1,0:T(8,128)(2,1)} %collective-permute-done.13.refs_7_), channel_id=1, source_target_pairs={{0,8},{4,12},{8,0},{12,4},{16,24},{20,28},{24,16},{28,20},{1,9},{5... | collective-permute-start | bytes 2359304 | tf_op jit(solution)/shard_map/ppermute | solution.py:33
  101.3 26.4 %collective-permute-start.17 = (bf16[512,768]{1,0:T(8,128)(2,1)}, bf16[512,768]{1,0:T(8,128)(2,1)}, u32[]{:S(2)}, u32[]{:S(2)}) collective-permute-start(bf16[512,768]{1,0:T(8,128)(2,1)} %collective-permute-done.13.refs_7_), channel_id=1, source_target_pairs={{0,16},{4,20},{8,24},{12,28},{16,0},{20,4},{24,8},{28,12},{1,17},{... | collective-permute-start | bytes 2359304 | tf_op jit(solution)/shard_map/ppermute | solution.py:33
  103.1 23.8 %collective-permute-start.14 = (bf16[256,768]{1,0:T(8,128)(2,1)S(1)}, bf16[256,768]{1,0:T(8,128)(2,1)S(1)}, u32[]{:S(2)}, u32[]{:S(2)}) collective-permute-start(bf16[256,768]{1,0:T(8,128)(2,1)S(1)} %slice.214), channel_id=1, source_target_pairs={{0,16},{4,20},{8,24},{12,28},{16,0},{20,4},{24,8},{28,12},{1,17},{... | collective-permute-start | bytes 1179656 | tf_op jit(solution)/shard_map/ppermute | solution.py:33
  105.7 22.0 %collective-permute-start.15 = (bf16[256,768]{1,0:T(8,128)(2,1)S(1)}, bf16[256,768]{1,0:T(8,128)(2,1)}, u32[]{:S(2)}, u32[]{:S(2)}) collective-permute-start(bf16[256,768]{1,0:T(8,128)(2,1)S(1)} %slice.215), channel_id=1, source_target_pairs={{0,8},{4,12},{8,0},{12,4},{16,24},{20,28},{24,16},{28,20},{1,9},{5... | collective-permute-start | bytes 1179656 | tf_op jit(solution)/shard_map/ppermute | solution.py:33
  127.7 166.6 %all-gather.8.cloned.1.call-start = ((), (), s32[]{:S(2)}) async-start(), calls=%async_computation.7 | async-start | bytes 3604480 | tf_op jit(solution)/shard_map/all_gather | solution.py:569
  130.7 45.8 %collective-permute-start.20 = (bf16[256,2048]{1,0:T(8,128)(2,1)}, bf16[256,2048]{1,0:T(8,128)(2,1)S(1)}, u32[]{:S(2)}, u32[]{:S(2)}) collective-permute-start(bf16[256,2048]{1,0:T(8,128)(2,1)} %all-gather.4.cloned.1.call-done.out_ref), channel_id=1, source_target_pairs={{0,8},{4,12},{8,0},{12,4},{16,24},{20,28},{24,16},{28,20},{1,9},{5... | collective-permute-start | bytes 3145736 | tf_op jit(solution)/shard_map/ppermute | solution.py:33
  131.3 45.3 %collective-permute-start.21 = (bf16[256,2048]{1,0:T(8,128)(2,1)}, bf16[256,2048]{1,0:T(8,128)(2,1)S(1)}, u32[]{:S(2)}, u32[]{:S(2)}) collective-permute-start(bf16[256,2048]{1,0:T(8,128)(2,1)} %all-gather.4.cloned.1.call-done.out_ref), channel_id=1, source_target_pairs={{0,16},{4,20},{8,24},{12,28},{16,0},{20,4},{24,8},{28,12},{1,17},{... | collective-permute-start | bytes 3145736 | tf_op jit(solution)/shard_map/ppermute | solution.py:33
  132.8 33.9 %collective-permute-start.18 = (bf16[256,768]{1,0:T(8,128)(2,1)S(1)}, bf16[256,768]{1,0:T(8,128)(2,1)S(1)}, u32[]{:S(2)}, u32[]{:S(2)}) collective-permute-start(bf16[256,768]{1,0:T(8,128)(2,1)S(1)} %slice.216), channel_id=1, source_target_pairs={{0,16},{4,20},{8,24},{12,28},{16,0},{20,4},{24,8},{28,12},{1,17},{... | collective-permute-start | bytes 1179656 | tf_op jit(solution)/shard_map/ppermute | solution.py:33
  135.5 31.3 %collective-permute-start.19 = (bf16[256,768]{1,0:T(8,128)(2,1)S(1)}, bf16[256,768]{1,0:T(8,128)(2,1)S(1)}, u32[]{:S(2)}, u32[]{:S(2)}) collective-permute-start(bf16[256,768]{1,0:T(8,128)(2,1)S(1)} %slice.217), channel_id=1, source_target_pairs={{0,8},{4,12},{8,0},{12,4},{16,24},{20,28},{24,16},{28,20},{1,9},{5... | collective-permute-start | bytes 1179656 | tf_op jit(solution)/shard_map/ppermute | solution.py:33
  234.5 17.9 %collective-permute-start.29 = (bf16[512,2048]{1,0:T(8,128)(2,1)}, bf16[512,2048]{1,0:T(8,128)(2,1)}, u32[]{:S(2)}, u32[]{:S(2)}) collective-permute-start(bf16[512,2048]{1,0:T(8,128)(2,1)} %get-tuple-element.385), channel_id=1, source_target_pairs={{0,4},{4,0},{8,12},{12,8},{16,20},{20,16},{24,28},{28,24},{1,5},{5... | collective-permute-start | bytes 6291464 | tf_op jit(solution)/shard_map/ppermute | solution.py:33
  236.6 254.1 %reduce-scatter.6.cloned.1.call-start = ((), (), s32[]{:S(2)}) async-start(), calls=%async_computation.8 | async-start | bytes 3604480 | tf_op jit(solution)/shard_map/reduce_scatter | solution.py:618
  323.3 179.0 %reduce-scatter.8.cloned.1.call-start = ((), (), s32[]{:S(2)}) async-start(), calls=%async_computation.9 | async-start | bytes 3604480 | tf_op jit(solution)/shard_map/reduce_scatter | solution.py:618
  349.3 173.4 %reduce-scatter.10.cloned.1.call-start = ((), (), s32[]{:S(2)}) async-start(), calls=%async_computation.10 | async-start | bytes 3604480 | tf_op jit(solution)/shard_map/reduce_scatter | solution.py:618
  392.1 41.6 %collective-permute-start.43 = (bf16[1024,768]{1,0:T(8,128)(2,1)}, bf16[1024,768]{1,0:T(8,128)(2,1)}, u32[]{:S(2)}, u32[]{:S(2)}) collective-permute-start(bf16[1024,768]{1,0:T(8,128)(2,1)} %get-tuple-element.226), channel_id=1, source_target_pairs={{0,8},{4,12},{8,0},{12,4},{16,24},{20,28},{24,16},{28,20},{1,9},{5... | collective-permute-start | bytes 4718600 | tf_op jit(solution)/shard_map/ppermute | solution.py:33
  393.6 40.1 %collective-permute-start.44 = (bf16[1024,768]{1,0:T(8,128)(2,1)}, bf16[1024,768]{1,0:T(8,128)(2,1)}, u32[]{:S(2)}, u32[]{:S(2)}) collective-permute-start(bf16[1024,768]{1,0:T(8,128)(2,1)} %get-tuple-element.227), channel_id=1, source_target_pairs={{0,16},{4,20},{8,24},{12,28},{16,0},{20,4},{24,8},{28,12},{1,17},{... | collective-permute-start | bytes 4718600 | tf_op jit(solution)/shard_map/ppermute | solution.py:33
  394.2 227.8 %reduce-scatter.12.cloned.1.call-start = ((), (), s32[]{:S(2)}) async-start(), calls=%async_computation.11 | async-start | bytes 3932160 | tf_op jit(solution)/shard_map/reduce_scatter | solution.py:653
  414.9 54.8 %collective-permute-start.47 = (bf16[1024,768]{1,0:T(8,128)(2,1)S(1)}, bf16[1024,768]{1,0:T(8,128)(2,1)S(1)}, u32[]{:S(2)}, u32[]{:S(2)}) collective-permute-start(bf16[1024,768]{1,0:T(8,128)(2,1)S(1)} %get-tuple-element.231), channel_id=1, source_target_pairs={{0,8},{4,12},{8,0},{12,4},{16,24},{20,28},{24,16},{28,20},{1,9},{5... | collective-permute-start | bytes 4718600 | tf_op jit(solution)/shard_map/ppermute | solution.py:33
  432.6 38.2 %collective-permute-start.48 = (bf16[1024,768]{1,0:T(8,128)(2,1)}, bf16[1024,768]{1,0:T(8,128)(2,1)}, u32[]{:S(2)}, u32[]{:S(2)}) collective-permute-start(bf16[1024,768]{1,0:T(8,128)(2,1)} %get-tuple-element.234), channel_id=1, source_target_pairs={{0,16},{4,20},{8,24},{12,28},{16,0},{20,4},{24,8},{28,12},{1,17},{... | collective-permute-start | bytes 4718600 | tf_op jit(solution)/shard_map/ppermute | solution.py:33
  436.7 65.5 %collective-permute-start.45 = (bf16[1024,768]{1,0:T(8,128)(2,1)}, bf16[1024,768]{1,0:T(8,128)(2,1)}, u32[]{:S(2)}, u32[]{:S(2)}) collective-permute-start(bf16[1024,768]{1,0:T(8,128)(2,1)} %add_convert_fusion.6), channel_id=1, source_target_pairs={{0,16},{4,20},{8,24},{12,28},{16,0},{20,4},{24,8},{28,12},{1,17},{... | collective-permute-start | bytes 4718600 | tf_op jit(solution)/shard_map/ppermute | solution.py:33
  441.0 61.3 %collective-permute-start.46 = (bf16[1024,768]{1,0:T(8,128)(2,1)}, bf16[1024,768]{1,0:T(8,128)(2,1)}, u32[]{:S(2)}, u32[]{:S(2)}) collective-permute-start(bf16[1024,768]{1,0:T(8,128)(2,1)} %add_convert_fusion.5), channel_id=1, source_target_pairs={{0,8},{4,12},{8,0},{12,4},{16,24},{20,28},{24,16},{28,20},{1,9},{5... | collective-permute-start | bytes 4718600 | tf_op jit(solution)/shard_map/ppermute | solution.py:33
  506.1 22.1 %collective-permute-start.54 = (bf16[512,2048]{1,0:T(8,128)(2,1)}, bf16[512,2048]{1,0:T(8,128)(2,1)}, u32[]{:S(2)}, u32[]{:S(2)}) collective-permute-start(bf16[512,2048]{1,0:T(8,128)(2,1)} %slice.329), channel_id=1, source_target_pairs={{0,4},{4,0},{8,12},{12,8},{16,20},{20,16},{24,28},{28,24},{1,5},{5... | collective-permute-start | bytes 6291464 | tf_op jit(solution)/shard_map/ppermute | solution.py:33
  512.7 26.1 %collective-permute-start.53 = (bf16[512,2048]{1,0:T(8,128)(2,1)}, bf16[512,2048]{1,0:T(8,128)(2,1)}, u32[]{:S(2)}, u32[]{:S(2)}) collective-permute-start(bf16[512,2048]{1,0:T(8,128)(2,1)} %slice.285), channel_id=1, source_target_pairs={{0,4},{4,0},{8,12},{12,8},{16,20},{20,16},{24,28},{28,24},{1,5},{5... | collective-permute-start | bytes 6291464 | tf_op jit(solution)/shard_map/ppermute | solution.py:33
  513.2 25.6 %collective-permute-start.49 = (bf16[704,512]{1,0:T(8,128)(2,1)}, bf16[704,512]{1,0:T(8,128)(2,1)}, u32[]{:S(2)}, u32[]{:S(2)}) collective-permute-start(bf16[704,512]{1,0:T(8,128)(2,1)} %reduce-scatter.6.cloned.1.call-done), channel_id=1, source_target_pairs={{0,8},{4,12},{8,0},{12,4},{16,24},{20,28},{24,16},{28,20},{1,9},{5... | collective-permute-start | bytes 2162696 | tf_op jit(solution)/shard_map/ppermute | solution.py:33
  514.4 24.4 %collective-permute-start.50 = (bf16[704,512]{1,0:T(8,128)(2,1)}, bf16[704,512]{1,0:T(8,128)(2,1)}, u32[]{:S(2)}, u32[]{:S(2)}) collective-permute-start(bf16[704,512]{1,0:T(8,128)(2,1)} %reduce-scatter.6.cloned.1.call-done), channel_id=1, source_target_pairs={{0,16},{4,20},{8,24},{12,28},{16,0},{20,4},{24,8},{28,12},{1,17},{... | collective-permute-start | bytes 2162696 | tf_op jit(solution)/shard_map/ppermute | solution.py:33
  515.8 31.2 %collective-permute-start.51 = (bf16[704,512]{1,0:T(8,128)(2,1)}, bf16[704,512]{1,0:T(8,128)(2,1)}, u32[]{:S(2)}, u32[]{:S(2)}) collective-permute-start(bf16[704,512]{1,0:T(8,128)(2,1)} %reduce-scatter.8.cloned.1.call-done), channel_id=1, source_target_pairs={{0,8},{4,12},{8,0},{12,4},{16,24},{20,28},{24,16},{28,20},{1,9},{5... | collective-permute-start | bytes 2162696 | tf_op jit(solution)/shard_map/ppermute | solution.py:33
  522.8 179.2 %reduce-scatter.14.cloned.1.call-start = ((), (), s32[]{:S(2)}) async-start(), calls=%async_computation.12 | async-start | bytes 1310720 | tf_op jit(solution)/shard_map/reduce_scatter | solution.py:674
  528.2 19.6 %collective-permute-start.52 = (bf16[704,512]{1,0:T(8,128)(2,1)}, bf16[704,512]{1,0:T(8,128)(2,1)S(1)}, u32[]{:S(2)}, u32[]{:S(2)}) collective-permute-start(bf16[704,512]{1,0:T(8,128)(2,1)} %reduce-scatter.8.cloned.1.call-done), channel_id=1, source_target_pairs={{0,16},{4,20},{8,24},{12,28},{16,0},{20,4},{24,8},{28,12},{1,17},{... | collective-permute-start | bytes 2162696 | tf_op jit(solution)/shard_map/ppermute | solution.py:33
  568.2 17.6 %collective-permute-start.60 = (bf16[2816,512]{1,0:T(8,128)(2,1)S(1)}, bf16[2816,512]{1,0:T(8,128)(2,1)S(1)}, u32[]{:S(2)}, u32[]{:S(2)}) collective-permute-start(bf16[2816,512]{1,0:T(8,128)(2,1)S(1)} %constant_dynamic-update-slice_fusion.45.same_ref), channel_id=1, source_target_pairs={{0,4},{4,0},{8,12},{12,8},{16,20},{20,16},{24,28},{28,24},{1,5},{5... | collective-permute-start | bytes 8650760 | tf_op jit(solution)/shard_map/ppermute | solution.py:33
  568.3 18.9 %collective-permute-start.61 = (bf16[2816,512]{1,0:T(8,128)(2,1)S(1)}, bf16[2816,512]{1,0:T(8,128)(2,1)S(1)}, u32[]{:S(2)}, u32[]{:S(2)}) collective-permute-start(bf16[2816,512]{1,0:T(8,128)(2,1)S(1)} %constant_dynamic-update-slice_fusion.50.same_ref), channel_id=1, source_target_pairs={{0,4},{4,0},{8,12},{12,8},{16,20},{20,16},{24,28},{28,24},{1,5},{5... | collective-permute-start | bytes 8650760 | tf_op jit(solution)/shard_map/ppermute | solution.py:33
  569.5 15.1 %collective-permute-start.63 = (bf16[128,2048]{1,0:T(8,128)(2,1)S(1)}, bf16[128,2048]{1,0:T(8,128)(2,1)S(1)}, u32[]{:S(2)}, u32[]{:S(2)}) collective-permute-start(bf16[128,2048]{1,0:T(8,128)(2,1)S(1)} %get-tuple-element.266), channel_id=1, source_target_pairs={{0,16},{4,20},{8,24},{12,28},{16,0},{20,4},{24,8},{28,12},{1,17},{... | collective-permute-start | bytes 1572872 | tf_op jit(solution)/shard_map/ppermute | solution.py:33
  583.2 22.5 %collective-permute-start.69 = (bf16[128,2048]{1,0:T(8,128)(2,1)S(1)}, bf16[128,2048]{1,0:T(8,128)(2,1)S(1)}, u32[]{:S(2)}, u32[]{:S(2)}) collective-permute-start(bf16[128,2048]{1,0:T(8,128)(2,1)S(1)} %get-tuple-element.281), channel_id=1, source_target_pairs={{0,8},{4,12},{8,0},{12,4},{16,24},{20,28},{24,16},{28,20},{1,9},{5... | collective-permute-start | bytes 1572872 | tf_op jit(solution)/shard_map/ppermute | solution.py:33
  583.8 22.5 %collective-permute-start.70 = (bf16[128,2048]{1,0:T(8,128)(2,1)S(1)}, bf16[128,2048]{1,0:T(8,128)(2,1)S(1)}, u32[]{:S(2)}, u32[]{:S(2)}) collective-permute-start(bf16[128,2048]{1,0:T(8,128)(2,1)S(1)} %get-tuple-element.282), channel_id=1, source_target_pairs={{0,16},{4,20},{8,24},{12,28},{16,0},{20,4},{24,8},{28,12},{1,17},{... | collective-permute-start | bytes 1572872 | tf_op jit(solution)/shard_map/ppermute | solution.py:33
  584.6 17.2 %collective-permute-start.71 = (bf16[64,2048]{1,0:T(8,128)(2,1)S(1)}, bf16[64,2048]{1,0:T(8,128)(2,1)S(1)}, u32[]{:S(2)}, u32[]{:S(2)}) collective-permute-start(bf16[64,2048]{1,0:T(8,128)(2,1)S(1)} %get-tuple-element.351), channel_id=1, source_target_pairs={{0,8},{4,12},{8,0},{12,4},{16,24},{20,28},{24,16},{28,20},{1,9},{5... | collective-permute-start | bytes 786440 | tf_op jit(solution)/shard_map/ppermute | solution.py:33
  585.8 18.5 %collective-permute-start.72 = (bf16[64,2048]{1,0:T(8,128)(2,1)S(1)}, bf16[64,2048]{1,0:T(8,128)(2,1)S(1)}, u32[]{:S(2)}, u32[]{:S(2)}) collective-permute-start(bf16[64,2048]{1,0:T(8,128)(2,1)S(1)} %get-tuple-element.350), channel_id=1, source_target_pairs={{0,16},{4,20},{8,24},{12,28},{16,0},{20,4},{24,8},{28,12},{1,17},{... | collective-permute-start | bytes 786440 | tf_op jit(solution)/shard_map/ppermute | solution.py:33
  587.4 32.3 %collective-permute-start.65 = (bf16[128,2048]{1,0:T(8,128)(2,1)S(1)}, bf16[128,2048]{1,0:T(8,128)(2,1)S(1)}, u32[]{:S(2)}, u32[]{:S(2)}) collective-permute-start(bf16[128,2048]{1,0:T(8,128)(2,1)S(1)} %add_convert_fusion.10), channel_id=1, source_target_pairs={{0,16},{4,20},{8,24},{12,28},{16,0},{20,4},{24,8},{28,12},{1,17},{... | collective-permute-start | bytes 1572872 | tf_op jit(solution)/shard_map/ppermute | solution.py:33
  601.8 18.6 %collective-permute-start.66 = (bf16[128,2048]{1,0:T(8,128)(2,1)S(1)}, bf16[128,2048]{1,0:T(8,128)(2,1)S(1)}, u32[]{:S(2)}, u32[]{:S(2)}) collective-permute-start(bf16[128,2048]{1,0:T(8,128)(2,1)S(1)} %add_convert_fusion.9), channel_id=1, source_target_pairs={{0,8},{4,12},{8,0},{12,4},{16,24},{20,28},{24,16},{28,20},{1,9},{5... | collective-permute-start | bytes 1572872 | tf_op jit(solution)/shard_map/ppermute | solution.py:33
  604.2 15.4 %collective-permute-start.67 = (bf16[64,2048]{1,0:T(8,128)(2,1)S(1)}, bf16[64,2048]{1,0:T(8,128)(2,1)S(1)}, u32[]{:S(2)}, u32[]{:S(2)}) collective-permute-start(bf16[64,2048]{1,0:T(8,128)(2,1)S(1)} %get-tuple-element.353), channel_id=1, source_target_pairs={{0,8},{4,12},{8,0},{12,4},{16,24},{20,28},{24,16},{28,20},{1,9},{5... | collective-permute-start | bytes 786440 | tf_op jit(solution)/shard_map/ppermute | solution.py:33
  622.0 34.5 %collective-permute-start.76 = (bf16[512,768]{1,0:T(8,128)(2,1)}, bf16[512,768]{1,0:T(8,128)(2,1)S(1)}, u32[]{:S(2)}, u32[]{:S(2)}) collective-permute-start(bf16[512,768]{1,0:T(8,128)(2,1)} %reduce-scatter.12.cloned.1.call-done), channel_id=1, source_target_pairs={{0,8},{4,12},{8,0},{12,4},{16,24},{20,28},{24,16},{28,20},{1,9},{5... | collective-permute-start | bytes 2359304 | tf_op jit(solution)/shard_map/ppermute | solution.py:33
  623.2 33.3 %collective-permute-start.77 = (bf16[512,768]{1,0:T(8,128)(2,1)}, bf16[512,768]{1,0:T(8,128)(2,1)S(1)}, u32[]{:S(2)}, u32[]{:S(2)}) collective-permute-start(bf16[512,768]{1,0:T(8,128)(2,1)} %reduce-scatter.12.cloned.1.call-done), channel_id=1, source_target_pairs={{0,16},{4,20},{8,24},{12,28},{16,0},{20,4},{24,8},{28,12},{1,17},{... | collective-permute-start | bytes 2359304 | tf_op jit(solution)/shard_map/ppermute | solution.py:33
  623.7 31.1 %collective-permute-start.74 = (bf16[704,512]{1,0:T(8,128)(2,1)}, bf16[704,512]{1,0:T(8,128)(2,1)S(1)}, u32[]{:S(2)}, u32[]{:S(2)}) collective-permute-start(bf16[704,512]{1,0:T(8,128)(2,1)} %reduce-scatter.10.cloned.1.call-done), channel_id=1, source_target_pairs={{0,8},{4,12},{8,0},{12,4},{16,24},{20,28},{24,16},{28,20},{1,9},{5... | collective-permute-start | bytes 2162696 | tf_op jit(solution)/shard_map/ppermute | solution.py:33
  624.6 31.8 %collective-permute-start.75 = (bf16[704,512]{1,0:T(8,128)(2,1)}, bf16[704,512]{1,0:T(8,128)(2,1)S(1)}, u32[]{:S(2)}, u32[]{:S(2)}) collective-permute-start(bf16[704,512]{1,0:T(8,128)(2,1)} %reduce-scatter.10.cloned.1.call-done), channel_id=1, source_target_pairs={{0,16},{4,20},{8,24},{12,28},{16,0},{20,4},{24,8},{28,12},{1,17},{... | collective-permute-start | bytes 2162696 | tf_op jit(solution)/shard_map/ppermute | solution.py:33
  656.5 15.7 %collective-permute-start.78 = (bf16[256,768]{1,0:T(8,128)(2,1)S(1)}, bf16[256,768]{1,0:T(8,128)(2,1)S(1)}, u32[]{:S(2)}, u32[]{:S(2)}) collective-permute-start(bf16[256,768]{1,0:T(8,128)(2,1)S(1)} %slice.259), channel_id=1, source_target_pairs={{0,16},{4,20},{8,24},{12,28},{16,0},{20,4},{24,8},{28,12},{1,17},{... | collective-permute-start | bytes 1179656 | tf_op jit(solution)/shard_map/ppermute | solution.py:33
  673.7 32.9 %collective-permute-start.82 = (bf16[2048,768]{1,0:T(8,128)(2,1)}, bf16[2048,768]{1,0:T(8,128)(2,1)}, u32[]{:S(2)}, u32[]{:S(2)}) collective-permute-start(bf16[2048,768]{1,0:T(8,128)(2,1)} %constant_dynamic-update-slice_fusion.55.same_ref), channel_id=1, source_target_pairs={{0,4},{4,0},{8,12},{12,8},{16,20},{20,16},{24,28},{28,24},{1,5},{5... | collective-permute-start | bytes 9437192 | tf_op jit(solution)/shard_map/ppermute | solution.py:33
  676.2 28.9 %collective-permute-start.83 = (bf16[2816,512]{1,0:T(8,128)(2,1)}, bf16[2816,512]{1,0:T(8,128)(2,1)}, u32[]{:S(2)}, u32[]{:S(2)}) collective-permute-start(bf16[2816,512]{1,0:T(8,128)(2,1)} %constant_dynamic-update-slice_fusion.60.same_ref), channel_id=1, source_target_pairs={{0,4},{4,0},{8,12},{12,8},{16,20},{20,16},{24,28},{28,24},{1,5},{5... | collective-permute-start | bytes 8650760 | tf_op jit(solution)/shard_map/ppermute | solution.py:33
  676.8 26.6 %collective-permute-start.84 = (bf16[64,2048]{1,0:T(8,128)(2,1)S(1)}, bf16[64,2048]{1,0:T(8,128)(2,1)S(1)}, u32[]{:S(2)}, u32[]{:S(2)}) collective-permute-start(bf16[64,2048]{1,0:T(8,128)(2,1)S(1)} %get-tuple-element.349), channel_id=1, source_target_pairs={{0,16},{4,20},{8,24},{12,28},{16,0},{20,4},{24,8},{28,12},{1,17},{... | collective-permute-start | bytes 786440 | tf_op jit(solution)/shard_map/ppermute | solution.py:33
  678.3 26.7 %collective-permute-start.85 = (bf16[64,2048]{1,0:T(8,128)(2,1)S(1)}, bf16[64,2048]{1,0:T(8,128)(2,1)S(1)}, u32[]{:S(2)}, u32[]{:S(2)}) collective-permute-start(bf16[64,2048]{1,0:T(8,128)(2,1)S(1)} %get-tuple-element.348), channel_id=1, source_target_pairs={{0,8},{4,12},{8,0},{12,4},{16,24},{20,28},{24,16},{28,20},{1,9},{5... | collective-permute-start | bytes 786440 | tf_op jit(solution)/shard_map/ppermute | solution.py:33
  702.0 19.2 %collective-permute-start.86 = (bf16[256,512]{1,0:T(8,128)(2,1)}, bf16[256,512]{1,0:T(8,128)(2,1)S(1)}, u32[]{:S(2)}, u32[]{:S(2)}) collective-permute-start(bf16[256,512]{1,0:T(8,128)(2,1)} %reduce-scatter.14.cloned.1.call-done), channel_id=1, source_target_pairs={{0,8},{4,12},{8,0},{12,4},{16,24},{20,28},{24,16},{28,20},{1,9},{5... | collective-permute-start | bytes 786440 | tf_op jit(solution)/shard_map/ppermute | solution.py:33
  703.4 17.8 %collective-permute-start.87 = (bf16[256,512]{1,0:T(8,128)(2,1)}, bf16[256,512]{1,0:T(8,128)(2,1)S(1)}, u32[]{:S(2)}, u32[]{:S(2)}) collective-permute-start(bf16[256,512]{1,0:T(8,128)(2,1)} %reduce-scatter.14.cloned.1.call-done), channel_id=1, source_target_pairs={{0,16},{4,20},{8,24},{12,28},{16,0},{20,4},{24,8},{28,12},{1,17},{... | collective-permute-start | bytes 786440 | tf_op jit(solution)/shard_map/ppermute | solution.py:33
  705.0 16.2 %collective-permute-start.88 = (f32[2,512]{1,0:T(2,128)S(1)}, f32[2,512]{1,0:T(2,128)S(1)}, u32[]{:S(2)}, u32[]{:S(2)}) collective-permute-start(f32[2,512]{1,0:T(2,128)S(1)} %get-tuple-element.394), channel_id=1, source_target_pairs={{0,1},{1,2},{2,3},{3,0},{4,5},{5,6},{6,7},{7,4},{8,9},{9,10},{10,1... | collective-permute-start | bytes 12296 | tf_op jit(solution)/shard_map/ppermute | solution.py:159
  705.1 16.1 %collective-permute-start.89 = (f32[2,512]{1,0:T(2,128)S(1)}, f32[2,512]{1,0:T(2,128)S(1)}, u32[]{:S(2)}, u32[]{:S(2)}) collective-permute-start(f32[2,512]{1,0:T(2,128)S(1)} %get-tuple-element.393), channel_id=1, source_target_pairs={{0,2},{1,3},{2,0},{3,1},{4,6},{5,7},{6,4},{7,5},{8,10},{9,11},{10,... | collective-permute-start | bytes 12296 | tf_op jit(solution)/shard_map/ppermute | solution.py:159
  723.1 15.3 %collective-permute-start.92 = (bf16[128,512]{1,0:T(8,128)(2,1)}, bf16[128,512]{1,0:T(8,128)(2,1)S(1)}, u32[]{:S(2)}, u32[]{:S(2)}) collective-permute-start(bf16[128,512]{1,0:T(8,128)(2,1)} %slice.268), channel_id=1, source_target_pairs={{0,8},{4,12},{8,0},{12,4},{16,24},{20,28},{24,16},{28,20},{1,9},{5... | collective-permute-start | bytes 393224 | tf_op jit(solution)/shard_map/ppermute | solution.py:33
  (137 other events, 1286.1 us)
Sparse Core Ops, SparseCore 0:
  94.5 25.1 all-gather.3
  127.8 103.0 all-gather.5
  236.7 57.5 all-gather.7
  323.4 54.9 reduce-scatter.5
  381.1 56.0 reduce-scatter.7
  439.3 56.0 reduce-scatter.9
  522.9 58.3 reduce-scatter.11
  676.8 25.0 reduce-scatter.13

commit v4 on v3

--- a/solution.py
+++ b/solution.py
@@ -138,6 +138,35 @@
     return sums[0]
 
 
+def exchange_steps(blocks):
+    bits = chip_bits()
+    if len(bits) == 2:
+        one, two = bits
+        top, bottom = yield [swap(h, bit) for h, bit in zip(halves(blocks[one ^ two]), bits)]
+        near = [swap(blocks[one], one), swap(blocks[two], two)]
+        by_one, by_two, top, bottom = yield [*near, swap(top, two), swap(bottom, one)]
+        both = lambda v: [(v, 0), (v, 1)]
+        return {
+            0: both(blocks[0]),
+            one: both(by_one),
+            two: both(by_two),
+            one ^ two: [(top, 0), (bottom, 0)],
+        }
+    while len(blocks) < len(chip_offsets()):
+        yield []
+    size = lax.axis_size("rep")
+    away = [d for d in chip_offsets() if d]
+    new = yield [lax.ppermute(blocks[d], "rep", [(i, i ^ d) for i in range(size)]) for d in away]
+    return {d: [(v, 0), (v, 1)] for d, v in zip([0, *away], [blocks[0], *new])}
+
+
+def token_steps(own, other):
+    blocks = yield from gather_steps(own)
+    away = [d for d in chip_offsets() if d]
+    new = yield [swap(blocks[d], 1) for d in away]
+    return {0: (own, other), **{d: (blocks[d], n) for d, n in zip(away, new)}}
+
+
 def plane_sum_steps(partial):
     half = partial.shape[0] // 2
     (other,) = yield [swap(partial[half:], 1)]
@@ -279,12 +308,11 @@
 
 
 def attend_back_kernel(
-    grad_ref, out_ref, qkv_ref, lse_ref, x_ref, cos_ref, sin_ref, col_ref, row_ref,
-    lin_ref, top_ref, bottom_ref, kept_ref, context_ref, keys_ref, values_ref,
+    grad_ref, out_ref, qkv_ref, lse_ref, cos_ref, sin_ref, col_ref, row_ref,
+    lin_ref, context_ref, keys_ref, values_ref,
 ):
     length, wide = qkv_ref.shape
     width = wide // 3
-    seq = pl.program_id(0)
     tile = min(length, 256)
 
     @pl.loop(0, length // tile)
@@ -315,23 +343,10 @@
             lin_ref[rows, q_at] = rotate(grad_queries, cos[rows], -sin[rows]).astype(BF)
         lin_ref[:, k_at] = rotate(keys_ref[...] * scale, cos, -sin).astype(BF)
         lin_ref[:, v_at] = values_ref[...].astype(BF)
-    kept_ref[pl.ds(pl.multiple_of(seq * length, length), length), :] = lin_ref[...]
-
-    @pl.when(seq == pl.num_programs(0) - 1)
-    def _():
-        half = top_ref.shape[0]
-        step = 256
-        for n, ref in enumerate((top_ref, bottom_ref)):
-
-            @pl.loop(0, half // step)
-            def _(t):
-                cols = pl.ds(pl.multiple_of(n * half + t * step, step), step)
-                rows = pl.ds(pl.multiple_of(t * step, step), step)
-                ref[rows, :] = mm_tn(x_ref[:, cols], kept_ref[...]).astype(BF)
-
-
-def attend_back(grad, out_w, qkv, lse, both, tables, seg):
-    rows, depth = both.shape
+
+
+def attend_back(grad, out_w, qkv, lse, tables, seg):
+    rows, depth = grad.shape
     length = tables[0].shape[0]
     wide = qkv.shape[1]
     width = wide // 3
@@ -341,31 +356,58 @@
         attend_back_kernel,
         grid=(rows // length,),
         in_specs=[by_seq(depth), whole(width, depth), by_seq(wide), by_seq(width // HD)]
-        + [whole(rows, depth), whole(length, HD), whole(length, HD)]
+        + [whole(length, HD)] * 2
         + [
             pl.BlockSpec((1, length, 1), lambda s: (s, 0, 0)),
             pl.BlockSpec((1, 1, length), lambda s: (s, 0, 0)),
         ],
-        out_specs=[by_seq(wide), whole(depth // 2, wide), whole(depth // 2, wide)],
+        out_specs=by_seq(wide),
         scratch_shapes=[
-            pltpu.VMEM((rows, wide), BF),
             pltpu.VMEM((length, width), BF),
             pltpu.VMEM((length, HD), F32),
             pltpu.VMEM((length, HD), F32),
         ],
-        out_shape=[
-            jax.ShapeDtypeStruct((rows, wide), BF),
-            jax.ShapeDtypeStruct((depth // 2, wide), BF),
-            jax.ShapeDtypeStruct((depth // 2, wide), BF),
-        ],
+        out_shape=jax.ShapeDtypeStruct((rows, wide), BF),
         compiler_params=pltpu.CompilerParams(vmem_limit_bytes=48 << 20),
         cost_estimate=pl.CostEstimate(
-            flops=2 * rows * depth * (wide + width) + 10 * rows * 2 * WIN * width,
-            bytes_accessed=2 * (2 * rows * depth + depth * (wide + width) + 2 * rows * wide),
+            flops=2 * rows * depth * width + 10 * rows * 2 * WIN * width,
+            bytes_accessed=2 * (rows * depth + depth * width + 2 * rows * wide),
             transcendentals=rows * 2 * WIN * width // HD,
         ),
         name="attend_back",
-    )(grad, out_w, qkv, lse, both, *tables, *seg)
+    )(grad, out_w, qkv, lse, *tables, *seg)
+
+
+def weight_grad_kernel(count, *refs):
+    total = mm_tn(refs[0][...], refs[count][...])
+    for n in range(1, count):
+        total += mm_tn(refs[n][...], refs[count + n][...])
+    refs[-1][...] = total.astype(BF)
+
+
+def weight_grad(tokens, grads):
+    rows, depth = tokens[0].shape
+    wide = grads[0][0].shape[1]
+    tile = min(depth, 256)
+
+    def part(index):
+        return pl.BlockSpec((rows, wide), lambda i: (index, 0), pipeline_mode=pl.Buffered(1))
+
+    return pl.pallas_call(
+        functools.partial(weight_grad_kernel, len(tokens)),
+        grid=(depth // tile,),
+        in_specs=[pl.BlockSpec((rows, tile), lambda i: (0, i))] * len(tokens)
+        + [part(index) for _, index in grads],
+        out_specs=pl.BlockSpec((tile, wide), lambda i: (i, 0)),
+        out_shape=jax.ShapeDtypeStruct((depth, wide), BF),
+        compiler_params=pltpu.CompilerParams(vmem_limit_bytes=40 << 20),
+        cost_estimate=pl.CostEstimate(
+            flops=2 * rows * len(tokens) * depth * wide,
+            bytes_accessed=2 * len(tokens) * rows * (depth + wide) + 2 * depth * wide,
+            transcendentals=0,
+        ),
+        name="weight_grad",
+    )(*tokens, *[g for g, _ in grads])
 
 
 def normed_back_kernel(blocks, parts, z_ref, *refs):
@@ -592,12 +634,13 @@
     normed_two = (hidden * root_two * gain_two).astype(BF)
 
     disp_flow = Flow(copies_steps(mm(pick, normed_two).astype(BF)))
-    stage([disp_flow])
-    slot_grad, gate_up = stage([disp_flow], (slot_grad, gate_up))
+    slot_grad = stage([disp_flow], slot_grad)
     slot_flow = Flow(copies_steps(slot_grad))
+    gate_up, normed = stage([disp_flow, slot_flow], (gate_up, normed))
     stage([disp_flow, slot_flow])
+    token_flow = Flow(token_steps(normed, other))
     dispatched = jnp.concatenate(finish(disp_flow), axis=0)
-    act = mm(dispatched, gate_up)
+    act = stage([token_flow, slot_flow], mm(dispatched, gate_up))
     all_slot_grad = jnp.concatenate(finish(slot_flow), axis=0)
     gate_act, up_act = act[:, :units], act[:, units:]
     sigmoid = jax.nn.sigmoid(gate_act)
@@ -608,13 +651,13 @@
     grad_up_act = (grad_inner * silu).astype(BF)
     grad_act = jnp.concatenate([grad_gate_act, grad_up_act], axis=1)
     back_flow = Flow(plane_sum_steps(mm_nt(grad_act, gate_up).astype(BF)))
-    grad_mlp, sums = [], []
+    sums = []
     for left, right in (
         (grad_gate_act, dispatched),
         (grad_up_act, dispatched),
         (inner, all_slot_grad),
     ):
-        grad = stage([back_flow], mm_tn(left, right).astype(BF))
+        grad = stage([back_flow, token_flow], mm_tn(left, right).astype(BF))
         sums.append(lax.psum_scatter(grad, "shard", scatter_dimension=1, tiled=True))
     grad_normed_two = mm_tn(pick, finish(back_flow))
     grad_gain_two, through = norm_back(grad_normed_two, hidden, root_two, gain_two)
@@ -622,64 +665,62 @@
 
     grad_projected = (grad_hidden * attn_weight).astype(BF)
     both_grad = jnp.concatenate([grad_projected, swap(grad_projected, 1)], axis=0)
-    lins, grad_qkv_w = {}, {}
+    lins = {}
 
     def run_back(*ds):
         for d in ds:
-            lins[d], *grad_qkv_w[d] = attend_back(
-                both_grad, out_w[d], *saved[d], both, tables, seg
-            )
-        return [(lins[d], grad_qkv_w[d]) for d in ds]
-
-    def keep(ds, values):
-        for d, (lin, grad) in zip(ds, values):
-            lins[d], grad_qkv_w[d] = lin, grad
+            lins[d] = attend_back(both_grad, out_w[d], *saved[d], tables, seg)
+        return [lins[d] for d in ds]
 
     far, near = offsets[-1:], offsets[1:-1]
-    values, both_grad = lax.optimization_barrier((run_back(*far), both_grad))
-    keep(far, values)
-    qkv_flow = Flow(scatter_steps(grad_qkv_w))
-    values, both_grad = stage([qkv_flow], (run_back(*near), both_grad))
-    keep(near, values)
-    values, grad_out_w = stage([qkv_flow], (run_back(0), mm_tn(all_context, both_grad).astype(BF)))
-    keep([0], values)
+    tokens = finish(token_flow)
+    expert_flow = Flow(plane_sum_steps(mm(inner, down).astype(BF)))
+    far_lin, both_grad = lax.optimization_barrier((run_back(*far), both_grad))
+    lins.update(zip(far, far_lin))
+    lin_flow = Flow(exchange_steps(lins))
+    near_lin, both_grad = stage([lin_flow, expert_flow], (run_back(*near), both_grad))
+    lins.update(zip(near, near_lin))
+    own_lin, grad_out_w = (run_back(0), mm_tn(all_context, both_grad).astype(BF))
     grad_normed = normed_back(
         shard, [lins[d] for d in offsets], [qkv_w[d] for d in offsets], both.shape[1]
     )
-    sums[0], sums[1], grad_normed, grad_out_w = stage(
-        [qkv_flow], (sums[0], sums[1], grad_normed, grad_out_w)
+    grad_normed, grad_out_w, sums[0] = stage([lin_flow], (grad_normed, grad_out_w, sums[0]))
+    parts = finish(lin_flow)
+    own_grad_qkv = weight_grad(
+        [x for d in offsets for x in tokens[d]], [g for d in offsets for g in parts[d]]
     )
-    own_grad_qkv, sums[2] = lax.optimization_barrier((finish(qkv_flow), sums[2]))
+    own_grad_qkv, sums[2] = lax.optimization_barrier((own_grad_qkv, sums[2]))
     sum_qkv = lax.psum_scatter(own_grad_qkv, "shard", scatter_dimension=0, tiled=True)
-    grad_normed = grad_normed[:length] + swap(grad_normed[length:].astype(BF), 1).astype(F32)
+
+    out_blocks = {d: halves(grad_out_w[i * block : (i + 1) * block]) for i, d in enumerate(offsets)}
+    out_flow = Flow(scatter_steps(out_blocks))
+    gate_flow = Flow(copies_steps(sums[0]))
+    sums[1], other_normed = stage(
+        [out_flow, gate_flow], (sums[1], swap(grad_normed[length:].astype(BF), 1))
+    )
+    grad_normed = grad_normed[:length] + other_normed.astype(F32)
     grad_gain_one, first = norm_back(grad_normed, inputs, root_one, gain_one)
     grad_input = (grad_hidden + first).astype(BF)
-
-    out_blocks = {d: halves(grad_out_w[i * block : (i + 1) * block]) for i, d in enumerate(offsets)}
-    expert_out = mm(inner, down).astype(BF)
-    gate_flow, expert_flow = Flow(copies_steps(sums[0])), Flow(plane_sum_steps(expert_out))
+    grad_input, gains = stage(
+        [out_flow, gate_flow], (grad_input, jnp.stack([grad_gain_one, grad_gain_two]))
+    )
     up_flow = Flow(copies_steps(sums[1]))
-    grad_input, gains, out_blocks = stage(
-        [gate_flow, up_flow, expert_flow],
-        (grad_input, jnp.stack([grad_gain_one, grad_gain_two]), out_blocks),
-    )
-    gain_flow, out_flow = Flow(vector_sum_steps(gains)), Flow(scatter_steps(out_blocks))
-    stage([gate_flow, up_flow, gain_flow])
-    stage([gate_flow, up_flow, out_flow, gain_flow])
-    stage([out_flow, expert_flow, gain_flow])
-    sums[2] = stage([out_flow, expert_flow], sums[2])
+    sums[2] = stage([out_flow, gate_flow, up_flow], sums[2])
+    own_grad_out, _ = lax.optimization_barrier((finish(out_flow), sum_qkv))
+    sum_out = lax.psum_scatter(own_grad_out, "shard", scatter_dimension=1, tiled=True)
+    down_flow, gain_flow = Flow(copies_steps(sums[2])), Flow(vector_sum_steps(gains))
     grad_gate = place_turned(whoami, *finish(gate_flow), units)
+    grad_gate, sum_qkv = stage([up_flow, down_flow, gain_flow], (grad_gate, sum_qkv))
+    qkv_flow = Flow(copies_steps(sum_qkv))
+    stage([qkv_flow, up_flow, down_flow])
     grad_up = place_turned(whoami, *finish(up_flow), units)
-    own_grad_out, sum_qkv = lax.optimization_barrier((finish(out_flow), sum_qkv))
-    sum_out = lax.psum_scatter(own_grad_out, "shard", scatter_dimension=1, tiled=True)
-    down_flow, qkv_flow = Flow(copies_steps(sums[2])), Flow(copies_steps(sum_qkv))
-    grad_gate, grad_up = stage([down_flow, qkv_flow], (grad_gate, grad_up))
-    stage([qkv_flow, down_flow])
-    stage([qkv_flow, down_flow, expert_flow])
+    grad_up, sum_out = stage([qkv_flow, down_flow, gain_flow], (grad_up, sum_out))
+    out_flow = Flow(copies_steps(sum_out))
     (grad_down,) = place(whoami, *finish(down_flow), units, own, False)
-    out_flow = Flow(copies_steps(sum_out))
-    grad_down = stage([out_flow, gain_flow], grad_down)
+    grad_down = stage([qkv_flow, out_flow, gain_flow], grad_down)
     grad_query, grad_key, grad_value = place(whoami, *finish(qkv_flow), own, block, True)
+    grad_query = stage([out_flow, expert_flow, gain_flow], grad_query)
+    stage([out_flow, expert_flow])
     output = (hidden + mm_tn(pick, finish(expert_flow)) * mix[:, None]).astype(BF)
     (grad_out,) = place(whoami, *finish(out_flow), block, own, False)
     gain_grads = finish(gain_flow)

time: 768 us -> 799 us (1.040)
  waiting for transfers between devices: 249 us -> 274 us
  local copies, waits for them, and re-layouts: 104 us -> 119 us
  Pallas kernels: 170 us -> 158 us
    ppermute x85 -> x92, waiting for transfers between devices: 182 us -> 229 us  [swap(): return lax.ppermute(value, 'rep', [(i, i ^ bit) for i in range(size)])]
    pallas_call x4, Pallas kernels: 68.7 us -> 37.7 us  [attend_back(): pl.pallas_call(attend_back_kernel, grid=(rows // length,), in_specs=[by_s...]
    all_gather x1, waiting for transfers between devices: 21.9 us -> 0.01 us  [per_device(): down = lax.all_gather(own_down, 'shard', axis=1, tiled=True)]
    pallas_call x0 -> x1, Pallas kernels: none -> 19.1 us  [weight_grad(): pl.pallas_call(functools.partial(weight_grad_kernel, len(tokens)), grid=(...]
    ppermute x2, waiting for transfers between devices: 3.14 us -> 19.1 us  [per_device(): piece, other = stage(flows, (lax.ppermute(piece, 'shard', ring), other))]
    reduce_scatter x1, waiting for transfers between devices: 23.1 us -> 9.76 us  [per_device(): lax.psum_scatter(own_grad_out, 'shard', scatter_dimension=1, tiled=True)]
    slice x22 -> x24, local copies, waits for them, and re-layouts: 10.3 us -> 19.7 us  [gather_steps(): top, bottom = (yield [swap(by_one[:half], two), swap(by_two[half:], one)])]
    ppermute x85 -> x92, starting transfers between devices: 76.2 us -> 84.5 us  [swap(): return lax.ppermute(value, 'rep', [(i, i ^ bit) for i in range(size)])]
  transfers between devices with their start and end apart: 102 -> 109, of which waited for: 39 -> 25; matrix products, arithmetic and copies ran while one was open for 23% -> 22% of each run, Pallas kernels for 21% -> 20%
where the time goes in v4:
time: 799 us; the launch traced here: 790 us
  waiting for transfers between devices  274 us (34%)
  Pallas kernels  158 us (20%)
  local copies, waits for them, and re-layouts  119 us (15%)
  starting transfers between devices  96.7 us (12%)
  matrix products  70.7 us (9%)
  other arithmetic  54.2 us (7%)
  between operations  16.4 us (2%)
    ppermute x92, waiting for transfers between devices, swap(): return lax.ppermute(value, 'rep', [(i, i ^ bit) for i in range(size)])  229 us
    ppermute x92, starting transfers between devices, swap(): return lax.ppermute(value, 'rep', [(i, i ^ bit) for i in range(size)])  84.5 us
    unnamed x287, local copies, waits for them, and re-layouts  64 us
    pallas_call x4, Pallas kernels, attend(): pl.pallas_call(functools.partial(attend_kernel, parts), grid_spec=pltpu.P...  41.7 us
    pallas_call x4, Pallas kernels, attend_back(): pl.pallas_call(attend_back_kernel, grid=(rows // length,), in_specs=[by_s...  37.7 us
    dot_general x6, matrix products, mm_tn(): lax.dot_general(left, right, (((0,), (0,)), ((), ())), preferred_element_...  33.2 us
    pallas_call x3, Pallas kernels, place(): pl.pallas_call(place_kernel, grid_spec=pltpu.PrefetchScalarGridSpec(num_s...  27.9 us
    pallas_call x1, Pallas kernels, normed_back(): pl.pallas_call(functools.partial(normed_back_kernel, len(lins), parts), g...  20.1 us
  transfers between devices with their start and end apart: 109, of which 25 were waited for; matrix products, arithmetic and copies ran while one was open for 22% of the time, Pallas kernels for 20%

profile of v4, /device:TPU:0, one launch (start us, length us, event | category | flops | bytes accessed | tf_op | source)
XLA Modules:
  0.0 789.8 jit_solution(7722688211504365417)
XLA Ops:
  8.8 3.1 collective-permute-start.2
  11.8 2.6 collective-permute-start.1
  17.7 2.7 constant_dynamic-slice_fusion.5
  21.2 2.3 constant_dynamic-slice_fusion.15
  26.2 16.2 %collective-permute-done.3.refs_5_ = bf16[512,768]{1,0:T(8,128)(2,1)} collective-permute-done((bf16[512,768]{1,0:T(8,128)(2,1)S(1)}, bf16[512,768]{1,0:T(8,128)(2,1)}, u32[]{:S(2)}, u32[]{:S(2)}) %collective-permute-start.3) | collective-permute-done | bytes 786464 | tf_op jit(solution)/shard_map/ppermute | solution.py:582
  49.0 19.1 %collective-permute-done.7.refs_6_ = bf16[512,768]{1,0:T(8,128)(2,1)} collective-permute-done((bf16[512,768]{1,0:T(8,128)(2,1)}, bf16[512,768]{1,0:T(8,128)(2,1)}, u32[]{:S(2)}, u32[]{:S(2)}) %collective-permute-start.7) | collective-permute-done | bytes 786464 | tf_op jit(solution)/shard_map/ppermute | solution.py:596
  74.7 22.7 %collective-permute-done.10 = bf16[256,768]{1,0:T(8,128)(2,1)} collective-permute-done((bf16[256,768]{1,0:T(8,128)(2,1)}, bf16[256,768]{1,0:T(8,128)(2,1)}, u32[]{:S(2)}, u32[]{:S(2)}) %collective-permute-start.10) | collective-permute-done | bytes 393248 | tf_op jit(solution)/shard_map/ppermute | solution.py:33
  100.7 2.2 pad_maximum_fusion.6.refs_4_.refs_8_
  114.4 10.9 %attend.4 = (bf16[1024,256]{1,0:T(8,128)(2,1)S(1)}, bf16[1024,768]{1,0:T(8,128)(2,1)S(1)}, f32[1024,2]{1,0:T(8,128)S(1)}) custom-call(s32[1]{0:T(128)} %bitcast.1.z_ref, bf16[1024,2048]{1,0:T(8,128)(2,1)S(1)} %pad_maximum_fusion.refs_0_.refs_1_.refs_2_.refs_3_, bf16[1024,2048]{1,0:T(8,128)(2,1)S(1)} %pad_maximum_fusion.refs_0_.refs_1_.refs_2_.refs_3_, ...), custom_call_target="tpu_custom_call" | custom-call | flops 3758096384 | bytes 10485760 | tf_op jit(solution)/shard_map/attend/pallas_call | solution.py:280
  128.0 3.1 collective-permute-done.15
  141.0 2.5 copy-done.3
  143.5 10.7 %attend.5 = (bf16[1024,256]{1,0:T(8,128)(2,1)S(1)}, bf16[1024,768]{1,0:T(8,128)(2,1)S(1)}, f32[1024,2]{1,0:T(8,128)S(1)}) custom-call(s32[1]{0:T(128)} %bitcast.1.z_ref, bf16[1024,2048]{1,0:T(8,128)(2,1)S(1)} %copy-done.3, bf16[1024,2048]{1,0:T(8,128)(2,1)S(1)} %copy-done.3, bf16[1024,2048]{1,0:T(8,128)(2,1)S(1)} %copy-done.3, ...), custom_call_target="tpu_custom_call" | custom-call | flops 3758096384 | bytes 10485760 | tf_op jit(solution)/shard_map/attend/pallas_call | solution.py:280
  156.3 10.5 %attend.6 = (bf16[1024,256]{1,0:T(8,128)(2,1)S(1)}, bf16[1024,768]{1,0:T(8,128)(2,1)S(1)}, f32[1024,2]{1,0:T(8,128)S(1)}) custom-call(s32[1]{0:T(128)} %bitcast.1.z_ref, bf16[1024,2048]{1,0:T(8,128)(2,1)S(1)} %copy-done.3, bf16[1024,2048]{1,0:T(8,128)(2,1)S(1)} %copy-done.3, bf16[1024,2048]{1,0:T(8,128)(2,1)S(1)} %copy-done.3, ...), custom_call_target="tpu_custom_call" | custom-call | flops 3758096384 | bytes 10485760 | tf_op jit(solution)/shard_map/attend/pallas_call | solution.py:280
  169.4 9.6 %attend.7 = (bf16[1024,256]{1,0:T(8,128)(2,1)S(1)}, bf16[1024,768]{1,0:T(8,128)(2,1)S(1)}, f32[1024,2]{1,0:T(8,128)S(1)}) custom-call(s32[1]{0:T(128)} %bitcast.1.z_ref, bf16[1024,2048]{1,0:T(8,128)(2,1)S(1)} %copy-done.3, bf16[1024,2048]{1,0:T(8,128)(2,1)S(1)} %copy-done.3, bf16[1024,2048]{1,0:T(8,128)(2,1)S(1)} %copy-done.3, ...), custom_call_target="tpu_custom_call" | custom-call | flops 3758096384 | bytes 10485760 | tf_op jit(solution)/shard_map/attend/pallas_call | solution.py:280
  182.6 7.0 collective-permute-done.22
  191.6 4.5 fusion.55
  197.1 3.6 collective-permute-done.24
  207.0 10.9 %collective-permute-done.26 = bf16[128,2048]{1,0:T(8,128)(2,1)S(1)} collective-permute-done((bf16[128,2048]{1,0:T(8,128)(2,1)S(1)}, bf16[128,2048]{1,0:T(8,128)(2,1)S(1)}, u32[]{:S(2)}, u32[]{:S(2)}) %collective-permute-start.26) | collective-permute-done | bytes 524320 | tf_op jit(solution)/shard_map/ppermute | solution.py:33
  223.0 15.0 %collective-permute-done.28 = bf16[64,2048]{1,0:T(8,128)(2,1)S(1)} collective-permute-done((bf16[64,2048]{1,0:T(8,128)(2,1)S(1)}, bf16[64,2048]{1,0:T(8,128)(2,1)S(1)}, u32[]{:S(2)}, u32[]{:S(2)}) %collective-permute-start.28) | collective-permute-done | bytes 262176 | tf_op jit(solution)/shard_map/ppermute | solution.py:33
  255.2 45.3 %collective-permute-done.35 = bf16[64,2048]{1,0:T(8,128)(2,1)S(1)} collective-permute-done((bf16[64,2048]{1,0:T(8,128)(2,1)S(1)}, bf16[64,2048]{1,0:T(8,128)(2,1)S(1)}, u32[]{:S(2)}, u32[]{:S(2)}) %collective-permute-start.35) | collective-permute-done | bytes 262176 | tf_op jit(solution)/shard_map/ppermute | solution.py:33
  302.0 2.2 constant_dynamic-update-slice_fusion.33
  304.2 8.6 %fusion.56 = f32[1024,1408]{1,0:T(8,128)} fusion(bf16[1024,2048]{1,0:T(8,128)(2,1)S(1)} %constant_dynamic-update-slice_fusion.33, bf16[2048,1408]{1,0:T(8,128)(2,1)S(1)} %copy-done.116), kind=kOutput, calls=%fused_computation.219 | convolution fusion | flops 5905580032 | bytes 15728640 | tf_op jit(solution)/shard_map/dot_general | solution.py:20
  316.5 10.2 %multiply_convert_fusion.3 = (bf16[1024,704]{1,0:T(8,128)(2,1)S(1)}, bf16[1024,704]{1,0:T(8,128)(2,1)S(1)}, bf16[1024,704]{1,0:T(8,128)(2,1)}) fusion(f32[1024,1408]{1,0:T(8,128)} %fusion.56, bf16[1024,2048]{1,0:T(8,128)(2,1)} %constant_dynamic-update-slice_fusion.39, bf16[704,2048]{1,0:T(8,128)(2,1)} %all-gather.8.cloned.1.call-done), kind=kOutput, calls=%fused_computation.39 | convolution fusion | flops 2963603456 | bytes 17170432 | tf_op jit(solution)/shard_map/dot_general | solution.py:24
  326.7 9.3 %convolution_convert_fusion = bf16[1024,2048]{1,0:T(8,128)(2,1)S(1)} fusion(bf16[2048,1408]{1,0:T(8,128)(2,1)} %all-gather.6.cloned.1.call-done, bf16[1024,704]{1,0:T(8,128)(2,1)S(1)} %get-tuple-element.316, bf16[1024,704]{1,0:T(8,128)(2,1)S(1)} %get-tuple-element.315), kind=kOutput, calls=%fused_computation.32 | convolution fusion | flops 5913444352 | bytes 12845056 | tf_op jit(solution)/shard_map/dot_general | solution.py:24
  344.6 4.5 convolution_convert_fusion.5
  349.1 18.4 %collective-permute-done.39 = bf16[256,2048]{1,0:T(8,128)(2,1)} collective-permute-done((bf16[256,2048]{1,0:T(8,128)(2,1)}, bf16[256,2048]{1,0:T(8,128)(2,1)}, u32[]{:S(2)}, u32[]{:S(2)}) %collective-permute-start.39) | collective-permute-done | bytes 1048608 | tf_op jit(solution)/shard_map/ppermute | solution.py:33
  369.8 2.3 constant_dynamic-update-slice_fusion.46
  372.1 2.3 constant_dynamic-update-slice_fusion.45.refs_6_
  374.4 3.1 add_convert_fusion.2
  382.0 7.0 convolution_convert_fusion.4
  391.0 7.4 convolution_convert_fusion.3
  400.9 6.2 collective-permute-done.47
  409.6 5.6 collective-permute-done.48
  416.3 3.6 multiply_reduce_fusion
  420.5 3.6 multiply_convert_fusion
  424.1 3.6 convolution_convert_fusion.1
  433.1 5.0 pad_maximum_fusion.1.grad_ref
  438.1 8.8 %attend_back.4.refs_3_ = bf16[1024,768]{1,0:T(8,128)(2,1)S(1)} custom-call(bf16[1024,2048]{1,0:T(8,128)(2,1)} %pad_maximum_fusion.1.grad_ref, bf16[256,2048]{1,0:T(8,128)(2,1)S(1)} %copy-done.13, bf16[1024,768]{1,0:T(8,128)(2,1)S(1)} %copy-done.38, f32[1024,2]{1,0:T(8,128)S(1)} %copy-done.48, f32[512,128]{1,0:T(8,128)S(1)} %get-tuple-element.396.refs_8_.cos_ref, ...), custom_call_target="tpu_custom_call" | custom-call | flops 2415919104 | bytes 8388608 | tf_op jit(solution)/shard_map/attend_back/pallas_call | solution.py:355
  449.7 9.9 %attend_back.5.refs_1_ = bf16[1024,768]{1,0:T(8,128)(2,1)} custom-call(bf16[1024,2048]{1,0:T(8,128)(2,1)} %pad_maximum_fusion.1.grad_ref, bf16[256,2048]{1,0:T(8,128)(2,1)S(1)} %copy-done.9, bf16[1024,768]{1,0:T(8,128)(2,1)S(1)} %copy-done.36, f32[1024,2]{1,0:T(8,128)S(1)} %copy-done.46, f32[512,128]{1,0:T(8,128)S(1)} %get-tuple-element.396.refs_8_.cos_ref, ...), custom_call_target="tpu_custom_call" | custom-call | flops 2415919104 | bytes 8388608 | tf_op jit(solution)/shard_map/attend_back/pallas_call | solution.py:355
  460.6 9.9 %attend_back.6.refs_2_ = bf16[1024,768]{1,0:T(8,128)(2,1)} custom-call(bf16[1024,2048]{1,0:T(8,128)(2,1)} %pad_maximum_fusion.1.grad_ref, bf16[256,2048]{1,0:T(8,128)(2,1)S(1)} %copy-done.7, bf16[1024,768]{1,0:T(8,128)(2,1)S(1)} %copy-done.34, f32[1024,2]{1,0:T(8,128)S(1)} %copy-done.44, f32[512,128]{1,0:T(8,128)S(1)} %get-tuple-element.396.refs_8_.cos_ref, ...), custom_call_target="tpu_custom_call" | custom-call | flops 2415919104 | bytes 8388608 | tf_op jit(solution)/shard_map/attend_back/pallas_call | solution.py:355
  473.8 9.0 %attend_back.7.refs_0_.refs_8_.refs_9_ = bf16[1024,768]{1,0:T(8,128)(2,1)S(1)} custom-call(bf16[1024,2048]{1,0:T(8,128)(2,1)} %pad_maximum_fusion.1.grad_ref, bf16[256,2048]{1,0:T(8,128)(2,1)S(1)} %copy-done.12, bf16[1024,768]{1,0:T(8,128)(2,1)S(1)} %copy-done.32, f32[1024,2]{1,0:T(8,128)S(1)} %copy-done.42, ...), custom_call_target="tpu_custom_call" | custom-call | flops 2415919104 | bytes 8388608 | tf_op jit(solution)/shard_map/attend_back/pallas_call | solution.py:355
  484.0 20.1 %normed_back.1 = f32[1024,2048]{1,0:T(8,128)} custom-call(s32[1]{0:T(128)} %bitcast.1.z_ref, bf16[1024,768]{1,0:T(8,128)(2,1)} %copy-done.39, bf16[1024,768]{1,0:T(8,128)(2,1)} %attend_back.5.refs_1_, bf16[1024,768]{1,0:T(8,128)(2,1)} %attend_back.6.refs_2_, bf16[1024,768]{1,0:T(8,128)(2,1)} %copy-done.10, bf16[512,768]{1,0:T(8,128)(2,1)S(1)} %copy-done.16, ...), custom_call_target="tpu_custom_call" | custom-call | flops 12884901888 | bytes 27262976 | tf_op jit(solution)/shard_map/normed_back/pallas_call | solution.py:429
  504.1 6.2 convolution_convert_fusion.2
  510.3 13.4 %collective-permute-done.55.refs_14_ = bf16[512,768]{1,0:T(8,128)(2,1)} collective-permute-done((bf16[512,768]{1,0:T(8,128)(2,1)}, bf16[512,768]{1,0:T(8,128)(2,1)}, u32[]{:S(2)}, u32[]{:S(2)}) %collective-permute-start.55) | collective-permute-done | bytes 786464 | tf_op jit(solution)/shard_map/ppermute | solution.py:33
  523.8 3.8 slice.347
  533.1 19.1 %weight_grad.1 = bf16[2048,768]{1,0:T(8,128)(2,1)} custom-call(bf16[512,2048]{1,0:T(8,128)(2,1)S(1)} %copy-done.5, bf16[512,2048]{1,0:T(8,128)(2,1)} %collective-permute-done.8.refs_1_, bf16[512,2048]{1,0:T(8,128)(2,1)S(1)} %copy-done.51, bf16[512,2048]{1,0:T(8,128)(2,1)} %collective-permute-done.44.refs_3_, bf16[512,2048]{1,0:T(8,128)(2,1)} %copy-done.83, ...), custom_call_target="tpu_custom_call" | custom-call | flops 12884901888 | bytes 26214400 | tf_op jit(solution)/shard_map/weight_grad/pallas_call | solution.py:396
  553.5 4.2 collective-permute-done.58
  564.0 5.0 fusion.9
  569.1 5.0 fusion.6
  576.6 3.6 collective-permute-done.67
  586.4 24.1 %collective-permute-done.63 = bf16[128,2048]{1,0:T(8,128)(2,1)S(1)} collective-permute-done((bf16[128,2048]{1,0:T(8,128)(2,1)S(1)}, bf16[128,2048]{1,0:T(8,128)(2,1)S(1)}, u32[]{:S(2)}, u32[]{:S(2)}) %collective-permute-start.63) | collective-permute-done | bytes 524320 | tf_op jit(solution)/shard_map/ppermute | solution.py:33
  617.5 5.0 place_turned.2
  622.5 14.4 %collective-permute-done.72 = bf16[352,512]{1,0:T(8,128)(2,1)S(1)} collective-permute-done((bf16[352,512]{1,0:T(8,128)(2,1)S(1)}, bf16[352,512]{1,0:T(8,128)(2,1)S(1)}, u32[]{:S(2)}, u32[]{:S(2)}) %collective-permute-start.72) | collective-permute-done | bytes 360480 | tf_op jit(solution)/shard_map/ppermute | solution.py:33
  653.5 16.1 %collective-permute-done.80 = bf16[352,512]{1,0:T(8,128)(2,1)S(1)} collective-permute-done((bf16[352,512]{1,0:T(8,128)(2,1)S(1)}, bf16[352,512]{1,0:T(8,128)(2,1)S(1)}, u32[]{:S(2)}, u32[]{:S(2)}) %collective-permute-start.80) | collective-permute-done | bytes 360480 | tf_op jit(solution)/shard_map/ppermute | solution.py:33
  685.2 6.8 place_turned.3
  692.0 9.8 %reduce-scatter.14.cloned.1.call-done = bf16[256,512]{1,0:T(8,128)(2,1)} async-done(((bf16[256,2048]{1,0:T(8,128)(2,1)}), bf16[256,512]{1,0:T(8,128)(2,1)}) %reduce-scatter.14.cloned.1.call-update) | async-done | bytes 262160 | tf_op jit(solution)/shard_map/reduce_scatter | solution.py:710
  704.4 3.0 add_convert_fusion.1
  713.5 3.6 collective-permute-done.88
  719.6 10.5 %place.3 = f32[5632,512]{1,0:T(8,128)} custom-call(s32[1]{0:T(128)} %bitcast.6.me_ref, bf16[2816,512]{1,0:T(8,128)(2,1)} %constant_dynamic-update-slice_fusion.57.same_ref, bf16[2816,512]{1,0:T(8,128)(2,1)} %collective-permute-done.83.other_ref), custom_call_target="tpu_custom_call" | custom-call | bytes 23068672 | tf_op jit(solution)/shard_map/place/pallas_call | solution.py:484
  739.0 11.0 %place.4 = (f32[512,2048]{1,0:T(8,128)}, f32[512,2048]{1,0:T(8,128)}, f32[512,2048]{1,0:T(8,128)}) custom-call(s32[1]{0:T(128)} %bitcast.6.me_ref, bf16[2048,768]{1,0:T(8,128)(2,1)} %constant_dynamic-update-slice_fusion.62.same_ref, bf16[2048,768]{1,0:T(8,128)(2,1)} %collective-permute-done.85.other_ref), custom_call_target="tpu_custom_call" | custom-call | bytes 25165824 | tf_op jit(solution)/shard_map/place/pallas_call | solution.py:484
  756.3 4.2 collective-permute-done.98
  761.3 4.5 collective-permute-done.99
  770.5 6.5 place.5
  778.1 4.4 add_convert_fusion
  (582 shorter events, 223.8 us)
Async XLA Ops:
  7.2 123.9 %all-gather.4.cloned.1.call-start = ((), (), s32[]{:S(2)}) async-start(), calls=%async_computation.5 | async-start | bytes 1310720 | tf_op jit(solution)/shard_map/all_gather | solution.py:600
  46.0 22.1 %collective-permute-start.8 = (bf16[512,2048]{1,0:T(8,128)(2,1)S(1)}, bf16[512,2048]{1,0:T(8,128)(2,1)}, u32[]{:S(2)}, u32[]{:S(2)}) collective-permute-start(bf16[512,2048]{1,0:T(8,128)(2,1)S(1)} %fusion.2.refs_0_), channel_id=1, source_target_pairs={{0,4},{4,0},{8,12},{12,8},{16,20},{20,16},{24,28},{28,24},{1,5},{5... | collective-permute-start | bytes 6291464 | tf_op jit(solution)/shard_map/ppermute | solution.py:33
  68.1 29.3 %collective-permute-start.13 = (bf16[512,768]{1,0:T(8,128)(2,1)}, bf16[512,768]{1,0:T(8,128)(2,1)}, u32[]{:S(2)}, u32[]{:S(2)}) collective-permute-start(bf16[512,768]{1,0:T(8,128)(2,1)} %collective-permute-done.7.refs_6_), channel_id=1, source_target_pairs={{0,1},{1,2},{2,3},{3,0},{4,5},{5,6},{6,7},{7,4},{8,9},{9,10},{10,1... | collective-permute-start | bytes 2359304 | tf_op jit(solution)/shard_map/ppermute | solution.py:596
  68.2 29.2 %collective-permute-start.12 = (bf16[512,768]{1,0:T(8,128)(2,1)}, bf16[512,768]{1,0:T(8,128)(2,1)S(1)}, u32[]{:S(2)}, u32[]{:S(2)}) collective-permute-start(bf16[512,768]{1,0:T(8,128)(2,1)} %collective-permute-done.7.refs_6_), channel_id=1, source_target_pairs={{0,16},{4,20},{8,24},{12,28},{16,0},{20,4},{24,8},{28,12},{1,17},{... | collective-permute-start | bytes 2359304 | tf_op jit(solution)/shard_map/ppermute | solution.py:33
  69.8 27.7 %collective-permute-start.11 = (bf16[512,768]{1,0:T(8,128)(2,1)}, bf16[512,768]{1,0:T(8,128)(2,1)}, u32[]{:S(2)}, u32[]{:S(2)}) collective-permute-start(bf16[512,768]{1,0:T(8,128)(2,1)} %collective-permute-done.7.refs_6_), channel_id=1, source_target_pairs={{0,8},{4,12},{8,0},{12,4},{16,24},{20,28},{24,16},{28,20},{1,9},{5... | collective-permute-start | bytes 2359304 | tf_op jit(solution)/shard_map/ppermute | solution.py:33
  72.8 24.6 %collective-permute-start.10 = (bf16[256,768]{1,0:T(8,128)(2,1)}, bf16[256,768]{1,0:T(8,128)(2,1)}, u32[]{:S(2)}, u32[]{:S(2)}) collective-permute-start(bf16[256,768]{1,0:T(8,128)(2,1)} %slice.225), channel_id=1, source_target_pairs={{0,8},{4,12},{8,0},{12,4},{16,24},{20,28},{24,16},{28,20},{1,9},{5... | collective-permute-start | bytes 1179656 | tf_op jit(solution)/shard_map/ppermute | solution.py:33
  73.4 24.0 %collective-permute-start.9 = (bf16[256,768]{1,0:T(8,128)(2,1)}, bf16[256,768]{1,0:T(8,128)(2,1)}, u32[]{:S(2)}, u32[]{:S(2)}) collective-permute-start(bf16[256,768]{1,0:T(8,128)(2,1)} %slice.224), channel_id=1, source_target_pairs={{0,16},{4,20},{8,24},{12,28},{16,0},{20,4},{24,8},{28,12},{1,17},{... | collective-permute-start | bytes 1179656 | tf_op jit(solution)/shard_map/ppermute | solution.py:33
  97.4 142.0 %all-gather.6.cloned.1.call-start = ((), (), s32[]{:S(2)}) async-start(), calls=%async_computation.6 | async-start | bytes 7208960 | tf_op jit(solution)/shard_map/all_gather | solution.py:609
  104.1 27.0 %collective-permute-start.17 = (bf16[512,768]{1,0:T(8,128)(2,1)}, bf16[512,768]{1,0:T(8,128)(2,1)}, u32[]{:S(2)}, u32[]{:S(2)}) collective-permute-start(bf16[512,768]{1,0:T(8,128)(2,1)} %collective-permute-done.13.refs_7_), channel_id=1, source_target_pairs={{0,16},{4,20},{8,24},{12,28},{16,0},{20,4},{24,8},{28,12},{1,17},{... | collective-permute-start | bytes 2359304 | tf_op jit(solution)/shard_map/ppermute | solution.py:33
  104.7 26.4 %collective-permute-start.16 = (bf16[512,768]{1,0:T(8,128)(2,1)}, bf16[512,768]{1,0:T(8,128)(2,1)}, u32[]{:S(2)}, u32[]{:S(2)}) collective-permute-start(bf16[512,768]{1,0:T(8,128)(2,1)} %collective-permute-done.13.refs_7_), channel_id=1, source_target_pairs={{0,8},{4,12},{8,0},{12,4},{16,24},{20,28},{24,16},{28,20},{1,9},{5... | collective-permute-start | bytes 2359304 | tf_op jit(solution)/shard_map/ppermute | solution.py:33
  108.2 22.9 %collective-permute-start.15 = (bf16[256,768]{1,0:T(8,128)(2,1)S(1)}, bf16[256,768]{1,0:T(8,128)(2,1)S(1)}, u32[]{:S(2)}, u32[]{:S(2)}) collective-permute-start(bf16[256,768]{1,0:T(8,128)(2,1)S(1)} %slice.227), channel_id=1, source_target_pairs={{0,8},{4,12},{8,0},{12,4},{16,24},{20,28},{24,16},{28,20},{1,9},{5... | collective-permute-start | bytes 1179656 | tf_op jit(solution)/shard_map/ppermute | solution.py:33
  108.8 22.2 %collective-permute-start.14 = (bf16[256,768]{1,0:T(8,128)(2,1)S(1)}, bf16[256,768]{1,0:T(8,128)(2,1)}, u32[]{:S(2)}, u32[]{:S(2)}) collective-permute-start(bf16[256,768]{1,0:T(8,128)(2,1)S(1)} %slice.226), channel_id=1, source_target_pairs={{0,16},{4,20},{8,24},{12,28},{16,0},{20,4},{24,8},{28,12},{1,17},{... | collective-permute-start | bytes 1179656 | tf_op jit(solution)/shard_map/ppermute | solution.py:33
  131.2 185.3 %all-gather.8.cloned.1.call-start = ((), (), s32[]{:S(2)}) async-start(), calls=%async_computation.7 | async-start | bytes 3604480 | tf_op jit(solution)/shard_map/all_gather | solution.py:611
  133.6 45.4 %collective-permute-start.21 = (bf16[256,2048]{1,0:T(8,128)(2,1)}, bf16[256,2048]{1,0:T(8,128)(2,1)S(1)}, u32[]{:S(2)}, u32[]{:S(2)}) collective-permute-start(bf16[256,2048]{1,0:T(8,128)(2,1)} %all-gather.4.cloned.1.call-done.out_ref), channel_id=1, source_target_pairs={{0,16},{4,20},{8,24},{12,28},{16,0},{20,4},{24,8},{28,12},{1,17},{... | collective-permute-start | bytes 3145736 | tf_op jit(solution)/shard_map/ppermute | solution.py:33
  135.1 43.9 %collective-permute-start.20 = (bf16[256,2048]{1,0:T(8,128)(2,1)}, bf16[256,2048]{1,0:T(8,128)(2,1)S(1)}, u32[]{:S(2)}, u32[]{:S(2)}) collective-permute-start(bf16[256,2048]{1,0:T(8,128)(2,1)} %all-gather.4.cloned.1.call-done.out_ref), channel_id=1, source_target_pairs={{0,8},{4,12},{8,0},{12,4},{16,24},{20,28},{24,16},{28,20},{1,9},{5... | collective-permute-start | bytes 3145736 | tf_op jit(solution)/shard_map/ppermute | solution.py:33
  138.7 29.4 %collective-permute-start.19 = (bf16[256,768]{1,0:T(8,128)(2,1)S(1)}, bf16[256,768]{1,0:T(8,128)(2,1)S(1)}, u32[]{:S(2)}, u32[]{:S(2)}) collective-permute-start(bf16[256,768]{1,0:T(8,128)(2,1)S(1)} %slice.229), channel_id=1, source_target_pairs={{0,8},{4,12},{8,0},{12,4},{16,24},{20,28},{24,16},{28,20},{1,9},{5... | collective-permute-start | bytes 1179656 | tf_op jit(solution)/shard_map/ppermute | solution.py:33
  139.2 28.8 %collective-permute-start.18 = (bf16[256,768]{1,0:T(8,128)(2,1)S(1)}, bf16[256,768]{1,0:T(8,128)(2,1)S(1)}, u32[]{:S(2)}, u32[]{:S(2)}) collective-permute-start(bf16[256,768]{1,0:T(8,128)(2,1)S(1)} %slice.228), channel_id=1, source_target_pairs={{0,16},{4,20},{8,24},{12,28},{16,0},{20,4},{24,8},{28,12},{1,17},{... | collective-permute-start | bytes 1179656 | tf_op jit(solution)/shard_map/ppermute | solution.py:33
  242.1 58.4 %collective-permute-start.33 = (bf16[512,2048]{1,0:T(8,128)(2,1)}, bf16[512,2048]{1,0:T(8,128)(2,1)}, u32[]{:S(2)}, u32[]{:S(2)}) collective-permute-start(bf16[512,2048]{1,0:T(8,128)(2,1)} %get-tuple-element.365), channel_id=1, source_target_pairs={{0,4},{4,0},{8,12},{12,8},{16,20},{20,16},{24,28},{28,24},{1,5},{5... | collective-permute-start | bytes 6291464 | tf_op jit(solution)/shard_map/ppermute | solution.py:33
  244.2 266.2 %reduce-scatter.6.cloned.1.call-start = ((), (), s32[]{:S(2)}) async-start(), calls=%async_computation.8 | async-start | bytes 3604480 | tf_op jit(solution)/shard_map/reduce_scatter | solution.py:661
  246.2 66.6 %collective-permute-start.32 = (bf16[512,2048]{1,0:T(8,128)(2,1)S(1)}, bf16[512,2048]{1,0:T(8,128)(2,1)S(1)}, u32[]{:S(2)}, u32[]{:S(2)}) collective-permute-start(bf16[512,2048]{1,0:T(8,128)(2,1)S(1)} %copy-done.5), channel_id=1, source_target_pairs={{0,16},{4,20},{8,24},{12,28},{16,0},{20,4},{24,8},{28,12},{1,17},{... | collective-permute-start | bytes 6291464 | tf_op jit(solution)/shard_map/ppermute | solution.py:33
  247.1 65.8 %collective-permute-start.31 = (bf16[512,2048]{1,0:T(8,128)(2,1)S(1)}, bf16[512,2048]{1,0:T(8,128)(2,1)S(1)}, u32[]{:S(2)}, u32[]{:S(2)}) collective-permute-start(bf16[512,2048]{1,0:T(8,128)(2,1)S(1)} %copy-done.5), channel_id=1, source_target_pairs={{0,8},{4,12},{8,0},{12,4},{16,24},{20,28},{24,16},{28,20},{1,9},{5... | collective-permute-start | bytes 6291464 | tf_op jit(solution)/shard_map/ppermute | solution.py:33
  250.6 49.9 %collective-permute-start.35 = (bf16[64,2048]{1,0:T(8,128)(2,1)S(1)}, bf16[64,2048]{1,0:T(8,128)(2,1)S(1)}, u32[]{:S(2)}, u32[]{:S(2)}) collective-permute-start(bf16[64,2048]{1,0:T(8,128)(2,1)S(1)} %slice.237), channel_id=1, source_target_pairs={{0,8},{4,12},{8,0},{12,4},{16,24},{20,28},{24,16},{28,20},{1,9},{5... | collective-permute-start | bytes 786440 | tf_op jit(solution)/shard_map/ppermute | solution.py:33
  251.2 49.3 %collective-permute-start.34 = (bf16[64,2048]{1,0:T(8,128)(2,1)S(1)}, bf16[64,2048]{1,0:T(8,128)(2,1)S(1)}, u32[]{:S(2)}, u32[]{:S(2)}) collective-permute-start(bf16[64,2048]{1,0:T(8,128)(2,1)S(1)} %slice.236), channel_id=1, source_target_pairs={{0,16},{4,20},{8,24},{12,28},{16,0},{20,4},{24,8},{28,12},{1,17},{... | collective-permute-start | bytes 786440 | tf_op jit(solution)/shard_map/ppermute | solution.py:33
  337.5 31.2 %collective-permute-start.37 = (bf16[512,2048]{1,0:T(8,128)(2,1)}, bf16[512,2048]{1,0:T(8,128)(2,1)}, u32[]{:S(2)}, u32[]{:S(2)}) collective-permute-start(bf16[512,2048]{1,0:T(8,128)(2,1)} %slice.290), channel_id=1, source_target_pairs={{0,4},{4,0},{8,12},{12,8},{16,20},{20,16},{24,28},{28,24},{1,5},{5... | collective-permute-start | bytes 6291464 | tf_op jit(solution)/shard_map/ppermute | solution.py:33
  341.9 25.5 %collective-permute-start.39 = (bf16[256,2048]{1,0:T(8,128)(2,1)}, bf16[256,2048]{1,0:T(8,128)(2,1)}, u32[]{:S(2)}, u32[]{:S(2)}) collective-permute-start(bf16[256,2048]{1,0:T(8,128)(2,1)} %slice.244), channel_id=1, source_target_pairs={{0,8},{4,12},{8,0},{12,4},{16,24},{20,28},{24,16},{28,20},{1,9},{5... | collective-permute-start | bytes 3145736 | tf_op jit(solution)/shard_map/ppermute | solution.py:33
  343.5 25.3 %collective-permute-start.38 = (bf16[256,2048]{1,0:T(8,128)(2,1)}, bf16[256,2048]{1,0:T(8,128)(2,1)}, u32[]{:S(2)}, u32[]{:S(2)}) collective-permute-start(bf16[256,2048]{1,0:T(8,128)(2,1)} %slice.243), channel_id=1, source_target_pairs={{0,16},{4,20},{8,24},{12,28},{16,0},{20,4},{24,8},{28,12},{1,17},{... | collective-permute-start | bytes 3145736 | tf_op jit(solution)/shard_map/ppermute | solution.py:33
  368.7 183.5 %reduce-scatter.10.cloned.1.call-start = ((), (), s32[]{:S(2)}) async-start(), calls=%async_computation.10 | async-start | bytes 3604480 | tf_op jit(solution)/shard_map/reduce_scatter | solution.py:661
  369.2 29.3 %collective-permute-start.44 = (bf16[512,2048]{1,0:T(8,128)(2,1)}, bf16[512,2048]{1,0:T(8,128)(2,1)}, u32[]{:S(2)}, u32[]{:S(2)}) collective-permute-start(bf16[512,2048]{1,0:T(8,128)(2,1)} %copy-done.49), channel_id=1, source_target_pairs={{0,4},{4,0},{8,12},{12,8},{16,20},{20,16},{24,28},{28,24},{1,5},{5... | collective-permute-start | bytes 6291464 | tf_op jit(solution)/shard_map/ppermute | solution.py:33
  369.3 29.2 %collective-permute-start.45 = (bf16[512,2048]{1,0:T(8,128)(2,1)}, bf16[512,2048]{1,0:T(8,128)(2,1)}, u32[]{:S(2)}, u32[]{:S(2)}) collective-permute-start(bf16[512,2048]{1,0:T(8,128)(2,1)} %copy-done.83), channel_id=1, source_target_pairs={{0,4},{4,0},{8,12},{12,8},{16,20},{20,16},{24,28},{28,24},{1,5},{5... | collective-permute-start | bytes 6291464 | tf_op jit(solution)/shard_map/ppermute | solution.py:33
  374.4 24.1 %collective-permute-start.46 = (bf16[512,2048]{1,0:T(8,128)(2,1)}, bf16[512,2048]{1,0:T(8,128)(2,1)}, u32[]{:S(2)}, u32[]{:S(2)}) collective-permute-start(bf16[512,2048]{1,0:T(8,128)(2,1)} %constant_dynamic-update-slice_fusion.45.refs_6_), channel_id=1, source_target_pairs={{0,4},{4,0},{8,12},{12,8},{16,20},{20,16},{24,28},{28,24},{1,5},{5... | collective-permute-start | bytes 6291464 | tf_op jit(solution)/shard_map/ppermute | solution.py:33
  391.0 169.1 %reduce-scatter.8.cloned.1.call-start = ((), (), s32[]{:S(2)}) async-start(), calls=%async_computation.9 | async-start | bytes 3604480 | tf_op jit(solution)/shard_map/reduce_scatter | solution.py:661
  431.3 40.5 %collective-permute-start.52 = (bf16[512,2048]{1,0:T(8,128)(2,1)}, bf16[512,2048]{1,0:T(8,128)(2,1)}, u32[]{:S(2)}, u32[]{:S(2)}) collective-permute-start(bf16[512,2048]{1,0:T(8,128)(2,1)} %slice.299), channel_id=1, source_target_pairs={{0,4},{4,0},{8,12},{12,8},{16,20},{20,16},{24,28},{28,24},{1,5},{5... | collective-permute-start | bytes 6291464 | tf_op jit(solution)/shard_map/ppermute | solution.py:33
  432.9 204.9 %reduce-scatter.12.cloned.1.call-start = ((), (), s32[]{:S(2)}) async-start(), calls=%async_computation.11 | async-start | bytes 3932160 | tf_op jit(solution)/shard_map/reduce_scatter | solution.py:693
  447.1 24.7 %collective-permute-start.51 = (bf16[512,768]{1,0:T(8,128)(2,1)S(1)}, bf16[512,768]{1,0:T(8,128)(2,1)}, u32[]{:S(2)}, u32[]{:S(2)}) collective-permute-start(bf16[512,768]{1,0:T(8,128)(2,1)S(1)} %get-tuple-element.350), channel_id=1, source_target_pairs={{0,16},{4,20},{8,24},{12,28},{16,0},{20,4},{24,8},{28,12},{1,17},{... | collective-permute-start | bytes 2359304 | tf_op jit(solution)/shard_map/ppermute | solution.py:33
  448.6 23.2 %collective-permute-start.50 = (bf16[512,768]{1,0:T(8,128)(2,1)S(1)}, bf16[512,768]{1,0:T(8,128)(2,1)}, u32[]{:S(2)}, u32[]{:S(2)}) collective-permute-start(bf16[512,768]{1,0:T(8,128)(2,1)S(1)} %get-tuple-element.351), channel_id=1, source_target_pairs={{0,8},{4,12},{8,0},{12,4},{16,24},{20,28},{24,16},{28,20},{1,9},{5... | collective-permute-start | bytes 2359304 | tf_op jit(solution)/shard_map/ppermute | solution.py:33
  459.6 64.2 %collective-permute-start.53 = (bf16[1024,768]{1,0:T(8,128)(2,1)}, bf16[1024,768]{1,0:T(8,128)(2,1)}, u32[]{:S(2)}, u32[]{:S(2)}) collective-permute-start(bf16[1024,768]{1,0:T(8,128)(2,1)} %attend_back.5.refs_1_), channel_id=1, source_target_pairs={{0,8},{4,12},{8,0},{12,4},{16,24},{20,28},{24,16},{28,20},{1,9},{5... | collective-permute-start | bytes 4718600 | tf_op jit(solution)/shard_map/ppermute | solution.py:33
  470.6 53.2 %collective-permute-start.54 = (bf16[1024,768]{1,0:T(8,128)(2,1)}, bf16[1024,768]{1,0:T(8,128)(2,1)}, u32[]{:S(2)}, u32[]{:S(2)}) collective-permute-start(bf16[1024,768]{1,0:T(8,128)(2,1)} %attend_back.6.refs_2_), channel_id=1, source_target_pairs={{0,16},{4,20},{8,24},{12,28},{16,0},{20,4},{24,8},{28,12},{1,17},{... | collective-permute-start | bytes 4718600 | tf_op jit(solution)/shard_map/ppermute | solution.py:33
  471.8 51.9 %collective-permute-start.55 = (bf16[512,768]{1,0:T(8,128)(2,1)}, bf16[512,768]{1,0:T(8,128)(2,1)}, u32[]{:S(2)}, u32[]{:S(2)}) collective-permute-start(bf16[512,768]{1,0:T(8,128)(2,1)} %collective-permute-done.50), channel_id=1, source_target_pairs={{0,16},{4,20},{8,24},{12,28},{16,0},{20,4},{24,8},{28,12},{1,17},{... | collective-permute-start | bytes 2359304 | tf_op jit(solution)/shard_map/ppermute | solution.py:33
  472.7 51.1 %collective-permute-start.56 = (bf16[512,768]{1,0:T(8,128)(2,1)}, bf16[512,768]{1,0:T(8,128)(2,1)}, u32[]{:S(2)}, u32[]{:S(2)}) collective-permute-start(bf16[512,768]{1,0:T(8,128)(2,1)} %collective-permute-done.51), channel_id=1, source_target_pairs={{0,8},{4,12},{8,0},{12,4},{16,24},{20,28},{24,16},{28,20},{1,9},{5... | collective-permute-start | bytes 2359304 | tf_op jit(solution)/shard_map/ppermute | solution.py:33
  527.6 32.5 %collective-permute-start.61 = (bf16[512,2048]{1,0:T(8,128)(2,1)}, bf16[512,2048]{1,0:T(8,128)(2,1)}, u32[]{:S(2)}, u32[]{:S(2)}) collective-permute-start(bf16[512,2048]{1,0:T(8,128)(2,1)} %slice.347), channel_id=1, source_target_pairs={{0,4},{4,0},{8,12},{12,8},{16,20},{20,16},{24,28},{28,24},{1,5},{5... | collective-permute-start | bytes 6291464 | tf_op jit(solution)/shard_map/ppermute | solution.py:33
  527.6 32.4 %collective-permute-start.60 = (bf16[704,512]{1,0:T(8,128)(2,1)}, bf16[704,512]{1,0:T(8,128)(2,1)}, u32[]{:S(2)}, u32[]{:S(2)}) collective-permute-start(bf16[704,512]{1,0:T(8,128)(2,1)} %reduce-scatter.6.cloned.1.call-done), channel_id=1, source_target_pairs={{0,16},{4,20},{8,24},{12,28},{16,0},{20,4},{24,8},{28,12},{1,17},{... | collective-permute-start | bytes 2162696 | tf_op jit(solution)/shard_map/ppermute | solution.py:33
  529.0 31.1 %collective-permute-start.59 = (bf16[704,512]{1,0:T(8,128)(2,1)}, bf16[704,512]{1,0:T(8,128)(2,1)}, u32[]{:S(2)}, u32[]{:S(2)}) collective-permute-start(bf16[704,512]{1,0:T(8,128)(2,1)} %reduce-scatter.6.cloned.1.call-done), channel_id=1, source_target_pairs={{0,8},{4,12},{8,0},{12,4},{16,24},{20,28},{24,16},{28,20},{1,9},{5... | collective-permute-start | bytes 2162696 | tf_op jit(solution)/shard_map/ppermute | solution.py:33
  531.3 26.4 %collective-permute-start.58 = (bf16[128,2048]{1,0:T(8,128)(2,1)}, bf16[128,2048]{1,0:T(8,128)(2,1)}, u32[]{:S(2)}, u32[]{:S(2)}) collective-permute-start(bf16[128,2048]{1,0:T(8,128)(2,1)} %get-tuple-element.322), channel_id=1, source_target_pairs={{0,16},{4,20},{8,24},{12,28},{16,0},{20,4},{24,8},{28,12},{1,17},{... | collective-permute-start | bytes 1572872 | tf_op jit(solution)/shard_map/ppermute | solution.py:33
  531.9 27.1 %collective-permute-start.57 = (bf16[128,2048]{1,0:T(8,128)(2,1)}, bf16[128,2048]{1,0:T(8,128)(2,1)}, u32[]{:S(2)}, u32[]{:S(2)}) collective-permute-start(bf16[128,2048]{1,0:T(8,128)(2,1)} %get-tuple-element.323), channel_id=1, source_target_pairs={{0,8},{4,12},{8,0},{12,4},{16,24},{20,28},{24,16},{28,20},{1,9},{5... | collective-permute-start | bytes 1572872 | tf_op jit(solution)/shard_map/ppermute | solution.py:33
  552.3 149.5 %reduce-scatter.14.cloned.1.call-start = ((), (), s32[]{:S(2)}) async-start(), calls=%async_computation.12 | async-start | bytes 1310720 | tf_op jit(solution)/shard_map/reduce_scatter | solution.py:710
  580.3 30.3 %collective-permute-start.68 = (bf16[2816,512]{1,0:T(8,128)(2,1)S(1)}, bf16[2816,512]{1,0:T(8,128)(2,1)S(1)}, u32[]{:S(2)}, u32[]{:S(2)}) collective-permute-start(bf16[2816,512]{1,0:T(8,128)(2,1)S(1)} %constant_dynamic-update-slice_fusion.47.same_ref), channel_id=1, source_target_pairs={{0,4},{4,0},{8,12},{12,8},{16,20},{20,16},{24,28},{28,24},{1,5},{5... | collective-permute-start | bytes 8650760 | tf_op jit(solution)/shard_map/ppermute | solution.py:33
  580.3 30.2 %collective-permute-start.70 = (bf16[704,512]{1,0:T(8,128)(2,1)S(1)}, bf16[704,512]{1,0:T(8,128)(2,1)S(1)}, u32[]{:S(2)}, u32[]{:S(2)}) collective-permute-start(bf16[704,512]{1,0:T(8,128)(2,1)S(1)} %copy-done.82), channel_id=1, source_target_pairs={{0,16},{4,20},{8,24},{12,28},{16,0},{20,4},{24,8},{28,12},{1,17},{... | collective-permute-start | bytes 2162696 | tf_op jit(solution)/shard_map/ppermute | solution.py:33
  581.1 29.5 %collective-permute-start.69 = (bf16[704,512]{1,0:T(8,128)(2,1)S(1)}, bf16[704,512]{1,0:T(8,128)(2,1)S(1)}, u32[]{:S(2)}, u32[]{:S(2)}) collective-permute-start(bf16[704,512]{1,0:T(8,128)(2,1)S(1)} %copy-done.82), channel_id=1, source_target_pairs={{0,8},{4,12},{8,0},{12,4},{16,24},{20,28},{24,16},{28,20},{1,9},{5... | collective-permute-start | bytes 2162696 | tf_op jit(solution)/shard_map/ppermute | solution.py:33
  583.9 26.7 %collective-permute-start.63 = (bf16[128,2048]{1,0:T(8,128)(2,1)S(1)}, bf16[128,2048]{1,0:T(8,128)(2,1)S(1)}, u32[]{:S(2)}, u32[]{:S(2)}) collective-permute-start(bf16[128,2048]{1,0:T(8,128)(2,1)S(1)} %get-tuple-element.324), channel_id=1, source_target_pairs={{0,8},{4,12},{8,0},{12,4},{16,24},{20,28},{24,16},{28,20},{1,9},{5... | collective-permute-start | bytes 1572872 | tf_op jit(solution)/shard_map/ppermute | solution.py:33
  585.1 25.4 %collective-permute-start.62 = (bf16[128,2048]{1,0:T(8,128)(2,1)S(1)}, bf16[128,2048]{1,0:T(8,128)(2,1)S(1)}, u32[]{:S(2)}, u32[]{:S(2)}) collective-permute-start(bf16[128,2048]{1,0:T(8,128)(2,1)S(1)} %get-tuple-element.325), channel_id=1, source_target_pairs={{0,16},{4,20},{8,24},{12,28},{16,0},{20,4},{24,8},{28,12},{1,17},{... | collective-permute-start | bytes 1572872 | tf_op jit(solution)/shard_map/ppermute | solution.py:33
  610.6 26.3 %collective-permute-start.74 = (bf16[704,512]{1,0:T(8,128)(2,1)S(1)}, bf16[704,512]{1,0:T(8,128)(2,1)}, u32[]{:S(2)}, u32[]{:S(2)}) collective-permute-start(bf16[704,512]{1,0:T(8,128)(2,1)S(1)} %copy-done.81), channel_id=1, source_target_pairs={{0,16},{4,20},{8,24},{12,28},{16,0},{20,4},{24,8},{28,12},{1,17},{... | collective-permute-start | bytes 2162696 | tf_op jit(solution)/shard_map/ppermute | solution.py:33
  612.0 25.8 %collective-permute-start.73 = (bf16[704,512]{1,0:T(8,128)(2,1)S(1)}, bf16[704,512]{1,0:T(8,128)(2,1)}, u32[]{:S(2)}, u32[]{:S(2)}) collective-permute-start(bf16[704,512]{1,0:T(8,128)(2,1)S(1)} %copy-done.81), channel_id=1, source_target_pairs={{0,8},{4,12},{8,0},{12,4},{16,24},{20,28},{24,16},{28,20},{1,9},{5... | collective-permute-start | bytes 2162696 | tf_op jit(solution)/shard_map/ppermute | solution.py:33
  613.0 23.9 %collective-permute-start.72 = (bf16[352,512]{1,0:T(8,128)(2,1)S(1)}, bf16[352,512]{1,0:T(8,128)(2,1)S(1)}, u32[]{:S(2)}, u32[]{:S(2)}) collective-permute-start(bf16[352,512]{1,0:T(8,128)(2,1)S(1)} %slice.268), channel_id=1, source_target_pairs={{0,8},{4,12},{8,0},{12,4},{16,24},{20,28},{24,16},{28,20},{1,9},{5... | collective-permute-start | bytes 1081352 | tf_op jit(solution)/shard_map/ppermute | solution.py:33
  614.1 22.8 %collective-permute-start.71 = (bf16[352,512]{1,0:T(8,128)(2,1)S(1)}, bf16[352,512]{1,0:T(8,128)(2,1)S(1)}, u32[]{:S(2)}, u32[]{:S(2)}) collective-permute-start(bf16[352,512]{1,0:T(8,128)(2,1)S(1)} %slice.267), channel_id=1, source_target_pairs={{0,16},{4,20},{8,24},{12,28},{16,0},{20,4},{24,8},{28,12},{1,17},{... | collective-permute-start | bytes 1081352 | tf_op jit(solution)/shard_map/ppermute | solution.py:33
  641.2 28.3 %collective-permute-start.78 = (bf16[2816,512]{1,0:T(8,128)(2,1)}, bf16[2816,512]{1,0:T(8,128)(2,1)S(1)}, u32[]{:S(2)}, u32[]{:S(2)}) collective-permute-start(bf16[2816,512]{1,0:T(8,128)(2,1)} %constant_dynamic-update-slice_fusion.52.same_ref), channel_id=1, source_target_pairs={{0,4},{4,0},{8,12},{12,8},{16,20},{20,16},{24,28},{28,24},{1,5},{5... | collective-permute-start | bytes 8650760 | tf_op jit(solution)/shard_map/ppermute | solution.py:33
  641.2 28.3 %collective-permute-start.77 = (bf16[512,768]{1,0:T(8,128)(2,1)}, bf16[512,768]{1,0:T(8,128)(2,1)S(1)}, u32[]{:S(2)}, u32[]{:S(2)}) collective-permute-start(bf16[512,768]{1,0:T(8,128)(2,1)} %reduce-scatter.12.cloned.1.call-done), channel_id=1, source_target_pairs={{0,16},{4,20},{8,24},{12,28},{16,0},{20,4},{24,8},{28,12},{1,17},{... | collective-permute-start | bytes 2359304 | tf_op jit(solution)/shard_map/ppermute | solution.py:33
  641.9 27.6 %collective-permute-start.76 = (bf16[512,768]{1,0:T(8,128)(2,1)}, bf16[512,768]{1,0:T(8,128)(2,1)S(1)}, u32[]{:S(2)}, u32[]{:S(2)}) collective-permute-start(bf16[512,768]{1,0:T(8,128)(2,1)} %reduce-scatter.12.cloned.1.call-done), channel_id=1, source_target_pairs={{0,8},{4,12},{8,0},{12,4},{16,24},{20,28},{24,16},{28,20},{1,9},{5... | collective-permute-start | bytes 2359304 | tf_op jit(solution)/shard_map/ppermute | solution.py:33
  644.8 24.8 %collective-permute-start.80 = (bf16[352,512]{1,0:T(8,128)(2,1)S(1)}, bf16[352,512]{1,0:T(8,128)(2,1)S(1)}, u32[]{:S(2)}, u32[]{:S(2)}) collective-permute-start(bf16[352,512]{1,0:T(8,128)(2,1)S(1)} %slice.270), channel_id=1, source_target_pairs={{0,8},{4,12},{8,0},{12,4},{16,24},{20,28},{24,16},{28,20},{1,9},{5... | collective-permute-start | bytes 1081352 | tf_op jit(solution)/shard_map/ppermute | solution.py:33
  646.1 23.5 %collective-permute-start.79 = (bf16[352,512]{1,0:T(8,128)(2,1)S(1)}, bf16[352,512]{1,0:T(8,128)(2,1)S(1)}, u32[]{:S(2)}, u32[]{:S(2)}) collective-permute-start(bf16[352,512]{1,0:T(8,128)(2,1)S(1)} %slice.269), channel_id=1, source_target_pairs={{0,16},{4,20},{8,24},{12,28},{16,0},{20,4},{24,8},{28,12},{1,17},{... | collective-permute-start | bytes 1081352 | tf_op jit(solution)/shard_map/ppermute | solution.py:33
  671.2 30.6 %collective-permute-start.83 = (bf16[2816,512]{1,0:T(8,128)(2,1)}, bf16[2816,512]{1,0:T(8,128)(2,1)}, u32[]{:S(2)}, u32[]{:S(2)}) collective-permute-start(bf16[2816,512]{1,0:T(8,128)(2,1)} %constant_dynamic-update-slice_fusion.57.same_ref), channel_id=1, source_target_pairs={{0,4},{4,0},{8,12},{12,8},{16,20},{20,16},{24,28},{28,24},{1,5},{5... | collective-permute-start | bytes 8650760 | tf_op jit(solution)/shard_map/ppermute | solution.py:33
  678.6 23.2 %collective-permute-start.82 = (bf16[256,768]{1,0:T(8,128)(2,1)}, bf16[256,768]{1,0:T(8,128)(2,1)S(1)}, u32[]{:S(2)}, u32[]{:S(2)}) collective-permute-start(bf16[256,768]{1,0:T(8,128)(2,1)} %slice.272), channel_id=1, source_target_pairs={{0,8},{4,12},{8,0},{12,4},{16,24},{20,28},{24,16},{28,20},{1,9},{5... | collective-permute-start | bytes 1179656 | tf_op jit(solution)/shard_map/ppermute | solution.py:33
  704.4 25.7 %collective-permute-start.85 = (bf16[2048,768]{1,0:T(8,128)(2,1)}, bf16[2048,768]{1,0:T(8,128)(2,1)}, u32[]{:S(2)}, u32[]{:S(2)}) collective-permute-start(bf16[2048,768]{1,0:T(8,128)(2,1)} %constant_dynamic-update-slice_fusion.62.same_ref), channel_id=1, source_target_pairs={{0,4},{4,0},{8,12},{12,8},{16,20},{20,16},{24,28},{28,24},{1,5},{5... | collective-permute-start | bytes 9437192 | tf_op jit(solution)/shard_map/ppermute | solution.py:33
  707.4 22.7 %collective-permute-start.87 = (bf16[256,512]{1,0:T(8,128)(2,1)}, bf16[256,512]{1,0:T(8,128)(2,1)S(1)}, u32[]{:S(2)}, u32[]{:S(2)}) collective-permute-start(bf16[256,512]{1,0:T(8,128)(2,1)} %reduce-scatter.14.cloned.1.call-done), channel_id=1, source_target_pairs={{0,16},{4,20},{8,24},{12,28},{16,0},{20,4},{24,8},{28,12},{1,17},{... | collective-permute-start | bytes 786440 | tf_op jit(solution)/shard_map/ppermute | solution.py:33
  712.0 25.0 %collective-permute-start.92 = (bf16[64,2048]{1,0:T(8,128)(2,1)}, bf16[64,2048]{1,0:T(8,128)(2,1)}, u32[]{:S(2)}, u32[]{:S(2)}) collective-permute-start(bf16[64,2048]{1,0:T(8,128)(2,1)} %get-tuple-element.330), channel_id=1, source_target_pairs={{0,16},{4,20},{8,24},{12,28},{16,0},{20,4},{24,8},{28,12},{1,17},{... | collective-permute-start | bytes 786440 | tf_op jit(solution)/shard_map/ppermute | solution.py:33
  (166 other events, 1687.4 us)
Sparse Core Ops, SparseCore 0:
  97.6 28.0 all-gather.3
  131.3 107.4 all-gather.5
  244.3 58.9 all-gather.7
  368.9 55.1 reduce-scatter.5
  426.8 56.0 reduce-scatter.9
  485.6 56.0 reduce-scatter.7
  552.4 60.4 reduce-scatter.11
  674.3 27.4 reduce-scatter.13

commit v5 on v3

--- a/solution.py
+++ b/solution.py
@@ -427,8 +427,7 @@
 
 
 def place_kernel(me_ref, same_ref, other_ref, *out_refs):
-    odd = jnp.bitwise_xor(pl.program_id(0), me_ref[0]) % 2
-    block = jnp.where(odd == 0, same_ref[...], other_ref[...]).astype(F32)
+    block = jnp.where(pl.program_id(0) % 2 == 0, same_ref[...], other_ref[...]).astype(F32)
     width = out_refs[0].shape[1]
     for i, ref in enumerate(out_refs):
         ref[...] = block[:, i * width : (i + 1) * width]
@@ -436,7 +435,8 @@
 
 def place(me, same, other, height, width, columns):
     size, total = lax.axis_size("rep"), same.shape[1]
-    spec = pl.BlockSpec((height, total), lambda j, me: (jnp.bitwise_xor(j, me[0]) // 2, 0))
+    spec = pl.BlockSpec((height, total), lambda d, me: (d // 2, 0))
+    at = lambda d, me: jnp.bitwise_xor(d, me[0])
     shape = (height, size * width) if columns else (size * height, width)
     count = total // width
     return pl.pallas_call(
@@ -447,7 +447,8 @@
             in_specs=[spec, spec],
             out_specs=[
                 pl.BlockSpec(
-                    (height, width), (lambda j, me: (0, j)) if columns else (lambda j, me: (j, 0))
+                    (height, width),
+                    (lambda d, me: (0, at(d, me))) if columns else (lambda d, me: (at(d, me), 0)),
                 )
             ] * count,
         ),
@@ -486,6 +487,24 @@
         ),
         name="place_turned",
     )(me, same, other)
+
+
+def turn_kernel(in_ref, out_ref):
+    out_ref[...] = in_ref[...].T.astype(F32)
+
+
+def turn(value):
+    rows, width = value.shape
+    tile = 512 if rows % 512 == 0 else rows
+    return pl.pallas_call(
+        turn_kernel,
+        grid=(rows // tile,),
+        in_specs=[pl.BlockSpec((tile, width), lambda i: (i, 0))],
+        out_specs=pl.BlockSpec((width, tile), lambda i: (0, i)),
+        out_shape=jax.ShapeDtypeStruct((width, rows), F32),
+        cost_estimate=pl.CostEstimate(flops=0, bytes_accessed=6 * value.size, transcendentals=0),
+        name="turn",
+    )(value)
 
 
 def per_device(
@@ -646,42 +665,45 @@
     grad_normed = normed_back(
         shard, [lins[d] for d in offsets], [qkv_w[d] for d in offsets], both.shape[1]
     )
-    sums[0], sums[1], grad_normed, grad_out_w = stage(
-        [qkv_flow], (sums[0], sums[1], grad_normed, grad_out_w)
+    own_lin, sums[1] = lax.optimization_barrier((lins[0], (sums[1], sums[2])))
+    sums[1], sums[2] = sums[1]
+    lins[0] = own_lin
+    sums[0], grad_normed, grad_out_w = stage([qkv_flow], (sums[0], grad_normed, grad_out_w))
+    all_up = lax.all_gather(sums[1], "rep", axis=0, tiled=True)
+    own_grad_qkv, all_up = lax.optimization_barrier((finish(qkv_flow), all_up))
+    sum_qkv = lax.psum_scatter(own_grad_qkv, "shard", scatter_dimension=0, tiled=True)
+
+    out_blocks = {d: halves(grad_out_w[i * block : (i + 1) * block]) for i, d in enumerate(offsets)}
+    out_flow, gate_flow = Flow(scatter_steps(out_blocks)), Flow(copies_steps(sums[0]))
+    expert_flow = Flow(plane_sum_steps(mm(inner, down).astype(BF)))
+    other_normed = stage(
+        [out_flow, gate_flow, expert_flow], swap(grad_normed[length:].astype(BF), 1)
     )
-    own_grad_qkv, sums[2] = lax.optimization_barrier((finish(qkv_flow), sums[2]))
-    sum_qkv = lax.psum_scatter(own_grad_qkv, "shard", scatter_dimension=0, tiled=True)
-    grad_normed = grad_normed[:length] + swap(grad_normed[length:].astype(BF), 1).astype(F32)
+    grad_normed = grad_normed[:length] + other_normed.astype(F32)
     grad_gain_one, first = norm_back(grad_normed, inputs, root_one, gain_one)
     grad_input = (grad_hidden + first).astype(BF)
-
-    out_blocks = {d: halves(grad_out_w[i * block : (i + 1) * block]) for i, d in enumerate(offsets)}
-    expert_out = mm(inner, down).astype(BF)
-    gate_flow, expert_flow = Flow(copies_steps(sums[0])), Flow(plane_sum_steps(expert_out))
-    up_flow = Flow(copies_steps(sums[1]))
-    grad_input, gains, out_blocks = stage(
-        [gate_flow, up_flow, expert_flow],
-        (grad_input, jnp.stack([grad_gain_one, grad_gain_two]), out_blocks),
+    grad_input, gains = stage(
+        [out_flow, gate_flow, expert_flow], (grad_input, jnp.stack([grad_gain_one, grad_gain_two]))
     )
-    gain_flow, out_flow = Flow(vector_sum_steps(gains)), Flow(scatter_steps(out_blocks))
-    stage([gate_flow, up_flow, gain_flow])
-    stage([gate_flow, up_flow, out_flow, gain_flow])
-    stage([out_flow, expert_flow, gain_flow])
-    sums[2] = stage([out_flow, expert_flow], sums[2])
+    gain_flow = Flow(vector_sum_steps(gains))
+    stage([out_flow, gate_flow, gain_flow])
     grad_gate = place_turned(whoami, *finish(gate_flow), units)
-    grad_up = place_turned(whoami, *finish(up_flow), units)
     own_grad_out, sum_qkv = lax.optimization_barrier((finish(out_flow), sum_qkv))
     sum_out = lax.psum_scatter(own_grad_out, "shard", scatter_dimension=1, tiled=True)
-    down_flow, qkv_flow = Flow(copies_steps(sums[2])), Flow(copies_steps(sum_qkv))
-    grad_gate, grad_up = stage([down_flow, qkv_flow], (grad_gate, grad_up))
-    stage([qkv_flow, down_flow])
-    stage([qkv_flow, down_flow, expert_flow])
-    (grad_down,) = place(whoami, *finish(down_flow), units, own, False)
+    grad_gate, all_up = stage([expert_flow, gain_flow], (grad_gate, all_up))
+    grad_up = turn(all_up)
+    qkv_flow = Flow(copies_steps(sum_qkv))
+    grad_up, sum_out = stage([qkv_flow, expert_flow], (grad_up, sum_out))
+    down_sum, sum_out = lax.optimization_barrier((sums[2], sum_out))
+    all_down = lax.all_gather(down_sum, "rep", axis=0, tiled=True)
+    stage([qkv_flow, gain_flow])
     out_flow = Flow(copies_steps(sum_out))
-    grad_down = stage([out_flow, gain_flow], grad_down)
+    output = (hidden + mm_tn(pick, finish(expert_flow)) * mix[:, None]).astype(BF)
+    output = stage([qkv_flow, out_flow, gain_flow], output)
     grad_query, grad_key, grad_value = place(whoami, *finish(qkv_flow), own, block, True)
-    output = (hidden + mm_tn(pick, finish(expert_flow)) * mix[:, None]).astype(BF)
+    grad_query = stage([out_flow], grad_query)
     (grad_out,) = place(whoami, *finish(out_flow), block, own, False)
+    grad_down = all_down.astype(F32)
     gain_grads = finish(gain_flow)
     return (
         output,

time: 768 us -> 771 us (level)
  other arithmetic: 56.2 us -> 74.2 us
    reduce_scatter x1, waiting for transfers between devices: 23.1 us -> 0.02 us  [per_device(): lax.psum_scatter(own_grad_out, 'shard', scatter_dimension=1, tiled=True)]
    reduce_scatter x1, waiting for transfers between devices: 0.01 us -> 16.2 us  [per_device(): lax.psum_scatter(own_grad_qkv, 'shard', scatter_dimension=0, tiled=True)]
    pallas_call x3 -> x2, Pallas kernels: 27.9 us -> 17.5 us  [place(): pl.pallas_call(place_kernel, grid_spec=pltpu.PrefetchScalarGridSpec(num_s...]
    pallas_call x0 -> x1, Pallas kernels: none -> 10.4 us  [turn(): pl.pallas_call(turn_kernel, grid=(rows // tile,), in_specs=[pl.BlockSpec(...]
    convert_element_type x0 -> x1, other arithmetic: none -> 8.87 us  [per_device(): grad_down = all_down.astype(F32)]
    ppermute x85 -> x75, starting transfers between devices: 76.2 us -> 67.6 us  [swap(): return lax.ppermute(value, 'rep', [(i, i ^ bit) for i in range(size)])]
    ppermute x85 -> x75, waiting for transfers between devices: 182 us -> 189 us  [swap(): return lax.ppermute(value, 'rep', [(i, i ^ bit) for i in range(size)])]
  transfers between devices with their start and end apart: 102 -> 94, of which waited for: 39 -> 41; matrix products, arithmetic and copies ran while one was open for 23% -> 23% of each run, Pallas kernels for 21% -> 22%
where the time goes in v5:
time: 771 us; the launch traced here: 762 us
  waiting for transfers between devices  251 us (33%)
  Pallas kernels  165 us (21%)
  local copies, waits for them, and re-layouts  99.4 us (13%)
  starting transfers between devices  83.7 us (11%)
  other arithmetic  74.2 us (10%)
  matrix products  73.3 us (10%)
  between operations  15.8 us (2%)
    ppermute x75, waiting for transfers between devices, swap(): return lax.ppermute(value, 'rep', [(i, i ^ bit) for i in range(size)])  189 us
    pallas_call x4, Pallas kernels, attend_back(): pl.pallas_call(attend_back_kernel, grid=(rows // length,), in_specs=[by_s...  68.9 us
    ppermute x75, starting transfers between devices, swap(): return lax.ppermute(value, 'rep', [(i, i ^ bit) for i in range(size)])  67.6 us
    unnamed x242, local copies, waits for them, and re-layouts  52.7 us
    pallas_call x4, Pallas kernels, attend(): pl.pallas_call(functools.partial(attend_kernel, parts), grid_spec=pltpu.P...  43.2 us
    dot_general x6, matrix products, mm_tn(): lax.dot_general(left, right, (((0,), (0,)), ((), ())), preferred_element_...  33.7 us
    all_gather x1, waiting for transfers between devices, per_device(): down = lax.all_gather(own_down, 'shard', axis=1, tiled=True)  22.2 us
    dot_general x5, matrix products, mm(): return jnp.dot(left, right, preferred_element_type=F32)  20.3 us
  transfers between devices with their start and end apart: 94, of which 41 were waited for; matrix products, arithmetic and copies ran while one was open for 23% of the time, Pallas kernels for 22%

profile of v5, /device:TPU:0, one launch (start us, length us, event | category | flops | bytes accessed | tf_op | source)
XLA Modules:
  0.0 762.2 jit_solution(15277515134157894416)
XLA Ops:
  8.8 5.1 collective-permute-start
  16.8 2.7 constant_dynamic-slice_fusion.5
  19.6 2.5 collective-permute-start.3
  27.1 12.9 %collective-permute-done.3.refs_5_ = bf16[512,768]{1,0:T(8,128)(2,1)} collective-permute-done((bf16[512,768]{1,0:T(8,128)(2,1)S(1)}, bf16[512,768]{1,0:T(8,128)(2,1)}, u32[]{:S(2)}, u32[]{:S(2)}) %collective-permute-start.3) | collective-permute-done | bytes 786464 | tf_op jit(solution)/shard_map/ppermute | solution.py:559
  46.1 16.4 %collective-permute-done.5.refs_5_.refs_9_ = bf16[512,768]{1,0:T(8,128)(2,1)S(1)} collective-permute-done((bf16[512,768]{1,0:T(8,128)(2,1)}, bf16[512,768]{1,0:T(8,128)(2,1)S(1)}, u32[]{:S(2)}, u32[]{:S(2)}) %collective-permute-start.5) | collective-permute-done | bytes 786464 | tf_op jit(solution)/shard_map/ppermute | solution.py:33
  63.7 3.1 collective-permute-done.7.refs_6_
  74.2 20.1 %collective-permute-done.9 = bf16[256,768]{1,0:T(8,128)(2,1)} collective-permute-done((bf16[256,768]{1,0:T(8,128)(2,1)}, bf16[256,768]{1,0:T(8,128)(2,1)}, u32[]{:S(2)}, u32[]{:S(2)}) %collective-permute-start.9) | collective-permute-done | bytes 393248 | tf_op jit(solution)/shard_map/ppermute | solution.py:33
  106.2 2.8 pad_maximum_fusion.refs_0_.refs_1_.refs_2_.refs_3_.x_ref
  109.1 12.2 %attend.4 = (bf16[1024,256]{1,0:T(8,128)(2,1)S(1)}, bf16[1024,768]{1,0:T(8,128)(2,1)S(1)}, f32[1024,2]{1,0:T(8,128)S(1)}) custom-call(s32[1]{0:T(128)} %bitcast.1.z_ref, bf16[1024,2048]{1,0:T(8,128)(2,1)S(1)} %pad_maximum_fusion.refs_0_.refs_1_.refs_2_.refs_3_.x_ref, bf16[1024,2048]{1,0:T(8,128)(2,1)S(1)} %pad_maximum_fusion.refs_0_.refs_1_.refs_2_.refs_3_.x_ref, ...), custom_call_target="tpu_custom_call" | custom-call | flops 3758096384 | bytes 10485760 | tf_op jit(solution)/shard_map/attend/pallas_call | solution.py:251
  123.2 3.6 collective-permute-done.14
  139.7 10.7 %attend.5 = (bf16[1024,256]{1,0:T(8,128)(2,1)S(1)}, bf16[1024,768]{1,0:T(8,128)(2,1)S(1)}, f32[1024,2]{1,0:T(8,128)S(1)}) custom-call(s32[1]{0:T(128)} %bitcast.1.z_ref, bf16[1024,2048]{1,0:T(8,128)(2,1)S(1)} %copy-done.3, bf16[1024,2048]{1,0:T(8,128)(2,1)S(1)} %copy-done.3, bf16[1024,2048]{1,0:T(8,128)(2,1)S(1)} %copy-done.3, ...), custom_call_target="tpu_custom_call" | custom-call | flops 3758096384 | bytes 10485760 | tf_op jit(solution)/shard_map/attend/pallas_call | solution.py:251
  153.2 10.7 %attend.6 = (bf16[1024,256]{1,0:T(8,128)(2,1)S(1)}, bf16[1024,768]{1,0:T(8,128)(2,1)S(1)}, f32[1024,2]{1,0:T(8,128)S(1)}) custom-call(s32[1]{0:T(128)} %bitcast.1.z_ref, bf16[1024,2048]{1,0:T(8,128)(2,1)S(1)} %copy-done.3, bf16[1024,2048]{1,0:T(8,128)(2,1)S(1)} %copy-done.3, bf16[1024,2048]{1,0:T(8,128)(2,1)S(1)} %copy-done.3, ...), custom_call_target="tpu_custom_call" | custom-call | flops 3758096384 | bytes 10485760 | tf_op jit(solution)/shard_map/attend/pallas_call | solution.py:251
  166.4 9.6 %attend.7 = (bf16[1024,256]{1,0:T(8,128)(2,1)S(1)}, bf16[1024,768]{1,0:T(8,128)(2,1)S(1)}, f32[1024,2]{1,0:T(8,128)S(1)}) custom-call(s32[1]{0:T(128)} %bitcast.1.z_ref, bf16[1024,2048]{1,0:T(8,128)(2,1)S(1)} %copy-done.3, bf16[1024,2048]{1,0:T(8,128)(2,1)S(1)} %copy-done.3, bf16[1024,2048]{1,0:T(8,128)(2,1)S(1)} %copy-done.3, ...), custom_call_target="tpu_custom_call" | custom-call | flops 3758096384 | bytes 10485760 | tf_op jit(solution)/shard_map/attend/pallas_call | solution.py:251
  179.0 6.9 collective-permute-done.22
  188.4 6.1 fusion.54
  195.4 3.6 collective-permute-done.24
  205.4 10.8 %collective-permute-done.25 = bf16[128,2048]{1,0:T(8,128)(2,1)S(1)} collective-permute-done((bf16[128,2048]{1,0:T(8,128)(2,1)S(1)}, bf16[128,2048]{1,0:T(8,128)(2,1)S(1)}, u32[]{:S(2)}, u32[]{:S(2)}) %collective-permute-start.25) | collective-permute-done | bytes 524320 | tf_op jit(solution)/shard_map/ppermute | solution.py:33
  219.5 4.5 collective-permute-done.27
  225.0 5.8 all-gather.8.cloned.1.call-done
  241.6 9.6 %collective-permute-done.30 = bf16[128,2048]{1,0:T(8,128)(2,1)S(1)} collective-permute-done((bf16[128,2048]{1,0:T(8,128)(2,1)}, bf16[128,2048]{1,0:T(8,128)(2,1)S(1)}, u32[]{:S(2)}, u32[]{:S(2)}) %collective-permute-start.30) | collective-permute-done | bytes 524320 | tf_op jit(solution)/shard_map/ppermute | solution.py:33
  254.5 3.2 constant_dynamic-update-slice_fusion.39
  262.1 8.4 %fusion.55 = f32[1024,1408]{0,1:T(8,128)} fusion(bf16[1024,2048]{1,0:T(8,128)(2,1)S(1)} %copy-done.85, bf16[2048,1408]{1,0:T(8,128)(2,1)S(1)} %copy-done.98), kind=kOutput, calls=%fused_computation.211 | convolution fusion | flops 5905580032 | bytes 15728640 | tf_op jit(solution)/shard_map/dot_general | solution.py:20
  272.0 22.2 %all-gather.10.cloned.1.call-done = bf16[704,2048]{1,0:T(8,128)(2,1)} async-done(((bf16[704,512]{1,0:T(8,128)(2,1)}), bf16[704,2048]{1,0:T(8,128)(2,1)}) %all-gather.10.cloned.1.call-update) | async-done | bytes 2883600 | tf_op jit(solution)/shard_map/all_gather | solution.py:588
  294.2 10.0 %multiply_convert_fusion.4 = (bf16[1024,704]{0,1:T(8,128)(2,1)S(1)}, bf16[1024,704]{0,1:T(8,128)(2,1)S(1)}, bf16[1024,704]{0,1:T(8,128)(2,1)}) fusion(f32[1024,1408]{0,1:T(8,128)} %fusion.55, bf16[1024,2048]{1,0:T(8,128)(2,1)} %constant_dynamic-update-slice_fusion.33, bf16[704,2048]{1,0:T(8,128)(2,1)} %all-gather.10.cloned.1.call-done), kind=kOutput, calls=%fused_computation.48 | convolution fusion | flops 2963603456 | bytes 17170432 | tf_op jit(solution)/shard_map/dot_general | solution.py:24
  304.3 9.3 %convolution_convert_fusion.1 = bf16[1024,2048]{1,0:T(8,128)(2,1)S(1)} fusion(bf16[2048,1408]{1,0:T(8,128)(2,1)} %all-gather.8.cloned.1.call-done, bf16[1024,704]{0,1:T(8,128)(2,1)S(1)} %get-tuple-element.316, bf16[1024,704]{0,1:T(8,128)(2,1)S(1)} %get-tuple-element.315), kind=kOutput, calls=%fused_computation.33 | convolution fusion | flops 5913444352 | bytes 12845056 | tf_op jit(solution)/shard_map/dot_general | solution.py:24
  318.5 4.6 convolution_convert_fusion.5
  323.2 3.2 add_convert_fusion.2
  331.7 4.4 convolution_convert_fusion.3
  340.5 7.9 %convolution_convert_fusion.4 = bf16[704,2048]{1,0:T(8,128)(2,1)} fusion(bf16[1024,704]{0,1:T(8,128)(2,1)} %get-tuple-element.317, bf16[1024,2048]{1,0:T(8,128)(2,1)} %constant_dynamic-update-slice_fusion.33), kind=kOutput, calls=%fused_computation.36 | convolution fusion | flops 2954231808 | bytes 8519680 | tf_op jit(solution)/shard_map/dot_general | solution.py:28
  349.7 6.3 collective-permute-done.40
  358.7 5.1 collective-permute-done.41
  364.9 3.6 multiply_reduce_fusion
  369.1 3.6 multiply_convert_fusion
  374.1 3.1 collective-permute-done.42
  377.2 4.8 pad_maximum_fusion.1.grad_ref
  382.1 17.3 %attend_back.4 = (bf16[1024,768]{1,0:T(8,128)(2,1)S(1)}, bf16[1024,768]{1,0:T(8,128)(2,1)S(1)}, bf16[1024,768]{1,0:T(8,128)(2,1)}) custom-call(bf16[1024,2048]{1,0:T(8,128)(2,1)} %pad_maximum_fusion.1.grad_ref, bf16[256,2048]{1,0:T(8,128)(2,1)S(1)} %pad_maximum_fusion.4.out_ref, bf16[1024,768]{1,0:T(8,128)(2,1)} %copy-done.28, f32[1024,2]{1,0:T(8,128)S(1)} %copy-done.34, ...), custom_call_target="tpu_custom_call" | custom-call | flops 5637144576 | bytes 15728640 | tf_op jit(solution)/shard_map/attend_back/pallas_call | solution.py:340
  402.0 17.1 %attend_back.6 = (bf16[1024,768]{1,0:T(8,128)(2,1)S(1)}, bf16[1024,768]{1,0:T(8,128)(2,1)S(1)}, bf16[1024,768]{1,0:T(8,128)(2,1)}) custom-call(bf16[1024,2048]{1,0:T(8,128)(2,1)} %pad_maximum_fusion.1.grad_ref, bf16[256,2048]{1,0:T(8,128)(2,1)S(1)} %copy-done.11, bf16[1024,768]{1,0:T(8,128)(2,1)} %copy-done.27, f32[1024,2]{1,0:T(8,128)S(1)} %copy-done.32, ...), custom_call_target="tpu_custom_call" | custom-call | flops 5637144576 | bytes 15728640 | tf_op jit(solution)/shard_map/attend_back/pallas_call | solution.py:340
  421.1 17.0 %attend_back.5 = (bf16[1024,768]{1,0:T(8,128)(2,1)S(1)}, bf16[1024,768]{1,0:T(8,128)(2,1)S(1)}, bf16[1024,768]{1,0:T(8,128)(2,1)}) custom-call(bf16[1024,2048]{1,0:T(8,128)(2,1)} %pad_maximum_fusion.1.grad_ref, bf16[256,2048]{1,0:T(8,128)(2,1)S(1)} %copy-done.9, bf16[1024,768]{1,0:T(8,128)(2,1)} %copy-done.26, f32[1024,2]{1,0:T(8,128)S(1)} %get-tuple-element.214.lse_ref, ...), custom_call_target="tpu_custom_call" | custom-call | flops 5637144576 | bytes 15728640 | tf_op jit(solution)/shard_map/attend_back/pallas_call | solution.py:340
  443.5 17.5 %attend_back.7 = (bf16[1024,768]{1,0:T(8,128)(2,1)S(1)}, bf16[1024,768]{1,0:T(8,128)(2,1)S(1)}, bf16[1024,768]{1,0:T(8,128)(2,1)}) custom-call(bf16[1024,2048]{1,0:T(8,128)(2,1)} %pad_maximum_fusion.1.grad_ref, bf16[256,2048]{1,0:T(8,128)(2,1)S(1)} %copy-done.24, bf16[1024,768]{1,0:T(8,128)(2,1)} %copy-done.25, f32[1024,2]{1,0:T(8,128)S(1)} %copy-done.30, ...), custom_call_target="tpu_custom_call" | custom-call | flops 5637144576 | bytes 15728640 | tf_op jit(solution)/shard_map/attend_back/pallas_call | solution.py:340
  461.0 8.8 %convolution_convert_fusion.2 = bf16[1024,2048]{1,0:T(8,128)(2,1)} fusion(bf16[1024,1024]{1,0:T(8,128)(2,1)} %constant_dynamic-update-slice_fusion.14, bf16[1024,2048]{1,0:T(8,128)(2,1)S(1)} %copy-done.53), kind=kOutput, calls=%fused_computation.34 | convolution fusion | flops 4297064448 | bytes 10485760 | tf_op jit(solution)/shard_map/dot_general | solution.py:28
  471.9 4.9 collective-permute-done.48
  478.0 3.4 add_convert_fusion.6
  483.0 3.5 add_convert_fusion.5
  487.5 3.9 convolution_convert_fusion
  494.9 19.8 %normed_back.1 = f32[1024,2048]{1,0:T(8,128)} custom-call(s32[1]{0:T(128)} %bitcast.1.z_ref, bf16[1024,768]{1,0:T(8,128)(2,1)} %copy-done.38, bf16[1024,768]{1,0:T(8,128)(2,1)} %copy-done.36, bf16[1024,768]{1,0:T(8,128)(2,1)} %copy-done.37, bf16[1024,768]{1,0:T(8,128)(2,1)} %copy-done.35, bf16[512,768]{1,0:T(8,128)(2,1)S(1)} %pad_maximum_fusion.6.refs_4_, ...), custom_call_target="tpu_custom_call" | custom-call | flops 12884901888 | bytes 27262976 | tf_op jit(solution)/shard_map/normed_back/pallas_call | solution.py:387
  517.0 4.7 collective-permute-done.46
  521.7 3.8 slice.317
  537.1 34.1 %collective-permute-done.51 = bf16[128,2048]{1,0:T(8,128)(2,1)S(1)} collective-permute-done((bf16[128,2048]{1,0:T(8,128)(2,1)}, bf16[128,2048]{1,0:T(8,128)(2,1)S(1)}, u32[]{:S(2)}, u32[]{:S(2)}) %collective-permute-start.51) | collective-permute-done | bytes 524320 | tf_op jit(solution)/shard_map/ppermute | solution.py:33
  579.2 4.4 add_convert_fusion.1
  586.6 4.9 fusion.9
  591.5 4.9 fusion.6
  599.7 4.4 collective-permute-done.60
  611.7 10.4 %collective-permute-done.61 = bf16[128,2048]{1,0:T(8,128)(2,1)S(1)} collective-permute-done((bf16[128,2048]{1,0:T(8,128)(2,1)S(1)}, bf16[128,2048]{1,0:T(8,128)(2,1)S(1)}, u32[]{:S(2)}, u32[]{:S(2)}) %collective-permute-start.61) | collective-permute-done | bytes 524320 | tf_op jit(solution)/shard_map/ppermute | solution.py:33
  627.5 16.2 %reduce-scatter.12.cloned.1.call-done = bf16[512,768]{1,0:T(8,128)(2,1)} async-done(((bf16[2048,768]{1,0:T(8,128)(2,1)}), bf16[512,768]{1,0:T(8,128)(2,1)}) %reduce-scatter.12.cloned.1.call-update) | async-done | bytes 786448 | tf_op jit(solution)/shard_map/reduce_scatter | solution.py:674
  651.3 17.5 %collective-permute-done.69 = bf16[64,2048]{1,0:T(8,128)(2,1)S(1)} collective-permute-done((bf16[64,2048]{1,0:T(8,128)(2,1)}, bf16[64,2048]{1,0:T(8,128)(2,1)S(1)}, u32[]{:S(2)}, u32[]{:S(2)}) %collective-permute-start.69) | collective-permute-done | bytes 262176 | tf_op jit(solution)/shard_map/ppermute | solution.py:33
  674.1 5.0 place_turned.1
  679.1 10.4 %turn.1 = f32[512,5632]{1,0:T(8,128)} custom-call(bf16[5632,512]{1,0:T(8,128)(2,1)} %all-gather.12.cloned.1.call-done.in_ref), custom_call_target="tpu_custom_call" | custom-call | bytes 17301504 | tf_op jit(solution)/shard_map/turn/pallas_call | solution.py:499
  700.7 5.4 collective-permute-done.73
  712.4 4.3 add_convert_fusion
  717.6 2.5 collective-permute-start.79
  720.1 2.8 collective-permute-start.80
  725.0 11.0 %place.2 = (f32[512,2048]{1,0:T(8,128)}, f32[512,2048]{1,0:T(8,128)}, f32[512,2048]{1,0:T(8,128)}) custom-call(s32[1]{0:T(128)} %bitcast.6.me_ref, bf16[2048,768]{1,0:T(8,128)(2,1)} %constant_dynamic-update-slice_fusion.50.same_ref, bf16[2048,768]{1,0:T(8,128)(2,1)} %collective-permute-done.75.other_ref), custom_call_target="tpu_custom_call" | custom-call | bytes 25165824 | tf_op jit(solution)/shard_map/place/pallas_call | solution.py:442
  739.8 6.4 place.3
  746.3 8.9 %convert_element_type.342 = f32[5632,512]{1,0:T(8,128)} convert(bf16[5632,512]{1,0:T(8,128)(2,1)} %all-gather.14.cloned.1.call-done) | non-fusion elementwise | flops 2883584 | bytes 17301504 | tf_op jit(solution)/shard_map/convert_element_type | solution.py:706
  (502 shorter events, 211.6 us)
Async XLA Ops:
  7.2 120.4 %all-gather.6.cloned.1.call-start = ((), (), s32[]{:S(2)}) async-start(), calls=%async_computation.5 | async-start | bytes 1310720 | tf_op jit(solution)/shard_map/all_gather | solution.py:577
  8.8 18.3 %collective-permute-start = (bf16[2,512]{1,0:T(2,128)(2,1)S(1)}, bf16[2,512]{1,0:T(2,128)(2,1)S(1)}, u32[]{:S(2)}, u32[]{:S(2)}) collective-permute-start(bf16[2,512]{1,0:T(2,128)(2,1)S(1)} %get-tuple-element.314), channel_id=1, source_target_pairs={{0,3},{1,0},{2,1},{3,2},{4,7},{5,4},{6,5},{7,6},{8,11},{9,8},{10,9... | collective-permute-start | bytes 6152 | tf_op jit(solution)/shard_map/ppermute | solution.py:172
  13.9 13.2 %collective-permute-start.1 = (bf16[2,512]{1,0:T(2,128)(2,1)S(1)}, bf16[2,512]{1,0:T(2,128)(2,1)S(1)}, u32[]{:S(2)}, u32[]{:S(2)}) collective-permute-start(bf16[2,512]{1,0:T(2,128)(2,1)S(1)} %get-tuple-element.314), channel_id=1, source_target_pairs={{0,2},{1,3},{2,0},{3,1},{4,6},{5,7},{6,4},{7,5},{8,10},{9,11},{10,... | collective-permute-start | bytes 6152 | tf_op jit(solution)/shard_map/ppermute | solution.py:172
  13.9 13.2 %collective-permute-start.2 = (bf16[2,512]{1,0:T(2,128)(2,1)S(1)}, bf16[2,512]{1,0:T(2,128)(2,1)S(1)}, u32[]{:S(2)}, u32[]{:S(2)}) collective-permute-start(bf16[2,512]{1,0:T(2,128)(2,1)S(1)} %get-tuple-element.314), channel_id=1, source_target_pairs={{0,1},{1,2},{2,3},{3,0},{4,5},{5,6},{6,7},{7,4},{8,9},{9,10},{10,1... | collective-permute-start | bytes 6152 | tf_op jit(solution)/shard_map/ppermute | solution.py:172
  19.6 20.4 %collective-permute-start.3 = (bf16[512,768]{1,0:T(8,128)(2,1)S(1)}, bf16[512,768]{1,0:T(8,128)(2,1)}, u32[]{:S(2)}, u32[]{:S(2)}) collective-permute-start(bf16[512,768]{1,0:T(8,128)(2,1)S(1)} %pad_maximum_fusion.6.refs_4_), channel_id=1, source_target_pairs={{0,1},{1,2},{2,3},{3,0},{4,5},{5,6},{6,7},{7,4},{8,9},{9,10},{10,1... | collective-permute-start | bytes 2359304 | tf_op jit(solution)/shard_map/ppermute | solution.py:559
  42.3 24.6 %collective-permute-start.8 = (bf16[512,2048]{1,0:T(8,128)(2,1)S(1)}, bf16[512,2048]{1,0:T(8,128)(2,1)S(1)}, u32[]{:S(2)}, u32[]{:S(2)}) collective-permute-start(bf16[512,2048]{1,0:T(8,128)(2,1)S(1)} %fusion.2), channel_id=1, source_target_pairs={{0,4},{4,0},{8,12},{12,8},{16,20},{20,16},{24,28},{28,24},{1,5},{5... | collective-permute-start | bytes 6291464 | tf_op jit(solution)/shard_map/ppermute | solution.py:33
  42.4 20.2 %collective-permute-start.5 = (bf16[512,768]{1,0:T(8,128)(2,1)}, bf16[512,768]{1,0:T(8,128)(2,1)S(1)}, u32[]{:S(2)}, u32[]{:S(2)}) collective-permute-start(bf16[512,768]{1,0:T(8,128)(2,1)} %collective-permute-done.3.refs_5_), channel_id=1, source_target_pairs={{0,8},{4,12},{8,0},{12,4},{16,24},{20,28},{24,16},{28,20},{1,9},{5... | collective-permute-start | bytes 2359304 | tf_op jit(solution)/shard_map/ppermute | solution.py:33
  43.9 19.8 %collective-permute-start.6 = (bf16[512,768]{1,0:T(8,128)(2,1)}, bf16[512,768]{1,0:T(8,128)(2,1)S(1)}, u32[]{:S(2)}, u32[]{:S(2)}) collective-permute-start(bf16[512,768]{1,0:T(8,128)(2,1)} %collective-permute-done.3.refs_5_), channel_id=1, source_target_pairs={{0,16},{4,20},{8,24},{12,28},{16,0},{20,4},{24,8},{28,12},{1,17},{... | collective-permute-start | bytes 2359304 | tf_op jit(solution)/shard_map/ppermute | solution.py:33
  45.4 21.4 %collective-permute-start.7 = (bf16[512,768]{1,0:T(8,128)(2,1)}, bf16[512,768]{1,0:T(8,128)(2,1)}, u32[]{:S(2)}, u32[]{:S(2)}) collective-permute-start(bf16[512,768]{1,0:T(8,128)(2,1)} %collective-permute-done.3.refs_5_), channel_id=1, source_target_pairs={{0,1},{1,2},{2,3},{3,0},{4,5},{5,6},{6,7},{7,4},{8,9},{9,10},{10,1... | collective-permute-start | bytes 2359304 | tf_op jit(solution)/shard_map/ppermute | solution.py:573
  66.9 27.5 %collective-permute-start.11 = (bf16[512,768]{1,0:T(8,128)(2,1)}, bf16[512,768]{1,0:T(8,128)(2,1)}, u32[]{:S(2)}, u32[]{:S(2)}) collective-permute-start(bf16[512,768]{1,0:T(8,128)(2,1)} %collective-permute-done.7.refs_6_), channel_id=1, source_target_pairs={{0,8},{4,12},{8,0},{12,4},{16,24},{20,28},{24,16},{28,20},{1,9},{5... | collective-permute-start | bytes 2359304 | tf_op jit(solution)/shard_map/ppermute | solution.py:33
  67.4 26.9 %collective-permute-start.12 = (bf16[512,768]{1,0:T(8,128)(2,1)}, bf16[512,768]{1,0:T(8,128)(2,1)}, u32[]{:S(2)}, u32[]{:S(2)}) collective-permute-start(bf16[512,768]{1,0:T(8,128)(2,1)} %collective-permute-done.7.refs_6_), channel_id=1, source_target_pairs={{0,16},{4,20},{8,24},{12,28},{16,0},{20,4},{24,8},{28,12},{1,17},{... | collective-permute-start | bytes 2359304 | tf_op jit(solution)/shard_map/ppermute | solution.py:33
  67.9 26.4 %collective-permute-start.13 = (bf16[512,768]{1,0:T(8,128)(2,1)}, bf16[512,768]{1,0:T(8,128)(2,1)}, u32[]{:S(2)}, u32[]{:S(2)}) collective-permute-start(bf16[512,768]{1,0:T(8,128)(2,1)} %collective-permute-done.7.refs_6_), channel_id=1, source_target_pairs={{0,1},{1,2},{2,3},{3,0},{4,5},{5,6},{6,7},{7,4},{8,9},{9,10},{10,1... | collective-permute-start | bytes 2359304 | tf_op jit(solution)/shard_map/ppermute | solution.py:573
  69.6 24.7 %collective-permute-start.9 = (bf16[256,768]{1,0:T(8,128)(2,1)}, bf16[256,768]{1,0:T(8,128)(2,1)}, u32[]{:S(2)}, u32[]{:S(2)}) collective-permute-start(bf16[256,768]{1,0:T(8,128)(2,1)} %slice.200), channel_id=1, source_target_pairs={{0,16},{4,20},{8,24},{12,28},{16,0},{20,4},{24,8},{28,12},{1,17},{... | collective-permute-start | bytes 1179656 | tf_op jit(solution)/shard_map/ppermute | solution.py:33
  71.9 22.4 %collective-permute-start.10 = (bf16[256,768]{1,0:T(8,128)(2,1)}, bf16[256,768]{1,0:T(8,128)(2,1)}, u32[]{:S(2)}, u32[]{:S(2)}) collective-permute-start(bf16[256,768]{1,0:T(8,128)(2,1)} %slice.201), channel_id=1, source_target_pairs={{0,8},{4,12},{8,0},{12,4},{16,24},{20,28},{24,16},{28,20},{1,9},{5... | collective-permute-start | bytes 1179656 | tf_op jit(solution)/shard_map/ppermute | solution.py:33
  94.4 136.4 %all-gather.8.cloned.1.call-start = ((), (), s32[]{:S(2)}) async-start(), calls=%async_computation.6 | async-start | bytes 7208960 | tf_op jit(solution)/shard_map/all_gather | solution.py:586
  99.7 27.9 %collective-permute-start.16 = (bf16[512,768]{1,0:T(8,128)(2,1)}, bf16[512,768]{1,0:T(8,128)(2,1)}, u32[]{:S(2)}, u32[]{:S(2)}) collective-permute-start(bf16[512,768]{1,0:T(8,128)(2,1)} %collective-permute-done.13.refs_7_), channel_id=1, source_target_pairs={{0,8},{4,12},{8,0},{12,4},{16,24},{20,28},{24,16},{28,20},{1,9},{5... | collective-permute-start | bytes 2359304 | tf_op jit(solution)/shard_map/ppermute | solution.py:33
  101.2 26.4 %collective-permute-start.17 = (bf16[512,768]{1,0:T(8,128)(2,1)}, bf16[512,768]{1,0:T(8,128)(2,1)}, u32[]{:S(2)}, u32[]{:S(2)}) collective-permute-start(bf16[512,768]{1,0:T(8,128)(2,1)} %collective-permute-done.13.refs_7_), channel_id=1, source_target_pairs={{0,16},{4,20},{8,24},{12,28},{16,0},{20,4},{24,8},{28,12},{1,17},{... | collective-permute-start | bytes 2359304 | tf_op jit(solution)/shard_map/ppermute | solution.py:33
  103.0 23.8 %collective-permute-start.14 = (bf16[256,768]{1,0:T(8,128)(2,1)S(1)}, bf16[256,768]{1,0:T(8,128)(2,1)S(1)}, u32[]{:S(2)}, u32[]{:S(2)}) collective-permute-start(bf16[256,768]{1,0:T(8,128)(2,1)S(1)} %slice.202), channel_id=1, source_target_pairs={{0,16},{4,20},{8,24},{12,28},{16,0},{20,4},{24,8},{28,12},{1,17},{... | collective-permute-start | bytes 1179656 | tf_op jit(solution)/shard_map/ppermute | solution.py:33
  105.6 22.0 %collective-permute-start.15 = (bf16[256,768]{1,0:T(8,128)(2,1)S(1)}, bf16[256,768]{1,0:T(8,128)(2,1)}, u32[]{:S(2)}, u32[]{:S(2)}) collective-permute-start(bf16[256,768]{1,0:T(8,128)(2,1)S(1)} %slice.203), channel_id=1, source_target_pairs={{0,8},{4,12},{8,0},{12,4},{16,24},{20,28},{24,16},{28,20},{1,9},{5... | collective-permute-start | bytes 1179656 | tf_op jit(solution)/shard_map/ppermute | solution.py:33
  127.7 166.5 %all-gather.10.cloned.1.call-start = ((), (), s32[]{:S(2)}) async-start(), calls=%async_computation.7 | async-start | bytes 3604480 | tf_op jit(solution)/shard_map/all_gather | solution.py:588
  130.3 45.8 %collective-permute-start.20 = (bf16[256,2048]{1,0:T(8,128)(2,1)}, bf16[256,2048]{1,0:T(8,128)(2,1)S(1)}, u32[]{:S(2)}, u32[]{:S(2)}) collective-permute-start(bf16[256,2048]{1,0:T(8,128)(2,1)} %all-gather.6.cloned.1.call-done.out_ref), channel_id=1, source_target_pairs={{0,8},{4,12},{8,0},{12,4},{16,24},{20,28},{24,16},{28,20},{1,9},{5... | collective-permute-start | bytes 3145736 | tf_op jit(solution)/shard_map/ppermute | solution.py:33
  130.9 45.2 %collective-permute-start.21 = (bf16[256,2048]{1,0:T(8,128)(2,1)}, bf16[256,2048]{1,0:T(8,128)(2,1)S(1)}, u32[]{:S(2)}, u32[]{:S(2)}) collective-permute-start(bf16[256,2048]{1,0:T(8,128)(2,1)} %all-gather.6.cloned.1.call-done.out_ref), channel_id=1, source_target_pairs={{0,16},{4,20},{8,24},{12,28},{16,0},{20,4},{24,8},{28,12},{1,17},{... | collective-permute-start | bytes 3145736 | tf_op jit(solution)/shard_map/ppermute | solution.py:33
  132.5 33.8 %collective-permute-start.18 = (bf16[256,768]{1,0:T(8,128)(2,1)S(1)}, bf16[256,768]{1,0:T(8,128)(2,1)S(1)}, u32[]{:S(2)}, u32[]{:S(2)}) collective-permute-start(bf16[256,768]{1,0:T(8,128)(2,1)S(1)} %slice.204), channel_id=1, source_target_pairs={{0,16},{4,20},{8,24},{12,28},{16,0},{20,4},{24,8},{28,12},{1,17},{... | collective-permute-start | bytes 1179656 | tf_op jit(solution)/shard_map/ppermute | solution.py:33
  135.1 31.2 %collective-permute-start.19 = (bf16[256,768]{1,0:T(8,128)(2,1)S(1)}, bf16[256,768]{1,0:T(8,128)(2,1)S(1)}, u32[]{:S(2)}, u32[]{:S(2)}) collective-permute-start(bf16[256,768]{1,0:T(8,128)(2,1)S(1)} %slice.205), channel_id=1, source_target_pairs={{0,8},{4,12},{8,0},{12,4},{16,24},{20,28},{24,16},{28,20},{1,9},{5... | collective-permute-start | bytes 1179656 | tf_op jit(solution)/shard_map/ppermute | solution.py:33
  202.3 14.0 %collective-permute-start.25 = (bf16[128,2048]{1,0:T(8,128)(2,1)S(1)}, bf16[128,2048]{1,0:T(8,128)(2,1)S(1)}, u32[]{:S(2)}, u32[]{:S(2)}) collective-permute-start(bf16[128,2048]{1,0:T(8,128)(2,1)S(1)} %get-tuple-element.388), channel_id=1, source_target_pairs={{0,8},{4,12},{8,0},{12,4},{16,24},{20,28},{24,16},{28,20},{1,9},{5... | collective-permute-start | bytes 1572872 | tf_op jit(solution)/shard_map/ppermute | solution.py:33
  202.7 13.7 %collective-permute-start.26 = (bf16[128,2048]{1,0:T(8,128)(2,1)S(1)}, bf16[128,2048]{1,0:T(8,128)(2,1)S(1)}, u32[]{:S(2)}, u32[]{:S(2)}) collective-permute-start(bf16[128,2048]{1,0:T(8,128)(2,1)S(1)} %get-tuple-element.388), channel_id=1, source_target_pairs={{0,16},{4,20},{8,24},{12,28},{16,0},{20,4},{24,8},{28,12},{1,17},{... | collective-permute-start | bytes 1572872 | tf_op jit(solution)/shard_map/ppermute | solution.py:33
  234.4 17.9 %collective-permute-start.29 = (bf16[512,2048]{1,0:T(8,128)(2,1)}, bf16[512,2048]{1,0:T(8,128)(2,1)}, u32[]{:S(2)}, u32[]{:S(2)}) collective-permute-start(bf16[512,2048]{1,0:T(8,128)(2,1)} %get-tuple-element.365), channel_id=1, source_target_pairs={{0,4},{4,0},{8,12},{12,8},{16,20},{20,16},{24,28},{28,24},{1,5},{5... | collective-permute-start | bytes 6291464 | tf_op jit(solution)/shard_map/ppermute | solution.py:33
  236.5 241.4 %reduce-scatter.8.cloned.1.call-start = ((), (), s32[]{:S(2)}) async-start(), calls=%async_computation.9 | async-start | bytes 3604480 | tf_op jit(solution)/shard_map/reduce_scatter | solution.py:637
  236.6 14.6 %collective-permute-start.30 = (bf16[128,2048]{1,0:T(8,128)(2,1)}, bf16[128,2048]{1,0:T(8,128)(2,1)S(1)}, u32[]{:S(2)}, u32[]{:S(2)}) collective-permute-start(bf16[128,2048]{1,0:T(8,128)(2,1)} %fusion.15), channel_id=1, source_target_pairs={{0,8},{4,12},{8,0},{12,4},{16,24},{20,28},{24,16},{28,20},{1,9},{5... | collective-permute-start | bytes 1572872 | tf_op jit(solution)/shard_map/ppermute | solution.py:33
  238.1 14.2 %collective-permute-start.31 = (bf16[128,2048]{1,0:T(8,128)(2,1)}, bf16[128,2048]{1,0:T(8,128)(2,1)S(1)}, u32[]{:S(2)}, u32[]{:S(2)}) collective-permute-start(bf16[128,2048]{1,0:T(8,128)(2,1)} %fusion.15), channel_id=1, source_target_pairs={{0,16},{4,20},{8,24},{12,28},{16,0},{20,4},{24,8},{28,12},{1,17},{... | collective-permute-start | bytes 1572872 | tf_op jit(solution)/shard_map/ppermute | solution.py:33
  338.4 139.5 %reduce-scatter.10.cloned.1.call-start = ((), (), s32[]{:S(2)}) async-start(), calls=%async_computation.10 | async-start | bytes 3604480 | tf_op jit(solution)/shard_map/reduce_scatter | solution.py:637
  348.4 166.3 %reduce-scatter.6.cloned.1.call-start = ((), (), s32[]{:S(2)}) async-start(), calls=%async_computation.8 | async-start | bytes 3604480 | tf_op jit(solution)/shard_map/reduce_scatter | solution.py:637
  372.8 210.9 %all-gather.12.cloned.1.call-start = ((), (), s32[]{:S(2)}) async-start(), calls=%async_computation.11 | async-start | bytes 6488064 | tf_op jit(solution)/shard_map/all_gather | solution.py:672
  400.6 41.7 %collective-permute-start.43 = (bf16[1024,768]{1,0:T(8,128)(2,1)S(1)}, bf16[1024,768]{1,0:T(8,128)(2,1)}, u32[]{:S(2)}, u32[]{:S(2)}) collective-permute-start(bf16[1024,768]{1,0:T(8,128)(2,1)S(1)} %get-tuple-element.216), channel_id=1, source_target_pairs={{0,8},{4,12},{8,0},{12,4},{16,24},{20,28},{24,16},{28,20},{1,9},{5... | collective-permute-start | bytes 4718600 | tf_op jit(solution)/shard_map/ppermute | solution.py:33
  401.8 40.5 %collective-permute-start.44 = (bf16[1024,768]{1,0:T(8,128)(2,1)}, bf16[1024,768]{1,0:T(8,128)(2,1)S(1)}, u32[]{:S(2)}, u32[]{:S(2)}) collective-permute-start(bf16[1024,768]{1,0:T(8,128)(2,1)} %get-tuple-element.217), channel_id=1, source_target_pairs={{0,16},{4,20},{8,24},{12,28},{16,0},{20,4},{24,8},{28,12},{1,17},{... | collective-permute-start | bytes 4718600 | tf_op jit(solution)/shard_map/ppermute | solution.py:33
  420.2 50.5 %collective-permute-start.47 = (bf16[1024,768]{1,0:T(8,128)(2,1)S(1)}, bf16[1024,768]{1,0:T(8,128)(2,1)S(1)}, u32[]{:S(2)}, u32[]{:S(2)}) collective-permute-start(bf16[1024,768]{1,0:T(8,128)(2,1)S(1)} %get-tuple-element.221), channel_id=1, source_target_pairs={{0,8},{4,12},{8,0},{12,4},{16,24},{20,28},{24,16},{28,20},{1,9},{5... | collective-permute-start | bytes 4718600 | tf_op jit(solution)/shard_map/ppermute | solution.py:33
  440.5 36.3 %collective-permute-start.48 = (bf16[1024,768]{1,0:T(8,128)(2,1)}, bf16[1024,768]{1,0:T(8,128)(2,1)S(1)}, u32[]{:S(2)}, u32[]{:S(2)}) collective-permute-start(bf16[1024,768]{1,0:T(8,128)(2,1)} %get-tuple-element.224), channel_id=1, source_target_pairs={{0,16},{4,20},{8,24},{12,28},{16,0},{20,4},{24,8},{28,12},{1,17},{... | collective-permute-start | bytes 4718600 | tf_op jit(solution)/shard_map/ppermute | solution.py:33
  477.9 165.8 %reduce-scatter.12.cloned.1.call-start = ((), (), s32[]{:S(2)}) async-start(), calls=%async_computation.12 | async-start | bytes 3932160 | tf_op jit(solution)/shard_map/reduce_scatter | solution.py:674
  481.4 35.6 %collective-permute-start.45 = (bf16[1024,768]{1,0:T(8,128)(2,1)}, bf16[1024,768]{1,0:T(8,128)(2,1)}, u32[]{:S(2)}, u32[]{:S(2)}) collective-permute-start(bf16[1024,768]{1,0:T(8,128)(2,1)} %add_convert_fusion.6), channel_id=1, source_target_pairs={{0,16},{4,20},{8,24},{12,28},{16,0},{20,4},{24,8},{28,12},{1,17},{... | collective-permute-start | bytes 4718600 | tf_op jit(solution)/shard_map/ppermute | solution.py:33
  486.5 35.2 %collective-permute-start.46 = (bf16[1024,768]{1,0:T(8,128)(2,1)}, bf16[1024,768]{1,0:T(8,128)(2,1)}, u32[]{:S(2)}, u32[]{:S(2)}) collective-permute-start(bf16[1024,768]{1,0:T(8,128)(2,1)} %add_convert_fusion.5), channel_id=1, source_target_pairs={{0,8},{4,12},{8,0},{12,4},{16,24},{20,28},{24,16},{28,20},{1,9},{5... | collective-permute-start | bytes 4718600 | tf_op jit(solution)/shard_map/ppermute | solution.py:33
  494.9 36.8 %collective-permute-start.55 = (bf16[512,2048]{1,0:T(8,128)(2,1)}, bf16[512,2048]{1,0:T(8,128)(2,1)}, u32[]{:S(2)}, u32[]{:S(2)}) collective-permute-start(bf16[512,2048]{1,0:T(8,128)(2,1)} %slice.268), channel_id=1, source_target_pairs={{0,4},{4,0},{8,12},{12,8},{16,20},{20,16},{24,28},{28,24},{1,5},{5... | collective-permute-start | bytes 6291464 | tf_op jit(solution)/shard_map/ppermute | solution.py:33
  525.5 47.7 %collective-permute-start.56 = (bf16[512,2048]{1,0:T(8,128)(2,1)}, bf16[512,2048]{1,0:T(8,128)(2,1)}, u32[]{:S(2)}, u32[]{:S(2)}) collective-permute-start(bf16[512,2048]{1,0:T(8,128)(2,1)} %slice.317), channel_id=1, source_target_pairs={{0,4},{4,0},{8,12},{12,8},{16,20},{20,16},{24,28},{28,24},{1,5},{5... | collective-permute-start | bytes 6291464 | tf_op jit(solution)/shard_map/ppermute | solution.py:33
  525.5 47.7 %collective-permute-start.53 = (bf16[704,512]{1,0:T(8,128)(2,1)}, bf16[704,512]{1,0:T(8,128)(2,1)}, u32[]{:S(2)}, u32[]{:S(2)}) collective-permute-start(bf16[704,512]{1,0:T(8,128)(2,1)} %reduce-scatter.6.cloned.1.call-done), channel_id=1, source_target_pairs={{0,8},{4,12},{8,0},{12,4},{16,24},{20,28},{24,16},{28,20},{1,9},{5... | collective-permute-start | bytes 2162696 | tf_op jit(solution)/shard_map/ppermute | solution.py:33
  526.3 47.0 %collective-permute-start.54 = (bf16[704,512]{1,0:T(8,128)(2,1)}, bf16[704,512]{1,0:T(8,128)(2,1)}, u32[]{:S(2)}, u32[]{:S(2)}) collective-permute-start(bf16[704,512]{1,0:T(8,128)(2,1)} %reduce-scatter.6.cloned.1.call-done), channel_id=1, source_target_pairs={{0,16},{4,20},{8,24},{12,28},{16,0},{20,4},{24,8},{28,12},{1,17},{... | collective-permute-start | bytes 2162696 | tf_op jit(solution)/shard_map/ppermute | solution.py:33
  528.4 42.8 %collective-permute-start.51 = (bf16[128,2048]{1,0:T(8,128)(2,1)}, bf16[128,2048]{1,0:T(8,128)(2,1)S(1)}, u32[]{:S(2)}, u32[]{:S(2)}) collective-permute-start(bf16[128,2048]{1,0:T(8,128)(2,1)} %get-tuple-element.323), channel_id=1, source_target_pairs={{0,8},{4,12},{8,0},{12,4},{16,24},{20,28},{24,16},{28,20},{1,9},{5... | collective-permute-start | bytes 1572872 | tf_op jit(solution)/shard_map/ppermute | solution.py:33
  531.8 40.4 %collective-permute-start.52 = (bf16[128,2048]{1,0:T(8,128)(2,1)}, bf16[128,2048]{1,0:T(8,128)(2,1)}, u32[]{:S(2)}, u32[]{:S(2)}) collective-permute-start(bf16[128,2048]{1,0:T(8,128)(2,1)} %get-tuple-element.322), channel_id=1, source_target_pairs={{0,16},{4,20},{8,24},{12,28},{16,0},{20,4},{24,8},{28,12},{1,17},{... | collective-permute-start | bytes 1572872 | tf_op jit(solution)/shard_map/ppermute | solution.py:33
  571.2 26.4 %collective-permute-start.49 = (bf16[128,2048]{1,0:T(8,128)(2,1)}, bf16[128,2048]{1,0:T(8,128)(2,1)}, u32[]{:S(2)}, u32[]{:S(2)}) collective-permute-start(bf16[128,2048]{1,0:T(8,128)(2,1)} %get-tuple-element.325), channel_id=1, source_target_pairs={{0,8},{4,12},{8,0},{12,4},{16,24},{20,28},{24,16},{28,20},{1,9},{5... | collective-permute-start | bytes 1572872 | tf_op jit(solution)/shard_map/ppermute | solution.py:33
  572.2 27.5 %collective-permute-start.50 = (bf16[128,2048]{1,0:T(8,128)(2,1)}, bf16[128,2048]{1,0:T(8,128)(2,1)}, u32[]{:S(2)}, u32[]{:S(2)}) collective-permute-start(bf16[128,2048]{1,0:T(8,128)(2,1)} %get-tuple-element.324), channel_id=1, source_target_pairs={{0,16},{4,20},{8,24},{12,28},{16,0},{20,4},{24,8},{28,12},{1,17},{... | collective-permute-start | bytes 1572872 | tf_op jit(solution)/shard_map/ppermute | solution.py:33
  575.0 29.1 %collective-permute-start.57 = (bf16[352,512]{1,0:T(8,128)(2,1)}, bf16[352,512]{1,0:T(8,128)(2,1)}, u32[]{:S(2)}, u32[]{:S(2)}) collective-permute-start(bf16[352,512]{1,0:T(8,128)(2,1)} %slice.233), channel_id=1, source_target_pairs={{0,16},{4,20},{8,24},{12,28},{16,0},{20,4},{24,8},{28,12},{1,17},{... | collective-permute-start | bytes 1081352 | tf_op jit(solution)/shard_map/ppermute | solution.py:33
  577.7 26.4 %collective-permute-start.58 = (bf16[352,512]{1,0:T(8,128)(2,1)}, bf16[352,512]{1,0:T(8,128)(2,1)}, u32[]{:S(2)}, u32[]{:S(2)}) collective-permute-start(bf16[352,512]{1,0:T(8,128)(2,1)} %slice.234), channel_id=1, source_target_pairs={{0,8},{4,12},{8,0},{12,4},{16,24},{20,28},{24,16},{28,20},{1,9},{5... | collective-permute-start | bytes 1081352 | tf_op jit(solution)/shard_map/ppermute | solution.py:33
  583.7 105.9 %reduce-scatter.14.cloned.1.call-start = ((), (), s32[]{:S(2)}) async-start(), calls=%async_computation.13 | async-start | bytes 1310720 | tf_op jit(solution)/shard_map/reduce_scatter | solution.py:692
  586.0 13.7 %collective-permute-start.59 = (bf16[64,2048]{1,0:T(8,128)(2,1)S(1)}, bf16[64,2048]{1,0:T(8,128)(2,1)S(1)}, u32[]{:S(2)}, u32[]{:S(2)}) collective-permute-start(bf16[64,2048]{1,0:T(8,128)(2,1)S(1)} %get-tuple-element.331), channel_id=1, source_target_pairs={{0,8},{4,12},{8,0},{12,4},{16,24},{20,28},{24,16},{28,20},{1,9},{5... | collective-permute-start | bytes 786440 | tf_op jit(solution)/shard_map/ppermute | solution.py:33
  606.3 16.9 %collective-permute-start.63 = (bf16[2816,512]{1,0:T(8,128)(2,1)S(1)}, bf16[2816,512]{1,0:T(8,128)(2,1)S(1)}, u32[]{:S(2)}, u32[]{:S(2)}) collective-permute-start(bf16[2816,512]{1,0:T(8,128)(2,1)S(1)} %constant_dynamic-update-slice_fusion.45.same_ref), channel_id=1, source_target_pairs={{0,4},{4,0},{8,12},{12,8},{16,20},{20,16},{24,28},{28,24},{1,5},{5... | collective-permute-start | bytes 8650760 | tf_op jit(solution)/shard_map/ppermute | solution.py:33
  607.8 14.4 %collective-permute-start.61 = (bf16[128,2048]{1,0:T(8,128)(2,1)S(1)}, bf16[128,2048]{1,0:T(8,128)(2,1)S(1)}, u32[]{:S(2)}, u32[]{:S(2)}) collective-permute-start(bf16[128,2048]{1,0:T(8,128)(2,1)S(1)} %get-tuple-element.321), channel_id=1, source_target_pairs={{0,16},{4,20},{8,24},{12,28},{16,0},{20,4},{24,8},{28,12},{1,17},{... | collective-permute-start | bytes 1572872 | tf_op jit(solution)/shard_map/ppermute | solution.py:33
  609.1 14.0 %collective-permute-start.62 = (bf16[128,2048]{1,0:T(8,128)(2,1)S(1)}, bf16[128,2048]{1,0:T(8,128)(2,1)S(1)}, u32[]{:S(2)}, u32[]{:S(2)}) collective-permute-start(bf16[128,2048]{1,0:T(8,128)(2,1)S(1)} %get-tuple-element.320), channel_id=1, source_target_pairs={{0,8},{4,12},{8,0},{12,4},{16,24},{20,28},{24,16},{28,20},{1,9},{5... | collective-permute-start | bytes 1572872 | tf_op jit(solution)/shard_map/ppermute | solution.py:33
  643.7 102.6 %all-gather.14.cloned.1.call-start = ((), (), s32[]{:S(2)}) async-start(), calls=%async_computation.14 | async-start | bytes 6488064 | tf_op jit(solution)/shard_map/all_gather | solution.py:698
  643.8 45.8 %collective-permute-start.65 = (bf16[512,768]{1,0:T(8,128)(2,1)}, bf16[512,768]{1,0:T(8,128)(2,1)}, u32[]{:S(2)}, u32[]{:S(2)}) collective-permute-start(bf16[512,768]{1,0:T(8,128)(2,1)} %reduce-scatter.12.cloned.1.call-done), channel_id=1, source_target_pairs={{0,8},{4,12},{8,0},{12,4},{16,24},{20,28},{24,16},{28,20},{1,9},{5... | collective-permute-start | bytes 2359304 | tf_op jit(solution)/shard_map/ppermute | solution.py:33
  645.3 44.3 %collective-permute-start.66 = (bf16[512,768]{1,0:T(8,128)(2,1)}, bf16[512,768]{1,0:T(8,128)(2,1)}, u32[]{:S(2)}, u32[]{:S(2)}) collective-permute-start(bf16[512,768]{1,0:T(8,128)(2,1)} %reduce-scatter.12.cloned.1.call-done), channel_id=1, source_target_pairs={{0,16},{4,20},{8,24},{12,28},{16,0},{20,4},{24,8},{28,12},{1,17},{... | collective-permute-start | bytes 2359304 | tf_op jit(solution)/shard_map/ppermute | solution.py:33
  646.8 22.0 %collective-permute-start.69 = (bf16[64,2048]{1,0:T(8,128)(2,1)}, bf16[64,2048]{1,0:T(8,128)(2,1)S(1)}, u32[]{:S(2)}, u32[]{:S(2)}) collective-permute-start(bf16[64,2048]{1,0:T(8,128)(2,1)} %get-tuple-element.329), channel_id=1, source_target_pairs={{0,8},{4,12},{8,0},{12,4},{16,24},{20,28},{24,16},{28,20},{1,9},{5... | collective-permute-start | bytes 786440 | tf_op jit(solution)/shard_map/ppermute | solution.py:33
  647.3 24.3 %collective-permute-start.70 = (bf16[64,2048]{1,0:T(8,128)(2,1)}, bf16[64,2048]{1,0:T(8,128)(2,1)S(1)}, u32[]{:S(2)}, u32[]{:S(2)}) collective-permute-start(bf16[64,2048]{1,0:T(8,128)(2,1)} %get-tuple-element.328), channel_id=1, source_target_pairs={{0,16},{4,20},{8,24},{12,28},{16,0},{20,4},{24,8},{28,12},{1,17},{... | collective-permute-start | bytes 786440 | tf_op jit(solution)/shard_map/ppermute | solution.py:33
  649.8 39.7 %collective-permute-start.67 = (bf16[64,2048]{1,0:T(8,128)(2,1)}, bf16[64,2048]{1,0:T(8,128)(2,1)S(1)}, u32[]{:S(2)}, u32[]{:S(2)}) collective-permute-start(bf16[64,2048]{1,0:T(8,128)(2,1)} %get-tuple-element.333), channel_id=1, source_target_pairs={{0,16},{4,20},{8,24},{12,28},{16,0},{20,4},{24,8},{28,12},{1,17},{... | collective-permute-start | bytes 786440 | tf_op jit(solution)/shard_map/ppermute | solution.py:33
  668.7 20.8 %collective-permute-start.68 = (bf16[64,2048]{1,0:T(8,128)(2,1)}, bf16[64,2048]{1,0:T(8,128)(2,1)S(1)}, u32[]{:S(2)}, u32[]{:S(2)}) collective-permute-start(bf16[64,2048]{1,0:T(8,128)(2,1)} %get-tuple-element.332), channel_id=1, source_target_pairs={{0,8},{4,12},{8,0},{12,4},{16,24},{20,28},{24,16},{28,20},{1,9},{5... | collective-permute-start | bytes 786440 | tf_op jit(solution)/shard_map/ppermute | solution.py:33
  707.6 16.7 %collective-permute-start.75 = (bf16[2048,768]{1,0:T(8,128)(2,1)}, bf16[2048,768]{1,0:T(8,128)(2,1)}, u32[]{:S(2)}, u32[]{:S(2)}) collective-permute-start(bf16[2048,768]{1,0:T(8,128)(2,1)} %constant_dynamic-update-slice_fusion.50.same_ref), channel_id=1, source_target_pairs={{0,4},{4,0},{8,12},{12,8},{16,20},{20,16},{24,28},{28,24},{1,5},{5... | collective-permute-start | bytes 9437192 | tf_op jit(solution)/shard_map/ppermute | solution.py:33
  710.1 12.9 %collective-permute-start.77 = (bf16[256,512]{1,0:T(8,128)(2,1)S(1)}, bf16[256,512]{1,0:T(8,128)(2,1)S(1)}, u32[]{:S(2)}, u32[]{:S(2)}) collective-permute-start(bf16[256,512]{1,0:T(8,128)(2,1)S(1)} %copy-done.70), channel_id=1, source_target_pairs={{0,16},{4,20},{8,24},{12,28},{16,0},{20,4},{24,8},{28,12},{1,17},{... | collective-permute-start | bytes 786440 | tf_op jit(solution)/shard_map/ppermute | solution.py:33
  (133 other events, 1131.1 us)
Sparse Core Ops, SparseCore 0:
  94.5 25.1 all-gather.5
  127.8 103.0 all-gather.7
  236.6 57.5 all-gather.9
  338.5 54.0 reduce-scatter.7
  395.3 56.0 reduce-scatter.9
  454.2 56.0 reduce-scatter.5
  512.1 62.1 all-gather.11
  583.8 59.8 reduce-scatter.11
  646.6 27.1 reduce-scatter.13
  689.8 49.5 all-gather.13

commit v6 on v5

--- a/solution.py
+++ b/solution.py
@@ -489,24 +489,6 @@
     )(me, same, other)
 
 
-def turn_kernel(in_ref, out_ref):
-    out_ref[...] = in_ref[...].T.astype(F32)
-
-
-def turn(value):
-    rows, width = value.shape
-    tile = 512 if rows % 512 == 0 else rows
-    return pl.pallas_call(
-        turn_kernel,
-        grid=(rows // tile,),
-        in_specs=[pl.BlockSpec((tile, width), lambda i: (i, 0))],
-        out_specs=pl.BlockSpec((width, tile), lambda i: (0, i)),
-        out_shape=jax.ShapeDtypeStruct((width, rows), F32),
-        cost_estimate=pl.CostEstimate(flops=0, bytes_accessed=6 * value.size, transcendentals=0),
-        name="turn",
-    )(value)
-
-
 def per_device(
     layer_input,
     gain_attn,
@@ -627,14 +609,18 @@
     grad_up_act = (grad_inner * silu).astype(BF)
     grad_act = jnp.concatenate([grad_gate_act, grad_up_act], axis=1)
     back_flow = Flow(plane_sum_steps(mm_nt(grad_act, gate_up).astype(BF)))
-    grad_mlp, sums = [], []
+    flows, sums = [back_flow], []
     for left, right in (
         (grad_gate_act, dispatched),
         (grad_up_act, dispatched),
         (inner, all_slot_grad),
     ):
-        grad = stage([back_flow], mm_tn(left, right).astype(BF))
+        grad = stage(flows, mm_tn(left, right).astype(BF))
         sums.append(lax.psum_scatter(grad, "shard", scatter_dimension=1, tiled=True))
+        if len(flows) == 1:
+            expert_flow = Flow(plane_sum_steps(mm(inner, down).astype(BF)))
+            flows.append(expert_flow)
+    stage(flows)
     grad_normed_two = mm_tn(pick, finish(back_flow))
     grad_gain_two, through = norm_back(grad_normed_two, hidden, root_two, gain_two)
     grad_hidden = upstream + through
@@ -655,7 +641,7 @@
             lins[d], grad_qkv_w[d] = lin, grad
 
     far, near = offsets[-1:], offsets[1:-1]
-    values, both_grad = lax.optimization_barrier((run_back(*far), both_grad))
+    values, both_grad = stage([expert_flow], (run_back(*far), both_grad))
     keep(far, values)
     qkv_flow = Flow(scatter_steps(grad_qkv_w))
     values, both_grad = stage([qkv_flow], (run_back(*near), both_grad))
@@ -665,41 +651,37 @@
     grad_normed = normed_back(
         shard, [lins[d] for d in offsets], [qkv_w[d] for d in offsets], both.shape[1]
     )
-    own_lin, sums[1] = lax.optimization_barrier((lins[0], (sums[1], sums[2])))
-    sums[1], sums[2] = sums[1]
-    lins[0] = own_lin
-    sums[0], grad_normed, grad_out_w = stage([qkv_flow], (sums[0], grad_normed, grad_out_w))
-    all_up = lax.all_gather(sums[1], "rep", axis=0, tiled=True)
-    own_grad_qkv, all_up = lax.optimization_barrier((finish(qkv_flow), all_up))
+    sums[0], sums[1], grad_normed, grad_out_w = stage(
+        [qkv_flow], (sums[0], sums[1], grad_normed, grad_out_w)
+    )
+    own_grad_qkv, sums[2] = lax.optimization_barrier((finish(qkv_flow), sums[2]))
     sum_qkv = lax.psum_scatter(own_grad_qkv, "shard", scatter_dimension=0, tiled=True)
 
     out_blocks = {d: halves(grad_out_w[i * block : (i + 1) * block]) for i, d in enumerate(offsets)}
     out_flow, gate_flow = Flow(scatter_steps(out_blocks)), Flow(copies_steps(sums[0]))
-    expert_flow = Flow(plane_sum_steps(mm(inner, down).astype(BF)))
-    other_normed = stage(
-        [out_flow, gate_flow, expert_flow], swap(grad_normed[length:].astype(BF), 1)
+    other_normed, up_sum = stage(
+        [out_flow, gate_flow], (swap(grad_normed[length:].astype(BF), 1), sums[1])
     )
     grad_normed = grad_normed[:length] + other_normed.astype(F32)
     grad_gain_one, first = norm_back(grad_normed, inputs, root_one, gain_one)
     grad_input = (grad_hidden + first).astype(BF)
-    grad_input, gains = stage(
-        [out_flow, gate_flow, expert_flow], (grad_input, jnp.stack([grad_gain_one, grad_gain_two]))
+    grad_input, gains, up_sum = stage(
+        [out_flow, gate_flow],
+        (grad_input, jnp.stack([grad_gain_one, grad_gain_two]), up_sum),
     )
-    gain_flow = Flow(vector_sum_steps(gains))
-    stage([out_flow, gate_flow, gain_flow])
+    gain_flow, up_flow = Flow(vector_sum_steps(gains)), Flow(copies_steps(up_sum))
+    sum_qkv = stage([out_flow, gate_flow, up_flow, gain_flow], sum_qkv)
+    sum_out = lax.psum_scatter(finish(out_flow), "shard", scatter_dimension=1, tiled=True)
+    qkv_flow = Flow(copies_steps(sum_qkv))
     grad_gate = place_turned(whoami, *finish(gate_flow), units)
-    own_grad_out, sum_qkv = lax.optimization_barrier((finish(out_flow), sum_qkv))
-    sum_out = lax.psum_scatter(own_grad_out, "shard", scatter_dimension=1, tiled=True)
-    grad_gate, all_up = stage([expert_flow, gain_flow], (grad_gate, all_up))
-    grad_up = turn(all_up)
-    qkv_flow = Flow(copies_steps(sum_qkv))
-    grad_up, sum_out = stage([qkv_flow, expert_flow], (grad_up, sum_out))
+    grad_gate, sum_out = stage([up_flow, qkv_flow, gain_flow], (grad_gate, sum_out))
     down_sum, sum_out = lax.optimization_barrier((sums[2], sum_out))
     all_down = lax.all_gather(down_sum, "rep", axis=0, tiled=True)
-    stage([qkv_flow, gain_flow])
     out_flow = Flow(copies_steps(sum_out))
     output = (hidden + mm_tn(pick, finish(expert_flow)) * mix[:, None]).astype(BF)
-    output = stage([qkv_flow, out_flow, gain_flow], output)
+    output = stage([up_flow, qkv_flow, out_flow, gain_flow], output)
+    grad_up = place_turned(whoami, *finish(up_flow), units)
+    grad_up = stage([qkv_flow, out_flow, gain_flow], grad_up)
     grad_query, grad_key, grad_value = place(whoami, *finish(qkv_flow), own, block, True)
     grad_query = stage([out_flow], grad_query)
     (grad_out,) = place(whoami, *finish(out_flow), block, own, False)

time: 771 us -> 753 us (0.977)
  waiting for transfers between devices: 251 us -> 229 us
  local copies, waits for them, and re-layouts: 99.4 us -> 110 us
    reduce_scatter x1, waiting for transfers between devices: 16.2 us -> 0.01 us  [per_device(): lax.psum_scatter(own_grad_qkv, 'shard', scatter_dimension=0, tiled=True)]
    unnamed x242 -> x234, local copies, waits for them, and re-layouts: 52.7 us -> 64.6 us
    pallas_call x1 -> x0, Pallas kernels: 10.4 us -> none  [turn(): pl.pallas_call(turn_kernel, grid=(rows // tile,), in_specs=[pl.BlockSpec(...]
    ppermute x75 -> x80, waiting for transfers between devices: 189 us -> 184 us  [swap(): return lax.ppermute(value, 'rep', [(i, i ^ bit) for i in range(size)])]
    ppermute x75 -> x80, starting transfers between devices: 67.6 us -> 70.9 us  [swap(): return lax.ppermute(value, 'rep', [(i, i ^ bit) for i in range(size)])]
  transfers between devices with their start and end apart: 94 -> 98, of which waited for: 41 -> 37; matrix products, arithmetic and copies ran while one was open for 23% -> 24% of each run, Pallas kernels for 22% -> 21%
where the time goes in v6:
time: 753 us; the launch traced here: 744 us
  waiting for transfers between devices  229 us (30%)
  Pallas kernels  159 us (21%)
  local copies, waits for them, and re-layouts  110 us (15%)
  starting transfers between devices  87 us (12%)
  matrix products  71.9 us (10%)
  other arithmetic  70.9 us (9%)
  between operations  15.7 us (2%)
    ppermute x80, waiting for transfers between devices, swap(): return lax.ppermute(value, 'rep', [(i, i ^ bit) for i in range(size)])  184 us
    ppermute x80, starting transfers between devices, swap(): return lax.ppermute(value, 'rep', [(i, i ^ bit) for i in range(size)])  70.9 us
    pallas_call x4, Pallas kernels, attend_back(): pl.pallas_call(attend_back_kernel, grid=(rows // length,), in_specs=[by_s...  68.6 us
    unnamed x234, local copies, waits for them, and re-layouts  64.6 us
    pallas_call x4, Pallas kernels, attend(): pl.pallas_call(functools.partial(attend_kernel, parts), grid_spec=pltpu.P...  43.4 us
    dot_general x6, matrix products, mm_tn(): lax.dot_general(left, right, (((0,), (0,)), ((), ())), preferred_element_...  29.9 us
    dot_general x5, matrix products, mm(): return jnp.dot(left, right, preferred_element_type=F32)  22.4 us
    all_gather x1, waiting for transfers between devices, per_device(): down = lax.all_gather(own_down, 'shard', axis=1, tiled=True)  21.9 us
  transfers between devices with their start and end apart: 98, of which 37 were waited for; matrix products, arithmetic and copies ran while one was open for 24% of the time, Pallas kernels for 21%

profile of v6, /device:TPU:0, one launch (start us, length us, event | category | flops | bytes accessed | tf_op | source)
XLA Modules:
  0.0 743.6 jit_solution(17951498489462796156)
XLA Ops:
  8.8 5.1 collective-permute-start
  16.8 2.7 constant_dynamic-slice_fusion.5
  19.6 2.5 collective-permute-start.3
  22.1 2.3 constant_dynamic-slice_fusion.15
  27.1 12.9 %collective-permute-done.3.refs_5_ = bf16[512,768]{1,0:T(8,128)(2,1)} collective-permute-done((bf16[512,768]{1,0:T(8,128)(2,1)S(1)}, bf16[512,768]{1,0:T(8,128)(2,1)}, u32[]{:S(2)}, u32[]{:S(2)}) %collective-permute-start.3) | collective-permute-done | bytes 786464 | tf_op jit(solution)/shard_map/ppermute | solution.py:541
  40.1 2.1 fusion.2
  46.1 16.4 %collective-permute-done.5.refs_5_.refs_9_ = bf16[512,768]{1,0:T(8,128)(2,1)S(1)} collective-permute-done((bf16[512,768]{1,0:T(8,128)(2,1)}, bf16[512,768]{1,0:T(8,128)(2,1)S(1)}, u32[]{:S(2)}, u32[]{:S(2)}) %collective-permute-start.5) | collective-permute-done | bytes 786464 | tf_op jit(solution)/shard_map/ppermute | solution.py:33
  63.8 3.1 collective-permute-done.7.refs_6_
  74.1 20.2 %collective-permute-done.9 = bf16[256,768]{1,0:T(8,128)(2,1)} collective-permute-done((bf16[256,768]{1,0:T(8,128)(2,1)}, bf16[256,768]{1,0:T(8,128)(2,1)}, u32[]{:S(2)}, u32[]{:S(2)}) %collective-permute-start.9) | collective-permute-done | bytes 393248 | tf_op jit(solution)/shard_map/ppermute | solution.py:33
  107.3 2.8 pad_maximum_fusion.refs_0_.refs_1_.refs_2_.refs_3_.x_ref
  110.2 12.2 %attend.4 = (bf16[1024,256]{1,0:T(8,128)(2,1)S(1)}, bf16[1024,768]{1,0:T(8,128)(2,1)S(1)}, f32[1024,2]{1,0:T(8,128)S(1)}) custom-call(s32[1]{0:T(128)} %bitcast.1.z_ref, bf16[1024,2048]{1,0:T(8,128)(2,1)S(1)} %pad_maximum_fusion.refs_0_.refs_1_.refs_2_.refs_3_.x_ref, bf16[1024,2048]{1,0:T(8,128)(2,1)S(1)} %pad_maximum_fusion.refs_0_.refs_1_.refs_2_.refs_3_.x_ref, ...), custom_call_target="tpu_custom_call" | custom-call | flops 3758096384 | bytes 10485760 | tf_op jit(solution)/shard_map/attend/pallas_call | solution.py:251
  124.3 3.6 collective-permute-done.14
  140.8 10.7 %attend.5 = (bf16[1024,256]{1,0:T(8,128)(2,1)S(1)}, bf16[1024,768]{1,0:T(8,128)(2,1)S(1)}, f32[1024,2]{1,0:T(8,128)S(1)}) custom-call(s32[1]{0:T(128)} %bitcast.1.z_ref, bf16[1024,2048]{1,0:T(8,128)(2,1)S(1)} %copy-done.3, bf16[1024,2048]{1,0:T(8,128)(2,1)S(1)} %copy-done.3, bf16[1024,2048]{1,0:T(8,128)(2,1)S(1)} %copy-done.3, ...), custom_call_target="tpu_custom_call" | custom-call | flops 3758096384 | bytes 10485760 | tf_op jit(solution)/shard_map/attend/pallas_call | solution.py:251
  154.4 10.7 %attend.6 = (bf16[1024,256]{1,0:T(8,128)(2,1)S(1)}, bf16[1024,768]{1,0:T(8,128)(2,1)S(1)}, f32[1024,2]{1,0:T(8,128)S(1)}) custom-call(s32[1]{0:T(128)} %bitcast.1.z_ref, bf16[1024,2048]{1,0:T(8,128)(2,1)S(1)} %copy-done.3, bf16[1024,2048]{1,0:T(8,128)(2,1)S(1)} %copy-done.3, bf16[1024,2048]{1,0:T(8,128)(2,1)S(1)} %copy-done.3, ...), custom_call_target="tpu_custom_call" | custom-call | flops 3758096384 | bytes 10485760 | tf_op jit(solution)/shard_map/attend/pallas_call | solution.py:251
  167.6 9.8 %attend.7 = (bf16[1024,256]{1,0:T(8,128)(2,1)S(1)}, bf16[1024,768]{1,0:T(8,128)(2,1)S(1)}, f32[1024,2]{1,0:T(8,128)S(1)}) custom-call(s32[1]{0:T(128)} %bitcast.1.z_ref, bf16[1024,2048]{1,0:T(8,128)(2,1)S(1)} %copy-done.3, bf16[1024,2048]{1,0:T(8,128)(2,1)S(1)} %copy-done.3, bf16[1024,2048]{1,0:T(8,128)(2,1)S(1)} %copy-done.3, ...), custom_call_target="tpu_custom_call" | custom-call | flops 3758096384 | bytes 10485760 | tf_op jit(solution)/shard_map/attend/pallas_call | solution.py:251
  180.4 6.8 collective-permute-done.22
  189.8 6.1 fusion.54
  196.8 3.6 collective-permute-done.24
  205.9 10.4 %collective-permute-done.25 = bf16[128,2048]{1,0:T(8,128)(2,1)S(1)} collective-permute-done((bf16[128,2048]{1,0:T(8,128)(2,1)S(1)}, bf16[128,2048]{1,0:T(8,128)(2,1)S(1)}, u32[]{:S(2)}, u32[]{:S(2)}) %collective-permute-start.25) | collective-permute-done | bytes 524320 | tf_op jit(solution)/shard_map/ppermute | solution.py:33
  219.6 4.6 collective-permute-done.27
  225.1 6.8 all-gather.7.cloned.1.call-done
  242.7 9.6 %collective-permute-done.30 = bf16[128,2048]{1,0:T(8,128)(2,1)S(1)} collective-permute-done((bf16[128,2048]{1,0:T(8,128)(2,1)}, bf16[128,2048]{1,0:T(8,128)(2,1)S(1)}, u32[]{:S(2)}, u32[]{:S(2)}) %collective-permute-start.30) | collective-permute-done | bytes 524320 | tf_op jit(solution)/shard_map/ppermute | solution.py:33
  255.6 3.2 constant_dynamic-update-slice_fusion.28
  263.2 8.6 %fusion.55 = f32[1024,1408]{1,0:T(8,128)} fusion(bf16[1024,2048]{1,0:T(8,128)(2,1)S(1)} %copy-done.81, bf16[2048,1408]{1,0:T(8,128)(2,1)S(1)} %copy-done.94), kind=kOutput, calls=%fused_computation.216 | convolution fusion | flops 5905580032 | bytes 15728640 | tf_op jit(solution)/shard_map/dot_general | solution.py:20
  273.4 21.9 %all-gather.9.cloned.1.call-done = bf16[704,2048]{1,0:T(8,128)(2,1)} async-done(((bf16[704,512]{1,0:T(8,128)(2,1)}), bf16[704,2048]{1,0:T(8,128)(2,1)}) %all-gather.9.cloned.1.call-update) | async-done | bytes 2883600 | tf_op jit(solution)/shard_map/all_gather | solution.py:570
  295.3 10.2 %multiply_convert_fusion.3 = (bf16[1024,704]{1,0:T(8,128)(2,1)S(1)}, bf16[1024,704]{1,0:T(8,128)(2,1)S(1)}, bf16[1024,704]{1,0:T(8,128)(2,1)}) fusion(f32[1024,1408]{1,0:T(8,128)} %fusion.55, bf16[1024,2048]{1,0:T(8,128)(2,1)} %constant_dynamic-update-slice_fusion.39, bf16[704,2048]{1,0:T(8,128)(2,1)} %all-gather.9.cloned.1.call-done), kind=kOutput, calls=%fused_computation.44 | convolution fusion | flops 2963603456 | bytes 17170432 | tf_op jit(solution)/shard_map/dot_general | solution.py:24
  305.5 9.3 %convolution_convert_fusion = bf16[1024,2048]{1,0:T(8,128)(2,1)S(1)} fusion(bf16[2048,1408]{1,0:T(8,128)(2,1)} %all-gather.7.cloned.1.call-done, bf16[1024,704]{1,0:T(8,128)(2,1)S(1)} %get-tuple-element.330, bf16[1024,704]{1,0:T(8,128)(2,1)S(1)} %get-tuple-element.329), kind=kOutput, calls=%fused_computation.32 | convolution fusion | flops 5913444352 | bytes 12845056 | tf_op jit(solution)/shard_map/dot_general | solution.py:24
  319.8 4.5 convolution_convert_fusion.5
  324.6 5.7 convolution_convert_fusion.1
  334.8 3.1 add_convert_fusion.2
  343.2 4.5 convolution_convert_fusion.4
  349.8 3.0 add_convert_fusion.1
  365.1 7.5 %convolution_convert_fusion.3 = bf16[704,2048]{1,0:T(8,128)(2,1)} fusion(bf16[1024,704]{1,0:T(8,128)(2,1)} %get-tuple-element.331, bf16[1024,2048]{1,0:T(8,128)(2,1)} %constant_dynamic-update-slice_fusion.39), kind=kOutput, calls=%fused_computation.35 | convolution fusion | flops 2954231808 | bytes 8519680 | tf_op jit(solution)/shard_map/dot_general | solution.py:28
  375.5 3.6 multiply_reduce_fusion
  379.6 3.2 multiply_convert_fusion
  387.3 2.6 pad_maximum_fusion.1.grad_ref
  389.9 17.4 %attend_back.4 = (bf16[1024,768]{1,0:T(8,128)(2,1)S(1)}, bf16[1024,768]{1,0:T(8,128)(2,1)}, bf16[1024,768]{1,0:T(8,128)(2,1)}) custom-call(bf16[1024,2048]{1,0:T(8,128)(2,1)} %pad_maximum_fusion.1.grad_ref, bf16[256,2048]{1,0:T(8,128)(2,1)S(1)} %pad_maximum_fusion.4.out_ref, bf16[1024,768]{1,0:T(8,128)(2,1)} %copy-done.29, f32[1024,2]{1,0:T(8,128)S(1)} %copy-done.35, ...), custom_call_target="tpu_custom_call" | custom-call | flops 5637144576 | bytes 15728640 | tf_op jit(solution)/shard_map/attend_back/pallas_call | solution.py:340
  415.1 17.0 %attend_back.6 = (bf16[1024,768]{1,0:T(8,128)(2,1)S(1)}, bf16[1024,768]{1,0:T(8,128)(2,1)S(1)}, bf16[1024,768]{1,0:T(8,128)(2,1)}) custom-call(bf16[1024,2048]{1,0:T(8,128)(2,1)} %pad_maximum_fusion.1.grad_ref, bf16[256,2048]{1,0:T(8,128)(2,1)S(1)} %copy-done.13, bf16[1024,768]{1,0:T(8,128)(2,1)} %copy-done.28, f32[1024,2]{1,0:T(8,128)S(1)} %copy-done.33, ...), custom_call_target="tpu_custom_call" | custom-call | flops 5637144576 | bytes 15728640 | tf_op jit(solution)/shard_map/attend_back/pallas_call | solution.py:340
  434.0 17.0 %attend_back.5 = (bf16[1024,768]{1,0:T(8,128)(2,1)S(1)}, bf16[1024,768]{1,0:T(8,128)(2,1)S(1)}, bf16[1024,768]{1,0:T(8,128)(2,1)}) custom-call(bf16[1024,2048]{1,0:T(8,128)(2,1)} %pad_maximum_fusion.1.grad_ref, bf16[256,2048]{1,0:T(8,128)(2,1)S(1)} %copy-done.11, bf16[1024,768]{1,0:T(8,128)(2,1)} %copy-done.27, f32[1024,2]{1,0:T(8,128)S(1)} %get-tuple-element.226.lse_ref, ...), custom_call_target="tpu_custom_call" | custom-call | flops 5637144576 | bytes 15728640 | tf_op jit(solution)/shard_map/attend_back/pallas_call | solution.py:340
  451.8 3.1 add_convert_fusion.6
  455.9 3.3 add_convert_fusion.5
  460.6 7.7 %convolution_convert_fusion.2 = bf16[1024,2048]{1,0:T(8,128)(2,1)} fusion(bf16[1024,1024]{1,0:T(8,128)(2,1)} %constant_dynamic-update-slice_fusion.14, bf16[1024,2048]{1,0:T(8,128)(2,1)S(1)} %copy-done.55), kind=kOutput, calls=%fused_computation.34 | convolution fusion | flops 4297064448 | bytes 10485760 | tf_op jit(solution)/shard_map/dot_general | solution.py:28
  468.3 17.3 %attend_back.7 = (bf16[1024,768]{1,0:T(8,128)(2,1)S(1)}, bf16[1024,768]{1,0:T(8,128)(2,1)S(1)}, bf16[1024,768]{1,0:T(8,128)(2,1)}) custom-call(bf16[1024,2048]{1,0:T(8,128)(2,1)} %pad_maximum_fusion.1.grad_ref, bf16[256,2048]{1,0:T(8,128)(2,1)S(1)} %copy-done.25, bf16[1024,768]{1,0:T(8,128)(2,1)} %copy-done.26, f32[1024,2]{1,0:T(8,128)S(1)} %copy-done.31, ...), custom_call_target="tpu_custom_call" | custom-call | flops 5637144576 | bytes 15728640 | tf_op jit(solution)/shard_map/attend_back/pallas_call | solution.py:340
  488.6 19.8 %normed_back.1 = f32[1024,2048]{1,0:T(8,128)} custom-call(s32[1]{0:T(128)} %bitcast.1.z_ref, bf16[1024,768]{1,0:T(8,128)(2,1)} %copy-done.39, bf16[1024,768]{1,0:T(8,128)(2,1)} %copy-done.37, bf16[1024,768]{1,0:T(8,128)(2,1)} %copy-done.38, bf16[1024,768]{1,0:T(8,128)(2,1)} %copy-done.36, bf16[512,768]{1,0:T(8,128)(2,1)S(1)} %pad_maximum_fusion.6.refs_4_, ...), custom_call_target="tpu_custom_call" | custom-call | flops 12884901888 | bytes 27262976 | tf_op jit(solution)/shard_map/normed_back/pallas_call | solution.py:387
  508.4 12.1 %collective-permute-done.52 = bf16[1024,768]{1,0:T(8,128)(2,1)} collective-permute-done((bf16[1024,768]{1,0:T(8,128)(2,1)}, bf16[1024,768]{1,0:T(8,128)(2,1)}, u32[]{:S(2)}, u32[]{:S(2)}) %collective-permute-start.52) | collective-permute-done | bytes 1572896 | tf_op jit(solution)/shard_map/ppermute | solution.py:33
  520.6 3.8 slice.325
  524.4 3.1 add_convert_fusion.3
  538.8 22.6 %collective-permute-done.58 = bf16[128,2048]{1,0:T(8,128)(2,1)S(1)} collective-permute-done((bf16[128,2048]{1,0:T(8,128)(2,1)S(1)}, bf16[128,2048]{1,0:T(8,128)(2,1)S(1)}, u32[]{:S(2)}, u32[]{:S(2)}) %collective-permute-start.58) | collective-permute-done | bytes 524320 | tf_op jit(solution)/shard_map/ppermute | solution.py:33
  565.7 4.8 fusion.9
  570.5 4.9 fusion.6
  577.7 5.8 collective-permute-done.63
  589.6 24.2 %collective-permute-done.65 = bf16[128,2048]{1,0:T(8,128)(2,1)S(1)} collective-permute-done((bf16[128,2048]{1,0:T(8,128)(2,1)S(1)}, bf16[128,2048]{1,0:T(8,128)(2,1)S(1)}, u32[]{:S(2)}, u32[]{:S(2)}) %collective-permute-start.65) | collective-permute-done | bytes 524320 | tf_op jit(solution)/shard_map/ppermute | solution.py:33
  617.4 2.2 add_convert_fusion.8
  630.4 5.0 place_turned.2
  635.3 12.5 %collective-permute-done.75 = f32[2,2048]{1,0:T(2,128)S(1)} collective-permute-done((f32[2,2048]{1,0:T(2,128)S(1)}, f32[2,2048]{1,0:T(2,128)S(1)}, u32[]{:S(2)}, u32[]{:S(2)}) %collective-permute-start.75) | collective-permute-done | bytes 16416 | tf_op jit(solution)/shard_map/ppermute | solution.py:33
  655.4 2.1 add_convert_fusion
  664.8 9.3 %collective-permute-done.81 = f32[2,2048]{1,0:T(2,128)S(1)} collective-permute-done((f32[2,2048]{1,0:T(2,128)S(1)}, f32[2,2048]{1,0:T(2,128)S(1)}, u32[]{:S(2)}, u32[]{:S(2)}) %collective-permute-start.81) | collective-permute-done | bytes 16416 | tf_op jit(solution)/shard_map/ppermute | solution.py:33
  676.5 2.1 constant_dynamic-update-slice_fusion.57
  679.0 6.9 collective-permute-done.80
  694.4 2.4 collective-permute-start.86
  702.5 5.0 place_turned.3
  708.8 11.0 %place.2 = (f32[512,2048]{1,0:T(8,128)}, f32[512,2048]{1,0:T(8,128)}, f32[512,2048]{1,0:T(8,128)}) custom-call(s32[1]{0:T(128)} %bitcast.6.me_ref, bf16[2048,768]{1,0:T(8,128)(2,1)} %constant_dynamic-update-slice_fusion.55.same_ref, bf16[2048,768]{1,0:T(8,128)(2,1)} %collective-permute-done.82.other_ref), custom_call_target="tpu_custom_call" | custom-call | bytes 25165824 | tf_op jit(solution)/shard_map/place/pallas_call | solution.py:442
  721.3 6.4 place.3
  727.8 8.9 %convert_element_type.342 = f32[5632,512]{1,0:T(8,128)} convert(bf16[5632,512]{1,0:T(8,128)(2,1)} %all-gather.11.cloned.1.call-done) | non-fusion elementwise | flops 2883584 | bytes 17301504 | tf_op jit(solution)/shard_map/convert_element_type | solution.py:688
  (503 shorter events, 214.1 us)
Async XLA Ops:
  7.2 121.5 %all-gather.5.cloned.1.call-start = ((), (), s32[]{:S(2)}) async-start(), calls=%async_computation.5 | async-start | bytes 1310720 | tf_op jit(solution)/shard_map/all_gather | solution.py:559
  8.8 18.3 %collective-permute-start = (bf16[2,512]{1,0:T(2,128)(2,1)S(1)}, bf16[2,512]{1,0:T(2,128)(2,1)S(1)}, u32[]{:S(2)}, u32[]{:S(2)}) collective-permute-start(bf16[2,512]{1,0:T(2,128)(2,1)S(1)} %get-tuple-element.328), channel_id=1, source_target_pairs={{0,3},{1,0},{2,1},{3,2},{4,7},{5,4},{6,5},{7,6},{8,11},{9,8},{10,9... | collective-permute-start | bytes 6152 | tf_op jit(solution)/shard_map/ppermute | solution.py:172
  19.6 20.4 %collective-permute-start.3 = (bf16[512,768]{1,0:T(8,128)(2,1)S(1)}, bf16[512,768]{1,0:T(8,128)(2,1)}, u32[]{:S(2)}, u32[]{:S(2)}) collective-permute-start(bf16[512,768]{1,0:T(8,128)(2,1)S(1)} %pad_maximum_fusion.6.refs_4_), channel_id=1, source_target_pairs={{0,1},{1,2},{2,3},{3,0},{4,5},{5,6},{6,7},{7,4},{8,9},{9,10},{10,1... | collective-permute-start | bytes 2359304 | tf_op jit(solution)/shard_map/ppermute | solution.py:541
  42.3 24.6 %collective-permute-start.8 = (bf16[512,2048]{1,0:T(8,128)(2,1)S(1)}, bf16[512,2048]{1,0:T(8,128)(2,1)S(1)}, u32[]{:S(2)}, u32[]{:S(2)}) collective-permute-start(bf16[512,2048]{1,0:T(8,128)(2,1)S(1)} %fusion.2), channel_id=1, source_target_pairs={{0,4},{4,0},{8,12},{12,8},{16,20},{20,16},{24,28},{28,24},{1,5},{5... | collective-permute-start | bytes 6291464 | tf_op jit(solution)/shard_map/ppermute | solution.py:33
  42.4 20.2 %collective-permute-start.5 = (bf16[512,768]{1,0:T(8,128)(2,1)}, bf16[512,768]{1,0:T(8,128)(2,1)S(1)}, u32[]{:S(2)}, u32[]{:S(2)}) collective-permute-start(bf16[512,768]{1,0:T(8,128)(2,1)} %collective-permute-done.3.refs_5_), channel_id=1, source_target_pairs={{0,8},{4,12},{8,0},{12,4},{16,24},{20,28},{24,16},{28,20},{1,9},{5... | collective-permute-start | bytes 2359304 | tf_op jit(solution)/shard_map/ppermute | solution.py:33
  43.9 19.8 %collective-permute-start.6 = (bf16[512,768]{1,0:T(8,128)(2,1)}, bf16[512,768]{1,0:T(8,128)(2,1)S(1)}, u32[]{:S(2)}, u32[]{:S(2)}) collective-permute-start(bf16[512,768]{1,0:T(8,128)(2,1)} %collective-permute-done.3.refs_5_), channel_id=1, source_target_pairs={{0,16},{4,20},{8,24},{12,28},{16,0},{20,4},{24,8},{28,12},{1,17},{... | collective-permute-start | bytes 2359304 | tf_op jit(solution)/shard_map/ppermute | solution.py:33
  45.4 21.4 %collective-permute-start.7 = (bf16[512,768]{1,0:T(8,128)(2,1)}, bf16[512,768]{1,0:T(8,128)(2,1)}, u32[]{:S(2)}, u32[]{:S(2)}) collective-permute-start(bf16[512,768]{1,0:T(8,128)(2,1)} %collective-permute-done.3.refs_5_), channel_id=1, source_target_pairs={{0,1},{1,2},{2,3},{3,0},{4,5},{5,6},{6,7},{7,4},{8,9},{9,10},{10,1... | collective-permute-start | bytes 2359304 | tf_op jit(solution)/shard_map/ppermute | solution.py:555
  66.9 27.5 %collective-permute-start.11 = (bf16[512,768]{1,0:T(8,128)(2,1)}, bf16[512,768]{1,0:T(8,128)(2,1)}, u32[]{:S(2)}, u32[]{:S(2)}) collective-permute-start(bf16[512,768]{1,0:T(8,128)(2,1)} %collective-permute-done.7.refs_6_), channel_id=1, source_target_pairs={{0,8},{4,12},{8,0},{12,4},{16,24},{20,28},{24,16},{28,20},{1,9},{5... | collective-permute-start | bytes 2359304 | tf_op jit(solution)/shard_map/ppermute | solution.py:33
  67.4 26.9 %collective-permute-start.12 = (bf16[512,768]{1,0:T(8,128)(2,1)}, bf16[512,768]{1,0:T(8,128)(2,1)}, u32[]{:S(2)}, u32[]{:S(2)}) collective-permute-start(bf16[512,768]{1,0:T(8,128)(2,1)} %collective-permute-done.7.refs_6_), channel_id=1, source_target_pairs={{0,16},{4,20},{8,24},{12,28},{16,0},{20,4},{24,8},{28,12},{1,17},{... | collective-permute-start | bytes 2359304 | tf_op jit(solution)/shard_map/ppermute | solution.py:33
  67.9 26.4 %collective-permute-start.13 = (bf16[512,768]{1,0:T(8,128)(2,1)}, bf16[512,768]{1,0:T(8,128)(2,1)}, u32[]{:S(2)}, u32[]{:S(2)}) collective-permute-start(bf16[512,768]{1,0:T(8,128)(2,1)} %collective-permute-done.7.refs_6_), channel_id=1, source_target_pairs={{0,1},{1,2},{2,3},{3,0},{4,5},{5,6},{6,7},{7,4},{8,9},{9,10},{10,1... | collective-permute-start | bytes 2359304 | tf_op jit(solution)/shard_map/ppermute | solution.py:555
  69.6 24.7 %collective-permute-start.9 = (bf16[256,768]{1,0:T(8,128)(2,1)}, bf16[256,768]{1,0:T(8,128)(2,1)}, u32[]{:S(2)}, u32[]{:S(2)}) collective-permute-start(bf16[256,768]{1,0:T(8,128)(2,1)} %slice.206), channel_id=1, source_target_pairs={{0,16},{4,20},{8,24},{12,28},{16,0},{20,4},{24,8},{28,12},{1,17},{... | collective-permute-start | bytes 1179656 | tf_op jit(solution)/shard_map/ppermute | solution.py:33
  71.9 22.4 %collective-permute-start.10 = (bf16[256,768]{1,0:T(8,128)(2,1)}, bf16[256,768]{1,0:T(8,128)(2,1)}, u32[]{:S(2)}, u32[]{:S(2)}) collective-permute-start(bf16[256,768]{1,0:T(8,128)(2,1)} %slice.207), channel_id=1, source_target_pairs={{0,8},{4,12},{8,0},{12,4},{16,24},{20,28},{24,16},{28,20},{1,9},{5... | collective-permute-start | bytes 1179656 | tf_op jit(solution)/shard_map/ppermute | solution.py:33
  94.4 137.5 %all-gather.7.cloned.1.call-start = ((), (), s32[]{:S(2)}) async-start(), calls=%async_computation.6 | async-start | bytes 7208960 | tf_op jit(solution)/shard_map/all_gather | solution.py:568
  100.8 27.9 %collective-permute-start.16 = (bf16[512,768]{1,0:T(8,128)(2,1)}, bf16[512,768]{1,0:T(8,128)(2,1)}, u32[]{:S(2)}, u32[]{:S(2)}) collective-permute-start(bf16[512,768]{1,0:T(8,128)(2,1)} %collective-permute-done.13.refs_7_), channel_id=1, source_target_pairs={{0,8},{4,12},{8,0},{12,4},{16,24},{20,28},{24,16},{28,20},{1,9},{5... | collective-permute-start | bytes 2359304 | tf_op jit(solution)/shard_map/ppermute | solution.py:33
  102.4 26.4 %collective-permute-start.17 = (bf16[512,768]{1,0:T(8,128)(2,1)}, bf16[512,768]{1,0:T(8,128)(2,1)}, u32[]{:S(2)}, u32[]{:S(2)}) collective-permute-start(bf16[512,768]{1,0:T(8,128)(2,1)} %collective-permute-done.13.refs_7_), channel_id=1, source_target_pairs={{0,16},{4,20},{8,24},{12,28},{16,0},{20,4},{24,8},{28,12},{1,17},{... | collective-permute-start | bytes 2359304 | tf_op jit(solution)/shard_map/ppermute | solution.py:33
  104.1 23.8 %collective-permute-start.14 = (bf16[256,768]{1,0:T(8,128)(2,1)S(1)}, bf16[256,768]{1,0:T(8,128)(2,1)S(1)}, u32[]{:S(2)}, u32[]{:S(2)}) collective-permute-start(bf16[256,768]{1,0:T(8,128)(2,1)S(1)} %slice.208), channel_id=1, source_target_pairs={{0,16},{4,20},{8,24},{12,28},{16,0},{20,4},{24,8},{28,12},{1,17},{... | collective-permute-start | bytes 1179656 | tf_op jit(solution)/shard_map/ppermute | solution.py:33
  106.7 22.0 %collective-permute-start.15 = (bf16[256,768]{1,0:T(8,128)(2,1)S(1)}, bf16[256,768]{1,0:T(8,128)(2,1)}, u32[]{:S(2)}, u32[]{:S(2)}) collective-permute-start(bf16[256,768]{1,0:T(8,128)(2,1)S(1)} %slice.209), channel_id=1, source_target_pairs={{0,8},{4,12},{8,0},{12,4},{16,24},{20,28},{24,16},{28,20},{1,9},{5... | collective-permute-start | bytes 1179656 | tf_op jit(solution)/shard_map/ppermute | solution.py:33
  128.8 166.5 %all-gather.9.cloned.1.call-start = ((), (), s32[]{:S(2)}) async-start(), calls=%async_computation.7 | async-start | bytes 3604480 | tf_op jit(solution)/shard_map/all_gather | solution.py:570
  131.4 46.1 %collective-permute-start.20 = (bf16[256,2048]{1,0:T(8,128)(2,1)}, bf16[256,2048]{1,0:T(8,128)(2,1)S(1)}, u32[]{:S(2)}, u32[]{:S(2)}) collective-permute-start(bf16[256,2048]{1,0:T(8,128)(2,1)} %all-gather.5.cloned.1.call-done.out_ref), channel_id=1, source_target_pairs={{0,8},{4,12},{8,0},{12,4},{16,24},{20,28},{24,16},{28,20},{1,9},{5... | collective-permute-start | bytes 3145736 | tf_op jit(solution)/shard_map/ppermute | solution.py:33
  132.1 45.5 %collective-permute-start.21 = (bf16[256,2048]{1,0:T(8,128)(2,1)}, bf16[256,2048]{1,0:T(8,128)(2,1)S(1)}, u32[]{:S(2)}, u32[]{:S(2)}) collective-permute-start(bf16[256,2048]{1,0:T(8,128)(2,1)} %all-gather.5.cloned.1.call-done.out_ref), channel_id=1, source_target_pairs={{0,16},{4,20},{8,24},{12,28},{16,0},{20,4},{24,8},{28,12},{1,17},{... | collective-permute-start | bytes 3145736 | tf_op jit(solution)/shard_map/ppermute | solution.py:33
  133.6 33.9 %collective-permute-start.18 = (bf16[256,768]{1,0:T(8,128)(2,1)S(1)}, bf16[256,768]{1,0:T(8,128)(2,1)S(1)}, u32[]{:S(2)}, u32[]{:S(2)}) collective-permute-start(bf16[256,768]{1,0:T(8,128)(2,1)S(1)} %slice.210), channel_id=1, source_target_pairs={{0,16},{4,20},{8,24},{12,28},{16,0},{20,4},{24,8},{28,12},{1,17},{... | collective-permute-start | bytes 1179656 | tf_op jit(solution)/shard_map/ppermute | solution.py:33
  136.3 31.2 %collective-permute-start.19 = (bf16[256,768]{1,0:T(8,128)(2,1)S(1)}, bf16[256,768]{1,0:T(8,128)(2,1)S(1)}, u32[]{:S(2)}, u32[]{:S(2)}) collective-permute-start(bf16[256,768]{1,0:T(8,128)(2,1)S(1)} %slice.211), channel_id=1, source_target_pairs={{0,8},{4,12},{8,0},{12,4},{16,24},{20,28},{24,16},{28,20},{1,9},{5... | collective-permute-start | bytes 1179656 | tf_op jit(solution)/shard_map/ppermute | solution.py:33
  235.5 17.9 %collective-permute-start.29 = (bf16[512,2048]{1,0:T(8,128)(2,1)}, bf16[512,2048]{1,0:T(8,128)(2,1)}, u32[]{:S(2)}, u32[]{:S(2)}) collective-permute-start(bf16[512,2048]{1,0:T(8,128)(2,1)} %get-tuple-element.381), channel_id=1, source_target_pairs={{0,4},{4,0},{8,12},{12,8},{16,20},{20,16},{24,28},{28,24},{1,5},{5... | collective-permute-start | bytes 6291464 | tf_op jit(solution)/shard_map/ppermute | solution.py:33
  237.6 282.9 %reduce-scatter.6.cloned.1.call-start = ((), (), s32[]{:S(2)}) async-start(), calls=%async_computation.8 | async-start | bytes 3604480 | tf_op jit(solution)/shard_map/reduce_scatter | solution.py:619
  324.4 196.2 %reduce-scatter.8.cloned.1.call-start = ((), (), s32[]{:S(2)}) async-start(), calls=%async_computation.9 | async-start | bytes 3604480 | tf_op jit(solution)/shard_map/reduce_scatter | solution.py:619
  333.5 15.3 %collective-permute-start.38 = (bf16[512,2048]{1,0:T(8,128)(2,1)}, bf16[512,2048]{1,0:T(8,128)(2,1)}, u32[]{:S(2)}, u32[]{:S(2)}) collective-permute-start(bf16[512,2048]{1,0:T(8,128)(2,1)} %slice.271), channel_id=1, source_target_pairs={{0,4},{4,0},{8,12},{12,8},{16,20},{20,16},{24,28},{28,24},{1,5},{5... | collective-permute-start | bytes 6291464 | tf_op jit(solution)/shard_map/ppermute | solution.py:33
  355.8 16.8 %collective-permute-start.42 = (bf16[64,2048]{1,0:T(8,128)(2,1)}, bf16[64,2048]{1,0:T(8,128)(2,1)}, u32[]{:S(2)}, u32[]{:S(2)}) collective-permute-start(bf16[64,2048]{1,0:T(8,128)(2,1)} %get-tuple-element.346), channel_id=1, source_target_pairs={{0,16},{4,20},{8,24},{12,28},{16,0},{20,4},{24,8},{28,12},{1,17},{... | collective-permute-start | bytes 786440 | tf_op jit(solution)/shard_map/ppermute | solution.py:33
  359.9 171.6 %reduce-scatter.10.cloned.1.call-start = ((), (), s32[]{:S(2)}) async-start(), calls=%async_computation.10 | async-start | bytes 3604480 | tf_op jit(solution)/shard_map/reduce_scatter | solution.py:619
  384.3 24.2 %collective-permute-start.43 = (bf16[64,2048]{1,0:T(8,128)(2,1)S(1)}, bf16[64,2048]{1,0:T(8,128)(2,1)S(1)}, u32[]{:S(2)}, u32[]{:S(2)}) collective-permute-start(bf16[64,2048]{1,0:T(8,128)(2,1)S(1)} %get-tuple-element.351), channel_id=1, source_target_pairs={{0,16},{4,20},{8,24},{12,28},{16,0},{20,4},{24,8},{28,12},{1,17},{... | collective-permute-start | bytes 786440 | tf_op jit(solution)/shard_map/ppermute | solution.py:33
  385.9 22.7 %collective-permute-start.44 = (bf16[64,2048]{1,0:T(8,128)(2,1)S(1)}, bf16[64,2048]{1,0:T(8,128)(2,1)S(1)}, u32[]{:S(2)}, u32[]{:S(2)}) collective-permute-start(bf16[64,2048]{1,0:T(8,128)(2,1)S(1)} %get-tuple-element.350), channel_id=1, source_target_pairs={{0,8},{4,12},{8,0},{12,4},{16,24},{20,28},{24,16},{28,20},{1,9},{5... | collective-permute-start | bytes 786440 | tf_op jit(solution)/shard_map/ppermute | solution.py:33
  409.9 41.9 %collective-permute-start.50 = (bf16[1024,768]{1,0:T(8,128)(2,1)}, bf16[1024,768]{1,0:T(8,128)(2,1)}, u32[]{:S(2)}, u32[]{:S(2)}) collective-permute-start(bf16[1024,768]{1,0:T(8,128)(2,1)} %get-tuple-element.228), channel_id=1, source_target_pairs={{0,8},{4,12},{8,0},{12,4},{16,24},{20,28},{24,16},{28,20},{1,9},{5... | collective-permute-start | bytes 4718600 | tf_op jit(solution)/shard_map/ppermute | solution.py:33
  411.1 40.7 %collective-permute-start.51 = (bf16[1024,768]{1,0:T(8,128)(2,1)}, bf16[1024,768]{1,0:T(8,128)(2,1)}, u32[]{:S(2)}, u32[]{:S(2)}) collective-permute-start(bf16[1024,768]{1,0:T(8,128)(2,1)} %get-tuple-element.229), channel_id=1, source_target_pairs={{0,16},{4,20},{8,24},{12,28},{16,0},{20,4},{24,8},{28,12},{1,17},{... | collective-permute-start | bytes 4718600 | tf_op jit(solution)/shard_map/ppermute | solution.py:33
  412.6 204.8 %reduce-scatter.12.cloned.1.call-start = ((), (), s32[]{:S(2)}) async-start(), calls=%async_computation.11 | async-start | bytes 3932160 | tf_op jit(solution)/shard_map/reduce_scatter | solution.py:658
  433.4 54.5 %collective-permute-start.54 = (bf16[1024,768]{1,0:T(8,128)(2,1)S(1)}, bf16[1024,768]{1,0:T(8,128)(2,1)S(1)}, u32[]{:S(2)}, u32[]{:S(2)}) collective-permute-start(bf16[1024,768]{1,0:T(8,128)(2,1)S(1)} %get-tuple-element.233), channel_id=1, source_target_pairs={{0,8},{4,12},{8,0},{12,4},{16,24},{20,28},{24,16},{28,20},{1,9},{5... | collective-permute-start | bytes 4718600 | tf_op jit(solution)/shard_map/ppermute | solution.py:33
  450.9 37.6 %collective-permute-start.55 = (bf16[1024,768]{1,0:T(8,128)(2,1)}, bf16[1024,768]{1,0:T(8,128)(2,1)}, u32[]{:S(2)}, u32[]{:S(2)}) collective-permute-start(bf16[1024,768]{1,0:T(8,128)(2,1)} %get-tuple-element.236), channel_id=1, source_target_pairs={{0,16},{4,20},{8,24},{12,28},{16,0},{20,4},{24,8},{28,12},{1,17},{... | collective-permute-start | bytes 4718600 | tf_op jit(solution)/shard_map/ppermute | solution.py:33
  454.9 65.6 %collective-permute-start.52 = (bf16[1024,768]{1,0:T(8,128)(2,1)}, bf16[1024,768]{1,0:T(8,128)(2,1)}, u32[]{:S(2)}, u32[]{:S(2)}) collective-permute-start(bf16[1024,768]{1,0:T(8,128)(2,1)} %add_convert_fusion.6), channel_id=1, source_target_pairs={{0,16},{4,20},{8,24},{12,28},{16,0},{20,4},{24,8},{28,12},{1,17},{... | collective-permute-start | bytes 4718600 | tf_op jit(solution)/shard_map/ppermute | solution.py:33
  459.2 61.4 %collective-permute-start.53 = (bf16[1024,768]{1,0:T(8,128)(2,1)}, bf16[1024,768]{1,0:T(8,128)(2,1)}, u32[]{:S(2)}, u32[]{:S(2)}) collective-permute-start(bf16[1024,768]{1,0:T(8,128)(2,1)} %add_convert_fusion.5), channel_id=1, source_target_pairs={{0,8},{4,12},{8,0},{12,4},{16,24},{20,28},{24,16},{28,20},{1,9},{5... | collective-permute-start | bytes 4718600 | tf_op jit(solution)/shard_map/ppermute | solution.py:33
  524.4 39.1 %collective-permute-start.62 = (bf16[512,2048]{1,0:T(8,128)(2,1)}, bf16[512,2048]{1,0:T(8,128)(2,1)}, u32[]{:S(2)}, u32[]{:S(2)}) collective-permute-start(bf16[512,2048]{1,0:T(8,128)(2,1)} %slice.325), channel_id=1, source_target_pairs={{0,4},{4,0},{8,12},{12,8},{16,20},{20,16},{24,28},{28,24},{1,5},{5... | collective-permute-start | bytes 6291464 | tf_op jit(solution)/shard_map/ppermute | solution.py:33
  531.6 117.1 %reduce-scatter.14.cloned.1.call-start = ((), (), s32[]{:S(2)}) async-start(), calls=%async_computation.12 | async-start | bytes 1310720 | tf_op jit(solution)/shard_map/reduce_scatter | solution.py:674
  531.7 31.8 %collective-permute-start.60 = (bf16[704,512]{1,0:T(8,128)(2,1)}, bf16[704,512]{1,0:T(8,128)(2,1)S(1)}, u32[]{:S(2)}, u32[]{:S(2)}) collective-permute-start(bf16[704,512]{1,0:T(8,128)(2,1)} %reduce-scatter.6.cloned.1.call-done), channel_id=1, source_target_pairs={{0,8},{4,12},{8,0},{12,4},{16,24},{20,28},{24,16},{28,20},{1,9},{5... | collective-permute-start | bytes 2162696 | tf_op jit(solution)/shard_map/ppermute | solution.py:33
  533.2 30.2 %collective-permute-start.61 = (bf16[704,512]{1,0:T(8,128)(2,1)}, bf16[704,512]{1,0:T(8,128)(2,1)S(1)}, u32[]{:S(2)}, u32[]{:S(2)}) collective-permute-start(bf16[704,512]{1,0:T(8,128)(2,1)} %reduce-scatter.6.cloned.1.call-done), channel_id=1, source_target_pairs={{0,16},{4,20},{8,24},{12,28},{16,0},{20,4},{24,8},{28,12},{1,17},{... | collective-permute-start | bytes 2162696 | tf_op jit(solution)/shard_map/ppermute | solution.py:33
  535.6 25.8 %collective-permute-start.58 = (bf16[128,2048]{1,0:T(8,128)(2,1)S(1)}, bf16[128,2048]{1,0:T(8,128)(2,1)S(1)}, u32[]{:S(2)}, u32[]{:S(2)}) collective-permute-start(bf16[128,2048]{1,0:T(8,128)(2,1)S(1)} %get-tuple-element.337), channel_id=1, source_target_pairs={{0,8},{4,12},{8,0},{12,4},{16,24},{20,28},{24,16},{28,20},{1,9},{5... | collective-permute-start | bytes 1572872 | tf_op jit(solution)/shard_map/ppermute | solution.py:33
  536.2 26.6 %collective-permute-start.59 = (bf16[128,2048]{1,0:T(8,128)(2,1)S(1)}, bf16[128,2048]{1,0:T(8,128)(2,1)S(1)}, u32[]{:S(2)}, u32[]{:S(2)}) collective-permute-start(bf16[128,2048]{1,0:T(8,128)(2,1)S(1)} %get-tuple-element.336), channel_id=1, source_target_pairs={{0,16},{4,20},{8,24},{12,28},{16,0},{20,4},{24,8},{28,12},{1,17},{... | collective-permute-start | bytes 1572872 | tf_op jit(solution)/shard_map/ppermute | solution.py:33
  561.4 14.9 %collective-permute-start.56 = (bf16[128,2048]{1,0:T(8,128)(2,1)S(1)}, bf16[128,2048]{1,0:T(8,128)(2,1)S(1)}, u32[]{:S(2)}, u32[]{:S(2)}) collective-permute-start(bf16[128,2048]{1,0:T(8,128)(2,1)S(1)} %get-tuple-element.339), channel_id=1, source_target_pairs={{0,8},{4,12},{8,0},{12,4},{16,24},{20,28},{24,16},{28,20},{1,9},{5... | collective-permute-start | bytes 1572872 | tf_op jit(solution)/shard_map/ppermute | solution.py:33
  563.5 20.1 %collective-permute-start.63 = (bf16[352,512]{1,0:T(8,128)(2,1)S(1)}, bf16[352,512]{1,0:T(8,128)(2,1)S(1)}, u32[]{:S(2)}, u32[]{:S(2)}) collective-permute-start(bf16[352,512]{1,0:T(8,128)(2,1)S(1)} %slice.245), channel_id=1, source_target_pairs={{0,16},{4,20},{8,24},{12,28},{16,0},{20,4},{24,8},{28,12},{1,17},{... | collective-permute-start | bytes 1081352 | tf_op jit(solution)/shard_map/ppermute | solution.py:33
  565.0 18.5 %collective-permute-start.64 = (bf16[352,512]{1,0:T(8,128)(2,1)S(1)}, bf16[352,512]{1,0:T(8,128)(2,1)S(1)}, u32[]{:S(2)}, u32[]{:S(2)}) collective-permute-start(bf16[352,512]{1,0:T(8,128)(2,1)S(1)} %slice.246), channel_id=1, source_target_pairs={{0,8},{4,12},{8,0},{12,4},{16,24},{20,28},{24,16},{28,20},{1,9},{5... | collective-permute-start | bytes 1081352 | tf_op jit(solution)/shard_map/ppermute | solution.py:33
  583.6 32.2 %collective-permute-start.67 = (bf16[2816,512]{1,0:T(8,128)(2,1)S(1)}, bf16[2816,512]{1,0:T(8,128)(2,1)S(1)}, u32[]{:S(2)}, u32[]{:S(2)}) collective-permute-start(bf16[2816,512]{1,0:T(8,128)(2,1)S(1)} %constant_dynamic-update-slice_fusion.45.same_ref), channel_id=1, source_target_pairs={{0,4},{4,0},{8,12},{12,8},{16,20},{20,16},{24,28},{28,24},{1,5},{5... | collective-permute-start | bytes 8650760 | tf_op jit(solution)/shard_map/ppermute | solution.py:33
  583.7 30.1 %collective-permute-start.68 = (bf16[704,512]{1,0:T(8,128)(2,1)S(1)}, bf16[704,512]{1,0:T(8,128)(2,1)S(1)}, u32[]{:S(2)}, u32[]{:S(2)}) collective-permute-start(bf16[704,512]{1,0:T(8,128)(2,1)S(1)} %copy-done.68), channel_id=1, source_target_pairs={{0,8},{4,12},{8,0},{12,4},{16,24},{20,28},{24,16},{28,20},{1,9},{5... | collective-permute-start | bytes 2162696 | tf_op jit(solution)/shard_map/ppermute | solution.py:33
  584.3 30.4 %collective-permute-start.69 = (bf16[704,512]{1,0:T(8,128)(2,1)S(1)}, bf16[704,512]{1,0:T(8,128)(2,1)S(1)}, u32[]{:S(2)}, u32[]{:S(2)}) collective-permute-start(bf16[704,512]{1,0:T(8,128)(2,1)S(1)} %copy-done.68), channel_id=1, source_target_pairs={{0,16},{4,20},{8,24},{12,28},{16,0},{20,4},{24,8},{28,12},{1,17},{... | collective-permute-start | bytes 2162696 | tf_op jit(solution)/shard_map/ppermute | solution.py:33
  586.6 27.2 %collective-permute-start.65 = (bf16[128,2048]{1,0:T(8,128)(2,1)S(1)}, bf16[128,2048]{1,0:T(8,128)(2,1)S(1)}, u32[]{:S(2)}, u32[]{:S(2)}) collective-permute-start(bf16[128,2048]{1,0:T(8,128)(2,1)S(1)} %get-tuple-element.335), channel_id=1, source_target_pairs={{0,16},{4,20},{8,24},{12,28},{16,0},{20,4},{24,8},{28,12},{1,17},{... | collective-permute-start | bytes 1572872 | tf_op jit(solution)/shard_map/ppermute | solution.py:33
  589.0 24.8 %collective-permute-start.66 = (bf16[128,2048]{1,0:T(8,128)(2,1)S(1)}, bf16[128,2048]{1,0:T(8,128)(2,1)S(1)}, u32[]{:S(2)}, u32[]{:S(2)}) collective-permute-start(bf16[128,2048]{1,0:T(8,128)(2,1)S(1)} %get-tuple-element.334), channel_id=1, source_target_pairs={{0,8},{4,12},{8,0},{12,4},{16,24},{20,28},{24,16},{28,20},{1,9},{5... | collective-permute-start | bytes 1572872 | tf_op jit(solution)/shard_map/ppermute | solution.py:33
  620.7 107.1 %all-gather.11.cloned.1.call-start = ((), (), s32[]{:S(2)}) async-start(), calls=%async_computation.13 | async-start | bytes 6488064 | tf_op jit(solution)/shard_map/all_gather | solution.py:679
  620.7 28.0 %collective-permute-start.73 = (bf16[512,768]{1,0:T(8,128)(2,1)}, bf16[512,768]{1,0:T(8,128)(2,1)}, u32[]{:S(2)}, u32[]{:S(2)}) collective-permute-start(bf16[512,768]{1,0:T(8,128)(2,1)} %reduce-scatter.12.cloned.1.call-done), channel_id=1, source_target_pairs={{0,8},{4,12},{8,0},{12,4},{16,24},{20,28},{24,16},{28,20},{1,9},{5... | collective-permute-start | bytes 2359304 | tf_op jit(solution)/shard_map/ppermute | solution.py:33
  622.3 26.4 %collective-permute-start.74 = (bf16[512,768]{1,0:T(8,128)(2,1)}, bf16[512,768]{1,0:T(8,128)(2,1)}, u32[]{:S(2)}, u32[]{:S(2)}) collective-permute-start(bf16[512,768]{1,0:T(8,128)(2,1)} %reduce-scatter.12.cloned.1.call-done), channel_id=1, source_target_pairs={{0,16},{4,20},{8,24},{12,28},{16,0},{20,4},{24,8},{28,12},{1,17},{... | collective-permute-start | bytes 2359304 | tf_op jit(solution)/shard_map/ppermute | solution.py:33
  623.9 24.8 %collective-permute-start.71 = (bf16[352,512]{1,0:T(8,128)(2,1)S(1)}, bf16[352,512]{1,0:T(8,128)(2,1)S(1)}, u32[]{:S(2)}, u32[]{:S(2)}) collective-permute-start(bf16[352,512]{1,0:T(8,128)(2,1)S(1)} %slice.250), channel_id=1, source_target_pairs={{0,16},{4,20},{8,24},{12,28},{16,0},{20,4},{24,8},{28,12},{1,17},{... | collective-permute-start | bytes 1081352 | tf_op jit(solution)/shard_map/ppermute | solution.py:33
  626.4 22.3 %collective-permute-start.72 = (bf16[352,512]{1,0:T(8,128)(2,1)S(1)}, bf16[352,512]{1,0:T(8,128)(2,1)}, u32[]{:S(2)}, u32[]{:S(2)}) collective-permute-start(bf16[352,512]{1,0:T(8,128)(2,1)S(1)} %slice.251), channel_id=1, source_target_pairs={{0,8},{4,12},{8,0},{12,4},{16,24},{20,28},{24,16},{28,20},{1,9},{5... | collective-permute-start | bytes 1081352 | tf_op jit(solution)/shard_map/ppermute | solution.py:33
  627.0 20.8 %collective-permute-start.75 = (f32[2,2048]{1,0:T(2,128)S(1)}, f32[2,2048]{1,0:T(2,128)S(1)}, u32[]{:S(2)}, u32[]{:S(2)}) collective-permute-start(f32[2,2048]{1,0:T(2,128)S(1)} %add.252), channel_id=1, source_target_pairs={{0,8},{4,12},{8,0},{12,4},{16,24},{20,28},{24,16},{28,20},{1,9},{5... | collective-permute-start | bytes 49160 | tf_op jit(solution)/shard_map/ppermute | solution.py:33
  653.6 32.3 %collective-permute-start.76 = (bf16[2816,512]{1,0:T(8,128)(2,1)S(1)}, bf16[2816,512]{1,0:T(8,128)(2,1)S(1)}, u32[]{:S(2)}, u32[]{:S(2)}) collective-permute-start(bf16[2816,512]{1,0:T(8,128)(2,1)S(1)} %constant_dynamic-update-slice_fusion.50.same_ref), channel_id=1, source_target_pairs={{0,4},{4,0},{8,12},{12,8},{16,20},{20,16},{24,28},{28,24},{1,5},{5... | collective-permute-start | bytes 8650760 | tf_op jit(solution)/shard_map/ppermute | solution.py:33
  658.6 27.3 %collective-permute-start.77 = (bf16[256,768]{1,0:T(8,128)(2,1)S(1)}, bf16[256,768]{1,0:T(8,128)(2,1)S(1)}, u32[]{:S(2)}, u32[]{:S(2)}) collective-permute-start(bf16[256,768]{1,0:T(8,128)(2,1)S(1)} %slice.254), channel_id=1, source_target_pairs={{0,16},{4,20},{8,24},{12,28},{16,0},{20,4},{24,8},{28,12},{1,17},{... | collective-permute-start | bytes 1179656 | tf_op jit(solution)/shard_map/ppermute | solution.py:33
  660.2 25.7 %collective-permute-start.78 = (bf16[256,768]{1,0:T(8,128)(2,1)S(1)}, bf16[256,768]{1,0:T(8,128)(2,1)S(1)}, u32[]{:S(2)}, u32[]{:S(2)}) collective-permute-start(bf16[256,768]{1,0:T(8,128)(2,1)S(1)} %slice.255), channel_id=1, source_target_pairs={{0,8},{4,12},{8,0},{12,4},{16,24},{20,28},{24,16},{28,20},{1,9},{5... | collective-permute-start | bytes 1179656 | tf_op jit(solution)/shard_map/ppermute | solution.py:33
  663.4 15.7 %collective-permute-start.79 = (bf16[256,512]{1,0:T(8,128)(2,1)S(1)}, bf16[256,512]{1,0:T(8,128)(2,1)S(1)}, u32[]{:S(2)}, u32[]{:S(2)}) collective-permute-start(bf16[256,512]{1,0:T(8,128)(2,1)S(1)} %copy-done.73), channel_id=1, source_target_pairs={{0,8},{4,12},{8,0},{12,4},{16,24},{20,28},{24,16},{28,20},{1,9},{5... | collective-permute-start | bytes 786440 | tf_op jit(solution)/shard_map/ppermute | solution.py:33
  689.1 18.4 %collective-permute-start.82 = (bf16[2048,768]{1,0:T(8,128)(2,1)}, bf16[2048,768]{1,0:T(8,128)(2,1)}, u32[]{:S(2)}, u32[]{:S(2)}) collective-permute-start(bf16[2048,768]{1,0:T(8,128)(2,1)} %constant_dynamic-update-slice_fusion.55.same_ref), channel_id=1, source_target_pairs={{0,4},{4,0},{8,12},{12,8},{16,20},{20,16},{24,28},{28,24},{1,5},{5... | collective-permute-start | bytes 9437192 | tf_op jit(solution)/shard_map/ppermute | solution.py:33
  690.8 16.7 %collective-permute-start.83 = (bf16[128,512]{1,0:T(8,128)(2,1)S(1)}, bf16[128,512]{1,0:T(8,128)(2,1)S(1)}, u32[]{:S(2)}, u32[]{:S(2)}) collective-permute-start(bf16[128,512]{1,0:T(8,128)(2,1)S(1)} %slice.258), channel_id=1, source_target_pairs={{0,16},{4,20},{8,24},{12,28},{16,0},{20,4},{24,8},{28,12},{1,17},{... | collective-permute-start | bytes 393224 | tf_op jit(solution)/shard_map/ppermute | solution.py:33
  691.2 16.3 %collective-permute-start.84 = (bf16[128,512]{1,0:T(8,128)(2,1)S(1)}, bf16[128,512]{1,0:T(8,128)(2,1)S(1)}, u32[]{:S(2)}, u32[]{:S(2)}) collective-permute-start(bf16[128,512]{1,0:T(8,128)(2,1)S(1)} %slice.259), channel_id=1, source_target_pairs={{0,8},{4,12},{8,0},{12,4},{16,24},{20,28},{24,16},{28,20},{1,9},{5... | collective-permute-start | bytes 393224 | tf_op jit(solution)/shard_map/ppermute | solution.py:33
  (131 other events, 1123.7 us)
Sparse Core Ops, SparseCore 0:
  94.5 25.1 all-gather.4
  128.9 103.0 all-gather.6
  237.7 57.5 all-gather.8
  324.5 54.9 reduce-scatter.5
  381.6 56.0 reduce-scatter.7
  439.8 56.0 reduce-scatter.9
  531.7 58.5 reduce-scatter.11
  620.8 25.3 reduce-scatter.13
  648.9 53.4 all-gather.10

commit v7 on v6

--- a/solution.py
+++ b/solution.py
@@ -102,8 +102,19 @@
     return blocks
 
 
-def copies_steps(value):
-    blocks = yield from gather_steps(value)
+def jump(value, offset):
+    size = lax.axis_size("rep")
+    return lax.ppermute(value, "rep", [(i, i ^ offset) for i in range(size)])
+
+
+def straight_steps(value):
+    away = [d for d in chip_offsets() if d]
+    new = yield [jump(value, d) for d in away]
+    return dict(zip([0, *away], [value, *new]))
+
+
+def copies_steps(value, gather=gather_steps):
+    blocks = yield from gather(value)
     same = jnp.concatenate([blocks[d] for d in chip_offsets()], axis=0)
     (other,) = yield [swap(same, 1)]
     return same, other
@@ -144,8 +155,9 @@
     same = add(partial[:half], other).astype(BF)
     offsets = chip_offsets()
     rows = half // len(offsets)
-    blocks = {d: halves(same[i * rows : (i + 1) * rows]) for i, d in enumerate(offsets)}
-    return (yield from scatter_steps(blocks))
+    blocks = {d: same[i * rows : (i + 1) * rows] for i, d in enumerate(offsets)}
+    new = yield [jump(blocks[d], d) for d in offsets if d]
+    return sum((n.astype(F32) for n in new), blocks[0].astype(F32)).astype(BF)
 
 
 def vector_sum_steps(rows):
@@ -369,20 +381,29 @@
 
 
 def normed_back_kernel(blocks, parts, z_ref, *refs):
-    lins, weights, total_ref = refs[:blocks], refs[blocks:-1], refs[-1]
-    piece = total_ref.shape[1] // parts
+    lins, weights, (own_ref, other_ref) = refs[:blocks], refs[blocks:-2], refs[-2:]
+    piece = own_ref.shape[1] // parts
+    own = pl.program_id(0) < pl.num_programs(0) // 2
     for k in range(parts):
         total = mm_nt(lins[0][...], weights[k][...])
         for n in range(1, blocks):
             total += mm_nt(lins[n][...], weights[n * parts + k][...])
         at = pl.multiple_of(((z_ref[0] + parts - k) % parts) * piece, piece)
-        total_ref[:, pl.ds(at, piece)] = total
+
+        @pl.when(own)
+        def _():
+            own_ref[:, pl.ds(at, piece)] = total
+
+        @pl.when(jnp.logical_not(own))
+        def _():
+            other_ref[:, pl.ds(at, piece)] = total.astype(BF)
 
 
 def normed_back(shard, lins, weights, depth):
     parts = len(weights[0])
     rows, wide = lins[0].shape
-    tile = min(rows, 256)
+    tile = min(rows // 2, 256)
+    steps = rows // 2 // tile
     flat = [w for block in weights for w in block]
     return pl.pallas_call(
         functools.partial(normed_back_kernel, len(lins), parts),
@@ -393,9 +414,15 @@
             + [
                 pl.BlockSpec(flat[0].shape, lambda s, z: (0, 0), pipeline_mode=pl.Buffered(1))
             ] * len(flat),
-            out_specs=pl.BlockSpec((tile, depth), lambda s, z: (s, 0)),
-        ),
-        out_shape=jax.ShapeDtypeStruct((rows, depth), F32),
+            out_specs=[
+                pl.BlockSpec((tile, depth), lambda s, z: (jnp.minimum(s, steps - 1), 0)),
+                pl.BlockSpec((tile, depth), lambda s, z: (jnp.maximum(s - steps, 0), 0)),
+            ],
+        ),
+        out_shape=[
+            jax.ShapeDtypeStruct((rows // 2, depth), F32),
+            jax.ShapeDtypeStruct((rows // 2, depth), BF),
+        ],
         compiler_params=pltpu.CompilerParams(vmem_limit_bytes=48 << 20),
         cost_estimate=pl.CostEstimate(
             flops=2 * rows * depth * wide * len(lins),
@@ -553,8 +580,8 @@
         flows.append(Flow(gather_steps(piece, lambda d, b: qkv_w[d].append(b))))
         if step < shards - 1:
             piece, other = stage(flows, (lax.ppermute(piece, "shard", ring), other))
-    own_out, own_gate_up, qkv_w[0][-1] = lax.optimization_barrier(
-        (rows_of(w_out, block), own_gate_up, qkv_w[0][-1])
+    own_out, own_gate_up, own_down, qkv_w[0][-1] = lax.optimization_barrier(
+        (rows_of(w_out, block), own_gate_up, rows_of(w_down, units), qkv_w[0][-1])
     )
     own_out = lax.all_gather(own_out, "shard", axis=1, tiled=True)
     both = jnp.concatenate([normed, other], axis=0)
@@ -564,9 +591,7 @@
         return context[d]
 
     context[0], own_out = stage(flows, (run(0), own_out))
-    own_gate_up, own_out = lax.optimization_barrier((own_gate_up, own_out))
     gate_up = lax.all_gather(own_gate_up, "shard", axis=0, tiled=True)
-    own_down, _ = lax.optimization_barrier((rows_of(w_down, units), gate_up))
     down = lax.all_gather(own_down, "shard", axis=1, tiled=True)
     early = offsets[1:2] if staged else []
     early = stage(flows, [run(d) for d in early])
@@ -592,11 +617,10 @@
     root_two = lax.rsqrt(jnp.mean(hidden * hidden, axis=-1, keepdims=True) + EPSILON)
     normed_two = (hidden * root_two * gain_two).astype(BF)
 
-    disp_flow = Flow(copies_steps(mm(pick, normed_two).astype(BF)))
+    disp_flow = Flow(copies_steps(mm(pick, normed_two).astype(BF), straight_steps))
+    slot_grad, gate_up = stage([disp_flow], (slot_grad, gate_up))
+    slot_flow = Flow(copies_steps(slot_grad, straight_steps))
     stage([disp_flow])
-    slot_grad, gate_up = stage([disp_flow], (slot_grad, gate_up))
-    slot_flow = Flow(copies_steps(slot_grad))
-    stage([disp_flow, slot_flow])
     dispatched = jnp.concatenate(finish(disp_flow), axis=0)
     act = mm(dispatched, gate_up)
     all_slot_grad = jnp.concatenate(finish(slot_flow), axis=0)
@@ -609,18 +633,16 @@
     grad_up_act = (grad_inner * silu).astype(BF)
     grad_act = jnp.concatenate([grad_gate_act, grad_up_act], axis=1)
     back_flow = Flow(plane_sum_steps(mm_nt(grad_act, gate_up).astype(BF)))
-    flows, sums = [back_flow], []
-    for left, right in (
-        (grad_gate_act, dispatched),
-        (grad_up_act, dispatched),
-        (inner, all_slot_grad),
-    ):
-        grad = stage(flows, mm_tn(left, right).astype(BF))
-        sums.append(lax.psum_scatter(grad, "shard", scatter_dimension=1, tiled=True))
-        if len(flows) == 1:
-            expert_flow = Flow(plane_sum_steps(mm(inner, down).astype(BF)))
-            flows.append(expert_flow)
-    stage(flows)
+    grad_gate = stage([back_flow], mm_tn(grad_gate_act, dispatched).astype(BF))
+    expert_flow = Flow(plane_sum_steps(mm(inner, down).astype(BF)))
+    grad_up, grad_down = stage(
+        [back_flow, expert_flow],
+        (mm_tn(grad_up_act, dispatched).astype(BF), mm_tn(inner, all_slot_grad).astype(BF)),
+    )
+    sums = [
+        lax.psum_scatter(g, "shard", scatter_dimension=1, tiled=True)
+        for g in (grad_gate, grad_up, grad_down)
+    ]
     grad_normed_two = mm_tn(pick, finish(back_flow))
     grad_gain_two, through = norm_back(grad_normed_two, hidden, root_two, gain_two)
     grad_hidden = upstream + through
@@ -660,9 +682,9 @@
     out_blocks = {d: halves(grad_out_w[i * block : (i + 1) * block]) for i, d in enumerate(offsets)}
     out_flow, gate_flow = Flow(scatter_steps(out_blocks)), Flow(copies_steps(sums[0]))
     other_normed, up_sum = stage(
-        [out_flow, gate_flow], (swap(grad_normed[length:].astype(BF), 1), sums[1])
-    )
-    grad_normed = grad_normed[:length] + other_normed.astype(F32)
+        [out_flow, gate_flow], (swap(grad_normed[1], 1), sums[1])
+    )
+    grad_normed = grad_normed[0] + other_normed.astype(F32)
     grad_gain_one, first = norm_back(grad_normed, inputs, root_one, gain_one)
     grad_input = (grad_hidden + first).astype(BF)
     grad_input, gains, up_sum = stage(
@@ -672,18 +694,17 @@
     gain_flow, up_flow = Flow(vector_sum_steps(gains)), Flow(copies_steps(up_sum))
     sum_qkv = stage([out_flow, gate_flow, up_flow, gain_flow], sum_qkv)
     sum_out = lax.psum_scatter(finish(out_flow), "shard", scatter_dimension=1, tiled=True)
-    qkv_flow = Flow(copies_steps(sum_qkv))
+    qkv_flow = Flow(copies_steps(sum_qkv, straight_steps))
     grad_gate = place_turned(whoami, *finish(gate_flow), units)
     grad_gate, sum_out = stage([up_flow, qkv_flow, gain_flow], (grad_gate, sum_out))
     down_sum, sum_out = lax.optimization_barrier((sums[2], sum_out))
     all_down = lax.all_gather(down_sum, "rep", axis=0, tiled=True)
-    out_flow = Flow(copies_steps(sum_out))
+    out_flow = Flow(copies_steps(sum_out, straight_steps))
     output = (hidden + mm_tn(pick, finish(expert_flow)) * mix[:, None]).astype(BF)
     output = stage([up_flow, qkv_flow, out_flow, gain_flow], output)
     grad_up = place_turned(whoami, *finish(up_flow), units)
-    grad_up = stage([qkv_flow, out_flow, gain_flow], grad_up)
     grad_query, grad_key, grad_value = place(whoami, *finish(qkv_flow), own, block, True)
-    grad_query = stage([out_flow], grad_query)
+    grad_up, grad_query = stage([out_flow, gain_flow], (grad_up, grad_query))
     (grad_out,) = place(whoami, *finish(out_flow), block, own, False)
     grad_down = all_down.astype(F32)
     gain_grads = finish(gain_flow)

time: 753 us -> 754 us (level)
  waiting for transfers between devices: 229 us -> 253 us
  local copies, waits for them, and re-layouts: 110 us -> 98.1 us
  starting transfers between devices: 87 us -> 77.8 us
    ppermute x0 -> x18, waiting for transfers between devices: none -> 68.3 us  [jump(): return lax.ppermute(value, 'rep', [(i, i ^ offset) for i in range(size)])]
    ppermute x80 -> x52, waiting for transfers between devices: 184 us -> 133 us  [swap(): return lax.ppermute(value, 'rep', [(i, i ^ bit) for i in range(size)])]
    ppermute x80 -> x52, starting transfers between devices: 70.9 us -> 43.2 us  [swap(): return lax.ppermute(value, 'rep', [(i, i ^ bit) for i in range(size)])]
    ppermute x0 -> x18, starting transfers between devices: none -> 21.1 us  [jump(): return lax.ppermute(value, 'rep', [(i, i ^ offset) for i in range(size)])]
    ppermute x2, waiting for transfers between devices: 3.14 us -> 18.9 us  [per_device(): piece, other = stage(flows, (lax.ppermute(piece, 'shard', ring), other))]
    unnamed x234 -> x253, local copies, waits for them, and re-layouts: 64.6 us -> 61 us
  transfers between devices with their start and end apart: 98 -> 88, of which waited for: 37 -> 28; matrix products, arithmetic and copies ran while one was open for 24% -> 22% of each run, Pallas kernels for 21% -> 22%
where the time goes in v7:
time: 754 us; the launch traced here: 746 us
  waiting for transfers between devices  253 us (34%)
  Pallas kernels  161 us (21%)
  local copies, waits for them, and re-layouts  98.1 us (13%)
  starting transfers between devices  77.8 us (10%)
  matrix products  73.1 us (10%)
  other arithmetic  67 us (9%)
  between operations  15.8 us (2%)
    ppermute x52, waiting for transfers between devices, swap(): return lax.ppermute(value, 'rep', [(i, i ^ bit) for i in range(size)])  133 us
    pallas_call x4, Pallas kernels, attend_back(): pl.pallas_call(attend_back_kernel, grid=(rows // length,), in_specs=[by_s...  68.8 us
    ppermute x18, waiting for transfers between devices, jump(): return lax.ppermute(value, 'rep', [(i, i ^ offset) for i in range(size)])  68.3 us
    unnamed x253, local copies, waits for them, and re-layouts  61 us
    ppermute x52, starting transfers between devices, swap(): return lax.ppermute(value, 'rep', [(i, i ^ bit) for i in range(size)])  43.2 us
    pallas_call x4, Pallas kernels, attend(): pl.pallas_call(functools.partial(attend_kernel, parts), grid_spec=pltpu.P...  42.3 us
    dot_general x6, matrix products, mm_tn(): lax.dot_general(left, right, (((0,), (0,)), ((), ())), preferred_element_...  31 us
    pallas_call x1, Pallas kernels, normed_back(): pl.pallas_call(functools.partial(normed_back_kernel, len(lins), parts), g...  22.9 us
  transfers between devices with their start and end apart: 88, of which 28 were waited for; matrix products, arithmetic and copies ran while one was open for 22% of the time, Pallas kernels for 22%

profile of v7, /device:TPU:0, one launch (start us, length us, event | category | flops | bytes accessed | tf_op | source)
XLA Modules:
  0.0 746.5 jit_solution(9019847326380783800)
XLA Ops:
  8.8 3.1 collective-permute-start.2
  11.8 2.6 collective-permute-start.1
  17.8 2.7 constant_dynamic-slice_fusion.4
  21.2 2.3 constant_dynamic-slice_fusion.15
  26.2 16.2 %collective-permute-done.3.refs_5_ = bf16[512,768]{1,0:T(8,128)(2,1)} collective-permute-done((bf16[512,768]{1,0:T(8,128)(2,1)S(1)}, bf16[512,768]{1,0:T(8,128)(2,1)}, u32[]{:S(2)}, u32[]{:S(2)}) %collective-permute-start.3) | collective-permute-done | bytes 786464 | tf_op jit(solution)/shard_map/ppermute | solution.py:568
  47.9 18.9 %collective-permute-done.7.refs_6_ = bf16[512,768]{1,0:T(8,128)(2,1)} collective-permute-done((bf16[512,768]{1,0:T(8,128)(2,1)}, bf16[512,768]{1,0:T(8,128)(2,1)}, u32[]{:S(2)}, u32[]{:S(2)}) %collective-permute-start.7) | collective-permute-done | bytes 786464 | tf_op jit(solution)/shard_map/ppermute | solution.py:582
  75.4 20.7 %collective-permute-done.10 = bf16[256,768]{1,0:T(8,128)(2,1)} collective-permute-done((bf16[256,768]{1,0:T(8,128)(2,1)}, bf16[256,768]{1,0:T(8,128)(2,1)}, u32[]{:S(2)}, u32[]{:S(2)}) %collective-permute-start.10) | collective-permute-done | bytes 393248 | tf_op jit(solution)/shard_map/ppermute | solution.py:33
  105.2 2.8 pad_maximum_fusion.refs_0_.refs_1_.refs_2_.refs_3_.x_ref
  114.9 11.1 %attend.4 = (bf16[1024,256]{1,0:T(8,128)(2,1)S(1)}, bf16[1024,768]{1,0:T(8,128)(2,1)S(1)}, f32[1024,2]{1,0:T(8,128)S(1)}) custom-call(s32[1]{0:T(128)} %bitcast.1.z_ref, bf16[1024,2048]{1,0:T(8,128)(2,1)S(1)} %pad_maximum_fusion.refs_0_.refs_1_.refs_2_.refs_3_.x_ref, bf16[1024,2048]{1,0:T(8,128)(2,1)S(1)} %pad_maximum_fusion.refs_0_.refs_1_.refs_2_.refs_3_.x_ref, ...), custom_call_target="tpu_custom_call" | custom-call | flops 3758096384 | bytes 10485760 | tf_op jit(solution)/shard_map/attend/pallas_call | solution.py:263
  144.2 10.7 %attend.5 = (bf16[1024,256]{1,0:T(8,128)(2,1)S(1)}, bf16[1024,768]{1,0:T(8,128)(2,1)S(1)}, f32[1024,2]{1,0:T(8,128)S(1)}) custom-call(s32[1]{0:T(128)} %bitcast.1.z_ref, bf16[1024,2048]{1,0:T(8,128)(2,1)S(1)} %copy-done.3, bf16[1024,2048]{1,0:T(8,128)(2,1)S(1)} %copy-done.3, bf16[1024,2048]{1,0:T(8,128)(2,1)S(1)} %copy-done.3, ...), custom_call_target="tpu_custom_call" | custom-call | flops 3758096384 | bytes 10485760 | tf_op jit(solution)/shard_map/attend/pallas_call | solution.py:263
  156.8 10.7 %attend.6 = (bf16[1024,256]{1,0:T(8,128)(2,1)S(1)}, bf16[1024,768]{1,0:T(8,128)(2,1)S(1)}, f32[1024,2]{1,0:T(8,128)S(1)}) custom-call(s32[1]{0:T(128)} %bitcast.1.z_ref, bf16[1024,2048]{1,0:T(8,128)(2,1)S(1)} %copy-done.3, bf16[1024,2048]{1,0:T(8,128)(2,1)S(1)} %copy-done.3, bf16[1024,2048]{1,0:T(8,128)(2,1)S(1)} %copy-done.3, ...), custom_call_target="tpu_custom_call" | custom-call | flops 3758096384 | bytes 10485760 | tf_op jit(solution)/shard_map/attend/pallas_call | solution.py:263
  169.3 9.8 %attend.7 = (bf16[1024,256]{1,0:T(8,128)(2,1)S(1)}, bf16[1024,768]{1,0:T(8,128)(2,1)S(1)}, f32[1024,2]{1,0:T(8,128)S(1)}) custom-call(s32[1]{0:T(128)} %bitcast.1.z_ref, bf16[1024,2048]{1,0:T(8,128)(2,1)S(1)} %copy-done.3, bf16[1024,2048]{1,0:T(8,128)(2,1)S(1)} %copy-done.3, bf16[1024,2048]{1,0:T(8,128)(2,1)S(1)} %copy-done.3, ...), custom_call_target="tpu_custom_call" | custom-call | flops 3758096384 | bytes 10485760 | tf_op jit(solution)/shard_map/attend/pallas_call | solution.py:263
  183.4 6.2 collective-permute-done.22
  191.9 6.2 fusion.48
  199.1 3.6 collective-permute-done.24
  211.5 11.6 %collective-permute-done.27 = bf16[128,2048]{1,0:T(8,128)(2,1)S(1)} collective-permute-done((bf16[128,2048]{1,0:T(8,128)(2,1)S(1)}, bf16[128,2048]{1,0:T(8,128)(2,1)S(1)}, u32[]{:S(2)}, u32[]{:S(2)}) %collective-permute-start.27) | collective-permute-done | bytes 524320 | tf_op jit(solution)/shard_map/ppermute | solution.py:107
  223.2 10.4 %collective-permute-done.26 = bf16[128,2048]{1,0:T(8,128)(2,1)S(1)} collective-permute-done((bf16[128,2048]{1,0:T(8,128)(2,1)S(1)}, bf16[128,2048]{1,0:T(8,128)(2,1)S(1)}, u32[]{:S(2)}, u32[]{:S(2)}) %collective-permute-start.26) | collective-permute-done | bytes 524320 | tf_op jit(solution)/shard_map/ppermute | solution.py:107
  234.3 3.1 pad_maximum_fusion.3
  246.6 6.7 collective-permute-done.31
  253.3 10.8 %collective-permute-done.30 = bf16[128,2048]{1,0:T(8,128)(2,1)S(1)} collective-permute-done((bf16[128,2048]{1,0:T(8,128)(2,1)S(1)}, bf16[128,2048]{1,0:T(8,128)(2,1)S(1)}, u32[]{:S(2)}, u32[]{:S(2)}) %collective-permute-start.30) | collective-permute-done | bytes 524320 | tf_op jit(solution)/shard_map/ppermute | solution.py:107
  269.3 8.6 %fusion.49 = f32[1024,1408]{1,0:T(8,128)} fusion(bf16[1024,2048]{1,0:T(8,128)(2,1)S(1)} %constant_dynamic-update-slice_fusion.23, bf16[2048,1408]{1,0:T(8,128)(2,1)S(1)} %copy-done.104), kind=kOutput, calls=%fused_computation.191 | convolution fusion | flops 5905580032 | bytes 15728640 | tf_op jit(solution)/shard_map/dot_general | solution.py:20
  279.5 17.2 %all-gather.9.cloned.1.call-done = bf16[704,2048]{1,0:T(8,128)(2,1)} async-done(((bf16[704,512]{1,0:T(8,128)(2,1)}), bf16[704,2048]{1,0:T(8,128)(2,1)}) %all-gather.9.cloned.1.call-update) | async-done | bytes 2883600 | tf_op jit(solution)/shard_map/all_gather | solution.py:595
  296.7 10.2 %multiply_convert_fusion.3 = (bf16[1024,704]{1,0:T(8,128)(2,1)S(1)}, bf16[1024,704]{1,0:T(8,128)(2,1)S(1)}, bf16[1024,704]{1,0:T(8,128)(2,1)}) fusion(f32[1024,1408]{1,0:T(8,128)} %fusion.49, bf16[1024,2048]{1,0:T(8,128)(2,1)} %constant_dynamic-update-slice_fusion.28, bf16[704,2048]{1,0:T(8,128)(2,1)} %all-gather.9.cloned.1.call-done), kind=kOutput, calls=%fused_computation.43 | convolution fusion | flops 2963603456 | bytes 17170432 | tf_op jit(solution)/shard_map/dot_general | solution.py:24
  306.9 9.3 %convolution_convert_fusion = bf16[1024,2048]{1,0:T(8,128)(2,1)S(1)} fusion(bf16[2048,1408]{1,0:T(8,128)(2,1)} %all-gather.7.cloned.1.call-done, bf16[1024,704]{1,0:T(8,128)(2,1)S(1)} %get-tuple-element.308, bf16[1024,704]{1,0:T(8,128)(2,1)S(1)} %get-tuple-element.307), kind=kOutput, calls=%fused_computation.31 | convolution fusion | flops 5913444352 | bytes 12845056 | tf_op jit(solution)/shard_map/dot_general | solution.py:24
  321.2 4.5 convolution_convert_fusion.5
  326.0 5.7 convolution_convert_fusion.1
  335.7 7.0 convolution_convert_fusion.3
  342.7 4.6 add_convert_fusion.2
  347.3 2.7 fusion.45
  349.9 2.4 collective-permute-start.36
  353.4 4.5 convolution_convert_fusion.4
  358.0 7.9 %collective-permute-done.36 = bf16[128,2048]{1,0:T(8,128)(2,1)S(1)} collective-permute-done((bf16[128,2048]{1,0:T(8,128)(2,1)}, bf16[128,2048]{1,0:T(8,128)(2,1)S(1)}, u32[]{:S(2)}, u32[]{:S(2)}) %collective-permute-start.36) | collective-permute-done | bytes 524320 | tf_op jit(solution)/shard_map/ppermute | solution.py:107
  365.9 10.6 %collective-permute-done.35 = bf16[128,2048]{1,0:T(8,128)(2,1)} collective-permute-done((bf16[128,2048]{1,0:T(8,128)(2,1)}, bf16[128,2048]{1,0:T(8,128)(2,1)}, u32[]{:S(2)}, u32[]{:S(2)}) %collective-permute-start.35) | collective-permute-done | bytes 524320 | tf_op jit(solution)/shard_map/ppermute | solution.py:107
  377.0 4.1 multiply_reduce_fusion
  381.6 3.2 multiply_convert_fusion
  385.1 2.5 add_convert_fusion.1
  391.3 2.6 pad_maximum_fusion.1.grad_ref
  393.9 17.5 %attend_back.4 = (bf16[1024,768]{1,0:T(8,128)(2,1)S(1)}, bf16[1024,768]{1,0:T(8,128)(2,1)}, bf16[1024,768]{1,0:T(8,128)(2,1)}) custom-call(bf16[1024,2048]{1,0:T(8,128)(2,1)} %pad_maximum_fusion.1.grad_ref, bf16[256,2048]{1,0:T(8,128)(2,1)S(1)} %pad_maximum_fusion.6.out_ref, bf16[1024,768]{1,0:T(8,128)(2,1)} %copy-done.32, f32[1024,2]{1,0:T(8,128)S(1)} %copy-done.38, ...), custom_call_target="tpu_custom_call" | custom-call | flops 5637144576 | bytes 15728640 | tf_op jit(solution)/shard_map/attend_back/pallas_call | solution.py:352
  418.7 17.1 %attend_back.5 = (bf16[1024,768]{1,0:T(8,128)(2,1)S(1)}, bf16[1024,768]{1,0:T(8,128)(2,1)S(1)}, bf16[1024,768]{1,0:T(8,128)(2,1)}) custom-call(bf16[1024,2048]{1,0:T(8,128)(2,1)} %pad_maximum_fusion.1.grad_ref, bf16[256,2048]{1,0:T(8,128)(2,1)S(1)} %copy-done.15, bf16[1024,768]{1,0:T(8,128)(2,1)} %copy-done.31, f32[1024,2]{1,0:T(8,128)S(1)} %copy-done.36, ...), custom_call_target="tpu_custom_call" | custom-call | flops 5637144576 | bytes 15728640 | tf_op jit(solution)/shard_map/attend_back/pallas_call | solution.py:352
  438.2 17.0 %attend_back.6 = (bf16[1024,768]{1,0:T(8,128)(2,1)S(1)}, bf16[1024,768]{1,0:T(8,128)(2,1)S(1)}, bf16[1024,768]{1,0:T(8,128)(2,1)}) custom-call(bf16[1024,2048]{1,0:T(8,128)(2,1)} %pad_maximum_fusion.1.grad_ref, bf16[256,2048]{1,0:T(8,128)(2,1)S(1)} %copy-done.13, bf16[1024,768]{1,0:T(8,128)(2,1)} %copy-done.30, f32[1024,2]{1,0:T(8,128)S(1)} %get-tuple-element.209.lse_ref, ...), custom_call_target="tpu_custom_call" | custom-call | flops 5637144576 | bytes 15728640 | tf_op jit(solution)/shard_map/attend_back/pallas_call | solution.py:352
  455.7 3.4 add_convert_fusion.6
  459.2 3.2 add_convert_fusion.5
  464.4 7.7 %convolution_convert_fusion.2 = bf16[1024,2048]{1,0:T(8,128)(2,1)} fusion(bf16[1024,1024]{1,0:T(8,128)(2,1)} %constant_dynamic-update-slice_fusion.14, bf16[1024,2048]{1,0:T(8,128)(2,1)S(1)} %copy-done.59), kind=kOutput, calls=%fused_computation.33 | convolution fusion | flops 4297064448 | bytes 10485760 | tf_op jit(solution)/shard_map/dot_general | solution.py:28
  472.1 17.2 %attend_back.7 = (bf16[1024,768]{1,0:T(8,128)(2,1)S(1)}, bf16[1024,768]{1,0:T(8,128)(2,1)S(1)}, bf16[1024,768]{1,0:T(8,128)(2,1)}) custom-call(bf16[1024,2048]{1,0:T(8,128)(2,1)} %pad_maximum_fusion.1.grad_ref, bf16[256,2048]{1,0:T(8,128)(2,1)S(1)} %copy-done.28, bf16[1024,768]{1,0:T(8,128)(2,1)} %copy-done.29, f32[1024,2]{1,0:T(8,128)S(1)} %copy-done.34, ...), custom_call_target="tpu_custom_call" | custom-call | flops 5637144576 | bytes 15728640 | tf_op jit(solution)/shard_map/attend_back/pallas_call | solution.py:352
  492.9 22.9 %normed_back.1 = (f32[512,2048]{1,0:T(8,128)}, bf16[512,2048]{1,0:T(8,128)(2,1)}) custom-call(s32[1]{0:T(128)} %bitcast.1.z_ref, bf16[1024,768]{1,0:T(8,128)(2,1)} %copy-done.42, bf16[1024,768]{1,0:T(8,128)(2,1)} %copy-done.41, bf16[1024,768]{1,0:T(8,128)(2,1)} %copy-done.40, bf16[1024,768]{1,0:T(8,128)(2,1)} %copy-done.39, ...), custom_call_target="tpu_custom_call" | custom-call | flops 12884901888 | bytes 27262976 | tf_op jit(solution)/shard_map/normed_back/pallas_call | solution.py:408
  515.9 8.7 %collective-permute-done.45 = bf16[1024,768]{1,0:T(8,128)(2,1)} collective-permute-done((bf16[1024,768]{1,0:T(8,128)(2,1)}, bf16[1024,768]{1,0:T(8,128)(2,1)}, u32[]{:S(2)}, u32[]{:S(2)}) %collective-permute-start.45) | collective-permute-done | bytes 1572896 | tf_op jit(solution)/shard_map/ppermute | solution.py:33
  524.7 3.0 add_convert_fusion.3
  527.7 2.4 add_convert_fusion.4
  539.3 22.8 %collective-permute-done.51 = bf16[128,2048]{1,0:T(8,128)(2,1)S(1)} collective-permute-done((bf16[128,2048]{1,0:T(8,128)(2,1)S(1)}, bf16[128,2048]{1,0:T(8,128)(2,1)S(1)}, u32[]{:S(2)}, u32[]{:S(2)}) %collective-permute-start.51) | collective-permute-done | bytes 524320 | tf_op jit(solution)/shard_map/ppermute | solution.py:33
  566.3 3.2 fusion.9
  569.5 4.2 fusion.6
  573.8 3.1 collective-permute-done.49
  577.7 6.1 collective-permute-done.56
  590.5 24.2 %collective-permute-done.58 = bf16[128,2048]{1,0:T(8,128)(2,1)S(1)} collective-permute-done((bf16[128,2048]{1,0:T(8,128)(2,1)S(1)}, bf16[128,2048]{1,0:T(8,128)(2,1)S(1)}, u32[]{:S(2)}, u32[]{:S(2)}) %collective-permute-start.58) | collective-permute-done | bytes 524320 | tf_op jit(solution)/shard_map/ppermute | solution.py:33
  629.4 30.4 %collective-permute-done.68 = f32[2,2048]{1,0:T(2,128)S(1)} collective-permute-done((f32[2,2048]{1,0:T(2,128)S(1)}, f32[2,2048]{1,0:T(2,128)S(1)}, u32[]{:S(2)}, u32[]{:S(2)}) %collective-permute-start.68) | collective-permute-done | bytes 16416 | tf_op jit(solution)/shard_map/ppermute | solution.py:33
  662.9 5.0 place_turned.2
  683.1 3.2 add_convert_fusion
  687.0 3.7 collective-permute-done.73
  690.7 5.1 collective-permute-done.72
  701.3 3.4 collective-permute-start.78
  707.6 5.0 place_turned.3
  712.5 11.0 %place.2 = (f32[512,2048]{1,0:T(8,128)}, f32[512,2048]{1,0:T(8,128)}, f32[512,2048]{1,0:T(8,128)}) custom-call(s32[1]{0:T(128)} %bitcast.6.me_ref, bf16[2048,768]{1,0:T(8,128)(2,1)} %copy-done.55, bf16[2048,768]{1,0:T(8,128)(2,1)} %copy-done.60), custom_call_target="tpu_custom_call" | custom-call | bytes 25165824 | tf_op jit(solution)/shard_map/place/pallas_call | solution.py:469
  723.6 6.5 place.3
  730.6 8.9 %convert_element_type.269 = f32[5632,512]{1,0:T(8,128)} convert(bf16[5632,512]{1,0:T(8,128)(2,1)} %all-gather.11.cloned.1.call-done) | non-fusion elementwise | flops 2883584 | bytes 17301504 | tf_op jit(solution)/shard_map/convert_element_type | solution.py:709
  (490 shorter events, 187.1 us)
Async XLA Ops:
  7.2 124.3 %all-gather.5.cloned.1.call-start = ((), (), s32[]{:S(2)}) async-start(), calls=%async_computation.5 | async-start | bytes 1310720 | tf_op jit(solution)/shard_map/all_gather | solution.py:586
  20.5 21.9 %collective-permute-start.3 = (bf16[512,768]{1,0:T(8,128)(2,1)S(1)}, bf16[512,768]{1,0:T(8,128)(2,1)}, u32[]{:S(2)}, u32[]{:S(2)}) collective-permute-start(bf16[512,768]{1,0:T(8,128)(2,1)S(1)} %pad_maximum_fusion.8.refs_4_), channel_id=1, source_target_pairs={{0,1},{1,2},{2,3},{3,0},{4,5},{5,6},{6,7},{7,4},{8,9},{9,10},{10,1... | collective-permute-start | bytes 2359304 | tf_op jit(solution)/shard_map/ppermute | solution.py:568
  44.7 22.2 %collective-permute-start.8 = (bf16[512,2048]{1,0:T(8,128)(2,1)S(1)}, bf16[512,2048]{1,0:T(8,128)(2,1)S(1)}, u32[]{:S(2)}, u32[]{:S(2)}) collective-permute-start(bf16[512,2048]{1,0:T(8,128)(2,1)S(1)} %fusion.2), channel_id=1, source_target_pairs={{0,4},{4,0},{8,12},{12,8},{16,20},{20,16},{24,28},{28,24},{1,5},{5... | collective-permute-start | bytes 6291464 | tf_op jit(solution)/shard_map/ppermute | solution.py:33
  44.8 22.1 %collective-permute-start.7 = (bf16[512,768]{1,0:T(8,128)(2,1)}, bf16[512,768]{1,0:T(8,128)(2,1)}, u32[]{:S(2)}, u32[]{:S(2)}) collective-permute-start(bf16[512,768]{1,0:T(8,128)(2,1)} %collective-permute-done.3.refs_5_), channel_id=1, source_target_pairs={{0,1},{1,2},{2,3},{3,0},{4,5},{5,6},{6,7},{7,4},{8,9},{9,10},{10,1... | collective-permute-start | bytes 2359304 | tf_op jit(solution)/shard_map/ppermute | solution.py:582
  44.8 22.0 %collective-permute-start.6 = (bf16[512,768]{1,0:T(8,128)(2,1)}, bf16[512,768]{1,0:T(8,128)(2,1)S(1)}, u32[]{:S(2)}, u32[]{:S(2)}) collective-permute-start(bf16[512,768]{1,0:T(8,128)(2,1)} %collective-permute-done.3.refs_5_), channel_id=1, source_target_pairs={{0,16},{4,20},{8,24},{12,28},{16,0},{20,4},{24,8},{28,12},{1,17},{... | collective-permute-start | bytes 2359304 | tf_op jit(solution)/shard_map/ppermute | solution.py:33
  46.4 20.4 %collective-permute-start.5 = (bf16[512,768]{1,0:T(8,128)(2,1)}, bf16[512,768]{1,0:T(8,128)(2,1)S(1)}, u32[]{:S(2)}, u32[]{:S(2)}) collective-permute-start(bf16[512,768]{1,0:T(8,128)(2,1)} %collective-permute-done.3.refs_5_), channel_id=1, source_target_pairs={{0,8},{4,12},{8,0},{12,4},{16,24},{20,28},{24,16},{28,20},{1,9},{5... | collective-permute-start | bytes 2359304 | tf_op jit(solution)/shard_map/ppermute | solution.py:33
  66.9 29.2 %collective-permute-start.13 = (bf16[512,768]{1,0:T(8,128)(2,1)}, bf16[512,768]{1,0:T(8,128)(2,1)}, u32[]{:S(2)}, u32[]{:S(2)}) collective-permute-start(bf16[512,768]{1,0:T(8,128)(2,1)} %collective-permute-done.7.refs_6_), channel_id=1, source_target_pairs={{0,1},{1,2},{2,3},{3,0},{4,5},{5,6},{6,7},{7,4},{8,9},{9,10},{10,1... | collective-permute-start | bytes 2359304 | tf_op jit(solution)/shard_map/ppermute | solution.py:582
  66.9 29.2 %collective-permute-start.12 = (bf16[512,768]{1,0:T(8,128)(2,1)}, bf16[512,768]{1,0:T(8,128)(2,1)}, u32[]{:S(2)}, u32[]{:S(2)}) collective-permute-start(bf16[512,768]{1,0:T(8,128)(2,1)} %collective-permute-done.7.refs_6_), channel_id=1, source_target_pairs={{0,16},{4,20},{8,24},{12,28},{16,0},{20,4},{24,8},{28,12},{1,17},{... | collective-permute-start | bytes 2359304 | tf_op jit(solution)/shard_map/ppermute | solution.py:33
  68.5 27.6 %collective-permute-start.11 = (bf16[512,768]{1,0:T(8,128)(2,1)}, bf16[512,768]{1,0:T(8,128)(2,1)}, u32[]{:S(2)}, u32[]{:S(2)}) collective-permute-start(bf16[512,768]{1,0:T(8,128)(2,1)} %collective-permute-done.7.refs_6_), channel_id=1, source_target_pairs={{0,8},{4,12},{8,0},{12,4},{16,24},{20,28},{24,16},{28,20},{1,9},{5... | collective-permute-start | bytes 2359304 | tf_op jit(solution)/shard_map/ppermute | solution.py:33
  71.6 24.5 %collective-permute-start.10 = (bf16[256,768]{1,0:T(8,128)(2,1)}, bf16[256,768]{1,0:T(8,128)(2,1)}, u32[]{:S(2)}, u32[]{:S(2)}) collective-permute-start(bf16[256,768]{1,0:T(8,128)(2,1)} %slice.128), channel_id=1, source_target_pairs={{0,8},{4,12},{8,0},{12,4},{16,24},{20,28},{24,16},{28,20},{1,9},{5... | collective-permute-start | bytes 1179656 | tf_op jit(solution)/shard_map/ppermute | solution.py:33
  72.1 24.0 %collective-permute-start.9 = (bf16[256,768]{1,0:T(8,128)(2,1)}, bf16[256,768]{1,0:T(8,128)(2,1)}, u32[]{:S(2)}, u32[]{:S(2)}) collective-permute-start(bf16[256,768]{1,0:T(8,128)(2,1)} %slice.127), channel_id=1, source_target_pairs={{0,16},{4,20},{8,24},{12,28},{16,0},{20,4},{24,8},{28,12},{1,17},{... | collective-permute-start | bytes 1179656 | tf_op jit(solution)/shard_map/ppermute | solution.py:33
  96.2 138.2 %all-gather.7.cloned.1.call-start = ((), (), s32[]{:S(2)}) async-start(), calls=%async_computation.6 | async-start | bytes 7208960 | tf_op jit(solution)/shard_map/all_gather | solution.py:594
  103.1 28.4 %collective-permute-start.17 = (bf16[512,768]{1,0:T(8,128)(2,1)}, bf16[512,768]{1,0:T(8,128)(2,1)}, u32[]{:S(2)}, u32[]{:S(2)}) collective-permute-start(bf16[512,768]{1,0:T(8,128)(2,1)} %collective-permute-done.13.refs_7_), channel_id=1, source_target_pairs={{0,16},{4,20},{8,24},{12,28},{16,0},{20,4},{24,8},{28,12},{1,17},{... | collective-permute-start | bytes 2359304 | tf_op jit(solution)/shard_map/ppermute | solution.py:33
  103.7 27.8 %collective-permute-start.16 = (bf16[512,768]{1,0:T(8,128)(2,1)}, bf16[512,768]{1,0:T(8,128)(2,1)}, u32[]{:S(2)}, u32[]{:S(2)}) collective-permute-start(bf16[512,768]{1,0:T(8,128)(2,1)} %collective-permute-done.13.refs_7_), channel_id=1, source_target_pairs={{0,8},{4,12},{8,0},{12,4},{16,24},{20,28},{24,16},{28,20},{1,9},{5... | collective-permute-start | bytes 2359304 | tf_op jit(solution)/shard_map/ppermute | solution.py:33
  105.2 191.5 %all-gather.9.cloned.1.call-start = ((), (), s32[]{:S(2)}) async-start(), calls=%async_computation.7 | async-start | bytes 3604480 | tf_op jit(solution)/shard_map/all_gather | solution.py:595
  110.6 19.4 %collective-permute-start.15 = (bf16[256,768]{1,0:T(8,128)(2,1)S(1)}, bf16[256,768]{1,0:T(8,128)(2,1)S(1)}, u32[]{:S(2)}, u32[]{:S(2)}) collective-permute-start(bf16[256,768]{1,0:T(8,128)(2,1)S(1)} %slice.130), channel_id=1, source_target_pairs={{0,8},{4,12},{8,0},{12,4},{16,24},{20,28},{24,16},{28,20},{1,9},{5... | collective-permute-start | bytes 1179656 | tf_op jit(solution)/shard_map/ppermute | solution.py:33
  111.3 19.4 %collective-permute-start.14 = (bf16[256,768]{1,0:T(8,128)(2,1)S(1)}, bf16[256,768]{1,0:T(8,128)(2,1)S(1)}, u32[]{:S(2)}, u32[]{:S(2)}) collective-permute-start(bf16[256,768]{1,0:T(8,128)(2,1)S(1)} %slice.129), channel_id=1, source_target_pairs={{0,16},{4,20},{8,24},{12,28},{16,0},{20,4},{24,8},{28,12},{1,17},{... | collective-permute-start | bytes 1179656 | tf_op jit(solution)/shard_map/ppermute | solution.py:33
  131.5 47.7 %collective-permute-start.21 = (bf16[256,2048]{1,0:T(8,128)(2,1)}, bf16[256,2048]{1,0:T(8,128)(2,1)S(1)}, u32[]{:S(2)}, u32[]{:S(2)}) collective-permute-start(bf16[256,2048]{1,0:T(8,128)(2,1)} %all-gather.5.cloned.1.call-done.out_ref), channel_id=1, source_target_pairs={{0,16},{4,20},{8,24},{12,28},{16,0},{20,4},{24,8},{28,12},{1,17},{... | collective-permute-start | bytes 3145736 | tf_op jit(solution)/shard_map/ppermute | solution.py:33
  133.0 46.2 %collective-permute-start.20 = (bf16[256,2048]{1,0:T(8,128)(2,1)}, bf16[256,2048]{1,0:T(8,128)(2,1)S(1)}, u32[]{:S(2)}, u32[]{:S(2)}) collective-permute-start(bf16[256,2048]{1,0:T(8,128)(2,1)} %all-gather.5.cloned.1.call-done.out_ref), channel_id=1, source_target_pairs={{0,8},{4,12},{8,0},{12,4},{16,24},{20,28},{24,16},{28,20},{1,9},{5... | collective-permute-start | bytes 3145736 | tf_op jit(solution)/shard_map/ppermute | solution.py:33
  136.6 32.0 %collective-permute-start.19 = (bf16[256,768]{1,0:T(8,128)(2,1)S(1)}, bf16[256,768]{1,0:T(8,128)(2,1)S(1)}, u32[]{:S(2)}, u32[]{:S(2)}) collective-permute-start(bf16[256,768]{1,0:T(8,128)(2,1)S(1)} %slice.132), channel_id=1, source_target_pairs={{0,8},{4,12},{8,0},{12,4},{16,24},{20,28},{24,16},{28,20},{1,9},{5... | collective-permute-start | bytes 1179656 | tf_op jit(solution)/shard_map/ppermute | solution.py:33
  137.2 31.4 %collective-permute-start.18 = (bf16[256,768]{1,0:T(8,128)(2,1)S(1)}, bf16[256,768]{1,0:T(8,128)(2,1)S(1)}, u32[]{:S(2)}, u32[]{:S(2)}) collective-permute-start(bf16[256,768]{1,0:T(8,128)(2,1)S(1)} %slice.131), channel_id=1, source_target_pairs={{0,16},{4,20},{8,24},{12,28},{16,0},{20,4},{24,8},{28,12},{1,17},{... | collective-permute-start | bytes 1179656 | tf_op jit(solution)/shard_map/ppermute | solution.py:33
  209.3 24.2 %collective-permute-start.26 = (bf16[128,2048]{1,0:T(8,128)(2,1)S(1)}, bf16[128,2048]{1,0:T(8,128)(2,1)S(1)}, u32[]{:S(2)}, u32[]{:S(2)}) collective-permute-start(bf16[128,2048]{1,0:T(8,128)(2,1)S(1)} %get-tuple-element.353), channel_id=1, source_target_pairs={{0,16},{4,20},{8,24},{12,28},{16,0},{20,4},{24,8},{28,12},{1,17},{... | collective-permute-start | bytes 1572872 | tf_op jit(solution)/shard_map/ppermute | solution.py:107
  210.4 24.0 %collective-permute-start.25 = (bf16[128,2048]{1,0:T(8,128)(2,1)S(1)}, bf16[128,2048]{1,0:T(8,128)(2,1)}, u32[]{:S(2)}, u32[]{:S(2)}) collective-permute-start(bf16[128,2048]{1,0:T(8,128)(2,1)S(1)} %get-tuple-element.353), channel_id=1, source_target_pairs={{0,8},{4,12},{8,0},{12,4},{16,24},{20,28},{24,16},{28,20},{1,9},{5... | collective-permute-start | bytes 1572872 | tf_op jit(solution)/shard_map/ppermute | solution.py:107
  237.4 29.6 %collective-permute-start.28 = (bf16[512,2048]{1,0:T(8,128)(2,1)}, bf16[512,2048]{1,0:T(8,128)(2,1)}, u32[]{:S(2)}, u32[]{:S(2)}) collective-permute-start(bf16[512,2048]{1,0:T(8,128)(2,1)} %pad_maximum_fusion.3), channel_id=1, source_target_pairs={{0,4},{4,0},{8,12},{12,8},{16,20},{20,16},{24,28},{28,24},{1,5},{5... | collective-permute-start | bytes 6291464 | tf_op jit(solution)/shard_map/ppermute | solution.py:33
  237.5 278.4 %reduce-scatter.6.cloned.1.call-start = ((), (), s32[]{:S(2)}) async-start(), calls=%async_computation.8 | async-start | bytes 3604480 | tf_op jit(solution)/shard_map/reduce_scatter | solution.py:643
  239.3 24.7 %collective-permute-start.30 = (bf16[128,2048]{1,0:T(8,128)(2,1)S(1)}, bf16[128,2048]{1,0:T(8,128)(2,1)S(1)}, u32[]{:S(2)}, u32[]{:S(2)}) collective-permute-start(bf16[128,2048]{1,0:T(8,128)(2,1)S(1)} %fusion.15), channel_id=1, source_target_pairs={{0,16},{4,20},{8,24},{12,28},{16,0},{20,4},{24,8},{28,12},{1,17},{... | collective-permute-start | bytes 1572872 | tf_op jit(solution)/shard_map/ppermute | solution.py:107
  240.4 23.7 %collective-permute-start.29 = (bf16[128,2048]{1,0:T(8,128)(2,1)S(1)}, bf16[128,2048]{1,0:T(8,128)(2,1)S(1)}, u32[]{:S(2)}, u32[]{:S(2)}) collective-permute-start(bf16[128,2048]{1,0:T(8,128)(2,1)S(1)} %fusion.15), channel_id=1, source_target_pairs={{0,8},{4,12},{8,0},{12,4},{16,24},{20,28},{24,16},{28,20},{1,9},{5... | collective-permute-start | bytes 1572872 | tf_op jit(solution)/shard_map/ppermute | solution.py:107
  325.7 198.8 %reduce-scatter.8.cloned.1.call-start = ((), (), s32[]{:S(2)}) async-start(), calls=%async_computation.9 | async-start | bytes 3604480 | tf_op jit(solution)/shard_map/reduce_scatter | solution.py:643
  335.3 22.6 %collective-permute-start.37 = (bf16[512,2048]{1,0:T(8,128)(2,1)}, bf16[512,2048]{1,0:T(8,128)(2,1)}, u32[]{:S(2)}, u32[]{:S(2)}) collective-permute-start(bf16[512,2048]{1,0:T(8,128)(2,1)} %slice.175), channel_id=1, source_target_pairs={{0,4},{4,0},{8,12},{12,8},{16,20},{20,16},{24,28},{28,24},{1,5},{5... | collective-permute-start | bytes 6291464 | tf_op jit(solution)/shard_map/ppermute | solution.py:33
  352.3 24.1 %collective-permute-start.35 = (bf16[128,2048]{1,0:T(8,128)(2,1)}, bf16[128,2048]{1,0:T(8,128)(2,1)}, u32[]{:S(2)}, u32[]{:S(2)}) collective-permute-start(bf16[128,2048]{1,0:T(8,128)(2,1)} %get-tuple-element.322), channel_id=1, source_target_pairs={{0,16},{4,20},{8,24},{12,28},{16,0},{20,4},{24,8},{28,12},{1,17},{... | collective-permute-start | bytes 1572872 | tf_op jit(solution)/shard_map/ppermute | solution.py:107
  352.9 23.6 %collective-permute-start.34 = (bf16[128,2048]{1,0:T(8,128)(2,1)}, bf16[128,2048]{1,0:T(8,128)(2,1)}, u32[]{:S(2)}, u32[]{:S(2)}) collective-permute-start(bf16[128,2048]{1,0:T(8,128)(2,1)} %get-tuple-element.323), channel_id=1, source_target_pairs={{0,8},{4,12},{8,0},{12,4},{16,24},{20,28},{24,16},{28,20},{1,9},{5... | collective-permute-start | bytes 1572872 | tf_op jit(solution)/shard_map/ppermute | solution.py:107
  376.5 155.5 %reduce-scatter.10.cloned.1.call-start = ((), (), s32[]{:S(2)}) async-start(), calls=%async_computation.10 | async-start | bytes 3604480 | tf_op jit(solution)/shard_map/reduce_scatter | solution.py:643
  387.7 24.9 %collective-permute-start.40 = (bf16[128,2048]{1,0:T(8,128)(2,1)S(1)}, bf16[128,2048]{1,0:T(8,128)(2,1)S(1)}, u32[]{:S(2)}, u32[]{:S(2)}) collective-permute-start(bf16[128,2048]{1,0:T(8,128)(2,1)S(1)} %get-tuple-element.318), channel_id=1, source_target_pairs={{0,24},{4,28},{8,16},{12,20},{16,8},{20,12},{24,0},{28,4},{1,25},{... | collective-permute-start | bytes 1572872 | tf_op jit(solution)/shard_map/ppermute | solution.py:107
  389.5 24.6 %collective-permute-start.39 = (bf16[128,2048]{1,0:T(8,128)(2,1)S(1)}, bf16[128,2048]{1,0:T(8,128)(2,1)S(1)}, u32[]{:S(2)}, u32[]{:S(2)}) collective-permute-start(bf16[128,2048]{1,0:T(8,128)(2,1)S(1)} %get-tuple-element.319), channel_id=1, source_target_pairs={{0,16},{4,20},{8,24},{12,28},{16,0},{20,4},{24,8},{28,12},{1,17},{... | collective-permute-start | bytes 1572872 | tf_op jit(solution)/shard_map/ppermute | solution.py:107
  390.8 23.4 %collective-permute-start.38 = (bf16[128,2048]{1,0:T(8,128)(2,1)S(1)}, bf16[128,2048]{1,0:T(8,128)(2,1)S(1)}, u32[]{:S(2)}, u32[]{:S(2)}) collective-permute-start(bf16[128,2048]{1,0:T(8,128)(2,1)S(1)} %get-tuple-element.320), channel_id=1, source_target_pairs={{0,8},{4,12},{8,0},{12,4},{16,24},{20,28},{24,16},{28,20},{1,9},{5... | collective-permute-start | bytes 1572872 | tf_op jit(solution)/shard_map/ppermute | solution.py:107
  415.2 40.6 %collective-permute-start.42 = (bf16[1024,768]{1,0:T(8,128)(2,1)}, bf16[1024,768]{1,0:T(8,128)(2,1)}, u32[]{:S(2)}, u32[]{:S(2)}) collective-permute-start(bf16[1024,768]{1,0:T(8,128)(2,1)} %get-tuple-element.206), channel_id=1, source_target_pairs={{0,8},{4,12},{8,0},{12,4},{16,24},{20,28},{24,16},{28,20},{1,9},{5... | collective-permute-start | bytes 4718600 | tf_op jit(solution)/shard_map/ppermute | solution.py:33
  416.7 39.1 %collective-permute-start.43 = (bf16[1024,768]{1,0:T(8,128)(2,1)}, bf16[1024,768]{1,0:T(8,128)(2,1)}, u32[]{:S(2)}, u32[]{:S(2)}) collective-permute-start(bf16[1024,768]{1,0:T(8,128)(2,1)} %get-tuple-element.207), channel_id=1, source_target_pairs={{0,16},{4,20},{8,24},{12,28},{16,0},{20,4},{24,8},{28,12},{1,17},{... | collective-permute-start | bytes 4718600 | tf_op jit(solution)/shard_map/ppermute | solution.py:33
  417.4 200.9 %reduce-scatter.12.cloned.1.call-start = ((), (), s32[]{:S(2)}) async-start(), calls=%async_computation.11 | async-start | bytes 3932160 | tf_op jit(solution)/shard_map/reduce_scatter | solution.py:680
  437.0 54.7 %collective-permute-start.47 = (bf16[1024,768]{1,0:T(8,128)(2,1)}, bf16[1024,768]{1,0:T(8,128)(2,1)S(1)}, u32[]{:S(2)}, u32[]{:S(2)}) collective-permute-start(bf16[1024,768]{1,0:T(8,128)(2,1)} %get-tuple-element.214), channel_id=1, source_target_pairs={{0,16},{4,20},{8,24},{12,28},{16,0},{20,4},{24,8},{28,12},{1,17},{... | collective-permute-start | bytes 4718600 | tf_op jit(solution)/shard_map/ppermute | solution.py:33
  455.2 37.4 %collective-permute-start.46 = (bf16[1024,768]{1,0:T(8,128)(2,1)S(1)}, bf16[1024,768]{1,0:T(8,128)(2,1)}, u32[]{:S(2)}, u32[]{:S(2)}) collective-permute-start(bf16[1024,768]{1,0:T(8,128)(2,1)S(1)} %get-tuple-element.211), channel_id=1, source_target_pairs={{0,8},{4,12},{8,0},{12,4},{16,24},{20,28},{24,16},{28,20},{1,9},{5... | collective-permute-start | bytes 4718600 | tf_op jit(solution)/shard_map/ppermute | solution.py:33
  462.3 62.2 %collective-permute-start.45 = (bf16[1024,768]{1,0:T(8,128)(2,1)}, bf16[1024,768]{1,0:T(8,128)(2,1)}, u32[]{:S(2)}, u32[]{:S(2)}) collective-permute-start(bf16[1024,768]{1,0:T(8,128)(2,1)} %add_convert_fusion.5), channel_id=1, source_target_pairs={{0,8},{4,12},{8,0},{12,4},{16,24},{20,28},{24,16},{28,20},{1,9},{5... | collective-permute-start | bytes 4718600 | tf_op jit(solution)/shard_map/ppermute | solution.py:33
  463.4 61.2 %collective-permute-start.44 = (bf16[1024,768]{1,0:T(8,128)(2,1)}, bf16[1024,768]{1,0:T(8,128)(2,1)}, u32[]{:S(2)}, u32[]{:S(2)}) collective-permute-start(bf16[1024,768]{1,0:T(8,128)(2,1)} %add_convert_fusion.6), channel_id=1, source_target_pairs={{0,16},{4,20},{8,24},{12,28},{16,0},{20,4},{24,8},{28,12},{1,17},{... | collective-permute-start | bytes 4718600 | tf_op jit(solution)/shard_map/ppermute | solution.py:33
  524.6 39.4 %collective-permute-start.54 = (bf16[512,2048]{1,0:T(8,128)(2,1)}, bf16[512,2048]{1,0:T(8,128)(2,1)}, u32[]{:S(2)}, u32[]{:S(2)}) collective-permute-start(bf16[512,2048]{1,0:T(8,128)(2,1)} %get-tuple-element.234), channel_id=1, source_target_pairs={{0,4},{4,0},{8,12},{12,8},{16,20},{20,16},{24,28},{28,24},{1,5},{5... | collective-permute-start | bytes 6291464 | tf_op jit(solution)/shard_map/ppermute | solution.py:33
  532.1 135.9 %reduce-scatter.14.cloned.1.call-start = ((), (), s32[]{:S(2)}) async-start(), calls=%async_computation.12 | async-start | bytes 1310720 | tf_op jit(solution)/shard_map/reduce_scatter | solution.py:696
  532.1 31.9 %collective-permute-start.53 = (bf16[704,512]{1,0:T(8,128)(2,1)}, bf16[704,512]{1,0:T(8,128)(2,1)S(1)}, u32[]{:S(2)}, u32[]{:S(2)}) collective-permute-start(bf16[704,512]{1,0:T(8,128)(2,1)} %reduce-scatter.6.cloned.1.call-done), channel_id=1, source_target_pairs={{0,16},{4,20},{8,24},{12,28},{16,0},{20,4},{24,8},{28,12},{1,17},{... | collective-permute-start | bytes 2162696 | tf_op jit(solution)/shard_map/ppermute | solution.py:33
  533.0 31.0 %collective-permute-start.52 = (bf16[704,512]{1,0:T(8,128)(2,1)}, bf16[704,512]{1,0:T(8,128)(2,1)S(1)}, u32[]{:S(2)}, u32[]{:S(2)}) collective-permute-start(bf16[704,512]{1,0:T(8,128)(2,1)} %reduce-scatter.6.cloned.1.call-done), channel_id=1, source_target_pairs={{0,8},{4,12},{8,0},{12,4},{16,24},{20,28},{24,16},{28,20},{1,9},{5... | collective-permute-start | bytes 2162696 | tf_op jit(solution)/shard_map/ppermute | solution.py:33
  535.9 26.2 %collective-permute-start.51 = (bf16[128,2048]{1,0:T(8,128)(2,1)S(1)}, bf16[128,2048]{1,0:T(8,128)(2,1)S(1)}, u32[]{:S(2)}, u32[]{:S(2)}) collective-permute-start(bf16[128,2048]{1,0:T(8,128)(2,1)S(1)} %get-tuple-element.314), channel_id=1, source_target_pairs={{0,16},{4,20},{8,24},{12,28},{16,0},{20,4},{24,8},{28,12},{1,17},{... | collective-permute-start | bytes 1572872 | tf_op jit(solution)/shard_map/ppermute | solution.py:33
  536.6 26.2 %collective-permute-start.50 = (bf16[128,2048]{1,0:T(8,128)(2,1)S(1)}, bf16[128,2048]{1,0:T(8,128)(2,1)S(1)}, u32[]{:S(2)}, u32[]{:S(2)}) collective-permute-start(bf16[128,2048]{1,0:T(8,128)(2,1)S(1)} %get-tuple-element.315), channel_id=1, source_target_pairs={{0,8},{4,12},{8,0},{12,4},{16,24},{20,28},{24,16},{28,20},{1,9},{5... | collective-permute-start | bytes 1572872 | tf_op jit(solution)/shard_map/ppermute | solution.py:33
  564.1 19.7 %collective-permute-start.56 = (bf16[352,512]{1,0:T(8,128)(2,1)S(1)}, bf16[352,512]{1,0:T(8,128)(2,1)S(1)}, u32[]{:S(2)}, u32[]{:S(2)}) collective-permute-start(bf16[352,512]{1,0:T(8,128)(2,1)S(1)} %slice.155), channel_id=1, source_target_pairs={{0,8},{4,12},{8,0},{12,4},{16,24},{20,28},{24,16},{28,20},{1,9},{5... | collective-permute-start | bytes 1081352 | tf_op jit(solution)/shard_map/ppermute | solution.py:33
  583.8 32.9 %collective-permute-start.59 = (bf16[2816,512]{1,0:T(8,128)(2,1)S(1)}, bf16[2816,512]{1,0:T(8,128)(2,1)S(1)}, u32[]{:S(2)}, u32[]{:S(2)}) collective-permute-start(bf16[2816,512]{1,0:T(8,128)(2,1)S(1)} %constant_dynamic-update-slice_fusion.33.same_ref), channel_id=1, source_target_pairs={{0,4},{4,0},{8,12},{12,8},{16,20},{20,16},{24,28},{28,24},{1,5},{5... | collective-permute-start | bytes 8650760 | tf_op jit(solution)/shard_map/ppermute | solution.py:33
  583.9 30.8 %collective-permute-start.61 = (bf16[704,512]{1,0:T(8,128)(2,1)S(1)}, bf16[704,512]{1,0:T(8,128)(2,1)S(1)}, u32[]{:S(2)}, u32[]{:S(2)}) collective-permute-start(bf16[704,512]{1,0:T(8,128)(2,1)S(1)} %copy-done.74), channel_id=1, source_target_pairs={{0,16},{4,20},{8,24},{12,28},{16,0},{20,4},{24,8},{28,12},{1,17},{... | collective-permute-start | bytes 2162696 | tf_op jit(solution)/shard_map/ppermute | solution.py:33
  585.3 30.4 %collective-permute-start.60 = (bf16[704,512]{1,0:T(8,128)(2,1)S(1)}, bf16[704,512]{1,0:T(8,128)(2,1)S(1)}, u32[]{:S(2)}, u32[]{:S(2)}) collective-permute-start(bf16[704,512]{1,0:T(8,128)(2,1)S(1)} %copy-done.74), channel_id=1, source_target_pairs={{0,8},{4,12},{8,0},{12,4},{16,24},{20,28},{24,16},{28,20},{1,9},{5... | collective-permute-start | bytes 2162696 | tf_op jit(solution)/shard_map/ppermute | solution.py:33
  587.4 27.3 %collective-permute-start.58 = (bf16[128,2048]{1,0:T(8,128)(2,1)S(1)}, bf16[128,2048]{1,0:T(8,128)(2,1)S(1)}, u32[]{:S(2)}, u32[]{:S(2)}) collective-permute-start(bf16[128,2048]{1,0:T(8,128)(2,1)S(1)} %get-tuple-element.312), channel_id=1, source_target_pairs={{0,8},{4,12},{8,0},{12,4},{16,24},{20,28},{24,16},{28,20},{1,9},{5... | collective-permute-start | bytes 1572872 | tf_op jit(solution)/shard_map/ppermute | solution.py:33
  589.2 25.5 %collective-permute-start.57 = (bf16[128,2048]{1,0:T(8,128)(2,1)S(1)}, bf16[128,2048]{1,0:T(8,128)(2,1)S(1)}, u32[]{:S(2)}, u32[]{:S(2)}) collective-permute-start(bf16[128,2048]{1,0:T(8,128)(2,1)S(1)} %get-tuple-element.313), channel_id=1, source_target_pairs={{0,16},{4,20},{8,24},{12,28},{16,0},{20,4},{24,8},{28,12},{1,17},{... | collective-permute-start | bytes 1572872 | tf_op jit(solution)/shard_map/ppermute | solution.py:33
  621.6 109.0 %all-gather.11.cloned.1.call-start = ((), (), s32[]{:S(2)}) async-start(), calls=%async_computation.13 | async-start | bytes 6488064 | tf_op jit(solution)/shard_map/all_gather | solution.py:701
  621.7 46.2 %collective-permute-start.67 = (bf16[512,768]{1,0:T(8,128)(2,1)}, bf16[512,768]{1,0:T(8,128)(2,1)}, u32[]{:S(2)}, u32[]{:S(2)}) collective-permute-start(bf16[512,768]{1,0:T(8,128)(2,1)} %reduce-scatter.12.cloned.1.call-done), channel_id=1, source_target_pairs={{0,24},{4,28},{8,16},{12,20},{16,8},{20,12},{24,0},{28,4},{1,25},{... | collective-permute-start | bytes 2359304 | tf_op jit(solution)/shard_map/ppermute | solution.py:107
  623.1 44.8 %collective-permute-start.66 = (bf16[512,768]{1,0:T(8,128)(2,1)}, bf16[512,768]{1,0:T(8,128)(2,1)}, u32[]{:S(2)}, u32[]{:S(2)}) collective-permute-start(bf16[512,768]{1,0:T(8,128)(2,1)} %reduce-scatter.12.cloned.1.call-done), channel_id=1, source_target_pairs={{0,16},{4,20},{8,24},{12,28},{16,0},{20,4},{24,8},{28,12},{1,17},{... | collective-permute-start | bytes 2359304 | tf_op jit(solution)/shard_map/ppermute | solution.py:107
  623.7 44.2 %collective-permute-start.65 = (bf16[512,768]{1,0:T(8,128)(2,1)}, bf16[512,768]{1,0:T(8,128)(2,1)}, u32[]{:S(2)}, u32[]{:S(2)}) collective-permute-start(bf16[512,768]{1,0:T(8,128)(2,1)} %reduce-scatter.12.cloned.1.call-done), channel_id=1, source_target_pairs={{0,8},{4,12},{8,0},{12,4},{16,24},{20,28},{24,16},{28,20},{1,9},{5... | collective-permute-start | bytes 2359304 | tf_op jit(solution)/shard_map/ppermute | solution.py:107
  625.2 34.6 %collective-permute-start.68 = (f32[2,2048]{1,0:T(2,128)S(1)}, f32[2,2048]{1,0:T(2,128)S(1)}, u32[]{:S(2)}, u32[]{:S(2)}) collective-permute-start(f32[2,2048]{1,0:T(2,128)S(1)} %add.229), channel_id=1, source_target_pairs={{0,8},{4,12},{8,0},{12,4},{16,24},{20,28},{24,16},{28,20},{1,9},{5... | collective-permute-start | bytes 49160 | tf_op jit(solution)/shard_map/ppermute | solution.py:33
  627.9 40.0 %collective-permute-start.64 = (bf16[352,512]{1,0:T(8,128)(2,1)S(1)}, bf16[352,512]{1,0:T(8,128)(2,1)S(1)}, u32[]{:S(2)}, u32[]{:S(2)}) collective-permute-start(bf16[352,512]{1,0:T(8,128)(2,1)S(1)} %slice.159), channel_id=1, source_target_pairs={{0,8},{4,12},{8,0},{12,4},{16,24},{20,28},{24,16},{28,20},{1,9},{5... | collective-permute-start | bytes 1081352 | tf_op jit(solution)/shard_map/ppermute | solution.py:33
  676.3 21.0 %collective-permute-start.70 = (bf16[2048,768]{1,0:T(8,128)(2,1)S(1)}, bf16[2048,768]{1,0:T(8,128)(2,1)S(1)}, u32[]{:S(2)}, u32[]{:S(2)}) collective-permute-start(bf16[2048,768]{1,0:T(8,128)(2,1)S(1)} %constant_dynamic-update-slice_fusion.43.same_ref), channel_id=1, source_target_pairs={{0,4},{4,0},{8,12},{12,8},{16,20},{20,16},{24,28},{28,24},{1,5},{5... | collective-permute-start | bytes 9437192 | tf_op jit(solution)/shard_map/ppermute | solution.py:33
  701.2 22.3 %collective-permute-start.75 = (bf16[1024,512]{1,0:T(8,128)(2,1)}, bf16[1024,512]{1,0:T(8,128)(2,1)}, u32[]{:S(2)}, u32[]{:S(2)}) collective-permute-start(bf16[1024,512]{1,0:T(8,128)(2,1)} %constant_dynamic-update-slice_fusion.47.same_ref), channel_id=1, source_target_pairs={{0,4},{4,0},{8,12},{12,8},{16,20},{20,16},{24,28},{28,24},{1,5},{5... | collective-permute-start | bytes 3145736 | tf_op jit(solution)/shard_map/ppermute | solution.py:33
  701.3 22.3 %collective-permute-start.78 = (f32[2,512]{1,0:T(2,128)S(1)}, f32[2,512]{1,0:T(2,128)S(1)}, u32[]{:S(2)}, u32[]{:S(2)}) collective-permute-start(f32[2,512]{1,0:T(2,128)S(1)} %get-tuple-element.336), channel_id=1, source_target_pairs={{0,3},{1,0},{2,1},{3,2},{4,7},{5,4},{6,5},{7,6},{8,11},{9,8},{10,9... | collective-permute-start | bytes 12296 | tf_op jit(solution)/shard_map/ppermute | solution.py:171
  704.6 18.9 %collective-permute-start.76 = (f32[2,512]{1,0:T(2,128)S(1)}, f32[2,512]{1,0:T(2,128)S(1)}, u32[]{:S(2)}, u32[]{:S(2)}) collective-permute-start(f32[2,512]{1,0:T(2,128)S(1)} %get-tuple-element.338), channel_id=1, source_target_pairs={{0,1},{1,2},{2,3},{3,0},{4,5},{5,6},{6,7},{7,4},{8,9},{9,10},{10,1... | collective-permute-start | bytes 12296 | tf_op jit(solution)/shard_map/ppermute | solution.py:171
  (132 other events, 1293.0 us)
Sparse Core Ops, SparseCore 0:
  96.3 28.0 all-gather.4
  126.5 106.1 all-gather.6
  237.6 59.0 all-gather.8
  325.9 54.9 reduce-scatter.5
  383.5 56.0 reduce-scatter.7
  441.8 56.0 reduce-scatter.9
  532.2 57.9 reduce-scatter.11
  621.7 24.8 reduce-scatter.13
  668.1 51.5 all-gather.10

commit v8 on v7

--- a/solution.py
+++ b/solution.py
@@ -100,6 +100,141 @@
             blocks[d ^ bit] = b
             sink(d ^ bit, b)
     return blocks
+
+
+def peers():
+    return [1, *[d for d in chip_offsets() if d]]
+
+
+def greet(others):
+    barrier = pltpu.get_barrier_semaphore()
+    for device in others.values():
+        pl.semaphore_signal(barrier, inc=1, device_id={"rep": device})
+    pl.semaphore_wait(barrier, len(others))
+
+
+def gather_kernel(offsets, in_ref, out_ref, own_sem, send_sem, recv_sem):
+    me, rows = lax.axis_index("rep"), in_ref.shape[0]
+    others = {d: jnp.bitwise_xor(me, d) for d in offsets}
+    spot = {d: pl.ds((d // 2 + d % 2 * len(offsets)) * rows, rows) for d in range(2 * len(offsets))}
+    greet(others)
+    own = pltpu.make_async_copy(in_ref, out_ref.at[spot[0]], own_sem)
+    own.start()
+
+    def send(source, offset, to):
+        return pltpu.make_async_remote_copy(
+            src_ref=source,
+            dst_ref=out_ref.at[spot[offset]],
+            send_sem=send_sem.at[offset],
+            recv_sem=recv_sem.at[offset],
+            device_id={"rep": others[to]},
+        )
+
+    chips = [d for d in offsets if d != 1]
+    first = {d: send(in_ref, d, d) for d in [*reversed(chips), 1]}
+    for copy in first.values():
+        copy.start()
+    second = {}
+    for d in chips:
+        first[d].wait_recv()
+        second[d] = send(out_ref.at[spot[d]], d + 1, 1)
+        second[d].start()
+    first[1].wait_recv()
+    for copy in second.values():
+        copy.wait_recv()
+    own.wait()
+    for copy in [*first.values(), *second.values()]:
+        copy.wait_send()
+
+
+def gather_rows(value, number):
+    rows, width = value.shape
+    size = lax.axis_size("rep")
+    return pl.pallas_call(
+        functools.partial(gather_kernel, peers()),
+        out_shape=jax.ShapeDtypeStruct((size * rows, width), value.dtype),
+        in_specs=[pl.BlockSpec(memory_space=pltpu.VMEM)],
+        out_specs=pl.BlockSpec(memory_space=pltpu.VMEM),
+        scratch_shapes=[
+            pltpu.SemaphoreType.DMA,
+            pltpu.SemaphoreType.DMA((size,)),
+            pltpu.SemaphoreType.DMA((size,)),
+        ],
+        compiler_params=pltpu.CompilerParams(
+            collective_id=number, has_side_effects=True, vmem_limit_bytes=16 << 20
+        ),
+        cost_estimate=pl.CostEstimate(
+            flops=0, bytes_accessed=30 * value.size * size, transcendentals=0
+        ),
+        name="gather_rows",
+    )(value)
+
+
+def reduce_kernel(offsets, in_ref, out_ref, core_ref, held_ref, chip_ref, send_sem, recv_sem):
+    me, rows = lax.axis_index("rep"), out_ref.shape[0]
+    others = {d: jnp.bitwise_xor(me, d) for d in offsets}
+    chips = [0, *[d for d in offsets if d != 1]]
+    count = len(chips)
+    greet(others)
+
+    def block(ref, i):
+        return ref.at[pl.ds(i * rows, rows)]
+
+    def send(source, target, index, to):
+        return pltpu.make_async_remote_copy(
+            src_ref=source,
+            dst_ref=target,
+            send_sem=send_sem.at[index],
+            recv_sem=recv_sem.at[index],
+            device_id={"rep": others[to]},
+        )
+
+    order = list(reversed(range(count)))
+    core = {i: send(block(in_ref, count + i), block(core_ref, i), i, 1) for i in order}
+    for copy in core.values():
+        copy.start()
+    chip = {}
+    for i in order:
+        core[i].wait_recv()
+        at = pl.ds(i * rows, rows)
+        total = in_ref[at, :].astype(F32) + core_ref[at, :].astype(F32)
+        held_ref[at, :] = total.astype(BF)
+        if i:
+            chip[i] = send(block(held_ref, i), block(chip_ref, i), count + i, chips[i])
+            chip[i].start()
+    total = held_ref[pl.ds(0, rows), :].astype(F32)
+    for i in chip:
+        chip[i].wait_recv()
+        total += chip_ref[pl.ds(i * rows, rows), :].astype(F32)
+    out_ref[...] = total.astype(BF)
+    for copy in [*core.values(), *chip.values()]:
+        copy.wait_send()
+
+
+def reduce_rows(partial, number):
+    size = lax.axis_size("rep")
+    rows, width = partial.shape[0] // size, partial.shape[1]
+    half = pltpu.VMEM((size // 2 * rows, width), BF)
+    return pl.pallas_call(
+        functools.partial(reduce_kernel, peers()),
+        out_shape=jax.ShapeDtypeStruct((rows, width), BF),
+        in_specs=[pl.BlockSpec(memory_space=pltpu.VMEM)],
+        out_specs=pl.BlockSpec(memory_space=pltpu.VMEM),
+        scratch_shapes=[
+            half,
+            half,
+            half,
+            pltpu.SemaphoreType.DMA((size,)),
+            pltpu.SemaphoreType.DMA((size,)),
+        ],
+        compiler_params=pltpu.CompilerParams(
+            collective_id=number, has_side_effects=True, vmem_limit_bytes=24 << 20
+        ),
+        cost_estimate=pl.CostEstimate(
+            flops=0, bytes_accessed=30 * partial.size, transcendentals=0
+        ),
+        name="reduce_rows",
+    )(partial)
 
 
 def jump(value, offset):
@@ -617,13 +752,10 @@
     root_two = lax.rsqrt(jnp.mean(hidden * hidden, axis=-1, keepdims=True) + EPSILON)
     normed_two = (hidden * root_two * gain_two).astype(BF)
 
-    disp_flow = Flow(copies_steps(mm(pick, normed_two).astype(BF), straight_steps))
-    slot_grad, gate_up = stage([disp_flow], (slot_grad, gate_up))
-    slot_flow = Flow(copies_steps(slot_grad, straight_steps))
-    stage([disp_flow])
-    dispatched = jnp.concatenate(finish(disp_flow), axis=0)
+    dispatched = gather_rows(mm(pick, normed_two).astype(BF), 0)
     act = mm(dispatched, gate_up)
-    all_slot_grad = jnp.concatenate(finish(slot_flow), axis=0)
+    slot_grad, act = lax.optimization_barrier((slot_grad, act))
+    all_slot_grad = gather_rows(slot_grad, 0)
     gate_act, up_act = act[:, :units], act[:, units:]
     sigmoid = jax.nn.sigmoid(gate_act)
     silu = gate_act * sigmoid
@@ -632,18 +764,16 @@
     grad_gate_act = (grad_inner * up_act * sigmoid * (1.0 + gate_act * (1.0 - sigmoid))).astype(BF)
     grad_up_act = (grad_inner * silu).astype(BF)
     grad_act = jnp.concatenate([grad_gate_act, grad_up_act], axis=1)
-    back_flow = Flow(plane_sum_steps(mm_nt(grad_act, gate_up).astype(BF)))
-    grad_gate = stage([back_flow], mm_tn(grad_gate_act, dispatched).astype(BF))
+    grad_gate, back = lax.optimization_barrier(
+        (mm_tn(grad_gate_act, dispatched).astype(BF), mm_nt(grad_act, gate_up).astype(BF))
+    )
+    grad_disp = reduce_rows(back, 1)
     expert_flow = Flow(plane_sum_steps(mm(inner, down).astype(BF)))
-    grad_up, grad_down = stage(
-        [back_flow, expert_flow],
-        (mm_tn(grad_up_act, dispatched).astype(BF), mm_tn(inner, all_slot_grad).astype(BF)),
-    )
-    sums = [
-        lax.psum_scatter(g, "shard", scatter_dimension=1, tiled=True)
-        for g in (grad_gate, grad_up, grad_down)
-    ]
-    grad_normed_two = mm_tn(pick, finish(back_flow))
+    grad_up, grad_down = (
+        mm_tn(grad_up_act, dispatched).astype(BF),
+        mm_tn(inner, all_slot_grad).astype(BF),
+    )
+    grad_normed_two = mm_tn(pick, grad_disp)
     grad_gain_two, through = norm_back(grad_normed_two, hidden, root_two, gain_two)
     grad_hidden = upstream + through
 
@@ -663,8 +793,14 @@
             lins[d], grad_qkv_w[d] = lin, grad
 
     far, near = offsets[-1:], offsets[1:-1]
-    values, both_grad = stage([expert_flow], (run_back(*far), both_grad))
+    values, both_grad, grad_up, grad_down = stage(
+        [expert_flow], (run_back(*far), both_grad, grad_up, grad_down)
+    )
     keep(far, values)
+    sums = [
+        lax.psum_scatter(g, "shard", scatter_dimension=1, tiled=True)
+        for g in (grad_gate, grad_up, grad_down)
+    ]
     qkv_flow = Flow(scatter_steps(grad_qkv_w))
     values, both_grad = stage([qkv_flow], (run_back(*near), both_grad))
     keep(near, values)

time: 754 us -> 786 us (1.042)
  Pallas kernels: 161 us -> 260 us
  waiting for transfers between devices: 253 us -> 206 us
  starting transfers between devices: 77.8 us -> 64.8 us
    pallas_call x0 -> x3, Pallas kernels: none -> 86.9 us  [the longest x2 58.2 us: gather_rows(): pl.pallas_call(functools.partial(gather_kernel, peers()), out_shape=jax.S...]
    ppermute x18 -> x9, waiting for transfers between devices: 68.3 us -> 42.9 us  [jump(): return lax.ppermute(value, 'rep', [(i, i ^ offset) for i in range(size)])]
    all_gather x1, waiting for transfers between devices: 17.2 us -> 0.01 us  [per_device(): down = lax.all_gather(own_down, 'shard', axis=1, tiled=True)]
    ppermute x2, waiting for transfers between devices: 18.9 us -> 3.15 us  [per_device(): piece, other = stage(flows, (lax.ppermute(piece, 'shard', ring), other))]
    ppermute x52 -> x49, waiting for transfers between devices: 133 us -> 146 us  [swap(): return lax.ppermute(value, 'rep', [(i, i ^ bit) for i in range(size)])]
    pallas_call x4, Pallas kernels: 42.3 us -> 55 us  [attend(): pl.pallas_call(functools.partial(attend_kernel, parts), grid_spec=pltpu.P...]
    ppermute x18 -> x9, starting transfers between devices: 21.1 us -> 10.9 us  [jump(): return lax.ppermute(value, 'rep', [(i, i ^ offset) for i in range(size)])]
    ppermute x52 -> x49, starting transfers between devices: 43.2 us -> 40 us  [swap(): return lax.ppermute(value, 'rep', [(i, i ^ bit) for i in range(size)])]
  transfers between devices with their start and end apart: 88 -> 76, of which waited for: 28 -> 26; matrix products, arithmetic and copies ran while one was open for 22% -> 19% of each run, Pallas kernels for 22% -> 33%
where the time goes in v8:
time: 786 us; the launch traced here: 779 us
  Pallas kernels  260 us (33%)
  waiting for transfers between devices  206 us (26%)
  local copies, waits for them, and re-layouts  92.9 us (12%)
  matrix products  73.9 us (9%)
  other arithmetic  65.4 us (8%)
  starting transfers between devices  64.8 us (8%)
  between operations  15.6 us (2%)
    ppermute x49, waiting for transfers between devices, swap(): return lax.ppermute(value, 'rep', [(i, i ^ bit) for i in range(size)])  146 us
    pallas_call x4, Pallas kernels, attend_back(): pl.pallas_call(attend_back_kernel, grid=(rows // length,), in_specs=[by_s...  68.2 us
    unnamed x226, local copies, waits for them, and re-layouts  59.8 us
    pallas_call x2, Pallas kernels, gather_rows(): pl.pallas_call(functools.partial(gather_kernel, peers()), out_shape=jax.S...  58.2 us
    pallas_call x4, Pallas kernels, attend(): pl.pallas_call(functools.partial(attend_kernel, parts), grid_spec=pltpu.P...  55 us
    ppermute x9, waiting for transfers between devices, jump(): return lax.ppermute(value, 'rep', [(i, i ^ offset) for i in range(size)])  42.9 us
    ppermute x49, starting transfers between devices, swap(): return lax.ppermute(value, 'rep', [(i, i ^ bit) for i in range(size)])  40 us
    pallas_call x1, Pallas kernels, reduce_rows(): pl.pallas_call(functools.partial(reduce_kernel, peers()), out_shape=jax.S...  28.7 us
  transfers between devices with their start and end apart: 76, of which 26 were waited for; matrix products, arithmetic and copies ran while one was open for 19% of the time, Pallas kernels for 33%

profile of v8, /device:TPU:0, one launch (start us, length us, event | category | flops | bytes accessed | tf_op | source)
XLA Modules:
  0.0 778.6 jit_solution(2047239781949908746)
XLA Ops:
  8.8 5.1 collective-permute-start
  16.9 2.7 constant_dynamic-slice_fusion.4
  19.6 2.5 collective-permute-start.3
  22.2 2.3 constant_dynamic-slice_fusion.15
  27.2 12.9 %collective-permute-done.3.refs_5_ = bf16[512,768]{1,0:T(8,128)(2,1)} collective-permute-done((bf16[512,768]{1,0:T(8,128)(2,1)S(1)}, bf16[512,768]{1,0:T(8,128)(2,1)}, u32[]{:S(2)}, u32[]{:S(2)}) %collective-permute-start.3) | collective-permute-done | bytes 786464 | tf_op jit(solution)/shard_map/ppermute | solution.py:703
  46.2 16.4 %collective-permute-done.5.refs_5_.refs_9_ = bf16[512,768]{1,0:T(8,128)(2,1)S(1)} collective-permute-done((bf16[512,768]{1,0:T(8,128)(2,1)}, bf16[512,768]{1,0:T(8,128)(2,1)S(1)}, u32[]{:S(2)}, u32[]{:S(2)}) %collective-permute-start.5) | collective-permute-done | bytes 786464 | tf_op jit(solution)/shard_map/ppermute | solution.py:33
  63.8 3.1 collective-permute-done.7.refs_6_
  75.3 18.8 %collective-permute-done.10 = bf16[256,768]{1,0:T(8,128)(2,1)} collective-permute-done((bf16[256,768]{1,0:T(8,128)(2,1)}, bf16[256,768]{1,0:T(8,128)(2,1)}, u32[]{:S(2)}, u32[]{:S(2)}) %collective-permute-start.10) | collective-permute-done | bytes 393248 | tf_op jit(solution)/shard_map/ppermute | solution.py:33
  108.1 2.2 pad_maximum_fusion.refs_0_.refs_1_.refs_2_.refs_3_.x_ref
  112.6 11.1 %attend.4 = (bf16[1024,256]{1,0:T(8,128)(2,1)S(1)}, bf16[1024,768]{1,0:T(8,128)(2,1)S(1)}, f32[1024,2]{1,0:T(8,128)S(1)}) custom-call(s32[1]{0:T(128)} %bitcast.1.z_ref, bf16[1024,2048]{1,0:T(8,128)(2,1)S(1)} %pad_maximum_fusion.refs_0_.refs_1_.refs_2_.refs_3_.x_ref, bf16[1024,2048]{1,0:T(8,128)(2,1)S(1)} %pad_maximum_fusion.refs_0_.refs_1_.refs_2_.refs_3_.x_ref, ...), custom_call_target="tpu_custom_call" | custom-call | flops 3758096384 | bytes 10485760 | tf_op jit(solution)/shard_map/attend/pallas_call | solution.py:398
  125.7 2.3 collective-permute-done.14
  137.0 2.2 copy-done.3
  140.3 10.7 %attend.5 = (bf16[1024,256]{1,0:T(8,128)(2,1)S(1)}, bf16[1024,768]{1,0:T(8,128)(2,1)S(1)}, f32[1024,2]{1,0:T(8,128)S(1)}) custom-call(s32[1]{0:T(128)} %bitcast.1.z_ref, bf16[1024,2048]{1,0:T(8,128)(2,1)S(1)} %copy-done.3, bf16[1024,2048]{1,0:T(8,128)(2,1)S(1)} %copy-done.3, bf16[1024,2048]{1,0:T(8,128)(2,1)S(1)} %copy-done.3, ...), custom_call_target="tpu_custom_call" | custom-call | flops 3758096384 | bytes 10485760 | tf_op jit(solution)/shard_map/attend/pallas_call | solution.py:398
  153.8 10.7 %attend.6 = (bf16[1024,256]{1,0:T(8,128)(2,1)S(1)}, bf16[1024,768]{1,0:T(8,128)(2,1)S(1)}, f32[1024,2]{1,0:T(8,128)S(1)}) custom-call(s32[1]{0:T(128)} %bitcast.1.z_ref, bf16[1024,2048]{1,0:T(8,128)(2,1)S(1)} %copy-done.3, bf16[1024,2048]{1,0:T(8,128)(2,1)S(1)} %copy-done.3, bf16[1024,2048]{1,0:T(8,128)(2,1)S(1)} %copy-done.3, ...), custom_call_target="tpu_custom_call" | custom-call | flops 3758096384 | bytes 10485760 | tf_op jit(solution)/shard_map/attend/pallas_call | solution.py:398
  167.2 22.6 %attend.7 = (bf16[1024,256]{1,0:T(8,128)(2,1)S(1)}, bf16[1024,768]{1,0:T(8,128)(2,1)S(1)}, f32[1024,2]{1,0:T(8,128)S(1)}) custom-call(s32[1]{0:T(128)} %bitcast.1.z_ref, bf16[1024,2048]{1,0:T(8,128)(2,1)S(1)} %copy-done.3, bf16[1024,2048]{1,0:T(8,128)(2,1)S(1)} %copy-done.3, bf16[1024,2048]{1,0:T(8,128)(2,1)S(1)} %copy-done.3, ...), custom_call_target="tpu_custom_call" | custom-call | flops 3758096384 | bytes 10485760 | tf_op jit(solution)/shard_map/attend/pallas_call | solution.py:398
  192.6 6.8 collective-permute-done.22
  201.4 6.2 fusion.46
  207.7 3.4 copy-done.61
  213.2 2.2 fusion.15.in_ref
  217.2 4.0 multiply_reduce_fusion.2
  224.0 29.0 %gather_rows.2 = bf16[1024,2048]{1,0:T(8,128)(2,1)S(1)} custom-call(bf16[128,2048]{1,0:T(8,128)(2,1)S(1)} %convolution_convert_fusion.6.in_ref), custom_call_target="tpu_custom_call" | custom-call | bytes 62914560 | tf_op jit(solution)/shard_map/gather_rows/pallas_call | solution.py:153
  254.9 11.7 %fusion.47 = f32[1024,1408]{1,0:T(8,128)} fusion(bf16[1024,2048]{1,0:T(8,128)(2,1)} %copy-done.4, bf16[2048,1408]{1,0:T(8,128)(2,1)} %all-gather.7.cloned.1.call-done), kind=kOutput, calls=%fused_computation.175 | convolution fusion | flops 5905580032 | bytes 15728640 | tf_op jit(solution)/shard_map/dot_general | solution.py:20
  266.6 29.2 %gather_rows.3 = bf16[1024,2048]{1,0:T(8,128)(2,1)S(1)} custom-call(bf16[128,2048]{1,0:T(8,128)(2,1)S(1)} %fusion.15.in_ref), custom_call_target="tpu_custom_call" | custom-call | bytes 62914560 | tf_op jit(solution)/shard_map/gather_rows/pallas_call | solution.py:153
  297.9 10.8 %multiply_convert_fusion.2 = (bf16[1024,704]{1,0:T(8,128)(2,1)}, bf16[1024,704]{1,0:T(8,128)(2,1)S(1)}, bf16[1024,704]{1,0:T(8,128)(2,1)}) fusion(f32[1024,1408]{1,0:T(8,128)} %fusion.47, bf16[1024,2048]{1,0:T(8,128)(2,1)} %copy-done.6, bf16[704,2048]{1,0:T(8,128)(2,1)} %all-gather.9.cloned.1.call-done), kind=kOutput, calls=%fused_computation.41 | convolution fusion | flops 2963603456 | bytes 17170432 | tf_op jit(solution)/shard_map/dot_general | solution.py:24
  309.8 4.5 convolution_convert_fusion.5
  314.3 11.0 %convolution_convert_fusion.in_ref = bf16[1024,2048]{1,0:T(8,128)(2,1)} fusion(bf16[2048,1408]{1,0:T(8,128)(2,1)} %all-gather.7.cloned.1.call-done, bf16[1024,704]{1,0:T(8,128)(2,1)} %get-tuple-element.289, bf16[1024,704]{1,0:T(8,128)(2,1)} %copy-done.97), kind=kOutput, calls=%fused_computation.30 | convolution fusion | flops 5913444352 | bytes 12845056 | tf_op jit(solution)/shard_map/dot_general | solution.py:24
  328.5 2.2 copy-done.8
  330.7 28.7 %reduce_rows.1 = bf16[128,2048]{1,0:T(8,128)(2,1)S(1)} custom-call(bf16[1024,2048]{1,0:T(8,128)(2,1)S(1)} %copy-done.8), custom_call_target="tpu_custom_call" | custom-call | bytes 62914560 | tf_op jit(solution)/shard_map/reduce_rows/pallas_call | solution.py:218
  361.1 4.1 multiply_convert_fusion
  365.4 3.6 convolution_convert_fusion.1
  374.0 4.6 convolution_convert_fusion.3
  378.5 7.5 convolution_convert_fusion.4
  386.0 4.9 pad_maximum_fusion.1.grad_ref
  390.9 16.9 %attend_back.4 = (bf16[1024,768]{1,0:T(8,128)(2,1)S(1)}, bf16[1024,768]{1,0:T(8,128)(2,1)S(1)}, bf16[1024,768]{1,0:T(8,128)(2,1)}) custom-call(bf16[1024,2048]{1,0:T(8,128)(2,1)} %pad_maximum_fusion.1.grad_ref, bf16[256,2048]{1,0:T(8,128)(2,1)S(1)} %copy-done.31, bf16[1024,768]{1,0:T(8,128)(2,1)} %copy-done.35, f32[1024,2]{1,0:T(8,128)S(1)} %copy-done.44, ...), custom_call_target="tpu_custom_call" | custom-call | flops 5637144576 | bytes 15728640 | tf_op jit(solution)/shard_map/attend_back/pallas_call | solution.py:487
  414.0 17.3 %attend_back.5 = (bf16[1024,768]{1,0:T(8,128)(2,1)S(1)}, bf16[1024,768]{1,0:T(8,128)(2,1)S(1)}, bf16[1024,768]{1,0:T(8,128)(2,1)}) custom-call(bf16[1024,2048]{1,0:T(8,128)(2,1)} %pad_maximum_fusion.1.grad_ref, bf16[256,2048]{1,0:T(8,128)(2,1)S(1)} %copy-done.18, bf16[1024,768]{1,0:T(8,128)(2,1)} %copy-done.34, f32[1024,2]{1,0:T(8,128)S(1)} %copy-done.42, ...), custom_call_target="tpu_custom_call" | custom-call | flops 5637144576 | bytes 15728640 | tf_op jit(solution)/shard_map/attend_back/pallas_call | solution.py:487
  433.6 16.9 %attend_back.6 = (bf16[1024,768]{1,0:T(8,128)(2,1)S(1)}, bf16[1024,768]{1,0:T(8,128)(2,1)S(1)}, bf16[1024,768]{1,0:T(8,128)(2,1)}) custom-call(bf16[1024,2048]{1,0:T(8,128)(2,1)} %pad_maximum_fusion.1.grad_ref, bf16[256,2048]{1,0:T(8,128)(2,1)S(1)} %copy-done.16, bf16[1024,768]{1,0:T(8,128)(2,1)} %copy-done.33, f32[1024,2]{1,0:T(8,128)S(1)} %copy-done.40, ...), custom_call_target="tpu_custom_call" | custom-call | flops 5637144576 | bytes 15728640 | tf_op jit(solution)/shard_map/attend_back/pallas_call | solution.py:487
  451.6 3.5 add_convert_fusion.4
  456.1 3.3 add_convert_fusion.5
  460.2 7.7 convolution_convert_fusion.2
  467.9 17.1 %attend_back.7 = (bf16[1024,768]{1,0:T(8,128)(2,1)S(1)}, bf16[1024,768]{1,0:T(8,128)(2,1)S(1)}, bf16[1024,768]{1,0:T(8,128)(2,1)}) custom-call(bf16[1024,2048]{1,0:T(8,128)(2,1)} %pad_maximum_fusion.1.grad_ref, bf16[256,2048]{1,0:T(8,128)(2,1)S(1)} %copy-done.30, bf16[1024,768]{1,0:T(8,128)(2,1)} %copy-done.32, f32[1024,2]{1,0:T(8,128)S(1)} %copy-done.38, ...), custom_call_target="tpu_custom_call" | custom-call | flops 5637144576 | bytes 15728640 | tf_op jit(solution)/shard_map/attend_back/pallas_call | solution.py:487
  488.0 22.9 %normed_back.1 = (f32[512,2048]{1,0:T(8,128)}, bf16[512,2048]{1,0:T(8,128)(2,1)}) custom-call(s32[1]{0:T(128)} %bitcast.1.z_ref, bf16[1024,768]{1,0:T(8,128)(2,1)} %copy-done.48, bf16[1024,768]{1,0:T(8,128)(2,1)} %copy-done.47, bf16[1024,768]{1,0:T(8,128)(2,1)} %copy-done.46, bf16[1024,768]{1,0:T(8,128)(2,1)} %copy-done.45, ...), custom_call_target="tpu_custom_call" | custom-call | flops 12884901888 | bytes 27262976 | tf_op jit(solution)/shard_map/normed_back/pallas_call | solution.py:543
  510.9 9.3 %collective-permute-done.30 = bf16[1024,768]{1,0:T(8,128)(2,1)} collective-permute-done((bf16[1024,768]{1,0:T(8,128)(2,1)}, bf16[1024,768]{1,0:T(8,128)(2,1)}, u32[]{:S(2)}, u32[]{:S(2)}) %collective-permute-start.30) | collective-permute-done | bytes 1572896 | tf_op jit(solution)/shard_map/ppermute | solution.py:33
  520.3 3.1 add_convert_fusion.3
  534.7 22.6 %collective-permute-done.35 = bf16[128,2048]{1,0:T(8,128)(2,1)S(1)} collective-permute-done((bf16[128,2048]{1,0:T(8,128)(2,1)S(1)}, bf16[128,2048]{1,0:T(8,128)(2,1)S(1)}, u32[]{:S(2)}, u32[]{:S(2)}) %collective-permute-start.35) | collective-permute-done | bytes 524320 | tf_op jit(solution)/shard_map/ppermute | solution.py:33
  561.7 3.4 fusion.9
  565.1 4.2 fusion.6
  569.4 2.8 collective-permute-done.33
  573.3 5.9 collective-permute-done.40
  585.6 24.2 %collective-permute-done.42 = bf16[128,2048]{1,0:T(8,128)(2,1)S(1)} collective-permute-done((bf16[128,2048]{1,0:T(8,128)(2,1)S(1)}, bf16[128,2048]{1,0:T(8,128)(2,1)S(1)}, u32[]{:S(2)}, u32[]{:S(2)}) %collective-permute-start.42) | collective-permute-done | bytes 524320 | tf_op jit(solution)/shard_map/ppermute | solution.py:33
  612.7 2.2 add_convert_fusion.8
  624.1 28.2 %collective-permute-done.53 = f32[2,2048]{1,0:T(2,128)S(1)} collective-permute-done((f32[2,2048]{1,0:T(2,128)S(1)}, f32[2,2048]{1,0:T(2,128)S(1)}, u32[]{:S(2)}, u32[]{:S(2)}) %collective-permute-start.53) | collective-permute-done | bytes 16416 | tf_op jit(solution)/shard_map/ppermute | solution.py:33
  655.1 5.0 place_turned.2
  672.0 2.5 add_convert_fusion.1
  678.3 12.1 %collective-permute-done.60 = bf16[128,2048]{1,0:T(8,128)(2,1)S(1)} collective-permute-done((bf16[128,2048]{1,0:T(8,128)(2,1)S(1)}, bf16[128,2048]{1,0:T(8,128)(2,1)S(1)}, u32[]{:S(2)}, u32[]{:S(2)}) %collective-permute-start.60) | collective-permute-done | bytes 524320 | tf_op jit(solution)/shard_map/ppermute | solution.py:242
  690.8 4.3 collective-permute-done.61
  695.1 17.6 %collective-permute-done.62 = bf16[128,2048]{1,0:T(8,128)(2,1)S(1)} collective-permute-done((bf16[128,2048]{1,0:T(8,128)(2,1)S(1)}, bf16[128,2048]{1,0:T(8,128)(2,1)S(1)}, u32[]{:S(2)}, u32[]{:S(2)}) %collective-permute-start.62) | collective-permute-done | bytes 524320 | tf_op jit(solution)/shard_map/ppermute | solution.py:242
  714.3 2.2 collective-permute-start.58
  719.3 2.5 collective-permute-done.56
  721.9 6.4 collective-permute-done.57
  734.1 2.4 collective-permute-start.65
  737.9 11.0 %place.2 = (f32[512,2048]{1,0:T(8,128)}, f32[512,2048]{1,0:T(8,128)}, f32[512,2048]{1,0:T(8,128)}) custom-call(s32[1]{0:T(128)} %bitcast.6.me_ref, bf16[2048,768]{1,0:T(8,128)(2,1)} %copy-done.60, bf16[2048,768]{1,0:T(8,128)(2,1)} %copy-done.65), custom_call_target="tpu_custom_call" | custom-call | bytes 25165824 | tf_op jit(solution)/shard_map/place/pallas_call | solution.py:604
  750.7 5.0 place_turned.3
  755.7 6.5 place.3
  762.8 8.9 %convert_element_type.237 = f32[5632,512]{1,0:T(8,128)} convert(bf16[5632,512]{1,0:T(8,128)(2,1)} %all-gather.11.cloned.1.call-done) | non-fusion elementwise | flops 2883584 | bytes 17301504 | tf_op jit(solution)/shard_map/convert_element_type | solution.py:845
  (435 shorter events, 165.2 us)
Async XLA Ops:
  7.2 121.5 %all-gather.5.cloned.1.call-start = ((), (), s32[]{:S(2)}) async-start(), calls=%async_computation.5 | async-start | bytes 1310720 | tf_op jit(solution)/shard_map/all_gather | solution.py:721
  8.8 18.4 %collective-permute-start = (bf16[2,512]{1,0:T(2,128)(2,1)S(1)}, bf16[2,512]{1,0:T(2,128)(2,1)S(1)}, u32[]{:S(2)}, u32[]{:S(2)}) collective-permute-start(bf16[2,512]{1,0:T(2,128)(2,1)S(1)} %get-tuple-element.286), channel_id=1, source_target_pairs={{0,3},{1,0},{2,1},{3,2},{4,7},{5,4},{6,5},{7,6},{8,11},{9,8},{10,9... | collective-permute-start | bytes 6152 | tf_op jit(solution)/shard_map/ppermute | solution.py:319
  19.6 20.4 %collective-permute-start.3 = (bf16[512,768]{1,0:T(8,128)(2,1)S(1)}, bf16[512,768]{1,0:T(8,128)(2,1)}, u32[]{:S(2)}, u32[]{:S(2)}) collective-permute-start(bf16[512,768]{1,0:T(8,128)(2,1)S(1)} %pad_maximum_fusion.6.refs_4_), channel_id=1, source_target_pairs={{0,1},{1,2},{2,3},{3,0},{4,5},{5,6},{6,7},{7,4},{8,9},{9,10},{10,1... | collective-permute-start | bytes 2359304 | tf_op jit(solution)/shard_map/ppermute | solution.py:703
  42.3 24.6 %collective-permute-start.8 = (bf16[512,2048]{1,0:T(8,128)(2,1)S(1)}, bf16[512,2048]{1,0:T(8,128)(2,1)S(1)}, u32[]{:S(2)}, u32[]{:S(2)}) collective-permute-start(bf16[512,2048]{1,0:T(8,128)(2,1)S(1)} %fusion.2), channel_id=1, source_target_pairs={{0,4},{4,0},{8,12},{12,8},{16,20},{20,16},{24,28},{28,24},{1,5},{5... | collective-permute-start | bytes 6291464 | tf_op jit(solution)/shard_map/ppermute | solution.py:33
  42.4 20.2 %collective-permute-start.5 = (bf16[512,768]{1,0:T(8,128)(2,1)}, bf16[512,768]{1,0:T(8,128)(2,1)S(1)}, u32[]{:S(2)}, u32[]{:S(2)}) collective-permute-start(bf16[512,768]{1,0:T(8,128)(2,1)} %collective-permute-done.3.refs_5_), channel_id=1, source_target_pairs={{0,8},{4,12},{8,0},{12,4},{16,24},{20,28},{24,16},{28,20},{1,9},{5... | collective-permute-start | bytes 2359304 | tf_op jit(solution)/shard_map/ppermute | solution.py:33
  44.0 19.8 %collective-permute-start.6 = (bf16[512,768]{1,0:T(8,128)(2,1)}, bf16[512,768]{1,0:T(8,128)(2,1)S(1)}, u32[]{:S(2)}, u32[]{:S(2)}) collective-permute-start(bf16[512,768]{1,0:T(8,128)(2,1)} %collective-permute-done.3.refs_5_), channel_id=1, source_target_pairs={{0,16},{4,20},{8,24},{12,28},{16,0},{20,4},{24,8},{28,12},{1,17},{... | collective-permute-start | bytes 2359304 | tf_op jit(solution)/shard_map/ppermute | solution.py:33
  45.5 21.4 %collective-permute-start.7 = (bf16[512,768]{1,0:T(8,128)(2,1)}, bf16[512,768]{1,0:T(8,128)(2,1)}, u32[]{:S(2)}, u32[]{:S(2)}) collective-permute-start(bf16[512,768]{1,0:T(8,128)(2,1)} %collective-permute-done.3.refs_5_), channel_id=1, source_target_pairs={{0,1},{1,2},{2,3},{3,0},{4,5},{5,6},{6,7},{7,4},{8,9},{9,10},{10,1... | collective-permute-start | bytes 2359304 | tf_op jit(solution)/shard_map/ppermute | solution.py:717
  66.9 27.5 %collective-permute-start.11 = (bf16[512,768]{1,0:T(8,128)(2,1)}, bf16[512,768]{1,0:T(8,128)(2,1)}, u32[]{:S(2)}, u32[]{:S(2)}) collective-permute-start(bf16[512,768]{1,0:T(8,128)(2,1)} %collective-permute-done.7.refs_6_), channel_id=1, source_target_pairs={{0,8},{4,12},{8,0},{12,4},{16,24},{20,28},{24,16},{28,20},{1,9},{5... | collective-permute-start | bytes 2359304 | tf_op jit(solution)/shard_map/ppermute | solution.py:33
  67.5 26.9 %collective-permute-start.12 = (bf16[512,768]{1,0:T(8,128)(2,1)}, bf16[512,768]{1,0:T(8,128)(2,1)}, u32[]{:S(2)}, u32[]{:S(2)}) collective-permute-start(bf16[512,768]{1,0:T(8,128)(2,1)} %collective-permute-done.7.refs_6_), channel_id=1, source_target_pairs={{0,16},{4,20},{8,24},{12,28},{16,0},{20,4},{24,8},{28,12},{1,17},{... | collective-permute-start | bytes 2359304 | tf_op jit(solution)/shard_map/ppermute | solution.py:33
  68.0 26.4 %collective-permute-start.13 = (bf16[512,768]{1,0:T(8,128)(2,1)}, bf16[512,768]{1,0:T(8,128)(2,1)}, u32[]{:S(2)}, u32[]{:S(2)}) collective-permute-start(bf16[512,768]{1,0:T(8,128)(2,1)} %collective-permute-done.7.refs_6_), channel_id=1, source_target_pairs={{0,1},{1,2},{2,3},{3,0},{4,5},{5,6},{6,7},{7,4},{8,9},{9,10},{10,1... | collective-permute-start | bytes 2359304 | tf_op jit(solution)/shard_map/ppermute | solution.py:717
  68.7 25.4 %collective-permute-start.10 = (bf16[256,768]{1,0:T(8,128)(2,1)}, bf16[256,768]{1,0:T(8,128)(2,1)}, u32[]{:S(2)}, u32[]{:S(2)}) collective-permute-start(bf16[256,768]{1,0:T(8,128)(2,1)} %slice.110), channel_id=1, source_target_pairs={{0,8},{4,12},{8,0},{12,4},{16,24},{20,28},{24,16},{28,20},{1,9},{5... | collective-permute-start | bytes 1179656 | tf_op jit(solution)/shard_map/ppermute | solution.py:33
  71.0 23.4 %collective-permute-start.9 = (bf16[256,768]{1,0:T(8,128)(2,1)}, bf16[256,768]{1,0:T(8,128)(2,1)}, u32[]{:S(2)}, u32[]{:S(2)}) collective-permute-start(bf16[256,768]{1,0:T(8,128)(2,1)} %slice.109), channel_id=1, source_target_pairs={{0,16},{4,20},{8,24},{12,28},{16,0},{20,4},{24,8},{28,12},{1,17},{... | collective-permute-start | bytes 1179656 | tf_op jit(solution)/shard_map/ppermute | solution.py:33
  94.5 160.5 %all-gather.7.cloned.1.call-start = ((), (), s32[]{:S(2)}) async-start(), calls=%async_computation.6 | async-start | bytes 7208960 | tf_op jit(solution)/shard_map/all_gather | solution.py:729
  95.2 202.7 %all-gather.9.cloned.1.call-start = ((), (), s32[]{:S(2)}) async-start(), calls=%async_computation.7 | async-start | bytes 3604480 | tf_op jit(solution)/shard_map/all_gather | solution.py:730
  100.8 27.9 %collective-permute-start.16 = (bf16[512,768]{1,0:T(8,128)(2,1)}, bf16[512,768]{1,0:T(8,128)(2,1)}, u32[]{:S(2)}, u32[]{:S(2)}) collective-permute-start(bf16[512,768]{1,0:T(8,128)(2,1)} %collective-permute-done.13.refs_7_), channel_id=1, source_target_pairs={{0,8},{4,12},{8,0},{12,4},{16,24},{20,28},{24,16},{28,20},{1,9},{5... | collective-permute-start | bytes 2359304 | tf_op jit(solution)/shard_map/ppermute | solution.py:33
  102.3 26.4 %collective-permute-start.17 = (bf16[512,768]{1,0:T(8,128)(2,1)}, bf16[512,768]{1,0:T(8,128)(2,1)}, u32[]{:S(2)}, u32[]{:S(2)}) collective-permute-start(bf16[512,768]{1,0:T(8,128)(2,1)} %collective-permute-done.13.refs_7_), channel_id=1, source_target_pairs={{0,16},{4,20},{8,24},{12,28},{16,0},{20,4},{24,8},{28,12},{1,17},{... | collective-permute-start | bytes 2359304 | tf_op jit(solution)/shard_map/ppermute | solution.py:33
  103.8 24.1 %collective-permute-start.14 = (bf16[256,768]{1,0:T(8,128)(2,1)S(1)}, bf16[256,768]{1,0:T(8,128)(2,1)S(1)}, u32[]{:S(2)}, u32[]{:S(2)}) collective-permute-start(bf16[256,768]{1,0:T(8,128)(2,1)S(1)} %slice.111), channel_id=1, source_target_pairs={{0,16},{4,20},{8,24},{12,28},{16,0},{20,4},{24,8},{28,12},{1,17},{... | collective-permute-start | bytes 1179656 | tf_op jit(solution)/shard_map/ppermute | solution.py:33
  106.5 22.2 %collective-permute-start.15 = (bf16[256,768]{1,0:T(8,128)(2,1)S(1)}, bf16[256,768]{1,0:T(8,128)(2,1)}, u32[]{:S(2)}, u32[]{:S(2)}) collective-permute-start(bf16[256,768]{1,0:T(8,128)(2,1)S(1)} %slice.112), channel_id=1, source_target_pairs={{0,8},{4,12},{8,0},{12,4},{16,24},{20,28},{24,16},{28,20},{1,9},{5... | collective-permute-start | bytes 1179656 | tf_op jit(solution)/shard_map/ppermute | solution.py:33
  128.7 61.1 %collective-permute-start.20 = (bf16[256,2048]{1,0:T(8,128)(2,1)}, bf16[256,2048]{1,0:T(8,128)(2,1)S(1)}, u32[]{:S(2)}, u32[]{:S(2)}) collective-permute-start(bf16[256,2048]{1,0:T(8,128)(2,1)} %all-gather.5.cloned.1.call-done.out_ref), channel_id=1, source_target_pairs={{0,8},{4,12},{8,0},{12,4},{16,24},{20,28},{24,16},{28,20},{1,9},{5... | collective-permute-start | bytes 3145736 | tf_op jit(solution)/shard_map/ppermute | solution.py:33
  129.4 60.4 %collective-permute-start.21 = (bf16[256,2048]{1,0:T(8,128)(2,1)}, bf16[256,2048]{1,0:T(8,128)(2,1)S(1)}, u32[]{:S(2)}, u32[]{:S(2)}) collective-permute-start(bf16[256,2048]{1,0:T(8,128)(2,1)} %all-gather.5.cloned.1.call-done.out_ref), channel_id=1, source_target_pairs={{0,16},{4,20},{8,24},{12,28},{16,0},{20,4},{24,8},{28,12},{1,17},{... | collective-permute-start | bytes 3145736 | tf_op jit(solution)/shard_map/ppermute | solution.py:33
  130.9 36.1 %collective-permute-start.18 = (bf16[256,768]{1,0:T(8,128)(2,1)S(1)}, bf16[256,768]{1,0:T(8,128)(2,1)S(1)}, u32[]{:S(2)}, u32[]{:S(2)}) collective-permute-start(bf16[256,768]{1,0:T(8,128)(2,1)S(1)} %slice.113), channel_id=1, source_target_pairs={{0,16},{4,20},{8,24},{12,28},{16,0},{20,4},{24,8},{28,12},{1,17},{... | collective-permute-start | bytes 1179656 | tf_op jit(solution)/shard_map/ppermute | solution.py:33
  133.6 33.5 %collective-permute-start.19 = (bf16[256,768]{1,0:T(8,128)(2,1)S(1)}, bf16[256,768]{1,0:T(8,128)(2,1)S(1)}, u32[]{:S(2)}, u32[]{:S(2)}) collective-permute-start(bf16[256,768]{1,0:T(8,128)(2,1)S(1)} %slice.114), channel_id=1, source_target_pairs={{0,8},{4,12},{8,0},{12,4},{16,24},{20,28},{24,16},{28,20},{1,9},{5... | collective-permute-start | bytes 1179656 | tf_op jit(solution)/shard_map/ppermute | solution.py:33
  212.7 307.5 %reduce-scatter.6.cloned.1.call-start = ((), (), s32[]{:S(2)}) async-start(), calls=%async_computation.8 | async-start | bytes 3604480 | tf_op jit(solution)/shard_map/reduce_scatter | solution.py:801
  325.4 194.8 %reduce-scatter.8.cloned.1.call-start = ((), (), s32[]{:S(2)}) async-start(), calls=%async_computation.9 | async-start | bytes 3604480 | tf_op jit(solution)/shard_map/reduce_scatter | solution.py:801
  365.2 20.8 %collective-permute-start.26 = (bf16[512,2048]{1,0:T(8,128)(2,1)}, bf16[512,2048]{1,0:T(8,128)(2,1)}, u32[]{:S(2)}, u32[]{:S(2)}) collective-permute-start(bf16[512,2048]{1,0:T(8,128)(2,1)} %get-tuple-element.281), channel_id=1, source_target_pairs={{0,4},{4,0},{8,12},{12,8},{16,20},{20,16},{24,28},{28,24},{1,5},{5... | collective-permute-start | bytes 6291464 | tf_op jit(solution)/shard_map/ppermute | solution.py:33
  372.6 37.6 %collective-permute-start.25 = (bf16[512,2048]{1,0:T(8,128)(2,1)}, bf16[512,2048]{1,0:T(8,128)(2,1)}, u32[]{:S(2)}, u32[]{:S(2)}) collective-permute-start(bf16[512,2048]{1,0:T(8,128)(2,1)} %slice.143), channel_id=1, source_target_pairs={{0,4},{4,0},{8,12},{12,8},{16,20},{20,16},{24,28},{28,24},{1,5},{5... | collective-permute-start | bytes 6291464 | tf_op jit(solution)/shard_map/ppermute | solution.py:33
  410.2 117.2 %reduce-scatter.10.cloned.1.call-start = ((), (), s32[]{:S(2)}) async-start(), calls=%async_computation.10 | async-start | bytes 3604480 | tf_op jit(solution)/shard_map/reduce_scatter | solution.py:801
  410.3 41.3 %collective-permute-start.27 = (bf16[1024,768]{1,0:T(8,128)(2,1)}, bf16[1024,768]{1,0:T(8,128)(2,1)}, u32[]{:S(2)}, u32[]{:S(2)}) collective-permute-start(bf16[1024,768]{1,0:T(8,128)(2,1)} %copy-done.36), channel_id=1, source_target_pairs={{0,8},{4,12},{8,0},{12,4},{16,24},{20,28},{24,16},{28,20},{1,9},{5... | collective-permute-start | bytes 4718600 | tf_op jit(solution)/shard_map/ppermute | solution.py:33
  411.4 40.2 %collective-permute-start.28 = (bf16[1024,768]{1,0:T(8,128)(2,1)}, bf16[1024,768]{1,0:T(8,128)(2,1)}, u32[]{:S(2)}, u32[]{:S(2)}) collective-permute-start(bf16[1024,768]{1,0:T(8,128)(2,1)} %get-tuple-element.191), channel_id=1, source_target_pairs={{0,16},{4,20},{8,24},{12,28},{16,0},{20,4},{24,8},{28,12},{1,17},{... | collective-permute-start | bytes 4718600 | tf_op jit(solution)/shard_map/ppermute | solution.py:33
  412.5 200.1 %reduce-scatter.12.cloned.1.call-start = ((), (), s32[]{:S(2)}) async-start(), calls=%async_computation.11 | async-start | bytes 3932160 | tf_op jit(solution)/shard_map/reduce_scatter | solution.py:816
  432.4 54.9 %collective-permute-start.32 = (bf16[1024,768]{1,0:T(8,128)(2,1)}, bf16[1024,768]{1,0:T(8,128)(2,1)S(1)}, u32[]{:S(2)}, u32[]{:S(2)}) collective-permute-start(bf16[1024,768]{1,0:T(8,128)(2,1)} %get-tuple-element.198), channel_id=1, source_target_pairs={{0,16},{4,20},{8,24},{12,28},{16,0},{20,4},{24,8},{28,12},{1,17},{... | collective-permute-start | bytes 4718600 | tf_op jit(solution)/shard_map/ppermute | solution.py:33
  450.5 37.4 %collective-permute-start.31 = (bf16[1024,768]{1,0:T(8,128)(2,1)S(1)}, bf16[1024,768]{1,0:T(8,128)(2,1)}, u32[]{:S(2)}, u32[]{:S(2)}) collective-permute-start(bf16[1024,768]{1,0:T(8,128)(2,1)S(1)} %get-tuple-element.195), channel_id=1, source_target_pairs={{0,8},{4,12},{8,0},{12,4},{16,24},{20,28},{24,16},{28,20},{1,9},{5... | collective-permute-start | bytes 4718600 | tf_op jit(solution)/shard_map/ppermute | solution.py:33
  455.1 65.1 %collective-permute-start.30 = (bf16[1024,768]{1,0:T(8,128)(2,1)}, bf16[1024,768]{1,0:T(8,128)(2,1)}, u32[]{:S(2)}, u32[]{:S(2)}) collective-permute-start(bf16[1024,768]{1,0:T(8,128)(2,1)} %add_convert_fusion.4), channel_id=1, source_target_pairs={{0,8},{4,12},{8,0},{12,4},{16,24},{20,28},{24,16},{28,20},{1,9},{5... | collective-permute-start | bytes 4718600 | tf_op jit(solution)/shard_map/ppermute | solution.py:33
  459.4 60.8 %collective-permute-start.29 = (bf16[1024,768]{1,0:T(8,128)(2,1)}, bf16[1024,768]{1,0:T(8,128)(2,1)}, u32[]{:S(2)}, u32[]{:S(2)}) collective-permute-start(bf16[1024,768]{1,0:T(8,128)(2,1)} %add_convert_fusion.5), channel_id=1, source_target_pairs={{0,16},{4,20},{8,24},{12,28},{16,0},{20,4},{24,8},{28,12},{1,17},{... | collective-permute-start | bytes 4718600 | tf_op jit(solution)/shard_map/ppermute | solution.py:33
  520.2 39.5 %collective-permute-start.39 = (bf16[512,2048]{1,0:T(8,128)(2,1)}, bf16[512,2048]{1,0:T(8,128)(2,1)}, u32[]{:S(2)}, u32[]{:S(2)}) collective-permute-start(bf16[512,2048]{1,0:T(8,128)(2,1)} %get-tuple-element.218), channel_id=1, source_target_pairs={{0,4},{4,0},{8,12},{12,8},{16,20},{20,16},{24,28},{28,24},{1,5},{5... | collective-permute-start | bytes 6291464 | tf_op jit(solution)/shard_map/ppermute | solution.py:33
  527.5 133.7 %reduce-scatter.14.cloned.1.call-start = ((), (), s32[]{:S(2)}) async-start(), calls=%async_computation.12 | async-start | bytes 1310720 | tf_op jit(solution)/shard_map/reduce_scatter | solution.py:832
  527.6 32.1 %collective-permute-start.37 = (bf16[704,512]{1,0:T(8,128)(2,1)}, bf16[704,512]{1,0:T(8,128)(2,1)S(1)}, u32[]{:S(2)}, u32[]{:S(2)}) collective-permute-start(bf16[704,512]{1,0:T(8,128)(2,1)} %reduce-scatter.6.cloned.1.call-done), channel_id=1, source_target_pairs={{0,8},{4,12},{8,0},{12,4},{16,24},{20,28},{24,16},{28,20},{1,9},{5... | collective-permute-start | bytes 2162696 | tf_op jit(solution)/shard_map/ppermute | solution.py:33
  528.7 31.0 %collective-permute-start.38 = (bf16[704,512]{1,0:T(8,128)(2,1)}, bf16[704,512]{1,0:T(8,128)(2,1)S(1)}, u32[]{:S(2)}, u32[]{:S(2)}) collective-permute-start(bf16[704,512]{1,0:T(8,128)(2,1)} %reduce-scatter.6.cloned.1.call-done), channel_id=1, source_target_pairs={{0,16},{4,20},{8,24},{12,28},{16,0},{20,4},{24,8},{28,12},{1,17},{... | collective-permute-start | bytes 2162696 | tf_op jit(solution)/shard_map/ppermute | solution.py:33
  532.2 25.2 %collective-permute-start.35 = (bf16[128,2048]{1,0:T(8,128)(2,1)S(1)}, bf16[128,2048]{1,0:T(8,128)(2,1)S(1)}, u32[]{:S(2)}, u32[]{:S(2)}) collective-permute-start(bf16[128,2048]{1,0:T(8,128)(2,1)S(1)} %get-tuple-element.297), channel_id=1, source_target_pairs={{0,8},{4,12},{8,0},{12,4},{16,24},{20,28},{24,16},{28,20},{1,9},{5... | collective-permute-start | bytes 1572872 | tf_op jit(solution)/shard_map/ppermute | solution.py:33
  532.4 26.0 %collective-permute-start.36 = (bf16[128,2048]{1,0:T(8,128)(2,1)S(1)}, bf16[128,2048]{1,0:T(8,128)(2,1)S(1)}, u32[]{:S(2)}, u32[]{:S(2)}) collective-permute-start(bf16[128,2048]{1,0:T(8,128)(2,1)S(1)} %get-tuple-element.296), channel_id=1, source_target_pairs={{0,16},{4,20},{8,24},{12,28},{16,0},{20,4},{24,8},{28,12},{1,17},{... | collective-permute-start | bytes 1572872 | tf_op jit(solution)/shard_map/ppermute | solution.py:33
  559.8 19.5 %collective-permute-start.40 = (bf16[352,512]{1,0:T(8,128)(2,1)S(1)}, bf16[352,512]{1,0:T(8,128)(2,1)S(1)}, u32[]{:S(2)}, u32[]{:S(2)}) collective-permute-start(bf16[352,512]{1,0:T(8,128)(2,1)S(1)} %slice.126), channel_id=1, source_target_pairs={{0,16},{4,20},{8,24},{12,28},{16,0},{20,4},{24,8},{28,12},{1,17},{... | collective-permute-start | bytes 1081352 | tf_op jit(solution)/shard_map/ppermute | solution.py:33
  560.6 18.6 %collective-permute-start.41 = (bf16[352,512]{1,0:T(8,128)(2,1)S(1)}, bf16[352,512]{1,0:T(8,128)(2,1)S(1)}, u32[]{:S(2)}, u32[]{:S(2)}) collective-permute-start(bf16[352,512]{1,0:T(8,128)(2,1)S(1)} %slice.127), channel_id=1, source_target_pairs={{0,8},{4,12},{8,0},{12,4},{16,24},{20,28},{24,16},{28,20},{1,9},{5... | collective-permute-start | bytes 1081352 | tf_op jit(solution)/shard_map/ppermute | solution.py:33
  579.3 31.8 %collective-permute-start.44 = (bf16[2816,512]{1,0:T(8,128)(2,1)S(1)}, bf16[2816,512]{1,0:T(8,128)(2,1)S(1)}, u32[]{:S(2)}, u32[]{:S(2)}) collective-permute-start(bf16[2816,512]{1,0:T(8,128)(2,1)S(1)} %constant_dynamic-update-slice_fusion.23.same_ref), channel_id=1, source_target_pairs={{0,4},{4,0},{8,12},{12,8},{16,20},{20,16},{24,28},{28,24},{1,5},{5... | collective-permute-start | bytes 8650760 | tf_op jit(solution)/shard_map/ppermute | solution.py:33
  579.4 30.5 %collective-permute-start.45 = (bf16[704,512]{1,0:T(8,128)(2,1)S(1)}, bf16[704,512]{1,0:T(8,128)(2,1)S(1)}, u32[]{:S(2)}, u32[]{:S(2)}) collective-permute-start(bf16[704,512]{1,0:T(8,128)(2,1)S(1)} %copy-done.77), channel_id=1, source_target_pairs={{0,8},{4,12},{8,0},{12,4},{16,24},{20,28},{24,16},{28,20},{1,9},{5... | collective-permute-start | bytes 2162696 | tf_op jit(solution)/shard_map/ppermute | solution.py:33
  580.4 30.3 %collective-permute-start.46 = (bf16[704,512]{1,0:T(8,128)(2,1)S(1)}, bf16[704,512]{1,0:T(8,128)(2,1)}, u32[]{:S(2)}, u32[]{:S(2)}) collective-permute-start(bf16[704,512]{1,0:T(8,128)(2,1)S(1)} %copy-done.77), channel_id=1, source_target_pairs={{0,16},{4,20},{8,24},{12,28},{16,0},{20,4},{24,8},{28,12},{1,17},{... | collective-permute-start | bytes 2162696 | tf_op jit(solution)/shard_map/ppermute | solution.py:33
  582.9 27.0 %collective-permute-start.42 = (bf16[128,2048]{1,0:T(8,128)(2,1)S(1)}, bf16[128,2048]{1,0:T(8,128)(2,1)S(1)}, u32[]{:S(2)}, u32[]{:S(2)}) collective-permute-start(bf16[128,2048]{1,0:T(8,128)(2,1)S(1)} %get-tuple-element.295), channel_id=1, source_target_pairs={{0,16},{4,20},{8,24},{12,28},{16,0},{20,4},{24,8},{28,12},{1,17},{... | collective-permute-start | bytes 1572872 | tf_op jit(solution)/shard_map/ppermute | solution.py:33
  584.7 25.2 %collective-permute-start.43 = (bf16[128,2048]{1,0:T(8,128)(2,1)S(1)}, bf16[128,2048]{1,0:T(8,128)(2,1)S(1)}, u32[]{:S(2)}, u32[]{:S(2)}) collective-permute-start(bf16[128,2048]{1,0:T(8,128)(2,1)S(1)} %get-tuple-element.294), channel_id=1, source_target_pairs={{0,8},{4,12},{8,0},{12,4},{16,24},{20,28},{24,16},{28,20},{1,9},{5... | collective-permute-start | bytes 1572872 | tf_op jit(solution)/shard_map/ppermute | solution.py:33
  615.9 146.8 %all-gather.11.cloned.1.call-start = ((), (), s32[]{:S(2)}) async-start(), calls=%async_computation.13 | async-start | bytes 6488064 | tf_op jit(solution)/shard_map/all_gather | solution.py:837
  616.0 45.2 %collective-permute-start.50 = (bf16[512,768]{1,0:T(8,128)(2,1)}, bf16[512,768]{1,0:T(8,128)(2,1)}, u32[]{:S(2)}, u32[]{:S(2)}) collective-permute-start(bf16[512,768]{1,0:T(8,128)(2,1)} %reduce-scatter.12.cloned.1.call-done), channel_id=1, source_target_pairs={{0,8},{4,12},{8,0},{12,4},{16,24},{20,28},{24,16},{28,20},{1,9},{5... | collective-permute-start | bytes 2359304 | tf_op jit(solution)/shard_map/ppermute | solution.py:242
  617.1 44.1 %collective-permute-start.51 = (bf16[512,768]{1,0:T(8,128)(2,1)}, bf16[512,768]{1,0:T(8,128)(2,1)}, u32[]{:S(2)}, u32[]{:S(2)}) collective-permute-start(bf16[512,768]{1,0:T(8,128)(2,1)} %reduce-scatter.12.cloned.1.call-done), channel_id=1, source_target_pairs={{0,16},{4,20},{8,24},{12,28},{16,0},{20,4},{24,8},{28,12},{1,17},{... | collective-permute-start | bytes 2359304 | tf_op jit(solution)/shard_map/ppermute | solution.py:242
  618.4 42.8 %collective-permute-start.52 = (bf16[512,768]{1,0:T(8,128)(2,1)}, bf16[512,768]{1,0:T(8,128)(2,1)}, u32[]{:S(2)}, u32[]{:S(2)}) collective-permute-start(bf16[512,768]{1,0:T(8,128)(2,1)} %reduce-scatter.12.cloned.1.call-done), channel_id=1, source_target_pairs={{0,24},{4,28},{8,16},{12,20},{16,8},{20,12},{24,0},{28,4},{1,25},{... | collective-permute-start | bytes 2359304 | tf_op jit(solution)/shard_map/ppermute | solution.py:242
  619.5 32.7 %collective-permute-start.53 = (f32[2,2048]{1,0:T(2,128)S(1)}, f32[2,2048]{1,0:T(2,128)S(1)}, u32[]{:S(2)}, u32[]{:S(2)}) collective-permute-start(f32[2,2048]{1,0:T(2,128)S(1)} %add.212), channel_id=1, source_target_pairs={{0,8},{4,12},{8,0},{12,4},{16,24},{20,28},{24,16},{28,20},{1,9},{5... | collective-permute-start | bytes 49160 | tf_op jit(solution)/shard_map/ppermute | solution.py:33
  621.7 38.7 %collective-permute-start.48 = (bf16[352,512]{1,0:T(8,128)(2,1)S(1)}, bf16[352,512]{1,0:T(8,128)(2,1)S(1)}, u32[]{:S(2)}, u32[]{:S(2)}) collective-permute-start(bf16[352,512]{1,0:T(8,128)(2,1)S(1)} %slice.130), channel_id=1, source_target_pairs={{0,16},{4,20},{8,24},{12,28},{16,0},{20,4},{24,8},{28,12},{1,17},{... | collective-permute-start | bytes 1081352 | tf_op jit(solution)/shard_map/ppermute | solution.py:33
  669.1 60.8 %collective-permute-start.55 = (bf16[2048,768]{1,0:T(8,128)(2,1)S(1)}, bf16[2048,768]{1,0:T(8,128)(2,1)S(1)}, u32[]{:S(2)}, u32[]{:S(2)}) collective-permute-start(bf16[2048,768]{1,0:T(8,128)(2,1)S(1)} %constant_dynamic-update-slice_fusion.33.same_ref), channel_id=1, source_target_pairs={{0,4},{4,0},{8,12},{12,8},{16,20},{20,16},{24,28},{28,24},{1,5},{5... | collective-permute-start | bytes 9437192 | tf_op jit(solution)/shard_map/ppermute | solution.py:33
  671.9 56.4 %collective-permute-start.54 = (bf16[2816,512]{1,0:T(8,128)(2,1)S(1)}, bf16[2816,512]{1,0:T(8,128)(2,1)S(1)}, u32[]{:S(2)}, u32[]{:S(2)}) collective-permute-start(bf16[2816,512]{1,0:T(8,128)(2,1)S(1)} %constant_dynamic-update-slice_fusion.28.same_ref), channel_id=1, source_target_pairs={{0,4},{4,0},{8,12},{12,8},{16,20},{20,16},{24,28},{28,24},{1,5},{5... | collective-permute-start | bytes 8650760 | tf_op jit(solution)/shard_map/ppermute | solution.py:33
  674.8 15.6 %collective-permute-start.60 = (bf16[128,2048]{1,0:T(8,128)(2,1)S(1)}, bf16[128,2048]{1,0:T(8,128)(2,1)S(1)}, u32[]{:S(2)}, u32[]{:S(2)}) collective-permute-start(bf16[128,2048]{1,0:T(8,128)(2,1)S(1)} %get-tuple-element.300), channel_id=1, source_target_pairs={{0,8},{4,12},{8,0},{12,4},{16,24},{20,28},{24,16},{28,20},{1,9},{5... | collective-permute-start | bytes 1572872 | tf_op jit(solution)/shard_map/ppermute | solution.py:242
  676.0 19.1 %collective-permute-start.61 = (bf16[128,2048]{1,0:T(8,128)(2,1)S(1)}, bf16[128,2048]{1,0:T(8,128)(2,1)S(1)}, u32[]{:S(2)}, u32[]{:S(2)}) collective-permute-start(bf16[128,2048]{1,0:T(8,128)(2,1)S(1)} %get-tuple-element.302), channel_id=1, source_target_pairs={{0,16},{4,20},{8,24},{12,28},{16,0},{20,4},{24,8},{28,12},{1,17},{... | collective-permute-start | bytes 1572872 | tf_op jit(solution)/shard_map/ppermute | solution.py:242
  677.2 35.5 %collective-permute-start.62 = (bf16[128,2048]{1,0:T(8,128)(2,1)S(1)}, bf16[128,2048]{1,0:T(8,128)(2,1)S(1)}, u32[]{:S(2)}, u32[]{:S(2)}) collective-permute-start(bf16[128,2048]{1,0:T(8,128)(2,1)S(1)} %get-tuple-element.301), channel_id=1, source_target_pairs={{0,24},{4,28},{8,16},{12,20},{16,8},{20,12},{24,0},{28,4},{1,25},{... | collective-permute-start | bytes 1572872 | tf_op jit(solution)/shard_map/ppermute | solution.py:242
  690.4 23.9 %collective-permute-start.59 = (f32[2,2048]{1,0:T(2,128)S(1)}, f32[2,2048]{1,0:T(2,128)S(1)}, u32[]{:S(2)}, u32[]{:S(2)}) collective-permute-start(f32[2,2048]{1,0:T(2,128)S(1)} %add.217), channel_id=1, source_target_pairs={{0,16},{4,20},{8,24},{12,28},{16,0},{20,4},{24,8},{28,12},{1,17},{... | collective-permute-start | bytes 49160 | tf_op jit(solution)/shard_map/ppermute | solution.py:33
  695.1 26.7 %collective-permute-start.56 = (bf16[256,512]{1,0:T(8,128)(2,1)S(1)}, bf16[256,512]{1,0:T(8,128)(2,1)S(1)}, u32[]{:S(2)}, u32[]{:S(2)}) collective-permute-start(bf16[256,512]{1,0:T(8,128)(2,1)S(1)} %copy-done.82), channel_id=1, source_target_pairs={{0,8},{4,12},{8,0},{12,4},{16,24},{20,28},{24,16},{28,20},{1,9},{5... | collective-permute-start | bytes 786440 | tf_op jit(solution)/shard_map/ppermute | solution.py:242
  733.7 21.9 %collective-permute-start.63 = (bf16[1024,512]{1,0:T(8,128)(2,1)}, bf16[1024,512]{1,0:T(8,128)(2,1)}, u32[]{:S(2)}, u32[]{:S(2)}) collective-permute-start(bf16[1024,512]{1,0:T(8,128)(2,1)} %constant_dynamic-update-slice_fusion.37.same_ref), channel_id=1, source_target_pairs={{0,4},{4,0},{8,12},{12,8},{16,20},{20,16},{24,28},{28,24},{1,5},{5... | collective-permute-start | bytes 3145736 | tf_op jit(solution)/shard_map/ppermute | solution.py:33
  733.8 21.9 %collective-permute-start.64 = (f32[2,512]{1,0:T(2,128)S(1)}, f32[2,512]{1,0:T(2,128)S(1)}, u32[]{:S(2)}, u32[]{:S(2)}) collective-permute-start(f32[2,512]{1,0:T(2,128)S(1)} %get-tuple-element.317), channel_id=1, source_target_pairs={{0,1},{1,2},{2,3},{3,0},{4,5},{5,6},{6,7},{7,4},{8,9},{9,10},{10,1... | collective-permute-start | bytes 12296 | tf_op jit(solution)/shard_map/ppermute | solution.py:306
  734.1 21.6 %collective-permute-start.65 = (f32[2,512]{1,0:T(2,128)S(1)}, f32[2,512]{1,0:T(2,128)S(1)}, u32[]{:S(2)}, u32[]{:S(2)}) collective-permute-start(f32[2,512]{1,0:T(2,128)S(1)} %get-tuple-element.316), channel_id=1, source_target_pairs={{0,2},{1,3},{2,0},{3,1},{4,6},{5,7},{6,4},{7,5},{8,10},{9,11},{10,... | collective-permute-start | bytes 12296 | tf_op jit(solution)/shard_map/ppermute | solution.py:306
  736.5 19.2 %collective-permute-start.66 = (f32[2,512]{1,0:T(2,128)S(1)}, f32[2,512]{1,0:T(2,128)S(1)}, u32[]{:S(2)}, u32[]{:S(2)}) collective-permute-start(f32[2,512]{1,0:T(2,128)S(1)} %get-tuple-element.315), channel_id=1, source_target_pairs={{0,3},{1,0},{2,1},{3,2},{4,7},{5,4},{6,5},{7,6},{8,11},{9,8},{10,9... | collective-permute-start | bytes 12296 | tf_op jit(solution)/shard_map/ppermute | solution.py:306
  (110 other events, 1096.3 us)
Sparse Core Ops, SparseCore 0:
  94.6 25.1 all-gather.4
  121.9 106.1 all-gather.6
  230.3 57.4 all-gather.8
  325.5 53.0 reduce-scatter.5
  410.4 53.5 reduce-scatter.7
  466.1 56.0 reduce-scatter.9
  527.6 57.7 reduce-scatter.11
  616.0 24.6 reduce-scatter.13
  661.4 59.9 all-gather.10

commit v9 on v8

--- a/solution.py
+++ b/solution.py
@@ -760,18 +760,17 @@
     sigmoid = jax.nn.sigmoid(gate_act)
     silu = gate_act * sigmoid
     inner = (silu * up_act).astype(BF)
+    expert_flow = Flow(plane_sum_steps(mm(inner, down).astype(BF)))
     grad_inner = mm_nt(all_slot_grad, down)
     grad_gate_act = (grad_inner * up_act * sigmoid * (1.0 + gate_act * (1.0 - sigmoid))).astype(BF)
     grad_up_act = (grad_inner * silu).astype(BF)
+    grad_gate_act, grad_up_act = stage([expert_flow], (grad_gate_act, grad_up_act))
     grad_act = jnp.concatenate([grad_gate_act, grad_up_act], axis=1)
     grad_gate, back = lax.optimization_barrier(
         (mm_tn(grad_gate_act, dispatched).astype(BF), mm_nt(grad_act, gate_up).astype(BF))
     )
-    grad_disp = reduce_rows(back, 1)
-    expert_flow = Flow(plane_sum_steps(mm(inner, down).astype(BF)))
-    grad_up, grad_down = (
-        mm_tn(grad_up_act, dispatched).astype(BF),
-        mm_tn(inner, all_slot_grad).astype(BF),
+    grad_disp, grad_up_act, inner = lax.optimization_barrier(
+        (reduce_rows(back, 1), grad_up_act, inner)
     )
     grad_normed_two = mm_tn(pick, grad_disp)
     grad_gain_two, through = norm_back(grad_normed_two, hidden, root_two, gain_two)
@@ -793,18 +792,25 @@
             lins[d], grad_qkv_w[d] = lin, grad
 
     far, near = offsets[-1:], offsets[1:-1]
-    values, both_grad, grad_up, grad_down = stage(
-        [expert_flow], (run_back(*far), both_grad, grad_up, grad_down)
+    values, both_grad, grad_up, inner = stage(
+        [expert_flow],
+        (run_back(*far), both_grad, mm_tn(grad_up_act, dispatched).astype(BF), inner),
     )
     keep(far, values)
+    qkv_flow = Flow(scatter_steps(grad_qkv_w))
+    grad_down = mm_tn(inner, all_slot_grad).astype(BF)
+    values, both_grad, grad_down, expert_out = stage(
+        [qkv_flow], (run_back(*near), both_grad, grad_down, finish(expert_flow))
+    )
+    keep(near, values)
     sums = [
         lax.psum_scatter(g, "shard", scatter_dimension=1, tiled=True)
         for g in (grad_gate, grad_up, grad_down)
     ]
-    qkv_flow = Flow(scatter_steps(grad_qkv_w))
-    values, both_grad = stage([qkv_flow], (run_back(*near), both_grad))
-    keep(near, values)
-    values, grad_out_w = stage([qkv_flow], (run_back(0), mm_tn(all_context, both_grad).astype(BF)))
+    output = (hidden + mm_tn(pick, expert_out) * mix[:, None]).astype(BF)
+    values, grad_out_w, output = stage(
+        [qkv_flow], (run_back(0), mm_tn(all_context, both_grad).astype(BF), output)
+    )
     keep([0], values)
     grad_normed = normed_back(
         shard, [lins[d] for d in offsets], [qkv_w[d] for d in offsets], both.shape[1]
@@ -830,17 +836,16 @@
     gain_flow, up_flow = Flow(vector_sum_steps(gains)), Flow(copies_steps(up_sum))
     sum_qkv = stage([out_flow, gate_flow, up_flow, gain_flow], sum_qkv)
     sum_out = lax.psum_scatter(finish(out_flow), "shard", scatter_dimension=1, tiled=True)
-    qkv_flow = Flow(copies_steps(sum_qkv, straight_steps))
+    qkv_flow = Flow(copies_steps(sum_qkv))
     grad_gate = place_turned(whoami, *finish(gate_flow), units)
     grad_gate, sum_out = stage([up_flow, qkv_flow, gain_flow], (grad_gate, sum_out))
     down_sum, sum_out = lax.optimization_barrier((sums[2], sum_out))
     all_down = lax.all_gather(down_sum, "rep", axis=0, tiled=True)
     out_flow = Flow(copies_steps(sum_out, straight_steps))
-    output = (hidden + mm_tn(pick, finish(expert_flow)) * mix[:, None]).astype(BF)
-    output = stage([up_flow, qkv_flow, out_flow, gain_flow], output)
+    stage([up_flow, qkv_flow, out_flow, gain_flow])
     grad_up = place_turned(whoami, *finish(up_flow), units)
+    grad_up = stage([qkv_flow, out_flow, gain_flow], grad_up)
     grad_query, grad_key, grad_value = place(whoami, *finish(qkv_flow), own, block, True)
-    grad_up, grad_query = stage([out_flow, gain_flow], (grad_up, grad_query))
     (grad_out,) = place(whoami, *finish(out_flow), block, own, False)
     grad_down = all_down.astype(F32)
     gain_grads = finish(gain_flow)

time: 786 us -> 743 us (0.945)
  waiting for transfers between devices: 206 us -> 172 us
  Pallas kernels: 260 us -> 250 us
    ppermute x49 -> x53, waiting for transfers between devices: 146 us -> 113 us  [swap(): return lax.ppermute(value, 'rep', [(i, i ^ bit) for i in range(size)])]
    ppermute x9 -> x6, waiting for transfers between devices: 42.9 us -> 19.9 us  [jump(): return lax.ppermute(value, 'rep', [(i, i ^ offset) for i in range(size)])]
    ppermute x2, waiting for transfers between devices: 3.15 us -> 18.9 us  [per_device(): piece, other = stage(flows, (lax.ppermute(piece, 'shard', ring), other))]
    pallas_call x4, Pallas kernels: 55 us -> 42.5 us  [attend(): pl.pallas_call(functools.partial(attend_kernel, parts), grid_spec=pltpu.P...]
    ppermute x49 -> x53, starting transfers between devices: 40 us -> 47.9 us  [swap(): return lax.ppermute(value, 'rep', [(i, i ^ bit) for i in range(size)])]
    unnamed x226 -> x243, local copies, waits for them, and re-layouts: 59.8 us -> 62 us
  transfers between devices with their start and end apart: 76 -> 77, of which waited for: 26 -> 18; matrix products, arithmetic and copies ran while one was open for 19% -> 20% of each run, Pallas kernels for 33% -> 34%
where the time goes in v9:
time: 743 us; the launch traced here: 736 us
  Pallas kernels  250 us (34%)
  waiting for transfers between devices  172 us (23%)
  local copies, waits for them, and re-layouts  93.6 us (13%)
  matrix products  71.6 us (10%)
  other arithmetic  68.1 us (9%)
  starting transfers between devices  65.2 us (9%)
  between operations  15.5 us (2%)
    ppermute x53, waiting for transfers between devices, swap(): return lax.ppermute(value, 'rep', [(i, i ^ bit) for i in range(size)])  113 us
    pallas_call x4, Pallas kernels, attend_back(): pl.pallas_call(attend_back_kernel, grid=(rows // length,), in_specs=[by_s...  69.1 us
    unnamed x243, local copies, waits for them, and re-layouts  62 us
    pallas_call x2, Pallas kernels, gather_rows(): pl.pallas_call(functools.partial(gather_kernel, peers()), out_shape=jax.S...  58.4 us
    ppermute x53, starting transfers between devices, swap(): return lax.ppermute(value, 'rep', [(i, i ^ bit) for i in range(size)])  47.9 us
    pallas_call x4, Pallas kernels, attend(): pl.pallas_call(functools.partial(attend_kernel, parts), grid_spec=pltpu.P...  42.5 us
    pallas_call x1, Pallas kernels, reduce_rows(): pl.pallas_call(functools.partial(reduce_kernel, peers()), out_shape=jax.S...  28.7 us
    dot_general x6, matrix products, mm_tn(): lax.dot_general(left, right, (((0,), (0,)), ((), ())), preferred_element_...  25.8 us
  transfers between devices with their start and end apart: 77, of which 18 were waited for; matrix products, arithmetic and copies ran while one was open for 20% of the time, Pallas kernels for 34%

profile of v9, /device:TPU:0, one launch (start us, length us, event | category | flops | bytes accessed | tf_op | source)
XLA Modules:
  0.0 735.6 jit_solution(1767587880889150402)
XLA Ops:
  8.8 3.1 collective-permute-start.2
  11.8 2.6 collective-permute-start.1
  17.7 2.7 constant_dynamic-slice_fusion.4
  21.2 2.3 constant_dynamic-slice_fusion.15
  26.2 16.2 %collective-permute-done.3.refs_5_ = bf16[512,768]{1,0:T(8,128)(2,1)} collective-permute-done((bf16[512,768]{1,0:T(8,128)(2,1)S(1)}, bf16[512,768]{1,0:T(8,128)(2,1)}, u32[]{:S(2)}, u32[]{:S(2)}) %collective-permute-start.3) | collective-permute-done | bytes 786464 | tf_op jit(solution)/shard_map/ppermute | solution.py:703
  47.9 18.9 %collective-permute-done.7.refs_6_ = bf16[512,768]{1,0:T(8,128)(2,1)} collective-permute-done((bf16[512,768]{1,0:T(8,128)(2,1)}, bf16[512,768]{1,0:T(8,128)(2,1)}, u32[]{:S(2)}, u32[]{:S(2)}) %collective-permute-start.7) | collective-permute-done | bytes 786464 | tf_op jit(solution)/shard_map/ppermute | solution.py:717
  75.3 20.7 %collective-permute-done.10 = bf16[256,768]{1,0:T(8,128)(2,1)} collective-permute-done((bf16[256,768]{1,0:T(8,128)(2,1)}, bf16[256,768]{1,0:T(8,128)(2,1)}, u32[]{:S(2)}, u32[]{:S(2)}) %collective-permute-start.10) | collective-permute-done | bytes 393248 | tf_op jit(solution)/shard_map/ppermute | solution.py:33
  99.3 2.2 pad_maximum_fusion.7.refs_4_.refs_8_
  111.0 2.2 pad_maximum_fusion.refs_0_.refs_1_.refs_2_.refs_3_.x_ref
  115.5 11.1 %attend.4 = (bf16[1024,256]{1,0:T(8,128)(2,1)S(1)}, bf16[1024,768]{1,0:T(8,128)(2,1)S(1)}, f32[1024,2]{1,0:T(8,128)S(1)}) custom-call(s32[1]{0:T(128)} %bitcast.1.z_ref, bf16[1024,2048]{1,0:T(8,128)(2,1)S(1)} %pad_maximum_fusion.refs_0_.refs_1_.refs_2_.refs_3_.x_ref, bf16[1024,2048]{1,0:T(8,128)(2,1)S(1)} %pad_maximum_fusion.refs_0_.refs_1_.refs_2_.refs_3_.x_ref, ...), custom_call_target="tpu_custom_call" | custom-call | flops 3758096384 | bytes 10485760 | tf_op jit(solution)/shard_map/attend/pallas_call | solution.py:398
  140.4 2.2 copy-done.3
  144.9 10.7 %attend.5 = (bf16[1024,256]{1,0:T(8,128)(2,1)S(1)}, bf16[1024,768]{1,0:T(8,128)(2,1)S(1)}, f32[1024,2]{1,0:T(8,128)S(1)}) custom-call(s32[1]{0:T(128)} %bitcast.1.z_ref, bf16[1024,2048]{1,0:T(8,128)(2,1)S(1)} %copy-done.3, bf16[1024,2048]{1,0:T(8,128)(2,1)S(1)} %copy-done.3, bf16[1024,2048]{1,0:T(8,128)(2,1)S(1)} %copy-done.3, ...), custom_call_target="tpu_custom_call" | custom-call | flops 3758096384 | bytes 10485760 | tf_op jit(solution)/shard_map/attend/pallas_call | solution.py:398
  157.5 10.8 %attend.6 = (bf16[1024,256]{1,0:T(8,128)(2,1)S(1)}, bf16[1024,768]{1,0:T(8,128)(2,1)S(1)}, f32[1024,2]{1,0:T(8,128)S(1)}) custom-call(s32[1]{0:T(128)} %bitcast.1.z_ref, bf16[1024,2048]{1,0:T(8,128)(2,1)S(1)} %copy-done.3, bf16[1024,2048]{1,0:T(8,128)(2,1)S(1)} %copy-done.3, bf16[1024,2048]{1,0:T(8,128)(2,1)S(1)} %copy-done.3, ...), custom_call_target="tpu_custom_call" | custom-call | flops 3758096384 | bytes 10485760 | tf_op jit(solution)/shard_map/attend/pallas_call | solution.py:398
  170.0 9.9 %attend.7 = (bf16[1024,256]{1,0:T(8,128)(2,1)S(1)}, bf16[1024,768]{1,0:T(8,128)(2,1)S(1)}, f32[1024,2]{1,0:T(8,128)S(1)}) custom-call(s32[1]{0:T(128)} %bitcast.1.z_ref, bf16[1024,2048]{1,0:T(8,128)(2,1)S(1)} %copy-done.3, bf16[1024,2048]{1,0:T(8,128)(2,1)S(1)} %copy-done.3, bf16[1024,2048]{1,0:T(8,128)(2,1)S(1)} %copy-done.3, ...), custom_call_target="tpu_custom_call" | custom-call | flops 3758096384 | bytes 10485760 | tf_op jit(solution)/shard_map/attend/pallas_call | solution.py:398
  184.2 6.2 collective-permute-done.22
  192.6 6.2 fusion.45
  198.9 3.4 copy-done.65
  204.4 2.2 fusion.15.in_ref
  208.4 4.0 multiply_reduce_fusion.2
  215.2 29.2 %gather_rows.2 = bf16[1024,2048]{1,0:T(8,128)(2,1)S(1)} custom-call(bf16[128,2048]{1,0:T(8,128)(2,1)S(1)} %convolution_convert_fusion.6.in_ref), custom_call_target="tpu_custom_call" | custom-call | bytes 62914560 | tf_op jit(solution)/shard_map/gather_rows/pallas_call | solution.py:153
  246.4 11.7 %fusion.46 = f32[1024,1408]{1,0:T(8,128)} fusion(bf16[1024,2048]{1,0:T(8,128)(2,1)} %copy-done.6, bf16[2048,1408]{1,0:T(8,128)(2,1)} %all-gather.7.cloned.1.call-done), kind=kOutput, calls=%fused_computation.175 | convolution fusion | flops 5905580032 | bytes 15728640 | tf_op jit(solution)/shard_map/dot_general | solution.py:20
  258.1 29.2 %gather_rows.3 = bf16[1024,2048]{1,0:T(8,128)(2,1)S(1)} custom-call(bf16[128,2048]{1,0:T(8,128)(2,1)S(1)} %fusion.15.in_ref), custom_call_target="tpu_custom_call" | custom-call | bytes 62914560 | tf_op jit(solution)/shard_map/gather_rows/pallas_call | solution.py:153
  289.3 3.0 all-gather.9.cloned.1.call-done
  292.4 10.3 %multiply_convert_fusion.2 = (bf16[1024,704]{1,0:T(8,128)(2,1)}, bf16[1024,704]{1,0:T(8,128)(2,1)S(1)}, bf16[1024,704]{1,0:T(8,128)(2,1)S(1)}) fusion(f32[1024,1408]{1,0:T(8,128)} %fusion.46, bf16[1024,2048]{1,0:T(8,128)(2,1)} %copy-done.4, bf16[704,2048]{1,0:T(8,128)(2,1)} %all-gather.9.cloned.1.call-done), kind=kOutput, calls=%fused_computation.41 | convolution fusion | flops 2963603456 | bytes 17170432 | tf_op jit(solution)/shard_map/dot_general | solution.py:24
  302.7 3.6 convolution_convert_fusion.1
  308.7 4.3 collective-permute-done.25
  312.9 4.5 convolution_convert_fusion.5
  317.4 11.0 %convolution_convert_fusion.in_ref = bf16[1024,2048]{1,0:T(8,128)(2,1)} fusion(bf16[2048,1408]{1,0:T(8,128)(2,1)} %all-gather.7.cloned.1.call-done, bf16[1024,704]{1,0:T(8,128)(2,1)} %get-tuple-element.200, bf16[1024,704]{1,0:T(8,128)(2,1)} %copy-done.105), kind=kOutput, calls=%fused_computation.30 | convolution fusion | flops 5913444352 | bytes 12845056 | tf_op jit(solution)/shard_map/dot_general | solution.py:24
  328.7 2.2 copy-done.9
  330.9 28.7 %reduce_rows.1 = bf16[128,2048]{1,0:T(8,128)(2,1)S(1)} custom-call(bf16[1024,2048]{1,0:T(8,128)(2,1)S(1)} %copy-done.9), custom_call_target="tpu_custom_call" | custom-call | bytes 62914560 | tf_op jit(solution)/shard_map/reduce_rows/pallas_call | solution.py:218
  361.2 3.8 multiply_convert_fusion
  366.3 2.5 add_convert_fusion.1
  371.4 2.2 collective-permute-start.28
  374.9 4.5 convolution_convert_fusion.4
  379.4 4.9 pad_maximum_fusion.1.grad_ref
  384.3 17.0 %attend_back.4 = (bf16[1024,768]{1,0:T(8,128)(2,1)S(1)}, bf16[1024,768]{1,0:T(8,128)(2,1)S(1)}, bf16[1024,768]{1,0:T(8,128)(2,1)}) custom-call(bf16[1024,2048]{1,0:T(8,128)(2,1)} %pad_maximum_fusion.1.grad_ref, bf16[256,2048]{1,0:T(8,128)(2,1)S(1)} %copy-done.36, bf16[1024,768]{1,0:T(8,128)(2,1)} %copy-done.40, f32[1024,2]{1,0:T(8,128)S(1)} %copy-done.48, ...), custom_call_target="tpu_custom_call" | custom-call | flops 5637144576 | bytes 15728640 | tf_op jit(solution)/shard_map/attend_back/pallas_call | solution.py:487
  408.1 17.2 %attend_back.6 = (bf16[1024,768]{1,0:T(8,128)(2,1)S(1)}, bf16[1024,768]{1,0:T(8,128)(2,1)S(1)}, bf16[1024,768]{1,0:T(8,128)(2,1)}) custom-call(bf16[1024,2048]{1,0:T(8,128)(2,1)} %pad_maximum_fusion.1.grad_ref, bf16[256,2048]{1,0:T(8,128)(2,1)S(1)} %copy-done.21, bf16[1024,768]{1,0:T(8,128)(2,1)} %copy-done.39, f32[1024,2]{1,0:T(8,128)S(1)} %copy-done.46, ...), custom_call_target="tpu_custom_call" | custom-call | flops 5637144576 | bytes 15728640 | tf_op jit(solution)/shard_map/attend_back/pallas_call | solution.py:487
  426.5 3.2 add_convert_fusion.10
  429.7 17.1 %attend_back.5 = (bf16[1024,768]{1,0:T(8,128)(2,1)S(1)}, bf16[1024,768]{1,0:T(8,128)(2,1)S(1)}, bf16[1024,768]{1,0:T(8,128)(2,1)}) custom-call(bf16[1024,2048]{1,0:T(8,128)(2,1)} %pad_maximum_fusion.1.grad_ref, bf16[256,2048]{1,0:T(8,128)(2,1)S(1)} %copy-done.19, bf16[1024,768]{1,0:T(8,128)(2,1)} %copy-done.38, f32[1024,2]{1,0:T(8,128)S(1)} %get-tuple-element.204.lse_ref, ...), custom_call_target="tpu_custom_call" | custom-call | flops 5637144576 | bytes 15728640 | tf_op jit(solution)/shard_map/attend_back/pallas_call | solution.py:487
  449.1 4.5 convolution_convert_fusion.3
  455.3 3.4 add_convert_fusion.4
  460.1 3.4 add_convert_fusion.5
  464.6 17.7 %attend_back.7 = (bf16[1024,768]{1,0:T(8,128)(2,1)S(1)}, bf16[1024,768]{1,0:T(8,128)(2,1)S(1)}, bf16[1024,768]{1,0:T(8,128)(2,1)}) custom-call(bf16[1024,2048]{1,0:T(8,128)(2,1)} %pad_maximum_fusion.1.grad_ref, bf16[256,2048]{1,0:T(8,128)(2,1)S(1)} %copy-done.35, bf16[1024,768]{1,0:T(8,128)(2,1)} %copy-done.37, f32[1024,2]{1,0:T(8,128)S(1)} %copy-done.44, ...), custom_call_target="tpu_custom_call" | custom-call | flops 5637144576 | bytes 15728640 | tf_op jit(solution)/shard_map/attend_back/pallas_call | solution.py:487
  482.4 8.9 %convolution_convert_fusion.2 = bf16[1024,2048]{1,0:T(8,128)(2,1)} fusion(bf16[1024,1024]{1,0:T(8,128)(2,1)} %constant_dynamic-update-slice_fusion.14, bf16[1024,2048]{1,0:T(8,128)(2,1)S(1)} %copy-done.68), kind=kOutput, calls=%fused_computation.32 | convolution fusion | flops 4297064448 | bytes 10485760 | tf_op jit(solution)/shard_map/dot_general | solution.py:28
  491.3 2.2 add_convert_fusion
  493.5 24.0 %normed_back.1 = (f32[512,2048]{1,0:T(8,128)}, bf16[512,2048]{1,0:T(8,128)(2,1)}) custom-call(s32[1]{0:T(128)} %bitcast.1.z_ref, bf16[1024,768]{1,0:T(8,128)(2,1)} %copy-done.52, bf16[1024,768]{1,0:T(8,128)(2,1)} %copy-done.51, bf16[1024,768]{1,0:T(8,128)(2,1)} %copy-done.50, bf16[1024,768]{1,0:T(8,128)(2,1)} %copy-done.49, ...), custom_call_target="tpu_custom_call" | custom-call | flops 12884901888 | bytes 27262976 | tf_op jit(solution)/shard_map/normed_back/pallas_call | solution.py:543
  517.5 5.7 collective-permute-done.35
  524.4 3.1 add_convert_fusion.2
  532.9 2.8 fusion.41
  539.0 22.7 %collective-permute-done.39 = bf16[128,2048]{1,0:T(8,128)(2,1)S(1)} collective-permute-done((bf16[128,2048]{1,0:T(8,128)(2,1)S(1)}, bf16[128,2048]{1,0:T(8,128)(2,1)S(1)}, u32[]{:S(2)}, u32[]{:S(2)}) %collective-permute-start.39) | collective-permute-done | bytes 524320 | tf_op jit(solution)/shard_map/ppermute | solution.py:33
  565.9 3.1 fusion.9
  569.0 3.9 fusion.6
  573.1 3.4 collective-permute-done.37
  576.8 5.9 collective-permute-done.44
  589.9 24.2 %collective-permute-done.46 = bf16[128,2048]{1,0:T(8,128)(2,1)S(1)} collective-permute-done((bf16[128,2048]{1,0:T(8,128)(2,1)S(1)}, bf16[128,2048]{1,0:T(8,128)(2,1)S(1)}, u32[]{:S(2)}, u32[]{:S(2)}) %collective-permute-start.46) | collective-permute-done | bytes 524320 | tf_op jit(solution)/shard_map/ppermute | solution.py:33
  617.8 2.2 add_convert_fusion.7
  629.9 5.0 place_turned.2
  634.9 13.5 %collective-permute-done.55 = f32[2,2048]{1,0:T(2,128)S(1)} collective-permute-done((f32[2,2048]{1,0:T(2,128)S(1)}, f32[2,2048]{1,0:T(2,128)S(1)}, u32[]{:S(2)}, u32[]{:S(2)}) %collective-permute-start.55) | collective-permute-done | bytes 16416 | tf_op jit(solution)/shard_map/ppermute | solution.py:33
  661.9 6.8 collective-permute-done.61
  673.3 13.2 %collective-permute-done.60 = bf16[256,512]{1,0:T(8,128)(2,1)S(1)} collective-permute-done((bf16[256,512]{1,0:T(8,128)(2,1)S(1)}, bf16[256,512]{1,0:T(8,128)(2,1)S(1)}, u32[]{:S(2)}, u32[]{:S(2)}) %collective-permute-start.60) | collective-permute-done | bytes 262176 | tf_op jit(solution)/shard_map/ppermute | solution.py:242
  697.0 5.0 place_turned.3
  702.0 6.5 place.3
  708.4 11.0 %place.2 = (f32[512,2048]{1,0:T(8,128)}, f32[512,2048]{1,0:T(8,128)}, f32[512,2048]{1,0:T(8,128)}) custom-call(s32[1]{0:T(128)} %bitcast.6.me_ref, bf16[2048,768]{1,0:T(8,128)(2,1)} %constant_dynamic-update-slice_fusion.33.same_ref, bf16[2048,768]{1,0:T(8,128)(2,1)} %collective-permute-done.63.other_ref), custom_call_target="tpu_custom_call" | custom-call | bytes 25165824 | tf_op jit(solution)/shard_map/place/pallas_call | solution.py:604
  720.0 8.9 %convert_element_type.237 = f32[5632,512]{1,0:T(8,128)} convert(bf16[5632,512]{1,0:T(8,128)(2,1)} %all-gather.11.cloned.1.call-done) | non-fusion elementwise | flops 2883584 | bytes 17301504 | tf_op jit(solution)/shard_map/convert_element_type | solution.py:850
  (457 shorter events, 161.7 us)
Async XLA Ops:
  7.2 125.0 %all-gather.5.cloned.1.call-start = ((), (), s32[]{:S(2)}) async-start(), calls=%async_computation.5 | async-start | bytes 1310720 | tf_op jit(solution)/shard_map/all_gather | solution.py:721
  8.8 17.4 %collective-permute-start.2 = (bf16[2,512]{1,0:T(2,128)(2,1)S(1)}, bf16[2,512]{1,0:T(2,128)(2,1)S(1)}, u32[]{:S(2)}, u32[]{:S(2)}) collective-permute-start(bf16[2,512]{1,0:T(2,128)(2,1)S(1)} %get-tuple-element.306), channel_id=1, source_target_pairs={{0,1},{1,2},{2,3},{3,0},{4,5},{5,6},{6,7},{7,4},{8,9},{9,10},{10,1... | collective-permute-start | bytes 6152 | tf_op jit(solution)/shard_map/ppermute | solution.py:319
  11.8 14.3 %collective-permute-start.1 = (bf16[2,512]{1,0:T(2,128)(2,1)S(1)}, bf16[2,512]{1,0:T(2,128)(2,1)S(1)}, u32[]{:S(2)}, u32[]{:S(2)}) collective-permute-start(bf16[2,512]{1,0:T(2,128)(2,1)S(1)} %get-tuple-element.306), channel_id=1, source_target_pairs={{0,2},{1,3},{2,0},{3,1},{4,6},{5,7},{6,4},{7,5},{8,10},{9,11},{10,... | collective-permute-start | bytes 6152 | tf_op jit(solution)/shard_map/ppermute | solution.py:319
  20.5 21.9 %collective-permute-start.3 = (bf16[512,768]{1,0:T(8,128)(2,1)S(1)}, bf16[512,768]{1,0:T(8,128)(2,1)}, u32[]{:S(2)}, u32[]{:S(2)}) collective-permute-start(bf16[512,768]{1,0:T(8,128)(2,1)S(1)} %pad_maximum_fusion.6.refs_4_), channel_id=1, source_target_pairs={{0,1},{1,2},{2,3},{3,0},{4,5},{5,6},{6,7},{7,4},{8,9},{9,10},{10,1... | collective-permute-start | bytes 2359304 | tf_op jit(solution)/shard_map/ppermute | solution.py:703
  44.7 22.2 %collective-permute-start.8 = (bf16[512,2048]{1,0:T(8,128)(2,1)S(1)}, bf16[512,2048]{1,0:T(8,128)(2,1)S(1)}, u32[]{:S(2)}, u32[]{:S(2)}) collective-permute-start(bf16[512,2048]{1,0:T(8,128)(2,1)S(1)} %fusion.2), channel_id=1, source_target_pairs={{0,4},{4,0},{8,12},{12,8},{16,20},{20,16},{24,28},{28,24},{1,5},{5... | collective-permute-start | bytes 6291464 | tf_op jit(solution)/shard_map/ppermute | solution.py:33
  44.8 22.1 %collective-permute-start.7 = (bf16[512,768]{1,0:T(8,128)(2,1)}, bf16[512,768]{1,0:T(8,128)(2,1)}, u32[]{:S(2)}, u32[]{:S(2)}) collective-permute-start(bf16[512,768]{1,0:T(8,128)(2,1)} %collective-permute-done.3.refs_5_), channel_id=1, source_target_pairs={{0,1},{1,2},{2,3},{3,0},{4,5},{5,6},{6,7},{7,4},{8,9},{9,10},{10,1... | collective-permute-start | bytes 2359304 | tf_op jit(solution)/shard_map/ppermute | solution.py:717
  44.8 22.0 %collective-permute-start.6 = (bf16[512,768]{1,0:T(8,128)(2,1)}, bf16[512,768]{1,0:T(8,128)(2,1)S(1)}, u32[]{:S(2)}, u32[]{:S(2)}) collective-permute-start(bf16[512,768]{1,0:T(8,128)(2,1)} %collective-permute-done.3.refs_5_), channel_id=1, source_target_pairs={{0,16},{4,20},{8,24},{12,28},{16,0},{20,4},{24,8},{28,12},{1,17},{... | collective-permute-start | bytes 2359304 | tf_op jit(solution)/shard_map/ppermute | solution.py:33
  46.4 20.4 %collective-permute-start.5 = (bf16[512,768]{1,0:T(8,128)(2,1)}, bf16[512,768]{1,0:T(8,128)(2,1)S(1)}, u32[]{:S(2)}, u32[]{:S(2)}) collective-permute-start(bf16[512,768]{1,0:T(8,128)(2,1)} %collective-permute-done.3.refs_5_), channel_id=1, source_target_pairs={{0,8},{4,12},{8,0},{12,4},{16,24},{20,28},{24,16},{28,20},{1,9},{5... | collective-permute-start | bytes 2359304 | tf_op jit(solution)/shard_map/ppermute | solution.py:33
  66.9 29.2 %collective-permute-start.13 = (bf16[512,768]{1,0:T(8,128)(2,1)}, bf16[512,768]{1,0:T(8,128)(2,1)}, u32[]{:S(2)}, u32[]{:S(2)}) collective-permute-start(bf16[512,768]{1,0:T(8,128)(2,1)} %collective-permute-done.7.refs_6_), channel_id=1, source_target_pairs={{0,1},{1,2},{2,3},{3,0},{4,5},{5,6},{6,7},{7,4},{8,9},{9,10},{10,1... | collective-permute-start | bytes 2359304 | tf_op jit(solution)/shard_map/ppermute | solution.py:717
  66.9 29.2 %collective-permute-start.12 = (bf16[512,768]{1,0:T(8,128)(2,1)}, bf16[512,768]{1,0:T(8,128)(2,1)}, u32[]{:S(2)}, u32[]{:S(2)}) collective-permute-start(bf16[512,768]{1,0:T(8,128)(2,1)} %collective-permute-done.7.refs_6_), channel_id=1, source_target_pairs={{0,16},{4,20},{8,24},{12,28},{16,0},{20,4},{24,8},{28,12},{1,17},{... | collective-permute-start | bytes 2359304 | tf_op jit(solution)/shard_map/ppermute | solution.py:33
  68.5 27.6 %collective-permute-start.11 = (bf16[512,768]{1,0:T(8,128)(2,1)}, bf16[512,768]{1,0:T(8,128)(2,1)}, u32[]{:S(2)}, u32[]{:S(2)}) collective-permute-start(bf16[512,768]{1,0:T(8,128)(2,1)} %collective-permute-done.7.refs_6_), channel_id=1, source_target_pairs={{0,8},{4,12},{8,0},{12,4},{16,24},{20,28},{24,16},{28,20},{1,9},{5... | collective-permute-start | bytes 2359304 | tf_op jit(solution)/shard_map/ppermute | solution.py:33
  71.6 24.5 %collective-permute-start.10 = (bf16[256,768]{1,0:T(8,128)(2,1)}, bf16[256,768]{1,0:T(8,128)(2,1)}, u32[]{:S(2)}, u32[]{:S(2)}) collective-permute-start(bf16[256,768]{1,0:T(8,128)(2,1)} %slice.116), channel_id=1, source_target_pairs={{0,8},{4,12},{8,0},{12,4},{16,24},{20,28},{24,16},{28,20},{1,9},{5... | collective-permute-start | bytes 1179656 | tf_op jit(solution)/shard_map/ppermute | solution.py:33
  72.1 24.0 %collective-permute-start.9 = (bf16[256,768]{1,0:T(8,128)(2,1)}, bf16[256,768]{1,0:T(8,128)(2,1)}, u32[]{:S(2)}, u32[]{:S(2)}) collective-permute-start(bf16[256,768]{1,0:T(8,128)(2,1)} %slice.115), channel_id=1, source_target_pairs={{0,16},{4,20},{8,24},{12,28},{16,0},{20,4},{24,8},{28,12},{1,17},{... | collective-permute-start | bytes 1179656 | tf_op jit(solution)/shard_map/ppermute | solution.py:33
  96.1 150.2 %all-gather.7.cloned.1.call-start = ((), (), s32[]{:S(2)}) async-start(), calls=%async_computation.6 | async-start | bytes 7208960 | tf_op jit(solution)/shard_map/all_gather | solution.py:729
  96.9 195.5 %all-gather.9.cloned.1.call-start = ((), (), s32[]{:S(2)}) async-start(), calls=%async_computation.7 | async-start | bytes 3604480 | tf_op jit(solution)/shard_map/all_gather | solution.py:730
  103.8 28.4 %collective-permute-start.17 = (bf16[512,768]{1,0:T(8,128)(2,1)}, bf16[512,768]{1,0:T(8,128)(2,1)}, u32[]{:S(2)}, u32[]{:S(2)}) collective-permute-start(bf16[512,768]{1,0:T(8,128)(2,1)} %collective-permute-done.13.refs_7_), channel_id=1, source_target_pairs={{0,16},{4,20},{8,24},{12,28},{16,0},{20,4},{24,8},{28,12},{1,17},{... | collective-permute-start | bytes 2359304 | tf_op jit(solution)/shard_map/ppermute | solution.py:33
  104.4 27.8 %collective-permute-start.16 = (bf16[512,768]{1,0:T(8,128)(2,1)}, bf16[512,768]{1,0:T(8,128)(2,1)}, u32[]{:S(2)}, u32[]{:S(2)}) collective-permute-start(bf16[512,768]{1,0:T(8,128)(2,1)} %collective-permute-done.13.refs_7_), channel_id=1, source_target_pairs={{0,8},{4,12},{8,0},{12,4},{16,24},{20,28},{24,16},{28,20},{1,9},{5... | collective-permute-start | bytes 2359304 | tf_op jit(solution)/shard_map/ppermute | solution.py:33
  107.9 22.8 %collective-permute-start.15 = (bf16[256,768]{1,0:T(8,128)(2,1)S(1)}, bf16[256,768]{1,0:T(8,128)(2,1)S(1)}, u32[]{:S(2)}, u32[]{:S(2)}) collective-permute-start(bf16[256,768]{1,0:T(8,128)(2,1)S(1)} %slice.118), channel_id=1, source_target_pairs={{0,8},{4,12},{8,0},{12,4},{16,24},{20,28},{24,16},{28,20},{1,9},{5... | collective-permute-start | bytes 1179656 | tf_op jit(solution)/shard_map/ppermute | solution.py:33
  108.5 22.9 %collective-permute-start.14 = (bf16[256,768]{1,0:T(8,128)(2,1)S(1)}, bf16[256,768]{1,0:T(8,128)(2,1)S(1)}, u32[]{:S(2)}, u32[]{:S(2)}) collective-permute-start(bf16[256,768]{1,0:T(8,128)(2,1)S(1)} %slice.117), channel_id=1, source_target_pairs={{0,16},{4,20},{8,24},{12,28},{16,0},{20,4},{24,8},{28,12},{1,17},{... | collective-permute-start | bytes 1179656 | tf_op jit(solution)/shard_map/ppermute | solution.py:33
  132.2 47.8 %collective-permute-start.21 = (bf16[256,2048]{1,0:T(8,128)(2,1)}, bf16[256,2048]{1,0:T(8,128)(2,1)S(1)}, u32[]{:S(2)}, u32[]{:S(2)}) collective-permute-start(bf16[256,2048]{1,0:T(8,128)(2,1)} %all-gather.5.cloned.1.call-done.out_ref), channel_id=1, source_target_pairs={{0,16},{4,20},{8,24},{12,28},{16,0},{20,4},{24,8},{28,12},{1,17},{... | collective-permute-start | bytes 3145736 | tf_op jit(solution)/shard_map/ppermute | solution.py:33
  133.7 46.3 %collective-permute-start.20 = (bf16[256,2048]{1,0:T(8,128)(2,1)}, bf16[256,2048]{1,0:T(8,128)(2,1)S(1)}, u32[]{:S(2)}, u32[]{:S(2)}) collective-permute-start(bf16[256,2048]{1,0:T(8,128)(2,1)} %all-gather.5.cloned.1.call-done.out_ref), channel_id=1, source_target_pairs={{0,8},{4,12},{8,0},{12,4},{16,24},{20,28},{24,16},{28,20},{1,9},{5... | collective-permute-start | bytes 3145736 | tf_op jit(solution)/shard_map/ppermute | solution.py:33
  137.3 32.0 %collective-permute-start.19 = (bf16[256,768]{1,0:T(8,128)(2,1)S(1)}, bf16[256,768]{1,0:T(8,128)(2,1)S(1)}, u32[]{:S(2)}, u32[]{:S(2)}) collective-permute-start(bf16[256,768]{1,0:T(8,128)(2,1)S(1)} %slice.120), channel_id=1, source_target_pairs={{0,8},{4,12},{8,0},{12,4},{16,24},{20,28},{24,16},{28,20},{1,9},{5... | collective-permute-start | bytes 1179656 | tf_op jit(solution)/shard_map/ppermute | solution.py:33
  138.0 31.4 %collective-permute-start.18 = (bf16[256,768]{1,0:T(8,128)(2,1)S(1)}, bf16[256,768]{1,0:T(8,128)(2,1)S(1)}, u32[]{:S(2)}, u32[]{:S(2)}) collective-permute-start(bf16[256,768]{1,0:T(8,128)(2,1)S(1)} %slice.119), channel_id=1, source_target_pairs={{0,16},{4,20},{8,24},{12,28},{16,0},{20,4},{24,8},{28,12},{1,17},{... | collective-permute-start | bytes 1179656 | tf_op jit(solution)/shard_map/ppermute | solution.py:33
  204.0 320.4 %reduce-scatter.6.cloned.1.call-start = ((), (), s32[]{:S(2)}) async-start(), calls=%async_computation.8 | async-start | bytes 3604480 | tf_op jit(solution)/shard_map/reduce_scatter | solution.py:807
  328.5 195.9 %reduce-scatter.8.cloned.1.call-start = ((), (), s32[]{:S(2)}) async-start(), calls=%async_computation.9 | async-start | bytes 3604480 | tf_op jit(solution)/shard_map/reduce_scatter | solution.py:807
  365.0 14.4 %collective-permute-start.29 = (bf16[512,2048]{1,0:T(8,128)(2,1)}, bf16[512,2048]{1,0:T(8,128)(2,1)}, u32[]{:S(2)}, u32[]{:S(2)}) collective-permute-start(bf16[512,2048]{1,0:T(8,128)(2,1)} %get-tuple-element.301), channel_id=1, source_target_pairs={{0,4},{4,0},{8,12},{12,8},{16,20},{20,16},{24,28},{28,24},{1,5},{5... | collective-permute-start | bytes 6291464 | tf_op jit(solution)/shard_map/ppermute | solution.py:33
  371.4 32.3 %collective-permute-start.28 = (bf16[128,2048]{1,0:T(8,128)(2,1)}, bf16[128,2048]{1,0:T(8,128)(2,1)}, u32[]{:S(2)}, u32[]{:S(2)}) collective-permute-start(bf16[128,2048]{1,0:T(8,128)(2,1)} %get-tuple-element.320), channel_id=1, source_target_pairs={{0,24},{4,28},{8,16},{12,20},{16,8},{20,12},{24,0},{28,4},{1,25},{... | collective-permute-start | bytes 1572872 | tf_op jit(solution)/shard_map/ppermute | solution.py:242
  373.6 30.1 %collective-permute-start.27 = (bf16[128,2048]{1,0:T(8,128)(2,1)}, bf16[128,2048]{1,0:T(8,128)(2,1)}, u32[]{:S(2)}, u32[]{:S(2)}) collective-permute-start(bf16[128,2048]{1,0:T(8,128)(2,1)} %get-tuple-element.321), channel_id=1, source_target_pairs={{0,16},{4,20},{8,24},{12,28},{16,0},{20,4},{24,8},{28,12},{1,17},{... | collective-permute-start | bytes 1572872 | tf_op jit(solution)/shard_map/ppermute | solution.py:242
  374.2 29.5 %collective-permute-start.26 = (bf16[128,2048]{1,0:T(8,128)(2,1)}, bf16[128,2048]{1,0:T(8,128)(2,1)}, u32[]{:S(2)}, u32[]{:S(2)}) collective-permute-start(bf16[128,2048]{1,0:T(8,128)(2,1)} %get-tuple-element.322), channel_id=1, source_target_pairs={{0,8},{4,12},{8,0},{12,4},{16,24},{20,28},{24,16},{28,20},{1,9},{5... | collective-permute-start | bytes 1572872 | tf_op jit(solution)/shard_map/ppermute | solution.py:242
  403.7 127.8 %reduce-scatter.10.cloned.1.call-start = ((), (), s32[]{:S(2)}) async-start(), calls=%async_computation.10 | async-start | bytes 3604480 | tf_op jit(solution)/shard_map/reduce_scatter | solution.py:807
  404.2 49.4 %collective-permute-start.32 = (bf16[1024,768]{1,0:T(8,128)(2,1)}, bf16[1024,768]{1,0:T(8,128)(2,1)}, u32[]{:S(2)}, u32[]{:S(2)}) collective-permute-start(bf16[1024,768]{1,0:T(8,128)(2,1)} %copy-done.42), channel_id=1, source_target_pairs={{0,8},{4,12},{8,0},{12,4},{16,24},{20,28},{24,16},{28,20},{1,9},{5... | collective-permute-start | bytes 4718600 | tf_op jit(solution)/shard_map/ppermute | solution.py:33
  405.6 48.0 %collective-permute-start.33 = (bf16[1024,768]{1,0:T(8,128)(2,1)}, bf16[1024,768]{1,0:T(8,128)(2,1)}, u32[]{:S(2)}, u32[]{:S(2)}) collective-permute-start(bf16[1024,768]{1,0:T(8,128)(2,1)} %get-tuple-element.210), channel_id=1, source_target_pairs={{0,16},{4,20},{8,24},{12,28},{16,0},{20,4},{24,8},{28,12},{1,17},{... | collective-permute-start | bytes 4718600 | tf_op jit(solution)/shard_map/ppermute | solution.py:33
  453.6 164.1 %reduce-scatter.12.cloned.1.call-start = ((), (), s32[]{:S(2)}) async-start(), calls=%async_computation.11 | async-start | bytes 3932160 | tf_op jit(solution)/shard_map/reduce_scatter | solution.py:822
  453.7 39.8 %collective-permute-start.30 = (bf16[1024,768]{1,0:T(8,128)(2,1)}, bf16[1024,768]{1,0:T(8,128)(2,1)S(1)}, u32[]{:S(2)}, u32[]{:S(2)}) collective-permute-start(bf16[1024,768]{1,0:T(8,128)(2,1)} %copy-done.41), channel_id=1, source_target_pairs={{0,8},{4,12},{8,0},{12,4},{16,24},{20,28},{24,16},{28,20},{1,9},{5... | collective-permute-start | bytes 4718600 | tf_op jit(solution)/shard_map/ppermute | solution.py:33
  454.7 38.7 %collective-permute-start.31 = (bf16[1024,768]{1,0:T(8,128)(2,1)}, bf16[1024,768]{1,0:T(8,128)(2,1)S(1)}, u32[]{:S(2)}, u32[]{:S(2)}) collective-permute-start(bf16[1024,768]{1,0:T(8,128)(2,1)} %get-tuple-element.208), channel_id=1, source_target_pairs={{0,16},{4,20},{8,24},{12,28},{16,0},{20,4},{24,8},{28,12},{1,17},{... | collective-permute-start | bytes 4718600 | tf_op jit(solution)/shard_map/ppermute | solution.py:33
  458.7 64.4 %collective-permute-start.35 = (bf16[1024,768]{1,0:T(8,128)(2,1)}, bf16[1024,768]{1,0:T(8,128)(2,1)S(1)}, u32[]{:S(2)}, u32[]{:S(2)}) collective-permute-start(bf16[1024,768]{1,0:T(8,128)(2,1)} %add_convert_fusion.4), channel_id=1, source_target_pairs={{0,8},{4,12},{8,0},{12,4},{16,24},{20,28},{24,16},{28,20},{1,9},{5... | collective-permute-start | bytes 4718600 | tf_op jit(solution)/shard_map/ppermute | solution.py:33
  463.5 60.9 %collective-permute-start.34 = (bf16[1024,768]{1,0:T(8,128)(2,1)}, bf16[1024,768]{1,0:T(8,128)(2,1)}, u32[]{:S(2)}, u32[]{:S(2)}) collective-permute-start(bf16[1024,768]{1,0:T(8,128)(2,1)} %add_convert_fusion.5), channel_id=1, source_target_pairs={{0,16},{4,20},{8,24},{12,28},{16,0},{20,4},{24,8},{28,12},{1,17},{... | collective-permute-start | bytes 4718600 | tf_op jit(solution)/shard_map/ppermute | solution.py:33
  524.4 38.3 %collective-permute-start.42 = (bf16[512,2048]{1,0:T(8,128)(2,1)}, bf16[512,2048]{1,0:T(8,128)(2,1)}, u32[]{:S(2)}, u32[]{:S(2)}) collective-permute-start(bf16[512,2048]{1,0:T(8,128)(2,1)} %get-tuple-element.240), channel_id=1, source_target_pairs={{0,4},{4,0},{8,12},{12,8},{16,20},{20,16},{24,28},{28,24},{1,5},{5... | collective-permute-start | bytes 6291464 | tf_op jit(solution)/shard_map/ppermute | solution.py:33
  531.6 116.8 %reduce-scatter.14.cloned.1.call-start = ((), (), s32[]{:S(2)}) async-start(), calls=%async_computation.12 | async-start | bytes 1310720 | tf_op jit(solution)/shard_map/reduce_scatter | solution.py:838
  531.9 30.8 %collective-permute-start.41 = (bf16[704,512]{1,0:T(8,128)(2,1)}, bf16[704,512]{1,0:T(8,128)(2,1)S(1)}, u32[]{:S(2)}, u32[]{:S(2)}) collective-permute-start(bf16[704,512]{1,0:T(8,128)(2,1)} %reduce-scatter.6.cloned.1.call-done), channel_id=1, source_target_pairs={{0,16},{4,20},{8,24},{12,28},{16,0},{20,4},{24,8},{28,12},{1,17},{... | collective-permute-start | bytes 2162696 | tf_op jit(solution)/shard_map/ppermute | solution.py:33
  532.2 30.4 %collective-permute-start.40 = (bf16[704,512]{1,0:T(8,128)(2,1)}, bf16[704,512]{1,0:T(8,128)(2,1)S(1)}, u32[]{:S(2)}, u32[]{:S(2)}) collective-permute-start(bf16[704,512]{1,0:T(8,128)(2,1)} %reduce-scatter.6.cloned.1.call-done), channel_id=1, source_target_pairs={{0,8},{4,12},{8,0},{12,4},{16,24},{20,28},{24,16},{28,20},{1,9},{5... | collective-permute-start | bytes 2162696 | tf_op jit(solution)/shard_map/ppermute | solution.py:33
  535.7 25.9 %collective-permute-start.39 = (bf16[128,2048]{1,0:T(8,128)(2,1)S(1)}, bf16[128,2048]{1,0:T(8,128)(2,1)S(1)}, u32[]{:S(2)}, u32[]{:S(2)}) collective-permute-start(bf16[128,2048]{1,0:T(8,128)(2,1)S(1)} %get-tuple-element.316), channel_id=1, source_target_pairs={{0,16},{4,20},{8,24},{12,28},{16,0},{20,4},{24,8},{28,12},{1,17},{... | collective-permute-start | bytes 1572872 | tf_op jit(solution)/shard_map/ppermute | solution.py:33
  536.5 25.4 %collective-permute-start.38 = (bf16[128,2048]{1,0:T(8,128)(2,1)S(1)}, bf16[128,2048]{1,0:T(8,128)(2,1)S(1)}, u32[]{:S(2)}, u32[]{:S(2)}) collective-permute-start(bf16[128,2048]{1,0:T(8,128)(2,1)S(1)} %get-tuple-element.317), channel_id=1, source_target_pairs={{0,8},{4,12},{8,0},{12,4},{16,24},{20,28},{24,16},{28,20},{1,9},{5... | collective-permute-start | bytes 1572872 | tf_op jit(solution)/shard_map/ppermute | solution.py:33
  561.6 14.9 %collective-permute-start.37 = (bf16[128,2048]{1,0:T(8,128)(2,1)S(1)}, bf16[128,2048]{1,0:T(8,128)(2,1)S(1)}, u32[]{:S(2)}, u32[]{:S(2)}) collective-permute-start(bf16[128,2048]{1,0:T(8,128)(2,1)S(1)} %get-tuple-element.318), channel_id=1, source_target_pairs={{0,16},{4,20},{8,24},{12,28},{16,0},{20,4},{24,8},{28,12},{1,17},{... | collective-permute-start | bytes 1572872 | tf_op jit(solution)/shard_map/ppermute | solution.py:33
  561.9 14.9 %collective-permute-start.36 = (bf16[128,2048]{1,0:T(8,128)(2,1)S(1)}, bf16[128,2048]{1,0:T(8,128)(2,1)S(1)}, u32[]{:S(2)}, u32[]{:S(2)}) collective-permute-start(bf16[128,2048]{1,0:T(8,128)(2,1)S(1)} %get-tuple-element.319), channel_id=1, source_target_pairs={{0,8},{4,12},{8,0},{12,4},{16,24},{20,28},{24,16},{28,20},{1,9},{5... | collective-permute-start | bytes 1572872 | tf_op jit(solution)/shard_map/ppermute | solution.py:33
  562.7 20.0 %collective-permute-start.44 = (bf16[352,512]{1,0:T(8,128)(2,1)S(1)}, bf16[352,512]{1,0:T(8,128)(2,1)S(1)}, u32[]{:S(2)}, u32[]{:S(2)}) collective-permute-start(bf16[352,512]{1,0:T(8,128)(2,1)S(1)} %slice.138), channel_id=1, source_target_pairs={{0,8},{4,12},{8,0},{12,4},{16,24},{20,28},{24,16},{28,20},{1,9},{5... | collective-permute-start | bytes 1081352 | tf_op jit(solution)/shard_map/ppermute | solution.py:33
  564.1 18.6 %collective-permute-start.43 = (bf16[352,512]{1,0:T(8,128)(2,1)S(1)}, bf16[352,512]{1,0:T(8,128)(2,1)S(1)}, u32[]{:S(2)}, u32[]{:S(2)}) collective-permute-start(bf16[352,512]{1,0:T(8,128)(2,1)S(1)} %slice.137), channel_id=1, source_target_pairs={{0,16},{4,20},{8,24},{12,28},{16,0},{20,4},{24,8},{28,12},{1,17},{... | collective-permute-start | bytes 1081352 | tf_op jit(solution)/shard_map/ppermute | solution.py:33
  582.8 33.4 %collective-permute-start.47 = (bf16[2816,512]{1,0:T(8,128)(2,1)S(1)}, bf16[2816,512]{1,0:T(8,128)(2,1)S(1)}, u32[]{:S(2)}, u32[]{:S(2)}) collective-permute-start(bf16[2816,512]{1,0:T(8,128)(2,1)S(1)} %constant_dynamic-update-slice_fusion.23.same_ref), channel_id=1, source_target_pairs={{0,4},{4,0},{8,12},{12,8},{16,20},{20,16},{24,28},{28,24},{1,5},{5... | collective-permute-start | bytes 8650760 | tf_op jit(solution)/shard_map/ppermute | solution.py:33
  582.9 31.2 %collective-permute-start.49 = (bf16[704,512]{1,0:T(8,128)(2,1)S(1)}, bf16[704,512]{1,0:T(8,128)(2,1)S(1)}, u32[]{:S(2)}, u32[]{:S(2)}) collective-permute-start(bf16[704,512]{1,0:T(8,128)(2,1)S(1)} %copy-done.83), channel_id=1, source_target_pairs={{0,16},{4,20},{8,24},{12,28},{16,0},{20,4},{24,8},{28,12},{1,17},{... | collective-permute-start | bytes 2162696 | tf_op jit(solution)/shard_map/ppermute | solution.py:33
  584.7 30.3 %collective-permute-start.48 = (bf16[704,512]{1,0:T(8,128)(2,1)S(1)}, bf16[704,512]{1,0:T(8,128)(2,1)S(1)}, u32[]{:S(2)}, u32[]{:S(2)}) collective-permute-start(bf16[704,512]{1,0:T(8,128)(2,1)S(1)} %copy-done.83), channel_id=1, source_target_pairs={{0,8},{4,12},{8,0},{12,4},{16,24},{20,28},{24,16},{28,20},{1,9},{5... | collective-permute-start | bytes 2162696 | tf_op jit(solution)/shard_map/ppermute | solution.py:33
  586.9 27.2 %collective-permute-start.46 = (bf16[128,2048]{1,0:T(8,128)(2,1)S(1)}, bf16[128,2048]{1,0:T(8,128)(2,1)S(1)}, u32[]{:S(2)}, u32[]{:S(2)}) collective-permute-start(bf16[128,2048]{1,0:T(8,128)(2,1)S(1)} %get-tuple-element.314), channel_id=1, source_target_pairs={{0,8},{4,12},{8,0},{12,4},{16,24},{20,28},{24,16},{28,20},{1,9},{5... | collective-permute-start | bytes 1572872 | tf_op jit(solution)/shard_map/ppermute | solution.py:33
  588.4 25.8 %collective-permute-start.45 = (bf16[128,2048]{1,0:T(8,128)(2,1)S(1)}, bf16[128,2048]{1,0:T(8,128)(2,1)S(1)}, u32[]{:S(2)}, u32[]{:S(2)}) collective-permute-start(bf16[128,2048]{1,0:T(8,128)(2,1)S(1)} %get-tuple-element.315), channel_id=1, source_target_pairs={{0,16},{4,20},{8,24},{12,28},{16,0},{20,4},{24,8},{28,12},{1,17},{... | collective-permute-start | bytes 1572872 | tf_op jit(solution)/shard_map/ppermute | solution.py:33
  621.0 99.0 %all-gather.11.cloned.1.call-start = ((), (), s32[]{:S(2)}) async-start(), calls=%async_computation.13 | async-start | bytes 6488064 | tf_op jit(solution)/shard_map/all_gather | solution.py:843
  621.1 27.3 %collective-permute-start.54 = (bf16[512,768]{1,0:T(8,128)(2,1)}, bf16[512,768]{1,0:T(8,128)(2,1)}, u32[]{:S(2)}, u32[]{:S(2)}) collective-permute-start(bf16[512,768]{1,0:T(8,128)(2,1)} %reduce-scatter.12.cloned.1.call-done), channel_id=1, source_target_pairs={{0,16},{4,20},{8,24},{12,28},{16,0},{20,4},{24,8},{28,12},{1,17},{... | collective-permute-start | bytes 2359304 | tf_op jit(solution)/shard_map/ppermute | solution.py:33
  621.4 26.9 %collective-permute-start.53 = (bf16[512,768]{1,0:T(8,128)(2,1)}, bf16[512,768]{1,0:T(8,128)(2,1)}, u32[]{:S(2)}, u32[]{:S(2)}) collective-permute-start(bf16[512,768]{1,0:T(8,128)(2,1)} %reduce-scatter.12.cloned.1.call-done), channel_id=1, source_target_pairs={{0,8},{4,12},{8,0},{12,4},{16,24},{20,28},{24,16},{28,20},{1,9},{5... | collective-permute-start | bytes 2359304 | tf_op jit(solution)/shard_map/ppermute | solution.py:33
  624.2 24.2 %collective-permute-start.52 = (bf16[352,512]{1,0:T(8,128)(2,1)S(1)}, bf16[352,512]{1,0:T(8,128)(2,1)S(1)}, u32[]{:S(2)}, u32[]{:S(2)}) collective-permute-start(bf16[352,512]{1,0:T(8,128)(2,1)S(1)} %slice.142), channel_id=1, source_target_pairs={{0,8},{4,12},{8,0},{12,4},{16,24},{20,28},{24,16},{28,20},{1,9},{5... | collective-permute-start | bytes 1081352 | tf_op jit(solution)/shard_map/ppermute | solution.py:33
  625.6 22.8 %collective-permute-start.51 = (bf16[352,512]{1,0:T(8,128)(2,1)S(1)}, bf16[352,512]{1,0:T(8,128)(2,1)}, u32[]{:S(2)}, u32[]{:S(2)}) collective-permute-start(bf16[352,512]{1,0:T(8,128)(2,1)S(1)} %slice.141), channel_id=1, source_target_pairs={{0,16},{4,20},{8,24},{12,28},{16,0},{20,4},{24,8},{28,12},{1,17},{... | collective-permute-start | bytes 1081352 | tf_op jit(solution)/shard_map/ppermute | solution.py:33
  627.3 21.0 %collective-permute-start.55 = (f32[2,2048]{1,0:T(2,128)S(1)}, f32[2,2048]{1,0:T(2,128)S(1)}, u32[]{:S(2)}, u32[]{:S(2)}) collective-permute-start(f32[2,2048]{1,0:T(2,128)S(1)} %add.217), channel_id=1, source_target_pairs={{0,8},{4,12},{8,0},{12,4},{16,24},{20,28},{24,16},{28,20},{1,9},{5... | collective-permute-start | bytes 49160 | tf_op jit(solution)/shard_map/ppermute | solution.py:33
  653.1 33.4 %collective-permute-start.56 = (bf16[2816,512]{1,0:T(8,128)(2,1)S(1)}, bf16[2816,512]{1,0:T(8,128)(2,1)S(1)}, u32[]{:S(2)}, u32[]{:S(2)}) collective-permute-start(bf16[2816,512]{1,0:T(8,128)(2,1)S(1)} %constant_dynamic-update-slice_fusion.28.same_ref), channel_id=1, source_target_pairs={{0,4},{4,0},{8,12},{12,8},{16,20},{20,16},{24,28},{28,24},{1,5},{5... | collective-permute-start | bytes 8650760 | tf_op jit(solution)/shard_map/ppermute | solution.py:33
  653.2 15.5 %collective-permute-start.61 = (bf16[256,512]{1,0:T(8,128)(2,1)S(1)}, bf16[256,512]{1,0:T(8,128)(2,1)S(1)}, u32[]{:S(2)}, u32[]{:S(2)}) collective-permute-start(bf16[256,512]{1,0:T(8,128)(2,1)S(1)} %copy-done.90), channel_id=1, source_target_pairs={{0,24},{4,28},{8,16},{12,20},{16,8},{20,12},{24,0},{28,4},{1,25},{... | collective-permute-start | bytes 786440 | tf_op jit(solution)/shard_map/ppermute | solution.py:242
  657.5 29.0 %collective-permute-start.58 = (bf16[256,768]{1,0:T(8,128)(2,1)S(1)}, bf16[256,768]{1,0:T(8,128)(2,1)S(1)}, u32[]{:S(2)}, u32[]{:S(2)}) collective-permute-start(bf16[256,768]{1,0:T(8,128)(2,1)S(1)} %slice.146), channel_id=1, source_target_pairs={{0,8},{4,12},{8,0},{12,4},{16,24},{20,28},{24,16},{28,20},{1,9},{5... | collective-permute-start | bytes 1179656 | tf_op jit(solution)/shard_map/ppermute | solution.py:33
  658.9 27.6 %collective-permute-start.57 = (bf16[256,768]{1,0:T(8,128)(2,1)S(1)}, bf16[256,768]{1,0:T(8,128)(2,1)S(1)}, u32[]{:S(2)}, u32[]{:S(2)}) collective-permute-start(bf16[256,768]{1,0:T(8,128)(2,1)S(1)} %slice.145), channel_id=1, source_target_pairs={{0,16},{4,20},{8,24},{12,28},{16,0},{20,4},{24,8},{28,12},{1,17},{... | collective-permute-start | bytes 1179656 | tf_op jit(solution)/shard_map/ppermute | solution.py:33
  661.5 25.0 %collective-permute-start.60 = (bf16[256,512]{1,0:T(8,128)(2,1)S(1)}, bf16[256,512]{1,0:T(8,128)(2,1)S(1)}, u32[]{:S(2)}, u32[]{:S(2)}) collective-permute-start(bf16[256,512]{1,0:T(8,128)(2,1)S(1)} %copy-done.90), channel_id=1, source_target_pairs={{0,16},{4,20},{8,24},{12,28},{16,0},{20,4},{24,8},{28,12},{1,17},{... | collective-permute-start | bytes 786440 | tf_op jit(solution)/shard_map/ppermute | solution.py:242
  668.7 17.8 %collective-permute-start.59 = (bf16[256,512]{1,0:T(8,128)(2,1)S(1)}, bf16[256,512]{1,0:T(8,128)(2,1)S(1)}, u32[]{:S(2)}, u32[]{:S(2)}) collective-permute-start(bf16[256,512]{1,0:T(8,128)(2,1)S(1)} %copy-done.90), channel_id=1, source_target_pairs={{0,8},{4,12},{8,0},{12,4},{16,24},{20,28},{24,16},{28,20},{1,9},{5... | collective-permute-start | bytes 786440 | tf_op jit(solution)/shard_map/ppermute | solution.py:242
  (119 other events, 1096.7 us)
Sparse Core Ops, SparseCore 0:
  96.3 28.0 all-gather.4
  126.5 106.1 all-gather.6
  234.9 57.4 all-gather.8
  328.6 54.9 reduce-scatter.5
  403.9 54.8 reduce-scatter.7
  461.5 56.0 reduce-scatter.9
  531.7 56.8 reduce-scatter.11
  621.1 23.7 reduce-scatter.13
  648.6 53.3 all-gather.10

commit v10 on v9

--- a/solution.py
+++ b/solution.py
@@ -689,6 +689,12 @@
     def local(d):
         return jnp.concatenate([columns(w, d, block) for w in (w_query, w_key, w_value)], axis=1)
 
+    table, mix = plan_slots(mlp_route, mlp_gate)
+    pick = table.astype(BF)
+    upstream = cotangent.astype(F32)
+    slot_weight = jnp.sum(jnp.where(table, mix[None, :], 0.0), axis=1)[:, None]
+    slot_grad = (mm(pick, cotangent) * slot_weight).astype(BF)
+
     inputs = layer_input.astype(F32)
     root_one = lax.rsqrt(jnp.mean(inputs * inputs, axis=-1, keepdims=True) + EPSILON)
     tables = rotary_tables(length)
@@ -697,8 +703,9 @@
     qkv_w = {d: [local(d)] for d in offsets}
     flows, context, saved = [], {}, {}
     gain_flow = Flow(vector_gather_steps(jnp.stack([gain_attn, gain_mlp])))
+    slot_flow = Flow(copies_steps(slot_grad, straight_steps))
     piece, seg_other, own_gate_up = stage(
-        [gain_flow],
+        [gain_flow, slot_flow],
         (
             lax.ppermute(piece, "shard", ring),
             swap(segments, 1),
@@ -710,15 +717,20 @@
     seg = jnp.concatenate([segments, seg_other], axis=0)
     seg = (seg[:, :, None], seg[:, None, :])
     other = swap(normed, 1)
+    own_out, piece = lax.optimization_barrier((rows_of(w_out, block), piece))
+    own_out = lax.all_gather(own_out, "shard", axis=1, tiled=True)
     for step in range(1, shards):
         qkv_w[0].append(piece)
         flows.append(Flow(gather_steps(piece, lambda d, b: qkv_w[d].append(b))))
         if step < shards - 1:
-            piece, other = stage(flows, (lax.ppermute(piece, "shard", ring), other))
-    own_out, own_gate_up, own_down, qkv_w[0][-1] = lax.optimization_barrier(
-        (rows_of(w_out, block), own_gate_up, rows_of(w_down, units), qkv_w[0][-1])
-    )
-    own_out = lax.all_gather(own_out, "shard", axis=1, tiled=True)
+            extra = (lax.ppermute(piece, "shard", ring), other)
+            if step == shards - 2:
+                extra = (*extra, own_out)
+            piece, other, *rest = stage([*flows, slot_flow], extra)
+            own_out = rest[0] if rest else own_out
+    own_gate_up, own_down, qkv_w[0][-1] = lax.optimization_barrier(
+        (own_gate_up, rows_of(w_down, units), qkv_w[0][-1])
+    )
     both = jnp.concatenate([normed, other], axis=0)
 
     def run(d):
@@ -737,12 +749,6 @@
     stage([out_flow], [run(d) for d in rest])
     out_w = finish(out_flow)
 
-    table, mix = plan_slots(mlp_route, mlp_gate)
-    pick = table.astype(BF)
-    upstream = cotangent.astype(F32)
-    slot_weight = jnp.sum(jnp.where(table, mix[None, :], 0.0), axis=1)[:, None]
-    slot_grad = (mm(pick, cotangent) * slot_weight).astype(BF)
-
     all_context = jnp.concatenate([context[d] for d in offsets], axis=1)
     all_out = jnp.concatenate([out_w[d] for d in offsets], axis=0)
     projected = mm(all_context, all_out)
@@ -754,8 +760,7 @@
 
     dispatched = gather_rows(mm(pick, normed_two).astype(BF), 0)
     act = mm(dispatched, gate_up)
-    slot_grad, act = lax.optimization_barrier((slot_grad, act))
-    all_slot_grad = gather_rows(slot_grad, 0)
+    all_slot_grad = jnp.concatenate(finish(slot_flow), axis=0)
     gate_act, up_act = act[:, :units], act[:, units:]
     sigmoid = jax.nn.sigmoid(gate_act)
     silu = gate_act * sigmoid
@@ -823,26 +828,25 @@
 
     out_blocks = {d: halves(grad_out_w[i * block : (i + 1) * block]) for i, d in enumerate(offsets)}
     out_flow, gate_flow = Flow(scatter_steps(out_blocks)), Flow(copies_steps(sums[0]))
-    other_normed, up_sum = stage(
-        [out_flow, gate_flow], (swap(grad_normed[1], 1), sums[1])
-    )
+    other_normed, up_sum = stage([out_flow], (swap(grad_normed[1], 1), sums[1]))
     grad_normed = grad_normed[0] + other_normed.astype(F32)
     grad_gain_one, first = norm_back(grad_normed, inputs, root_one, gain_one)
     grad_input = (grad_hidden + first).astype(BF)
-    grad_input, gains, up_sum = stage(
-        [out_flow, gate_flow],
-        (grad_input, jnp.stack([grad_gain_one, grad_gain_two]), up_sum),
+    grad_input, gains = stage(
+        [out_flow, gate_flow], (grad_input, jnp.stack([grad_gain_one, grad_gain_two]))
     )
     gain_flow, up_flow = Flow(vector_sum_steps(gains)), Flow(copies_steps(up_sum))
-    sum_qkv = stage([out_flow, gate_flow, up_flow, gain_flow], sum_qkv)
-    sum_out = lax.psum_scatter(finish(out_flow), "shard", scatter_dimension=1, tiled=True)
+    stage([out_flow, gate_flow, gain_flow])
+    own_grad_out, sum_qkv = lax.optimization_barrier((finish(out_flow), sum_qkv))
+    sum_out = lax.psum_scatter(own_grad_out, "shard", scatter_dimension=1, tiled=True)
     qkv_flow = Flow(copies_steps(sum_qkv))
+    sum_out = stage([gate_flow, up_flow, gain_flow], sum_out)
     grad_gate = place_turned(whoami, *finish(gate_flow), units)
-    grad_gate, sum_out = stage([up_flow, qkv_flow, gain_flow], (grad_gate, sum_out))
     down_sum, sum_out = lax.optimization_barrier((sums[2], sum_out))
     all_down = lax.all_gather(down_sum, "rep", axis=0, tiled=True)
     out_flow = Flow(copies_steps(sum_out, straight_steps))
-    stage([up_flow, qkv_flow, out_flow, gain_flow])
+    grad_gate = stage([up_flow, qkv_flow, gain_flow], grad_gate)
+    stage([up_flow, qkv_flow, out_flow])
     grad_up = place_turned(whoami, *finish(up_flow), units)
     grad_up = stage([qkv_flow, out_flow, gain_flow], grad_up)
     grad_query, grad_key, grad_value = place(whoami, *finish(qkv_flow), own, block, True)

time: 743 us -> 750 us (level)
  waiting for transfers between devices: 172 us -> 200 us
  local copies, waits for them, and re-layouts: 93.6 us -> 75.8 us
  Pallas kernels: 250 us -> 236 us
    pallas_call x2 -> x1, Pallas kernels: 58.4 us -> 30.1 us  [gather_rows(): pl.pallas_call(functools.partial(gather_kernel, peers()), out_shape=jax.S...]
    ppermute x3, waiting for transfers between devices: 0.01 us -> 17.9 us  [vector_gather_steps(): lax.ppermute(rows, 'shard', [(i, (i - k) % size) for i in range(size)])]
    ppermute x1, waiting for transfers between devices: 16.2 us -> 0.01 us  [per_device(): lax.ppermute(piece, 'shard', ring)]
    unnamed x243 -> x228, local copies, waits for them, and re-layouts: 62 us -> 48.2 us
    pallas_call x4, Pallas kernels: 42.5 us -> 54.3 us  [attend(): pl.pallas_call(functools.partial(attend_kernel, parts), grid_spec=pltpu.P...]
    ppermute x53 -> x54, waiting for transfers between devices: 113 us -> 115 us  [swap(): return lax.ppermute(value, 'rep', [(i, i ^ bit) for i in range(size)])]
    ppermute x6 -> x9, waiting for transfers between devices: 19.9 us -> 21.9 us  [jump(): return lax.ppermute(value, 'rep', [(i, i ^ offset) for i in range(size)])]
    ppermute x53 -> x54, starting transfers between devices: 47.9 us -> 47.1 us  [swap(): return lax.ppermute(value, 'rep', [(i, i ^ bit) for i in range(size)])]
  transfers between devices with their start and end apart: 77 -> 81, of which waited for: 18 -> 28; matrix products, arithmetic and copies ran while one was open for 20% -> 20% of each run, Pallas kernels for 34% -> 32%
where the time goes in v10:
time: 750 us; the launch traced here: 742 us
  Pallas kernels  236 us (31%)
  waiting for transfers between devices  200 us (27%)
  local copies, waits for them, and re-layouts  75.8 us (10%)
  other arithmetic  72.4 us (10%)
  matrix products  72.2 us (10%)
  starting transfers between devices  70.4 us (9%)
  between operations  15.7 us (2%)
    ppermute x54, waiting for transfers between devices, swap(): return lax.ppermute(value, 'rep', [(i, i ^ bit) for i in range(size)])  115 us
    pallas_call x4, Pallas kernels, attend_back(): pl.pallas_call(attend_back_kernel, grid=(rows // length,), in_specs=[by_s...  68.9 us
    pallas_call x4, Pallas kernels, attend(): pl.pallas_call(functools.partial(attend_kernel, parts), grid_spec=pltpu.P...  54.3 us
    unnamed x228, local copies, waits for them, and re-layouts  48.2 us
    ppermute x54, starting transfers between devices, swap(): return lax.ppermute(value, 'rep', [(i, i ^ bit) for i in range(size)])  47.1 us
    pallas_call x1, Pallas kernels, gather_rows(): pl.pallas_call(functools.partial(gather_kernel, peers()), out_shape=jax.S...  30.1 us
    pallas_call x1, Pallas kernels, reduce_rows(): pl.pallas_call(functools.partial(reduce_kernel, peers()), out_shape=jax.S...  28.7 us
    dot_general x6, matrix products, mm_tn(): lax.dot_general(left, right, (((0,), (0,)), ((), ())), preferred_element_...  27.6 us
  transfers between devices with their start and end apart: 81, of which 28 were waited for; matrix products, arithmetic and copies ran while one was open for 20% of the time, Pallas kernels for 32%

profile of v10, /device:TPU:0, one launch (start us, length us, event | category | flops | bytes accessed | tf_op | source)
XLA Modules:
  0.0 742.3 jit_solution(3056178022878798623)
XLA Ops:
  9.1 2.8 constant_dynamic-update-slice_fusion.27
  12.0 3.9 collective-permute-start.5
  18.6 2.7 constant_dynamic-slice_fusion.4
  23.4 2.2 constant_dynamic-slice_fusion.14
  28.9 14.9 %collective-permute-done.2 = bf16[2,512]{1,0:T(2,128)(2,1)S(1)} collective-permute-done((bf16[2,512]{1,0:T(2,128)(2,1)S(1)}, bf16[2,512]{1,0:T(2,128)(2,1)S(1)}, u32[]{:S(2)}, u32[]{:S(2)}) %collective-permute-start.2) | collective-permute-done | bytes 2080 | tf_op jit(solution)/shard_map/ppermute | solution.py:319
  52.6 3.5 fusion.2
  56.1 2.9 pad_maximum_fusion.3
  63.4 25.8 %collective-permute-done.11.refs_6_ = bf16[512,768]{1,0:T(8,128)(2,1)} collective-permute-done((bf16[512,768]{1,0:T(8,128)(2,1)}, bf16[512,768]{1,0:T(8,128)(2,1)}, u32[]{:S(2)}, u32[]{:S(2)}) %collective-permute-start.11) | collective-permute-done | bytes 786464 | tf_op jit(solution)/shard_map/ppermute | solution.py:726
  97.3 3.6 all-gather.5.cloned.1.call-done.out_ref
  100.9 15.1 %collective-permute-done.14 = bf16[256,768]{1,0:T(8,128)(2,1)} collective-permute-done((bf16[256,768]{1,0:T(8,128)(2,1)}, bf16[256,768]{1,0:T(8,128)(2,1)}, u32[]{:S(2)}, u32[]{:S(2)}) %collective-permute-start.14) | collective-permute-done | bytes 393248 | tf_op jit(solution)/shard_map/ppermute | solution.py:33
  118.5 2.2 pad_maximum_fusion.8.refs_4_.refs_8_
  130.2 3.0 pad_maximum_fusion.refs_0_.refs_1_.refs_2_.refs_3_.x_ref
  134.6 11.7 %attend.4 = (bf16[1024,256]{1,0:T(8,128)(2,1)S(1)}, bf16[1024,768]{1,0:T(8,128)(2,1)S(1)}, f32[1024,2]{1,0:T(8,128)S(1)}) custom-call(s32[1]{0:T(128)} %bitcast.1.z_ref, bf16[1024,2048]{1,0:T(8,128)(2,1)S(1)} %pad_maximum_fusion.refs_0_.refs_1_.refs_2_.refs_3_.x_ref, bf16[1024,2048]{1,0:T(8,128)(2,1)S(1)} %pad_maximum_fusion.refs_0_.refs_1_.refs_2_.refs_3_.x_ref, ...), custom_call_target="tpu_custom_call" | custom-call | flops 3758096384 | bytes 10485760 | tf_op jit(solution)/shard_map/attend/pallas_call | solution.py:398
  146.4 3.6 collective-permute-done.19
  155.2 10.5 %attend.5 = (bf16[1024,256]{1,0:T(8,128)(2,1)S(1)}, bf16[1024,768]{1,0:T(8,128)(2,1)S(1)}, f32[1024,2]{1,0:T(8,128)S(1)}) custom-call(s32[1]{0:T(128)} %bitcast.1.z_ref, bf16[1024,2048]{1,0:T(8,128)(2,1)S(1)} %pad_maximum_fusion.refs_0_.refs_1_.refs_2_.refs_3_.x_ref, bf16[1024,2048]{1,0:T(8,128)(2,1)S(1)} %pad_maximum_fusion.refs_0_.refs_1_.refs_2_.refs_3_.x_ref, ...), custom_call_target="tpu_custom_call" | custom-call | flops 3758096384 | bytes 10485760 | tf_op jit(solution)/shard_map/attend/pallas_call | solution.py:398
  167.8 10.4 %attend.6 = (bf16[1024,256]{1,0:T(8,128)(2,1)S(1)}, bf16[1024,768]{1,0:T(8,128)(2,1)S(1)}, f32[1024,2]{1,0:T(8,128)S(1)}) custom-call(s32[1]{0:T(128)} %bitcast.1.z_ref, bf16[1024,2048]{1,0:T(8,128)(2,1)S(1)} %pad_maximum_fusion.refs_0_.refs_1_.refs_2_.refs_3_.x_ref, bf16[1024,2048]{1,0:T(8,128)(2,1)S(1)} %pad_maximum_fusion.refs_0_.refs_1_.refs_2_.refs_3_.x_ref, ...), custom_call_target="tpu_custom_call" | custom-call | flops 3758096384 | bytes 10485760 | tf_op jit(solution)/shard_map/attend/pallas_call | solution.py:398
  180.5 21.6 %attend.7 = (bf16[1024,256]{1,0:T(8,128)(2,1)S(1)}, bf16[1024,768]{1,0:T(8,128)(2,1)S(1)}, f32[1024,2]{1,0:T(8,128)S(1)}) custom-call(s32[1]{0:T(128)} %bitcast.1.z_ref, bf16[1024,2048]{1,0:T(8,128)(2,1)S(1)} %pad_maximum_fusion.refs_0_.refs_1_.refs_2_.refs_3_.x_ref, bf16[1024,2048]{1,0:T(8,128)(2,1)S(1)} %pad_maximum_fusion.refs_0_.refs_1_.refs_2_.refs_3_.x_ref, ...), custom_call_target="tpu_custom_call" | custom-call | flops 3758096384 | bytes 10485760 | tf_op jit(solution)/shard_map/attend/pallas_call | solution.py:398
  204.5 7.0 collective-permute-done.26
  212.0 4.5 fusion.45
  216.6 3.4 copy-done.60
  227.5 3.2 constant_dynamic-update-slice_fusion.23
  230.7 4.0 multiply_reduce_fusion.2
  237.4 30.1 %gather_rows.1 = bf16[1024,2048]{1,0:T(8,128)(2,1)S(1)} custom-call(bf16[128,2048]{1,0:T(8,128)(2,1)S(1)} %convolution_convert_fusion.6.in_ref), custom_call_target="tpu_custom_call" | custom-call | bytes 62914560 | tf_op jit(solution)/shard_map/gather_rows/pallas_call | solution.py:153
  269.5 11.7 %fusion.46 = f32[1024,1408]{1,0:T(8,128)} fusion(bf16[1024,2048]{1,0:T(8,128)(2,1)} %copy-done.5, bf16[2048,1408]{1,0:T(8,128)(2,1)} %all-gather.7.cloned.1.call-done), kind=kOutput, calls=%fused_computation.181 | convolution fusion | flops 5905580032 | bytes 15728640 | tf_op jit(solution)/shard_map/dot_general | solution.py:20
  281.3 9.1 %all-gather.9.cloned.1.call-done = bf16[704,2048]{1,0:T(8,128)(2,1)} async-done(((bf16[704,512]{1,0:T(8,128)(2,1)}), bf16[704,2048]{1,0:T(8,128)(2,1)}) %all-gather.9.cloned.1.call-update) | async-done | bytes 2883600 | tf_op jit(solution)/shard_map/all_gather | solution.py:742
  290.3 10.3 %multiply_convert_fusion.2 = (bf16[1024,704]{1,0:T(8,128)(2,1)}, bf16[1024,704]{1,0:T(8,128)(2,1)S(1)}, bf16[1024,704]{1,0:T(8,128)(2,1)S(1)}) fusion(f32[1024,1408]{1,0:T(8,128)} %fusion.46, bf16[1024,2048]{1,0:T(8,128)(2,1)} %constant_dynamic-update-slice_fusion.23, bf16[704,2048]{1,0:T(8,128)(2,1)} %all-gather.9.cloned.1.call-done), kind=kOutput, calls=%fused_computation.41 | convolution fusion | flops 2963603456 | bytes 17170432 | tf_op jit(solution)/shard_map/dot_general | solution.py:24
  300.6 3.6 convolution_convert_fusion.1
  306.6 4.3 collective-permute-done.29
  310.9 4.5 convolution_convert_fusion.5
  315.4 11.0 %convolution_convert_fusion.in_ref = bf16[1024,2048]{1,0:T(8,128)(2,1)} fusion(bf16[2048,1408]{1,0:T(8,128)(2,1)} %all-gather.7.cloned.1.call-done, bf16[1024,704]{1,0:T(8,128)(2,1)} %get-tuple-element.208, bf16[1024,704]{1,0:T(8,128)(2,1)} %copy-done.96), kind=kOutput, calls=%fused_computation.30 | convolution fusion | flops 5913444352 | bytes 12845056 | tf_op jit(solution)/shard_map/dot_general | solution.py:24
  329.1 28.7 %reduce_rows.1 = bf16[128,2048]{1,0:T(8,128)(2,1)S(1)} custom-call(bf16[1024,2048]{1,0:T(8,128)(2,1)S(1)} %copy-done.8), custom_call_target="tpu_custom_call" | custom-call | bytes 62914560 | tf_op jit(solution)/shard_map/reduce_rows/pallas_call | solution.py:218
  359.4 3.6 multiply_convert_fusion
  364.3 2.5 add_convert_fusion.1
  372.9 4.5 convolution_convert_fusion.4
  377.4 5.0 pad_maximum_fusion.1.grad_ref
  382.4 17.0 %attend_back.4 = (bf16[1024,768]{1,0:T(8,128)(2,1)S(1)}, bf16[1024,768]{1,0:T(8,128)(2,1)S(1)}, bf16[1024,768]{1,0:T(8,128)(2,1)}) custom-call(bf16[1024,2048]{1,0:T(8,128)(2,1)} %pad_maximum_fusion.1.grad_ref, bf16[256,2048]{1,0:T(8,128)(2,1)S(1)} %copy-done.34, bf16[1024,768]{1,0:T(8,128)(2,1)} %copy-done.38, f32[1024,2]{1,0:T(8,128)S(1)} %copy-done.46, ...), custom_call_target="tpu_custom_call" | custom-call | flops 5637144576 | bytes 15728640 | tf_op jit(solution)/shard_map/attend_back/pallas_call | solution.py:487
  405.8 17.5 %attend_back.6 = (bf16[1024,768]{1,0:T(8,128)(2,1)S(1)}, bf16[1024,768]{1,0:T(8,128)(2,1)S(1)}, bf16[1024,768]{1,0:T(8,128)(2,1)}) custom-call(bf16[1024,2048]{1,0:T(8,128)(2,1)} %pad_maximum_fusion.1.grad_ref, bf16[256,2048]{1,0:T(8,128)(2,1)S(1)} %copy-done.18, bf16[1024,768]{1,0:T(8,128)(2,1)} %copy-done.37, f32[1024,2]{1,0:T(8,128)S(1)} %copy-done.44, ...), custom_call_target="tpu_custom_call" | custom-call | flops 5637144576 | bytes 15728640 | tf_op jit(solution)/shard_map/attend_back/pallas_call | solution.py:487
  424.4 2.4 add_convert_fusion.10
  426.9 17.1 %attend_back.5 = (bf16[1024,768]{1,0:T(8,128)(2,1)S(1)}, bf16[1024,768]{1,0:T(8,128)(2,1)S(1)}, bf16[1024,768]{1,0:T(8,128)(2,1)}) custom-call(bf16[1024,2048]{1,0:T(8,128)(2,1)} %pad_maximum_fusion.1.grad_ref, bf16[256,2048]{1,0:T(8,128)(2,1)S(1)} %copy-done.16, bf16[1024,768]{1,0:T(8,128)(2,1)} %copy-done.36, f32[1024,2]{1,0:T(8,128)S(1)} %copy-done.42, ...), custom_call_target="tpu_custom_call" | custom-call | flops 5637144576 | bytes 15728640 | tf_op jit(solution)/shard_map/attend_back/pallas_call | solution.py:487
  446.3 4.6 convolution_convert_fusion.3
  452.1 3.5 add_convert_fusion.4
  457.3 3.4 add_convert_fusion.5
  462.0 17.4 %attend_back.7 = (bf16[1024,768]{1,0:T(8,128)(2,1)S(1)}, bf16[1024,768]{1,0:T(8,128)(2,1)S(1)}, bf16[1024,768]{1,0:T(8,128)(2,1)}) custom-call(bf16[1024,2048]{1,0:T(8,128)(2,1)} %pad_maximum_fusion.1.grad_ref, bf16[256,2048]{1,0:T(8,128)(2,1)S(1)} %copy-done.33, bf16[1024,768]{1,0:T(8,128)(2,1)} %copy-done.35, f32[1024,2]{1,0:T(8,128)S(1)} %get-tuple-element.229.lse_ref, ...), custom_call_target="tpu_custom_call" | custom-call | flops 5637144576 | bytes 15728640 | tf_op jit(solution)/shard_map/attend_back/pallas_call | solution.py:487
  479.3 10.6 %convolution_convert_fusion.2 = bf16[1024,2048]{1,0:T(8,128)(2,1)} fusion(bf16[1024,1024]{1,0:T(8,128)(2,1)} %copy-done.78, bf16[1024,2048]{1,0:T(8,128)(2,1)} %pad_maximum_fusion.1.grad_ref), kind=kOutput, calls=%fused_computation.32 | convolution fusion | flops 4297064448 | bytes 10485760 | tf_op jit(solution)/shard_map/dot_general | solution.py:28
  492.2 24.3 %normed_back.1 = (f32[512,2048]{1,0:T(8,128)}, bf16[512,2048]{1,0:T(8,128)(2,1)}) custom-call(s32[1]{0:T(128)} %bitcast.1.z_ref, bf16[1024,768]{1,0:T(8,128)(2,1)} %copy-done.50, bf16[1024,768]{1,0:T(8,128)(2,1)} %copy-done.49, bf16[1024,768]{1,0:T(8,128)(2,1)} %copy-done.48, bf16[1024,768]{1,0:T(8,128)(2,1)} %copy-done.47, ...), custom_call_target="tpu_custom_call" | custom-call | flops 12884901888 | bytes 27262976 | tf_op jit(solution)/shard_map/normed_back/pallas_call | solution.py:543
  516.5 3.9 collective-permute-done.39
  520.5 2.6 add_convert_fusion.2
  533.5 10.7 %collective-permute-done.45 = bf16[128,2048]{1,0:T(8,128)(2,1)S(1)} collective-permute-done((bf16[128,2048]{1,0:T(8,128)(2,1)S(1)}, bf16[128,2048]{1,0:T(8,128)(2,1)S(1)}, u32[]{:S(2)}, u32[]{:S(2)}) %collective-permute-start.45) | collective-permute-done | bytes 524320 | tf_op jit(solution)/shard_map/ppermute | solution.py:33
  550.0 2.7 fusion.6
  552.6 17.7 %collective-permute-done.41 = bf16[128,2048]{1,0:T(8,128)(2,1)S(1)} collective-permute-done((bf16[128,2048]{1,0:T(8,128)(2,1)S(1)}, bf16[128,2048]{1,0:T(8,128)(2,1)S(1)}, u32[]{:S(2)}, u32[]{:S(2)}) %collective-permute-start.41) | collective-permute-done | bytes 524320 | tf_op jit(solution)/shard_map/ppermute | solution.py:33
  576.0 13.3 %collective-permute-done.50 = bf16[352,512]{1,0:T(8,128)(2,1)S(1)} collective-permute-done((bf16[352,512]{1,0:T(8,128)(2,1)S(1)}, bf16[352,512]{1,0:T(8,128)(2,1)S(1)}, u32[]{:S(2)}, u32[]{:S(2)}) %collective-permute-start.50) | collective-permute-done | bytes 360480 | tf_op jit(solution)/shard_map/ppermute | solution.py:33
  591.7 2.5 add_convert_fusion.7
  597.8 16.0 %collective-permute-done.55 = f32[2,2048]{1,0:T(2,128)S(1)} collective-permute-done((f32[2,2048]{1,0:T(2,128)S(1)}, f32[2,2048]{1,0:T(2,128)S(1)}, u32[]{:S(2)}, u32[]{:S(2)}) %collective-permute-start.55) | collective-permute-done | bytes 16416 | tf_op jit(solution)/shard_map/ppermute | solution.py:33
  613.8 6.8 reduce-scatter.14.cloned.1.call-done
  633.8 6.8 place_turned.2
  640.6 8.4 %collective-permute-done.59 = bf16[512,768]{1,0:T(8,128)(2,1)S(1)} collective-permute-done((bf16[512,768]{1,0:T(8,128)(2,1)}, bf16[512,768]{1,0:T(8,128)(2,1)S(1)}, u32[]{:S(2)}, u32[]{:S(2)}) %collective-permute-start.59) | collective-permute-done | bytes 786464 | tf_op jit(solution)/shard_map/ppermute | solution.py:33
  650.5 7.2 collective-permute-done.60
  665.5 10.1 %collective-permute-done.66 = bf16[256,512]{1,0:T(8,128)(2,1)S(1)} collective-permute-done((bf16[256,512]{1,0:T(8,128)(2,1)S(1)}, bf16[256,512]{1,0:T(8,128)(2,1)S(1)}, u32[]{:S(2)}, u32[]{:S(2)}) %collective-permute-start.66) | collective-permute-done | bytes 262176 | tf_op jit(solution)/shard_map/ppermute | solution.py:242
  675.6 2.5 collective-permute-start.64
  679.9 11.0 %collective-permute-done.65 = bf16[256,512]{1,0:T(8,128)(2,1)S(1)} collective-permute-done((bf16[256,512]{1,0:T(8,128)(2,1)S(1)}, bf16[256,512]{1,0:T(8,128)(2,1)S(1)}, u32[]{:S(2)}, u32[]{:S(2)}) %collective-permute-start.65) | collective-permute-done | bytes 262176 | tf_op jit(solution)/shard_map/ppermute | solution.py:242
  703.5 5.0 place_turned.3
  708.5 6.5 place.3
  714.9 11.0 %place.2 = (f32[512,2048]{1,0:T(8,128)}, f32[512,2048]{1,0:T(8,128)}, f32[512,2048]{1,0:T(8,128)}) custom-call(s32[1]{0:T(128)} %bitcast.6.me_ref, bf16[2048,768]{1,0:T(8,128)(2,1)} %constant_dynamic-update-slice_fusion.38.same_ref, bf16[2048,768]{1,0:T(8,128)(2,1)} %collective-permute-done.67.other_ref), custom_call_target="tpu_custom_call" | custom-call | bytes 25165824 | tf_op jit(solution)/shard_map/place/pallas_call | solution.py:604
  726.5 8.9 %convert_element_type.237 = f32[5632,512]{1,0:T(8,128)} convert(bf16[5632,512]{1,0:T(8,128)(2,1)} %all-gather.11.cloned.1.call-done) | non-fusion elementwise | flops 2883584 | bytes 17301504 | tf_op jit(solution)/shard_map/convert_element_type | solution.py:854
  (451 shorter events, 164.0 us)
Async XLA Ops:
  7.2 93.7 %all-gather.5.cloned.1.call-start = ((), (), s32[]{:S(2)}) async-start(), calls=%async_computation.5 | async-start | bytes 1310720 | tf_op jit(solution)/shard_map/all_gather | solution.py:721
  12.0 39.9 %collective-permute-start.5 = (bf16[128,2048]{1,0:T(8,128)(2,1)S(1)}, bf16[128,2048]{1,0:T(8,128)(2,1)}, u32[]{:S(2)}, u32[]{:S(2)}) collective-permute-start(bf16[128,2048]{1,0:T(8,128)(2,1)S(1)} %get-tuple-element.360), channel_id=1, source_target_pairs={{0,24},{4,28},{8,16},{12,20},{16,8},{20,12},{24,0},{28,4},{1,25},{... | collective-permute-start | bytes 1572872 | tf_op jit(solution)/shard_map/ppermute | solution.py:242
  15.9 36.0 %collective-permute-start.4 = (bf16[128,2048]{1,0:T(8,128)(2,1)S(1)}, bf16[128,2048]{1,0:T(8,128)(2,1)}, u32[]{:S(2)}, u32[]{:S(2)}) collective-permute-start(bf16[128,2048]{1,0:T(8,128)(2,1)S(1)} %get-tuple-element.360), channel_id=1, source_target_pairs={{0,16},{4,20},{8,24},{12,28},{16,0},{20,4},{24,8},{28,12},{1,17},{... | collective-permute-start | bytes 1572872 | tf_op jit(solution)/shard_map/ppermute | solution.py:242
  16.4 35.5 %collective-permute-start.3 = (bf16[128,2048]{1,0:T(8,128)(2,1)S(1)}, bf16[128,2048]{1,0:T(8,128)(2,1)}, u32[]{:S(2)}, u32[]{:S(2)}) collective-permute-start(bf16[128,2048]{1,0:T(8,128)(2,1)S(1)} %get-tuple-element.360), channel_id=1, source_target_pairs={{0,8},{4,12},{8,0},{12,4},{16,24},{20,28},{24,16},{28,20},{1,9},{5... | collective-permute-start | bytes 1572872 | tf_op jit(solution)/shard_map/ppermute | solution.py:242
  21.3 30.6 %collective-permute-start.6 = (bf16[512,768]{1,0:T(8,128)(2,1)S(1)}, bf16[512,768]{1,0:T(8,128)(2,1)}, u32[]{:S(2)}, u32[]{:S(2)}) collective-permute-start(bf16[512,768]{1,0:T(8,128)(2,1)S(1)} %pad_maximum_fusion.7.refs_4_), channel_id=1, source_target_pairs={{0,1},{1,2},{2,3},{3,0},{4,5},{5,6},{6,7},{7,4},{8,9},{9,10},{10,1... | collective-permute-start | bytes 2359304 | tf_op jit(solution)/shard_map/ppermute | solution.py:710
  25.7 18.1 %collective-permute-start.2 = (bf16[2,512]{1,0:T(2,128)(2,1)S(1)}, bf16[2,512]{1,0:T(2,128)(2,1)S(1)}, u32[]{:S(2)}, u32[]{:S(2)}) collective-permute-start(bf16[2,512]{1,0:T(2,128)(2,1)S(1)} %get-tuple-element.314), channel_id=1, source_target_pairs={{0,1},{1,2},{2,3},{3,0},{4,5},{5,6},{6,7},{7,4},{8,9},{9,10},{10,1... | collective-permute-start | bytes 6152 | tf_op jit(solution)/shard_map/ppermute | solution.py:319
  56.1 33.0 %collective-permute-start.12 = (bf16[512,2048]{1,0:T(8,128)(2,1)}, bf16[512,2048]{1,0:T(8,128)(2,1)}, u32[]{:S(2)}, u32[]{:S(2)}) collective-permute-start(bf16[512,2048]{1,0:T(8,128)(2,1)} %fusion.2), channel_id=1, source_target_pairs={{0,4},{4,0},{8,12},{12,8},{16,20},{20,16},{24,28},{28,24},{1,5},{5... | collective-permute-start | bytes 6291464 | tf_op jit(solution)/shard_map/ppermute | solution.py:33
  59.0 30.1 %collective-permute-start.10 = (bf16[512,2048]{1,0:T(8,128)(2,1)}, bf16[512,2048]{1,0:T(8,128)(2,1)}, u32[]{:S(2)}, u32[]{:S(2)}) collective-permute-start(bf16[512,2048]{1,0:T(8,128)(2,1)} %pad_maximum_fusion.3), channel_id=1, source_target_pairs={{0,4},{4,0},{8,12},{12,8},{16,20},{20,16},{24,28},{28,24},{1,5},{5... | collective-permute-start | bytes 6291464 | tf_op jit(solution)/shard_map/ppermute | solution.py:33
  60.3 28.8 %collective-permute-start.11 = (bf16[512,768]{1,0:T(8,128)(2,1)}, bf16[512,768]{1,0:T(8,128)(2,1)}, u32[]{:S(2)}, u32[]{:S(2)}) collective-permute-start(bf16[512,768]{1,0:T(8,128)(2,1)} %collective-permute-done.6.refs_5_), channel_id=1, source_target_pairs={{0,1},{1,2},{2,3},{3,0},{4,5},{5,6},{6,7},{7,4},{8,9},{9,10},{10,1... | collective-permute-start | bytes 2359304 | tf_op jit(solution)/shard_map/ppermute | solution.py:726
  60.3 28.8 %collective-permute-start.9 = (bf16[512,768]{1,0:T(8,128)(2,1)}, bf16[512,768]{1,0:T(8,128)(2,1)S(1)}, u32[]{:S(2)}, u32[]{:S(2)}) collective-permute-start(bf16[512,768]{1,0:T(8,128)(2,1)} %collective-permute-done.6.refs_5_), channel_id=1, source_target_pairs={{0,16},{4,20},{8,24},{12,28},{16,0},{20,4},{24,8},{28,12},{1,17},{... | collective-permute-start | bytes 2359304 | tf_op jit(solution)/shard_map/ppermute | solution.py:33
  61.8 27.3 %collective-permute-start.8 = (bf16[512,768]{1,0:T(8,128)(2,1)}, bf16[512,768]{1,0:T(8,128)(2,1)S(1)}, u32[]{:S(2)}, u32[]{:S(2)}) collective-permute-start(bf16[512,768]{1,0:T(8,128)(2,1)} %collective-permute-done.6.refs_5_), channel_id=1, source_target_pairs={{0,8},{4,12},{8,0},{12,4},{16,24},{20,28},{24,16},{28,20},{1,9},{5... | collective-permute-start | bytes 2359304 | tf_op jit(solution)/shard_map/ppermute | solution.py:33
  63.3 206.2 %all-gather.7.cloned.1.call-start = ((), (), s32[]{:S(2)}) async-start(), calls=%async_computation.6 | async-start | bytes 7208960 | tf_op jit(solution)/shard_map/all_gather | solution.py:741
  89.2 26.9 %collective-permute-start.17 = (bf16[512,768]{1,0:T(8,128)(2,1)}, bf16[512,768]{1,0:T(8,128)(2,1)}, u32[]{:S(2)}, u32[]{:S(2)}) collective-permute-start(bf16[512,768]{1,0:T(8,128)(2,1)} %collective-permute-done.11.refs_6_), channel_id=1, source_target_pairs={{0,1},{1,2},{2,3},{3,0},{4,5},{5,6},{6,7},{7,4},{8,9},{9,10},{10,1... | collective-permute-start | bytes 2359304 | tf_op jit(solution)/shard_map/ppermute | solution.py:726
  89.7 26.3 %collective-permute-start.16 = (bf16[512,768]{1,0:T(8,128)(2,1)}, bf16[512,768]{1,0:T(8,128)(2,1)}, u32[]{:S(2)}, u32[]{:S(2)}) collective-permute-start(bf16[512,768]{1,0:T(8,128)(2,1)} %collective-permute-done.11.refs_6_), channel_id=1, source_target_pairs={{0,16},{4,20},{8,24},{12,28},{16,0},{20,4},{24,8},{28,12},{1,17},{... | collective-permute-start | bytes 2359304 | tf_op jit(solution)/shard_map/ppermute | solution.py:33
  91.2 24.9 %collective-permute-start.15 = (bf16[512,768]{1,0:T(8,128)(2,1)}, bf16[512,768]{1,0:T(8,128)(2,1)}, u32[]{:S(2)}, u32[]{:S(2)}) collective-permute-start(bf16[512,768]{1,0:T(8,128)(2,1)} %collective-permute-done.11.refs_6_), channel_id=1, source_target_pairs={{0,8},{4,12},{8,0},{12,4},{16,24},{20,28},{24,16},{28,20},{1,9},{5... | collective-permute-start | bytes 2359304 | tf_op jit(solution)/shard_map/ppermute | solution.py:33
  94.2 21.8 %collective-permute-start.14 = (bf16[256,768]{1,0:T(8,128)(2,1)}, bf16[256,768]{1,0:T(8,128)(2,1)}, u32[]{:S(2)}, u32[]{:S(2)}) collective-permute-start(bf16[256,768]{1,0:T(8,128)(2,1)} %slice.116), channel_id=1, source_target_pairs={{0,8},{4,12},{8,0},{12,4},{16,24},{20,28},{24,16},{28,20},{1,9},{5... | collective-permute-start | bytes 1179656 | tf_op jit(solution)/shard_map/ppermute | solution.py:33
  94.8 21.3 %collective-permute-start.13 = (bf16[256,768]{1,0:T(8,128)(2,1)}, bf16[256,768]{1,0:T(8,128)(2,1)}, u32[]{:S(2)}, u32[]{:S(2)}) collective-permute-start(bf16[256,768]{1,0:T(8,128)(2,1)} %slice.115), channel_id=1, source_target_pairs={{0,16},{4,20},{8,24},{12,28},{16,0},{20,4},{24,8},{28,12},{1,17},{... | collective-permute-start | bytes 1179656 | tf_op jit(solution)/shard_map/ppermute | solution.py:33
  116.1 174.3 %all-gather.9.cloned.1.call-start = ((), (), s32[]{:S(2)}) async-start(), calls=%async_computation.7 | async-start | bytes 3604480 | tf_op jit(solution)/shard_map/all_gather | solution.py:742
  123.0 27.0 %collective-permute-start.21 = (bf16[512,768]{1,0:T(8,128)(2,1)}, bf16[512,768]{1,0:T(8,128)(2,1)S(1)}, u32[]{:S(2)}, u32[]{:S(2)}) collective-permute-start(bf16[512,768]{1,0:T(8,128)(2,1)} %collective-permute-done.17.refs_7_), channel_id=1, source_target_pairs={{0,16},{4,20},{8,24},{12,28},{16,0},{20,4},{24,8},{28,12},{1,17},{... | collective-permute-start | bytes 2359304 | tf_op jit(solution)/shard_map/ppermute | solution.py:33
  124.1 25.9 %collective-permute-start.20 = (bf16[512,768]{1,0:T(8,128)(2,1)}, bf16[512,768]{1,0:T(8,128)(2,1)S(1)}, u32[]{:S(2)}, u32[]{:S(2)}) collective-permute-start(bf16[512,768]{1,0:T(8,128)(2,1)} %collective-permute-done.17.refs_7_), channel_id=1, source_target_pairs={{0,8},{4,12},{8,0},{12,4},{16,24},{20,28},{24,16},{28,20},{1,9},{5... | collective-permute-start | bytes 2359304 | tf_op jit(solution)/shard_map/ppermute | solution.py:33
  127.7 22.3 %collective-permute-start.19 = (bf16[256,768]{1,0:T(8,128)(2,1)S(1)}, bf16[256,768]{1,0:T(8,128)(2,1)S(1)}, u32[]{:S(2)}, u32[]{:S(2)}) collective-permute-start(bf16[256,768]{1,0:T(8,128)(2,1)S(1)} %slice.118), channel_id=1, source_target_pairs={{0,8},{4,12},{8,0},{12,4},{16,24},{20,28},{24,16},{28,20},{1,9},{5... | collective-permute-start | bytes 1179656 | tf_op jit(solution)/shard_map/ppermute | solution.py:33
  128.3 21.7 %collective-permute-start.18 = (bf16[256,768]{1,0:T(8,128)(2,1)S(1)}, bf16[256,768]{1,0:T(8,128)(2,1)S(1)}, u32[]{:S(2)}, u32[]{:S(2)}) collective-permute-start(bf16[256,768]{1,0:T(8,128)(2,1)S(1)} %slice.117), channel_id=1, source_target_pairs={{0,16},{4,20},{8,24},{12,28},{16,0},{20,4},{24,8},{28,12},{1,17},{... | collective-permute-start | bytes 1179656 | tf_op jit(solution)/shard_map/ppermute | solution.py:33
  150.0 52.1 %collective-permute-start.25 = (bf16[256,2048]{1,0:T(8,128)(2,1)S(1)}, bf16[256,2048]{1,0:T(8,128)(2,1)S(1)}, u32[]{:S(2)}, u32[]{:S(2)}) collective-permute-start(bf16[256,2048]{1,0:T(8,128)(2,1)S(1)} %copy-done.32), channel_id=1, source_target_pairs={{0,16},{4,20},{8,24},{12,28},{16,0},{20,4},{24,8},{28,12},{1,17},{... | collective-permute-start | bytes 3145736 | tf_op jit(solution)/shard_map/ppermute | solution.py:33
  150.4 51.8 %collective-permute-start.24 = (bf16[256,2048]{1,0:T(8,128)(2,1)S(1)}, bf16[256,2048]{1,0:T(8,128)(2,1)S(1)}, u32[]{:S(2)}, u32[]{:S(2)}) collective-permute-start(bf16[256,2048]{1,0:T(8,128)(2,1)S(1)} %copy-done.32), channel_id=1, source_target_pairs={{0,8},{4,12},{8,0},{12,4},{16,24},{20,28},{24,16},{28,20},{1,9},{5... | collective-permute-start | bytes 3145736 | tf_op jit(solution)/shard_map/ppermute | solution.py:33
  151.9 28.4 %collective-permute-start.23 = (bf16[256,768]{1,0:T(8,128)(2,1)S(1)}, bf16[256,768]{1,0:T(8,128)(2,1)S(1)}, u32[]{:S(2)}, u32[]{:S(2)}) collective-permute-start(bf16[256,768]{1,0:T(8,128)(2,1)S(1)} %slice.120), channel_id=1, source_target_pairs={{0,8},{4,12},{8,0},{12,4},{16,24},{20,28},{24,16},{28,20},{1,9},{5... | collective-permute-start | bytes 1179656 | tf_op jit(solution)/shard_map/ppermute | solution.py:33
  152.5 27.8 %collective-permute-start.22 = (bf16[256,768]{1,0:T(8,128)(2,1)S(1)}, bf16[256,768]{1,0:T(8,128)(2,1)S(1)}, u32[]{:S(2)}, u32[]{:S(2)}) collective-permute-start(bf16[256,768]{1,0:T(8,128)(2,1)S(1)} %slice.119), channel_id=1, source_target_pairs={{0,16},{4,20},{8,24},{12,28},{16,0},{20,4},{24,8},{28,12},{1,17},{... | collective-permute-start | bytes 1179656 | tf_op jit(solution)/shard_map/ppermute | solution.py:33
  221.6 298.9 %reduce-scatter.6.cloned.1.call-start = ((), (), s32[]{:S(2)}) async-start(), calls=%async_computation.8 | async-start | bytes 3604480 | tf_op jit(solution)/shard_map/reduce_scatter | solution.py:812
  326.4 194.1 %reduce-scatter.8.cloned.1.call-start = ((), (), s32[]{:S(2)}) async-start(), calls=%async_computation.9 | async-start | bytes 3604480 | tf_op jit(solution)/shard_map/reduce_scatter | solution.py:812
  369.4 32.3 %collective-permute-start.32 = (bf16[128,2048]{1,0:T(8,128)(2,1)}, bf16[128,2048]{1,0:T(8,128)(2,1)}, u32[]{:S(2)}, u32[]{:S(2)}) collective-permute-start(bf16[128,2048]{1,0:T(8,128)(2,1)} %get-tuple-element.328), channel_id=1, source_target_pairs={{0,24},{4,28},{8,16},{12,20},{16,8},{20,12},{24,0},{28,4},{1,25},{... | collective-permute-start | bytes 1572872 | tf_op jit(solution)/shard_map/ppermute | solution.py:242
  371.5 30.1 %collective-permute-start.31 = (bf16[128,2048]{1,0:T(8,128)(2,1)}, bf16[128,2048]{1,0:T(8,128)(2,1)}, u32[]{:S(2)}, u32[]{:S(2)}) collective-permute-start(bf16[128,2048]{1,0:T(8,128)(2,1)} %get-tuple-element.329), channel_id=1, source_target_pairs={{0,16},{4,20},{8,24},{12,28},{16,0},{20,4},{24,8},{28,12},{1,17},{... | collective-permute-start | bytes 1572872 | tf_op jit(solution)/shard_map/ppermute | solution.py:242
  372.1 29.5 %collective-permute-start.30 = (bf16[128,2048]{1,0:T(8,128)(2,1)}, bf16[128,2048]{1,0:T(8,128)(2,1)}, u32[]{:S(2)}, u32[]{:S(2)}) collective-permute-start(bf16[128,2048]{1,0:T(8,128)(2,1)} %get-tuple-element.330), channel_id=1, source_target_pairs={{0,8},{4,12},{8,0},{12,4},{16,24},{20,28},{24,16},{28,20},{1,9},{5... | collective-permute-start | bytes 1572872 | tf_op jit(solution)/shard_map/ppermute | solution.py:242
  401.7 125.6 %reduce-scatter.10.cloned.1.call-start = ((), (), s32[]{:S(2)}) async-start(), calls=%async_computation.10 | async-start | bytes 3604480 | tf_op jit(solution)/shard_map/reduce_scatter | solution.py:812
  401.9 49.0 %collective-permute-start.36 = (bf16[1024,768]{1,0:T(8,128)(2,1)}, bf16[1024,768]{1,0:T(8,128)(2,1)}, u32[]{:S(2)}, u32[]{:S(2)}) collective-permute-start(bf16[1024,768]{1,0:T(8,128)(2,1)} %copy-done.40), channel_id=1, source_target_pairs={{0,8},{4,12},{8,0},{12,4},{16,24},{20,28},{24,16},{28,20},{1,9},{5... | collective-permute-start | bytes 4718600 | tf_op jit(solution)/shard_map/ppermute | solution.py:33
  403.3 47.6 %collective-permute-start.37 = (bf16[1024,768]{1,0:T(8,128)(2,1)}, bf16[1024,768]{1,0:T(8,128)(2,1)}, u32[]{:S(2)}, u32[]{:S(2)}) collective-permute-start(bf16[1024,768]{1,0:T(8,128)(2,1)} %get-tuple-element.218), channel_id=1, source_target_pairs={{0,16},{4,20},{8,24},{12,28},{16,0},{20,4},{24,8},{28,12},{1,17},{... | collective-permute-start | bytes 4718600 | tf_op jit(solution)/shard_map/ppermute | solution.py:33
  450.9 144.3 %reduce-scatter.12.cloned.1.call-start = ((), (), s32[]{:S(2)}) async-start(), calls=%async_computation.11 | async-start | bytes 3932160 | tf_op jit(solution)/shard_map/reduce_scatter | solution.py:827
  450.9 41.2 %collective-permute-start.34 = (bf16[1024,768]{1,0:T(8,128)(2,1)}, bf16[1024,768]{1,0:T(8,128)(2,1)S(1)}, u32[]{:S(2)}, u32[]{:S(2)}) collective-permute-start(bf16[1024,768]{1,0:T(8,128)(2,1)} %copy-done.39), channel_id=1, source_target_pairs={{0,8},{4,12},{8,0},{12,4},{16,24},{20,28},{24,16},{28,20},{1,9},{5... | collective-permute-start | bytes 4718600 | tf_op jit(solution)/shard_map/ppermute | solution.py:33
  451.9 40.2 %collective-permute-start.35 = (bf16[1024,768]{1,0:T(8,128)(2,1)}, bf16[1024,768]{1,0:T(8,128)(2,1)S(1)}, u32[]{:S(2)}, u32[]{:S(2)}) collective-permute-start(bf16[1024,768]{1,0:T(8,128)(2,1)} %get-tuple-element.216), channel_id=1, source_target_pairs={{0,16},{4,20},{8,24},{12,28},{16,0},{20,4},{24,8},{28,12},{1,17},{... | collective-permute-start | bytes 4718600 | tf_op jit(solution)/shard_map/ppermute | solution.py:33
  455.6 64.8 %collective-permute-start.39 = (bf16[1024,768]{1,0:T(8,128)(2,1)}, bf16[1024,768]{1,0:T(8,128)(2,1)}, u32[]{:S(2)}, u32[]{:S(2)}) collective-permute-start(bf16[1024,768]{1,0:T(8,128)(2,1)} %add_convert_fusion.4), channel_id=1, source_target_pairs={{0,8},{4,12},{8,0},{12,4},{16,24},{20,28},{24,16},{28,20},{1,9},{5... | collective-permute-start | bytes 4718600 | tf_op jit(solution)/shard_map/ppermute | solution.py:33
  460.7 59.8 %collective-permute-start.38 = (bf16[1024,768]{1,0:T(8,128)(2,1)}, bf16[1024,768]{1,0:T(8,128)(2,1)}, u32[]{:S(2)}, u32[]{:S(2)}) collective-permute-start(bf16[1024,768]{1,0:T(8,128)(2,1)} %add_convert_fusion.5), channel_id=1, source_target_pairs={{0,16},{4,20},{8,24},{12,28},{16,0},{20,4},{24,8},{28,12},{1,17},{... | collective-permute-start | bytes 4718600 | tf_op jit(solution)/shard_map/ppermute | solution.py:33
  527.3 93.2 %reduce-scatter.14.cloned.1.call-start = ((), (), s32[]{:S(2)}) async-start(), calls=%async_computation.12 | async-start | bytes 1310720 | tf_op jit(solution)/shard_map/reduce_scatter | solution.py:841
  527.4 18.8 %collective-permute-start.46 = (bf16[512,2048]{1,0:T(8,128)(2,1)}, bf16[512,2048]{1,0:T(8,128)(2,1)S(1)}, u32[]{:S(2)}, u32[]{:S(2)}) collective-permute-start(bf16[512,2048]{1,0:T(8,128)(2,1)} %get-tuple-element.249), channel_id=1, source_target_pairs={{0,4},{4,0},{8,12},{12,8},{16,20},{20,16},{24,28},{28,24},{1,5},{5... | collective-permute-start | bytes 6291464 | tf_op jit(solution)/shard_map/ppermute | solution.py:33
  531.4 39.8 %collective-permute-start.43 = (bf16[704,512]{1,0:T(8,128)(2,1)S(1)}, bf16[704,512]{1,0:T(8,128)(2,1)S(1)}, u32[]{:S(2)}, u32[]{:S(2)}) collective-permute-start(bf16[704,512]{1,0:T(8,128)(2,1)S(1)} %copy-done.73), channel_id=1, source_target_pairs={{0,16},{4,20},{8,24},{12,28},{16,0},{20,4},{24,8},{28,12},{1,17},{... | collective-permute-start | bytes 2162696 | tf_op jit(solution)/shard_map/ppermute | solution.py:33
  533.1 38.1 %collective-permute-start.42 = (bf16[704,512]{1,0:T(8,128)(2,1)S(1)}, bf16[704,512]{1,0:T(8,128)(2,1)S(1)}, u32[]{:S(2)}, u32[]{:S(2)}) collective-permute-start(bf16[704,512]{1,0:T(8,128)(2,1)S(1)} %copy-done.73), channel_id=1, source_target_pairs={{0,8},{4,12},{8,0},{12,4},{16,24},{20,28},{24,16},{28,20},{1,9},{5... | collective-permute-start | bytes 2162696 | tf_op jit(solution)/shard_map/ppermute | solution.py:33
  544.2 26.1 %collective-permute-start.41 = (bf16[128,2048]{1,0:T(8,128)(2,1)S(1)}, bf16[128,2048]{1,0:T(8,128)(2,1)S(1)}, u32[]{:S(2)}, u32[]{:S(2)}) collective-permute-start(bf16[128,2048]{1,0:T(8,128)(2,1)S(1)} %get-tuple-element.326), channel_id=1, source_target_pairs={{0,16},{4,20},{8,24},{12,28},{16,0},{20,4},{24,8},{28,12},{1,17},{... | collective-permute-start | bytes 1572872 | tf_op jit(solution)/shard_map/ppermute | solution.py:33
  544.5 26.7 %collective-permute-start.40 = (bf16[128,2048]{1,0:T(8,128)(2,1)S(1)}, bf16[128,2048]{1,0:T(8,128)(2,1)S(1)}, u32[]{:S(2)}, u32[]{:S(2)}) collective-permute-start(bf16[128,2048]{1,0:T(8,128)(2,1)S(1)} %get-tuple-element.327), channel_id=1, source_target_pairs={{0,8},{4,12},{8,0},{12,4},{16,24},{20,28},{24,16},{28,20},{1,9},{5... | collective-permute-start | bytes 1572872 | tf_op jit(solution)/shard_map/ppermute | solution.py:33
  547.8 43.7 %collective-permute-start.48 = (bf16[128,2048]{1,0:T(8,128)(2,1)S(1)}, bf16[128,2048]{1,0:T(8,128)(2,1)S(1)}, u32[]{:S(2)}, u32[]{:S(2)}) collective-permute-start(bf16[128,2048]{1,0:T(8,128)(2,1)S(1)} %get-tuple-element.322), channel_id=1, source_target_pairs={{0,8},{4,12},{8,0},{12,4},{16,24},{20,28},{24,16},{28,20},{1,9},{5... | collective-permute-start | bytes 1572872 | tf_op jit(solution)/shard_map/ppermute | solution.py:33
  570.3 21.2 %collective-permute-start.47 = (bf16[128,2048]{1,0:T(8,128)(2,1)S(1)}, bf16[128,2048]{1,0:T(8,128)(2,1)S(1)}, u32[]{:S(2)}, u32[]{:S(2)}) collective-permute-start(bf16[128,2048]{1,0:T(8,128)(2,1)S(1)} %get-tuple-element.323), channel_id=1, source_target_pairs={{0,16},{4,20},{8,24},{12,28},{16,0},{20,4},{24,8},{28,12},{1,17},{... | collective-permute-start | bytes 1572872 | tf_op jit(solution)/shard_map/ppermute | solution.py:33
  571.3 18.1 %collective-permute-start.50 = (bf16[352,512]{1,0:T(8,128)(2,1)S(1)}, bf16[352,512]{1,0:T(8,128)(2,1)S(1)}, u32[]{:S(2)}, u32[]{:S(2)}) collective-permute-start(bf16[352,512]{1,0:T(8,128)(2,1)S(1)} %slice.140), channel_id=1, source_target_pairs={{0,8},{4,12},{8,0},{12,4},{16,24},{20,28},{24,16},{28,20},{1,9},{5... | collective-permute-start | bytes 1081352 | tf_op jit(solution)/shard_map/ppermute | solution.py:33
  573.0 18.5 %collective-permute-start.49 = (bf16[352,512]{1,0:T(8,128)(2,1)S(1)}, bf16[352,512]{1,0:T(8,128)(2,1)S(1)}, u32[]{:S(2)}, u32[]{:S(2)}) collective-permute-start(bf16[352,512]{1,0:T(8,128)(2,1)S(1)} %slice.139), channel_id=1, source_target_pairs={{0,16},{4,20},{8,24},{12,28},{16,0},{20,4},{24,8},{28,12},{1,17},{... | collective-permute-start | bytes 1081352 | tf_op jit(solution)/shard_map/ppermute | solution.py:33
  591.6 22.2 %collective-permute-start.52 = (bf16[2816,512]{1,0:T(8,128)(2,1)S(1)}, bf16[2816,512]{1,0:T(8,128)(2,1)}, u32[]{:S(2)}, u32[]{:S(2)}) collective-permute-start(bf16[2816,512]{1,0:T(8,128)(2,1)S(1)} %constant_dynamic-update-slice_fusion.28.same_ref), channel_id=1, source_target_pairs={{0,4},{4,0},{8,12},{12,8},{16,20},{20,16},{24,28},{28,24},{1,5},{5... | collective-permute-start | bytes 8650760 | tf_op jit(solution)/shard_map/ppermute | solution.py:33
  595.3 131.2 %all-gather.11.cloned.1.call-start = ((), (), s32[]{:S(2)}) async-start(), calls=%async_computation.13 | async-start | bytes 6488064 | tf_op jit(solution)/shard_map/all_gather | solution.py:846
  595.3 18.4 %collective-permute-start.54 = (bf16[704,512]{1,0:T(8,128)(2,1)}, bf16[704,512]{1,0:T(8,128)(2,1)}, u32[]{:S(2)}, u32[]{:S(2)}) collective-permute-start(bf16[704,512]{1,0:T(8,128)(2,1)} %reduce-scatter.8.cloned.1.call-done), channel_id=1, source_target_pairs={{0,16},{4,20},{8,24},{12,28},{16,0},{20,4},{24,8},{28,12},{1,17},{... | collective-permute-start | bytes 2162696 | tf_op jit(solution)/shard_map/ppermute | solution.py:33
  595.7 18.1 %collective-permute-start.53 = (bf16[704,512]{1,0:T(8,128)(2,1)}, bf16[704,512]{1,0:T(8,128)(2,1)}, u32[]{:S(2)}, u32[]{:S(2)}) collective-permute-start(bf16[704,512]{1,0:T(8,128)(2,1)} %reduce-scatter.8.cloned.1.call-done), channel_id=1, source_target_pairs={{0,8},{4,12},{8,0},{12,4},{16,24},{20,28},{24,16},{28,20},{1,9},{5... | collective-permute-start | bytes 2162696 | tf_op jit(solution)/shard_map/ppermute | solution.py:33
  597.3 16.4 %collective-permute-start.55 = (f32[2,2048]{1,0:T(2,128)S(1)}, f32[2,2048]{1,0:T(2,128)S(1)}, u32[]{:S(2)}, u32[]{:S(2)}) collective-permute-start(f32[2,2048]{1,0:T(2,128)S(1)} %add.213), channel_id=1, source_target_pairs={{0,8},{4,12},{8,0},{12,4},{16,24},{20,28},{24,16},{28,20},{1,9},{5... | collective-permute-start | bytes 49160 | tf_op jit(solution)/shard_map/ppermute | solution.py:33
  620.6 28.5 %collective-permute-start.59 = (bf16[512,768]{1,0:T(8,128)(2,1)}, bf16[512,768]{1,0:T(8,128)(2,1)S(1)}, u32[]{:S(2)}, u32[]{:S(2)}) collective-permute-start(bf16[512,768]{1,0:T(8,128)(2,1)} %reduce-scatter.12.cloned.1.call-done), channel_id=1, source_target_pairs={{0,16},{4,20},{8,24},{12,28},{16,0},{20,4},{24,8},{28,12},{1,17},{... | collective-permute-start | bytes 2359304 | tf_op jit(solution)/shard_map/ppermute | solution.py:33
  622.1 28.4 %collective-permute-start.58 = (bf16[512,768]{1,0:T(8,128)(2,1)}, bf16[512,768]{1,0:T(8,128)(2,1)S(1)}, u32[]{:S(2)}, u32[]{:S(2)}) collective-permute-start(bf16[512,768]{1,0:T(8,128)(2,1)} %reduce-scatter.12.cloned.1.call-done), channel_id=1, source_target_pairs={{0,8},{4,12},{8,0},{12,4},{16,24},{20,28},{24,16},{28,20},{1,9},{5... | collective-permute-start | bytes 2359304 | tf_op jit(solution)/shard_map/ppermute | solution.py:33
  625.6 34.1 %collective-permute-start.57 = (bf16[352,512]{1,0:T(8,128)(2,1)S(1)}, bf16[352,512]{1,0:T(8,128)(2,1)S(1)}, u32[]{:S(2)}, u32[]{:S(2)}) collective-permute-start(bf16[352,512]{1,0:T(8,128)(2,1)S(1)} %slice.144), channel_id=1, source_target_pairs={{0,8},{4,12},{8,0},{12,4},{16,24},{20,28},{24,16},{28,20},{1,9},{5... | collective-permute-start | bytes 1081352 | tf_op jit(solution)/shard_map/ppermute | solution.py:33
  626.2 33.5 %collective-permute-start.56 = (bf16[352,512]{1,0:T(8,128)(2,1)S(1)}, bf16[352,512]{1,0:T(8,128)(2,1)S(1)}, u32[]{:S(2)}, u32[]{:S(2)}) collective-permute-start(bf16[352,512]{1,0:T(8,128)(2,1)S(1)} %slice.143), channel_id=1, source_target_pairs={{0,16},{4,20},{8,24},{12,28},{16,0},{20,4},{24,8},{28,12},{1,17},{... | collective-permute-start | bytes 1081352 | tf_op jit(solution)/shard_map/ppermute | solution.py:33
  628.0 29.7 %collective-permute-start.60 = (f32[2,2048]{1,0:T(2,128)S(1)}, f32[2,2048]{1,0:T(2,128)S(1)}, u32[]{:S(2)}, u32[]{:S(2)}) collective-permute-start(f32[2,2048]{1,0:T(2,128)S(1)} %add.222), channel_id=1, source_target_pairs={{0,16},{4,20},{8,24},{12,28},{16,0},{20,4},{24,8},{28,12},{1,17},{... | collective-permute-start | bytes 49160 | tf_op jit(solution)/shard_map/ppermute | solution.py:33
  659.8 32.0 %collective-permute-start.61 = (bf16[2816,512]{1,0:T(8,128)(2,1)S(1)}, bf16[2816,512]{1,0:T(8,128)(2,1)S(1)}, u32[]{:S(2)}, u32[]{:S(2)}) collective-permute-start(bf16[2816,512]{1,0:T(8,128)(2,1)S(1)} %constant_dynamic-update-slice_fusion.33.same_ref), channel_id=1, source_target_pairs={{0,4},{4,0},{8,12},{12,8},{16,20},{20,16},{24,28},{28,24},{1,5},{5... | collective-permute-start | bytes 8650760 | tf_op jit(solution)/shard_map/ppermute | solution.py:33
  661.2 30.5 %collective-permute-start.63 = (bf16[256,768]{1,0:T(8,128)(2,1)S(1)}, bf16[256,768]{1,0:T(8,128)(2,1)S(1)}, u32[]{:S(2)}, u32[]{:S(2)}) collective-permute-start(bf16[256,768]{1,0:T(8,128)(2,1)S(1)} %slice.146), channel_id=1, source_target_pairs={{0,8},{4,12},{8,0},{12,4},{16,24},{20,28},{24,16},{28,20},{1,9},{5... | collective-permute-start | bytes 1179656 | tf_op jit(solution)/shard_map/ppermute | solution.py:33
  662.6 29.2 %collective-permute-start.62 = (bf16[256,768]{1,0:T(8,128)(2,1)S(1)}, bf16[256,768]{1,0:T(8,128)(2,1)S(1)}, u32[]{:S(2)}, u32[]{:S(2)}) collective-permute-start(bf16[256,768]{1,0:T(8,128)(2,1)S(1)} %slice.145), channel_id=1, source_target_pairs={{0,16},{4,20},{8,24},{12,28},{16,0},{20,4},{24,8},{28,12},{1,17},{... | collective-permute-start | bytes 1179656 | tf_op jit(solution)/shard_map/ppermute | solution.py:33
  665.0 25.9 %collective-permute-start.65 = (bf16[256,512]{1,0:T(8,128)(2,1)S(1)}, bf16[256,512]{1,0:T(8,128)(2,1)S(1)}, u32[]{:S(2)}, u32[]{:S(2)}) collective-permute-start(bf16[256,512]{1,0:T(8,128)(2,1)S(1)} %copy-done.76), channel_id=1, source_target_pairs={{0,16},{4,20},{8,24},{12,28},{16,0},{20,4},{24,8},{28,12},{1,17},{... | collective-permute-start | bytes 786440 | tf_op jit(solution)/shard_map/ppermute | solution.py:242
  675.6 16.1 %collective-permute-start.64 = (bf16[256,512]{1,0:T(8,128)(2,1)S(1)}, bf16[256,512]{1,0:T(8,128)(2,1)S(1)}, u32[]{:S(2)}, u32[]{:S(2)}) collective-permute-start(bf16[256,512]{1,0:T(8,128)(2,1)S(1)} %copy-done.76), channel_id=1, source_target_pairs={{0,8},{4,12},{8,0},{12,4},{16,24},{20,28},{24,16},{28,20},{1,9},{5... | collective-permute-start | bytes 786440 | tf_op jit(solution)/shard_map/ppermute | solution.py:242
  (114 other events, 1371.1 us)
Sparse Core Ops, SparseCore 0:
  63.4 37.4 all-gather.4
  116.2 114.4 all-gather.6
  232.9 57.4 all-gather.8
  326.5 55.3 reduce-scatter.5
  401.8 55.0 reduce-scatter.7
  459.0 56.0 reduce-scatter.9
  527.4 58.2 reduce-scatter.11
  595.4 25.1 reduce-scatter.13
  622.6 62.4 all-gather.10

commit v11 on v9

--- a/solution.py
+++ b/solution.py
@@ -426,7 +426,7 @@
 
 
 def attend_back_kernel(
-    grad_ref, out_ref, qkv_ref, lse_ref, x_ref, cos_ref, sin_ref, col_ref, row_ref,
+    own_ref, other_ref, out_ref, qkv_ref, lse_ref, x_ref, cos_ref, sin_ref, col_ref, row_ref,
     lin_ref, top_ref, bottom_ref, kept_ref, context_ref, keys_ref, values_ref,
 ):
     length, wide = qkv_ref.shape
@@ -437,7 +437,14 @@
     @pl.loop(0, length // tile)
     def _(t):
         rows = pl.ds(pl.multiple_of(t * tile, tile), tile)
-        context_ref[rows, :] = mm_nt(grad_ref[rows, :], out_ref[...]).astype(BF)
+
+        @pl.when(seq == 0)
+        def _():
+            context_ref[rows, :] = mm_nt(own_ref[rows, :], out_ref[...]).astype(BF)
+
+        @pl.when(seq > 0)
+        def _():
+            context_ref[rows, :] = mm_nt(other_ref[rows, :], out_ref[...]).astype(BF)
 
     cos, sin = cos_ref[...], sin_ref[...]
     scale = HD**-0.5
@@ -487,7 +494,8 @@
     return pl.pallas_call(
         attend_back_kernel,
         grid=(rows // length,),
-        in_specs=[by_seq(depth), whole(width, depth), by_seq(wide), by_seq(width // HD)]
+        in_specs=[whole(length, depth)] * 2
+        + [whole(width, depth), by_seq(wide), by_seq(width // HD)]
         + [whole(rows, depth), whole(length, HD), whole(length, HD)]
         + [
             pl.BlockSpec((1, length, 1), lambda s: (s, 0, 0)),
@@ -512,7 +520,7 @@
             transcendentals=rows * 2 * WIN * width // HD,
         ),
         name="attend_back",
-    )(grad, out_w, qkv, lse, both, *tables, *seg)
+    )(*grad, out_w, qkv, lse, both, *tables, *seg)
 
 
 def normed_back_kernel(blocks, parts, z_ref, *refs):
@@ -588,35 +596,42 @@
     return grad_gain, root * scaled - source * (root * root * root) * mean
 
 
-def place_kernel(me_ref, same_ref, other_ref, *out_refs):
-    block = jnp.where(pl.program_id(0) % 2 == 0, same_ref[...], other_ref[...]).astype(F32)
-    width = out_refs[0].shape[1]
+def place_kernel(columns, me_ref, same_ref, other_ref, *out_refs):
+    even = me_ref[0] % 2 == 0
+    same, other = same_ref[...], other_ref[...]
+    blocks = (jnp.where(even, same, other).astype(F32), jnp.where(even, other, same).astype(F32))
+    width = same.shape[1] // len(out_refs)
     for i, ref in enumerate(out_refs):
-        ref[...] = block[:, i * width : (i + 1) * width]
+        for n, block in enumerate(blocks):
+            part = block[:, i * width : (i + 1) * width]
+            if columns:
+                ref[:, n * width : (n + 1) * width] = part
+            else:
+                ref[n * same.shape[0] : (n + 1) * same.shape[0], :] = part
 
 
 def place(me, same, other, height, width, columns):
     size, total = lax.axis_size("rep"), same.shape[1]
-    spec = pl.BlockSpec((height, total), lambda d, me: (d // 2, 0))
-    at = lambda d, me: jnp.bitwise_xor(d, me[0])
+    spec = pl.BlockSpec((height, total), lambda d, me: (d, 0))
     shape = (height, size * width) if columns else (size * height, width)
+    at = lambda d, me: jnp.bitwise_xor(d, me[0] // 2)
+    if columns:
+        out_spec = pl.BlockSpec((height, 2 * width), lambda d, me: (0, at(d, me)))
+    else:
+        out_spec = pl.BlockSpec((2 * height, width), lambda d, me: (at(d, me), 0))
     count = total // width
     return pl.pallas_call(
-        place_kernel,
+        functools.partial(place_kernel, columns),
         grid_spec=pltpu.PrefetchScalarGridSpec(
             num_scalar_prefetch=1,
-            grid=(size,),
+            grid=(size // 2,),
             in_specs=[spec, spec],
-            out_specs=[
-                pl.BlockSpec(
-                    (height, width),
-                    (lambda d, me: (0, at(d, me))) if columns else (lambda d, me: (at(d, me), 0)),
-                )
-            ] * count,
+            out_specs=[out_spec] * count,
         ),
         out_shape=[jax.ShapeDtypeStruct(shape, F32)] * count,
+        compiler_params=pltpu.CompilerParams(vmem_limit_bytes=32 << 20),
         cost_estimate=pl.CostEstimate(
-            flops=0, bytes_accessed=8 * size * height * total, transcendentals=0
+            flops=0, bytes_accessed=6 * size * height * total, transcendentals=0
         ),
         name="place",
     )(me, same, other)
@@ -764,20 +779,17 @@
     grad_inner = mm_nt(all_slot_grad, down)
     grad_gate_act = (grad_inner * up_act * sigmoid * (1.0 + gate_act * (1.0 - sigmoid))).astype(BF)
     grad_up_act = (grad_inner * silu).astype(BF)
-    grad_gate_act, grad_up_act = stage([expert_flow], (grad_gate_act, grad_up_act))
     grad_act = jnp.concatenate([grad_gate_act, grad_up_act], axis=1)
     grad_gate, back = lax.optimization_barrier(
         (mm_tn(grad_gate_act, dispatched).astype(BF), mm_nt(grad_act, gate_up).astype(BF))
     )
-    grad_disp, grad_up_act, inner = lax.optimization_barrier(
-        (reduce_rows(back, 1), grad_up_act, inner)
-    )
+    grad_disp, grad_up_act, inner = stage([expert_flow], (reduce_rows(back, 1), grad_up_act, inner))
     grad_normed_two = mm_tn(pick, grad_disp)
     grad_gain_two, through = norm_back(grad_normed_two, hidden, root_two, gain_two)
     grad_hidden = upstream + through
 
     grad_projected = (grad_hidden * attn_weight).astype(BF)
-    both_grad = jnp.concatenate([grad_projected, swap(grad_projected, 1)], axis=0)
+    both_grad = [grad_projected, swap(grad_projected, 1)]
     lins, grad_qkv_w = {}, {}
 
     def run_back(*ds):
@@ -809,7 +821,7 @@
     ]
     output = (hidden + mm_tn(pick, expert_out) * mix[:, None]).astype(BF)
     values, grad_out_w, output = stage(
-        [qkv_flow], (run_back(0), mm_tn(all_context, both_grad).astype(BF), output)
+        [qkv_flow], (run_back(0), mm_tn(all_context, jnp.concatenate(both_grad, axis=0)).astype(BF), output)
     )
     keep([0], values)
     grad_normed = normed_back(

time: 743 us -> 728 us (0.980)
  transfers between devices with their start and end apart: 77 -> 77, of which waited for: 18 -> 18; matrix products, arithmetic and copies ran while one was open for 20% -> 21% of each run, Pallas kernels for 34% -> 34%
where the time goes in v11:
time: 728 us; the launch traced here: 721 us
  Pallas kernels  245 us (34%)
  waiting for transfers between devices  167 us (23%)
  local copies, waits for them, and re-layouts  91 us (12%)
  matrix products  72.3 us (10%)
  starting transfers between devices  68.1 us (9%)
  other arithmetic  61.1 us (8%)
  between operations  15.8 us (2%)
    ppermute x53, waiting for transfers between devices, swap(): return lax.ppermute(value, 'rep', [(i, i ^ bit) for i in range(size)])  107 us
    pallas_call x4, Pallas kernels, attend_back(): pl.pallas_call(attend_back_kernel, grid=(rows // length,), in_specs=[whol...  71.9 us
    unnamed x243, local copies, waits for them, and re-layouts  59.2 us
    pallas_call x2, Pallas kernels, gather_rows(): pl.pallas_call(functools.partial(gather_kernel, peers()), out_shape=jax.S...  58.4 us
    ppermute x53, starting transfers between devices, swap(): return lax.ppermute(value, 'rep', [(i, i ^ bit) for i in range(size)])  48.3 us
    pallas_call x4, Pallas kernels, attend(): pl.pallas_call(functools.partial(attend_kernel, parts), grid_spec=pltpu.P...  42.5 us
    pallas_call x1, Pallas kernels, reduce_rows(): pl.pallas_call(functools.partial(reduce_kernel, peers()), out_shape=jax.S...  28.7 us
    dot_general x6, matrix products, mm_tn(): lax.dot_general(left, right, (((0,), (0,)), ((), ())), preferred_element_...  27.5 us
  transfers between devices with their start and end apart: 77, of which 18 were waited for; matrix products, arithmetic and copies ran while one was open for 21% of the time, Pallas kernels for 34%

profile of v11, /device:TPU:0, one launch (start us, length us, event | category | flops | bytes accessed | tf_op | source)
XLA Modules:
  0.0 720.8 jit_solution(15236944620660806689)
XLA Ops:
  8.8 3.1 collective-permute-start.2
  11.8 2.6 collective-permute-start.1
  17.7 2.7 constant_dynamic-slice_fusion.4
  21.2 2.3 constant_dynamic-slice_fusion.15
  26.2 16.2 %collective-permute-done.3.refs_5_ = bf16[512,768]{1,0:T(8,128)(2,1)} collective-permute-done((bf16[512,768]{1,0:T(8,128)(2,1)S(1)}, bf16[512,768]{1,0:T(8,128)(2,1)}, u32[]{:S(2)}, u32[]{:S(2)}) %collective-permute-start.3) | collective-permute-done | bytes 786464 | tf_op jit(solution)/shard_map/ppermute | solution.py:718
  42.5 2.1 fusion.2
  47.9 18.9 %collective-permute-done.7.refs_6_ = bf16[512,768]{1,0:T(8,128)(2,1)} collective-permute-done((bf16[512,768]{1,0:T(8,128)(2,1)}, bf16[512,768]{1,0:T(8,128)(2,1)}, u32[]{:S(2)}, u32[]{:S(2)}) %collective-permute-start.7) | collective-permute-done | bytes 786464 | tf_op jit(solution)/shard_map/ppermute | solution.py:732
  75.4 20.7 %collective-permute-done.10 = bf16[256,768]{1,0:T(8,128)(2,1)} collective-permute-done((bf16[256,768]{1,0:T(8,128)(2,1)}, bf16[256,768]{1,0:T(8,128)(2,1)}, u32[]{:S(2)}, u32[]{:S(2)}) %collective-permute-start.10) | collective-permute-done | bytes 393248 | tf_op jit(solution)/shard_map/ppermute | solution.py:33
  110.0 2.1 pad_maximum_fusion.refs_0_.refs_1_.refs_2_.refs_3_.x_ref
  114.4 11.3 %attend.4 = (bf16[1024,256]{1,0:T(8,128)(2,1)S(1)}, bf16[1024,768]{1,0:T(8,128)(2,1)S(1)}, f32[1024,2]{1,0:T(8,128)S(1)}) custom-call(s32[1]{0:T(128)} %bitcast.1.z_ref, bf16[1024,2048]{1,0:T(8,128)(2,1)S(1)} %pad_maximum_fusion.refs_0_.refs_1_.refs_2_.refs_3_.x_ref, bf16[1024,2048]{1,0:T(8,128)(2,1)S(1)} %pad_maximum_fusion.refs_0_.refs_1_.refs_2_.refs_3_.x_ref, ...), custom_call_target="tpu_custom_call" | custom-call | flops 3758096384 | bytes 10485760 | tf_op jit(solution)/shard_map/attend/pallas_call | solution.py:398
  139.3 2.2 copy-done.3
  143.8 10.7 %attend.5 = (bf16[1024,256]{1,0:T(8,128)(2,1)S(1)}, bf16[1024,768]{1,0:T(8,128)(2,1)S(1)}, f32[1024,2]{1,0:T(8,128)S(1)}) custom-call(s32[1]{0:T(128)} %bitcast.1.z_ref, bf16[1024,2048]{1,0:T(8,128)(2,1)S(1)} %copy-done.3, bf16[1024,2048]{1,0:T(8,128)(2,1)S(1)} %copy-done.3, bf16[1024,2048]{1,0:T(8,128)(2,1)S(1)} %copy-done.3, ...), custom_call_target="tpu_custom_call" | custom-call | flops 3758096384 | bytes 10485760 | tf_op jit(solution)/shard_map/attend/pallas_call | solution.py:398
  156.5 10.8 %attend.6 = (bf16[1024,256]{1,0:T(8,128)(2,1)S(1)}, bf16[1024,768]{1,0:T(8,128)(2,1)S(1)}, f32[1024,2]{1,0:T(8,128)S(1)}) custom-call(s32[1]{0:T(128)} %bitcast.1.z_ref, bf16[1024,2048]{1,0:T(8,128)(2,1)S(1)} %copy-done.3, bf16[1024,2048]{1,0:T(8,128)(2,1)S(1)} %copy-done.3, bf16[1024,2048]{1,0:T(8,128)(2,1)S(1)} %copy-done.3, ...), custom_call_target="tpu_custom_call" | custom-call | flops 3758096384 | bytes 10485760 | tf_op jit(solution)/shard_map/attend/pallas_call | solution.py:398
  169.1 9.6 %attend.7 = (bf16[1024,256]{1,0:T(8,128)(2,1)S(1)}, bf16[1024,768]{1,0:T(8,128)(2,1)S(1)}, f32[1024,2]{1,0:T(8,128)S(1)}) custom-call(s32[1]{0:T(128)} %bitcast.1.z_ref, bf16[1024,2048]{1,0:T(8,128)(2,1)S(1)} %copy-done.3, bf16[1024,2048]{1,0:T(8,128)(2,1)S(1)} %copy-done.3, bf16[1024,2048]{1,0:T(8,128)(2,1)S(1)} %copy-done.3, ...), custom_call_target="tpu_custom_call" | custom-call | flops 3758096384 | bytes 10485760 | tf_op jit(solution)/shard_map/attend/pallas_call | solution.py:398
  183.0 6.1 collective-permute-done.22
  191.3 6.3 fusion.53
  197.6 3.4 copy-done.67
  203.1 2.3 fusion.22.in_ref
  207.1 4.0 multiply_reduce_fusion.2
  213.9 29.1 %gather_rows.2 = bf16[1024,2048]{1,0:T(8,128)(2,1)S(1)} custom-call(bf16[128,2048]{1,0:T(8,128)(2,1)S(1)} %convolution_convert_fusion.5.in_ref), custom_call_target="tpu_custom_call" | custom-call | bytes 62914560 | tf_op jit(solution)/shard_map/gather_rows/pallas_call | solution.py:153
  245.1 11.7 %fusion.54 = f32[1024,1408]{1,0:T(8,128)} fusion(bf16[1024,2048]{1,0:T(8,128)(2,1)} %copy-done.8, bf16[2048,1408]{1,0:T(8,128)(2,1)} %all-gather.7.cloned.1.call-done), kind=kOutput, calls=%fused_computation.179 | convolution fusion | flops 5905580032 | bytes 15728640 | tf_op jit(solution)/shard_map/dot_general | solution.py:20
  256.8 29.3 %gather_rows.3 = bf16[1024,2048]{1,0:T(8,128)(2,1)S(1)} custom-call(bf16[128,2048]{1,0:T(8,128)(2,1)S(1)} %fusion.22.in_ref), custom_call_target="tpu_custom_call" | custom-call | bytes 62914560 | tf_op jit(solution)/shard_map/gather_rows/pallas_call | solution.py:153
  288.1 4.3 all-gather.9.cloned.1.call-done
  292.4 9.1 %multiply_convert_fusion.2 = (bf16[1024,704]{1,0:T(8,128)(2,1)S(1)}, bf16[1024,704]{1,0:T(8,128)(2,1)S(1)}, bf16[1024,704]{1,0:T(8,128)(2,1)S(1)}) fusion(f32[1024,1408]{1,0:T(8,128)} %fusion.54, bf16[1024,2048]{1,0:T(8,128)(2,1)} %copy-done.6, bf16[704,2048]{1,0:T(8,128)(2,1)} %all-gather.9.cloned.1.call-done), kind=kOutput, calls=%fused_computation.44 | convolution fusion | flops 2963603456 | bytes 17170432 | tf_op jit(solution)/shard_map/dot_general | solution.py:24
  301.5 3.6 convolution_convert_fusion.1
  307.8 11.1 %convolution_convert_fusion.in_ref = bf16[1024,2048]{1,0:T(8,128)(2,1)} fusion(bf16[2048,1408]{1,0:T(8,128)(2,1)} %all-gather.7.cloned.1.call-done, bf16[1024,704]{1,0:T(8,128)(2,1)S(1)} %get-tuple-element.198, bf16[1024,704]{1,0:T(8,128)(2,1)S(1)} %get-tuple-element.310), kind=kOutput, calls=%fused_computation.34 | convolution fusion | flops 5913444352 | bytes 12845056 | tf_op jit(solution)/shard_map/dot_general | solution.py:24
  318.9 4.5 convolution_convert_fusion.4
  323.9 2.2 copy-done.11
  326.1 28.7 %reduce_rows.1 = bf16[128,2048]{1,0:T(8,128)(2,1)S(1)} custom-call(bf16[1024,2048]{1,0:T(8,128)(2,1)S(1)} %copy-done.11), custom_call_target="tpu_custom_call" | custom-call | bytes 62914560 | tf_op jit(solution)/shard_map/reduce_rows/pallas_call | solution.py:218
  356.4 3.8 multiply_convert_fusion
  361.5 2.5 add_convert_fusion.1
  370.0 4.5 convolution_convert_fusion.3
  376.8 17.7 %attend_back.4 = (bf16[1024,768]{1,0:T(8,128)(2,1)S(1)}, bf16[1024,768]{1,0:T(8,128)(2,1)S(1)}, bf16[1024,768]{1,0:T(8,128)(2,1)}) custom-call(bf16[512,2048]{1,0:T(8,128)(2,1)} %get-tuple-element.218.own_ref, bf16[512,2048]{1,0:T(8,128)(2,1)} %collective-permute-done.29.other_ref, bf16[256,2048]{1,0:T(8,128)(2,1)S(1)} %copy-done.38, ...), custom_call_target="tpu_custom_call" | custom-call | flops 5637144576 | bytes 15728640 | tf_op jit(solution)/shard_map/attend_back/pallas_call | solution.py:494
  400.8 18.0 %attend_back.6 = (bf16[1024,768]{1,0:T(8,128)(2,1)S(1)}, bf16[1024,768]{1,0:T(8,128)(2,1)S(1)}, bf16[1024,768]{1,0:T(8,128)(2,1)}) custom-call(bf16[512,2048]{1,0:T(8,128)(2,1)} %get-tuple-element.218.own_ref, bf16[512,2048]{1,0:T(8,128)(2,1)} %collective-permute-done.29.other_ref, bf16[256,2048]{1,0:T(8,128)(2,1)S(1)} %copy-done.23, ...), custom_call_target="tpu_custom_call" | custom-call | flops 5637144576 | bytes 15728640 | tf_op jit(solution)/shard_map/attend_back/pallas_call | solution.py:494
  420.0 2.4 add_convert_fusion.10
  422.5 17.8 %attend_back.5 = (bf16[1024,768]{1,0:T(8,128)(2,1)S(1)}, bf16[1024,768]{1,0:T(8,128)(2,1)S(1)}, bf16[1024,768]{1,0:T(8,128)(2,1)}) custom-call(bf16[512,2048]{1,0:T(8,128)(2,1)} %get-tuple-element.218.own_ref, bf16[512,2048]{1,0:T(8,128)(2,1)} %collective-permute-done.29.other_ref, bf16[256,2048]{1,0:T(8,128)(2,1)S(1)} %copy-done.21, ...), custom_call_target="tpu_custom_call" | custom-call | flops 5637144576 | bytes 15728640 | tf_op jit(solution)/shard_map/attend_back/pallas_call | solution.py:494
  442.6 4.5 convolution_convert_fusion.2
  448.9 3.4 add_convert_fusion.4
  453.5 3.4 add_convert_fusion.5
  458.1 18.4 %attend_back.7 = (bf16[1024,768]{1,0:T(8,128)(2,1)S(1)}, bf16[1024,768]{1,0:T(8,128)(2,1)S(1)}, bf16[1024,768]{1,0:T(8,128)(2,1)}) custom-call(bf16[512,2048]{1,0:T(8,128)(2,1)} %get-tuple-element.218.own_ref, bf16[512,2048]{1,0:T(8,128)(2,1)} %collective-permute-done.29.other_ref, bf16[256,2048]{1,0:T(8,128)(2,1)S(1)} %copy-done.37, ...), custom_call_target="tpu_custom_call" | custom-call | flops 5637144576 | bytes 15728640 | tf_op jit(solution)/shard_map/attend_back/pallas_call | solution.py:494
  476.6 10.6 %fusion.15 = bf16[1024,2048]{1,0:T(8,128)(2,1)} fusion(bf16[1024,1024]{1,0:T(8,128)(2,1)} %constant_dynamic-update-slice_fusion.14, bf16[512,2048]{1,0:T(8,128)(2,1)} %collective-permute-done.29.other_ref, bf16[512,2048]{1,0:T(8,128)(2,1)} %get-tuple-element.218.own_ref), kind=kOutput, calls=%fused_computation.33 | convolution fusion | flops 4305453056 | bytes 10485760 | tf_op jit(solution)/shard_map/dot_general | solution.py:28
  487.3 2.2 add_convert_fusion
  489.4 23.3 %normed_back.1 = (f32[512,2048]{1,0:T(8,128)}, bf16[512,2048]{1,0:T(8,128)(2,1)}) custom-call(s32[1]{0:T(128)} %bitcast.1.z_ref, bf16[1024,768]{1,0:T(8,128)(2,1)} %copy-done.54, bf16[1024,768]{1,0:T(8,128)(2,1)} %copy-done.53, bf16[1024,768]{1,0:T(8,128)(2,1)} %copy-done.52, bf16[1024,768]{1,0:T(8,128)(2,1)} %copy-done.51, ...), custom_call_target="tpu_custom_call" | custom-call | flops 12884901888 | bytes 27262976 | tf_op jit(solution)/shard_map/normed_back/pallas_call | solution.py:551
  512.8 3.6 collective-permute-done.35
  517.0 2.6 add_convert_fusion.2
  519.6 2.5 add_convert_fusion.3
  526.2 2.1 fusion.49
  531.2 22.8 %collective-permute-done.39 = bf16[128,2048]{1,0:T(8,128)(2,1)S(1)} collective-permute-done((bf16[128,2048]{1,0:T(8,128)(2,1)S(1)}, bf16[128,2048]{1,0:T(8,128)(2,1)S(1)}, u32[]{:S(2)}, u32[]{:S(2)}) %collective-permute-start.39) | collective-permute-done | bytes 524320 | tf_op jit(solution)/shard_map/ppermute | solution.py:33
  558.3 3.1 fusion.9
  561.4 3.9 fusion.6
  565.5 3.4 collective-permute-done.37
  569.3 6.1 collective-permute-done.44
  582.5 24.2 %collective-permute-done.46 = bf16[128,2048]{1,0:T(8,128)(2,1)S(1)} collective-permute-done((bf16[128,2048]{1,0:T(8,128)(2,1)S(1)}, bf16[128,2048]{1,0:T(8,128)(2,1)S(1)}, u32[]{:S(2)}, u32[]{:S(2)}) %collective-permute-start.46) | collective-permute-done | bytes 524320 | tf_op jit(solution)/shard_map/ppermute | solution.py:33
  610.3 2.2 add_convert_fusion.7
  622.8 5.0 place_turned.2
  627.8 13.1 %collective-permute-done.55 = f32[2,2048]{1,0:T(2,128)S(1)} collective-permute-done((f32[2,2048]{1,0:T(2,128)S(1)}, f32[2,2048]{1,0:T(2,128)S(1)}, u32[]{:S(2)}, u32[]{:S(2)}) %collective-permute-start.55) | collective-permute-done | bytes 16416 | tf_op jit(solution)/shard_map/ppermute | solution.py:33
  644.6 2.2 collective-permute-start.61
  652.7 6.1 collective-permute-done.61
  658.8 2.8 collective-permute-start.59
  664.0 13.9 %collective-permute-done.60 = bf16[256,512]{1,0:T(8,128)(2,1)S(1)} collective-permute-done((bf16[256,512]{1,0:T(8,128)(2,1)S(1)}, bf16[256,512]{1,0:T(8,128)(2,1)S(1)}, u32[]{:S(2)}, u32[]{:S(2)}) %collective-permute-start.60) | collective-permute-done | bytes 262176 | tf_op jit(solution)/shard_map/ppermute | solution.py:242
  688.8 5.0 place_turned.3
  693.8 4.3 place.3
  698.0 6.3 place.2
  705.0 8.9 %convert_element_type.237 = f32[5632,512]{1,0:T(8,128)} convert(bf16[5632,512]{1,0:T(8,128)(2,1)} %all-gather.11.cloned.1.call-done) | non-fusion elementwise | flops 2883584 | bytes 17301504 | tf_op jit(solution)/shard_map/convert_element_type | solution.py:862
  (456 shorter events, 157.3 us)
Async XLA Ops:
  7.2 123.9 %all-gather.5.cloned.1.call-start = ((), (), s32[]{:S(2)}) async-start(), calls=%async_computation.5 | async-start | bytes 1310720 | tf_op jit(solution)/shard_map/all_gather | solution.py:736
  8.8 17.4 %collective-permute-start.2 = (bf16[2,512]{1,0:T(2,128)(2,1)S(1)}, bf16[2,512]{1,0:T(2,128)(2,1)S(1)}, u32[]{:S(2)}, u32[]{:S(2)}) collective-permute-start(bf16[2,512]{1,0:T(2,128)(2,1)S(1)} %get-tuple-element.306), channel_id=1, source_target_pairs={{0,1},{1,2},{2,3},{3,0},{4,5},{5,6},{6,7},{7,4},{8,9},{9,10},{10,1... | collective-permute-start | bytes 6152 | tf_op jit(solution)/shard_map/ppermute | solution.py:319
  11.8 14.4 %collective-permute-start.1 = (bf16[2,512]{1,0:T(2,128)(2,1)S(1)}, bf16[2,512]{1,0:T(2,128)(2,1)S(1)}, u32[]{:S(2)}, u32[]{:S(2)}) collective-permute-start(bf16[2,512]{1,0:T(2,128)(2,1)S(1)} %get-tuple-element.306), channel_id=1, source_target_pairs={{0,2},{1,3},{2,0},{3,1},{4,6},{5,7},{6,4},{7,5},{8,10},{9,11},{10,... | collective-permute-start | bytes 6152 | tf_op jit(solution)/shard_map/ppermute | solution.py:319
  20.5 21.9 %collective-permute-start.3 = (bf16[512,768]{1,0:T(8,128)(2,1)S(1)}, bf16[512,768]{1,0:T(8,128)(2,1)}, u32[]{:S(2)}, u32[]{:S(2)}) collective-permute-start(bf16[512,768]{1,0:T(8,128)(2,1)S(1)} %pad_maximum_fusion.5.refs_4_), channel_id=1, source_target_pairs={{0,1},{1,2},{2,3},{3,0},{4,5},{5,6},{6,7},{7,4},{8,9},{9,10},{10,1... | collective-permute-start | bytes 2359304 | tf_op jit(solution)/shard_map/ppermute | solution.py:718
  44.7 22.2 %collective-permute-start.8 = (bf16[512,2048]{1,0:T(8,128)(2,1)S(1)}, bf16[512,2048]{1,0:T(8,128)(2,1)S(1)}, u32[]{:S(2)}, u32[]{:S(2)}) collective-permute-start(bf16[512,2048]{1,0:T(8,128)(2,1)S(1)} %fusion.2), channel_id=1, source_target_pairs={{0,4},{4,0},{8,12},{12,8},{16,20},{20,16},{24,28},{28,24},{1,5},{5... | collective-permute-start | bytes 6291464 | tf_op jit(solution)/shard_map/ppermute | solution.py:33
  44.8 22.1 %collective-permute-start.7 = (bf16[512,768]{1,0:T(8,128)(2,1)}, bf16[512,768]{1,0:T(8,128)(2,1)}, u32[]{:S(2)}, u32[]{:S(2)}) collective-permute-start(bf16[512,768]{1,0:T(8,128)(2,1)} %collective-permute-done.3.refs_5_), channel_id=1, source_target_pairs={{0,1},{1,2},{2,3},{3,0},{4,5},{5,6},{6,7},{7,4},{8,9},{9,10},{10,1... | collective-permute-start | bytes 2359304 | tf_op jit(solution)/shard_map/ppermute | solution.py:732
  44.8 22.0 %collective-permute-start.6 = (bf16[512,768]{1,0:T(8,128)(2,1)}, bf16[512,768]{1,0:T(8,128)(2,1)S(1)}, u32[]{:S(2)}, u32[]{:S(2)}) collective-permute-start(bf16[512,768]{1,0:T(8,128)(2,1)} %collective-permute-done.3.refs_5_), channel_id=1, source_target_pairs={{0,16},{4,20},{8,24},{12,28},{16,0},{20,4},{24,8},{28,12},{1,17},{... | collective-permute-start | bytes 2359304 | tf_op jit(solution)/shard_map/ppermute | solution.py:33
  46.4 20.4 %collective-permute-start.5 = (bf16[512,768]{1,0:T(8,128)(2,1)}, bf16[512,768]{1,0:T(8,128)(2,1)S(1)}, u32[]{:S(2)}, u32[]{:S(2)}) collective-permute-start(bf16[512,768]{1,0:T(8,128)(2,1)} %collective-permute-done.3.refs_5_), channel_id=1, source_target_pairs={{0,8},{4,12},{8,0},{12,4},{16,24},{20,28},{24,16},{28,20},{1,9},{5... | collective-permute-start | bytes 2359304 | tf_op jit(solution)/shard_map/ppermute | solution.py:33
  66.9 29.2 %collective-permute-start.13 = (bf16[512,768]{1,0:T(8,128)(2,1)}, bf16[512,768]{1,0:T(8,128)(2,1)}, u32[]{:S(2)}, u32[]{:S(2)}) collective-permute-start(bf16[512,768]{1,0:T(8,128)(2,1)} %collective-permute-done.7.refs_6_), channel_id=1, source_target_pairs={{0,1},{1,2},{2,3},{3,0},{4,5},{5,6},{6,7},{7,4},{8,9},{9,10},{10,1... | collective-permute-start | bytes 2359304 | tf_op jit(solution)/shard_map/ppermute | solution.py:732
  66.9 29.2 %collective-permute-start.12 = (bf16[512,768]{1,0:T(8,128)(2,1)}, bf16[512,768]{1,0:T(8,128)(2,1)}, u32[]{:S(2)}, u32[]{:S(2)}) collective-permute-start(bf16[512,768]{1,0:T(8,128)(2,1)} %collective-permute-done.7.refs_6_), channel_id=1, source_target_pairs={{0,16},{4,20},{8,24},{12,28},{16,0},{20,4},{24,8},{28,12},{1,17},{... | collective-permute-start | bytes 2359304 | tf_op jit(solution)/shard_map/ppermute | solution.py:33
  68.5 27.6 %collective-permute-start.11 = (bf16[512,768]{1,0:T(8,128)(2,1)}, bf16[512,768]{1,0:T(8,128)(2,1)}, u32[]{:S(2)}, u32[]{:S(2)}) collective-permute-start(bf16[512,768]{1,0:T(8,128)(2,1)} %collective-permute-done.7.refs_6_), channel_id=1, source_target_pairs={{0,8},{4,12},{8,0},{12,4},{16,24},{20,28},{24,16},{28,20},{1,9},{5... | collective-permute-start | bytes 2359304 | tf_op jit(solution)/shard_map/ppermute | solution.py:33
  71.6 24.5 %collective-permute-start.10 = (bf16[256,768]{1,0:T(8,128)(2,1)}, bf16[256,768]{1,0:T(8,128)(2,1)}, u32[]{:S(2)}, u32[]{:S(2)}) collective-permute-start(bf16[256,768]{1,0:T(8,128)(2,1)} %slice.116), channel_id=1, source_target_pairs={{0,8},{4,12},{8,0},{12,4},{16,24},{20,28},{24,16},{28,20},{1,9},{5... | collective-permute-start | bytes 1179656 | tf_op jit(solution)/shard_map/ppermute | solution.py:33
  72.1 24.0 %collective-permute-start.9 = (bf16[256,768]{1,0:T(8,128)(2,1)}, bf16[256,768]{1,0:T(8,128)(2,1)}, u32[]{:S(2)}, u32[]{:S(2)}) collective-permute-start(bf16[256,768]{1,0:T(8,128)(2,1)} %slice.115), channel_id=1, source_target_pairs={{0,16},{4,20},{8,24},{12,28},{16,0},{20,4},{24,8},{28,12},{1,17},{... | collective-permute-start | bytes 1179656 | tf_op jit(solution)/shard_map/ppermute | solution.py:33
  96.2 148.9 %all-gather.7.cloned.1.call-start = ((), (), s32[]{:S(2)}) async-start(), calls=%async_computation.6 | async-start | bytes 7208960 | tf_op jit(solution)/shard_map/all_gather | solution.py:744
  96.9 195.5 %all-gather.9.cloned.1.call-start = ((), (), s32[]{:S(2)}) async-start(), calls=%async_computation.7 | async-start | bytes 3604480 | tf_op jit(solution)/shard_map/all_gather | solution.py:745
  102.7 28.4 %collective-permute-start.17 = (bf16[512,768]{1,0:T(8,128)(2,1)}, bf16[512,768]{1,0:T(8,128)(2,1)}, u32[]{:S(2)}, u32[]{:S(2)}) collective-permute-start(bf16[512,768]{1,0:T(8,128)(2,1)} %collective-permute-done.13.refs_7_), channel_id=1, source_target_pairs={{0,16},{4,20},{8,24},{12,28},{16,0},{20,4},{24,8},{28,12},{1,17},{... | collective-permute-start | bytes 2359304 | tf_op jit(solution)/shard_map/ppermute | solution.py:33
  103.3 27.8 %collective-permute-start.16 = (bf16[512,768]{1,0:T(8,128)(2,1)}, bf16[512,768]{1,0:T(8,128)(2,1)}, u32[]{:S(2)}, u32[]{:S(2)}) collective-permute-start(bf16[512,768]{1,0:T(8,128)(2,1)} %collective-permute-done.13.refs_7_), channel_id=1, source_target_pairs={{0,8},{4,12},{8,0},{12,4},{16,24},{20,28},{24,16},{28,20},{1,9},{5... | collective-permute-start | bytes 2359304 | tf_op jit(solution)/shard_map/ppermute | solution.py:33
  106.8 22.8 %collective-permute-start.15 = (bf16[256,768]{1,0:T(8,128)(2,1)S(1)}, bf16[256,768]{1,0:T(8,128)(2,1)S(1)}, u32[]{:S(2)}, u32[]{:S(2)}) collective-permute-start(bf16[256,768]{1,0:T(8,128)(2,1)S(1)} %slice.118), channel_id=1, source_target_pairs={{0,8},{4,12},{8,0},{12,4},{16,24},{20,28},{24,16},{28,20},{1,9},{5... | collective-permute-start | bytes 1179656 | tf_op jit(solution)/shard_map/ppermute | solution.py:33
  107.4 22.9 %collective-permute-start.14 = (bf16[256,768]{1,0:T(8,128)(2,1)S(1)}, bf16[256,768]{1,0:T(8,128)(2,1)S(1)}, u32[]{:S(2)}, u32[]{:S(2)}) collective-permute-start(bf16[256,768]{1,0:T(8,128)(2,1)S(1)} %slice.117), channel_id=1, source_target_pairs={{0,16},{4,20},{8,24},{12,28},{16,0},{20,4},{24,8},{28,12},{1,17},{... | collective-permute-start | bytes 1179656 | tf_op jit(solution)/shard_map/ppermute | solution.py:33
  131.1 47.6 %collective-permute-start.21 = (bf16[256,2048]{1,0:T(8,128)(2,1)}, bf16[256,2048]{1,0:T(8,128)(2,1)S(1)}, u32[]{:S(2)}, u32[]{:S(2)}) collective-permute-start(bf16[256,2048]{1,0:T(8,128)(2,1)} %all-gather.5.cloned.1.call-done.out_ref), channel_id=1, source_target_pairs={{0,16},{4,20},{8,24},{12,28},{16,0},{20,4},{24,8},{28,12},{1,17},{... | collective-permute-start | bytes 3145736 | tf_op jit(solution)/shard_map/ppermute | solution.py:33
  132.6 46.1 %collective-permute-start.20 = (bf16[256,2048]{1,0:T(8,128)(2,1)}, bf16[256,2048]{1,0:T(8,128)(2,1)S(1)}, u32[]{:S(2)}, u32[]{:S(2)}) collective-permute-start(bf16[256,2048]{1,0:T(8,128)(2,1)} %all-gather.5.cloned.1.call-done.out_ref), channel_id=1, source_target_pairs={{0,8},{4,12},{8,0},{12,4},{16,24},{20,28},{24,16},{28,20},{1,9},{5... | collective-permute-start | bytes 3145736 | tf_op jit(solution)/shard_map/ppermute | solution.py:33
  136.2 32.1 %collective-permute-start.19 = (bf16[256,768]{1,0:T(8,128)(2,1)S(1)}, bf16[256,768]{1,0:T(8,128)(2,1)S(1)}, u32[]{:S(2)}, u32[]{:S(2)}) collective-permute-start(bf16[256,768]{1,0:T(8,128)(2,1)S(1)} %slice.120), channel_id=1, source_target_pairs={{0,8},{4,12},{8,0},{12,4},{16,24},{20,28},{24,16},{28,20},{1,9},{5... | collective-permute-start | bytes 1179656 | tf_op jit(solution)/shard_map/ppermute | solution.py:33
  136.9 31.5 %collective-permute-start.18 = (bf16[256,768]{1,0:T(8,128)(2,1)S(1)}, bf16[256,768]{1,0:T(8,128)(2,1)S(1)}, u32[]{:S(2)}, u32[]{:S(2)}) collective-permute-start(bf16[256,768]{1,0:T(8,128)(2,1)S(1)} %slice.119), channel_id=1, source_target_pairs={{0,16},{4,20},{8,24},{12,28},{16,0},{20,4},{24,8},{28,12},{1,17},{... | collective-permute-start | bytes 1179656 | tf_op jit(solution)/shard_map/ppermute | solution.py:33
  202.7 310.1 %reduce-scatter.6.cloned.1.call-start = ((), (), s32[]{:S(2)}) async-start(), calls=%async_computation.8 | async-start | bytes 3604480 | tf_op jit(solution)/shard_map/reduce_scatter | solution.py:819
  307.0 47.8 %collective-permute-start.25 = (bf16[512,2048]{1,0:T(8,128)(2,1)}, bf16[512,2048]{1,0:T(8,128)(2,1)}, u32[]{:S(2)}, u32[]{:S(2)}) collective-permute-start(bf16[512,2048]{1,0:T(8,128)(2,1)} %slice.152), channel_id=1, source_target_pairs={{0,4},{4,0},{8,12},{12,8},{16,20},{20,16},{24,28},{28,24},{1,5},{5... | collective-permute-start | bytes 6291464 | tf_op jit(solution)/shard_map/ppermute | solution.py:33
  323.5 193.6 %reduce-scatter.8.cloned.1.call-start = ((), (), s32[]{:S(2)}) async-start(), calls=%async_computation.9 | async-start | bytes 3604480 | tf_op jit(solution)/shard_map/reduce_scatter | solution.py:819
  360.2 14.4 %collective-permute-start.29 = (bf16[512,2048]{1,0:T(8,128)(2,1)}, bf16[512,2048]{1,0:T(8,128)(2,1)}, u32[]{:S(2)}, u32[]{:S(2)}) collective-permute-start(bf16[512,2048]{1,0:T(8,128)(2,1)} %get-tuple-element.218.own_ref), channel_id=1, source_target_pairs={{0,4},{4,0},{8,12},{12,8},{16,20},{20,16},{24,28},{28,24},{1,5},{5... | collective-permute-start | bytes 6291464 | tf_op jit(solution)/shard_map/ppermute | solution.py:33
  366.5 30.4 %collective-permute-start.28 = (bf16[128,2048]{1,0:T(8,128)(2,1)}, bf16[128,2048]{1,0:T(8,128)(2,1)}, u32[]{:S(2)}, u32[]{:S(2)}) collective-permute-start(bf16[128,2048]{1,0:T(8,128)(2,1)} %get-tuple-element.320), channel_id=1, source_target_pairs={{0,24},{4,28},{8,16},{12,20},{16,8},{20,12},{24,0},{28,4},{1,25},{... | collective-permute-start | bytes 1572872 | tf_op jit(solution)/shard_map/ppermute | solution.py:242
  368.5 28.4 %collective-permute-start.27 = (bf16[128,2048]{1,0:T(8,128)(2,1)}, bf16[128,2048]{1,0:T(8,128)(2,1)}, u32[]{:S(2)}, u32[]{:S(2)}) collective-permute-start(bf16[128,2048]{1,0:T(8,128)(2,1)} %get-tuple-element.321), channel_id=1, source_target_pairs={{0,16},{4,20},{8,24},{12,28},{16,0},{20,4},{24,8},{28,12},{1,17},{... | collective-permute-start | bytes 1572872 | tf_op jit(solution)/shard_map/ppermute | solution.py:242
  369.2 27.7 %collective-permute-start.26 = (bf16[128,2048]{1,0:T(8,128)(2,1)}, bf16[128,2048]{1,0:T(8,128)(2,1)}, u32[]{:S(2)}, u32[]{:S(2)}) collective-permute-start(bf16[128,2048]{1,0:T(8,128)(2,1)} %get-tuple-element.322), channel_id=1, source_target_pairs={{0,8},{4,12},{8,0},{12,4},{16,24},{20,28},{24,16},{28,20},{1,9},{5... | collective-permute-start | bytes 1572872 | tf_op jit(solution)/shard_map/ppermute | solution.py:242
  396.9 127.1 %reduce-scatter.10.cloned.1.call-start = ((), (), s32[]{:S(2)}) async-start(), calls=%async_computation.10 | async-start | bytes 3604480 | tf_op jit(solution)/shard_map/reduce_scatter | solution.py:819
  397.2 49.9 %collective-permute-start.32 = (bf16[1024,768]{1,0:T(8,128)(2,1)}, bf16[1024,768]{1,0:T(8,128)(2,1)}, u32[]{:S(2)}, u32[]{:S(2)}) collective-permute-start(bf16[1024,768]{1,0:T(8,128)(2,1)} %copy-done.44), channel_id=1, source_target_pairs={{0,8},{4,12},{8,0},{12,4},{16,24},{20,28},{24,16},{28,20},{1,9},{5... | collective-permute-start | bytes 4718600 | tf_op jit(solution)/shard_map/ppermute | solution.py:33
  398.4 48.7 %collective-permute-start.33 = (bf16[1024,768]{1,0:T(8,128)(2,1)}, bf16[1024,768]{1,0:T(8,128)(2,1)}, u32[]{:S(2)}, u32[]{:S(2)}) collective-permute-start(bf16[1024,768]{1,0:T(8,128)(2,1)} %get-tuple-element.209), channel_id=1, source_target_pairs={{0,16},{4,20},{8,24},{12,28},{16,0},{20,4},{24,8},{28,12},{1,17},{... | collective-permute-start | bytes 4718600 | tf_op jit(solution)/shard_map/ppermute | solution.py:33
  447.1 163.2 %reduce-scatter.12.cloned.1.call-start = ((), (), s32[]{:S(2)}) async-start(), calls=%async_computation.11 | async-start | bytes 3932160 | tf_op jit(solution)/shard_map/reduce_scatter | solution.py:834
  447.2 42.2 %collective-permute-start.30 = (bf16[1024,768]{1,0:T(8,128)(2,1)}, bf16[1024,768]{1,0:T(8,128)(2,1)}, u32[]{:S(2)}, u32[]{:S(2)}) collective-permute-start(bf16[1024,768]{1,0:T(8,128)(2,1)} %copy-done.43), channel_id=1, source_target_pairs={{0,8},{4,12},{8,0},{12,4},{16,24},{20,28},{24,16},{28,20},{1,9},{5... | collective-permute-start | bytes 4718600 | tf_op jit(solution)/shard_map/ppermute | solution.py:33
  448.1 41.4 %collective-permute-start.31 = (bf16[1024,768]{1,0:T(8,128)(2,1)}, bf16[1024,768]{1,0:T(8,128)(2,1)}, u32[]{:S(2)}, u32[]{:S(2)}) collective-permute-start(bf16[1024,768]{1,0:T(8,128)(2,1)} %get-tuple-element.207), channel_id=1, source_target_pairs={{0,16},{4,20},{8,24},{12,28},{16,0},{20,4},{24,8},{28,12},{1,17},{... | collective-permute-start | bytes 4718600 | tf_op jit(solution)/shard_map/ppermute | solution.py:33
  452.3 64.0 %collective-permute-start.35 = (bf16[1024,768]{1,0:T(8,128)(2,1)}, bf16[1024,768]{1,0:T(8,128)(2,1)}, u32[]{:S(2)}, u32[]{:S(2)}) collective-permute-start(bf16[1024,768]{1,0:T(8,128)(2,1)} %add_convert_fusion.4), channel_id=1, source_target_pairs={{0,8},{4,12},{8,0},{12,4},{16,24},{20,28},{24,16},{28,20},{1,9},{5... | collective-permute-start | bytes 4718600 | tf_op jit(solution)/shard_map/ppermute | solution.py:33
  456.9 60.1 %collective-permute-start.34 = (bf16[1024,768]{1,0:T(8,128)(2,1)}, bf16[1024,768]{1,0:T(8,128)(2,1)}, u32[]{:S(2)}, u32[]{:S(2)}) collective-permute-start(bf16[1024,768]{1,0:T(8,128)(2,1)} %add_convert_fusion.5), channel_id=1, source_target_pairs={{0,16},{4,20},{8,24},{12,28},{16,0},{20,4},{24,8},{28,12},{1,17},{... | collective-permute-start | bytes 4718600 | tf_op jit(solution)/shard_map/ppermute | solution.py:33
  517.0 39.1 %collective-permute-start.42 = (bf16[512,2048]{1,0:T(8,128)(2,1)}, bf16[512,2048]{1,0:T(8,128)(2,1)}, u32[]{:S(2)}, u32[]{:S(2)}) collective-permute-start(bf16[512,2048]{1,0:T(8,128)(2,1)} %get-tuple-element.240), channel_id=1, source_target_pairs={{0,4},{4,0},{8,12},{12,8},{16,20},{20,16},{24,28},{28,24},{1,5},{5... | collective-permute-start | bytes 6291464 | tf_op jit(solution)/shard_map/ppermute | solution.py:33
  524.0 116.9 %reduce-scatter.14.cloned.1.call-start = ((), (), s32[]{:S(2)}) async-start(), calls=%async_computation.12 | async-start | bytes 1310720 | tf_op jit(solution)/shard_map/reduce_scatter | solution.py:850
  524.1 32.0 %collective-permute-start.41 = (bf16[704,512]{1,0:T(8,128)(2,1)}, bf16[704,512]{1,0:T(8,128)(2,1)S(1)}, u32[]{:S(2)}, u32[]{:S(2)}) collective-permute-start(bf16[704,512]{1,0:T(8,128)(2,1)} %reduce-scatter.6.cloned.1.call-done), channel_id=1, source_target_pairs={{0,16},{4,20},{8,24},{12,28},{16,0},{20,4},{24,8},{28,12},{1,17},{... | collective-permute-start | bytes 2162696 | tf_op jit(solution)/shard_map/ppermute | solution.py:33
  524.6 31.5 %collective-permute-start.40 = (bf16[704,512]{1,0:T(8,128)(2,1)}, bf16[704,512]{1,0:T(8,128)(2,1)S(1)}, u32[]{:S(2)}, u32[]{:S(2)}) collective-permute-start(bf16[704,512]{1,0:T(8,128)(2,1)} %reduce-scatter.6.cloned.1.call-done), channel_id=1, source_target_pairs={{0,8},{4,12},{8,0},{12,4},{16,24},{20,28},{24,16},{28,20},{1,9},{5... | collective-permute-start | bytes 2162696 | tf_op jit(solution)/shard_map/ppermute | solution.py:33
  528.4 25.7 %collective-permute-start.39 = (bf16[128,2048]{1,0:T(8,128)(2,1)S(1)}, bf16[128,2048]{1,0:T(8,128)(2,1)S(1)}, u32[]{:S(2)}, u32[]{:S(2)}) collective-permute-start(bf16[128,2048]{1,0:T(8,128)(2,1)S(1)} %get-tuple-element.316), channel_id=1, source_target_pairs={{0,16},{4,20},{8,24},{12,28},{16,0},{20,4},{24,8},{28,12},{1,17},{... | collective-permute-start | bytes 1572872 | tf_op jit(solution)/shard_map/ppermute | solution.py:33
  529.1 25.3 %collective-permute-start.38 = (bf16[128,2048]{1,0:T(8,128)(2,1)S(1)}, bf16[128,2048]{1,0:T(8,128)(2,1)S(1)}, u32[]{:S(2)}, u32[]{:S(2)}) collective-permute-start(bf16[128,2048]{1,0:T(8,128)(2,1)S(1)} %get-tuple-element.317), channel_id=1, source_target_pairs={{0,8},{4,12},{8,0},{12,4},{16,24},{20,28},{24,16},{28,20},{1,9},{5... | collective-permute-start | bytes 1572872 | tf_op jit(solution)/shard_map/ppermute | solution.py:33
  554.0 14.8 %collective-permute-start.37 = (bf16[128,2048]{1,0:T(8,128)(2,1)S(1)}, bf16[128,2048]{1,0:T(8,128)(2,1)S(1)}, u32[]{:S(2)}, u32[]{:S(2)}) collective-permute-start(bf16[128,2048]{1,0:T(8,128)(2,1)S(1)} %get-tuple-element.318), channel_id=1, source_target_pairs={{0,16},{4,20},{8,24},{12,28},{16,0},{20,4},{24,8},{28,12},{1,17},{... | collective-permute-start | bytes 1572872 | tf_op jit(solution)/shard_map/ppermute | solution.py:33
  554.4 14.9 %collective-permute-start.36 = (bf16[128,2048]{1,0:T(8,128)(2,1)S(1)}, bf16[128,2048]{1,0:T(8,128)(2,1)S(1)}, u32[]{:S(2)}, u32[]{:S(2)}) collective-permute-start(bf16[128,2048]{1,0:T(8,128)(2,1)S(1)} %get-tuple-element.319), channel_id=1, source_target_pairs={{0,8},{4,12},{8,0},{12,4},{16,24},{20,28},{24,16},{28,20},{1,9},{5... | collective-permute-start | bytes 1572872 | tf_op jit(solution)/shard_map/ppermute | solution.py:33
  556.2 19.2 %collective-permute-start.44 = (bf16[352,512]{1,0:T(8,128)(2,1)S(1)}, bf16[352,512]{1,0:T(8,128)(2,1)S(1)}, u32[]{:S(2)}, u32[]{:S(2)}) collective-permute-start(bf16[352,512]{1,0:T(8,128)(2,1)S(1)} %slice.138), channel_id=1, source_target_pairs={{0,8},{4,12},{8,0},{12,4},{16,24},{20,28},{24,16},{28,20},{1,9},{5... | collective-permute-start | bytes 1081352 | tf_op jit(solution)/shard_map/ppermute | solution.py:33
  556.6 18.7 %collective-permute-start.43 = (bf16[352,512]{1,0:T(8,128)(2,1)S(1)}, bf16[352,512]{1,0:T(8,128)(2,1)S(1)}, u32[]{:S(2)}, u32[]{:S(2)}) collective-permute-start(bf16[352,512]{1,0:T(8,128)(2,1)S(1)} %slice.137), channel_id=1, source_target_pairs={{0,16},{4,20},{8,24},{12,28},{16,0},{20,4},{24,8},{28,12},{1,17},{... | collective-permute-start | bytes 1081352 | tf_op jit(solution)/shard_map/ppermute | solution.py:33
  575.4 33.3 %collective-permute-start.47 = (bf16[2816,512]{1,0:T(8,128)(2,1)S(1)}, bf16[2816,512]{1,0:T(8,128)(2,1)S(1)}, u32[]{:S(2)}, u32[]{:S(2)}) collective-permute-start(bf16[2816,512]{1,0:T(8,128)(2,1)S(1)} %constant_dynamic-update-slice_fusion.23.same_ref), channel_id=1, source_target_pairs={{0,4},{4,0},{8,12},{12,8},{16,20},{20,16},{24,28},{28,24},{1,5},{5... | collective-permute-start | bytes 8650760 | tf_op jit(solution)/shard_map/ppermute | solution.py:33
  575.5 31.2 %collective-permute-start.49 = (bf16[704,512]{1,0:T(8,128)(2,1)S(1)}, bf16[704,512]{1,0:T(8,128)(2,1)S(1)}, u32[]{:S(2)}, u32[]{:S(2)}) collective-permute-start(bf16[704,512]{1,0:T(8,128)(2,1)S(1)} %copy-done.83), channel_id=1, source_target_pairs={{0,16},{4,20},{8,24},{12,28},{16,0},{20,4},{24,8},{28,12},{1,17},{... | collective-permute-start | bytes 2162696 | tf_op jit(solution)/shard_map/ppermute | solution.py:33
  577.2 30.3 %collective-permute-start.48 = (bf16[704,512]{1,0:T(8,128)(2,1)S(1)}, bf16[704,512]{1,0:T(8,128)(2,1)S(1)}, u32[]{:S(2)}, u32[]{:S(2)}) collective-permute-start(bf16[704,512]{1,0:T(8,128)(2,1)S(1)} %copy-done.83), channel_id=1, source_target_pairs={{0,8},{4,12},{8,0},{12,4},{16,24},{20,28},{24,16},{28,20},{1,9},{5... | collective-permute-start | bytes 2162696 | tf_op jit(solution)/shard_map/ppermute | solution.py:33
  579.9 26.8 %collective-permute-start.46 = (bf16[128,2048]{1,0:T(8,128)(2,1)S(1)}, bf16[128,2048]{1,0:T(8,128)(2,1)S(1)}, u32[]{:S(2)}, u32[]{:S(2)}) collective-permute-start(bf16[128,2048]{1,0:T(8,128)(2,1)S(1)} %get-tuple-element.314), channel_id=1, source_target_pairs={{0,8},{4,12},{8,0},{12,4},{16,24},{20,28},{24,16},{28,20},{1,9},{5... | collective-permute-start | bytes 1572872 | tf_op jit(solution)/shard_map/ppermute | solution.py:33
  580.9 25.8 %collective-permute-start.45 = (bf16[128,2048]{1,0:T(8,128)(2,1)S(1)}, bf16[128,2048]{1,0:T(8,128)(2,1)S(1)}, u32[]{:S(2)}, u32[]{:S(2)}) collective-permute-start(bf16[128,2048]{1,0:T(8,128)(2,1)S(1)} %get-tuple-element.315), channel_id=1, source_target_pairs={{0,16},{4,20},{8,24},{12,28},{16,0},{20,4},{24,8},{28,12},{1,17},{... | collective-permute-start | bytes 1572872 | tf_op jit(solution)/shard_map/ppermute | solution.py:33
  613.6 91.4 %all-gather.11.cloned.1.call-start = ((), (), s32[]{:S(2)}) async-start(), calls=%async_computation.13 | async-start | bytes 6488064 | tf_op jit(solution)/shard_map/all_gather | solution.py:855
  613.6 27.3 %collective-permute-start.54 = (bf16[512,768]{1,0:T(8,128)(2,1)}, bf16[512,768]{1,0:T(8,128)(2,1)}, u32[]{:S(2)}, u32[]{:S(2)}) collective-permute-start(bf16[512,768]{1,0:T(8,128)(2,1)} %reduce-scatter.12.cloned.1.call-done), channel_id=1, source_target_pairs={{0,16},{4,20},{8,24},{12,28},{16,0},{20,4},{24,8},{28,12},{1,17},{... | collective-permute-start | bytes 2359304 | tf_op jit(solution)/shard_map/ppermute | solution.py:33
  614.1 26.8 %collective-permute-start.53 = (bf16[512,768]{1,0:T(8,128)(2,1)}, bf16[512,768]{1,0:T(8,128)(2,1)}, u32[]{:S(2)}, u32[]{:S(2)}) collective-permute-start(bf16[512,768]{1,0:T(8,128)(2,1)} %reduce-scatter.12.cloned.1.call-done), channel_id=1, source_target_pairs={{0,8},{4,12},{8,0},{12,4},{16,24},{20,28},{24,16},{28,20},{1,9},{5... | collective-permute-start | bytes 2359304 | tf_op jit(solution)/shard_map/ppermute | solution.py:33
  617.8 23.1 %collective-permute-start.52 = (bf16[352,512]{1,0:T(8,128)(2,1)S(1)}, bf16[352,512]{1,0:T(8,128)(2,1)S(1)}, u32[]{:S(2)}, u32[]{:S(2)}) collective-permute-start(bf16[352,512]{1,0:T(8,128)(2,1)S(1)} %slice.142), channel_id=1, source_target_pairs={{0,8},{4,12},{8,0},{12,4},{16,24},{20,28},{24,16},{28,20},{1,9},{5... | collective-permute-start | bytes 1081352 | tf_op jit(solution)/shard_map/ppermute | solution.py:33
  618.2 22.7 %collective-permute-start.51 = (bf16[352,512]{1,0:T(8,128)(2,1)S(1)}, bf16[352,512]{1,0:T(8,128)(2,1)}, u32[]{:S(2)}, u32[]{:S(2)}) collective-permute-start(bf16[352,512]{1,0:T(8,128)(2,1)S(1)} %slice.141), channel_id=1, source_target_pairs={{0,16},{4,20},{8,24},{12,28},{16,0},{20,4},{24,8},{28,12},{1,17},{... | collective-permute-start | bytes 1081352 | tf_op jit(solution)/shard_map/ppermute | solution.py:33
  619.8 21.1 %collective-permute-start.55 = (f32[2,2048]{1,0:T(2,128)S(1)}, f32[2,2048]{1,0:T(2,128)S(1)}, u32[]{:S(2)}, u32[]{:S(2)}) collective-permute-start(f32[2,2048]{1,0:T(2,128)S(1)} %add.217), channel_id=1, source_target_pairs={{0,8},{4,12},{8,0},{12,4},{16,24},{20,28},{24,16},{28,20},{1,9},{5... | collective-permute-start | bytes 49160 | tf_op jit(solution)/shard_map/ppermute | solution.py:33
  644.6 33.3 %collective-permute-start.56 = (bf16[2816,512]{1,0:T(8,128)(2,1)S(1)}, bf16[2816,512]{1,0:T(8,128)(2,1)S(1)}, u32[]{:S(2)}, u32[]{:S(2)}) collective-permute-start(bf16[2816,512]{1,0:T(8,128)(2,1)S(1)} %constant_dynamic-update-slice_fusion.28.same_ref), channel_id=1, source_target_pairs={{0,4},{4,0},{8,12},{12,8},{16,20},{20,16},{24,28},{28,24},{1,5},{5... | collective-permute-start | bytes 8650760 | tf_op jit(solution)/shard_map/ppermute | solution.py:33
  649.9 27.9 %collective-permute-start.58 = (bf16[256,768]{1,0:T(8,128)(2,1)S(1)}, bf16[256,768]{1,0:T(8,128)(2,1)S(1)}, u32[]{:S(2)}, u32[]{:S(2)}) collective-permute-start(bf16[256,768]{1,0:T(8,128)(2,1)S(1)} %slice.146), channel_id=1, source_target_pairs={{0,8},{4,12},{8,0},{12,4},{16,24},{20,28},{24,16},{28,20},{1,9},{5... | collective-permute-start | bytes 1179656 | tf_op jit(solution)/shard_map/ppermute | solution.py:33
  650.5 27.4 %collective-permute-start.57 = (bf16[256,768]{1,0:T(8,128)(2,1)S(1)}, bf16[256,768]{1,0:T(8,128)(2,1)S(1)}, u32[]{:S(2)}, u32[]{:S(2)}) collective-permute-start(bf16[256,768]{1,0:T(8,128)(2,1)S(1)} %slice.145), channel_id=1, source_target_pairs={{0,16},{4,20},{8,24},{12,28},{16,0},{20,4},{24,8},{28,12},{1,17},{... | collective-permute-start | bytes 1179656 | tf_op jit(solution)/shard_map/ppermute | solution.py:33
  652.2 25.7 %collective-permute-start.60 = (bf16[256,512]{1,0:T(8,128)(2,1)S(1)}, bf16[256,512]{1,0:T(8,128)(2,1)S(1)}, u32[]{:S(2)}, u32[]{:S(2)}) collective-permute-start(bf16[256,512]{1,0:T(8,128)(2,1)S(1)} %copy-done.90), channel_id=1, source_target_pairs={{0,16},{4,20},{8,24},{12,28},{16,0},{20,4},{24,8},{28,12},{1,17},{... | collective-permute-start | bytes 786440 | tf_op jit(solution)/shard_map/ppermute | solution.py:242
  658.8 19.1 %collective-permute-start.59 = (bf16[256,512]{1,0:T(8,128)(2,1)S(1)}, bf16[256,512]{1,0:T(8,128)(2,1)S(1)}, u32[]{:S(2)}, u32[]{:S(2)}) collective-permute-start(bf16[256,512]{1,0:T(8,128)(2,1)S(1)} %copy-done.90), channel_id=1, source_target_pairs={{0,8},{4,12},{8,0},{12,4},{16,24},{20,28},{24,16},{28,20},{1,9},{5... | collective-permute-start | bytes 786440 | tf_op jit(solution)/shard_map/ppermute | solution.py:242
  (119 other events, 1095.3 us)
Sparse Core Ops, SparseCore 0:
  96.3 28.0 all-gather.4
  126.5 106.1 all-gather.6
  234.9 57.4 all-gather.8
  323.6 54.9 reduce-scatter.5
  397.1 54.5 reduce-scatter.7
  454.4 56.0 reduce-scatter.9
  524.1 57.5 reduce-scatter.11
  613.7 24.3 reduce-scatter.13
  641.1 52.5 all-gather.10

commit v12 on v11

--- a/solution.py
+++ b/solution.py
@@ -193,21 +193,46 @@
     core = {i: send(block(in_ref, count + i), block(core_ref, i), i, 1) for i in order}
     for copy in core.values():
         copy.start()
-    chip = {}
+    chip, half = [], rows // 2
+
+    def part(ref, i, n):
+        return ref.at[pl.ds(i * rows + n * half, half)]
+
+    def pass_on(i, n, index, to):
+        chip.append(send(part(held_ref, i, n), part(chip_ref, i, n), index, to))
+        chip[-1].start()
+        return chip[-1]
+
+    relay = count == 4
     for i in order:
         core[i].wait_recv()
         at = pl.ds(i * rows, rows)
         total = in_ref[at, :].astype(F32) + core_ref[at, :].astype(F32)
         held_ref[at, :] = total.astype(BF)
-        if i:
-            chip[i] = send(block(held_ref, i), block(chip_ref, i), count + i, chips[i])
-            chip[i].start()
+        if relay and i == 3:
+            far = [pass_on(3, 0, count, chips[1]), pass_on(3, 1, count + 1, chips[2])]
+        elif relay and i:
+            pass_on(i, i - 1, count + 1 + i, chips[i])
+        elif i:
+            chip.append(send(block(held_ref, i), block(chip_ref, i), count + i, chips[i]))
+            chip[-1].start()
+    if relay:
+        for i, n in ((2, 0), (1, 1)):
+            far[n].wait_recv()
+            at, moved = pl.ds(i * rows + n * half, half), pl.ds(3 * rows + n * half, half)
+            total = held_ref[at, :].astype(F32) + chip_ref[moved, :].astype(F32)
+            held_ref[at, :] = total.astype(BF)
+            pass_on(i, n, count + 4 + n, chips[i])
+        chip, sent = chip[2:], chip[:2]
+    else:
+        sent = []
     total = held_ref[pl.ds(0, rows), :].astype(F32)
-    for i in chip:
-        chip[i].wait_recv()
+    for copy in chip:
+        copy.wait_recv()
+    for i in range(1, 3 if relay else count):
         total += chip_ref[pl.ds(i * rows, rows), :].astype(F32)
     out_ref[...] = total.astype(BF)
-    for copy in [*core.values(), *chip.values()]:
+    for copy in [*core.values(), *sent, *chip]:
         copy.wait_send()
 
 
@@ -224,8 +249,8 @@
             half,
             half,
             half,
-            pltpu.SemaphoreType.DMA((size,)),
-            pltpu.SemaphoreType.DMA((size,)),
+            pltpu.SemaphoreType.DMA((size + 2,)),
+            pltpu.SemaphoreType.DMA((size + 2,)),
         ],
         compiler_params=pltpu.CompilerParams(
             collective_id=number, has_side_effects=True, vmem_limit_bytes=24 << 20
@@ -804,11 +829,13 @@
             lins[d], grad_qkv_w[d] = lin, grad
 
     far, near = offsets[-1:], offsets[1:-1]
-    values, both_grad, grad_up, inner = stage(
-        [expert_flow],
-        (run_back(*far), both_grad, mm_tn(grad_up_act, dispatched).astype(BF), inner),
+    values, both_grad, grad_up_act, inner = stage(
+        [expert_flow], (run_back(*far), both_grad, grad_up_act, inner)
     )
     keep(far, values)
+    grad_up, both_grad = lax.optimization_barrier(
+        (mm_tn(grad_up_act, dispatched).astype(BF), both_grad)
+    )
     qkv_flow = Flow(scatter_steps(grad_qkv_w))
     grad_down = mm_tn(inner, all_slot_grad).astype(BF)
     values, both_grad, grad_down, expert_out = stage(

time: 728 us -> 721 us (level)
    unnamed x243 -> x259, local copies, waits for them, and re-layouts: 59.2 us -> 58.1 us
  transfers between devices with their start and end apart: 77 -> 77, of which waited for: 18 -> 20; matrix products, arithmetic and copies ran while one was open for 21% -> 20% of each run, Pallas kernels for 34% -> 33%
where the time goes in v12:
time: 721 us; the launch traced here: 714 us
  Pallas kernels  239 us (33%)
  waiting for transfers between devices  173 us (24%)
  local copies, waits for them, and re-layouts  89.4 us (12%)
  matrix products  71.7 us (10%)
  starting transfers between devices  66.8 us (9%)
  other arithmetic  58.9 us (8%)
  between operations  15.8 us (2%)
    ppermute x53, waiting for transfers between devices, swap(): return lax.ppermute(value, 'rep', [(i, i ^ bit) for i in range(size)])  110 us
    pallas_call x4, Pallas kernels, attend_back(): pl.pallas_call(attend_back_kernel, grid=(rows // length,), in_specs=[whol...  71.9 us
    pallas_call x2, Pallas kernels, gather_rows(): pl.pallas_call(functools.partial(gather_kernel, peers()), out_shape=jax.S...  58.4 us
    unnamed x259, local copies, waits for them, and re-layouts  58.1 us
    ppermute x53, starting transfers between devices, swap(): return lax.ppermute(value, 'rep', [(i, i ^ bit) for i in range(size)])  47.9 us
    pallas_call x4, Pallas kernels, attend(): pl.pallas_call(functools.partial(attend_kernel, parts), grid_spec=pltpu.P...  42.5 us
    dot_general x6, matrix products, mm_tn(): lax.dot_general(left, right, (((0,), (0,)), ((), ())), preferred_element_...  26.9 us
    dot_general x5, matrix products, mm(): return jnp.dot(left, right, preferred_element_type=F32)  24.6 us
  transfers between devices with their start and end apart: 77, of which 20 were waited for; matrix products, arithmetic and copies ran while one was open for 20% of the time, Pallas kernels for 33%

profile of v12, /device:TPU:0, one launch (start us, length us, event | category | flops | bytes accessed | tf_op | source)
XLA Modules:
  0.0 714.4 jit_solution(1125807602248548254)
XLA Ops:
  8.8 3.1 collective-permute-start.2
  11.8 2.6 collective-permute-start.1
  17.7 2.7 constant_dynamic-slice_fusion.4
  21.2 2.3 constant_dynamic-slice_fusion.15
  26.2 16.2 %collective-permute-done.3.refs_5_ = bf16[512,768]{1,0:T(8,128)(2,1)} collective-permute-done((bf16[512,768]{1,0:T(8,128)(2,1)S(1)}, bf16[512,768]{1,0:T(8,128)(2,1)}, u32[]{:S(2)}, u32[]{:S(2)}) %collective-permute-start.3) | collective-permute-done | bytes 786464 | tf_op jit(solution)/shard_map/ppermute | solution.py:743
  42.5 2.1 fusion.2
  47.9 18.9 %collective-permute-done.7.refs_6_ = bf16[512,768]{1,0:T(8,128)(2,1)} collective-permute-done((bf16[512,768]{1,0:T(8,128)(2,1)}, bf16[512,768]{1,0:T(8,128)(2,1)}, u32[]{:S(2)}, u32[]{:S(2)}) %collective-permute-start.7) | collective-permute-done | bytes 786464 | tf_op jit(solution)/shard_map/ppermute | solution.py:757
  73.3 2.1 constant_dynamic-slice_fusion.13
  75.4 20.7 %collective-permute-done.10 = bf16[256,768]{1,0:T(8,128)(2,1)} collective-permute-done((bf16[256,768]{1,0:T(8,128)(2,1)}, bf16[256,768]{1,0:T(8,128)(2,1)}, u32[]{:S(2)}, u32[]{:S(2)}) %collective-permute-start.10) | collective-permute-done | bytes 393248 | tf_op jit(solution)/shard_map/ppermute | solution.py:33
  99.4 2.1 pad_maximum_fusion.6.refs_4_.refs_8_
  110.0 2.1 pad_maximum_fusion.refs_0_.refs_1_.refs_2_.refs_3_.x_ref
  114.4 11.3 %attend.4 = (bf16[1024,256]{1,0:T(8,128)(2,1)S(1)}, bf16[1024,768]{1,0:T(8,128)(2,1)S(1)}, f32[1024,2]{1,0:T(8,128)S(1)}) custom-call(s32[1]{0:T(128)} %bitcast.1.z_ref, bf16[1024,2048]{1,0:T(8,128)(2,1)S(1)} %pad_maximum_fusion.refs_0_.refs_1_.refs_2_.refs_3_.x_ref, bf16[1024,2048]{1,0:T(8,128)(2,1)S(1)} %pad_maximum_fusion.refs_0_.refs_1_.refs_2_.refs_3_.x_ref, ...), custom_call_target="tpu_custom_call" | custom-call | flops 3758096384 | bytes 10485760 | tf_op jit(solution)/shard_map/attend/pallas_call | solution.py:423
  139.3 2.2 copy-done.3
  143.8 10.7 %attend.5 = (bf16[1024,256]{1,0:T(8,128)(2,1)S(1)}, bf16[1024,768]{1,0:T(8,128)(2,1)S(1)}, f32[1024,2]{1,0:T(8,128)S(1)}) custom-call(s32[1]{0:T(128)} %bitcast.1.z_ref, bf16[1024,2048]{1,0:T(8,128)(2,1)S(1)} %copy-done.3, bf16[1024,2048]{1,0:T(8,128)(2,1)S(1)} %copy-done.3, bf16[1024,2048]{1,0:T(8,128)(2,1)S(1)} %copy-done.3, ...), custom_call_target="tpu_custom_call" | custom-call | flops 3758096384 | bytes 10485760 | tf_op jit(solution)/shard_map/attend/pallas_call | solution.py:423
  156.5 10.8 %attend.6 = (bf16[1024,256]{1,0:T(8,128)(2,1)S(1)}, bf16[1024,768]{1,0:T(8,128)(2,1)S(1)}, f32[1024,2]{1,0:T(8,128)S(1)}) custom-call(s32[1]{0:T(128)} %bitcast.1.z_ref, bf16[1024,2048]{1,0:T(8,128)(2,1)S(1)} %copy-done.3, bf16[1024,2048]{1,0:T(8,128)(2,1)S(1)} %copy-done.3, bf16[1024,2048]{1,0:T(8,128)(2,1)S(1)} %copy-done.3, ...), custom_call_target="tpu_custom_call" | custom-call | flops 3758096384 | bytes 10485760 | tf_op jit(solution)/shard_map/attend/pallas_call | solution.py:423
  169.1 9.6 %attend.7 = (bf16[1024,256]{1,0:T(8,128)(2,1)S(1)}, bf16[1024,768]{1,0:T(8,128)(2,1)S(1)}, f32[1024,2]{1,0:T(8,128)S(1)}) custom-call(s32[1]{0:T(128)} %bitcast.1.z_ref, bf16[1024,2048]{1,0:T(8,128)(2,1)S(1)} %copy-done.3, bf16[1024,2048]{1,0:T(8,128)(2,1)S(1)} %copy-done.3, bf16[1024,2048]{1,0:T(8,128)(2,1)S(1)} %copy-done.3, ...), custom_call_target="tpu_custom_call" | custom-call | flops 3758096384 | bytes 10485760 | tf_op jit(solution)/shard_map/attend/pallas_call | solution.py:423
  183.1 6.1 collective-permute-done.22
  189.2 2.1 collective-permute-done.23
  191.4 6.3 fusion.53
  197.7 3.4 copy-done.66
  203.2 2.3 fusion.22.in_ref
  207.2 4.0 multiply_reduce_fusion.2
  214.0 29.1 %gather_rows.2 = bf16[1024,2048]{1,0:T(8,128)(2,1)S(1)} custom-call(bf16[128,2048]{1,0:T(8,128)(2,1)S(1)} %convolution_convert_fusion.5.in_ref), custom_call_target="tpu_custom_call" | custom-call | bytes 62914560 | tf_op jit(solution)/shard_map/gather_rows/pallas_call | solution.py:153
  245.1 11.7 %fusion.54 = f32[1024,1408]{1,0:T(8,128)} fusion(bf16[1024,2048]{1,0:T(8,128)(2,1)} %copy-done.8, bf16[2048,1408]{1,0:T(8,128)(2,1)} %all-gather.7.cloned.1.call-done), kind=kOutput, calls=%fused_computation.179 | convolution fusion | flops 5905580032 | bytes 15728640 | tf_op jit(solution)/shard_map/dot_general | solution.py:20
  256.8 29.3 %gather_rows.3 = bf16[1024,2048]{1,0:T(8,128)(2,1)S(1)} custom-call(bf16[128,2048]{1,0:T(8,128)(2,1)S(1)} %fusion.22.in_ref), custom_call_target="tpu_custom_call" | custom-call | bytes 62914560 | tf_op jit(solution)/shard_map/gather_rows/pallas_call | solution.py:153
  288.1 4.2 all-gather.9.cloned.1.call-done
  292.4 9.1 %multiply_convert_fusion.2 = (bf16[1024,704]{1,0:T(8,128)(2,1)S(1)}, bf16[1024,704]{1,0:T(8,128)(2,1)S(1)}, bf16[1024,704]{1,0:T(8,128)(2,1)S(1)}) fusion(f32[1024,1408]{1,0:T(8,128)} %fusion.54, bf16[1024,2048]{1,0:T(8,128)(2,1)} %copy-done.6, bf16[704,2048]{1,0:T(8,128)(2,1)} %all-gather.9.cloned.1.call-done), kind=kOutput, calls=%fused_computation.44 | convolution fusion | flops 2963603456 | bytes 17170432 | tf_op jit(solution)/shard_map/dot_general | solution.py:24
  301.5 3.6 convolution_convert_fusion.1
  307.8 11.1 %convolution_convert_fusion.in_ref = bf16[1024,2048]{1,0:T(8,128)(2,1)} fusion(bf16[2048,1408]{1,0:T(8,128)(2,1)} %all-gather.7.cloned.1.call-done, bf16[1024,704]{1,0:T(8,128)(2,1)S(1)} %get-tuple-element.203, bf16[1024,704]{1,0:T(8,128)(2,1)S(1)} %get-tuple-element.316), kind=kOutput, calls=%fused_computation.34 | convolution fusion | flops 5913444352 | bytes 12845056 | tf_op jit(solution)/shard_map/dot_general | solution.py:24
  318.9 4.5 convolution_convert_fusion.4
  323.9 2.2 copy-done.11
  326.1 22.5 %reduce_rows.1 = bf16[128,2048]{1,0:T(8,128)(2,1)S(1)} custom-call(bf16[1024,2048]{1,0:T(8,128)(2,1)S(1)} %copy-done.11), custom_call_target="tpu_custom_call" | custom-call | bytes 62914560 | tf_op jit(solution)/shard_map/reduce_rows/pallas_call | solution.py:243
  350.2 3.2 multiply_convert_fusion
  354.2 2.5 add_convert_fusion.1
  362.5 17.7 %attend_back.4 = (bf16[1024,768]{1,0:T(8,128)(2,1)S(1)}, bf16[1024,768]{1,0:T(8,128)(2,1)S(1)}, bf16[1024,768]{1,0:T(8,128)(2,1)}) custom-call(bf16[512,2048]{1,0:T(8,128)(2,1)} %copy-done.69, bf16[512,2048]{1,0:T(8,128)(2,1)} %copy-done.109, bf16[256,2048]{1,0:T(8,128)(2,1)S(1)} %pad_maximum_fusion.3.out_ref, bf16[1024,768]{1,0:T(8,128)(2,1)} %copy-done.41, ...), custom_call_target="tpu_custom_call" | custom-call | flops 5637144576 | bytes 15728640 | tf_op jit(solution)/shard_map/attend_back/pallas_call | solution.py:519
  385.4 4.5 convolution_convert_fusion.3
  393.4 18.1 %attend_back.6 = (bf16[1024,768]{1,0:T(8,128)(2,1)S(1)}, bf16[1024,768]{1,0:T(8,128)(2,1)S(1)}, bf16[1024,768]{1,0:T(8,128)(2,1)}) custom-call(bf16[512,2048]{1,0:T(8,128)(2,1)} %copy-done.69, bf16[512,2048]{1,0:T(8,128)(2,1)} %copy-done.109, bf16[256,2048]{1,0:T(8,128)(2,1)S(1)} %copy-done.23, bf16[1024,768]{1,0:T(8,128)(2,1)} %copy-done.40, ...), custom_call_target="tpu_custom_call" | custom-call | flops 5637144576 | bytes 15728640 | tf_op jit(solution)/shard_map/attend_back/pallas_call | solution.py:519
  414.4 17.7 %attend_back.5 = (bf16[1024,768]{1,0:T(8,128)(2,1)S(1)}, bf16[1024,768]{1,0:T(8,128)(2,1)S(1)}, bf16[1024,768]{1,0:T(8,128)(2,1)}) custom-call(bf16[512,2048]{1,0:T(8,128)(2,1)} %copy-done.69, bf16[512,2048]{1,0:T(8,128)(2,1)} %copy-done.109, bf16[256,2048]{1,0:T(8,128)(2,1)S(1)} %copy-done.21, bf16[1024,768]{1,0:T(8,128)(2,1)} %copy-done.39, ...), custom_call_target="tpu_custom_call" | custom-call | flops 5637144576 | bytes 15728640 | tf_op jit(solution)/shard_map/attend_back/pallas_call | solution.py:519
  434.5 4.5 convolution_convert_fusion.2
  441.4 3.4 add_convert_fusion.4
  446.2 3.5 add_convert_fusion.5
  450.1 18.4 %attend_back.7 = (bf16[1024,768]{1,0:T(8,128)(2,1)S(1)}, bf16[1024,768]{1,0:T(8,128)(2,1)S(1)}, bf16[1024,768]{1,0:T(8,128)(2,1)}) custom-call(bf16[512,2048]{1,0:T(8,128)(2,1)} %copy-done.69, bf16[512,2048]{1,0:T(8,128)(2,1)} %copy-done.109, bf16[256,2048]{1,0:T(8,128)(2,1)S(1)} %copy-done.37, bf16[1024,768]{1,0:T(8,128)(2,1)} %copy-done.38, ...), custom_call_target="tpu_custom_call" | custom-call | flops 5637144576 | bytes 15728640 | tf_op jit(solution)/shard_map/attend_back/pallas_call | solution.py:519
  468.6 10.0 %fusion.15 = bf16[1024,2048]{1,0:T(8,128)(2,1)} fusion(bf16[1024,1024]{1,0:T(8,128)(2,1)} %constant_dynamic-update-slice_fusion.14, bf16[512,2048]{1,0:T(8,128)(2,1)} %copy-done.109, bf16[512,2048]{1,0:T(8,128)(2,1)S(1)} %copy-done.70), kind=kOutput, calls=%fused_computation.33 | convolution fusion | flops 4305453056 | bytes 10485760 | tf_op jit(solution)/shard_map/dot_general | solution.py:28
  478.6 2.2 add_convert_fusion
  480.8 23.3 %normed_back.1 = (f32[512,2048]{1,0:T(8,128)}, bf16[512,2048]{1,0:T(8,128)(2,1)}) custom-call(s32[1]{0:T(128)} %bitcast.1.z_ref, bf16[1024,768]{1,0:T(8,128)(2,1)} %copy-done.53, bf16[1024,768]{1,0:T(8,128)(2,1)} %copy-done.52, bf16[1024,768]{1,0:T(8,128)(2,1)} %copy-done.51, bf16[1024,768]{1,0:T(8,128)(2,1)} %copy-done.50, ...), custom_call_target="tpu_custom_call" | custom-call | flops 12884901888 | bytes 27262976 | tf_op jit(solution)/shard_map/normed_back/pallas_call | solution.py:576
  504.1 5.1 collective-permute-done.35
  510.3 2.6 add_convert_fusion.2
  512.9 2.5 add_convert_fusion.3
  524.5 22.8 %collective-permute-done.39 = bf16[128,2048]{1,0:T(8,128)(2,1)S(1)} collective-permute-done((bf16[128,2048]{1,0:T(8,128)(2,1)S(1)}, bf16[128,2048]{1,0:T(8,128)(2,1)S(1)}, u32[]{:S(2)}, u32[]{:S(2)}) %collective-permute-start.39) | collective-permute-done | bytes 524320 | tf_op jit(solution)/shard_map/ppermute | solution.py:33
  551.6 3.2 fusion.9
  554.8 3.9 fusion.6
  558.8 3.4 collective-permute-done.37
  562.8 6.1 collective-permute-done.44
  575.7 24.2 %collective-permute-done.46 = bf16[128,2048]{1,0:T(8,128)(2,1)S(1)} collective-permute-done((bf16[128,2048]{1,0:T(8,128)(2,1)S(1)}, bf16[128,2048]{1,0:T(8,128)(2,1)S(1)}, u32[]{:S(2)}, u32[]{:S(2)}) %collective-permute-start.46) | collective-permute-done | bytes 524320 | tf_op jit(solution)/shard_map/ppermute | solution.py:33
  603.6 2.2 add_convert_fusion.7
  615.6 5.0 place_turned.2
  620.6 13.8 %collective-permute-done.55 = f32[2,2048]{1,0:T(2,128)S(1)} collective-permute-done((f32[2,2048]{1,0:T(2,128)S(1)}, f32[2,2048]{1,0:T(2,128)S(1)}, u32[]{:S(2)}, u32[]{:S(2)}) %collective-permute-start.55) | collective-permute-done | bytes 16416 | tf_op jit(solution)/shard_map/ppermute | solution.py:33
  646.2 6.3 collective-permute-done.61
  652.4 2.3 collective-permute-start.59
  657.1 14.4 %collective-permute-done.60 = bf16[256,512]{1,0:T(8,128)(2,1)S(1)} collective-permute-done((bf16[256,512]{1,0:T(8,128)(2,1)S(1)}, bf16[256,512]{1,0:T(8,128)(2,1)S(1)}, u32[]{:S(2)}, u32[]{:S(2)}) %collective-permute-start.60) | collective-permute-done | bytes 262176 | tf_op jit(solution)/shard_map/ppermute | solution.py:267
  682.3 5.0 place_turned.3
  687.3 4.3 place.3
  691.6 6.3 place.2
  698.5 8.9 %convert_element_type.237 = f32[5632,512]{1,0:T(8,128)} convert(bf16[5632,512]{1,0:T(8,128)(2,1)} %all-gather.11.cloned.1.call-done) | non-fusion elementwise | flops 2883584 | bytes 17301504 | tf_op jit(solution)/shard_map/convert_element_type | solution.py:889
  (472 shorter events, 156.6 us)
Async XLA Ops:
  7.2 123.9 %all-gather.5.cloned.1.call-start = ((), (), s32[]{:S(2)}) async-start(), calls=%async_computation.5 | async-start | bytes 1310720 | tf_op jit(solution)/shard_map/all_gather | solution.py:761
  8.8 17.4 %collective-permute-start.2 = (bf16[2,512]{1,0:T(2,128)(2,1)S(1)}, bf16[2,512]{1,0:T(2,128)(2,1)S(1)}, u32[]{:S(2)}, u32[]{:S(2)}) collective-permute-start(bf16[2,512]{1,0:T(2,128)(2,1)S(1)} %get-tuple-element.312), channel_id=1, source_target_pairs={{0,1},{1,2},{2,3},{3,0},{4,5},{5,6},{6,7},{7,4},{8,9},{9,10},{10,1... | collective-permute-start | bytes 6152 | tf_op jit(solution)/shard_map/ppermute | solution.py:344
  11.8 14.3 %collective-permute-start.1 = (bf16[2,512]{1,0:T(2,128)(2,1)S(1)}, bf16[2,512]{1,0:T(2,128)(2,1)S(1)}, u32[]{:S(2)}, u32[]{:S(2)}) collective-permute-start(bf16[2,512]{1,0:T(2,128)(2,1)S(1)} %get-tuple-element.312), channel_id=1, source_target_pairs={{0,2},{1,3},{2,0},{3,1},{4,6},{5,7},{6,4},{7,5},{8,10},{9,11},{10,... | collective-permute-start | bytes 6152 | tf_op jit(solution)/shard_map/ppermute | solution.py:344
  20.5 21.9 %collective-permute-start.3 = (bf16[512,768]{1,0:T(8,128)(2,1)S(1)}, bf16[512,768]{1,0:T(8,128)(2,1)}, u32[]{:S(2)}, u32[]{:S(2)}) collective-permute-start(bf16[512,768]{1,0:T(8,128)(2,1)S(1)} %pad_maximum_fusion.5.refs_4_), channel_id=1, source_target_pairs={{0,1},{1,2},{2,3},{3,0},{4,5},{5,6},{6,7},{7,4},{8,9},{9,10},{10,1... | collective-permute-start | bytes 2359304 | tf_op jit(solution)/shard_map/ppermute | solution.py:743
  44.7 22.2 %collective-permute-start.8 = (bf16[512,2048]{1,0:T(8,128)(2,1)S(1)}, bf16[512,2048]{1,0:T(8,128)(2,1)S(1)}, u32[]{:S(2)}, u32[]{:S(2)}) collective-permute-start(bf16[512,2048]{1,0:T(8,128)(2,1)S(1)} %fusion.2), channel_id=1, source_target_pairs={{0,4},{4,0},{8,12},{12,8},{16,20},{20,16},{24,28},{28,24},{1,5},{5... | collective-permute-start | bytes 6291464 | tf_op jit(solution)/shard_map/ppermute | solution.py:33
  44.8 22.1 %collective-permute-start.7 = (bf16[512,768]{1,0:T(8,128)(2,1)}, bf16[512,768]{1,0:T(8,128)(2,1)}, u32[]{:S(2)}, u32[]{:S(2)}) collective-permute-start(bf16[512,768]{1,0:T(8,128)(2,1)} %collective-permute-done.3.refs_5_), channel_id=1, source_target_pairs={{0,1},{1,2},{2,3},{3,0},{4,5},{5,6},{6,7},{7,4},{8,9},{9,10},{10,1... | collective-permute-start | bytes 2359304 | tf_op jit(solution)/shard_map/ppermute | solution.py:757
  44.8 22.0 %collective-permute-start.6 = (bf16[512,768]{1,0:T(8,128)(2,1)}, bf16[512,768]{1,0:T(8,128)(2,1)S(1)}, u32[]{:S(2)}, u32[]{:S(2)}) collective-permute-start(bf16[512,768]{1,0:T(8,128)(2,1)} %collective-permute-done.3.refs_5_), channel_id=1, source_target_pairs={{0,16},{4,20},{8,24},{12,28},{16,0},{20,4},{24,8},{28,12},{1,17},{... | collective-permute-start | bytes 2359304 | tf_op jit(solution)/shard_map/ppermute | solution.py:33
  46.4 20.4 %collective-permute-start.5 = (bf16[512,768]{1,0:T(8,128)(2,1)}, bf16[512,768]{1,0:T(8,128)(2,1)S(1)}, u32[]{:S(2)}, u32[]{:S(2)}) collective-permute-start(bf16[512,768]{1,0:T(8,128)(2,1)} %collective-permute-done.3.refs_5_), channel_id=1, source_target_pairs={{0,8},{4,12},{8,0},{12,4},{16,24},{20,28},{24,16},{28,20},{1,9},{5... | collective-permute-start | bytes 2359304 | tf_op jit(solution)/shard_map/ppermute | solution.py:33
  66.9 29.2 %collective-permute-start.13 = (bf16[512,768]{1,0:T(8,128)(2,1)}, bf16[512,768]{1,0:T(8,128)(2,1)}, u32[]{:S(2)}, u32[]{:S(2)}) collective-permute-start(bf16[512,768]{1,0:T(8,128)(2,1)} %collective-permute-done.7.refs_6_), channel_id=1, source_target_pairs={{0,1},{1,2},{2,3},{3,0},{4,5},{5,6},{6,7},{7,4},{8,9},{9,10},{10,1... | collective-permute-start | bytes 2359304 | tf_op jit(solution)/shard_map/ppermute | solution.py:757
  66.9 29.2 %collective-permute-start.12 = (bf16[512,768]{1,0:T(8,128)(2,1)}, bf16[512,768]{1,0:T(8,128)(2,1)}, u32[]{:S(2)}, u32[]{:S(2)}) collective-permute-start(bf16[512,768]{1,0:T(8,128)(2,1)} %collective-permute-done.7.refs_6_), channel_id=1, source_target_pairs={{0,16},{4,20},{8,24},{12,28},{16,0},{20,4},{24,8},{28,12},{1,17},{... | collective-permute-start | bytes 2359304 | tf_op jit(solution)/shard_map/ppermute | solution.py:33
  68.5 27.6 %collective-permute-start.11 = (bf16[512,768]{1,0:T(8,128)(2,1)}, bf16[512,768]{1,0:T(8,128)(2,1)}, u32[]{:S(2)}, u32[]{:S(2)}) collective-permute-start(bf16[512,768]{1,0:T(8,128)(2,1)} %collective-permute-done.7.refs_6_), channel_id=1, source_target_pairs={{0,8},{4,12},{8,0},{12,4},{16,24},{20,28},{24,16},{28,20},{1,9},{5... | collective-permute-start | bytes 2359304 | tf_op jit(solution)/shard_map/ppermute | solution.py:33
  71.6 24.5 %collective-permute-start.10 = (bf16[256,768]{1,0:T(8,128)(2,1)}, bf16[256,768]{1,0:T(8,128)(2,1)}, u32[]{:S(2)}, u32[]{:S(2)}) collective-permute-start(bf16[256,768]{1,0:T(8,128)(2,1)} %slice.116), channel_id=1, source_target_pairs={{0,8},{4,12},{8,0},{12,4},{16,24},{20,28},{24,16},{28,20},{1,9},{5... | collective-permute-start | bytes 1179656 | tf_op jit(solution)/shard_map/ppermute | solution.py:33
  72.1 24.0 %collective-permute-start.9 = (bf16[256,768]{1,0:T(8,128)(2,1)}, bf16[256,768]{1,0:T(8,128)(2,1)}, u32[]{:S(2)}, u32[]{:S(2)}) collective-permute-start(bf16[256,768]{1,0:T(8,128)(2,1)} %slice.115), channel_id=1, source_target_pairs={{0,16},{4,20},{8,24},{12,28},{16,0},{20,4},{24,8},{28,12},{1,17},{... | collective-permute-start | bytes 1179656 | tf_op jit(solution)/shard_map/ppermute | solution.py:33
  96.2 149.0 %all-gather.7.cloned.1.call-start = ((), (), s32[]{:S(2)}) async-start(), calls=%async_computation.6 | async-start | bytes 7208960 | tf_op jit(solution)/shard_map/all_gather | solution.py:769
  96.9 195.5 %all-gather.9.cloned.1.call-start = ((), (), s32[]{:S(2)}) async-start(), calls=%async_computation.7 | async-start | bytes 3604480 | tf_op jit(solution)/shard_map/all_gather | solution.py:770
  102.7 28.4 %collective-permute-start.17 = (bf16[512,768]{1,0:T(8,128)(2,1)}, bf16[512,768]{1,0:T(8,128)(2,1)}, u32[]{:S(2)}, u32[]{:S(2)}) collective-permute-start(bf16[512,768]{1,0:T(8,128)(2,1)} %collective-permute-done.13.refs_7_), channel_id=1, source_target_pairs={{0,16},{4,20},{8,24},{12,28},{16,0},{20,4},{24,8},{28,12},{1,17},{... | collective-permute-start | bytes 2359304 | tf_op jit(solution)/shard_map/ppermute | solution.py:33
  103.3 27.8 %collective-permute-start.16 = (bf16[512,768]{1,0:T(8,128)(2,1)}, bf16[512,768]{1,0:T(8,128)(2,1)}, u32[]{:S(2)}, u32[]{:S(2)}) collective-permute-start(bf16[512,768]{1,0:T(8,128)(2,1)} %collective-permute-done.13.refs_7_), channel_id=1, source_target_pairs={{0,8},{4,12},{8,0},{12,4},{16,24},{20,28},{24,16},{28,20},{1,9},{5... | collective-permute-start | bytes 2359304 | tf_op jit(solution)/shard_map/ppermute | solution.py:33
  106.8 22.8 %collective-permute-start.15 = (bf16[256,768]{1,0:T(8,128)(2,1)S(1)}, bf16[256,768]{1,0:T(8,128)(2,1)S(1)}, u32[]{:S(2)}, u32[]{:S(2)}) collective-permute-start(bf16[256,768]{1,0:T(8,128)(2,1)S(1)} %slice.118), channel_id=1, source_target_pairs={{0,8},{4,12},{8,0},{12,4},{16,24},{20,28},{24,16},{28,20},{1,9},{5... | collective-permute-start | bytes 1179656 | tf_op jit(solution)/shard_map/ppermute | solution.py:33
  107.4 22.9 %collective-permute-start.14 = (bf16[256,768]{1,0:T(8,128)(2,1)S(1)}, bf16[256,768]{1,0:T(8,128)(2,1)S(1)}, u32[]{:S(2)}, u32[]{:S(2)}) collective-permute-start(bf16[256,768]{1,0:T(8,128)(2,1)S(1)} %slice.117), channel_id=1, source_target_pairs={{0,16},{4,20},{8,24},{12,28},{16,0},{20,4},{24,8},{28,12},{1,17},{... | collective-permute-start | bytes 1179656 | tf_op jit(solution)/shard_map/ppermute | solution.py:33
  131.1 47.7 %collective-permute-start.21 = (bf16[256,2048]{1,0:T(8,128)(2,1)}, bf16[256,2048]{1,0:T(8,128)(2,1)S(1)}, u32[]{:S(2)}, u32[]{:S(2)}) collective-permute-start(bf16[256,2048]{1,0:T(8,128)(2,1)} %all-gather.5.cloned.1.call-done.out_ref), channel_id=1, source_target_pairs={{0,16},{4,20},{8,24},{12,28},{16,0},{20,4},{24,8},{28,12},{1,17},{... | collective-permute-start | bytes 3145736 | tf_op jit(solution)/shard_map/ppermute | solution.py:33
  132.7 46.2 %collective-permute-start.20 = (bf16[256,2048]{1,0:T(8,128)(2,1)}, bf16[256,2048]{1,0:T(8,128)(2,1)S(1)}, u32[]{:S(2)}, u32[]{:S(2)}) collective-permute-start(bf16[256,2048]{1,0:T(8,128)(2,1)} %all-gather.5.cloned.1.call-done.out_ref), channel_id=1, source_target_pairs={{0,8},{4,12},{8,0},{12,4},{16,24},{20,28},{24,16},{28,20},{1,9},{5... | collective-permute-start | bytes 3145736 | tf_op jit(solution)/shard_map/ppermute | solution.py:33
  136.3 32.1 %collective-permute-start.19 = (bf16[256,768]{1,0:T(8,128)(2,1)S(1)}, bf16[256,768]{1,0:T(8,128)(2,1)S(1)}, u32[]{:S(2)}, u32[]{:S(2)}) collective-permute-start(bf16[256,768]{1,0:T(8,128)(2,1)S(1)} %slice.120), channel_id=1, source_target_pairs={{0,8},{4,12},{8,0},{12,4},{16,24},{20,28},{24,16},{28,20},{1,9},{5... | collective-permute-start | bytes 1179656 | tf_op jit(solution)/shard_map/ppermute | solution.py:33
  136.9 31.5 %collective-permute-start.18 = (bf16[256,768]{1,0:T(8,128)(2,1)S(1)}, bf16[256,768]{1,0:T(8,128)(2,1)S(1)}, u32[]{:S(2)}, u32[]{:S(2)}) collective-permute-start(bf16[256,768]{1,0:T(8,128)(2,1)S(1)} %slice.119), channel_id=1, source_target_pairs={{0,16},{4,20},{8,24},{12,28},{16,0},{20,4},{24,8},{28,12},{1,17},{... | collective-permute-start | bytes 1179656 | tf_op jit(solution)/shard_map/ppermute | solution.py:33
  202.7 301.3 %reduce-scatter.6.cloned.1.call-start = ((), (), s32[]{:S(2)}) async-start(), calls=%async_computation.8 | async-start | bytes 3604480 | tf_op jit(solution)/shard_map/reduce_scatter | solution.py:846
  306.9 41.7 %collective-permute-start.25 = (bf16[512,2048]{1,0:T(8,128)(2,1)}, bf16[512,2048]{1,0:T(8,128)(2,1)}, u32[]{:S(2)}, u32[]{:S(2)}) collective-permute-start(bf16[512,2048]{1,0:T(8,128)(2,1)} %slice.152), channel_id=1, source_target_pairs={{0,4},{4,0},{8,12},{12,8},{16,20},{20,16},{24,28},{28,24},{1,5},{5... | collective-permute-start | bytes 6291464 | tf_op jit(solution)/shard_map/ppermute | solution.py:33
  323.5 186.9 %reduce-scatter.8.cloned.1.call-start = ((), (), s32[]{:S(2)}) async-start(), calls=%async_computation.9 | async-start | bytes 3604480 | tf_op jit(solution)/shard_map/reduce_scatter | solution.py:846
  357.7 24.8 %collective-permute-start.28 = (bf16[128,2048]{1,0:T(8,128)(2,1)}, bf16[128,2048]{1,0:T(8,128)(2,1)S(1)}, u32[]{:S(2)}, u32[]{:S(2)}) collective-permute-start(bf16[128,2048]{1,0:T(8,128)(2,1)} %get-tuple-element.326), channel_id=1, source_target_pairs={{0,24},{4,28},{8,16},{12,20},{16,8},{20,12},{24,0},{28,4},{1,25},{... | collective-permute-start | bytes 1572872 | tf_op jit(solution)/shard_map/ppermute | solution.py:267
  359.2 25.2 %collective-permute-start.27 = (bf16[128,2048]{1,0:T(8,128)(2,1)S(1)}, bf16[128,2048]{1,0:T(8,128)(2,1)S(1)}, u32[]{:S(2)}, u32[]{:S(2)}) collective-permute-start(bf16[128,2048]{1,0:T(8,128)(2,1)S(1)} %get-tuple-element.327), channel_id=1, source_target_pairs={{0,16},{4,20},{8,24},{12,28},{16,0},{20,4},{24,8},{28,12},{1,17},{... | collective-permute-start | bytes 1572872 | tf_op jit(solution)/shard_map/ppermute | solution.py:267
  360.7 23.8 %collective-permute-start.26 = (bf16[128,2048]{1,0:T(8,128)(2,1)S(1)}, bf16[128,2048]{1,0:T(8,128)(2,1)S(1)}, u32[]{:S(2)}, u32[]{:S(2)}) collective-permute-start(bf16[128,2048]{1,0:T(8,128)(2,1)S(1)} %get-tuple-element.328), channel_id=1, source_target_pairs={{0,8},{4,12},{8,0},{12,4},{16,24},{20,28},{24,16},{28,20},{1,9},{5... | collective-permute-start | bytes 1572872 | tf_op jit(solution)/shard_map/ppermute | solution.py:267
  389.9 127.3 %reduce-scatter.10.cloned.1.call-start = ((), (), s32[]{:S(2)}) async-start(), calls=%async_computation.10 | async-start | bytes 3604480 | tf_op jit(solution)/shard_map/reduce_scatter | solution.py:846
  390.2 48.8 %collective-permute-start.32 = (bf16[1024,768]{1,0:T(8,128)(2,1)}, bf16[1024,768]{1,0:T(8,128)(2,1)}, u32[]{:S(2)}, u32[]{:S(2)}) collective-permute-start(bf16[1024,768]{1,0:T(8,128)(2,1)} %copy-done.43), channel_id=1, source_target_pairs={{0,8},{4,12},{8,0},{12,4},{16,24},{20,28},{24,16},{28,20},{1,9},{5... | collective-permute-start | bytes 4718600 | tf_op jit(solution)/shard_map/ppermute | solution.py:33
  391.7 47.3 %collective-permute-start.33 = (bf16[1024,768]{1,0:T(8,128)(2,1)}, bf16[1024,768]{1,0:T(8,128)(2,1)}, u32[]{:S(2)}, u32[]{:S(2)}) collective-permute-start(bf16[1024,768]{1,0:T(8,128)(2,1)} %get-tuple-element.215), channel_id=1, source_target_pairs={{0,16},{4,20},{8,24},{12,28},{16,0},{20,4},{24,8},{28,12},{1,17},{... | collective-permute-start | bytes 4718600 | tf_op jit(solution)/shard_map/ppermute | solution.py:33
  439.0 164.6 %reduce-scatter.12.cloned.1.call-start = ((), (), s32[]{:S(2)}) async-start(), calls=%async_computation.11 | async-start | bytes 3932160 | tf_op jit(solution)/shard_map/reduce_scatter | solution.py:861
  439.1 41.7 %collective-permute-start.30 = (bf16[1024,768]{1,0:T(8,128)(2,1)}, bf16[1024,768]{1,0:T(8,128)(2,1)}, u32[]{:S(2)}, u32[]{:S(2)}) collective-permute-start(bf16[1024,768]{1,0:T(8,128)(2,1)} %copy-done.42), channel_id=1, source_target_pairs={{0,8},{4,12},{8,0},{12,4},{16,24},{20,28},{24,16},{28,20},{1,9},{5... | collective-permute-start | bytes 4718600 | tf_op jit(solution)/shard_map/ppermute | solution.py:33
  440.7 40.0 %collective-permute-start.31 = (bf16[1024,768]{1,0:T(8,128)(2,1)}, bf16[1024,768]{1,0:T(8,128)(2,1)}, u32[]{:S(2)}, u32[]{:S(2)}) collective-permute-start(bf16[1024,768]{1,0:T(8,128)(2,1)} %get-tuple-element.213), channel_id=1, source_target_pairs={{0,16},{4,20},{8,24},{12,28},{16,0},{20,4},{24,8},{28,12},{1,17},{... | collective-permute-start | bytes 4718600 | tf_op jit(solution)/shard_map/ppermute | solution.py:33
  444.8 64.4 %collective-permute-start.35 = (bf16[1024,768]{1,0:T(8,128)(2,1)}, bf16[1024,768]{1,0:T(8,128)(2,1)}, u32[]{:S(2)}, u32[]{:S(2)}) collective-permute-start(bf16[1024,768]{1,0:T(8,128)(2,1)} %add_convert_fusion.4), channel_id=1, source_target_pairs={{0,8},{4,12},{8,0},{12,4},{16,24},{20,28},{24,16},{28,20},{1,9},{5... | collective-permute-start | bytes 4718600 | tf_op jit(solution)/shard_map/ppermute | solution.py:33
  449.6 60.7 %collective-permute-start.34 = (bf16[1024,768]{1,0:T(8,128)(2,1)}, bf16[1024,768]{1,0:T(8,128)(2,1)}, u32[]{:S(2)}, u32[]{:S(2)}) collective-permute-start(bf16[1024,768]{1,0:T(8,128)(2,1)} %add_convert_fusion.5), channel_id=1, source_target_pairs={{0,16},{4,20},{8,24},{12,28},{16,0},{20,4},{24,8},{28,12},{1,17},{... | collective-permute-start | bytes 4718600 | tf_op jit(solution)/shard_map/ppermute | solution.py:33
  510.3 39.1 %collective-permute-start.42 = (bf16[512,2048]{1,0:T(8,128)(2,1)}, bf16[512,2048]{1,0:T(8,128)(2,1)}, u32[]{:S(2)}, u32[]{:S(2)}) collective-permute-start(bf16[512,2048]{1,0:T(8,128)(2,1)} %get-tuple-element.246), channel_id=1, source_target_pairs={{0,4},{4,0},{8,12},{12,8},{16,20},{20,16},{24,28},{28,24},{1,5},{5... | collective-permute-start | bytes 6291464 | tf_op jit(solution)/shard_map/ppermute | solution.py:33
  517.3 117.1 %reduce-scatter.14.cloned.1.call-start = ((), (), s32[]{:S(2)}) async-start(), calls=%async_computation.12 | async-start | bytes 1310720 | tf_op jit(solution)/shard_map/reduce_scatter | solution.py:877
  517.4 32.0 %collective-permute-start.41 = (bf16[704,512]{1,0:T(8,128)(2,1)}, bf16[704,512]{1,0:T(8,128)(2,1)S(1)}, u32[]{:S(2)}, u32[]{:S(2)}) collective-permute-start(bf16[704,512]{1,0:T(8,128)(2,1)} %reduce-scatter.6.cloned.1.call-done), channel_id=1, source_target_pairs={{0,16},{4,20},{8,24},{12,28},{16,0},{20,4},{24,8},{28,12},{1,17},{... | collective-permute-start | bytes 2162696 | tf_op jit(solution)/shard_map/ppermute | solution.py:33
  518.1 31.3 %collective-permute-start.40 = (bf16[704,512]{1,0:T(8,128)(2,1)}, bf16[704,512]{1,0:T(8,128)(2,1)S(1)}, u32[]{:S(2)}, u32[]{:S(2)}) collective-permute-start(bf16[704,512]{1,0:T(8,128)(2,1)} %reduce-scatter.6.cloned.1.call-done), channel_id=1, source_target_pairs={{0,8},{4,12},{8,0},{12,4},{16,24},{20,28},{24,16},{28,20},{1,9},{5... | collective-permute-start | bytes 2162696 | tf_op jit(solution)/shard_map/ppermute | solution.py:33
  521.3 26.1 %collective-permute-start.39 = (bf16[128,2048]{1,0:T(8,128)(2,1)S(1)}, bf16[128,2048]{1,0:T(8,128)(2,1)S(1)}, u32[]{:S(2)}, u32[]{:S(2)}) collective-permute-start(bf16[128,2048]{1,0:T(8,128)(2,1)S(1)} %get-tuple-element.322), channel_id=1, source_target_pairs={{0,16},{4,20},{8,24},{12,28},{16,0},{20,4},{24,8},{28,12},{1,17},{... | collective-permute-start | bytes 1572872 | tf_op jit(solution)/shard_map/ppermute | solution.py:33
  521.9 26.0 %collective-permute-start.38 = (bf16[128,2048]{1,0:T(8,128)(2,1)S(1)}, bf16[128,2048]{1,0:T(8,128)(2,1)S(1)}, u32[]{:S(2)}, u32[]{:S(2)}) collective-permute-start(bf16[128,2048]{1,0:T(8,128)(2,1)S(1)} %get-tuple-element.323), channel_id=1, source_target_pairs={{0,8},{4,12},{8,0},{12,4},{16,24},{20,28},{24,16},{28,20},{1,9},{5... | collective-permute-start | bytes 1572872 | tf_op jit(solution)/shard_map/ppermute | solution.py:33
  547.3 14.8 %collective-permute-start.37 = (bf16[128,2048]{1,0:T(8,128)(2,1)S(1)}, bf16[128,2048]{1,0:T(8,128)(2,1)S(1)}, u32[]{:S(2)}, u32[]{:S(2)}) collective-permute-start(bf16[128,2048]{1,0:T(8,128)(2,1)S(1)} %get-tuple-element.324), channel_id=1, source_target_pairs={{0,16},{4,20},{8,24},{12,28},{16,0},{20,4},{24,8},{28,12},{1,17},{... | collective-permute-start | bytes 1572872 | tf_op jit(solution)/shard_map/ppermute | solution.py:33
  548.0 14.9 %collective-permute-start.36 = (bf16[128,2048]{1,0:T(8,128)(2,1)S(1)}, bf16[128,2048]{1,0:T(8,128)(2,1)S(1)}, u32[]{:S(2)}, u32[]{:S(2)}) collective-permute-start(bf16[128,2048]{1,0:T(8,128)(2,1)S(1)} %get-tuple-element.325), channel_id=1, source_target_pairs={{0,8},{4,12},{8,0},{12,4},{16,24},{20,28},{24,16},{28,20},{1,9},{5... | collective-permute-start | bytes 1572872 | tf_op jit(solution)/shard_map/ppermute | solution.py:33
  549.5 19.4 %collective-permute-start.44 = (bf16[352,512]{1,0:T(8,128)(2,1)S(1)}, bf16[352,512]{1,0:T(8,128)(2,1)S(1)}, u32[]{:S(2)}, u32[]{:S(2)}) collective-permute-start(bf16[352,512]{1,0:T(8,128)(2,1)S(1)} %slice.138), channel_id=1, source_target_pairs={{0,8},{4,12},{8,0},{12,4},{16,24},{20,28},{24,16},{28,20},{1,9},{5... | collective-permute-start | bytes 1081352 | tf_op jit(solution)/shard_map/ppermute | solution.py:33
  550.2 18.7 %collective-permute-start.43 = (bf16[352,512]{1,0:T(8,128)(2,1)S(1)}, bf16[352,512]{1,0:T(8,128)(2,1)S(1)}, u32[]{:S(2)}, u32[]{:S(2)}) collective-permute-start(bf16[352,512]{1,0:T(8,128)(2,1)S(1)} %slice.137), channel_id=1, source_target_pairs={{0,16},{4,20},{8,24},{12,28},{16,0},{20,4},{24,8},{28,12},{1,17},{... | collective-permute-start | bytes 1081352 | tf_op jit(solution)/shard_map/ppermute | solution.py:33
  569.0 33.0 %collective-permute-start.47 = (bf16[2816,512]{1,0:T(8,128)(2,1)S(1)}, bf16[2816,512]{1,0:T(8,128)(2,1)S(1)}, u32[]{:S(2)}, u32[]{:S(2)}) collective-permute-start(bf16[2816,512]{1,0:T(8,128)(2,1)S(1)} %constant_dynamic-update-slice_fusion.23.same_ref), channel_id=1, source_target_pairs={{0,4},{4,0},{8,12},{12,8},{16,20},{20,16},{24,28},{28,24},{1,5},{5... | collective-permute-start | bytes 8650760 | tf_op jit(solution)/shard_map/ppermute | solution.py:33
  569.1 30.9 %collective-permute-start.49 = (bf16[704,512]{1,0:T(8,128)(2,1)S(1)}, bf16[704,512]{1,0:T(8,128)(2,1)S(1)}, u32[]{:S(2)}, u32[]{:S(2)}) collective-permute-start(bf16[704,512]{1,0:T(8,128)(2,1)S(1)} %copy-done.84), channel_id=1, source_target_pairs={{0,16},{4,20},{8,24},{12,28},{16,0},{20,4},{24,8},{28,12},{1,17},{... | collective-permute-start | bytes 2162696 | tf_op jit(solution)/shard_map/ppermute | solution.py:33
  570.5 30.3 %collective-permute-start.48 = (bf16[704,512]{1,0:T(8,128)(2,1)S(1)}, bf16[704,512]{1,0:T(8,128)(2,1)S(1)}, u32[]{:S(2)}, u32[]{:S(2)}) collective-permute-start(bf16[704,512]{1,0:T(8,128)(2,1)S(1)} %copy-done.84), channel_id=1, source_target_pairs={{0,8},{4,12},{8,0},{12,4},{16,24},{20,28},{24,16},{28,20},{1,9},{5... | collective-permute-start | bytes 2162696 | tf_op jit(solution)/shard_map/ppermute | solution.py:33
  572.7 27.2 %collective-permute-start.46 = (bf16[128,2048]{1,0:T(8,128)(2,1)S(1)}, bf16[128,2048]{1,0:T(8,128)(2,1)S(1)}, u32[]{:S(2)}, u32[]{:S(2)}) collective-permute-start(bf16[128,2048]{1,0:T(8,128)(2,1)S(1)} %get-tuple-element.320), channel_id=1, source_target_pairs={{0,8},{4,12},{8,0},{12,4},{16,24},{20,28},{24,16},{28,20},{1,9},{5... | collective-permute-start | bytes 1572872 | tf_op jit(solution)/shard_map/ppermute | solution.py:33
  574.3 25.6 %collective-permute-start.45 = (bf16[128,2048]{1,0:T(8,128)(2,1)S(1)}, bf16[128,2048]{1,0:T(8,128)(2,1)S(1)}, u32[]{:S(2)}, u32[]{:S(2)}) collective-permute-start(bf16[128,2048]{1,0:T(8,128)(2,1)S(1)} %get-tuple-element.321), channel_id=1, source_target_pairs={{0,16},{4,20},{8,24},{12,28},{16,0},{20,4},{24,8},{28,12},{1,17},{... | collective-permute-start | bytes 1572872 | tf_op jit(solution)/shard_map/ppermute | solution.py:33
  606.9 91.7 %all-gather.11.cloned.1.call-start = ((), (), s32[]{:S(2)}) async-start(), calls=%async_computation.13 | async-start | bytes 6488064 | tf_op jit(solution)/shard_map/all_gather | solution.py:882
  606.9 27.5 %collective-permute-start.54 = (bf16[512,768]{1,0:T(8,128)(2,1)}, bf16[512,768]{1,0:T(8,128)(2,1)}, u32[]{:S(2)}, u32[]{:S(2)}) collective-permute-start(bf16[512,768]{1,0:T(8,128)(2,1)} %reduce-scatter.12.cloned.1.call-done), channel_id=1, source_target_pairs={{0,16},{4,20},{8,24},{12,28},{16,0},{20,4},{24,8},{28,12},{1,17},{... | collective-permute-start | bytes 2359304 | tf_op jit(solution)/shard_map/ppermute | solution.py:33
  607.6 26.8 %collective-permute-start.53 = (bf16[512,768]{1,0:T(8,128)(2,1)}, bf16[512,768]{1,0:T(8,128)(2,1)}, u32[]{:S(2)}, u32[]{:S(2)}) collective-permute-start(bf16[512,768]{1,0:T(8,128)(2,1)} %reduce-scatter.12.cloned.1.call-done), channel_id=1, source_target_pairs={{0,8},{4,12},{8,0},{12,4},{16,24},{20,28},{24,16},{28,20},{1,9},{5... | collective-permute-start | bytes 2359304 | tf_op jit(solution)/shard_map/ppermute | solution.py:33
  611.1 23.3 %collective-permute-start.52 = (bf16[352,512]{1,0:T(8,128)(2,1)S(1)}, bf16[352,512]{1,0:T(8,128)(2,1)S(1)}, u32[]{:S(2)}, u32[]{:S(2)}) collective-permute-start(bf16[352,512]{1,0:T(8,128)(2,1)S(1)} %slice.142), channel_id=1, source_target_pairs={{0,8},{4,12},{8,0},{12,4},{16,24},{20,28},{24,16},{28,20},{1,9},{5... | collective-permute-start | bytes 1081352 | tf_op jit(solution)/shard_map/ppermute | solution.py:33
  611.7 22.7 %collective-permute-start.51 = (bf16[352,512]{1,0:T(8,128)(2,1)S(1)}, bf16[352,512]{1,0:T(8,128)(2,1)}, u32[]{:S(2)}, u32[]{:S(2)}) collective-permute-start(bf16[352,512]{1,0:T(8,128)(2,1)S(1)} %slice.141), channel_id=1, source_target_pairs={{0,16},{4,20},{8,24},{12,28},{16,0},{20,4},{24,8},{28,12},{1,17},{... | collective-permute-start | bytes 1081352 | tf_op jit(solution)/shard_map/ppermute | solution.py:33
  613.1 21.3 %collective-permute-start.55 = (f32[2,2048]{1,0:T(2,128)S(1)}, f32[2,2048]{1,0:T(2,128)S(1)}, u32[]{:S(2)}, u32[]{:S(2)}) collective-permute-start(f32[2,2048]{1,0:T(2,128)S(1)} %add.217), channel_id=1, source_target_pairs={{0,8},{4,12},{8,0},{12,4},{16,24},{20,28},{24,16},{28,20},{1,9},{5... | collective-permute-start | bytes 49160 | tf_op jit(solution)/shard_map/ppermute | solution.py:33
  638.0 33.4 %collective-permute-start.56 = (bf16[2816,512]{1,0:T(8,128)(2,1)S(1)}, bf16[2816,512]{1,0:T(8,128)(2,1)S(1)}, u32[]{:S(2)}, u32[]{:S(2)}) collective-permute-start(bf16[2816,512]{1,0:T(8,128)(2,1)S(1)} %constant_dynamic-update-slice_fusion.28.same_ref), channel_id=1, source_target_pairs={{0,4},{4,0},{8,12},{12,8},{16,20},{20,16},{24,28},{28,24},{1,5},{5... | collective-permute-start | bytes 8650760 | tf_op jit(solution)/shard_map/ppermute | solution.py:33
  638.1 14.3 %collective-permute-start.61 = (bf16[256,512]{1,0:T(8,128)(2,1)S(1)}, bf16[256,512]{1,0:T(8,128)(2,1)S(1)}, u32[]{:S(2)}, u32[]{:S(2)}) collective-permute-start(bf16[256,512]{1,0:T(8,128)(2,1)S(1)} %copy-done.97), channel_id=1, source_target_pairs={{0,24},{4,28},{8,16},{12,20},{16,8},{20,12},{24,0},{28,4},{1,25},{... | collective-permute-start | bytes 786440 | tf_op jit(solution)/shard_map/ppermute | solution.py:267
  643.2 28.2 %collective-permute-start.58 = (bf16[256,768]{1,0:T(8,128)(2,1)S(1)}, bf16[256,768]{1,0:T(8,128)(2,1)S(1)}, u32[]{:S(2)}, u32[]{:S(2)}) collective-permute-start(bf16[256,768]{1,0:T(8,128)(2,1)S(1)} %slice.146), channel_id=1, source_target_pairs={{0,8},{4,12},{8,0},{12,4},{16,24},{20,28},{24,16},{28,20},{1,9},{5... | collective-permute-start | bytes 1179656 | tf_op jit(solution)/shard_map/ppermute | solution.py:33
  644.0 27.5 %collective-permute-start.57 = (bf16[256,768]{1,0:T(8,128)(2,1)S(1)}, bf16[256,768]{1,0:T(8,128)(2,1)S(1)}, u32[]{:S(2)}, u32[]{:S(2)}) collective-permute-start(bf16[256,768]{1,0:T(8,128)(2,1)S(1)} %slice.145), channel_id=1, source_target_pairs={{0,16},{4,20},{8,24},{12,28},{16,0},{20,4},{24,8},{28,12},{1,17},{... | collective-permute-start | bytes 1179656 | tf_op jit(solution)/shard_map/ppermute | solution.py:33
  645.5 26.0 %collective-permute-start.60 = (bf16[256,512]{1,0:T(8,128)(2,1)S(1)}, bf16[256,512]{1,0:T(8,128)(2,1)S(1)}, u32[]{:S(2)}, u32[]{:S(2)}) collective-permute-start(bf16[256,512]{1,0:T(8,128)(2,1)S(1)} %copy-done.97), channel_id=1, source_target_pairs={{0,16},{4,20},{8,24},{12,28},{16,0},{20,4},{24,8},{28,12},{1,17},{... | collective-permute-start | bytes 786440 | tf_op jit(solution)/shard_map/ppermute | solution.py:267
  652.4 19.0 %collective-permute-start.59 = (bf16[256,512]{1,0:T(8,128)(2,1)S(1)}, bf16[256,512]{1,0:T(8,128)(2,1)S(1)}, u32[]{:S(2)}, u32[]{:S(2)}) collective-permute-start(bf16[256,512]{1,0:T(8,128)(2,1)S(1)} %copy-done.97), channel_id=1, source_target_pairs={{0,8},{4,12},{8,0},{12,4},{16,24},{20,28},{24,16},{28,20},{1,9},{5... | collective-permute-start | bytes 786440 | tf_op jit(solution)/shard_map/ppermute | solution.py:267
  (127 other events, 1187.1 us)
Sparse Core Ops, SparseCore 0:
  96.3 28.0 all-gather.4
  126.5 106.1 all-gather.6
  234.9 57.4 all-gather.8
  323.6 54.9 reduce-scatter.5
  390.1 54.1 reduce-scatter.7
  447.0 56.0 reduce-scatter.9
  517.4 58.1 reduce-scatter.11
  607.0 24.9 reduce-scatter.13
  634.6 52.5 all-gather.10

commit v13 on v12

--- a/solution.py
+++ b/solution.py
@@ -506,11 +506,11 @@
             def _(t):
                 cols = pl.ds(pl.multiple_of(n * half + t * step, step), step)
                 rows = pl.ds(pl.multiple_of(t * step, step), step)
-                ref[rows, :] = mm_tn(x_ref[:, cols], kept_ref[...]).astype(BF)
-
-
-def attend_back(grad, out_w, qkv, lse, both, tables, seg):
-    rows, depth = both.shape
+                ref[rows, :] = mm(x_ref[cols, :], kept_ref[...]).astype(BF)
+
+
+def attend_back(grad, out_w, qkv, lse, turned, tables, seg):
+    depth, rows = turned.shape
     length = tables[0].shape[0]
     wide = qkv.shape[1]
     width = wide // 3
@@ -521,7 +521,7 @@
         grid=(rows // length,),
         in_specs=[whole(length, depth)] * 2
         + [whole(width, depth), by_seq(wide), by_seq(width // HD)]
-        + [whole(rows, depth), whole(length, HD), whole(length, HD)]
+        + [whole(depth, rows), whole(length, HD), whole(length, HD)]
         + [
             pl.BlockSpec((1, length, 1), lambda s: (s, 0, 0)),
             pl.BlockSpec((1, 1, length), lambda s: (s, 0, 0)),
@@ -545,7 +545,7 @@
             transcendentals=rows * 2 * WIN * width // HD,
         ),
         name="attend_back",
-    )(*grad, out_w, qkv, lse, both, *tables, *seg)
+    )(*grad, out_w, qkv, lse, turned, *tables, *seg)
 
 
 def normed_back_kernel(blocks, parts, z_ref, *refs):
@@ -689,6 +689,44 @@
         ),
         name="place_turned",
     )(me, same, other)
+
+
+def turn_kernel(in_ref, out_ref):
+    out_ref[...] = in_ref[...].T
+
+
+def turn(value):
+    rows, width = value.shape
+    tile = min(width, 512)
+    return pl.pallas_call(
+        turn_kernel,
+        grid=(width // tile,),
+        in_specs=[pl.BlockSpec((rows, tile), lambda i: (0, i))],
+        out_specs=pl.BlockSpec((tile, rows), lambda i: (i, 0)),
+        out_shape=jax.ShapeDtypeStruct((width, rows), value.dtype),
+        cost_estimate=pl.CostEstimate(flops=0, bytes_accessed=4 * value.size, transcendentals=0),
+        name="turn",
+    )(value)
+
+
+def widen_kernel(in_ref, out_ref):
+    out_ref[...] = in_ref[...].astype(F32)
+
+
+def widen(value):
+    rows, width = value.shape
+    tile = rows // 4
+    spec = pl.BlockSpec((tile, width), lambda i: (i, 0))
+    return pl.pallas_call(
+        widen_kernel,
+        grid=(4,),
+        in_specs=[spec],
+        out_specs=spec,
+        out_shape=jax.ShapeDtypeStruct(value.shape, F32),
+        compiler_params=pltpu.CompilerParams(vmem_limit_bytes=32 << 20),
+        cost_estimate=pl.CostEstimate(flops=0, bytes_accessed=6 * value.size, transcendentals=0),
+        name="widen",
+    )(value)
 
 
 def per_device(
@@ -765,7 +803,7 @@
         context[d], *saved[d] = attend(shard, both, qkv_w[d], tables, seg)
         return context[d]
 
-    context[0], own_out = stage(flows, (run(0), own_out))
+    context[0], own_out, turned = stage(flows, (run(0), own_out, turn(both)))
     gate_up = lax.all_gather(own_gate_up, "shard", axis=0, tiled=True)
     down = lax.all_gather(own_down, "shard", axis=1, tiled=True)
     early = offsets[1:2] if staged else []
@@ -820,7 +858,7 @@
     def run_back(*ds):
         for d in ds:
             lins[d], *grad_qkv_w[d] = attend_back(
-                both_grad, out_w[d], *saved[d], both, tables, seg
+                both_grad, out_w[d], *saved[d], turned, tables, seg
             )
         return [(lins[d], grad_qkv_w[d]) for d in ds]
 
@@ -886,7 +924,7 @@
     grad_up = stage([qkv_flow, out_flow, gain_flow], grad_up)
     grad_query, grad_key, grad_value = place(whoami, *finish(qkv_flow), own, block, True)
     (grad_out,) = place(whoami, *finish(out_flow), block, own, False)
-    grad_down = all_down.astype(F32)
+    grad_down = widen(all_down)
     gain_grads = finish(gain_flow)
     return (
         output,

time: 721 us -> 733 us (1.017)
  Pallas kernels: 239 us -> 258 us
    pallas_call x4, Pallas kernels: 42.5 us -> 54 us  [attend(): pl.pallas_call(functools.partial(attend_kernel, parts), grid_spec=pltpu.P...]
    pallas_call x0 -> x2, Pallas kernels: none -> 10 us  [the longest x1 5.49 us: turn(): pl.pallas_call(turn_kernel, grid=(width // tile,), in_specs=[pl.BlockSpec...]
    convert_element_type x1 -> x0, other arithmetic: 8.87 us -> none  [per_device(): grad_down = all_down.astype(F32)]
    unnamed x259 -> x255, local copies, waits for them, and re-layouts: 58.1 us -> 61.2 us
  transfers between devices with their start and end apart: 77 -> 77, of which waited for: 20 -> 19; matrix products, arithmetic and copies ran while one was open for 20% -> 21% of each run, Pallas kernels for 33% -> 35%
where the time goes in v13:
time: 733 us; the launch traced here: 726 us
  Pallas kernels  258 us (35%)
  waiting for transfers between devices  166 us (23%)
  local copies, waits for them, and re-layouts  95.5 us (13%)
  matrix products  71.8 us (10%)
  starting transfers between devices  66.3 us (9%)
  other arithmetic  52.1 us (7%)
  between operations  15.8 us (2%)
    ppermute x53, waiting for transfers between devices, swap(): return lax.ppermute(value, 'rep', [(i, i ^ bit) for i in range(size)])  110 us
    pallas_call x4, Pallas kernels, attend_back(): pl.pallas_call(attend_back_kernel, grid=(rows // length,), in_specs=[whol...  69.3 us
    unnamed x255, local copies, waits for them, and re-layouts  61.2 us
    pallas_call x2, Pallas kernels, gather_rows(): pl.pallas_call(functools.partial(gather_kernel, peers()), out_shape=jax.S...  58.2 us
    pallas_call x4, Pallas kernels, attend(): pl.pallas_call(functools.partial(attend_kernel, parts), grid_spec=pltpu.P...  54 us
    ppermute x53, starting transfers between devices, swap(): return lax.ppermute(value, 'rep', [(i, i ^ bit) for i in range(size)])  46.1 us
    dot_general x6, matrix products, mm_tn(): lax.dot_general(left, right, (((0,), (0,)), ((), ())), preferred_element_...  27 us
    dot_general x5, matrix products, mm(): return jnp.dot(left, right, preferred_element_type=F32)  24.6 us
  transfers between devices with their start and end apart: 77, of which 19 were waited for; matrix products, arithmetic and copies ran while one was open for 21% of the time, Pallas kernels for 35%

profile of v13, /device:TPU:0, one launch (start us, length us, event | category | flops | bytes accessed | tf_op | source)
XLA Modules:
  0.0 725.8 jit_solution(4214818208766397922)
XLA Ops:
  8.8 3.1 collective-permute-start.2
  11.8 2.6 collective-permute-start.1
  17.8 2.7 constant_dynamic-slice_fusion.4
  21.2 2.3 constant_dynamic-slice_fusion.15
  26.2 16.2 %collective-permute-done.3.refs_5_ = bf16[512,768]{1,0:T(8,128)(2,1)} collective-permute-done((bf16[512,768]{1,0:T(8,128)(2,1)S(1)}, bf16[512,768]{1,0:T(8,128)(2,1)}, u32[]{:S(2)}, u32[]{:S(2)}) %collective-permute-start.3) | collective-permute-done | bytes 786464 | tf_op jit(solution)/shard_map/ppermute | solution.py:781
  48.0 18.9 %collective-permute-done.7.refs_6_ = bf16[512,768]{1,0:T(8,128)(2,1)} collective-permute-done((bf16[512,768]{1,0:T(8,128)(2,1)}, bf16[512,768]{1,0:T(8,128)(2,1)}, u32[]{:S(2)}, u32[]{:S(2)}) %collective-permute-start.7) | collective-permute-done | bytes 786464 | tf_op jit(solution)/shard_map/ppermute | solution.py:795
  75.4 20.7 %collective-permute-done.10 = bf16[256,768]{1,0:T(8,128)(2,1)} collective-permute-done((bf16[256,768]{1,0:T(8,128)(2,1)}, bf16[256,768]{1,0:T(8,128)(2,1)}, u32[]{:S(2)}, u32[]{:S(2)}) %collective-permute-start.10) | collective-permute-done | bytes 393248 | tf_op jit(solution)/shard_map/ppermute | solution.py:33
  99.4 2.1 pad_maximum_fusion.6.refs_4_.refs_8_
  111.5 4.2 pad_maximum_fusion.refs_0_.refs_1_.refs_2_.refs_3_.in_ref
  117.6 5.5 turn.1.x_ref
  123.1 2.2 copy-done.2
  125.3 10.8 %attend.4 = (bf16[1024,256]{1,0:T(8,128)(2,1)S(1)}, bf16[1024,768]{1,0:T(8,128)(2,1)S(1)}, f32[1024,2]{1,0:T(8,128)S(1)}) custom-call(s32[1]{0:T(128)} %bitcast.1.z_ref, bf16[1024,2048]{1,0:T(8,128)(2,1)S(1)} %copy-done.2, bf16[1024,2048]{1,0:T(8,128)(2,1)S(1)} %copy-done.2, bf16[1024,2048]{1,0:T(8,128)(2,1)S(1)} %copy-done.2, ...), custom_call_target="tpu_custom_call" | custom-call | flops 3758096384 | bytes 10485760 | tf_op jit(solution)/shard_map/attend/pallas_call | solution.py:423
  146.2 2.2 copy-done.3
  150.7 10.7 %attend.5 = (bf16[1024,256]{1,0:T(8,128)(2,1)S(1)}, bf16[1024,768]{1,0:T(8,128)(2,1)S(1)}, f32[1024,2]{1,0:T(8,128)S(1)}) custom-call(s32[1]{0:T(128)} %bitcast.1.z_ref, bf16[1024,2048]{1,0:T(8,128)(2,1)S(1)} %copy-done.3, bf16[1024,2048]{1,0:T(8,128)(2,1)S(1)} %copy-done.3, bf16[1024,2048]{1,0:T(8,128)(2,1)S(1)} %copy-done.3, ...), custom_call_target="tpu_custom_call" | custom-call | flops 3758096384 | bytes 10485760 | tf_op jit(solution)/shard_map/attend/pallas_call | solution.py:423
  163.4 10.8 %attend.6 = (bf16[1024,256]{1,0:T(8,128)(2,1)S(1)}, bf16[1024,768]{1,0:T(8,128)(2,1)S(1)}, f32[1024,2]{1,0:T(8,128)S(1)}) custom-call(s32[1]{0:T(128)} %bitcast.1.z_ref, bf16[1024,2048]{1,0:T(8,128)(2,1)S(1)} %copy-done.3, bf16[1024,2048]{1,0:T(8,128)(2,1)S(1)} %copy-done.3, bf16[1024,2048]{1,0:T(8,128)(2,1)S(1)} %copy-done.3, ...), custom_call_target="tpu_custom_call" | custom-call | flops 3758096384 | bytes 10485760 | tf_op jit(solution)/shard_map/attend/pallas_call | solution.py:423
  176.8 21.7 %attend.7 = (bf16[1024,256]{1,0:T(8,128)(2,1)S(1)}, bf16[1024,768]{1,0:T(8,128)(2,1)S(1)}, f32[1024,2]{1,0:T(8,128)S(1)}) custom-call(s32[1]{0:T(128)} %bitcast.1.z_ref, bf16[1024,2048]{1,0:T(8,128)(2,1)S(1)} %copy-done.3, bf16[1024,2048]{1,0:T(8,128)(2,1)S(1)} %copy-done.3, bf16[1024,2048]{1,0:T(8,128)(2,1)S(1)} %copy-done.3, ...), custom_call_target="tpu_custom_call" | custom-call | flops 3758096384 | bytes 10485760 | tf_op jit(solution)/shard_map/attend/pallas_call | solution.py:423
  202.4 6.4 collective-permute-done.22
  210.5 6.3 fusion.53
  216.8 3.4 copy-done.67
  222.4 2.2 fusion.22.in_ref
  226.4 4.0 multiply_reduce_fusion.2
  233.1 29.0 %gather_rows.2 = bf16[1024,2048]{1,0:T(8,128)(2,1)S(1)} custom-call(bf16[128,2048]{1,0:T(8,128)(2,1)S(1)} %convolution_convert_fusion.5.in_ref), custom_call_target="tpu_custom_call" | custom-call | bytes 62914560 | tf_op jit(solution)/shard_map/gather_rows/pallas_call | solution.py:153
  264.2 11.7 %fusion.54 = f32[1024,1408]{1,0:T(8,128)} fusion(bf16[1024,2048]{1,0:T(8,128)(2,1)} %copy-done.9, bf16[2048,1408]{1,0:T(8,128)(2,1)} %all-gather.7.cloned.1.call-done), kind=kOutput, calls=%fused_computation.179 | convolution fusion | flops 5905580032 | bytes 15728640 | tf_op jit(solution)/shard_map/dot_general | solution.py:20
  275.9 29.1 %gather_rows.3 = bf16[1024,2048]{1,0:T(8,128)(2,1)S(1)} custom-call(bf16[128,2048]{1,0:T(8,128)(2,1)S(1)} %fusion.22.in_ref), custom_call_target="tpu_custom_call" | custom-call | bytes 62914560 | tf_op jit(solution)/shard_map/gather_rows/pallas_call | solution.py:153
  307.1 9.1 %multiply_convert_fusion.2 = (bf16[1024,704]{1,0:T(8,128)(2,1)S(1)}, bf16[1024,704]{1,0:T(8,128)(2,1)S(1)}, bf16[1024,704]{1,0:T(8,128)(2,1)S(1)}) fusion(f32[1024,1408]{1,0:T(8,128)} %fusion.54, bf16[1024,2048]{1,0:T(8,128)(2,1)} %copy-done.7, bf16[704,2048]{1,0:T(8,128)(2,1)} %all-gather.9.cloned.1.call-done), kind=kOutput, calls=%fused_computation.44 | convolution fusion | flops 2963603456 | bytes 17170432 | tf_op jit(solution)/shard_map/dot_general | solution.py:24
  316.2 3.6 convolution_convert_fusion.1
  322.5 11.1 %convolution_convert_fusion.in_ref = bf16[1024,2048]{1,0:T(8,128)(2,1)} fusion(bf16[2048,1408]{1,0:T(8,128)(2,1)} %all-gather.7.cloned.1.call-done, bf16[1024,704]{1,0:T(8,128)(2,1)S(1)} %get-tuple-element.205, bf16[1024,704]{1,0:T(8,128)(2,1)S(1)} %get-tuple-element.318), kind=kOutput, calls=%fused_computation.34 | convolution fusion | flops 5913444352 | bytes 12845056 | tf_op jit(solution)/shard_map/dot_general | solution.py:24
  333.6 4.5 convolution_convert_fusion.4
  338.6 2.2 copy-done.12
  340.8 23.0 %reduce_rows.1 = bf16[128,2048]{1,0:T(8,128)(2,1)S(1)} custom-call(bf16[1024,2048]{1,0:T(8,128)(2,1)S(1)} %copy-done.12), custom_call_target="tpu_custom_call" | custom-call | bytes 62914560 | tf_op jit(solution)/shard_map/reduce_rows/pallas_call | solution.py:243
  365.4 3.2 multiply_convert_fusion
  369.4 2.5 add_convert_fusion.1
  377.8 17.1 %attend_back.4 = (bf16[1024,768]{1,0:T(8,128)(2,1)S(1)}, bf16[1024,768]{1,0:T(8,128)(2,1)S(1)}, bf16[1024,768]{1,0:T(8,128)(2,1)}) custom-call(bf16[512,2048]{1,0:T(8,128)(2,1)} %copy-done.70, bf16[512,2048]{1,0:T(8,128)(2,1)} %copy-done.107, bf16[256,2048]{1,0:T(8,128)(2,1)S(1)} %pad_maximum_fusion.3.out_ref, bf16[1024,768]{1,0:T(8,128)(2,1)} %copy-done.42, ...), custom_call_target="tpu_custom_call" | custom-call | flops 5637144576 | bytes 15728640 | tf_op jit(solution)/shard_map/attend_back/pallas_call | solution.py:519
  400.0 4.5 convolution_convert_fusion.3
  408.0 17.7 %attend_back.6 = (bf16[1024,768]{1,0:T(8,128)(2,1)S(1)}, bf16[1024,768]{1,0:T(8,128)(2,1)S(1)}, bf16[1024,768]{1,0:T(8,128)(2,1)}) custom-call(bf16[512,2048]{1,0:T(8,128)(2,1)} %copy-done.70, bf16[512,2048]{1,0:T(8,128)(2,1)} %copy-done.107, bf16[256,2048]{1,0:T(8,128)(2,1)S(1)} %copy-done.24, bf16[1024,768]{1,0:T(8,128)(2,1)} %copy-done.41, ...), custom_call_target="tpu_custom_call" | custom-call | flops 5637144576 | bytes 15728640 | tf_op jit(solution)/shard_map/attend_back/pallas_call | solution.py:519
  428.6 17.2 %attend_back.5 = (bf16[1024,768]{1,0:T(8,128)(2,1)S(1)}, bf16[1024,768]{1,0:T(8,128)(2,1)S(1)}, bf16[1024,768]{1,0:T(8,128)(2,1)}) custom-call(bf16[512,2048]{1,0:T(8,128)(2,1)} %copy-done.70, bf16[512,2048]{1,0:T(8,128)(2,1)} %copy-done.107, bf16[256,2048]{1,0:T(8,128)(2,1)S(1)} %copy-done.22, bf16[1024,768]{1,0:T(8,128)(2,1)} %copy-done.40, ...), custom_call_target="tpu_custom_call" | custom-call | flops 5637144576 | bytes 15728640 | tf_op jit(solution)/shard_map/attend_back/pallas_call | solution.py:519
  448.2 4.6 convolution_convert_fusion.2
  454.2 3.4 add_convert_fusion.4
  459.1 3.4 add_convert_fusion.5
  463.8 17.3 %attend_back.7 = (bf16[1024,768]{1,0:T(8,128)(2,1)S(1)}, bf16[1024,768]{1,0:T(8,128)(2,1)S(1)}, bf16[1024,768]{1,0:T(8,128)(2,1)}) custom-call(bf16[512,2048]{1,0:T(8,128)(2,1)} %copy-done.70, bf16[512,2048]{1,0:T(8,128)(2,1)} %copy-done.107, bf16[256,2048]{1,0:T(8,128)(2,1)S(1)} %copy-done.38, bf16[1024,768]{1,0:T(8,128)(2,1)} %copy-done.39, ...), custom_call_target="tpu_custom_call" | custom-call | flops 5637144576 | bytes 15728640 | tf_op jit(solution)/shard_map/attend_back/pallas_call | solution.py:519
  481.1 10.0 %fusion.15 = bf16[1024,2048]{1,0:T(8,128)(2,1)} fusion(bf16[1024,1024]{1,0:T(8,128)(2,1)} %constant_dynamic-update-slice_fusion.14, bf16[512,2048]{1,0:T(8,128)(2,1)} %copy-done.107, bf16[512,2048]{1,0:T(8,128)(2,1)S(1)} %copy-done.71), kind=kOutput, calls=%fused_computation.33 | convolution fusion | flops 4305453056 | bytes 10485760 | tf_op jit(solution)/shard_map/dot_general | solution.py:28
  491.2 2.2 add_convert_fusion
  493.4 23.3 %normed_back.1 = (f32[512,2048]{1,0:T(8,128)}, bf16[512,2048]{1,0:T(8,128)(2,1)}) custom-call(s32[1]{0:T(128)} %bitcast.1.z_ref, bf16[1024,768]{1,0:T(8,128)(2,1)} %copy-done.54, bf16[1024,768]{1,0:T(8,128)(2,1)} %copy-done.53, bf16[1024,768]{1,0:T(8,128)(2,1)} %copy-done.52, bf16[1024,768]{1,0:T(8,128)(2,1)} %copy-done.51, ...), custom_call_target="tpu_custom_call" | custom-call | flops 12884901888 | bytes 27262976 | tf_op jit(solution)/shard_map/normed_back/pallas_call | solution.py:576
  516.7 5.7 collective-permute-done.35
  522.8 2.6 add_convert_fusion.2
  525.4 2.5 add_convert_fusion.3
  537.1 22.7 %collective-permute-done.39 = bf16[128,2048]{1,0:T(8,128)(2,1)S(1)} collective-permute-done((bf16[128,2048]{1,0:T(8,128)(2,1)S(1)}, bf16[128,2048]{1,0:T(8,128)(2,1)S(1)}, u32[]{:S(2)}, u32[]{:S(2)}) %collective-permute-start.39) | collective-permute-done | bytes 524320 | tf_op jit(solution)/shard_map/ppermute | solution.py:33
  564.0 3.1 fusion.9
  567.2 3.9 fusion.6
  571.2 3.4 collective-permute-done.37
  575.6 6.1 collective-permute-done.44
  588.2 24.2 %collective-permute-done.46 = bf16[128,2048]{1,0:T(8,128)(2,1)S(1)} collective-permute-done((bf16[128,2048]{1,0:T(8,128)(2,1)S(1)}, bf16[128,2048]{1,0:T(8,128)(2,1)S(1)}, u32[]{:S(2)}, u32[]{:S(2)}) %collective-permute-start.46) | collective-permute-done | bytes 524320 | tf_op jit(solution)/shard_map/ppermute | solution.py:33
  616.1 2.2 add_convert_fusion.7
  628.8 5.0 place_turned.2
  633.8 13.4 %collective-permute-done.55 = f32[2,2048]{1,0:T(2,128)S(1)} collective-permute-done((f32[2,2048]{1,0:T(2,128)S(1)}, f32[2,2048]{1,0:T(2,128)S(1)}, u32[]{:S(2)}, u32[]{:S(2)}) %collective-permute-start.55) | collective-permute-done | bytes 16416 | tf_op jit(solution)/shard_map/ppermute | solution.py:33
  657.8 2.2 collective-permute-done.62
  660.6 2.8 collective-permute-done.61
  667.4 15.3 %collective-permute-done.60 = bf16[256,512]{1,0:T(8,128)(2,1)S(1)} collective-permute-done((bf16[256,512]{1,0:T(8,128)(2,1)S(1)}, bf16[256,512]{1,0:T(8,128)(2,1)S(1)}, u32[]{:S(2)}, u32[]{:S(2)}) %collective-permute-start.60) | collective-permute-done | bytes 262176 | tf_op jit(solution)/shard_map/ppermute | solution.py:267
  687.8 3.2 collective-permute-start.67
  695.5 5.0 place_turned.3
  700.5 4.3 place.3
  704.7 6.3 place.2
  711.7 2.6 copy-done.4
  714.3 4.5 widen.1
  (469 shorter events, 160.2 us)
Async XLA Ops:
  7.2 130.9 %all-gather.5.cloned.1.call-start = ((), (), s32[]{:S(2)}) async-start(), calls=%async_computation.5 | async-start | bytes 1310720 | tf_op jit(solution)/shard_map/all_gather | solution.py:799
  8.8 17.5 %collective-permute-start.2 = (bf16[2,512]{1,0:T(2,128)(2,1)S(1)}, bf16[2,512]{1,0:T(2,128)(2,1)S(1)}, u32[]{:S(2)}, u32[]{:S(2)}) collective-permute-start(bf16[2,512]{1,0:T(2,128)(2,1)S(1)} %get-tuple-element.314), channel_id=1, source_target_pairs={{0,1},{1,2},{2,3},{3,0},{4,5},{5,6},{6,7},{7,4},{8,9},{9,10},{10,1... | collective-permute-start | bytes 6152 | tf_op jit(solution)/shard_map/ppermute | solution.py:344
  11.8 14.4 %collective-permute-start.1 = (bf16[2,512]{1,0:T(2,128)(2,1)S(1)}, bf16[2,512]{1,0:T(2,128)(2,1)S(1)}, u32[]{:S(2)}, u32[]{:S(2)}) collective-permute-start(bf16[2,512]{1,0:T(2,128)(2,1)S(1)} %get-tuple-element.314), channel_id=1, source_target_pairs={{0,2},{1,3},{2,0},{3,1},{4,6},{5,7},{6,4},{7,5},{8,10},{9,11},{10,... | collective-permute-start | bytes 6152 | tf_op jit(solution)/shard_map/ppermute | solution.py:344
  20.5 21.9 %collective-permute-start.3 = (bf16[512,768]{1,0:T(8,128)(2,1)S(1)}, bf16[512,768]{1,0:T(8,128)(2,1)}, u32[]{:S(2)}, u32[]{:S(2)}) collective-permute-start(bf16[512,768]{1,0:T(8,128)(2,1)S(1)} %pad_maximum_fusion.5.refs_4_), channel_id=1, source_target_pairs={{0,1},{1,2},{2,3},{3,0},{4,5},{5,6},{6,7},{7,4},{8,9},{9,10},{10,1... | collective-permute-start | bytes 2359304 | tf_op jit(solution)/shard_map/ppermute | solution.py:781
  44.7 22.2 %collective-permute-start.8 = (bf16[512,2048]{1,0:T(8,128)(2,1)S(1)}, bf16[512,2048]{1,0:T(8,128)(2,1)S(1)}, u32[]{:S(2)}, u32[]{:S(2)}) collective-permute-start(bf16[512,2048]{1,0:T(8,128)(2,1)S(1)} %fusion.2), channel_id=1, source_target_pairs={{0,4},{4,0},{8,12},{12,8},{16,20},{20,16},{24,28},{28,24},{1,5},{5... | collective-permute-start | bytes 6291464 | tf_op jit(solution)/shard_map/ppermute | solution.py:33
  44.8 22.1 %collective-permute-start.7 = (bf16[512,768]{1,0:T(8,128)(2,1)}, bf16[512,768]{1,0:T(8,128)(2,1)}, u32[]{:S(2)}, u32[]{:S(2)}) collective-permute-start(bf16[512,768]{1,0:T(8,128)(2,1)} %collective-permute-done.3.refs_5_), channel_id=1, source_target_pairs={{0,1},{1,2},{2,3},{3,0},{4,5},{5,6},{6,7},{7,4},{8,9},{9,10},{10,1... | collective-permute-start | bytes 2359304 | tf_op jit(solution)/shard_map/ppermute | solution.py:795
  44.9 22.0 %collective-permute-start.6 = (bf16[512,768]{1,0:T(8,128)(2,1)}, bf16[512,768]{1,0:T(8,128)(2,1)S(1)}, u32[]{:S(2)}, u32[]{:S(2)}) collective-permute-start(bf16[512,768]{1,0:T(8,128)(2,1)} %collective-permute-done.3.refs_5_), channel_id=1, source_target_pairs={{0,16},{4,20},{8,24},{12,28},{16,0},{20,4},{24,8},{28,12},{1,17},{... | collective-permute-start | bytes 2359304 | tf_op jit(solution)/shard_map/ppermute | solution.py:33
  46.5 20.4 %collective-permute-start.5 = (bf16[512,768]{1,0:T(8,128)(2,1)}, bf16[512,768]{1,0:T(8,128)(2,1)S(1)}, u32[]{:S(2)}, u32[]{:S(2)}) collective-permute-start(bf16[512,768]{1,0:T(8,128)(2,1)} %collective-permute-done.3.refs_5_), channel_id=1, source_target_pairs={{0,8},{4,12},{8,0},{12,4},{16,24},{20,28},{24,16},{28,20},{1,9},{5... | collective-permute-start | bytes 2359304 | tf_op jit(solution)/shard_map/ppermute | solution.py:33
  66.9 29.2 %collective-permute-start.13 = (bf16[512,768]{1,0:T(8,128)(2,1)}, bf16[512,768]{1,0:T(8,128)(2,1)}, u32[]{:S(2)}, u32[]{:S(2)}) collective-permute-start(bf16[512,768]{1,0:T(8,128)(2,1)} %collective-permute-done.7.refs_6_), channel_id=1, source_target_pairs={{0,1},{1,2},{2,3},{3,0},{4,5},{5,6},{6,7},{7,4},{8,9},{9,10},{10,1... | collective-permute-start | bytes 2359304 | tf_op jit(solution)/shard_map/ppermute | solution.py:795
  67.0 29.2 %collective-permute-start.12 = (bf16[512,768]{1,0:T(8,128)(2,1)}, bf16[512,768]{1,0:T(8,128)(2,1)}, u32[]{:S(2)}, u32[]{:S(2)}) collective-permute-start(bf16[512,768]{1,0:T(8,128)(2,1)} %collective-permute-done.7.refs_6_), channel_id=1, source_target_pairs={{0,16},{4,20},{8,24},{12,28},{16,0},{20,4},{24,8},{28,12},{1,17},{... | collective-permute-start | bytes 2359304 | tf_op jit(solution)/shard_map/ppermute | solution.py:33
  68.6 27.6 %collective-permute-start.11 = (bf16[512,768]{1,0:T(8,128)(2,1)}, bf16[512,768]{1,0:T(8,128)(2,1)}, u32[]{:S(2)}, u32[]{:S(2)}) collective-permute-start(bf16[512,768]{1,0:T(8,128)(2,1)} %collective-permute-done.7.refs_6_), channel_id=1, source_target_pairs={{0,8},{4,12},{8,0},{12,4},{16,24},{20,28},{24,16},{28,20},{1,9},{5... | collective-permute-start | bytes 2359304 | tf_op jit(solution)/shard_map/ppermute | solution.py:33
  71.6 24.5 %collective-permute-start.10 = (bf16[256,768]{1,0:T(8,128)(2,1)}, bf16[256,768]{1,0:T(8,128)(2,1)}, u32[]{:S(2)}, u32[]{:S(2)}) collective-permute-start(bf16[256,768]{1,0:T(8,128)(2,1)} %slice.116), channel_id=1, source_target_pairs={{0,8},{4,12},{8,0},{12,4},{16,24},{20,28},{24,16},{28,20},{1,9},{5... | collective-permute-start | bytes 1179656 | tf_op jit(solution)/shard_map/ppermute | solution.py:33
  72.1 24.0 %collective-permute-start.9 = (bf16[256,768]{1,0:T(8,128)(2,1)}, bf16[256,768]{1,0:T(8,128)(2,1)}, u32[]{:S(2)}, u32[]{:S(2)}) collective-permute-start(bf16[256,768]{1,0:T(8,128)(2,1)} %slice.115), channel_id=1, source_target_pairs={{0,16},{4,20},{8,24},{12,28},{16,0},{20,4},{24,8},{28,12},{1,17},{... | collective-permute-start | bytes 1179656 | tf_op jit(solution)/shard_map/ppermute | solution.py:33
  96.2 168.0 %all-gather.7.cloned.1.call-start = ((), (), s32[]{:S(2)}) async-start(), calls=%async_computation.6 | async-start | bytes 7208960 | tf_op jit(solution)/shard_map/all_gather | solution.py:807
  96.9 210.1 %all-gather.9.cloned.1.call-start = ((), (), s32[]{:S(2)}) async-start(), calls=%async_computation.7 | async-start | bytes 3604480 | tf_op jit(solution)/shard_map/all_gather | solution.py:808
  102.8 35.3 %collective-permute-start.17 = (bf16[512,768]{1,0:T(8,128)(2,1)}, bf16[512,768]{1,0:T(8,128)(2,1)}, u32[]{:S(2)}, u32[]{:S(2)}) collective-permute-start(bf16[512,768]{1,0:T(8,128)(2,1)} %collective-permute-done.13.refs_7_), channel_id=1, source_target_pairs={{0,16},{4,20},{8,24},{12,28},{16,0},{20,4},{24,8},{28,12},{1,17},{... | collective-permute-start | bytes 2359304 | tf_op jit(solution)/shard_map/ppermute | solution.py:33
  103.4 34.7 %collective-permute-start.16 = (bf16[512,768]{1,0:T(8,128)(2,1)}, bf16[512,768]{1,0:T(8,128)(2,1)}, u32[]{:S(2)}, u32[]{:S(2)}) collective-permute-start(bf16[512,768]{1,0:T(8,128)(2,1)} %collective-permute-done.13.refs_7_), channel_id=1, source_target_pairs={{0,8},{4,12},{8,0},{12,4},{16,24},{20,28},{24,16},{28,20},{1,9},{5... | collective-permute-start | bytes 2359304 | tf_op jit(solution)/shard_map/ppermute | solution.py:33
  108.4 29.7 %collective-permute-start.15 = (bf16[256,768]{1,0:T(8,128)(2,1)}, bf16[256,768]{1,0:T(8,128)(2,1)}, u32[]{:S(2)}, u32[]{:S(2)}) collective-permute-start(bf16[256,768]{1,0:T(8,128)(2,1)} %slice.118), channel_id=1, source_target_pairs={{0,8},{4,12},{8,0},{12,4},{16,24},{20,28},{24,16},{28,20},{1,9},{5... | collective-permute-start | bytes 1179656 | tf_op jit(solution)/shard_map/ppermute | solution.py:33
  108.9 29.2 %collective-permute-start.14 = (bf16[256,768]{1,0:T(8,128)(2,1)}, bf16[256,768]{1,0:T(8,128)(2,1)}, u32[]{:S(2)}, u32[]{:S(2)}) collective-permute-start(bf16[256,768]{1,0:T(8,128)(2,1)} %slice.117), channel_id=1, source_target_pairs={{0,16},{4,20},{8,24},{12,28},{16,0},{20,4},{24,8},{28,12},{1,17},{... | collective-permute-start | bytes 1179656 | tf_op jit(solution)/shard_map/ppermute | solution.py:33
  138.1 60.4 %collective-permute-start.21 = (bf16[256,2048]{1,0:T(8,128)(2,1)}, bf16[256,2048]{1,0:T(8,128)(2,1)S(1)}, u32[]{:S(2)}, u32[]{:S(2)}) collective-permute-start(bf16[256,2048]{1,0:T(8,128)(2,1)} %all-gather.5.cloned.1.call-done.out_ref), channel_id=1, source_target_pairs={{0,16},{4,20},{8,24},{12,28},{16,0},{20,4},{24,8},{28,12},{1,17},{... | collective-permute-start | bytes 3145736 | tf_op jit(solution)/shard_map/ppermute | solution.py:33
  138.7 59.8 %collective-permute-start.20 = (bf16[256,2048]{1,0:T(8,128)(2,1)}, bf16[256,2048]{1,0:T(8,128)(2,1)S(1)}, u32[]{:S(2)}, u32[]{:S(2)}) collective-permute-start(bf16[256,2048]{1,0:T(8,128)(2,1)} %all-gather.5.cloned.1.call-done.out_ref), channel_id=1, source_target_pairs={{0,8},{4,12},{8,0},{12,4},{16,24},{20,28},{24,16},{28,20},{1,9},{5... | collective-permute-start | bytes 3145736 | tf_op jit(solution)/shard_map/ppermute | solution.py:33
  142.3 34.4 %collective-permute-start.19 = (bf16[256,768]{1,0:T(8,128)(2,1)S(1)}, bf16[256,768]{1,0:T(8,128)(2,1)S(1)}, u32[]{:S(2)}, u32[]{:S(2)}) collective-permute-start(bf16[256,768]{1,0:T(8,128)(2,1)S(1)} %slice.120), channel_id=1, source_target_pairs={{0,8},{4,12},{8,0},{12,4},{16,24},{20,28},{24,16},{28,20},{1,9},{5... | collective-permute-start | bytes 1179656 | tf_op jit(solution)/shard_map/ppermute | solution.py:33
  142.9 33.8 %collective-permute-start.18 = (bf16[256,768]{1,0:T(8,128)(2,1)S(1)}, bf16[256,768]{1,0:T(8,128)(2,1)S(1)}, u32[]{:S(2)}, u32[]{:S(2)}) collective-permute-start(bf16[256,768]{1,0:T(8,128)(2,1)S(1)} %slice.119), channel_id=1, source_target_pairs={{0,16},{4,20},{8,24},{12,28},{16,0},{20,4},{24,8},{28,12},{1,17},{... | collective-permute-start | bytes 1179656 | tf_op jit(solution)/shard_map/ppermute | solution.py:33
  221.9 294.8 %reduce-scatter.6.cloned.1.call-start = ((), (), s32[]{:S(2)}) async-start(), calls=%async_computation.8 | async-start | bytes 3604480 | tf_op jit(solution)/shard_map/reduce_scatter | solution.py:884
  321.6 42.1 %collective-permute-start.25 = (bf16[512,2048]{1,0:T(8,128)(2,1)}, bf16[512,2048]{1,0:T(8,128)(2,1)}, u32[]{:S(2)}, u32[]{:S(2)}) collective-permute-start(bf16[512,2048]{1,0:T(8,128)(2,1)} %slice.152), channel_id=1, source_target_pairs={{0,4},{4,0},{8,12},{12,8},{16,20},{20,16},{24,28},{28,24},{1,5},{5... | collective-permute-start | bytes 6291464 | tf_op jit(solution)/shard_map/ppermute | solution.py:33
  338.1 184.7 %reduce-scatter.8.cloned.1.call-start = ((), (), s32[]{:S(2)}) async-start(), calls=%async_computation.9 | async-start | bytes 3604480 | tf_op jit(solution)/shard_map/reduce_scatter | solution.py:884
  372.9 24.4 %collective-permute-start.28 = (bf16[128,2048]{1,0:T(8,128)(2,1)}, bf16[128,2048]{1,0:T(8,128)(2,1)S(1)}, u32[]{:S(2)}, u32[]{:S(2)}) collective-permute-start(bf16[128,2048]{1,0:T(8,128)(2,1)} %get-tuple-element.328), channel_id=1, source_target_pairs={{0,24},{4,28},{8,16},{12,20},{16,8},{20,12},{24,0},{28,4},{1,25},{... | collective-permute-start | bytes 1572872 | tf_op jit(solution)/shard_map/ppermute | solution.py:267
  374.4 24.6 %collective-permute-start.27 = (bf16[128,2048]{1,0:T(8,128)(2,1)S(1)}, bf16[128,2048]{1,0:T(8,128)(2,1)S(1)}, u32[]{:S(2)}, u32[]{:S(2)}) collective-permute-start(bf16[128,2048]{1,0:T(8,128)(2,1)S(1)} %get-tuple-element.329), channel_id=1, source_target_pairs={{0,16},{4,20},{8,24},{12,28},{16,0},{20,4},{24,8},{28,12},{1,17},{... | collective-permute-start | bytes 1572872 | tf_op jit(solution)/shard_map/ppermute | solution.py:267
  375.5 23.5 %collective-permute-start.26 = (bf16[128,2048]{1,0:T(8,128)(2,1)S(1)}, bf16[128,2048]{1,0:T(8,128)(2,1)S(1)}, u32[]{:S(2)}, u32[]{:S(2)}) collective-permute-start(bf16[128,2048]{1,0:T(8,128)(2,1)S(1)} %get-tuple-element.330), channel_id=1, source_target_pairs={{0,8},{4,12},{8,0},{12,4},{16,24},{20,28},{24,16},{28,20},{1,9},{5... | collective-permute-start | bytes 1572872 | tf_op jit(solution)/shard_map/ppermute | solution.py:267
  404.6 125.2 %reduce-scatter.10.cloned.1.call-start = ((), (), s32[]{:S(2)}) async-start(), calls=%async_computation.10 | async-start | bytes 3604480 | tf_op jit(solution)/shard_map/reduce_scatter | solution.py:884
  404.8 48.0 %collective-permute-start.32 = (bf16[1024,768]{1,0:T(8,128)(2,1)}, bf16[1024,768]{1,0:T(8,128)(2,1)}, u32[]{:S(2)}, u32[]{:S(2)}) collective-permute-start(bf16[1024,768]{1,0:T(8,128)(2,1)} %copy-done.44), channel_id=1, source_target_pairs={{0,8},{4,12},{8,0},{12,4},{16,24},{20,28},{24,16},{28,20},{1,9},{5... | collective-permute-start | bytes 4718600 | tf_op jit(solution)/shard_map/ppermute | solution.py:33
  405.9 46.8 %collective-permute-start.33 = (bf16[1024,768]{1,0:T(8,128)(2,1)}, bf16[1024,768]{1,0:T(8,128)(2,1)}, u32[]{:S(2)}, u32[]{:S(2)}) collective-permute-start(bf16[1024,768]{1,0:T(8,128)(2,1)} %get-tuple-element.217), channel_id=1, source_target_pairs={{0,16},{4,20},{8,24},{12,28},{16,0},{20,4},{24,8},{28,12},{1,17},{... | collective-permute-start | bytes 4718600 | tf_op jit(solution)/shard_map/ppermute | solution.py:33
  452.8 163.3 %reduce-scatter.12.cloned.1.call-start = ((), (), s32[]{:S(2)}) async-start(), calls=%async_computation.11 | async-start | bytes 3932160 | tf_op jit(solution)/shard_map/reduce_scatter | solution.py:899
  452.8 40.5 %collective-permute-start.30 = (bf16[1024,768]{1,0:T(8,128)(2,1)}, bf16[1024,768]{1,0:T(8,128)(2,1)}, u32[]{:S(2)}, u32[]{:S(2)}) collective-permute-start(bf16[1024,768]{1,0:T(8,128)(2,1)} %copy-done.43), channel_id=1, source_target_pairs={{0,8},{4,12},{8,0},{12,4},{16,24},{20,28},{24,16},{28,20},{1,9},{5... | collective-permute-start | bytes 4718600 | tf_op jit(solution)/shard_map/ppermute | solution.py:33
  453.7 39.7 %collective-permute-start.31 = (bf16[1024,768]{1,0:T(8,128)(2,1)}, bf16[1024,768]{1,0:T(8,128)(2,1)}, u32[]{:S(2)}, u32[]{:S(2)}) collective-permute-start(bf16[1024,768]{1,0:T(8,128)(2,1)} %get-tuple-element.215), channel_id=1, source_target_pairs={{0,16},{4,20},{8,24},{12,28},{16,0},{20,4},{24,8},{28,12},{1,17},{... | collective-permute-start | bytes 4718600 | tf_op jit(solution)/shard_map/ppermute | solution.py:33
  457.7 64.7 %collective-permute-start.35 = (bf16[1024,768]{1,0:T(8,128)(2,1)}, bf16[1024,768]{1,0:T(8,128)(2,1)}, u32[]{:S(2)}, u32[]{:S(2)}) collective-permute-start(bf16[1024,768]{1,0:T(8,128)(2,1)} %add_convert_fusion.4), channel_id=1, source_target_pairs={{0,8},{4,12},{8,0},{12,4},{16,24},{20,28},{24,16},{28,20},{1,9},{5... | collective-permute-start | bytes 4718600 | tf_op jit(solution)/shard_map/ppermute | solution.py:33
  462.5 60.3 %collective-permute-start.34 = (bf16[1024,768]{1,0:T(8,128)(2,1)}, bf16[1024,768]{1,0:T(8,128)(2,1)}, u32[]{:S(2)}, u32[]{:S(2)}) collective-permute-start(bf16[1024,768]{1,0:T(8,128)(2,1)} %add_convert_fusion.5), channel_id=1, source_target_pairs={{0,16},{4,20},{8,24},{12,28},{16,0},{20,4},{24,8},{28,12},{1,17},{... | collective-permute-start | bytes 4718600 | tf_op jit(solution)/shard_map/ppermute | solution.py:33
  522.8 39.1 %collective-permute-start.42 = (bf16[512,2048]{1,0:T(8,128)(2,1)}, bf16[512,2048]{1,0:T(8,128)(2,1)}, u32[]{:S(2)}, u32[]{:S(2)}) collective-permute-start(bf16[512,2048]{1,0:T(8,128)(2,1)} %get-tuple-element.248), channel_id=1, source_target_pairs={{0,4},{4,0},{8,12},{12,8},{16,20},{20,16},{24,28},{28,24},{1,5},{5... | collective-permute-start | bytes 6291464 | tf_op jit(solution)/shard_map/ppermute | solution.py:33
  529.8 117.4 %reduce-scatter.14.cloned.1.call-start = ((), (), s32[]{:S(2)}) async-start(), calls=%async_computation.12 | async-start | bytes 1310720 | tf_op jit(solution)/shard_map/reduce_scatter | solution.py:915
  529.9 32.0 %collective-permute-start.41 = (bf16[704,512]{1,0:T(8,128)(2,1)}, bf16[704,512]{1,0:T(8,128)(2,1)S(1)}, u32[]{:S(2)}, u32[]{:S(2)}) collective-permute-start(bf16[704,512]{1,0:T(8,128)(2,1)} %reduce-scatter.6.cloned.1.call-done), channel_id=1, source_target_pairs={{0,16},{4,20},{8,24},{12,28},{16,0},{20,4},{24,8},{28,12},{1,17},{... | collective-permute-start | bytes 2162696 | tf_op jit(solution)/shard_map/ppermute | solution.py:33
  530.9 30.9 %collective-permute-start.40 = (bf16[704,512]{1,0:T(8,128)(2,1)}, bf16[704,512]{1,0:T(8,128)(2,1)S(1)}, u32[]{:S(2)}, u32[]{:S(2)}) collective-permute-start(bf16[704,512]{1,0:T(8,128)(2,1)} %reduce-scatter.6.cloned.1.call-done), channel_id=1, source_target_pairs={{0,8},{4,12},{8,0},{12,4},{16,24},{20,28},{24,16},{28,20},{1,9},{5... | collective-permute-start | bytes 2162696 | tf_op jit(solution)/shard_map/ppermute | solution.py:33
  533.7 26.1 %collective-permute-start.39 = (bf16[128,2048]{1,0:T(8,128)(2,1)S(1)}, bf16[128,2048]{1,0:T(8,128)(2,1)S(1)}, u32[]{:S(2)}, u32[]{:S(2)}) collective-permute-start(bf16[128,2048]{1,0:T(8,128)(2,1)S(1)} %get-tuple-element.324), channel_id=1, source_target_pairs={{0,16},{4,20},{8,24},{12,28},{16,0},{20,4},{24,8},{28,12},{1,17},{... | collective-permute-start | bytes 1572872 | tf_op jit(solution)/shard_map/ppermute | solution.py:33
  535.2 25.6 %collective-permute-start.38 = (bf16[128,2048]{1,0:T(8,128)(2,1)S(1)}, bf16[128,2048]{1,0:T(8,128)(2,1)S(1)}, u32[]{:S(2)}, u32[]{:S(2)}) collective-permute-start(bf16[128,2048]{1,0:T(8,128)(2,1)S(1)} %get-tuple-element.325), channel_id=1, source_target_pairs={{0,8},{4,12},{8,0},{12,4},{16,24},{20,28},{24,16},{28,20},{1,9},{5... | collective-permute-start | bytes 1572872 | tf_op jit(solution)/shard_map/ppermute | solution.py:33
  559.8 14.8 %collective-permute-start.37 = (bf16[128,2048]{1,0:T(8,128)(2,1)S(1)}, bf16[128,2048]{1,0:T(8,128)(2,1)S(1)}, u32[]{:S(2)}, u32[]{:S(2)}) collective-permute-start(bf16[128,2048]{1,0:T(8,128)(2,1)S(1)} %get-tuple-element.326), channel_id=1, source_target_pairs={{0,16},{4,20},{8,24},{12,28},{16,0},{20,4},{24,8},{28,12},{1,17},{... | collective-permute-start | bytes 1572872 | tf_op jit(solution)/shard_map/ppermute | solution.py:33
  560.8 14.9 %collective-permute-start.36 = (bf16[128,2048]{1,0:T(8,128)(2,1)S(1)}, bf16[128,2048]{1,0:T(8,128)(2,1)S(1)}, u32[]{:S(2)}, u32[]{:S(2)}) collective-permute-start(bf16[128,2048]{1,0:T(8,128)(2,1)S(1)} %get-tuple-element.327), channel_id=1, source_target_pairs={{0,8},{4,12},{8,0},{12,4},{16,24},{20,28},{24,16},{28,20},{1,9},{5... | collective-permute-start | bytes 1572872 | tf_op jit(solution)/shard_map/ppermute | solution.py:33
  561.9 19.8 %collective-permute-start.44 = (bf16[352,512]{1,0:T(8,128)(2,1)S(1)}, bf16[352,512]{1,0:T(8,128)(2,1)S(1)}, u32[]{:S(2)}, u32[]{:S(2)}) collective-permute-start(bf16[352,512]{1,0:T(8,128)(2,1)S(1)} %slice.138), channel_id=1, source_target_pairs={{0,8},{4,12},{8,0},{12,4},{16,24},{20,28},{24,16},{28,20},{1,9},{5... | collective-permute-start | bytes 1081352 | tf_op jit(solution)/shard_map/ppermute | solution.py:33
  563.0 18.7 %collective-permute-start.43 = (bf16[352,512]{1,0:T(8,128)(2,1)S(1)}, bf16[352,512]{1,0:T(8,128)(2,1)S(1)}, u32[]{:S(2)}, u32[]{:S(2)}) collective-permute-start(bf16[352,512]{1,0:T(8,128)(2,1)S(1)} %slice.137), channel_id=1, source_target_pairs={{0,16},{4,20},{8,24},{12,28},{16,0},{20,4},{24,8},{28,12},{1,17},{... | collective-permute-start | bytes 1081352 | tf_op jit(solution)/shard_map/ppermute | solution.py:33
  581.8 32.7 %collective-permute-start.47 = (bf16[2816,512]{1,0:T(8,128)(2,1)S(1)}, bf16[2816,512]{1,0:T(8,128)(2,1)S(1)}, u32[]{:S(2)}, u32[]{:S(2)}) collective-permute-start(bf16[2816,512]{1,0:T(8,128)(2,1)S(1)} %constant_dynamic-update-slice_fusion.23.same_ref), channel_id=1, source_target_pairs={{0,4},{4,0},{8,12},{12,8},{16,20},{20,16},{24,28},{28,24},{1,5},{5... | collective-permute-start | bytes 8650760 | tf_op jit(solution)/shard_map/ppermute | solution.py:33
  581.9 30.6 %collective-permute-start.49 = (bf16[704,512]{1,0:T(8,128)(2,1)S(1)}, bf16[704,512]{1,0:T(8,128)(2,1)S(1)}, u32[]{:S(2)}, u32[]{:S(2)}) collective-permute-start(bf16[704,512]{1,0:T(8,128)(2,1)S(1)} %copy-done.85), channel_id=1, source_target_pairs={{0,16},{4,20},{8,24},{12,28},{16,0},{20,4},{24,8},{28,12},{1,17},{... | collective-permute-start | bytes 2162696 | tf_op jit(solution)/shard_map/ppermute | solution.py:33
  583.0 30.4 %collective-permute-start.48 = (bf16[704,512]{1,0:T(8,128)(2,1)S(1)}, bf16[704,512]{1,0:T(8,128)(2,1)S(1)}, u32[]{:S(2)}, u32[]{:S(2)}) collective-permute-start(bf16[704,512]{1,0:T(8,128)(2,1)S(1)} %copy-done.85), channel_id=1, source_target_pairs={{0,8},{4,12},{8,0},{12,4},{16,24},{20,28},{24,16},{28,20},{1,9},{5... | collective-permute-start | bytes 2162696 | tf_op jit(solution)/shard_map/ppermute | solution.py:33
  585.9 26.5 %collective-permute-start.46 = (bf16[128,2048]{1,0:T(8,128)(2,1)S(1)}, bf16[128,2048]{1,0:T(8,128)(2,1)S(1)}, u32[]{:S(2)}, u32[]{:S(2)}) collective-permute-start(bf16[128,2048]{1,0:T(8,128)(2,1)S(1)} %get-tuple-element.322), channel_id=1, source_target_pairs={{0,8},{4,12},{8,0},{12,4},{16,24},{20,28},{24,16},{28,20},{1,9},{5... | collective-permute-start | bytes 1572872 | tf_op jit(solution)/shard_map/ppermute | solution.py:33
  587.1 25.3 %collective-permute-start.45 = (bf16[128,2048]{1,0:T(8,128)(2,1)S(1)}, bf16[128,2048]{1,0:T(8,128)(2,1)S(1)}, u32[]{:S(2)}, u32[]{:S(2)}) collective-permute-start(bf16[128,2048]{1,0:T(8,128)(2,1)S(1)} %get-tuple-element.323), channel_id=1, source_target_pairs={{0,16},{4,20},{8,24},{12,28},{16,0},{20,4},{24,8},{28,12},{1,17},{... | collective-permute-start | bytes 1572872 | tf_op jit(solution)/shard_map/ppermute | solution.py:33
  619.3 92.3 %all-gather.11.cloned.1.call-start = ((), (), s32[]{:S(2)}) async-start(), calls=%async_computation.13 | async-start | bytes 6488064 | tf_op jit(solution)/shard_map/all_gather | solution.py:920
  619.4 27.8 %collective-permute-start.54 = (bf16[512,768]{1,0:T(8,128)(2,1)}, bf16[512,768]{1,0:T(8,128)(2,1)}, u32[]{:S(2)}, u32[]{:S(2)}) collective-permute-start(bf16[512,768]{1,0:T(8,128)(2,1)} %reduce-scatter.12.cloned.1.call-done), channel_id=1, source_target_pairs={{0,16},{4,20},{8,24},{12,28},{16,0},{20,4},{24,8},{28,12},{1,17},{... | collective-permute-start | bytes 2359304 | tf_op jit(solution)/shard_map/ppermute | solution.py:33
  620.4 26.8 %collective-permute-start.53 = (bf16[512,768]{1,0:T(8,128)(2,1)}, bf16[512,768]{1,0:T(8,128)(2,1)}, u32[]{:S(2)}, u32[]{:S(2)}) collective-permute-start(bf16[512,768]{1,0:T(8,128)(2,1)} %reduce-scatter.12.cloned.1.call-done), channel_id=1, source_target_pairs={{0,8},{4,12},{8,0},{12,4},{16,24},{20,28},{24,16},{28,20},{1,9},{5... | collective-permute-start | bytes 2359304 | tf_op jit(solution)/shard_map/ppermute | solution.py:33
  623.5 23.7 %collective-permute-start.52 = (bf16[352,512]{1,0:T(8,128)(2,1)S(1)}, bf16[352,512]{1,0:T(8,128)(2,1)S(1)}, u32[]{:S(2)}, u32[]{:S(2)}) collective-permute-start(bf16[352,512]{1,0:T(8,128)(2,1)S(1)} %slice.142), channel_id=1, source_target_pairs={{0,8},{4,12},{8,0},{12,4},{16,24},{20,28},{24,16},{28,20},{1,9},{5... | collective-permute-start | bytes 1081352 | tf_op jit(solution)/shard_map/ppermute | solution.py:33
  624.5 22.7 %collective-permute-start.51 = (bf16[352,512]{1,0:T(8,128)(2,1)S(1)}, bf16[352,512]{1,0:T(8,128)(2,1)}, u32[]{:S(2)}, u32[]{:S(2)}) collective-permute-start(bf16[352,512]{1,0:T(8,128)(2,1)S(1)} %slice.141), channel_id=1, source_target_pairs={{0,16},{4,20},{8,24},{12,28},{16,0},{20,4},{24,8},{28,12},{1,17},{... | collective-permute-start | bytes 1081352 | tf_op jit(solution)/shard_map/ppermute | solution.py:33
  625.6 21.6 %collective-permute-start.55 = (f32[2,2048]{1,0:T(2,128)S(1)}, f32[2,2048]{1,0:T(2,128)S(1)}, u32[]{:S(2)}, u32[]{:S(2)}) collective-permute-start(f32[2,2048]{1,0:T(2,128)S(1)} %add.217), channel_id=1, source_target_pairs={{0,8},{4,12},{8,0},{12,4},{16,24},{20,28},{24,16},{28,20},{1,9},{5... | collective-permute-start | bytes 49160 | tf_op jit(solution)/shard_map/ppermute | solution.py:33
  650.8 31.8 %collective-permute-start.56 = (bf16[2816,512]{1,0:T(8,128)(2,1)S(1)}, bf16[2816,512]{1,0:T(8,128)(2,1)S(1)}, u32[]{:S(2)}, u32[]{:S(2)}) collective-permute-start(bf16[2816,512]{1,0:T(8,128)(2,1)S(1)} %constant_dynamic-update-slice_fusion.28.same_ref), channel_id=1, source_target_pairs={{0,4},{4,0},{8,12},{12,8},{16,20},{20,16},{24,28},{28,24},{1,5},{5... | collective-permute-start | bytes 8650760 | tf_op jit(solution)/shard_map/ppermute | solution.py:33
  655.7 26.9 %collective-permute-start.58 = (bf16[256,768]{1,0:T(8,128)(2,1)S(1)}, bf16[256,768]{1,0:T(8,128)(2,1)S(1)}, u32[]{:S(2)}, u32[]{:S(2)}) collective-permute-start(bf16[256,768]{1,0:T(8,128)(2,1)S(1)} %slice.146), channel_id=1, source_target_pairs={{0,8},{4,12},{8,0},{12,4},{16,24},{20,28},{24,16},{28,20},{1,9},{5... | collective-permute-start | bytes 1179656 | tf_op jit(solution)/shard_map/ppermute | solution.py:33
  656.8 25.9 %collective-permute-start.57 = (bf16[256,768]{1,0:T(8,128)(2,1)S(1)}, bf16[256,768]{1,0:T(8,128)(2,1)S(1)}, u32[]{:S(2)}, u32[]{:S(2)}) collective-permute-start(bf16[256,768]{1,0:T(8,128)(2,1)S(1)} %slice.145), channel_id=1, source_target_pairs={{0,16},{4,20},{8,24},{12,28},{16,0},{20,4},{24,8},{28,12},{1,17},{... | collective-permute-start | bytes 1179656 | tf_op jit(solution)/shard_map/ppermute | solution.py:33
  660.1 22.6 %collective-permute-start.60 = (bf16[256,512]{1,0:T(8,128)(2,1)S(1)}, bf16[256,512]{1,0:T(8,128)(2,1)S(1)}, u32[]{:S(2)}, u32[]{:S(2)}) collective-permute-start(bf16[256,512]{1,0:T(8,128)(2,1)S(1)} %copy-done.95), channel_id=1, source_target_pairs={{0,16},{4,20},{8,24},{12,28},{16,0},{20,4},{24,8},{28,12},{1,17},{... | collective-permute-start | bytes 786440 | tf_op jit(solution)/shard_map/ppermute | solution.py:267
  663.5 19.2 %collective-permute-start.59 = (bf16[256,512]{1,0:T(8,128)(2,1)S(1)}, bf16[256,512]{1,0:T(8,128)(2,1)S(1)}, u32[]{:S(2)}, u32[]{:S(2)}) collective-permute-start(bf16[256,512]{1,0:T(8,128)(2,1)S(1)} %copy-done.95), channel_id=1, source_target_pairs={{0,8},{4,12},{8,0},{12,4},{16,24},{20,28},{24,16},{28,20},{1,9},{5... | collective-permute-start | bytes 786440 | tf_op jit(solution)/shard_map/ppermute | solution.py:267
  684.3 16.1 %collective-permute-start.63 = (bf16[2048,768]{1,0:T(8,128)(2,1)S(1)}, bf16[2048,768]{1,0:T(8,128)(2,1)}, u32[]{:S(2)}, u32[]{:S(2)}) collective-permute-start(bf16[2048,768]{1,0:T(8,128)(2,1)S(1)} %constant_dynamic-update-slice_fusion.33.same_ref), channel_id=1, source_target_pairs={{0,4},{4,0},{8,12},{12,8},{16,20},{20,16},{24,28},{28,24},{1,5},{5... | collective-permute-start | bytes 9437192 | tf_op jit(solution)/shard_map/ppermute | solution.py:33
  (125 other events, 1203.1 us)
Sparse Core Ops, SparseCore 0:
  96.3 28.0 all-gather.4
  126.6 106.1 all-gather.6
  234.9 57.4 all-gather.8
  338.3 56.5 reduce-scatter.5
  404.7 56.1 reduce-scatter.7
  463.0 56.0 reduce-scatter.9
  529.9 60.1 reduce-scatter.11
  619.5 26.9 reduce-scatter.13
  648.6 52.3 all-gather.10

commit v14 on v12

--- a/solution.py
+++ b/solution.py
@@ -691,6 +691,26 @@
     )(me, same, other)
 
 
+def widen_kernel(in_ref, out_ref):
+    out_ref[...] = in_ref[...].astype(F32)
+
+
+def widen(value):
+    rows, width = value.shape
+    tile = rows // 4
+    spec = pl.BlockSpec((tile, width), lambda i: (i, 0))
+    return pl.pallas_call(
+        widen_kernel,
+        grid=(4,),
+        in_specs=[spec],
+        out_specs=spec,
+        out_shape=jax.ShapeDtypeStruct(value.shape, F32),
+        compiler_params=pltpu.CompilerParams(vmem_limit_bytes=32 << 20),
+        cost_estimate=pl.CostEstimate(flops=0, bytes_accessed=6 * value.size, transcendentals=0),
+        name="widen",
+    )(value)
+
+
 def per_device(
     layer_input,
     gain_attn,
@@ -868,25 +888,26 @@
     grad_normed = grad_normed[0] + other_normed.astype(F32)
     grad_gain_one, first = norm_back(grad_normed, inputs, root_one, gain_one)
     grad_input = (grad_hidden + first).astype(BF)
-    grad_input, gains, up_sum = stage(
+    grad_input, gains, up_sum, sum_qkv, down_sum = stage(
         [out_flow, gate_flow],
-        (grad_input, jnp.stack([grad_gain_one, grad_gain_two]), up_sum),
-    )
+        (grad_input, jnp.stack([grad_gain_one, grad_gain_two]), up_sum, sum_qkv, sums[2]),
+    )
+    all_down = lax.all_gather(down_sum, "rep", axis=0, tiled=True)
     gain_flow, up_flow = Flow(vector_sum_steps(gains)), Flow(copies_steps(up_sum))
-    sum_qkv = stage([out_flow, gate_flow, up_flow, gain_flow], sum_qkv)
+    stage([out_flow, gate_flow, up_flow, gain_flow])
     sum_out = lax.psum_scatter(finish(out_flow), "shard", scatter_dimension=1, tiled=True)
     qkv_flow = Flow(copies_steps(sum_qkv))
     grad_gate = place_turned(whoami, *finish(gate_flow), units)
-    grad_gate, sum_out = stage([up_flow, qkv_flow, gain_flow], (grad_gate, sum_out))
-    down_sum, sum_out = lax.optimization_barrier((sums[2], sum_out))
-    all_down = lax.all_gather(down_sum, "rep", axis=0, tiled=True)
+    grad_gate, all_down = stage([up_flow, qkv_flow, gain_flow], (grad_gate, all_down))
+    sum_out = stage([up_flow, qkv_flow, gain_flow], sum_out)
     out_flow = Flow(copies_steps(sum_out, straight_steps))
-    stage([up_flow, qkv_flow, out_flow, gain_flow])
-    grad_up = place_turned(whoami, *finish(up_flow), units)
-    grad_up = stage([qkv_flow, out_flow, gain_flow], grad_up)
+    grad_up, grad_down = stage(
+        [qkv_flow, out_flow, gain_flow],
+        (place_turned(whoami, *finish(up_flow), units), widen(all_down)),
+    )
     grad_query, grad_key, grad_value = place(whoami, *finish(qkv_flow), own, block, True)
+    grad_query = stage([out_flow], grad_query)
     (grad_out,) = place(whoami, *finish(out_flow), block, own, False)
-    grad_down = all_down.astype(F32)
     gain_grads = finish(gain_flow)
     return (
         output,

time: 721 us -> 749 us (1.039)
  waiting for transfers between devices: 173 us -> 203 us
  Pallas kernels: 239 us -> 247 us
  other arithmetic: 58.9 us -> 51.2 us
    ppermute x53, waiting for transfers between devices: 110 us -> 133 us  [swap(): return lax.ppermute(value, 'rep', [(i, i ^ bit) for i in range(size)])]
    ppermute x6, waiting for transfers between devices: 22.5 us -> 1.9 us  [jump(): return lax.ppermute(value, 'rep', [(i, i ^ offset) for i in range(size)])]
    reduce_scatter x1, waiting for transfers between devices: 0.02 us -> 19.2 us  [per_device(): lax.psum_scatter(finish(out_flow), 'shard', scatter_dimension=1, tiled=True)]
    convert_element_type x1 -> x0, other arithmetic: 8.87 us -> none  [per_device(): grad_down = all_down.astype(F32)]
    unnamed x259 -> x257, local copies, waits for them, and re-layouts: 58.1 us -> 54.3 us
  transfers between devices with their start and end apart: 77 -> 77, of which waited for: 20 -> 24; matrix products, arithmetic and copies ran while one was open for 20% -> 20% of each run, Pallas kernels for 33% -> 33%
where the time goes in v14:
time: 749 us; the launch traced here: 742 us
  Pallas kernels  247 us (33%)
  waiting for transfers between devices  203 us (27%)
  local copies, waits for them, and re-layouts  84.8 us (11%)
  matrix products  72.2 us (10%)
  starting transfers between devices  68.4 us (9%)
  other arithmetic  51.2 us (7%)
  between operations  15.8 us (2%)
    ppermute x53, waiting for transfers between devices, swap(): return lax.ppermute(value, 'rep', [(i, i ^ bit) for i in range(size)])  133 us
    pallas_call x4, Pallas kernels, attend_back(): pl.pallas_call(attend_back_kernel, grid=(rows // length,), in_specs=[whol...  72 us
    pallas_call x2, Pallas kernels, gather_rows(): pl.pallas_call(functools.partial(gather_kernel, peers()), out_shape=jax.S...  58.4 us
    unnamed x257, local copies, waits for them, and re-layouts  54.3 us
    ppermute x53, starting transfers between devices, swap(): return lax.ppermute(value, 'rep', [(i, i ^ bit) for i in range(size)])  48.1 us
    pallas_call x4, Pallas kernels, attend(): pl.pallas_call(functools.partial(attend_kernel, parts), grid_spec=pltpu.P...  42.5 us
    dot_general x6, matrix products, mm_tn(): lax.dot_general(left, right, (((0,), (0,)), ((), ())), preferred_element_...  27.4 us
    dot_general x5, matrix products, mm(): return jnp.dot(left, right, preferred_element_type=F32)  24.6 us
  transfers between devices with their start and end apart: 77, of which 24 were waited for; matrix products, arithmetic and copies ran while one was open for 20% of the time, Pallas kernels for 33%

profile of v14, /device:TPU:0, one launch (start us, length us, event | category | flops | bytes accessed | tf_op | source)
XLA Modules:
  0.0 742.1 jit_solution(12348703774293582441)
XLA Ops:
  8.8 3.1 collective-permute-start.2
  11.8 2.6 collective-permute-start.1
  17.8 2.7 constant_dynamic-slice_fusion.4
  21.2 2.3 constant_dynamic-slice_fusion.15
  26.2 16.2 %collective-permute-done.3.refs_5_ = bf16[512,768]{1,0:T(8,128)(2,1)} collective-permute-done((bf16[512,768]{1,0:T(8,128)(2,1)S(1)}, bf16[512,768]{1,0:T(8,128)(2,1)}, u32[]{:S(2)}, u32[]{:S(2)}) %collective-permute-start.3) | collective-permute-done | bytes 786464 | tf_op jit(solution)/shard_map/ppermute | solution.py:763
  48.0 18.9 %collective-permute-done.7.refs_6_ = bf16[512,768]{1,0:T(8,128)(2,1)} collective-permute-done((bf16[512,768]{1,0:T(8,128)(2,1)}, bf16[512,768]{1,0:T(8,128)(2,1)}, u32[]{:S(2)}, u32[]{:S(2)}) %collective-permute-start.7) | collective-permute-done | bytes 786464 | tf_op jit(solution)/shard_map/ppermute | solution.py:777
  75.5 20.7 %collective-permute-done.10 = bf16[256,768]{1,0:T(8,128)(2,1)} collective-permute-done((bf16[256,768]{1,0:T(8,128)(2,1)}, bf16[256,768]{1,0:T(8,128)(2,1)}, u32[]{:S(2)}, u32[]{:S(2)}) %collective-permute-start.10) | collective-permute-done | bytes 393248 | tf_op jit(solution)/shard_map/ppermute | solution.py:33
  114.4 11.3 %attend.4 = (bf16[1024,256]{1,0:T(8,128)(2,1)S(1)}, bf16[1024,768]{1,0:T(8,128)(2,1)S(1)}, f32[1024,2]{1,0:T(8,128)S(1)}) custom-call(s32[1]{0:T(128)} %bitcast.1.z_ref, bf16[1024,2048]{1,0:T(8,128)(2,1)S(1)} %pad_maximum_fusion.refs_0_.refs_1_.refs_2_.refs_3_.x_ref, bf16[1024,2048]{1,0:T(8,128)(2,1)S(1)} %pad_maximum_fusion.refs_0_.refs_1_.refs_2_.refs_3_.x_ref, ...), custom_call_target="tpu_custom_call" | custom-call | flops 3758096384 | bytes 10485760 | tf_op jit(solution)/shard_map/attend/pallas_call | solution.py:423
  139.3 2.2 copy-done.3
  143.8 10.7 %attend.5 = (bf16[1024,256]{1,0:T(8,128)(2,1)S(1)}, bf16[1024,768]{1,0:T(8,128)(2,1)S(1)}, f32[1024,2]{1,0:T(8,128)S(1)}) custom-call(s32[1]{0:T(128)} %bitcast.1.z_ref, bf16[1024,2048]{1,0:T(8,128)(2,1)S(1)} %copy-done.3, bf16[1024,2048]{1,0:T(8,128)(2,1)S(1)} %copy-done.3, bf16[1024,2048]{1,0:T(8,128)(2,1)S(1)} %copy-done.3, ...), custom_call_target="tpu_custom_call" | custom-call | flops 3758096384 | bytes 10485760 | tf_op jit(solution)/shard_map/attend/pallas_call | solution.py:423
  156.5 10.8 %attend.6 = (bf16[1024,256]{1,0:T(8,128)(2,1)S(1)}, bf16[1024,768]{1,0:T(8,128)(2,1)S(1)}, f32[1024,2]{1,0:T(8,128)S(1)}) custom-call(s32[1]{0:T(128)} %bitcast.1.z_ref, bf16[1024,2048]{1,0:T(8,128)(2,1)S(1)} %copy-done.3, bf16[1024,2048]{1,0:T(8,128)(2,1)S(1)} %copy-done.3, bf16[1024,2048]{1,0:T(8,128)(2,1)S(1)} %copy-done.3, ...), custom_call_target="tpu_custom_call" | custom-call | flops 3758096384 | bytes 10485760 | tf_op jit(solution)/shard_map/attend/pallas_call | solution.py:423
  169.1 9.6 %attend.7 = (bf16[1024,256]{1,0:T(8,128)(2,1)S(1)}, bf16[1024,768]{1,0:T(8,128)(2,1)S(1)}, f32[1024,2]{1,0:T(8,128)S(1)}) custom-call(s32[1]{0:T(128)} %bitcast.1.z_ref, bf16[1024,2048]{1,0:T(8,128)(2,1)S(1)} %copy-done.3, bf16[1024,2048]{1,0:T(8,128)(2,1)S(1)} %copy-done.3, bf16[1024,2048]{1,0:T(8,128)(2,1)S(1)} %copy-done.3, ...), custom_call_target="tpu_custom_call" | custom-call | flops 3758096384 | bytes 10485760 | tf_op jit(solution)/shard_map/attend/pallas_call | solution.py:423
  183.1 6.1 collective-permute-done.22
  191.4 6.3 fusion.53
  197.7 3.4 copy-done.61
  203.2 2.3 fusion.22.in_ref
  207.2 4.0 multiply_reduce_fusion.2
  214.0 29.1 %gather_rows.2 = bf16[1024,2048]{1,0:T(8,128)(2,1)S(1)} custom-call(bf16[128,2048]{1,0:T(8,128)(2,1)S(1)} %convolution_convert_fusion.5.in_ref), custom_call_target="tpu_custom_call" | custom-call | bytes 62914560 | tf_op jit(solution)/shard_map/gather_rows/pallas_call | solution.py:153
  245.1 11.7 %fusion.54 = f32[1024,1408]{1,0:T(8,128)} fusion(bf16[1024,2048]{1,0:T(8,128)(2,1)} %copy-done.7, bf16[2048,1408]{1,0:T(8,128)(2,1)} %all-gather.7.cloned.1.call-done), kind=kOutput, calls=%fused_computation.179 | convolution fusion | flops 5905580032 | bytes 15728640 | tf_op jit(solution)/shard_map/dot_general | solution.py:20
  256.8 29.3 %gather_rows.3 = bf16[1024,2048]{1,0:T(8,128)(2,1)S(1)} custom-call(bf16[128,2048]{1,0:T(8,128)(2,1)S(1)} %fusion.22.in_ref), custom_call_target="tpu_custom_call" | custom-call | bytes 62914560 | tf_op jit(solution)/shard_map/gather_rows/pallas_call | solution.py:153
  288.1 4.3 all-gather.9.cloned.1.call-done
  292.4 9.1 %multiply_convert_fusion.2 = (bf16[1024,704]{1,0:T(8,128)(2,1)S(1)}, bf16[1024,704]{1,0:T(8,128)(2,1)S(1)}, bf16[1024,704]{1,0:T(8,128)(2,1)S(1)}) fusion(f32[1024,1408]{1,0:T(8,128)} %fusion.54, bf16[1024,2048]{1,0:T(8,128)(2,1)} %copy-done.5, bf16[704,2048]{1,0:T(8,128)(2,1)} %all-gather.9.cloned.1.call-done), kind=kOutput, calls=%fused_computation.44 | convolution fusion | flops 2963603456 | bytes 17170432 | tf_op jit(solution)/shard_map/dot_general | solution.py:24
  301.6 3.6 convolution_convert_fusion.1
  307.9 11.1 %convolution_convert_fusion.in_ref = bf16[1024,2048]{1,0:T(8,128)(2,1)} fusion(bf16[2048,1408]{1,0:T(8,128)(2,1)} %all-gather.7.cloned.1.call-done, bf16[1024,704]{1,0:T(8,128)(2,1)S(1)} %get-tuple-element.205, bf16[1024,704]{1,0:T(8,128)(2,1)S(1)} %get-tuple-element.320), kind=kOutput, calls=%fused_computation.34 | convolution fusion | flops 5913444352 | bytes 12845056 | tf_op jit(solution)/shard_map/dot_general | solution.py:24
  319.0 4.5 convolution_convert_fusion.4
  324.0 2.2 copy-done.10
  326.2 22.5 %reduce_rows.1 = bf16[128,2048]{1,0:T(8,128)(2,1)S(1)} custom-call(bf16[1024,2048]{1,0:T(8,128)(2,1)S(1)} %copy-done.10), custom_call_target="tpu_custom_call" | custom-call | bytes 62914560 | tf_op jit(solution)/shard_map/reduce_rows/pallas_call | solution.py:243
  350.4 3.2 multiply_convert_fusion
  354.3 2.6 add_convert_fusion.1
  362.7 17.7 %attend_back.4 = (bf16[1024,768]{1,0:T(8,128)(2,1)S(1)}, bf16[1024,768]{1,0:T(8,128)(2,1)S(1)}, bf16[1024,768]{1,0:T(8,128)(2,1)}) custom-call(bf16[512,2048]{1,0:T(8,128)(2,1)} %copy-done.64, bf16[512,2048]{1,0:T(8,128)(2,1)} %copy-done.108, bf16[256,2048]{1,0:T(8,128)(2,1)S(1)} %pad_maximum_fusion.3.out_ref, bf16[1024,768]{1,0:T(8,128)(2,1)} %copy-done.36, ...), custom_call_target="tpu_custom_call" | custom-call | flops 5637144576 | bytes 15728640 | tf_op jit(solution)/shard_map/attend_back/pallas_call | solution.py:519
  385.6 4.5 convolution_convert_fusion.3
  393.5 18.1 %attend_back.6 = (bf16[1024,768]{1,0:T(8,128)(2,1)S(1)}, bf16[1024,768]{1,0:T(8,128)(2,1)S(1)}, bf16[1024,768]{1,0:T(8,128)(2,1)}) custom-call(bf16[512,2048]{1,0:T(8,128)(2,1)} %copy-done.64, bf16[512,2048]{1,0:T(8,128)(2,1)} %copy-done.108, bf16[256,2048]{1,0:T(8,128)(2,1)S(1)} %copy-done.18, bf16[1024,768]{1,0:T(8,128)(2,1)} %copy-done.35, ...), custom_call_target="tpu_custom_call" | custom-call | flops 5637144576 | bytes 15728640 | tf_op jit(solution)/shard_map/attend_back/pallas_call | solution.py:519
  414.6 17.7 %attend_back.5 = (bf16[1024,768]{1,0:T(8,128)(2,1)S(1)}, bf16[1024,768]{1,0:T(8,128)(2,1)S(1)}, bf16[1024,768]{1,0:T(8,128)(2,1)}) custom-call(bf16[512,2048]{1,0:T(8,128)(2,1)} %copy-done.64, bf16[512,2048]{1,0:T(8,128)(2,1)} %copy-done.108, bf16[256,2048]{1,0:T(8,128)(2,1)S(1)} %copy-done.16, bf16[1024,768]{1,0:T(8,128)(2,1)} %copy-done.34, ...), custom_call_target="tpu_custom_call" | custom-call | flops 5637144576 | bytes 15728640 | tf_op jit(solution)/shard_map/attend_back/pallas_call | solution.py:519
  434.7 4.5 convolution_convert_fusion.2
  441.6 3.4 add_convert_fusion.4
  446.4 3.5 add_convert_fusion.5
  450.3 18.4 %attend_back.7 = (bf16[1024,768]{1,0:T(8,128)(2,1)S(1)}, bf16[1024,768]{1,0:T(8,128)(2,1)S(1)}, bf16[1024,768]{1,0:T(8,128)(2,1)}) custom-call(bf16[512,2048]{1,0:T(8,128)(2,1)} %copy-done.64, bf16[512,2048]{1,0:T(8,128)(2,1)} %copy-done.108, bf16[256,2048]{1,0:T(8,128)(2,1)S(1)} %copy-done.32, bf16[1024,768]{1,0:T(8,128)(2,1)} %copy-done.33, ...), custom_call_target="tpu_custom_call" | custom-call | flops 5637144576 | bytes 15728640 | tf_op jit(solution)/shard_map/attend_back/pallas_call | solution.py:519
  468.8 10.0 %fusion.15 = bf16[1024,2048]{1,0:T(8,128)(2,1)} fusion(bf16[1024,1024]{1,0:T(8,128)(2,1)} %constant_dynamic-update-slice_fusion.14, bf16[512,2048]{1,0:T(8,128)(2,1)} %copy-done.108, bf16[512,2048]{1,0:T(8,128)(2,1)S(1)} %copy-done.65), kind=kOutput, calls=%fused_computation.33 | convolution fusion | flops 4305453056 | bytes 10485760 | tf_op jit(solution)/shard_map/dot_general | solution.py:28
  478.8 2.2 add_convert_fusion
  481.0 23.3 %normed_back.1 = (f32[512,2048]{1,0:T(8,128)}, bf16[512,2048]{1,0:T(8,128)(2,1)}) custom-call(s32[1]{0:T(128)} %bitcast.1.z_ref, bf16[1024,768]{1,0:T(8,128)(2,1)} %copy-done.48, bf16[1024,768]{1,0:T(8,128)(2,1)} %copy-done.47, bf16[1024,768]{1,0:T(8,128)(2,1)} %copy-done.46, bf16[1024,768]{1,0:T(8,128)(2,1)} %copy-done.45, ...), custom_call_target="tpu_custom_call" | custom-call | flops 12884901888 | bytes 27262976 | tf_op jit(solution)/shard_map/normed_back/pallas_call | solution.py:576
  504.3 5.0 collective-permute-done.35
  510.5 2.6 add_convert_fusion.2
  513.1 2.5 add_convert_fusion.3
  523.6 24.1 %collective-permute-done.39 = bf16[128,2048]{1,0:T(8,128)(2,1)S(1)} collective-permute-done((bf16[128,2048]{1,0:T(8,128)(2,1)S(1)}, bf16[128,2048]{1,0:T(8,128)(2,1)S(1)}, u32[]{:S(2)}, u32[]{:S(2)}) %collective-permute-start.39) | collective-permute-done | bytes 524320 | tf_op jit(solution)/shard_map/ppermute | solution.py:33
  551.9 4.1 fusion.9
  556.1 2.7 fusion.6
  558.9 3.7 collective-permute-done.37
  563.2 6.2 collective-permute-done.44
  569.4 6.3 reduce-scatter.12.cloned.1.call-done
  584.9 18.2 %collective-permute-done.46 = bf16[128,2048]{1,0:T(8,128)(2,1)S(1)} collective-permute-done((bf16[128,2048]{1,0:T(8,128)(2,1)S(1)}, bf16[128,2048]{1,0:T(8,128)(2,1)S(1)}, u32[]{:S(2)}, u32[]{:S(2)}) %collective-permute-start.46) | collective-permute-done | bytes 524320 | tf_op jit(solution)/shard_map/ppermute | solution.py:33
  606.9 22.2 %collective-permute-done.49 = bf16[704,512]{1,0:T(8,128)(2,1)S(1)} collective-permute-done((bf16[704,512]{1,0:T(8,128)(2,1)S(1)}, bf16[704,512]{1,0:T(8,128)(2,1)S(1)}, u32[]{:S(2)}, u32[]{:S(2)}) %collective-permute-start.49) | collective-permute-done | bytes 720928 | tf_op jit(solution)/shard_map/ppermute | solution.py:33
  629.3 2.5 collective-permute-start.51
  636.6 5.0 place_turned.2
  641.5 11.1 %collective-permute-done.54 = bf16[512,768]{1,0:T(8,128)(2,1)S(1)} collective-permute-done((bf16[512,768]{1,0:T(8,128)(2,1)S(1)}, bf16[512,768]{1,0:T(8,128)(2,1)S(1)}, u32[]{:S(2)}, u32[]{:S(2)}) %collective-permute-start.54) | collective-permute-done | bytes 786464 | tf_op jit(solution)/shard_map/ppermute | solution.py:33
  652.6 6.1 collective-permute-done.55
  672.3 19.2 %reduce-scatter.14.cloned.1.call-done = bf16[256,512]{1,0:T(8,128)(2,1)} async-done(((bf16[256,2048]{1,0:T(8,128)(2,1)}), bf16[256,512]{1,0:T(8,128)(2,1)}) %reduce-scatter.14.cloned.1.call-update) | async-done | bytes 262160 | tf_op jit(solution)/shard_map/reduce_scatter | solution.py:898
  692.6 2.4 collective-permute-start.63
  698.0 2.6 collective-permute-done.66
  701.6 2.6 copy-done.4
  704.3 4.5 widen.1
  708.8 2.3 collective-permute-start.64
  711.8 7.8 %place_turned.3 = f32[512,5632]{1,0:T(8,128)} custom-call(s32[1]{0:T(128)} %bitcast.6.me_ref, bf16[2816,512]{1,0:T(8,128)(2,1)} %constant_dynamic-update-slice_fusion.28.same_ref, bf16[2816,512]{1,0:T(8,128)(2,1)} %collective-permute-done.56.other_ref), custom_call_target="tpu_custom_call" | custom-call | bytes 17301504 | tf_op jit(solution)/shard_map/place_turned/pallas_call | solution.py:677
  723.8 6.3 place.2
  730.8 4.4 place.3
  (470 shorter events, 162.1 us)
Async XLA Ops:
  7.2 123.9 %all-gather.5.cloned.1.call-start = ((), (), s32[]{:S(2)}) async-start(), calls=%async_computation.5 | async-start | bytes 1310720 | tf_op jit(solution)/shard_map/all_gather | solution.py:781
  8.8 17.5 %collective-permute-start.2 = (bf16[2,512]{1,0:T(2,128)(2,1)S(1)}, bf16[2,512]{1,0:T(2,128)(2,1)S(1)}, u32[]{:S(2)}, u32[]{:S(2)}) collective-permute-start(bf16[2,512]{1,0:T(2,128)(2,1)S(1)} %get-tuple-element.316), channel_id=1, source_target_pairs={{0,1},{1,2},{2,3},{3,0},{4,5},{5,6},{6,7},{7,4},{8,9},{9,10},{10,1... | collective-permute-start | bytes 6152 | tf_op jit(solution)/shard_map/ppermute | solution.py:344
  20.5 21.9 %collective-permute-start.3 = (bf16[512,768]{1,0:T(8,128)(2,1)S(1)}, bf16[512,768]{1,0:T(8,128)(2,1)}, u32[]{:S(2)}, u32[]{:S(2)}) collective-permute-start(bf16[512,768]{1,0:T(8,128)(2,1)S(1)} %pad_maximum_fusion.5.refs_4_), channel_id=1, source_target_pairs={{0,1},{1,2},{2,3},{3,0},{4,5},{5,6},{6,7},{7,4},{8,9},{9,10},{10,1... | collective-permute-start | bytes 2359304 | tf_op jit(solution)/shard_map/ppermute | solution.py:763
  44.7 22.2 %collective-permute-start.8 = (bf16[512,2048]{1,0:T(8,128)(2,1)S(1)}, bf16[512,2048]{1,0:T(8,128)(2,1)S(1)}, u32[]{:S(2)}, u32[]{:S(2)}) collective-permute-start(bf16[512,2048]{1,0:T(8,128)(2,1)S(1)} %fusion.2), channel_id=1, source_target_pairs={{0,4},{4,0},{8,12},{12,8},{16,20},{20,16},{24,28},{28,24},{1,5},{5... | collective-permute-start | bytes 6291464 | tf_op jit(solution)/shard_map/ppermute | solution.py:33
  44.8 22.1 %collective-permute-start.7 = (bf16[512,768]{1,0:T(8,128)(2,1)}, bf16[512,768]{1,0:T(8,128)(2,1)}, u32[]{:S(2)}, u32[]{:S(2)}) collective-permute-start(bf16[512,768]{1,0:T(8,128)(2,1)} %collective-permute-done.3.refs_5_), channel_id=1, source_target_pairs={{0,1},{1,2},{2,3},{3,0},{4,5},{5,6},{6,7},{7,4},{8,9},{9,10},{10,1... | collective-permute-start | bytes 2359304 | tf_op jit(solution)/shard_map/ppermute | solution.py:777
  44.9 22.0 %collective-permute-start.6 = (bf16[512,768]{1,0:T(8,128)(2,1)}, bf16[512,768]{1,0:T(8,128)(2,1)S(1)}, u32[]{:S(2)}, u32[]{:S(2)}) collective-permute-start(bf16[512,768]{1,0:T(8,128)(2,1)} %collective-permute-done.3.refs_5_), channel_id=1, source_target_pairs={{0,16},{4,20},{8,24},{12,28},{16,0},{20,4},{24,8},{28,12},{1,17},{... | collective-permute-start | bytes 2359304 | tf_op jit(solution)/shard_map/ppermute | solution.py:33
  46.5 20.4 %collective-permute-start.5 = (bf16[512,768]{1,0:T(8,128)(2,1)}, bf16[512,768]{1,0:T(8,128)(2,1)S(1)}, u32[]{:S(2)}, u32[]{:S(2)}) collective-permute-start(bf16[512,768]{1,0:T(8,128)(2,1)} %collective-permute-done.3.refs_5_), channel_id=1, source_target_pairs={{0,8},{4,12},{8,0},{12,4},{16,24},{20,28},{24,16},{28,20},{1,9},{5... | collective-permute-start | bytes 2359304 | tf_op jit(solution)/shard_map/ppermute | solution.py:33
  66.9 29.2 %collective-permute-start.13 = (bf16[512,768]{1,0:T(8,128)(2,1)}, bf16[512,768]{1,0:T(8,128)(2,1)}, u32[]{:S(2)}, u32[]{:S(2)}) collective-permute-start(bf16[512,768]{1,0:T(8,128)(2,1)} %collective-permute-done.7.refs_6_), channel_id=1, source_target_pairs={{0,1},{1,2},{2,3},{3,0},{4,5},{5,6},{6,7},{7,4},{8,9},{9,10},{10,1... | collective-permute-start | bytes 2359304 | tf_op jit(solution)/shard_map/ppermute | solution.py:777
  67.0 29.2 %collective-permute-start.12 = (bf16[512,768]{1,0:T(8,128)(2,1)}, bf16[512,768]{1,0:T(8,128)(2,1)}, u32[]{:S(2)}, u32[]{:S(2)}) collective-permute-start(bf16[512,768]{1,0:T(8,128)(2,1)} %collective-permute-done.7.refs_6_), channel_id=1, source_target_pairs={{0,16},{4,20},{8,24},{12,28},{16,0},{20,4},{24,8},{28,12},{1,17},{... | collective-permute-start | bytes 2359304 | tf_op jit(solution)/shard_map/ppermute | solution.py:33
  68.6 27.6 %collective-permute-start.11 = (bf16[512,768]{1,0:T(8,128)(2,1)}, bf16[512,768]{1,0:T(8,128)(2,1)}, u32[]{:S(2)}, u32[]{:S(2)}) collective-permute-start(bf16[512,768]{1,0:T(8,128)(2,1)} %collective-permute-done.7.refs_6_), channel_id=1, source_target_pairs={{0,8},{4,12},{8,0},{12,4},{16,24},{20,28},{24,16},{28,20},{1,9},{5... | collective-permute-start | bytes 2359304 | tf_op jit(solution)/shard_map/ppermute | solution.py:33
  71.6 24.5 %collective-permute-start.10 = (bf16[256,768]{1,0:T(8,128)(2,1)}, bf16[256,768]{1,0:T(8,128)(2,1)}, u32[]{:S(2)}, u32[]{:S(2)}) collective-permute-start(bf16[256,768]{1,0:T(8,128)(2,1)} %slice.116), channel_id=1, source_target_pairs={{0,8},{4,12},{8,0},{12,4},{16,24},{20,28},{24,16},{28,20},{1,9},{5... | collective-permute-start | bytes 1179656 | tf_op jit(solution)/shard_map/ppermute | solution.py:33
  72.1 24.0 %collective-permute-start.9 = (bf16[256,768]{1,0:T(8,128)(2,1)}, bf16[256,768]{1,0:T(8,128)(2,1)}, u32[]{:S(2)}, u32[]{:S(2)}) collective-permute-start(bf16[256,768]{1,0:T(8,128)(2,1)} %slice.115), channel_id=1, source_target_pairs={{0,16},{4,20},{8,24},{12,28},{16,0},{20,4},{24,8},{28,12},{1,17},{... | collective-permute-start | bytes 1179656 | tf_op jit(solution)/shard_map/ppermute | solution.py:33
  96.2 148.9 %all-gather.7.cloned.1.call-start = ((), (), s32[]{:S(2)}) async-start(), calls=%async_computation.6 | async-start | bytes 7208960 | tf_op jit(solution)/shard_map/all_gather | solution.py:789
  97.0 195.5 %all-gather.9.cloned.1.call-start = ((), (), s32[]{:S(2)}) async-start(), calls=%async_computation.7 | async-start | bytes 3604480 | tf_op jit(solution)/shard_map/all_gather | solution.py:790
  102.7 28.4 %collective-permute-start.17 = (bf16[512,768]{1,0:T(8,128)(2,1)}, bf16[512,768]{1,0:T(8,128)(2,1)}, u32[]{:S(2)}, u32[]{:S(2)}) collective-permute-start(bf16[512,768]{1,0:T(8,128)(2,1)} %collective-permute-done.13.refs_7_), channel_id=1, source_target_pairs={{0,16},{4,20},{8,24},{12,28},{16,0},{20,4},{24,8},{28,12},{1,17},{... | collective-permute-start | bytes 2359304 | tf_op jit(solution)/shard_map/ppermute | solution.py:33
  103.3 27.8 %collective-permute-start.16 = (bf16[512,768]{1,0:T(8,128)(2,1)}, bf16[512,768]{1,0:T(8,128)(2,1)}, u32[]{:S(2)}, u32[]{:S(2)}) collective-permute-start(bf16[512,768]{1,0:T(8,128)(2,1)} %collective-permute-done.13.refs_7_), channel_id=1, source_target_pairs={{0,8},{4,12},{8,0},{12,4},{16,24},{20,28},{24,16},{28,20},{1,9},{5... | collective-permute-start | bytes 2359304 | tf_op jit(solution)/shard_map/ppermute | solution.py:33
  106.8 22.8 %collective-permute-start.15 = (bf16[256,768]{1,0:T(8,128)(2,1)S(1)}, bf16[256,768]{1,0:T(8,128)(2,1)S(1)}, u32[]{:S(2)}, u32[]{:S(2)}) collective-permute-start(bf16[256,768]{1,0:T(8,128)(2,1)S(1)} %slice.118), channel_id=1, source_target_pairs={{0,8},{4,12},{8,0},{12,4},{16,24},{20,28},{24,16},{28,20},{1,9},{5... | collective-permute-start | bytes 1179656 | tf_op jit(solution)/shard_map/ppermute | solution.py:33
  107.5 22.9 %collective-permute-start.14 = (bf16[256,768]{1,0:T(8,128)(2,1)S(1)}, bf16[256,768]{1,0:T(8,128)(2,1)S(1)}, u32[]{:S(2)}, u32[]{:S(2)}) collective-permute-start(bf16[256,768]{1,0:T(8,128)(2,1)S(1)} %slice.117), channel_id=1, source_target_pairs={{0,16},{4,20},{8,24},{12,28},{16,0},{20,4},{24,8},{28,12},{1,17},{... | collective-permute-start | bytes 1179656 | tf_op jit(solution)/shard_map/ppermute | solution.py:33
  131.1 47.7 %collective-permute-start.21 = (bf16[256,2048]{1,0:T(8,128)(2,1)}, bf16[256,2048]{1,0:T(8,128)(2,1)S(1)}, u32[]{:S(2)}, u32[]{:S(2)}) collective-permute-start(bf16[256,2048]{1,0:T(8,128)(2,1)} %all-gather.5.cloned.1.call-done.out_ref), channel_id=1, source_target_pairs={{0,16},{4,20},{8,24},{12,28},{16,0},{20,4},{24,8},{28,12},{1,17},{... | collective-permute-start | bytes 3145736 | tf_op jit(solution)/shard_map/ppermute | solution.py:33
  132.7 46.2 %collective-permute-start.20 = (bf16[256,2048]{1,0:T(8,128)(2,1)}, bf16[256,2048]{1,0:T(8,128)(2,1)S(1)}, u32[]{:S(2)}, u32[]{:S(2)}) collective-permute-start(bf16[256,2048]{1,0:T(8,128)(2,1)} %all-gather.5.cloned.1.call-done.out_ref), channel_id=1, source_target_pairs={{0,8},{4,12},{8,0},{12,4},{16,24},{20,28},{24,16},{28,20},{1,9},{5... | collective-permute-start | bytes 3145736 | tf_op jit(solution)/shard_map/ppermute | solution.py:33
  136.3 32.1 %collective-permute-start.19 = (bf16[256,768]{1,0:T(8,128)(2,1)S(1)}, bf16[256,768]{1,0:T(8,128)(2,1)S(1)}, u32[]{:S(2)}, u32[]{:S(2)}) collective-permute-start(bf16[256,768]{1,0:T(8,128)(2,1)S(1)} %slice.120), channel_id=1, source_target_pairs={{0,8},{4,12},{8,0},{12,4},{16,24},{20,28},{24,16},{28,20},{1,9},{5... | collective-permute-start | bytes 1179656 | tf_op jit(solution)/shard_map/ppermute | solution.py:33
  136.9 31.5 %collective-permute-start.18 = (bf16[256,768]{1,0:T(8,128)(2,1)S(1)}, bf16[256,768]{1,0:T(8,128)(2,1)S(1)}, u32[]{:S(2)}, u32[]{:S(2)}) collective-permute-start(bf16[256,768]{1,0:T(8,128)(2,1)S(1)} %slice.119), channel_id=1, source_target_pairs={{0,16},{4,20},{8,24},{12,28},{16,0},{20,4},{24,8},{28,12},{1,17},{... | collective-permute-start | bytes 1179656 | tf_op jit(solution)/shard_map/ppermute | solution.py:33
  202.7 301.5 %reduce-scatter.6.cloned.1.call-start = ((), (), s32[]{:S(2)}) async-start(), calls=%async_computation.8 | async-start | bytes 3604480 | tf_op jit(solution)/shard_map/reduce_scatter | solution.py:866
  307.0 41.7 %collective-permute-start.25 = (bf16[512,2048]{1,0:T(8,128)(2,1)}, bf16[512,2048]{1,0:T(8,128)(2,1)}, u32[]{:S(2)}, u32[]{:S(2)}) collective-permute-start(bf16[512,2048]{1,0:T(8,128)(2,1)} %slice.152), channel_id=1, source_target_pairs={{0,4},{4,0},{8,12},{12,8},{16,20},{20,16},{24,28},{28,24},{1,5},{5... | collective-permute-start | bytes 6291464 | tf_op jit(solution)/shard_map/ppermute | solution.py:33
  323.5 187.0 %reduce-scatter.8.cloned.1.call-start = ((), (), s32[]{:S(2)}) async-start(), calls=%async_computation.9 | async-start | bytes 3604480 | tf_op jit(solution)/shard_map/reduce_scatter | solution.py:866
  357.9 24.8 %collective-permute-start.28 = (bf16[128,2048]{1,0:T(8,128)(2,1)}, bf16[128,2048]{1,0:T(8,128)(2,1)S(1)}, u32[]{:S(2)}, u32[]{:S(2)}) collective-permute-start(bf16[128,2048]{1,0:T(8,128)(2,1)} %get-tuple-element.330), channel_id=1, source_target_pairs={{0,24},{4,28},{8,16},{12,20},{16,8},{20,12},{24,0},{28,4},{1,25},{... | collective-permute-start | bytes 1572872 | tf_op jit(solution)/shard_map/ppermute | solution.py:267
  359.4 25.2 %collective-permute-start.27 = (bf16[128,2048]{1,0:T(8,128)(2,1)S(1)}, bf16[128,2048]{1,0:T(8,128)(2,1)S(1)}, u32[]{:S(2)}, u32[]{:S(2)}) collective-permute-start(bf16[128,2048]{1,0:T(8,128)(2,1)S(1)} %get-tuple-element.331), channel_id=1, source_target_pairs={{0,16},{4,20},{8,24},{12,28},{16,0},{20,4},{24,8},{28,12},{1,17},{... | collective-permute-start | bytes 1572872 | tf_op jit(solution)/shard_map/ppermute | solution.py:267
  360.8 23.8 %collective-permute-start.26 = (bf16[128,2048]{1,0:T(8,128)(2,1)S(1)}, bf16[128,2048]{1,0:T(8,128)(2,1)S(1)}, u32[]{:S(2)}, u32[]{:S(2)}) collective-permute-start(bf16[128,2048]{1,0:T(8,128)(2,1)S(1)} %get-tuple-element.332), channel_id=1, source_target_pairs={{0,8},{4,12},{8,0},{12,4},{16,24},{20,28},{24,16},{28,20},{1,9},{5... | collective-permute-start | bytes 1572872 | tf_op jit(solution)/shard_map/ppermute | solution.py:267
  390.1 127.3 %reduce-scatter.10.cloned.1.call-start = ((), (), s32[]{:S(2)}) async-start(), calls=%async_computation.10 | async-start | bytes 3604480 | tf_op jit(solution)/shard_map/reduce_scatter | solution.py:866
  390.4 48.8 %collective-permute-start.32 = (bf16[1024,768]{1,0:T(8,128)(2,1)}, bf16[1024,768]{1,0:T(8,128)(2,1)}, u32[]{:S(2)}, u32[]{:S(2)}) collective-permute-start(bf16[1024,768]{1,0:T(8,128)(2,1)} %copy-done.38), channel_id=1, source_target_pairs={{0,8},{4,12},{8,0},{12,4},{16,24},{20,28},{24,16},{28,20},{1,9},{5... | collective-permute-start | bytes 4718600 | tf_op jit(solution)/shard_map/ppermute | solution.py:33
  391.9 47.3 %collective-permute-start.33 = (bf16[1024,768]{1,0:T(8,128)(2,1)}, bf16[1024,768]{1,0:T(8,128)(2,1)}, u32[]{:S(2)}, u32[]{:S(2)}) collective-permute-start(bf16[1024,768]{1,0:T(8,128)(2,1)} %get-tuple-element.217), channel_id=1, source_target_pairs={{0,16},{4,20},{8,24},{12,28},{16,0},{20,4},{24,8},{28,12},{1,17},{... | collective-permute-start | bytes 4718600 | tf_op jit(solution)/shard_map/ppermute | solution.py:33
  439.2 136.4 %reduce-scatter.12.cloned.1.call-start = ((), (), s32[]{:S(2)}) async-start(), calls=%async_computation.11 | async-start | bytes 3932160 | tf_op jit(solution)/shard_map/reduce_scatter | solution.py:881
  439.3 41.7 %collective-permute-start.30 = (bf16[1024,768]{1,0:T(8,128)(2,1)}, bf16[1024,768]{1,0:T(8,128)(2,1)}, u32[]{:S(2)}, u32[]{:S(2)}) collective-permute-start(bf16[1024,768]{1,0:T(8,128)(2,1)} %copy-done.37), channel_id=1, source_target_pairs={{0,8},{4,12},{8,0},{12,4},{16,24},{20,28},{24,16},{28,20},{1,9},{5... | collective-permute-start | bytes 4718600 | tf_op jit(solution)/shard_map/ppermute | solution.py:33
  440.9 40.0 %collective-permute-start.31 = (bf16[1024,768]{1,0:T(8,128)(2,1)}, bf16[1024,768]{1,0:T(8,128)(2,1)}, u32[]{:S(2)}, u32[]{:S(2)}) collective-permute-start(bf16[1024,768]{1,0:T(8,128)(2,1)} %get-tuple-element.215), channel_id=1, source_target_pairs={{0,16},{4,20},{8,24},{12,28},{16,0},{20,4},{24,8},{28,12},{1,17},{... | collective-permute-start | bytes 4718600 | tf_op jit(solution)/shard_map/ppermute | solution.py:33
  445.0 64.3 %collective-permute-start.35 = (bf16[1024,768]{1,0:T(8,128)(2,1)}, bf16[1024,768]{1,0:T(8,128)(2,1)}, u32[]{:S(2)}, u32[]{:S(2)}) collective-permute-start(bf16[1024,768]{1,0:T(8,128)(2,1)} %add_convert_fusion.4), channel_id=1, source_target_pairs={{0,8},{4,12},{8,0},{12,4},{16,24},{20,28},{24,16},{28,20},{1,9},{5... | collective-permute-start | bytes 4718600 | tf_op jit(solution)/shard_map/ppermute | solution.py:33
  449.8 60.7 %collective-permute-start.34 = (bf16[1024,768]{1,0:T(8,128)(2,1)}, bf16[1024,768]{1,0:T(8,128)(2,1)}, u32[]{:S(2)}, u32[]{:S(2)}) collective-permute-start(bf16[1024,768]{1,0:T(8,128)(2,1)} %add_convert_fusion.5), channel_id=1, source_target_pairs={{0,16},{4,20},{8,24},{12,28},{16,0},{20,4},{24,8},{28,12},{1,17},{... | collective-permute-start | bytes 4718600 | tf_op jit(solution)/shard_map/ppermute | solution.py:33
  517.5 142.1 %all-gather.11.cloned.1.call-start = ((), (), s32[]{:S(2)}) async-start(), calls=%async_computation.12 | async-start | bytes 6488064 | tf_op jit(solution)/shard_map/all_gather | solution.py:895
  517.6 32.1 %collective-permute-start.42 = (bf16[512,2048]{1,0:T(8,128)(2,1)}, bf16[512,2048]{1,0:T(8,128)(2,1)S(1)}, u32[]{:S(2)}, u32[]{:S(2)}) collective-permute-start(bf16[512,2048]{1,0:T(8,128)(2,1)} %get-tuple-element.248), channel_id=1, source_target_pairs={{0,4},{4,0},{8,12},{12,8},{16,20},{20,16},{24,28},{28,24},{1,5},{5... | collective-permute-start | bytes 6291464 | tf_op jit(solution)/shard_map/ppermute | solution.py:33
  517.7 32.0 %collective-permute-start.41 = (bf16[704,512]{1,0:T(8,128)(2,1)}, bf16[704,512]{1,0:T(8,128)(2,1)S(1)}, u32[]{:S(2)}, u32[]{:S(2)}) collective-permute-start(bf16[704,512]{1,0:T(8,128)(2,1)} %reduce-scatter.6.cloned.1.call-done), channel_id=1, source_target_pairs={{0,16},{4,20},{8,24},{12,28},{16,0},{20,4},{24,8},{28,12},{1,17},{... | collective-permute-start | bytes 2162696 | tf_op jit(solution)/shard_map/ppermute | solution.py:33
  518.3 31.4 %collective-permute-start.40 = (bf16[704,512]{1,0:T(8,128)(2,1)}, bf16[704,512]{1,0:T(8,128)(2,1)S(1)}, u32[]{:S(2)}, u32[]{:S(2)}) collective-permute-start(bf16[704,512]{1,0:T(8,128)(2,1)} %reduce-scatter.6.cloned.1.call-done), channel_id=1, source_target_pairs={{0,8},{4,12},{8,0},{12,4},{16,24},{20,28},{24,16},{28,20},{1,9},{5... | collective-permute-start | bytes 2162696 | tf_op jit(solution)/shard_map/ppermute | solution.py:33
  521.5 26.1 %collective-permute-start.39 = (bf16[128,2048]{1,0:T(8,128)(2,1)S(1)}, bf16[128,2048]{1,0:T(8,128)(2,1)S(1)}, u32[]{:S(2)}, u32[]{:S(2)}) collective-permute-start(bf16[128,2048]{1,0:T(8,128)(2,1)S(1)} %get-tuple-element.326), channel_id=1, source_target_pairs={{0,16},{4,20},{8,24},{12,28},{16,0},{20,4},{24,8},{28,12},{1,17},{... | collective-permute-start | bytes 1572872 | tf_op jit(solution)/shard_map/ppermute | solution.py:33
  522.1 26.1 %collective-permute-start.38 = (bf16[128,2048]{1,0:T(8,128)(2,1)S(1)}, bf16[128,2048]{1,0:T(8,128)(2,1)S(1)}, u32[]{:S(2)}, u32[]{:S(2)}) collective-permute-start(bf16[128,2048]{1,0:T(8,128)(2,1)S(1)} %get-tuple-element.327), channel_id=1, source_target_pairs={{0,8},{4,12},{8,0},{12,4},{16,24},{20,28},{24,16},{28,20},{1,9},{5... | collective-permute-start | bytes 1572872 | tf_op jit(solution)/shard_map/ppermute | solution.py:33
  548.3 15.0 %collective-permute-start.36 = (bf16[128,2048]{1,0:T(8,128)(2,1)S(1)}, bf16[128,2048]{1,0:T(8,128)(2,1)}, u32[]{:S(2)}, u32[]{:S(2)}) collective-permute-start(bf16[128,2048]{1,0:T(8,128)(2,1)S(1)} %get-tuple-element.329), channel_id=1, source_target_pairs={{0,8},{4,12},{8,0},{12,4},{16,24},{20,28},{24,16},{28,20},{1,9},{5... | collective-permute-start | bytes 1572872 | tf_op jit(solution)/shard_map/ppermute | solution.py:33
  549.8 19.6 %collective-permute-start.44 = (bf16[352,512]{1,0:T(8,128)(2,1)S(1)}, bf16[352,512]{1,0:T(8,128)(2,1)}, u32[]{:S(2)}, u32[]{:S(2)}) collective-permute-start(bf16[352,512]{1,0:T(8,128)(2,1)S(1)} %slice.138), channel_id=1, source_target_pairs={{0,8},{4,12},{8,0},{12,4},{16,24},{20,28},{24,16},{28,20},{1,9},{5... | collective-permute-start | bytes 1081352 | tf_op jit(solution)/shard_map/ppermute | solution.py:33
  550.5 18.9 %collective-permute-start.43 = (bf16[352,512]{1,0:T(8,128)(2,1)S(1)}, bf16[352,512]{1,0:T(8,128)(2,1)}, u32[]{:S(2)}, u32[]{:S(2)}) collective-permute-start(bf16[352,512]{1,0:T(8,128)(2,1)S(1)} %slice.137), channel_id=1, source_target_pairs={{0,16},{4,20},{8,24},{12,28},{16,0},{20,4},{24,8},{28,12},{1,17},{... | collective-permute-start | bytes 1081352 | tf_op jit(solution)/shard_map/ppermute | solution.py:33
  575.7 115.8 %reduce-scatter.14.cloned.1.call-start = ((), (), s32[]{:S(2)}) async-start(), calls=%async_computation.13 | async-start | bytes 1310720 | tf_op jit(solution)/shard_map/reduce_scatter | solution.py:898
  579.2 50.0 %collective-permute-start.47 = (bf16[2816,512]{1,0:T(8,128)(2,1)S(1)}, bf16[2816,512]{1,0:T(8,128)(2,1)S(1)}, u32[]{:S(2)}, u32[]{:S(2)}) collective-permute-start(bf16[2816,512]{1,0:T(8,128)(2,1)S(1)} %constant_dynamic-update-slice_fusion.23.same_ref), channel_id=1, source_target_pairs={{0,4},{4,0},{8,12},{12,8},{16,20},{20,16},{24,28},{28,24},{1,5},{5... | collective-permute-start | bytes 8650760 | tf_op jit(solution)/shard_map/ppermute | solution.py:33
  580.8 22.4 %collective-permute-start.46 = (bf16[128,2048]{1,0:T(8,128)(2,1)S(1)}, bf16[128,2048]{1,0:T(8,128)(2,1)S(1)}, u32[]{:S(2)}, u32[]{:S(2)}) collective-permute-start(bf16[128,2048]{1,0:T(8,128)(2,1)S(1)} %get-tuple-element.324), channel_id=1, source_target_pairs={{0,8},{4,12},{8,0},{12,4},{16,24},{20,28},{24,16},{28,20},{1,9},{5... | collective-permute-start | bytes 1572872 | tf_op jit(solution)/shard_map/ppermute | solution.py:33
  582.4 22.5 %collective-permute-start.45 = (bf16[128,2048]{1,0:T(8,128)(2,1)S(1)}, bf16[128,2048]{1,0:T(8,128)(2,1)S(1)}, u32[]{:S(2)}, u32[]{:S(2)}) collective-permute-start(bf16[128,2048]{1,0:T(8,128)(2,1)S(1)} %get-tuple-element.325), channel_id=1, source_target_pairs={{0,16},{4,20},{8,24},{12,28},{16,0},{20,4},{24,8},{28,12},{1,17},{... | collective-permute-start | bytes 1572872 | tf_op jit(solution)/shard_map/ppermute | solution.py:33
  583.8 45.3 %collective-permute-start.49 = (bf16[704,512]{1,0:T(8,128)(2,1)S(1)}, bf16[704,512]{1,0:T(8,128)(2,1)S(1)}, u32[]{:S(2)}, u32[]{:S(2)}) collective-permute-start(bf16[704,512]{1,0:T(8,128)(2,1)S(1)} %copy-done.79), channel_id=1, source_target_pairs={{0,16},{4,20},{8,24},{12,28},{16,0},{20,4},{24,8},{28,12},{1,17},{... | collective-permute-start | bytes 2162696 | tf_op jit(solution)/shard_map/ppermute | solution.py:33
  584.4 44.7 %collective-permute-start.48 = (bf16[704,512]{1,0:T(8,128)(2,1)S(1)}, bf16[704,512]{1,0:T(8,128)(2,1)S(1)}, u32[]{:S(2)}, u32[]{:S(2)}) collective-permute-start(bf16[704,512]{1,0:T(8,128)(2,1)S(1)} %copy-done.79), channel_id=1, source_target_pairs={{0,8},{4,12},{8,0},{12,4},{16,24},{20,28},{24,16},{28,20},{1,9},{5... | collective-permute-start | bytes 2162696 | tf_op jit(solution)/shard_map/ppermute | solution.py:33
  604.8 47.7 %collective-permute-start.54 = (bf16[512,768]{1,0:T(8,128)(2,1)S(1)}, bf16[512,768]{1,0:T(8,128)(2,1)S(1)}, u32[]{:S(2)}, u32[]{:S(2)}) collective-permute-start(bf16[512,768]{1,0:T(8,128)(2,1)S(1)} %copy-done.78), channel_id=1, source_target_pairs={{0,16},{4,20},{8,24},{12,28},{16,0},{20,4},{24,8},{28,12},{1,17},{... | collective-permute-start | bytes 2359304 | tf_op jit(solution)/shard_map/ppermute | solution.py:33
  606.3 46.3 %collective-permute-start.53 = (bf16[512,768]{1,0:T(8,128)(2,1)S(1)}, bf16[512,768]{1,0:T(8,128)(2,1)S(1)}, u32[]{:S(2)}, u32[]{:S(2)}) collective-permute-start(bf16[512,768]{1,0:T(8,128)(2,1)S(1)} %copy-done.78), channel_id=1, source_target_pairs={{0,8},{4,12},{8,0},{12,4},{16,24},{20,28},{24,16},{28,20},{1,9},{5... | collective-permute-start | bytes 2359304 | tf_op jit(solution)/shard_map/ppermute | solution.py:33
  629.2 29.6 %collective-permute-start.52 = (bf16[352,512]{1,0:T(8,128)(2,1)S(1)}, bf16[352,512]{1,0:T(8,128)(2,1)S(1)}, u32[]{:S(2)}, u32[]{:S(2)}) collective-permute-start(bf16[352,512]{1,0:T(8,128)(2,1)S(1)} %slice.142), channel_id=1, source_target_pairs={{0,8},{4,12},{8,0},{12,4},{16,24},{20,28},{24,16},{28,20},{1,9},{5... | collective-permute-start | bytes 1081352 | tf_op jit(solution)/shard_map/ppermute | solution.py:33
  629.3 30.3 %collective-permute-start.51 = (bf16[352,512]{1,0:T(8,128)(2,1)S(1)}, bf16[352,512]{1,0:T(8,128)(2,1)S(1)}, u32[]{:S(2)}, u32[]{:S(2)}) collective-permute-start(bf16[352,512]{1,0:T(8,128)(2,1)S(1)} %slice.141), channel_id=1, source_target_pairs={{0,16},{4,20},{8,24},{12,28},{16,0},{20,4},{24,8},{28,12},{1,17},{... | collective-permute-start | bytes 1081352 | tf_op jit(solution)/shard_map/ppermute | solution.py:33
  632.7 26.0 %collective-permute-start.55 = (f32[2,2048]{1,0:T(2,128)S(1)}, f32[2,2048]{1,0:T(2,128)S(1)}, u32[]{:S(2)}, u32[]{:S(2)}) collective-permute-start(f32[2,2048]{1,0:T(2,128)S(1)} %add.217), channel_id=1, source_target_pairs={{0,8},{4,12},{8,0},{12,4},{16,24},{20,28},{24,16},{28,20},{1,9},{5... | collective-permute-start | bytes 49160 | tf_op jit(solution)/shard_map/ppermute | solution.py:33
  661.1 30.4 %collective-permute-start.56 = (bf16[2816,512]{1,0:T(8,128)(2,1)}, bf16[2816,512]{1,0:T(8,128)(2,1)}, u32[]{:S(2)}, u32[]{:S(2)}) collective-permute-start(bf16[2816,512]{1,0:T(8,128)(2,1)} %constant_dynamic-update-slice_fusion.28.same_ref), channel_id=1, source_target_pairs={{0,4},{4,0},{8,12},{12,8},{16,20},{20,16},{24,28},{28,24},{1,5},{5... | collective-permute-start | bytes 8650760 | tf_op jit(solution)/shard_map/ppermute | solution.py:33
  665.8 25.7 %collective-permute-start.58 = (bf16[256,768]{1,0:T(8,128)(2,1)}, bf16[256,768]{1,0:T(8,128)(2,1)S(1)}, u32[]{:S(2)}, u32[]{:S(2)}) collective-permute-start(bf16[256,768]{1,0:T(8,128)(2,1)} %slice.144), channel_id=1, source_target_pairs={{0,8},{4,12},{8,0},{12,4},{16,24},{20,28},{24,16},{28,20},{1,9},{5... | collective-permute-start | bytes 1179656 | tf_op jit(solution)/shard_map/ppermute | solution.py:33
  667.0 24.5 %collective-permute-start.57 = (bf16[256,768]{1,0:T(8,128)(2,1)}, bf16[256,768]{1,0:T(8,128)(2,1)}, u32[]{:S(2)}, u32[]{:S(2)}) collective-permute-start(bf16[256,768]{1,0:T(8,128)(2,1)} %slice.143), channel_id=1, source_target_pairs={{0,16},{4,20},{8,24},{12,28},{16,0},{20,4},{24,8},{28,12},{1,17},{... | collective-permute-start | bytes 1179656 | tf_op jit(solution)/shard_map/ppermute | solution.py:33
  670.4 21.0 %collective-permute-start.59 = (f32[2,2048]{1,0:T(2,128)S(1)}, f32[2,2048]{1,0:T(2,128)}, u32[]{:S(2)}, u32[]{:S(2)}) collective-permute-start(f32[2,2048]{1,0:T(2,128)S(1)} %add.218), channel_id=1, source_target_pairs={{0,16},{4,20},{8,24},{12,28},{16,0},{20,4},{24,8},{28,12},{1,17},{... | collective-permute-start | bytes 49160 | tf_op jit(solution)/shard_map/ppermute | solution.py:33
  692.5 27.2 %collective-permute-start.60 = (bf16[2048,768]{1,0:T(8,128)(2,1)S(1)}, bf16[2048,768]{1,0:T(8,128)(2,1)}, u32[]{:S(2)}, u32[]{:S(2)}) collective-permute-start(bf16[2048,768]{1,0:T(8,128)(2,1)S(1)} %constant_dynamic-update-slice_fusion.33.same_ref), channel_id=1, source_target_pairs={{0,4},{4,0},{8,12},{12,8},{16,20},{20,16},{24,28},{28,24},{1,5},{5... | collective-permute-start | bytes 9437192 | tf_op jit(solution)/shard_map/ppermute | solution.py:33
  692.6 27.1 %collective-permute-start.63 = (bf16[256,512]{1,0:T(8,128)(2,1)}, bf16[256,512]{1,0:T(8,128)(2,1)S(1)}, u32[]{:S(2)}, u32[]{:S(2)}) collective-permute-start(bf16[256,512]{1,0:T(8,128)(2,1)} %reduce-scatter.14.cloned.1.call-done), channel_id=1, source_target_pairs={{0,24},{4,28},{8,16},{12,20},{16,8},{20,12},{24,0},{28,4},{1,25},{... | collective-permute-start | bytes 786440 | tf_op jit(solution)/shard_map/ppermute | solution.py:267
  695.0 24.6 %collective-permute-start.62 = (bf16[256,512]{1,0:T(8,128)(2,1)}, bf16[256,512]{1,0:T(8,128)(2,1)}, u32[]{:S(2)}, u32[]{:S(2)}) collective-permute-start(bf16[256,512]{1,0:T(8,128)(2,1)} %reduce-scatter.14.cloned.1.call-done), channel_id=1, source_target_pairs={{0,16},{4,20},{8,24},{12,28},{16,0},{20,4},{24,8},{28,12},{1,17},{... | collective-permute-start | bytes 786440 | tf_op jit(solution)/shard_map/ppermute | solution.py:267
  695.6 24.1 %collective-permute-start.61 = (bf16[256,512]{1,0:T(8,128)(2,1)}, bf16[256,512]{1,0:T(8,128)(2,1)}, u32[]{:S(2)}, u32[]{:S(2)}) collective-permute-start(bf16[256,512]{1,0:T(8,128)(2,1)} %reduce-scatter.14.cloned.1.call-done), channel_id=1, source_target_pairs={{0,8},{4,12},{8,0},{12,4},{16,24},{20,28},{24,16},{28,20},{1,9},{5... | collective-permute-start | bytes 786440 | tf_op jit(solution)/shard_map/ppermute | solution.py:267
  (126 other events, 1217.1 us)
Sparse Core Ops, SparseCore 0:
  96.3 28.0 all-gather.4
  126.6 106.1 all-gather.6
  234.9 57.4 all-gather.8
  323.6 54.9 reduce-scatter.5
  390.3 54.2 reduce-scatter.7
  447.2 56.0 reduce-scatter.9
  517.6 58.0 reduce-scatter.11
  577.5 66.7 all-gather.10
  664.3 27.0 reduce-scatter.13

commit v15 on v12

--- a/solution.py
+++ b/solution.py
@@ -691,6 +691,26 @@
     )(me, same, other)
 
 
+def widen_kernel(in_ref, out_ref):
+    out_ref[...] = in_ref[...].astype(F32)
+
+
+def widen(value):
+    rows, width = value.shape
+    tile = rows // 4
+    spec = pl.BlockSpec((tile, width), lambda i: (i, 0))
+    return pl.pallas_call(
+        widen_kernel,
+        grid=(4,),
+        in_specs=[spec],
+        out_specs=spec,
+        out_shape=jax.ShapeDtypeStruct(value.shape, F32),
+        compiler_params=pltpu.CompilerParams(vmem_limit_bytes=32 << 20),
+        cost_estimate=pl.CostEstimate(flops=0, bytes_accessed=6 * value.size, transcendentals=0),
+        name="widen",
+    )(value)
+
+
 def per_device(
     layer_input,
     gain_attn,
@@ -886,7 +906,7 @@
     grad_up = stage([qkv_flow, out_flow, gain_flow], grad_up)
     grad_query, grad_key, grad_value = place(whoami, *finish(qkv_flow), own, block, True)
     (grad_out,) = place(whoami, *finish(out_flow), block, own, False)
-    grad_down = all_down.astype(F32)
+    grad_down = widen(all_down)
     gain_grads = finish(gain_flow)
     return (
         output,

time: 721 us -> 720 us (level)
  other arithmetic: 58.9 us -> 50.1 us
    convert_element_type x1 -> x0, other arithmetic: 8.87 us -> none  [per_device(): grad_down = all_down.astype(F32)]
    unnamed x259 -> x261, local copies, waits for them, and re-layouts: 58.1 us -> 60.8 us
  transfers between devices with their start and end apart: 77 -> 77, of which waited for: 20 -> 20; matrix products, arithmetic and copies ran while one was open for 20% -> 20% of each run, Pallas kernels for 33% -> 34%
where the time goes in v15:
time: 720 us; the launch traced here: 713 us
  Pallas kernels  244 us (34%)
  waiting for transfers between devices  173 us (24%)
  local copies, waits for them, and re-layouts  92 us (13%)
  matrix products  71.7 us (10%)
  starting transfers between devices  66.8 us (9%)
  other arithmetic  50.1 us (7%)
  between operations  15.8 us (2%)
    ppermute x53, waiting for transfers between devices, swap(): return lax.ppermute(value, 'rep', [(i, i ^ bit) for i in range(size)])  110 us
    pallas_call x4, Pallas kernels, attend_back(): pl.pallas_call(attend_back_kernel, grid=(rows // length,), in_specs=[whol...  71.9 us
    unnamed x261, local copies, waits for them, and re-layouts  60.8 us
    pallas_call x2, Pallas kernels, gather_rows(): pl.pallas_call(functools.partial(gather_kernel, peers()), out_shape=jax.S...  58.4 us
    ppermute x53, starting transfers between devices, swap(): return lax.ppermute(value, 'rep', [(i, i ^ bit) for i in range(size)])  48 us
    pallas_call x4, Pallas kernels, attend(): pl.pallas_call(functools.partial(attend_kernel, parts), grid_spec=pltpu.P...  42.5 us
    dot_general x6, matrix products, mm_tn(): lax.dot_general(left, right, (((0,), (0,)), ((), ())), preferred_element_...  26.9 us
    dot_general x5, matrix products, mm(): return jnp.dot(left, right, preferred_element_type=F32)  24.6 us
  transfers between devices with their start and end apart: 77, of which 20 were waited for; matrix products, arithmetic and copies ran while one was open for 20% of the time, Pallas kernels for 34%

profile of v15, /device:TPU:0, one launch (start us, length us, event | category | flops | bytes accessed | tf_op | source)
XLA Modules:
  0.0 712.7 jit_solution(7098662600589351534)
XLA Ops:
  8.8 3.1 collective-permute-start.2
  11.8 2.6 collective-permute-start.1
  17.7 2.7 constant_dynamic-slice_fusion.4
  21.2 2.3 constant_dynamic-slice_fusion.15
  26.2 16.2 %collective-permute-done.3.refs_5_ = bf16[512,768]{1,0:T(8,128)(2,1)} collective-permute-done((bf16[512,768]{1,0:T(8,128)(2,1)S(1)}, bf16[512,768]{1,0:T(8,128)(2,1)}, u32[]{:S(2)}, u32[]{:S(2)}) %collective-permute-start.3) | collective-permute-done | bytes 786464 | tf_op jit(solution)/shard_map/ppermute | solution.py:763
  42.5 2.1 fusion.2
  47.9 18.9 %collective-permute-done.7.refs_6_ = bf16[512,768]{1,0:T(8,128)(2,1)} collective-permute-done((bf16[512,768]{1,0:T(8,128)(2,1)}, bf16[512,768]{1,0:T(8,128)(2,1)}, u32[]{:S(2)}, u32[]{:S(2)}) %collective-permute-start.7) | collective-permute-done | bytes 786464 | tf_op jit(solution)/shard_map/ppermute | solution.py:777
  75.4 20.7 %collective-permute-done.10 = bf16[256,768]{1,0:T(8,128)(2,1)} collective-permute-done((bf16[256,768]{1,0:T(8,128)(2,1)}, bf16[256,768]{1,0:T(8,128)(2,1)}, u32[]{:S(2)}, u32[]{:S(2)}) %collective-permute-start.10) | collective-permute-done | bytes 393248 | tf_op jit(solution)/shard_map/ppermute | solution.py:33
  99.4 2.1 pad_maximum_fusion.6.refs_4_.refs_8_
  110.0 2.1 pad_maximum_fusion.refs_0_.refs_1_.refs_2_.refs_3_.x_ref
  114.4 11.3 %attend.4 = (bf16[1024,256]{1,0:T(8,128)(2,1)S(1)}, bf16[1024,768]{1,0:T(8,128)(2,1)S(1)}, f32[1024,2]{1,0:T(8,128)S(1)}) custom-call(s32[1]{0:T(128)} %bitcast.1.z_ref, bf16[1024,2048]{1,0:T(8,128)(2,1)S(1)} %pad_maximum_fusion.refs_0_.refs_1_.refs_2_.refs_3_.x_ref, bf16[1024,2048]{1,0:T(8,128)(2,1)S(1)} %pad_maximum_fusion.refs_0_.refs_1_.refs_2_.refs_3_.x_ref, ...), custom_call_target="tpu_custom_call" | custom-call | flops 3758096384 | bytes 10485760 | tf_op jit(solution)/shard_map/attend/pallas_call | solution.py:423
  139.3 2.2 copy-done.3
  143.8 10.7 %attend.5 = (bf16[1024,256]{1,0:T(8,128)(2,1)S(1)}, bf16[1024,768]{1,0:T(8,128)(2,1)S(1)}, f32[1024,2]{1,0:T(8,128)S(1)}) custom-call(s32[1]{0:T(128)} %bitcast.1.z_ref, bf16[1024,2048]{1,0:T(8,128)(2,1)S(1)} %copy-done.3, bf16[1024,2048]{1,0:T(8,128)(2,1)S(1)} %copy-done.3, bf16[1024,2048]{1,0:T(8,128)(2,1)S(1)} %copy-done.3, ...), custom_call_target="tpu_custom_call" | custom-call | flops 3758096384 | bytes 10485760 | tf_op jit(solution)/shard_map/attend/pallas_call | solution.py:423
  156.6 10.8 %attend.6 = (bf16[1024,256]{1,0:T(8,128)(2,1)S(1)}, bf16[1024,768]{1,0:T(8,128)(2,1)S(1)}, f32[1024,2]{1,0:T(8,128)S(1)}) custom-call(s32[1]{0:T(128)} %bitcast.1.z_ref, bf16[1024,2048]{1,0:T(8,128)(2,1)S(1)} %copy-done.3, bf16[1024,2048]{1,0:T(8,128)(2,1)S(1)} %copy-done.3, bf16[1024,2048]{1,0:T(8,128)(2,1)S(1)} %copy-done.3, ...), custom_call_target="tpu_custom_call" | custom-call | flops 3758096384 | bytes 10485760 | tf_op jit(solution)/shard_map/attend/pallas_call | solution.py:423
  169.2 9.6 %attend.7 = (bf16[1024,256]{1,0:T(8,128)(2,1)S(1)}, bf16[1024,768]{1,0:T(8,128)(2,1)S(1)}, f32[1024,2]{1,0:T(8,128)S(1)}) custom-call(s32[1]{0:T(128)} %bitcast.1.z_ref, bf16[1024,2048]{1,0:T(8,128)(2,1)S(1)} %copy-done.3, bf16[1024,2048]{1,0:T(8,128)(2,1)S(1)} %copy-done.3, bf16[1024,2048]{1,0:T(8,128)(2,1)S(1)} %copy-done.3, ...), custom_call_target="tpu_custom_call" | custom-call | flops 3758096384 | bytes 10485760 | tf_op jit(solution)/shard_map/attend/pallas_call | solution.py:423
  183.1 6.1 collective-permute-done.22
  189.3 2.1 collective-permute-done.23
  191.4 6.3 fusion.53
  197.7 3.4 copy-done.67
  203.3 2.3 fusion.22.in_ref
  207.3 4.0 multiply_reduce_fusion.2
  214.0 29.1 %gather_rows.2 = bf16[1024,2048]{1,0:T(8,128)(2,1)S(1)} custom-call(bf16[128,2048]{1,0:T(8,128)(2,1)S(1)} %convolution_convert_fusion.5.in_ref), custom_call_target="tpu_custom_call" | custom-call | bytes 62914560 | tf_op jit(solution)/shard_map/gather_rows/pallas_call | solution.py:153
  245.2 11.7 %fusion.54 = f32[1024,1408]{1,0:T(8,128)} fusion(bf16[1024,2048]{1,0:T(8,128)(2,1)} %copy-done.9, bf16[2048,1408]{1,0:T(8,128)(2,1)} %all-gather.7.cloned.1.call-done), kind=kOutput, calls=%fused_computation.179 | convolution fusion | flops 5905580032 | bytes 15728640 | tf_op jit(solution)/shard_map/dot_general | solution.py:20
  256.9 29.3 %gather_rows.3 = bf16[1024,2048]{1,0:T(8,128)(2,1)S(1)} custom-call(bf16[128,2048]{1,0:T(8,128)(2,1)S(1)} %fusion.22.in_ref), custom_call_target="tpu_custom_call" | custom-call | bytes 62914560 | tf_op jit(solution)/shard_map/gather_rows/pallas_call | solution.py:153
  288.2 4.2 all-gather.9.cloned.1.call-done
  292.4 9.1 %multiply_convert_fusion.2 = (bf16[1024,704]{1,0:T(8,128)(2,1)S(1)}, bf16[1024,704]{1,0:T(8,128)(2,1)S(1)}, bf16[1024,704]{1,0:T(8,128)(2,1)S(1)}) fusion(f32[1024,1408]{1,0:T(8,128)} %fusion.54, bf16[1024,2048]{1,0:T(8,128)(2,1)} %copy-done.7, bf16[704,2048]{1,0:T(8,128)(2,1)} %all-gather.9.cloned.1.call-done), kind=kOutput, calls=%fused_computation.44 | convolution fusion | flops 2963603456 | bytes 17170432 | tf_op jit(solution)/shard_map/dot_general | solution.py:24
  301.5 3.6 convolution_convert_fusion.1
  307.8 11.1 %convolution_convert_fusion.in_ref = bf16[1024,2048]{1,0:T(8,128)(2,1)} fusion(bf16[2048,1408]{1,0:T(8,128)(2,1)} %all-gather.7.cloned.1.call-done, bf16[1024,704]{1,0:T(8,128)(2,1)S(1)} %get-tuple-element.203, bf16[1024,704]{1,0:T(8,128)(2,1)S(1)} %get-tuple-element.316), kind=kOutput, calls=%fused_computation.34 | convolution fusion | flops 5913444352 | bytes 12845056 | tf_op jit(solution)/shard_map/dot_general | solution.py:24
  318.9 4.5 convolution_convert_fusion.4
  323.9 2.2 copy-done.12
  326.1 22.5 %reduce_rows.1 = bf16[128,2048]{1,0:T(8,128)(2,1)S(1)} custom-call(bf16[1024,2048]{1,0:T(8,128)(2,1)S(1)} %copy-done.12), custom_call_target="tpu_custom_call" | custom-call | bytes 62914560 | tf_op jit(solution)/shard_map/reduce_rows/pallas_call | solution.py:243
  350.2 3.2 multiply_convert_fusion
  354.2 2.5 add_convert_fusion.1
  362.5 17.7 %attend_back.4 = (bf16[1024,768]{1,0:T(8,128)(2,1)S(1)}, bf16[1024,768]{1,0:T(8,128)(2,1)S(1)}, bf16[1024,768]{1,0:T(8,128)(2,1)}) custom-call(bf16[512,2048]{1,0:T(8,128)(2,1)} %copy-done.70, bf16[512,2048]{1,0:T(8,128)(2,1)} %copy-done.110, bf16[256,2048]{1,0:T(8,128)(2,1)S(1)} %pad_maximum_fusion.3.out_ref, bf16[1024,768]{1,0:T(8,128)(2,1)} %copy-done.42, ...), custom_call_target="tpu_custom_call" | custom-call | flops 5637144576 | bytes 15728640 | tf_op jit(solution)/shard_map/attend_back/pallas_call | solution.py:519
  385.4 4.5 convolution_convert_fusion.3
  393.4 18.1 %attend_back.6 = (bf16[1024,768]{1,0:T(8,128)(2,1)S(1)}, bf16[1024,768]{1,0:T(8,128)(2,1)S(1)}, bf16[1024,768]{1,0:T(8,128)(2,1)}) custom-call(bf16[512,2048]{1,0:T(8,128)(2,1)} %copy-done.70, bf16[512,2048]{1,0:T(8,128)(2,1)} %copy-done.110, bf16[256,2048]{1,0:T(8,128)(2,1)S(1)} %copy-done.24, bf16[1024,768]{1,0:T(8,128)(2,1)} %copy-done.41, ...), custom_call_target="tpu_custom_call" | custom-call | flops 5637144576 | bytes 15728640 | tf_op jit(solution)/shard_map/attend_back/pallas_call | solution.py:519
  414.4 17.7 %attend_back.5 = (bf16[1024,768]{1,0:T(8,128)(2,1)S(1)}, bf16[1024,768]{1,0:T(8,128)(2,1)S(1)}, bf16[1024,768]{1,0:T(8,128)(2,1)}) custom-call(bf16[512,2048]{1,0:T(8,128)(2,1)} %copy-done.70, bf16[512,2048]{1,0:T(8,128)(2,1)} %copy-done.110, bf16[256,2048]{1,0:T(8,128)(2,1)S(1)} %copy-done.22, bf16[1024,768]{1,0:T(8,128)(2,1)} %copy-done.40, ...), custom_call_target="tpu_custom_call" | custom-call | flops 5637144576 | bytes 15728640 | tf_op jit(solution)/shard_map/attend_back/pallas_call | solution.py:519
  434.5 4.5 convolution_convert_fusion.2
  441.4 3.4 add_convert_fusion.4
  446.2 3.5 add_convert_fusion.5
  450.1 18.4 %attend_back.7 = (bf16[1024,768]{1,0:T(8,128)(2,1)S(1)}, bf16[1024,768]{1,0:T(8,128)(2,1)S(1)}, bf16[1024,768]{1,0:T(8,128)(2,1)}) custom-call(bf16[512,2048]{1,0:T(8,128)(2,1)} %copy-done.70, bf16[512,2048]{1,0:T(8,128)(2,1)} %copy-done.110, bf16[256,2048]{1,0:T(8,128)(2,1)S(1)} %copy-done.38, bf16[1024,768]{1,0:T(8,128)(2,1)} %copy-done.39, ...), custom_call_target="tpu_custom_call" | custom-call | flops 5637144576 | bytes 15728640 | tf_op jit(solution)/shard_map/attend_back/pallas_call | solution.py:519
  468.6 10.0 %fusion.15 = bf16[1024,2048]{1,0:T(8,128)(2,1)} fusion(bf16[1024,1024]{1,0:T(8,128)(2,1)} %constant_dynamic-update-slice_fusion.14, bf16[512,2048]{1,0:T(8,128)(2,1)} %copy-done.110, bf16[512,2048]{1,0:T(8,128)(2,1)S(1)} %copy-done.71), kind=kOutput, calls=%fused_computation.33 | convolution fusion | flops 4305453056 | bytes 10485760 | tf_op jit(solution)/shard_map/dot_general | solution.py:28
  478.6 2.2 add_convert_fusion
  480.8 23.3 %normed_back.1 = (f32[512,2048]{1,0:T(8,128)}, bf16[512,2048]{1,0:T(8,128)(2,1)}) custom-call(s32[1]{0:T(128)} %bitcast.1.z_ref, bf16[1024,768]{1,0:T(8,128)(2,1)} %copy-done.54, bf16[1024,768]{1,0:T(8,128)(2,1)} %copy-done.53, bf16[1024,768]{1,0:T(8,128)(2,1)} %copy-done.52, bf16[1024,768]{1,0:T(8,128)(2,1)} %copy-done.51, ...), custom_call_target="tpu_custom_call" | custom-call | flops 12884901888 | bytes 27262976 | tf_op jit(solution)/shard_map/normed_back/pallas_call | solution.py:576
  504.1 5.1 collective-permute-done.35
  510.3 2.6 add_convert_fusion.2
  512.9 2.5 add_convert_fusion.3
  524.5 22.8 %collective-permute-done.39 = bf16[128,2048]{1,0:T(8,128)(2,1)S(1)} collective-permute-done((bf16[128,2048]{1,0:T(8,128)(2,1)S(1)}, bf16[128,2048]{1,0:T(8,128)(2,1)S(1)}, u32[]{:S(2)}, u32[]{:S(2)}) %collective-permute-start.39) | collective-permute-done | bytes 524320 | tf_op jit(solution)/shard_map/ppermute | solution.py:33
  551.6 3.2 fusion.9
  554.8 3.9 fusion.6
  558.8 3.4 collective-permute-done.37
  562.8 6.1 collective-permute-done.44
  575.8 24.2 %collective-permute-done.46 = bf16[128,2048]{1,0:T(8,128)(2,1)S(1)} collective-permute-done((bf16[128,2048]{1,0:T(8,128)(2,1)S(1)}, bf16[128,2048]{1,0:T(8,128)(2,1)S(1)}, u32[]{:S(2)}, u32[]{:S(2)}) %collective-permute-start.46) | collective-permute-done | bytes 524320 | tf_op jit(solution)/shard_map/ppermute | solution.py:33
  603.6 2.2 add_convert_fusion.7
  615.6 5.0 place_turned.2
  620.6 13.8 %collective-permute-done.55 = f32[2,2048]{1,0:T(2,128)S(1)} collective-permute-done((f32[2,2048]{1,0:T(2,128)S(1)}, f32[2,2048]{1,0:T(2,128)S(1)}, u32[]{:S(2)}, u32[]{:S(2)}) %collective-permute-start.55) | collective-permute-done | bytes 16416 | tf_op jit(solution)/shard_map/ppermute | solution.py:33
  646.2 6.2 collective-permute-done.61
  652.4 2.3 collective-permute-start.59
  657.1 14.3 %collective-permute-done.60 = bf16[256,512]{1,0:T(8,128)(2,1)S(1)} collective-permute-done((bf16[256,512]{1,0:T(8,128)(2,1)S(1)}, bf16[256,512]{1,0:T(8,128)(2,1)S(1)}, u32[]{:S(2)}, u32[]{:S(2)}) %collective-permute-start.60) | collective-permute-done | bytes 262176 | tf_op jit(solution)/shard_map/ppermute | solution.py:267
  682.3 5.0 place_turned.3
  687.3 4.3 place.3
  691.6 6.3 place.2
  698.5 2.6 copy-done.4
  701.2 4.5 widen.1
  (474 shorter events, 158.6 us)
Async XLA Ops:
  7.2 124.0 %all-gather.5.cloned.1.call-start = ((), (), s32[]{:S(2)}) async-start(), calls=%async_computation.5 | async-start | bytes 1310720 | tf_op jit(solution)/shard_map/all_gather | solution.py:781
  8.8 17.4 %collective-permute-start.2 = (bf16[2,512]{1,0:T(2,128)(2,1)S(1)}, bf16[2,512]{1,0:T(2,128)(2,1)S(1)}, u32[]{:S(2)}, u32[]{:S(2)}) collective-permute-start(bf16[2,512]{1,0:T(2,128)(2,1)S(1)} %get-tuple-element.312), channel_id=1, source_target_pairs={{0,1},{1,2},{2,3},{3,0},{4,5},{5,6},{6,7},{7,4},{8,9},{9,10},{10,1... | collective-permute-start | bytes 6152 | tf_op jit(solution)/shard_map/ppermute | solution.py:344
  11.8 14.3 %collective-permute-start.1 = (bf16[2,512]{1,0:T(2,128)(2,1)S(1)}, bf16[2,512]{1,0:T(2,128)(2,1)S(1)}, u32[]{:S(2)}, u32[]{:S(2)}) collective-permute-start(bf16[2,512]{1,0:T(2,128)(2,1)S(1)} %get-tuple-element.312), channel_id=1, source_target_pairs={{0,2},{1,3},{2,0},{3,1},{4,6},{5,7},{6,4},{7,5},{8,10},{9,11},{10,... | collective-permute-start | bytes 6152 | tf_op jit(solution)/shard_map/ppermute | solution.py:344
  20.5 21.9 %collective-permute-start.3 = (bf16[512,768]{1,0:T(8,128)(2,1)S(1)}, bf16[512,768]{1,0:T(8,128)(2,1)}, u32[]{:S(2)}, u32[]{:S(2)}) collective-permute-start(bf16[512,768]{1,0:T(8,128)(2,1)S(1)} %pad_maximum_fusion.5.refs_4_), channel_id=1, source_target_pairs={{0,1},{1,2},{2,3},{3,0},{4,5},{5,6},{6,7},{7,4},{8,9},{9,10},{10,1... | collective-permute-start | bytes 2359304 | tf_op jit(solution)/shard_map/ppermute | solution.py:763
  44.7 22.2 %collective-permute-start.8 = (bf16[512,2048]{1,0:T(8,128)(2,1)S(1)}, bf16[512,2048]{1,0:T(8,128)(2,1)S(1)}, u32[]{:S(2)}, u32[]{:S(2)}) collective-permute-start(bf16[512,2048]{1,0:T(8,128)(2,1)S(1)} %fusion.2), channel_id=1, source_target_pairs={{0,4},{4,0},{8,12},{12,8},{16,20},{20,16},{24,28},{28,24},{1,5},{5... | collective-permute-start | bytes 6291464 | tf_op jit(solution)/shard_map/ppermute | solution.py:33
  44.8 22.1 %collective-permute-start.7 = (bf16[512,768]{1,0:T(8,128)(2,1)}, bf16[512,768]{1,0:T(8,128)(2,1)}, u32[]{:S(2)}, u32[]{:S(2)}) collective-permute-start(bf16[512,768]{1,0:T(8,128)(2,1)} %collective-permute-done.3.refs_5_), channel_id=1, source_target_pairs={{0,1},{1,2},{2,3},{3,0},{4,5},{5,6},{6,7},{7,4},{8,9},{9,10},{10,1... | collective-permute-start | bytes 2359304 | tf_op jit(solution)/shard_map/ppermute | solution.py:777
  44.8 22.0 %collective-permute-start.6 = (bf16[512,768]{1,0:T(8,128)(2,1)}, bf16[512,768]{1,0:T(8,128)(2,1)S(1)}, u32[]{:S(2)}, u32[]{:S(2)}) collective-permute-start(bf16[512,768]{1,0:T(8,128)(2,1)} %collective-permute-done.3.refs_5_), channel_id=1, source_target_pairs={{0,16},{4,20},{8,24},{12,28},{16,0},{20,4},{24,8},{28,12},{1,17},{... | collective-permute-start | bytes 2359304 | tf_op jit(solution)/shard_map/ppermute | solution.py:33
  46.4 20.4 %collective-permute-start.5 = (bf16[512,768]{1,0:T(8,128)(2,1)}, bf16[512,768]{1,0:T(8,128)(2,1)S(1)}, u32[]{:S(2)}, u32[]{:S(2)}) collective-permute-start(bf16[512,768]{1,0:T(8,128)(2,1)} %collective-permute-done.3.refs_5_), channel_id=1, source_target_pairs={{0,8},{4,12},{8,0},{12,4},{16,24},{20,28},{24,16},{28,20},{1,9},{5... | collective-permute-start | bytes 2359304 | tf_op jit(solution)/shard_map/ppermute | solution.py:33
  66.9 29.2 %collective-permute-start.13 = (bf16[512,768]{1,0:T(8,128)(2,1)}, bf16[512,768]{1,0:T(8,128)(2,1)}, u32[]{:S(2)}, u32[]{:S(2)}) collective-permute-start(bf16[512,768]{1,0:T(8,128)(2,1)} %collective-permute-done.7.refs_6_), channel_id=1, source_target_pairs={{0,1},{1,2},{2,3},{3,0},{4,5},{5,6},{6,7},{7,4},{8,9},{9,10},{10,1... | collective-permute-start | bytes 2359304 | tf_op jit(solution)/shard_map/ppermute | solution.py:777
  66.9 29.2 %collective-permute-start.12 = (bf16[512,768]{1,0:T(8,128)(2,1)}, bf16[512,768]{1,0:T(8,128)(2,1)}, u32[]{:S(2)}, u32[]{:S(2)}) collective-permute-start(bf16[512,768]{1,0:T(8,128)(2,1)} %collective-permute-done.7.refs_6_), channel_id=1, source_target_pairs={{0,16},{4,20},{8,24},{12,28},{16,0},{20,4},{24,8},{28,12},{1,17},{... | collective-permute-start | bytes 2359304 | tf_op jit(solution)/shard_map/ppermute | solution.py:33
  68.5 27.6 %collective-permute-start.11 = (bf16[512,768]{1,0:T(8,128)(2,1)}, bf16[512,768]{1,0:T(8,128)(2,1)}, u32[]{:S(2)}, u32[]{:S(2)}) collective-permute-start(bf16[512,768]{1,0:T(8,128)(2,1)} %collective-permute-done.7.refs_6_), channel_id=1, source_target_pairs={{0,8},{4,12},{8,0},{12,4},{16,24},{20,28},{24,16},{28,20},{1,9},{5... | collective-permute-start | bytes 2359304 | tf_op jit(solution)/shard_map/ppermute | solution.py:33
  71.5 24.5 %collective-permute-start.10 = (bf16[256,768]{1,0:T(8,128)(2,1)}, bf16[256,768]{1,0:T(8,128)(2,1)}, u32[]{:S(2)}, u32[]{:S(2)}) collective-permute-start(bf16[256,768]{1,0:T(8,128)(2,1)} %slice.116), channel_id=1, source_target_pairs={{0,8},{4,12},{8,0},{12,4},{16,24},{20,28},{24,16},{28,20},{1,9},{5... | collective-permute-start | bytes 1179656 | tf_op jit(solution)/shard_map/ppermute | solution.py:33
  72.1 24.0 %collective-permute-start.9 = (bf16[256,768]{1,0:T(8,128)(2,1)}, bf16[256,768]{1,0:T(8,128)(2,1)}, u32[]{:S(2)}, u32[]{:S(2)}) collective-permute-start(bf16[256,768]{1,0:T(8,128)(2,1)} %slice.115), channel_id=1, source_target_pairs={{0,16},{4,20},{8,24},{12,28},{16,0},{20,4},{24,8},{28,12},{1,17},{... | collective-permute-start | bytes 1179656 | tf_op jit(solution)/shard_map/ppermute | solution.py:33
  96.1 149.0 %all-gather.7.cloned.1.call-start = ((), (), s32[]{:S(2)}) async-start(), calls=%async_computation.6 | async-start | bytes 7208960 | tf_op jit(solution)/shard_map/all_gather | solution.py:789
  96.9 195.5 %all-gather.9.cloned.1.call-start = ((), (), s32[]{:S(2)}) async-start(), calls=%async_computation.7 | async-start | bytes 3604480 | tf_op jit(solution)/shard_map/all_gather | solution.py:790
  102.7 28.4 %collective-permute-start.17 = (bf16[512,768]{1,0:T(8,128)(2,1)}, bf16[512,768]{1,0:T(8,128)(2,1)}, u32[]{:S(2)}, u32[]{:S(2)}) collective-permute-start(bf16[512,768]{1,0:T(8,128)(2,1)} %collective-permute-done.13.refs_7_), channel_id=1, source_target_pairs={{0,16},{4,20},{8,24},{12,28},{16,0},{20,4},{24,8},{28,12},{1,17},{... | collective-permute-start | bytes 2359304 | tf_op jit(solution)/shard_map/ppermute | solution.py:33
  103.3 27.8 %collective-permute-start.16 = (bf16[512,768]{1,0:T(8,128)(2,1)}, bf16[512,768]{1,0:T(8,128)(2,1)}, u32[]{:S(2)}, u32[]{:S(2)}) collective-permute-start(bf16[512,768]{1,0:T(8,128)(2,1)} %collective-permute-done.13.refs_7_), channel_id=1, source_target_pairs={{0,8},{4,12},{8,0},{12,4},{16,24},{20,28},{24,16},{28,20},{1,9},{5... | collective-permute-start | bytes 2359304 | tf_op jit(solution)/shard_map/ppermute | solution.py:33
  106.9 22.8 %collective-permute-start.15 = (bf16[256,768]{1,0:T(8,128)(2,1)S(1)}, bf16[256,768]{1,0:T(8,128)(2,1)S(1)}, u32[]{:S(2)}, u32[]{:S(2)}) collective-permute-start(bf16[256,768]{1,0:T(8,128)(2,1)S(1)} %slice.118), channel_id=1, source_target_pairs={{0,8},{4,12},{8,0},{12,4},{16,24},{20,28},{24,16},{28,20},{1,9},{5... | collective-permute-start | bytes 1179656 | tf_op jit(solution)/shard_map/ppermute | solution.py:33
  107.5 22.9 %collective-permute-start.14 = (bf16[256,768]{1,0:T(8,128)(2,1)S(1)}, bf16[256,768]{1,0:T(8,128)(2,1)S(1)}, u32[]{:S(2)}, u32[]{:S(2)}) collective-permute-start(bf16[256,768]{1,0:T(8,128)(2,1)S(1)} %slice.117), channel_id=1, source_target_pairs={{0,16},{4,20},{8,24},{12,28},{16,0},{20,4},{24,8},{28,12},{1,17},{... | collective-permute-start | bytes 1179656 | tf_op jit(solution)/shard_map/ppermute | solution.py:33
  131.2 47.7 %collective-permute-start.21 = (bf16[256,2048]{1,0:T(8,128)(2,1)}, bf16[256,2048]{1,0:T(8,128)(2,1)S(1)}, u32[]{:S(2)}, u32[]{:S(2)}) collective-permute-start(bf16[256,2048]{1,0:T(8,128)(2,1)} %all-gather.5.cloned.1.call-done.out_ref), channel_id=1, source_target_pairs={{0,16},{4,20},{8,24},{12,28},{16,0},{20,4},{24,8},{28,12},{1,17},{... | collective-permute-start | bytes 3145736 | tf_op jit(solution)/shard_map/ppermute | solution.py:33
  132.7 46.2 %collective-permute-start.20 = (bf16[256,2048]{1,0:T(8,128)(2,1)}, bf16[256,2048]{1,0:T(8,128)(2,1)S(1)}, u32[]{:S(2)}, u32[]{:S(2)}) collective-permute-start(bf16[256,2048]{1,0:T(8,128)(2,1)} %all-gather.5.cloned.1.call-done.out_ref), channel_id=1, source_target_pairs={{0,8},{4,12},{8,0},{12,4},{16,24},{20,28},{24,16},{28,20},{1,9},{5... | collective-permute-start | bytes 3145736 | tf_op jit(solution)/shard_map/ppermute | solution.py:33
  136.3 32.2 %collective-permute-start.19 = (bf16[256,768]{1,0:T(8,128)(2,1)S(1)}, bf16[256,768]{1,0:T(8,128)(2,1)S(1)}, u32[]{:S(2)}, u32[]{:S(2)}) collective-permute-start(bf16[256,768]{1,0:T(8,128)(2,1)S(1)} %slice.120), channel_id=1, source_target_pairs={{0,8},{4,12},{8,0},{12,4},{16,24},{20,28},{24,16},{28,20},{1,9},{5... | collective-permute-start | bytes 1179656 | tf_op jit(solution)/shard_map/ppermute | solution.py:33
  136.9 31.5 %collective-permute-start.18 = (bf16[256,768]{1,0:T(8,128)(2,1)S(1)}, bf16[256,768]{1,0:T(8,128)(2,1)S(1)}, u32[]{:S(2)}, u32[]{:S(2)}) collective-permute-start(bf16[256,768]{1,0:T(8,128)(2,1)S(1)} %slice.119), channel_id=1, source_target_pairs={{0,16},{4,20},{8,24},{12,28},{16,0},{20,4},{24,8},{28,12},{1,17},{... | collective-permute-start | bytes 1179656 | tf_op jit(solution)/shard_map/ppermute | solution.py:33
  202.8 301.3 %reduce-scatter.6.cloned.1.call-start = ((), (), s32[]{:S(2)}) async-start(), calls=%async_computation.8 | async-start | bytes 3604480 | tf_op jit(solution)/shard_map/reduce_scatter | solution.py:866
  306.9 41.7 %collective-permute-start.25 = (bf16[512,2048]{1,0:T(8,128)(2,1)}, bf16[512,2048]{1,0:T(8,128)(2,1)}, u32[]{:S(2)}, u32[]{:S(2)}) collective-permute-start(bf16[512,2048]{1,0:T(8,128)(2,1)} %slice.152), channel_id=1, source_target_pairs={{0,4},{4,0},{8,12},{12,8},{16,20},{20,16},{24,28},{28,24},{1,5},{5... | collective-permute-start | bytes 6291464 | tf_op jit(solution)/shard_map/ppermute | solution.py:33
  323.4 186.9 %reduce-scatter.8.cloned.1.call-start = ((), (), s32[]{:S(2)}) async-start(), calls=%async_computation.9 | async-start | bytes 3604480 | tf_op jit(solution)/shard_map/reduce_scatter | solution.py:866
  357.7 24.8 %collective-permute-start.28 = (bf16[128,2048]{1,0:T(8,128)(2,1)}, bf16[128,2048]{1,0:T(8,128)(2,1)S(1)}, u32[]{:S(2)}, u32[]{:S(2)}) collective-permute-start(bf16[128,2048]{1,0:T(8,128)(2,1)} %get-tuple-element.326), channel_id=1, source_target_pairs={{0,24},{4,28},{8,16},{12,20},{16,8},{20,12},{24,0},{28,4},{1,25},{... | collective-permute-start | bytes 1572872 | tf_op jit(solution)/shard_map/ppermute | solution.py:267
  359.2 25.2 %collective-permute-start.27 = (bf16[128,2048]{1,0:T(8,128)(2,1)S(1)}, bf16[128,2048]{1,0:T(8,128)(2,1)S(1)}, u32[]{:S(2)}, u32[]{:S(2)}) collective-permute-start(bf16[128,2048]{1,0:T(8,128)(2,1)S(1)} %get-tuple-element.327), channel_id=1, source_target_pairs={{0,16},{4,20},{8,24},{12,28},{16,0},{20,4},{24,8},{28,12},{1,17},{... | collective-permute-start | bytes 1572872 | tf_op jit(solution)/shard_map/ppermute | solution.py:267
  360.7 23.8 %collective-permute-start.26 = (bf16[128,2048]{1,0:T(8,128)(2,1)S(1)}, bf16[128,2048]{1,0:T(8,128)(2,1)S(1)}, u32[]{:S(2)}, u32[]{:S(2)}) collective-permute-start(bf16[128,2048]{1,0:T(8,128)(2,1)S(1)} %get-tuple-element.328), channel_id=1, source_target_pairs={{0,8},{4,12},{8,0},{12,4},{16,24},{20,28},{24,16},{28,20},{1,9},{5... | collective-permute-start | bytes 1572872 | tf_op jit(solution)/shard_map/ppermute | solution.py:267
  390.0 127.3 %reduce-scatter.10.cloned.1.call-start = ((), (), s32[]{:S(2)}) async-start(), calls=%async_computation.10 | async-start | bytes 3604480 | tf_op jit(solution)/shard_map/reduce_scatter | solution.py:866
  390.2 48.9 %collective-permute-start.32 = (bf16[1024,768]{1,0:T(8,128)(2,1)}, bf16[1024,768]{1,0:T(8,128)(2,1)}, u32[]{:S(2)}, u32[]{:S(2)}) collective-permute-start(bf16[1024,768]{1,0:T(8,128)(2,1)} %copy-done.44), channel_id=1, source_target_pairs={{0,8},{4,12},{8,0},{12,4},{16,24},{20,28},{24,16},{28,20},{1,9},{5... | collective-permute-start | bytes 4718600 | tf_op jit(solution)/shard_map/ppermute | solution.py:33
  391.7 47.3 %collective-permute-start.33 = (bf16[1024,768]{1,0:T(8,128)(2,1)}, bf16[1024,768]{1,0:T(8,128)(2,1)}, u32[]{:S(2)}, u32[]{:S(2)}) collective-permute-start(bf16[1024,768]{1,0:T(8,128)(2,1)} %get-tuple-element.215), channel_id=1, source_target_pairs={{0,16},{4,20},{8,24},{12,28},{16,0},{20,4},{24,8},{28,12},{1,17},{... | collective-permute-start | bytes 4718600 | tf_op jit(solution)/shard_map/ppermute | solution.py:33
  439.1 164.6 %reduce-scatter.12.cloned.1.call-start = ((), (), s32[]{:S(2)}) async-start(), calls=%async_computation.11 | async-start | bytes 3932160 | tf_op jit(solution)/shard_map/reduce_scatter | solution.py:881
  439.1 41.7 %collective-permute-start.30 = (bf16[1024,768]{1,0:T(8,128)(2,1)}, bf16[1024,768]{1,0:T(8,128)(2,1)}, u32[]{:S(2)}, u32[]{:S(2)}) collective-permute-start(bf16[1024,768]{1,0:T(8,128)(2,1)} %copy-done.43), channel_id=1, source_target_pairs={{0,8},{4,12},{8,0},{12,4},{16,24},{20,28},{24,16},{28,20},{1,9},{5... | collective-permute-start | bytes 4718600 | tf_op jit(solution)/shard_map/ppermute | solution.py:33
  440.8 40.0 %collective-permute-start.31 = (bf16[1024,768]{1,0:T(8,128)(2,1)}, bf16[1024,768]{1,0:T(8,128)(2,1)}, u32[]{:S(2)}, u32[]{:S(2)}) collective-permute-start(bf16[1024,768]{1,0:T(8,128)(2,1)} %get-tuple-element.213), channel_id=1, source_target_pairs={{0,16},{4,20},{8,24},{12,28},{16,0},{20,4},{24,8},{28,12},{1,17},{... | collective-permute-start | bytes 4718600 | tf_op jit(solution)/shard_map/ppermute | solution.py:33
  444.8 64.4 %collective-permute-start.35 = (bf16[1024,768]{1,0:T(8,128)(2,1)}, bf16[1024,768]{1,0:T(8,128)(2,1)}, u32[]{:S(2)}, u32[]{:S(2)}) collective-permute-start(bf16[1024,768]{1,0:T(8,128)(2,1)} %add_convert_fusion.4), channel_id=1, source_target_pairs={{0,8},{4,12},{8,0},{12,4},{16,24},{20,28},{24,16},{28,20},{1,9},{5... | collective-permute-start | bytes 4718600 | tf_op jit(solution)/shard_map/ppermute | solution.py:33
  449.6 60.7 %collective-permute-start.34 = (bf16[1024,768]{1,0:T(8,128)(2,1)}, bf16[1024,768]{1,0:T(8,128)(2,1)}, u32[]{:S(2)}, u32[]{:S(2)}) collective-permute-start(bf16[1024,768]{1,0:T(8,128)(2,1)} %add_convert_fusion.5), channel_id=1, source_target_pairs={{0,16},{4,20},{8,24},{12,28},{16,0},{20,4},{24,8},{28,12},{1,17},{... | collective-permute-start | bytes 4718600 | tf_op jit(solution)/shard_map/ppermute | solution.py:33
  510.3 39.1 %collective-permute-start.42 = (bf16[512,2048]{1,0:T(8,128)(2,1)}, bf16[512,2048]{1,0:T(8,128)(2,1)}, u32[]{:S(2)}, u32[]{:S(2)}) collective-permute-start(bf16[512,2048]{1,0:T(8,128)(2,1)} %get-tuple-element.246), channel_id=1, source_target_pairs={{0,4},{4,0},{8,12},{12,8},{16,20},{20,16},{24,28},{28,24},{1,5},{5... | collective-permute-start | bytes 6291464 | tf_op jit(solution)/shard_map/ppermute | solution.py:33
  517.3 117.1 %reduce-scatter.14.cloned.1.call-start = ((), (), s32[]{:S(2)}) async-start(), calls=%async_computation.12 | async-start | bytes 1310720 | tf_op jit(solution)/shard_map/reduce_scatter | solution.py:897
  517.4 32.0 %collective-permute-start.41 = (bf16[704,512]{1,0:T(8,128)(2,1)}, bf16[704,512]{1,0:T(8,128)(2,1)S(1)}, u32[]{:S(2)}, u32[]{:S(2)}) collective-permute-start(bf16[704,512]{1,0:T(8,128)(2,1)} %reduce-scatter.6.cloned.1.call-done), channel_id=1, source_target_pairs={{0,16},{4,20},{8,24},{12,28},{16,0},{20,4},{24,8},{28,12},{1,17},{... | collective-permute-start | bytes 2162696 | tf_op jit(solution)/shard_map/ppermute | solution.py:33
  518.1 31.3 %collective-permute-start.40 = (bf16[704,512]{1,0:T(8,128)(2,1)}, bf16[704,512]{1,0:T(8,128)(2,1)S(1)}, u32[]{:S(2)}, u32[]{:S(2)}) collective-permute-start(bf16[704,512]{1,0:T(8,128)(2,1)} %reduce-scatter.6.cloned.1.call-done), channel_id=1, source_target_pairs={{0,8},{4,12},{8,0},{12,4},{16,24},{20,28},{24,16},{28,20},{1,9},{5... | collective-permute-start | bytes 2162696 | tf_op jit(solution)/shard_map/ppermute | solution.py:33
  521.3 26.1 %collective-permute-start.39 = (bf16[128,2048]{1,0:T(8,128)(2,1)S(1)}, bf16[128,2048]{1,0:T(8,128)(2,1)S(1)}, u32[]{:S(2)}, u32[]{:S(2)}) collective-permute-start(bf16[128,2048]{1,0:T(8,128)(2,1)S(1)} %get-tuple-element.322), channel_id=1, source_target_pairs={{0,16},{4,20},{8,24},{12,28},{16,0},{20,4},{24,8},{28,12},{1,17},{... | collective-permute-start | bytes 1572872 | tf_op jit(solution)/shard_map/ppermute | solution.py:33
  522.0 26.0 %collective-permute-start.38 = (bf16[128,2048]{1,0:T(8,128)(2,1)S(1)}, bf16[128,2048]{1,0:T(8,128)(2,1)S(1)}, u32[]{:S(2)}, u32[]{:S(2)}) collective-permute-start(bf16[128,2048]{1,0:T(8,128)(2,1)S(1)} %get-tuple-element.323), channel_id=1, source_target_pairs={{0,8},{4,12},{8,0},{12,4},{16,24},{20,28},{24,16},{28,20},{1,9},{5... | collective-permute-start | bytes 1572872 | tf_op jit(solution)/shard_map/ppermute | solution.py:33
  547.3 14.8 %collective-permute-start.37 = (bf16[128,2048]{1,0:T(8,128)(2,1)S(1)}, bf16[128,2048]{1,0:T(8,128)(2,1)S(1)}, u32[]{:S(2)}, u32[]{:S(2)}) collective-permute-start(bf16[128,2048]{1,0:T(8,128)(2,1)S(1)} %get-tuple-element.324), channel_id=1, source_target_pairs={{0,16},{4,20},{8,24},{12,28},{16,0},{20,4},{24,8},{28,12},{1,17},{... | collective-permute-start | bytes 1572872 | tf_op jit(solution)/shard_map/ppermute | solution.py:33
  548.0 14.9 %collective-permute-start.36 = (bf16[128,2048]{1,0:T(8,128)(2,1)S(1)}, bf16[128,2048]{1,0:T(8,128)(2,1)S(1)}, u32[]{:S(2)}, u32[]{:S(2)}) collective-permute-start(bf16[128,2048]{1,0:T(8,128)(2,1)S(1)} %get-tuple-element.325), channel_id=1, source_target_pairs={{0,8},{4,12},{8,0},{12,4},{16,24},{20,28},{24,16},{28,20},{1,9},{5... | collective-permute-start | bytes 1572872 | tf_op jit(solution)/shard_map/ppermute | solution.py:33
  549.5 19.4 %collective-permute-start.44 = (bf16[352,512]{1,0:T(8,128)(2,1)S(1)}, bf16[352,512]{1,0:T(8,128)(2,1)S(1)}, u32[]{:S(2)}, u32[]{:S(2)}) collective-permute-start(bf16[352,512]{1,0:T(8,128)(2,1)S(1)} %slice.138), channel_id=1, source_target_pairs={{0,8},{4,12},{8,0},{12,4},{16,24},{20,28},{24,16},{28,20},{1,9},{5... | collective-permute-start | bytes 1081352 | tf_op jit(solution)/shard_map/ppermute | solution.py:33
  550.2 18.7 %collective-permute-start.43 = (bf16[352,512]{1,0:T(8,128)(2,1)S(1)}, bf16[352,512]{1,0:T(8,128)(2,1)S(1)}, u32[]{:S(2)}, u32[]{:S(2)}) collective-permute-start(bf16[352,512]{1,0:T(8,128)(2,1)S(1)} %slice.137), channel_id=1, source_target_pairs={{0,16},{4,20},{8,24},{12,28},{16,0},{20,4},{24,8},{28,12},{1,17},{... | collective-permute-start | bytes 1081352 | tf_op jit(solution)/shard_map/ppermute | solution.py:33
  569.0 33.1 %collective-permute-start.47 = (bf16[2816,512]{1,0:T(8,128)(2,1)S(1)}, bf16[2816,512]{1,0:T(8,128)(2,1)S(1)}, u32[]{:S(2)}, u32[]{:S(2)}) collective-permute-start(bf16[2816,512]{1,0:T(8,128)(2,1)S(1)} %constant_dynamic-update-slice_fusion.23.same_ref), channel_id=1, source_target_pairs={{0,4},{4,0},{8,12},{12,8},{16,20},{20,16},{24,28},{28,24},{1,5},{5... | collective-permute-start | bytes 8650760 | tf_op jit(solution)/shard_map/ppermute | solution.py:33
  569.1 30.9 %collective-permute-start.49 = (bf16[704,512]{1,0:T(8,128)(2,1)S(1)}, bf16[704,512]{1,0:T(8,128)(2,1)S(1)}, u32[]{:S(2)}, u32[]{:S(2)}) collective-permute-start(bf16[704,512]{1,0:T(8,128)(2,1)S(1)} %copy-done.85), channel_id=1, source_target_pairs={{0,16},{4,20},{8,24},{12,28},{16,0},{20,4},{24,8},{28,12},{1,17},{... | collective-permute-start | bytes 2162696 | tf_op jit(solution)/shard_map/ppermute | solution.py:33
  570.5 30.3 %collective-permute-start.48 = (bf16[704,512]{1,0:T(8,128)(2,1)S(1)}, bf16[704,512]{1,0:T(8,128)(2,1)S(1)}, u32[]{:S(2)}, u32[]{:S(2)}) collective-permute-start(bf16[704,512]{1,0:T(8,128)(2,1)S(1)} %copy-done.85), channel_id=1, source_target_pairs={{0,8},{4,12},{8,0},{12,4},{16,24},{20,28},{24,16},{28,20},{1,9},{5... | collective-permute-start | bytes 2162696 | tf_op jit(solution)/shard_map/ppermute | solution.py:33
  572.7 27.2 %collective-permute-start.46 = (bf16[128,2048]{1,0:T(8,128)(2,1)S(1)}, bf16[128,2048]{1,0:T(8,128)(2,1)S(1)}, u32[]{:S(2)}, u32[]{:S(2)}) collective-permute-start(bf16[128,2048]{1,0:T(8,128)(2,1)S(1)} %get-tuple-element.320), channel_id=1, source_target_pairs={{0,8},{4,12},{8,0},{12,4},{16,24},{20,28},{24,16},{28,20},{1,9},{5... | collective-permute-start | bytes 1572872 | tf_op jit(solution)/shard_map/ppermute | solution.py:33
  574.4 25.6 %collective-permute-start.45 = (bf16[128,2048]{1,0:T(8,128)(2,1)S(1)}, bf16[128,2048]{1,0:T(8,128)(2,1)S(1)}, u32[]{:S(2)}, u32[]{:S(2)}) collective-permute-start(bf16[128,2048]{1,0:T(8,128)(2,1)S(1)} %get-tuple-element.321), channel_id=1, source_target_pairs={{0,16},{4,20},{8,24},{12,28},{16,0},{20,4},{24,8},{28,12},{1,17},{... | collective-permute-start | bytes 1572872 | tf_op jit(solution)/shard_map/ppermute | solution.py:33
  606.9 91.7 %all-gather.11.cloned.1.call-start = ((), (), s32[]{:S(2)}) async-start(), calls=%async_computation.13 | async-start | bytes 6488064 | tf_op jit(solution)/shard_map/all_gather | solution.py:902
  606.9 27.5 %collective-permute-start.54 = (bf16[512,768]{1,0:T(8,128)(2,1)}, bf16[512,768]{1,0:T(8,128)(2,1)}, u32[]{:S(2)}, u32[]{:S(2)}) collective-permute-start(bf16[512,768]{1,0:T(8,128)(2,1)} %reduce-scatter.12.cloned.1.call-done), channel_id=1, source_target_pairs={{0,16},{4,20},{8,24},{12,28},{16,0},{20,4},{24,8},{28,12},{1,17},{... | collective-permute-start | bytes 2359304 | tf_op jit(solution)/shard_map/ppermute | solution.py:33
  607.6 26.8 %collective-permute-start.53 = (bf16[512,768]{1,0:T(8,128)(2,1)}, bf16[512,768]{1,0:T(8,128)(2,1)}, u32[]{:S(2)}, u32[]{:S(2)}) collective-permute-start(bf16[512,768]{1,0:T(8,128)(2,1)} %reduce-scatter.12.cloned.1.call-done), channel_id=1, source_target_pairs={{0,8},{4,12},{8,0},{12,4},{16,24},{20,28},{24,16},{28,20},{1,9},{5... | collective-permute-start | bytes 2359304 | tf_op jit(solution)/shard_map/ppermute | solution.py:33
  611.1 23.3 %collective-permute-start.52 = (bf16[352,512]{1,0:T(8,128)(2,1)S(1)}, bf16[352,512]{1,0:T(8,128)(2,1)S(1)}, u32[]{:S(2)}, u32[]{:S(2)}) collective-permute-start(bf16[352,512]{1,0:T(8,128)(2,1)S(1)} %slice.142), channel_id=1, source_target_pairs={{0,8},{4,12},{8,0},{12,4},{16,24},{20,28},{24,16},{28,20},{1,9},{5... | collective-permute-start | bytes 1081352 | tf_op jit(solution)/shard_map/ppermute | solution.py:33
  611.7 22.7 %collective-permute-start.51 = (bf16[352,512]{1,0:T(8,128)(2,1)S(1)}, bf16[352,512]{1,0:T(8,128)(2,1)}, u32[]{:S(2)}, u32[]{:S(2)}) collective-permute-start(bf16[352,512]{1,0:T(8,128)(2,1)S(1)} %slice.141), channel_id=1, source_target_pairs={{0,16},{4,20},{8,24},{12,28},{16,0},{20,4},{24,8},{28,12},{1,17},{... | collective-permute-start | bytes 1081352 | tf_op jit(solution)/shard_map/ppermute | solution.py:33
  613.1 21.3 %collective-permute-start.55 = (f32[2,2048]{1,0:T(2,128)S(1)}, f32[2,2048]{1,0:T(2,128)S(1)}, u32[]{:S(2)}, u32[]{:S(2)}) collective-permute-start(f32[2,2048]{1,0:T(2,128)S(1)} %add.217), channel_id=1, source_target_pairs={{0,8},{4,12},{8,0},{12,4},{16,24},{20,28},{24,16},{28,20},{1,9},{5... | collective-permute-start | bytes 49160 | tf_op jit(solution)/shard_map/ppermute | solution.py:33
  638.1 33.4 %collective-permute-start.56 = (bf16[2816,512]{1,0:T(8,128)(2,1)S(1)}, bf16[2816,512]{1,0:T(8,128)(2,1)S(1)}, u32[]{:S(2)}, u32[]{:S(2)}) collective-permute-start(bf16[2816,512]{1,0:T(8,128)(2,1)S(1)} %constant_dynamic-update-slice_fusion.28.same_ref), channel_id=1, source_target_pairs={{0,4},{4,0},{8,12},{12,8},{16,20},{20,16},{24,28},{28,24},{1,5},{5... | collective-permute-start | bytes 8650760 | tf_op jit(solution)/shard_map/ppermute | solution.py:33
  638.1 14.3 %collective-permute-start.61 = (bf16[256,512]{1,0:T(8,128)(2,1)S(1)}, bf16[256,512]{1,0:T(8,128)(2,1)S(1)}, u32[]{:S(2)}, u32[]{:S(2)}) collective-permute-start(bf16[256,512]{1,0:T(8,128)(2,1)S(1)} %copy-done.98), channel_id=1, source_target_pairs={{0,24},{4,28},{8,16},{12,20},{16,8},{20,12},{24,0},{28,4},{1,25},{... | collective-permute-start | bytes 786440 | tf_op jit(solution)/shard_map/ppermute | solution.py:267
  643.3 28.2 %collective-permute-start.58 = (bf16[256,768]{1,0:T(8,128)(2,1)S(1)}, bf16[256,768]{1,0:T(8,128)(2,1)S(1)}, u32[]{:S(2)}, u32[]{:S(2)}) collective-permute-start(bf16[256,768]{1,0:T(8,128)(2,1)S(1)} %slice.146), channel_id=1, source_target_pairs={{0,8},{4,12},{8,0},{12,4},{16,24},{20,28},{24,16},{28,20},{1,9},{5... | collective-permute-start | bytes 1179656 | tf_op jit(solution)/shard_map/ppermute | solution.py:33
  644.0 27.5 %collective-permute-start.57 = (bf16[256,768]{1,0:T(8,128)(2,1)S(1)}, bf16[256,768]{1,0:T(8,128)(2,1)S(1)}, u32[]{:S(2)}, u32[]{:S(2)}) collective-permute-start(bf16[256,768]{1,0:T(8,128)(2,1)S(1)} %slice.145), channel_id=1, source_target_pairs={{0,16},{4,20},{8,24},{12,28},{16,0},{20,4},{24,8},{28,12},{1,17},{... | collective-permute-start | bytes 1179656 | tf_op jit(solution)/shard_map/ppermute | solution.py:33
  645.5 26.0 %collective-permute-start.60 = (bf16[256,512]{1,0:T(8,128)(2,1)S(1)}, bf16[256,512]{1,0:T(8,128)(2,1)S(1)}, u32[]{:S(2)}, u32[]{:S(2)}) collective-permute-start(bf16[256,512]{1,0:T(8,128)(2,1)S(1)} %copy-done.98), channel_id=1, source_target_pairs={{0,16},{4,20},{8,24},{12,28},{16,0},{20,4},{24,8},{28,12},{1,17},{... | collective-permute-start | bytes 786440 | tf_op jit(solution)/shard_map/ppermute | solution.py:267
  652.4 19.0 %collective-permute-start.59 = (bf16[256,512]{1,0:T(8,128)(2,1)S(1)}, bf16[256,512]{1,0:T(8,128)(2,1)S(1)}, u32[]{:S(2)}, u32[]{:S(2)}) collective-permute-start(bf16[256,512]{1,0:T(8,128)(2,1)S(1)} %copy-done.98), channel_id=1, source_target_pairs={{0,8},{4,12},{8,0},{12,4},{16,24},{20,28},{24,16},{28,20},{1,9},{5... | collective-permute-start | bytes 786440 | tf_op jit(solution)/shard_map/ppermute | solution.py:267
  (128 other events, 1185.6 us)
Sparse Core Ops, SparseCore 0:
  96.2 28.0 all-gather.4
  126.5 106.1 all-gather.6
  234.9 57.4 all-gather.8
  323.6 54.9 reduce-scatter.5
  390.1 54.1 reduce-scatter.7
  447.0 56.0 reduce-scatter.9
  517.4 58.1 reduce-scatter.11
  607.0 24.9 reduce-scatter.13
  634.6 52.5 all-gather.10
